TPU v7x, 32 devices: a whole 2x2x4 slice. The times are simulated.
32 devices in a mesh: rep: 4 (over z), shard: 8 (over y, x, core).
Axes of the slice: x: 2, y: 2, z: 4, core: 2. Of those that a mesh axis runs over, the one named last changes fastest.
Arguments:
- tokens: bfloat16 [32, 1024, 512], P(('rep', 'shard')), may hold values from -6 to 6
- step_embed: bfloat16 [32, 512], P(('rep', 'shard')), may hold values from -3 to 3
- lengths: int32 [32], P(('rep', 'shard')), may hold values from 256 to 1024, as said below
- cotangent: bfloat16 [32, 1024, 512], P(('rep', 'shard')), may hold values from -6 to 6
- ln1_gain: bfloat16 [512], P('shard'), may hold values from 0.5 to 1.5
- ln1_bias: bfloat16 [512], P('shard'), may hold values from -1.1953125 to 1.1953125
- qkv_weight: bfloat16 [512, 1536], P('shard'), may hold values from -0.25 to 0.25
- q_bias: bfloat16 [512], P('shard'), may hold values from -1.1953125 to 1.1953125
- v_bias: bfloat16 [512], P('shard'), may hold values from -1.1953125 to 1.1953125
- out_weight: bfloat16 [512, 512], P('shard'), may hold values from -4 to 4
- out_bias: bfloat16 [512], P('shard'), may hold values from -1.1953125 to 1.1953125
- ln2_gain: bfloat16 [512], P('shard'), may hold values from 0.5 to 1.5
- ln2_bias: bfloat16 [512], P('shard'), may hold values from -1.1953125 to 1.1953125
- up_weight: bfloat16 [512, 2048], P('shard'), may hold values from -0.25 to 0.25
- up_bias: bfloat16 [2048], P('shard'), may hold values from -1.1953125 to 1.1953125
- down_weight: bfloat16 [2048, 512], P('shard'), may hold values from -0.25 to 0.25
- down_bias: bfloat16 [512], P('shard'), may hold values from -1.1953125 to 1.1953125
Outputs:
- output: bfloat16 [32, 1024, 512], P(('rep', 'shard'))
- tokens_grad: float32 [32, 1024, 512], P(('rep', 'shard'))
- ln1_gain_grad: float32 [512], P('shard')
- ln1_bias_grad: float32 [512], P('shard')
- qkv_weight_grad: float32 [512, 1536], P('shard')
- q_bias_grad: float32 [512], P('shard')
- v_bias_grad: float32 [512], P('shard')
- out_weight_grad: float32 [512, 512], P('shard')
- out_bias_grad: float32 [512], P('shard')
- ln2_gain_grad: float32 [512], P('shard')
- ln2_bias_grad: float32 [512], P('shard')
- up_weight_grad: float32 [512, 2048], P('shard')
- up_bias_grad: float32 [2048], P('shard')
- down_weight_grad: float32 [2048, 512], P('shard')
- down_bias_grad: float32 [512], P('shard')
Inputs may be any that keep to these rules, and one draw needn't show every extreme that they name: Sequence s holds valid characters at slots below lengths[s].
All inputs are finite; a program needn't handle non-finite values.
Results may differ from a plain program's by a relative error of at most 0.01.
Values may be sent and summed in bfloat16 or wider, within the bound.
No kernel may reach another device: no remote copies, remote signals or barrier semaphores. Data moves between devices by JAX's collectives and lax.ppermute only.
A program may use at most 192 MiB of HBM per device.

v0:
```python
import math

import jax
import jax.numpy as jnp
from jax import lax
from jax.sharding import PartitionSpec as P

HEADS = 8


epsilon = 1e-05


def norm_rows(values, gain_vec, shift_vec):
    center = values - jnp.mean(values, axis=-1, keepdims=True)
    spread = jnp.mean(center * center, axis=-1, keepdims=True)
    return center * lax.rsqrt(spread + epsilon) * gain_vec + shift_vec


def masked_scores(query_rows, key_rows, seq_mask, score_scale):
    raw_scores = (
        jnp.einsum("qhd,khd->hqk", query_rows, key_rows, preferred_element_type=jnp.float32)
        * score_scale
    )
    return jnp.where(seq_mask[None, None, :], raw_scores, jnp.float32(-1e30))


def attend_forward(query_all, key_all, value_all, key_mask):
    seq_count, length, heads, head_dim = query_all.shape
    score_scale = 1.0 / math.sqrt(head_dim)
    block_rows = min(512, length)
    seq_out = []
    seq_norm = []
    for row_start in range(0, length, block_rows):
        head_out = []
        head_norm = []
        for head_start in range(0, heads, 2):
            query_rows = query_all[
                0, row_start : row_start + block_rows, head_start : head_start + 2
            ]
            key_rows = key_all[0, :, head_start : head_start + 2]
            value_rows = value_all[0, :, head_start : head_start + 2]
            scores = masked_scores(query_rows, key_rows, key_mask[0], score_scale)
            row_max = jnp.max(scores, axis=-1, keepdims=True)
            expo = jnp.exp(scores - row_max)
            total = jnp.sum(expo, axis=-1, keepdims=True)
            probs_low = (expo / total).astype(jnp.bfloat16)
            head_out.append(
                jnp.einsum(
                    "hqk,khd->qhd", probs_low, value_rows, preferred_element_type=jnp.float32
                )
            )
            head_norm.append(row_max + jnp.log(total))
        seq_out.append(jnp.concatenate(head_out, axis=1))
        seq_norm.append(jnp.concatenate(head_norm, axis=0))
    outputs = [jnp.concatenate(seq_out, axis=0)]
    norms = [jnp.concatenate(seq_norm, axis=1)]
    mixed = jnp.stack(outputs).reshape(seq_count, length, heads * head_dim).astype(jnp.bfloat16)
    return (mixed, jnp.stack(norms))


def attend_backward(query_all, key_all, value_all, key_mask, log_norms, grad_mixed):
    seq_count, length, heads, head_dim = query_all.shape
    score_scale = 1.0 / math.sqrt(head_dim)
    block_rows = min(512, length)
    query_heads = []
    key_heads = []
    value_heads = []
    for head_start in range(0, heads, 2):
        key_rows = key_all[0, :, head_start : head_start + 2]
        value_rows = value_all[0, :, head_start : head_start + 2]
        key_total = jnp.zeros(key_rows.shape, jnp.float32)
        value_total = jnp.zeros(value_rows.shape, jnp.float32)
        query_blocks = []
        for row_start in range(0, length, block_rows):
            query_rows = query_all[
                0, row_start : row_start + block_rows, head_start : head_start + 2
            ]
            grad_rows = grad_mixed[
                0, row_start : row_start + block_rows, head_start : head_start + 2
            ]
            scores = masked_scores(query_rows, key_rows, key_mask[0], score_scale)
            lse_rows = log_norms[0, head_start : head_start + 2, row_start : row_start + block_rows]
            probs = jnp.exp(scores - lse_rows)
            probs_low = probs.astype(jnp.bfloat16)
            value_total = value_total + jnp.einsum(
                "hqk,qhd->khd", probs_low, grad_rows, preferred_element_type=jnp.float32
            )
            grad_probs = jnp.einsum(
                "qhd,khd->hqk", grad_rows, value_rows, preferred_element_type=jnp.float32
            )
            grad_scores = probs * (grad_probs - jnp.sum(grad_probs * probs, axis=-1, keepdims=True))
            grad_low = grad_scores.astype(jnp.bfloat16)
            query_blocks.append(
                jnp.einsum("hqk,khd->qhd", grad_low, key_rows, preferred_element_type=jnp.float32)
                * score_scale
            )
            key_total = (
                key_total
                + jnp.einsum(
                    "hqk,qhd->khd", grad_low, query_rows, preferred_element_type=jnp.float32
                )
                * score_scale
            )
        query_heads.append(jnp.concatenate(query_blocks, axis=0))
        key_heads.append(key_total)
        value_heads.append(value_total)
    query_grads = [jnp.concatenate(query_heads, axis=1)]
    key_grads = [jnp.concatenate(key_heads, axis=1)]
    value_grads = [jnp.concatenate(value_heads, axis=1)]
    shape_rows = (seq_count, length, heads * head_dim)
    return (
        jnp.stack(query_grads).reshape(shape_rows),
        jnp.stack(key_grads).reshape(shape_rows),
        jnp.stack(value_grads).reshape(shape_rows),
    )


def run_forward(tokens, step_embed, key_mask, weights):
    (
        w_ln1_gain,
        w_ln1_bias,
        query_key_value_matrix,
        w_q_bias,
        w_v_bias,
        output_matrix,
        w_out_bias,
        w_ln2_gain,
        w_ln2_bias,
        up_matrix,
        w_up_bias,
        down_matrix,
        w_down_bias,
    ) = weights
    seq_count, length, width = tokens.shape
    head_dim = width // HEADS
    start_x = tokens.astype(jnp.float32) + step_embed.astype(jnp.float32)[:, None, :]
    normed_one = norm_rows(
        start_x, w_ln1_gain.astype(jnp.float32), w_ln1_bias.astype(jnp.float32)
    ).astype(jnp.bfloat16)
    qkv_bias = jnp.concatenate(
        [
            w_q_bias.astype(jnp.float32),
            jnp.zeros((width,), jnp.float32),
            w_v_bias.astype(jnp.float32),
        ]
    )
    qkv_rows = (
        jnp.dot(normed_one, query_key_value_matrix, preferred_element_type=jnp.float32) + qkv_bias
    ).astype(jnp.bfloat16)
    query_all = qkv_rows[..., :width].reshape(seq_count, length, HEADS, head_dim)
    key_all = qkv_rows[..., width : 2 * width].reshape(seq_count, length, HEADS, head_dim)
    value_all = qkv_rows[..., 2 * width :].reshape(seq_count, length, HEADS, head_dim)
    mixed, log_norms = attend_forward(query_all, key_all, value_all, key_mask)
    middle_x = (
        start_x
        + jnp.dot(mixed, output_matrix, preferred_element_type=jnp.float32)
        + w_out_bias.astype(jnp.float32)
    )
    normed_two = norm_rows(
        middle_x, w_ln2_gain.astype(jnp.float32), w_ln2_bias.astype(jnp.float32)
    ).astype(jnp.bfloat16)
    up_rows = jnp.dot(normed_two, up_matrix, preferred_element_type=jnp.float32) + w_up_bias.astype(
        jnp.float32
    )
    act_rows = jax.nn.gelu(up_rows).astype(jnp.bfloat16)
    final_x = (
        middle_x
        + jnp.dot(act_rows, down_matrix, preferred_element_type=jnp.float32)
        + w_down_bias.astype(jnp.float32)
    )
    saved = (
        start_x,
        normed_one,
        query_all,
        key_all,
        value_all,
        mixed,
        log_norms,
        middle_x,
        normed_two,
        up_rows,
        act_rows,
    )
    return (final_x, saved)


def contract_rows(left_operand, right_operand):
    return jnp.einsum(
        "jvc,jva->ca", left_operand, right_operand, preferred_element_type=jnp.float32
    )


def column_sums(values):
    return jnp.sum(values.astype(jnp.float32), axis=(0, 1))


def shards(
    tokens,
    step_embed,
    lengths,
    cotangent,
    ln1_gain,
    ln1_bias,
    qkv_weight,
    q_bias,
    v_bias,
    out_weight,
    out_bias,
    ln2_gain,
    ln2_bias,
    up_weight,
    up_bias,
    down_weight,
    down_bias,
):
    seq_count, length, width = tokens.shape
    gathered = (
        lax.all_gather(ln1_gain, "shard", axis=0, tiled=True),
        lax.all_gather(ln1_bias, "shard", axis=0, tiled=True),
        lax.all_gather(qkv_weight, "shard", axis=0, tiled=True),
        lax.all_gather(q_bias, "shard", axis=0, tiled=True),
        lax.all_gather(v_bias, "shard", axis=0, tiled=True),
        lax.all_gather(out_weight, "shard", axis=0, tiled=True),
        lax.all_gather(out_bias, "shard", axis=0, tiled=True),
        lax.all_gather(ln2_gain, "shard", axis=0, tiled=True),
        lax.all_gather(ln2_bias, "shard", axis=0, tiled=True),
        lax.all_gather(up_weight, "shard", axis=0, tiled=True),
        lax.all_gather(up_bias, "shard", axis=0, tiled=True),
        lax.all_gather(down_weight, "shard", axis=0, tiled=True),
        lax.all_gather(down_bias, "shard", axis=0, tiled=True),
    )
    positions = lax.broadcasted_iota(jnp.int32, (seq_count, length), 1)
    key_mask = positions < lengths[:, None]
    valid = key_mask.astype(jnp.float32)[..., None]
    final_x, saved = run_forward(tokens, step_embed, key_mask, gathered)
    output = (final_x * valid).astype(jnp.bfloat16)
    weights_back = (
        lax.all_gather(ln1_gain, "shard", axis=0, tiled=True),
        lax.all_gather(ln1_bias, "shard", axis=0, tiled=True),
        lax.all_gather(qkv_weight, "shard", axis=0, tiled=True),
        lax.all_gather(q_bias, "shard", axis=0, tiled=True),
        lax.all_gather(v_bias, "shard", axis=0, tiled=True),
        lax.all_gather(out_weight, "shard", axis=0, tiled=True),
        lax.all_gather(out_bias, "shard", axis=0, tiled=True),
        lax.all_gather(ln2_gain, "shard", axis=0, tiled=True),
        lax.all_gather(ln2_bias, "shard", axis=0, tiled=True),
        lax.all_gather(up_weight, "shard", axis=0, tiled=True),
        lax.all_gather(up_bias, "shard", axis=0, tiled=True),
        lax.all_gather(down_weight, "shard", axis=0, tiled=True),
        lax.all_gather(down_bias, "shard", axis=0, tiled=True),
    )
    saved = run_forward(tokens, step_embed, key_mask, weights_back)[1]
    (
        w_ln1_gain,
        w_ln1_bias,
        query_key_value_matrix,
        w_q_bias,
        w_v_bias,
        output_matrix,
        w_out_bias,
        w_ln2_gain,
        w_ln2_bias,
        up_matrix,
        w_up_bias,
        down_matrix,
        w_down_bias,
    ) = weights_back
    (
        start_x,
        normed_one,
        query_all,
        key_all,
        value_all,
        mixed,
        log_norms,
        middle_x,
        normed_two,
        up_rows,
        act_rows,
    ) = saved
    grad_final = cotangent.astype(jnp.float32) * valid
    down_projection_gradient = grad_final.astype(jnp.bfloat16)
    down_weight_part = contract_rows(act_rows, down_projection_gradient)
    down_bias_part = column_sums(down_projection_gradient)
    activation_gradient = jnp.einsum(
        "vwe,pe->vwp", down_projection_gradient, down_matrix, preferred_element_type=jnp.float32
    )
    up_projection_gradient = jax.vjp(jax.nn.gelu, up_rows)[1](activation_gradient)[0].astype(
        jnp.bfloat16
    )
    up_weight_part = contract_rows(normed_two, up_projection_gradient)
    up_bias_part = column_sums(up_projection_gradient)
    second_normed_gradient = jnp.einsum(
        "zgb,jb->zgj", up_projection_gradient, up_matrix, preferred_element_type=jnp.float32
    )
    norm_pull_two = jax.vjp(
        norm_rows, middle_x, w_ln2_gain.astype(jnp.float32), w_ln2_bias.astype(jnp.float32)
    )[1]
    grad_mid_norm, ln2_gain_part, ln2_bias_part = norm_pull_two(second_normed_gradient)
    grad_middle = grad_final + grad_mid_norm
    attention_gradient = grad_middle.astype(jnp.bfloat16)
    out_weight_part = contract_rows(mixed, attention_gradient)
    out_bias_part = column_sums(attention_gradient)
    grad_mixed = jnp.einsum(
        "avu,gu->avg", attention_gradient, output_matrix, preferred_element_type=jnp.float32
    ).astype(jnp.bfloat16)
    grad_mixed = grad_mixed.reshape(seq_count, length, HEADS, width // HEADS)
    query_grad, key_grad, value_grad = attend_backward(
        query_all, key_all, value_all, key_mask, log_norms, grad_mixed
    )
    query_key_value_gradient = jnp.concatenate([query_grad, key_grad, value_grad], axis=-1).astype(
        jnp.bfloat16
    )
    qkv_weight_part = contract_rows(normed_one, query_key_value_gradient)
    q_bias_part = column_sums(query_key_value_gradient[..., :width])
    v_bias_part = column_sums(query_key_value_gradient[..., 2 * width :])
    first_normed_gradient = jnp.einsum(
        "zgb,jb->zgj",
        query_key_value_gradient,
        query_key_value_matrix,
        preferred_element_type=jnp.float32,
    )
    norm_pull_one = jax.vjp(
        norm_rows, start_x, w_ln1_gain.astype(jnp.float32), w_ln1_bias.astype(jnp.float32)
    )[1]
    grad_start_norm, ln1_gain_part, ln1_bias_part = norm_pull_one(first_normed_gradient)
    tokens_grad = grad_middle + grad_start_norm
    (
        s_ln1_gain,
        s_ln1_bias,
        s_qkv,
        s_q_bias,
        s_v_bias,
        s_out,
        s_out_bias,
        s_ln2_gain,
        s_ln2_bias,
        s_up,
        s_up_bias,
        s_down,
        s_down_bias,
    ) = (
        lax.psum_scatter(ln1_gain_part, "shard", scatter_dimension=0, tiled=True),
        lax.psum_scatter(ln1_bias_part, "shard", scatter_dimension=0, tiled=True),
        lax.psum_scatter(qkv_weight_part, "shard", scatter_dimension=0, tiled=True),
        lax.psum_scatter(q_bias_part, "shard", scatter_dimension=0, tiled=True),
        lax.psum_scatter(v_bias_part, "shard", scatter_dimension=0, tiled=True),
        lax.psum_scatter(out_weight_part, "shard", scatter_dimension=0, tiled=True),
        lax.psum_scatter(out_bias_part, "shard", scatter_dimension=0, tiled=True),
        lax.psum_scatter(ln2_gain_part, "shard", scatter_dimension=0, tiled=True),
        lax.psum_scatter(ln2_bias_part, "shard", scatter_dimension=0, tiled=True),
        lax.psum_scatter(up_weight_part, "shard", scatter_dimension=0, tiled=True),
        lax.psum_scatter(up_bias_part, "shard", scatter_dimension=0, tiled=True),
        lax.psum_scatter(down_weight_part, "shard", scatter_dimension=0, tiled=True),
        lax.psum_scatter(down_bias_part, "shard", scatter_dimension=0, tiled=True),
    )
    totals = lax.psum(
        (
            s_ln1_gain,
            s_ln1_bias,
            s_qkv,
            s_q_bias,
            s_v_bias,
            s_out,
            s_out_bias,
            s_ln2_gain,
            s_ln2_bias,
            s_up,
            s_up_bias,
            s_down,
            s_down_bias,
        ),
        "rep",
    )
    return (output, tokens_grad) + tuple(totals)


def solution(mesh):
    in_specs = (
        P(("rep", "shard"), None, None),
        P(("rep", "shard"), None),
        P(("rep", "shard")),
        P(("rep", "shard"), None, None),
        P("shard"),
        P("shard"),
        P("shard", None),
        P("shard"),
        P("shard"),
        P("shard", None),
        P("shard"),
        P("shard"),
        P("shard"),
        P("shard", None),
        P("shard"),
        P("shard", None),
        P("shard"),
    )
    out_specs = (
        P(("rep", "shard"), None, None),
        P(("rep", "shard"), None, None),
        P("shard"),
        P("shard"),
        P("shard", None),
        P("shard"),
        P("shard"),
        P("shard", None),
        P("shard"),
        P("shard"),
        P("shard"),
        P("shard", None),
        P("shard"),
        P("shard", None),
        P("shard"),
    )
    return jax.shard_map(shards, mesh=mesh, in_specs=in_specs, out_specs=out_specs, check_vma=False)
```

profile of v0, /device:TPU:0, one launch (start us, length us, event | category | flops | bytes accessed | tf_op | source)
XLA Modules:
  0.0 461.4 jit_solution(9767171510384160521)
XLA Ops:
  19.6 16.2 %all-reduce.20 = (bf16[512]{0:T(512)(128)(2,1)S(1)}, bf16[512]{0:T(512)(128)(2,1)S(1)}, bf16[512]{0:T(512)(128)(2,1)S(1)}, bf16[512]{0:T(512)(128)(2,1)S(1)}, bf...) all-reduce(bf16[512]{0:T(512)(128)(2,1)S(1)} %dynamic-update-slice., ...), channel_id=1, replica_groups=mesh['rep'=4,'shard'=8] {'shard'}, use_global_device_ids=true, to_apply=%add.3 | all-reduce | flops 4096 | bytes 16384
  36.5 7.7 %all-gather = bf16[8,1,256]{2,1,0:T(2,128)(2,1)S(1)} all-gather(bf16[1,1,256]{2,1,0:T(2,128)(2,1)S(1)} %reshape.578), channel_id=1, replica_groups=mesh['rep'=4,'shard'=8] {'shard'}, dimensions={0}, use_global_device_ids=true | all-gather | bytes 4608 | tf_op jit(solution)/shard_map/all_gather | solution.py:229
  44.3 12.1 %all_gather.56 = bf16[512,512]{1,0:T(8,128)(2,1)} all-gather(bf16[64,512]{1,0:T(8,128)(2,1)} %param.26), channel_id=1, replica_groups=mesh['rep'=4,'shard'=8] {'shard'}, dimensions={0}, use_global_device_ids=true | all-gather | bytes 589824 | tf_op jit(solution)/shard_map/all_gather | solution.py:224
  59.2 4.1 fusion.15
  68.9 3.6 fusion.165
  72.6 3.6 fusion.166
  78.9 3.3 fusion.14
  109.2 8.0 %fusion.157 = f32[1024,2048]{1,0:T(8,128)} fusion(bf16[512,2048]{1,0:T(8,128)(2,1)} %all-gather.7.cloned.1.call-done, f32[1,1024,512]{1,2,0:T(8,128)} %copy-done.21, f32[512]{0:T(512)S(1)} %convert_element_type.229, f32[512]{0:T(512)S(1)} %convert_element_type.228, f32[1024]{0:T(1024)S(1)} %fusion.149, f32[1024]{0:T(1024)S(1)} %broadcast_multiply_fusion), kind=kOutput, calls=%fused_computation.274 | convolution fusion | flops 2150105088 | bytes 12595200 | tf_op jit(solution)/shard_map/dot_general | solution.py:163
  117.2 10.7 %convert_reduce_fusion = (f32[2048]{0:T(1024)S(1)}, bf16[1024,2048]{1,0:T(8,128)(2,1)S(1)}) fusion(f32[1024,2048]{1,0:T(8,128)} %fusion.157, f32[2048]{0:T(1024)S(1)} %bitcast.442, bf16[2048,512]{1,0:T(8,128)(2,1)} %all-gather.9.cloned.1.call-done, f32[1024]{0:T(1024)S(1)} %fusion.150, bf16[1,1024,512]{1,2,0:T(8,128)(2,1)S(1)} %copy.74), kind=kOutput, calls=%fused_computation.9 | convolution fusion | flops 2197288960 | bytes 15749120 | tf_op jit(solution)/shard_map/vwe,pe->vwp/dot_general | solution.py:286
  127.9 3.7 fusion.175
  174.3 3.3 fusion.91
  177.6 3.3 fusion.85
  214.0 3.7 fusion.68
  217.7 9.7 %fusion.131 = f32[2048,512]{1,0:T(8,128)} fusion(bf16[1,1024,512]{1,2,0:T(8,128)(2,1)S(1)} %copy.74, f32[1024]{0:T(1024)S(1)} %fusion.150, f32[1024,2048]{1,0:T(8,128)} %fusion.157, f32[2048]{0:T(1024)S(1)} %bitcast.443), kind=kOutput, calls=%fused_computation.200 | convolution fusion | flops 2170028032 | bytes 13643776 | tf_op jit(solution)/shard_map/jvc,jva->ca/dot_general | solution.py:189
  229.2 6.7 %fusion.155 = f32[512,2048]{1,0:T(8,128)} fusion(bf16[1024,2048]{1,0:T(8,128)(2,1)} %copy-done.66, f32[1,1024,512]{1,2,0:T(8,128)S(1)} %copy-done.23, f32[512]{0:T(512)S(1)} %convert_element_type.229, f32[512]{0:T(512)S(1)} %convert_element_type.228, f32[1024]{0:T(1024)S(1)} %fusion.149, f32[1024]{0:T(1024)S(1)} %broadcast_multiply_fusion), kind=kOutput, calls=%fused_computation.273 | convolution fusion | flops 2150105088 | bytes 10498048 | tf_op jit(solution)/shard_map/jvc,jva->ca/dot_general | solution.py:189
  237.6 9.2 %fusion.46 = bf16[1,1024,512]{1,2,0:T(8,128)(2,1)} fusion(f32[1,1024,512]{1,2,0:T(8,128)S(1)} %copy-done.23, bf16[2048,512]{1,0:T(8,128)(2,1)} %all-gather.9.cloned.1.call-done, f32[1024]{0:T(1024)S(1)} %fusion.150, f32[512]{0:T(512)S(1)} %convert_element_type.233, f32[1024,2048]{1,0:T(8,128)} %fusion.157, f32[2048]{0:T(1024)S(1)} %bitcast.444), kind=kOutput, calls=%fused_computation.101 | convolution fusion | flops 2170552320 | bytes 13645824 | tf_op jit(solution)/shard_map/dot_general | solution.py:169
  246.9 17.1 %reduce-scatter.5.cloned.1.call-done = f32[64,1536]{1,0:T(8,128)} async-done(((f32[512,1536]{1,0:T(8,128)}), f32[64,1536]{1,0:T(8,128)}) %reduce-scatter.5.cloned.1.call-update) | async-done | bytes 393232 | tf_op jit(solution)/shard_map/reduce_scatter | solution.py:346
  264.0 54.9 %reduce-scatter.11.cloned.1.call-done = f32[256,512]{1,0:T(8,128)} async-done(((f32[2048,512]{1,0:T(8,128)}), f32[256,512]{1,0:T(8,128)}) %reduce-scatter.11.cloned.1.call-update) | async-done | bytes 524304 | tf_op jit(solution)/shard_map/reduce_scatter | solution.py:355
  318.9 54.7 %reduce-scatter.9.cloned.1.call-done = f32[64,2048]{1,0:T(8,128)} async-done(((f32[512,2048]{1,0:T(8,128)}), f32[64,2048]{1,0:T(8,128)}) %reduce-scatter.9.cloned.1.call-update) | async-done | bytes 524304 | tf_op jit(solution)/shard_map/reduce_scatter | solution.py:353
  373.7 5.6 %fusion.174 = (f32[512]{0:T(512)S(1)}, f32[1024,512]{1,0:T(8,128)}) fusion(bf16[512,1536]{1,0:T(8,128)(2,1)} %all-gather.5.cloned.1.call-done, bf16[1024,512]{0,1:T(8,128)(2,1)} %bitcast.428, bf16[1024,512]{0,1:T(8,128)(2,1)} %bitcast.430, bf16[1024,512]{0,1:T(8,128)(2,1)} %bitcast.432), kind=kOutput, calls=%fused_computation.287 | convolution fusion | flops 1620573696 | bytes 6817792 | tf_op jit(solution)/shard_map/zgb,jb->zgj/dot_general | solution.py:318
  384.4 24.4 %all-reduce.17 = (f32[512]{0:T(512)S(1)}, f32[512]{0:T(512)S(1)}, f32[512]{0:T(512)S(1)}, f32[512]{0:T(512)S(1)}, f32[512]{0:T(512)S(1)}, /*index=5*/f32[512]{0:...) all-reduce(f32[512]{0:T(512)S(1)} %get-tuple-element.62, ...), channel_id=2, replica_groups=mesh['rep'=4,'shard'=8] {'shard'}, use_global_device_ids=true, to_apply=%region_33.34.clone | all-reduce | flops 6144 | bytes 49152
  409.5 4.3 add_add_fusion.2
  416.7 12.9 %all-reduce.18 = (f32[64]{0:T(128)}, f32[64]{0:T(128)}, f32[64]{0:T(128)}, f32[64]{0:T(128)}, f32[64]{0:T(128)}, /*index=5*/f32[64]{0:T(128)}, f32[64]{0:T(128)}, f32[256]{0:T(256)}, f32[64]{0:T(128)}) all-reduce(f32[64]{0:T(128)S(1)} %dynamic-slice.9, f32[64]{0:T(128)S(1)} %dynamic-slice.11, ...), channel_id=1, replica_groups=mesh['rep'=4,'shard'=8] {'rep'}, use_global_device_ids=true, to_apply=%region_34.35 | all-reduce | flops 768 | bytes 6144 | tf_op jit(solution)/shard_map/psum | solution.py:358
  429.6 17.4 %all-reduce.23.cloned.1.call-done = (f32[64,1536]{1,0:T(8,128)}, f32[64,512]{1,0:T(8,128)}, f32[64,2048]{1,0:T(8,128)}, f32[256,512]{1,0:T(8,128)}) async-done(((f32[64,1536]{1,0:T(8,128)}, f32[64,512]{1,0:T(8,128)}, f32[64,2048]{1,0:T(8,128)}, f32[256,512]{1,0:T(8,128)}), (f32[64,1536]{1,0:T(8,128)}, f32[64,512]{1,0:T(8,128)}, f32[64,2048]{1,0:T(8,128)}, ...) | async-done | bytes 1572880 | tf_op jit(solution)/shard_map/psum | solution.py:358
  (300 shorter events, 142.7 us)
Async XLA Ops:
  7.2 51.4 %copy-start.47 = (bf16[1,1024,512]{2,1,0:T(8,128)(2,1)S(1)}, bf16[1,1024,512]{2,1,0:T(8,128)(2,1)}, u32[]{:S(2)}) copy-start(bf16[1,1024,512]{2,1,0:T(8,128)(2,1)} %param.20) | copy-start | bytes 3145732
  7.2 52.0 %all-gather.5.cloned.1.call-start = ((), (), s32[]{:S(2)}) async-start(), calls=%async_computation.4 | async-start | bytes 1769472 | tf_op jit(solution)/shard_map/all_gather | solution.py:221
  7.9 101.3 %all-gather.7.cloned.1.call-start = ((), (), s32[]{:S(2)}) async-start(), calls=%async_computation.5 | async-start | bytes 2359296 | tf_op jit(solution)/shard_map/all_gather | solution.py:228
  8.7 108.5 %all-gather.9.cloned.1.call-start = ((), (), s32[]{:S(2)}) async-start(), calls=%async_computation.6 | async-start | bytes 2359296 | tf_op jit(solution)/shard_map/all_gather | solution.py:230
  9.4 237.4 %reduce-scatter.7.cloned.1.call-start = ((), (), s32[]{:S(2)}) async-start(), calls=%async_computation.8 | async-start | bytes 1179648 | tf_op jit(solution)/shard_map/reduce_scatter | solution.py:349
  35.8 27.6 %copy-start.60 = (f32[512]{0:T(512)}, f32[512]{0:T(512)S(1)}, u32[]{:S(2)}) copy-start(f32[512]{0:T(512)S(1)} %convert_element_type.211) | copy-start | bytes 6148
  35.8 27.6 %copy-start.62 = (f32[512]{0:T(512)}, f32[512]{0:T(512)S(1)}, u32[]{:S(2)}) copy-start(f32[512]{0:T(512)S(1)} %convert_element_type.212) | copy-start | bytes 6148
  58.1 5.2 %copy-start.54 = (f32[1024]{0:T(1024)}, f32[1024]{0:T(1024)S(1)}, u32[]{:S(2)}) copy-start(f32[1024]{0:T(1024)S(1)} %broadcast_multiply_fusion.1) | copy-start | bytes 12292
  58.6 4.8 %copy-start.58 = (f32[1024]{0:T(1024)}, f32[1024]{0:T(1024)S(1)}, u32[]{:S(2)}) copy-start(f32[1024]{0:T(1024)S(1)} %multiply_reduce_fusion.9) | copy-start | bytes 12292
  58.6 4.8 %copy-start.56 = (f32[1024]{0:T(1024)}, f32[1024]{0:T(1024)S(1)}, u32[]{:S(2)}) copy-start(f32[1024]{0:T(1024)S(1)} %fusion.148) | copy-start | bytes 12292
  59.2 158.6 %copy-start.31 = (bf16[1,1024,512]{1,2,0:T(8,128)(2,1)}, bf16[1,1024,512]{1,2,0:T(8,128)(2,1)S(1)}, u32[]{:S(2)}) copy-start(bf16[1,1024,512]{1,2,0:T(8,128)(2,1)S(1)} %copy.74) | copy-start | bytes 3145732
  117.2 10.7 %copy-start.65 = (bf16[512,2048]{1,0:T(8,128)(2,1)S(1)}, bf16[512,2048]{1,0:T(8,128)(2,1)}, u32[]{:S(2)}) copy-start(bf16[512,2048]{1,0:T(8,128)(2,1)} %all-gather.7.cloned.1.call-done) | copy-start | bytes 6291460
  138.6 5.0 %copy-start.20 = (f32[1,1024,512]{1,2,0:T(8,128)}, f32[1,1024,512]{1,2,0:T(8,128)S(1)}, u32[]{:S(2)}) copy-start(f32[1,1024,512]{1,2,0:T(8,128)S(1)} %get-tuple-element.101) | copy-start | bytes 6291460
  139.2 4.4 copy-start.33
  139.9 29.3 %copy-start.37 = (bf16[1024,512]{0,1:T(8,128)(2,1)}, bf16[1024,512]{0,1:T(8,128)(2,1)S(1)}, u32[]{:S(2)}) copy-start(bf16[1024,512]{0,1:T(8,128)(2,1)S(1)} %convolution_convert_fusion) | copy-start | bytes 3145732
  174.1 89.9 %reduce-scatter.5.cloned.1.call-start = ((), (), s32[]{:S(2)}) async-start(), calls=%async_computation.7 | async-start | bytes 3538944 | tf_op jit(solution)/shard_map/reduce_scatter | solution.py:346
  174.3 6.6 %copy-start.15 = (f32[2,512,1024]{2,1,0:T(8,128)S(1)}, f32[2,512,1024]{2,1,0:T(8,128)}, u32[]{:S(2)}) copy-start(f32[2,512,1024]{2,1,0:T(8,128)} %copy-done.14) | copy-start | bytes 12582916
  174.3 6.6 %copy-start.34 = (bf16[1,1024,512]{1,2,0:T(8,128)(2,1)S(1)}, bf16[1,1024,512]{1,2,0:T(8,128)(2,1)}, u32[]{:S(2)}) copy-start(bf16[1,1024,512]{1,2,0:T(8,128)(2,1)} %copy.70) | copy-start | bytes 3145732
  174.3 6.6 %copy-start.38 = (bf16[1024,512]{0,1:T(8,128)(2,1)S(1)}, bf16[1024,512]{0,1:T(8,128)(2,1)}, u32[]{:S(2)}) copy-start(bf16[1024,512]{0,1:T(8,128)(2,1)} %copy-done.37) | copy-start | bytes 3145732
  186.4 3.9 copy-start.26
  217.7 101.3 %reduce-scatter.11.cloned.1.call-start = ((), (), s32[]{:S(2)}) async-start(), calls=%async_computation.10 | async-start | bytes 4718592 | tf_op jit(solution)/shard_map/reduce_scatter | solution.py:355
  227.5 146.2 %reduce-scatter.9.cloned.1.call-start = ((), (), s32[]{:S(2)}) async-start(), calls=%async_computation.9 | async-start | bytes 4718592 | tf_op jit(solution)/shard_map/reduce_scatter | solution.py:353
  236.0 211.1 %all-reduce.23.cloned.1.call-start = ((), (), s32[]{:S(2)}) async-start(), calls=%async_computation.11 | async-start | bytes 3145728 | tf_op jit(solution)/shard_map/psum | solution.py:358
  373.7 5.6 %copy-start.51 = (bf16[1,1024,512]{1,2,0:T(8,128)(2,1)S(1)}, bf16[1,1024,512]{1,2,0:T(8,128)(2,1)}, u32[]{:S(2)}) copy-start(bf16[1,1024,512]{1,2,0:T(8,128)(2,1)} %fusion.46) | copy-start | bytes 3145732
  (51 other events, 133.5 us)
Sparse Core Ops, SparseCore 0:
  9.9 28.5 all-gather.4
  40.4 29.3 all-gather.6
  71.7 27.8 all-gather.8
  174.2 36.1 reduce-scatter.6
  217.8 46.1 reduce-scatter.4
  267.6 51.3 reduce-scatter.10
  322.3 51.3 reduce-scatter.8
  376.5 70.5 all-reduce.22
where the time goes:
time: 469 us; the launch traced here: 461 us
  waiting for transfers between devices  146 us (31%)
  matrix products  137 us (29%)
  blocking collectives  73.4 us (16%)
  local copies, waits for them, and re-layouts  54.8 us (12%)
  other arithmetic  30.6 us (7%)
  between operations  18.2 us (4%)
    reduce_scatter x1, waiting for transfers between devices, shards(): lax.psum_scatter(down_weight_part, 'shard', scatter_dimension=0, tiled=True)  54.9 us
    reduce_scatter x1, waiting for transfers between devices, shards(): lax.psum_scatter(up_weight_part, 'shard', scatter_dimension=0, tiled=True)  54.7 us
    unnamed x169, local copies, waits for them, and re-layouts  41.4 us
    unnamed x2, blocking collectives  40.7 us
    dot_general x4, matrix products, contract_rows(): jnp.einsum('jvc,jva->ca', left_operand, right_operand, preferred_element_...  21.9 us
    dot_general x8, matrix products, attend_backward(): jnp.einsum('qhd,khd->hqk', grad_rows, value_rows, preferred_element_type=...  21.5 us
    psum x1, waiting for transfers between devices, shards(): lax.psum((s_ln1_gain, s_ln1_bias, s_qkv, s_q_bias, s_v_bias, s_out, s_out...  17.4 us
    reduce_scatter x1, waiting for transfers between devices, shards(): lax.psum_scatter(qkv_weight_part, 'shard', scatter_dimension=0, tiled=True)  17.1 us
  transfers between devices with their start and end apart: 8, of which 4 were waited for; matrix products, arithmetic and copies ran while one was open for 31% of the time, Pallas kernels for 0%

commit v1 on v0

v1 whole, which is shorter than its diff:
```python
import functools, math
import jax, jax.numpy as jnp
from jax import lax
from jax.experimental import pallas as pl
from jax.experimental.pallas import tpu as pltpu

f32 = jnp.float32
bf16 = jnp.bfloat16
EPS = 1e-05
HEADS = 8

def dot(a, b):
    return jnp.dot(a, b, preferred_element_type=f32)

def dot_t(a, b):
    return lax.dot_general(a, b, (((1,), (1,)), ((), ())), preferred_element_type=f32)

def cp(n=1, vmem=100):
    return pltpu.CompilerParams(dimension_semantics=("arbitrary",) * n, vmem_limit_bytes=60 * 1024 * 1024)

def norm(x):
    c = x - jnp.mean(x, axis=-1, keepdims=True)
    r = lax.rsqrt(jnp.mean(c * c, axis=-1, keepdims=True) + EPS)
    return c * r, r

def row(v, i):
    return v[i : i + 1, :].astype(f32)

def front_body(scale, tok, step, vec, w, h1t, kv, qkvt):
    D = tok.shape[-1]
    v = vec[...]
    x = tok[...].astype(f32) + step[...].astype(f32)
    n, _ = norm(x)
    h = (n * row(v, 0) + row(v, 1)).astype(bf16)
    h1t[...] = h.T
    for j in range(3):
        y = dot(h, w[:, j * D : (j + 1) * D])
        if j == 0:
            y = y + row(v, 2)
        if j == 2:
            y = y + row(v, 3)
        y = y.astype(bf16)
        if j == 0:
            y = y * bf16(scale)
        else:
            kv[:, (j - 1) * D : j * D] = y
        qkvt[j * D : (j + 1) * D, :] = y.T

def front(tok, step, vec, w, bm=256):
    T, D = tok.shape
    scale = 1.0 / math.sqrt(D // HEADS)
    full = lambda a: pl.BlockSpec(a.shape, lambda i: (0,) * a.ndim)
    return pl.pallas_call(
        functools.partial(front_body, scale),
        grid=(T // bm,),
        in_specs=[pl.BlockSpec((bm, D), lambda i: (i, 0)), full(step), full(vec), full(w)],
        out_specs=[pl.BlockSpec((D, bm), lambda i: (0, i)), pl.BlockSpec((bm, 2 * D), lambda i: (i, 0)), pl.BlockSpec((3 * D, bm), lambda i: (0, i))],
        out_shape=[jax.ShapeDtypeStruct((D, T), bf16), jax.ShapeDtypeStruct((T, 2 * D), bf16), jax.ShapeDtypeStruct((3 * D, T), bf16)],
        compiler_params=cp(), name="front",
    )(tok, step, vec, w)

def attn_fwd_body(HD, ln, k, qt, vt, et, mixed, mixedt, mixedf, linv):
    T = k.shape[0]
    bi = qt.shape[1]
    n = ln[0]
    q = qt[...]
    rid = lax.broadcasted_iota(jnp.int32, q.shape, 0) // HD
    keep = lax.broadcasted_iota(jnp.int32, (T, bi), 0) < n
    outs = []
    for h in range(2):
        s = dot(k[...], jnp.where(rid == h, q, jnp.zeros_like(q)))
        s = jnp.where(keep, s, f32(-1e30))
        m = jnp.max(s, axis=0, keepdims=True)
        e = jnp.exp(s - m).astype(bf16)
        et[h] = e
        va = jnp.concatenate([vt[h * HD : (h + 1) * HD, :], jnp.ones((16, T), bf16)], axis=0)
        o = dot(va, e)
        inv = 1.0 / o[HD : HD + 1, :]
        linv[h : h + 1, :] = inv
        outs.append(o[:HD, :] * inv)
    mt = jnp.concatenate(outs, axis=0)
    mixedf[...] = mt
    mt = mt.astype(bf16)
    mixedt[...] = mt
    mixed[...] = mt.T

def attn_fwd(ln, kv, qkvt, bi=512):
    T = kv.shape[0]
    D = kv.shape[1] // 2
    HD = D // HEADS
    PW = 2 * HD
    NP = D // PW
    return pl.pallas_call(
        functools.partial(attn_fwd_body, HD),
        grid_spec=pltpu.PrefetchScalarGridSpec(
            num_scalar_prefetch=1, grid=(NP, T // bi),
            in_specs=[pl.BlockSpec((T, PW), lambda p, i, r: (0, p)), pl.BlockSpec((PW, bi), lambda p, i, r: (p, i)), pl.BlockSpec((PW, T), lambda p, i, r: (2 * NP + p, 0))],
            out_specs=[pl.BlockSpec((2, T, bi), lambda p, i, r: (p, 0, i)), pl.BlockSpec((bi, PW), lambda p, i, r: (i, p)), pl.BlockSpec((PW, bi), lambda p, i, r: (p, i)), pl.BlockSpec((PW, bi), lambda p, i, r: (p, i)), pl.BlockSpec((None, 8, bi), lambda p, i, r: (p, 0, i))]),
        out_shape=[jax.ShapeDtypeStruct((HEADS, T, T), bf16), jax.ShapeDtypeStruct((T, D), bf16), jax.ShapeDtypeStruct((D, T), bf16), jax.ShapeDtypeStruct((D, T), f32), jax.ShapeDtypeStruct((NP, 8, T), f32)],
        compiler_params=cp(2), name="attn_fwd",
    )(ln, kv, qkvt, qkvt)

G0 = math.sqrt(2 / math.pi)
def ffn_body(ln, tok, step, vec, upb, cot, mixed, wo, wu, wd, out, act, gup, h2t, gx1, gattn, gdt, gmt, sums, upsum):
    i = pl.program_id(0)
    bm, D = tok.shape
    FF = wu.shape[1]
    v = vec[...]
    x1 = tok[...].astype(f32) + step[...].astype(f32) + dot(mixed[...], wo[...]) + row(v, 4)
    n, r = norm(x1)
    h2 = (n * row(v, 5) + row(v, 6)).astype(bf16)
    h2t[...] = h2.T
    live = (lax.broadcasted_iota(jnp.int32, (bm, 1), 0) + i * bm) < ln[0]
    gd = jnp.where(live, cot[...], jnp.zeros_like(cot))
    gdt[...] = gd.T
    acc = x1 + row(v, 7)
    gh = jnp.zeros((bm, D), f32)
    ch = 512
    @pl.when(i == 0)
    def _():
        sums[...] = jnp.zeros_like(sums)
        upsum[...] = jnp.zeros_like(upsum)
    for c in range(FF // ch):
        sl = slice(c * ch, (c + 1) * ch)
        u = dot(h2, wu[:, sl]) + upb[:, sl].astype(f32)
        u2 = u * u
        t = jnp.tanh(f32(G0) * u * (1.0 + f32(0.044715) * u2))
        half = 0.5 * (1.0 + t)
        a = (u * half).astype(bf16)
        act[:, sl] = a
        dg = half + 0.5 * u * (1.0 - t * t) * (f32(G0) * (1.0 + f32(3 * 0.044715) * u2))
        ga = dot_t(gd, wd[sl, :])
        gu = (ga * dg).astype(bf16)
        gup[:, sl] = gu
        upsum[:, sl] += jnp.sum(gu.astype(f32), axis=0, keepdims=True)
        acc = acc + dot(a, wd[sl, :])
        gh = gh + dot_t(gu, wu[:, sl])
    out[...] = jnp.where(live, acc, 0.0).astype(bf16)
    gn = gh * row(v, 5)
    gx = gd.astype(f32) + r * (gn - jnp.mean(gn, axis=-1, keepdims=True) - n * jnp.mean(gn * n, axis=-1, keepdims=True))
    gx1[...] = gx
    gab = gx.astype(bf16)
    gattn[...] = gab
    gmt[...] = dot_t(gab, wo[...]).astype(bf16).T
    s = lambda a: jnp.sum(a.astype(f32), axis=0, keepdims=True)
    sums[...] += jnp.concatenate([s(gab), s(gh * n), s(gh), s(gd), jnp.zeros((4, D), f32)], axis=0)

def ffn(ln, tok, step, vec, upb, cot, mixed, wo, wu, wd, bm=256):
    T, D = tok.shape
    FF = wu.shape[1]
    full = lambda a: pl.BlockSpec(a.shape, lambda i, r: (0,) * a.ndim)
    rows = lambda w: pl.BlockSpec((bm, w), lambda i, r: (i, 0))
    cols = lambda w: pl.BlockSpec((w, bm), lambda i, r: (0, i))
    S = jax.ShapeDtypeStruct
    return pl.pallas_call(
        ffn_body,
        grid_spec=pltpu.PrefetchScalarGridSpec(
            num_scalar_prefetch=1, grid=(T // bm,),
            in_specs=[rows(D), full(step), full(vec), full(upb), rows(D), rows(D), full(wo), full(wu), full(wd)],
            out_specs=[rows(D), rows(FF), rows(FF), cols(D), rows(D), rows(D), cols(D), cols(D), pl.BlockSpec((8, D), lambda i, r: (0, 0)), pl.BlockSpec((1, FF), lambda i, r: (0, 0))]),
        out_shape=[S((T, D), bf16), S((T, FF), bf16), S((T, FF), bf16), S((D, T), bf16), S((T, D), f32), S((T, D), bf16), S((D, T), bf16), S((D, T), bf16), S((8, D), f32), S((1, FF), f32)],
        compiler_params=cp(), name="ffn",
    )(ln, tok, step, vec, upb, cot, mixed, wo, wu, wd)

def mm_body(a, b, o):
    o[...] = dot(a[...], b[...]).astype(o.dtype)

def mm(a, b, bn=512, name="mm"):
    M, K = a.shape
    N = b.shape[1]
    bn = min(bn, N)
    return pl.pallas_call(
        mm_body, grid=(N // bn,),
        in_specs=[pl.BlockSpec((M, K), lambda j: (0, 0)), pl.BlockSpec((K, bn), lambda j: (0, j))],
        out_specs=pl.BlockSpec((M, bn), lambda j: (0, j)),
        out_shape=jax.ShapeDtypeStruct((M, N), bf16), compiler_params=cp(), name=name)(a, b)

def attn_bwd_body(HD, scale, v, kt, qt, gt, mt, linv, et, gq, gk, gv):
    T = v.shape[0]
    rid = lax.broadcasted_iota(jnp.int32, gt.shape, 0) // HD
    g = gt[...].astype(f32)
    for h in range(2):
        hs = slice(h * HD, (h + 1) * HD)
        inv = linv[h : h + 1, :]
        gs = (g * inv).astype(bf16)
        dl = jnp.sum(gs[hs, :].astype(f32) * mt[hs, :], axis=0, keepdims=True)
        dp = dot(v[...], jnp.where(rid == h, gs, jnp.zeros_like(gs)))
        e = et[h]
        ds = (e.astype(f32) * (dp - dl)).astype(bf16)
        gv[hs, :] = dot_t(gs[hs, :], e).astype(bf16)
        gk[hs, :] = dot_t(qt[hs, :], ds).astype(bf16)
        gq[hs, :] = (dot(kt[hs, :], ds) * scale).astype(bf16)

def attn_bwd(kv, qkvt, gmt, mixedt, linv, et):
    T = kv.shape[0]
    D = kv.shape[1] // 2
    HD = D // HEADS
    PW = 2 * HD
    NP = D // PW
    S = jax.ShapeDtypeStruct
    pr = lambda o: pl.BlockSpec((PW, T), lambda p: (o + p, 0))
    return pl.pallas_call(
        functools.partial(attn_bwd_body, HD, 1.0 / math.sqrt(HD)),
        grid=(NP,),
        in_specs=[pl.BlockSpec((T, PW), lambda p: (0, NP + p)), pr(NP), pr(0), pr(0), pr(0), pl.BlockSpec((None, 8, T), lambda p: (p, 0, 0)), pl.BlockSpec((2, T, T), lambda p: (p, 0, 0))],
        out_specs=[pr(0)] * 3,
        out_shape=[S((D, T), bf16)] * 3,
        compiler_params=cp(), name="attn_bwd",
    )(kv, qkvt, qkvt, gmt, mixedt, linv, et)

def wqkv_body(h1t, g, o):
    o[...] = dot_t(h1t[...], g[...])

def wqkv(h1t, g):
    return pl.pallas_call(wqkv_body, grid=(1,),
        in_specs=[pl.BlockSpec(h1t.shape, lambda i: (0, 0)), pl.BlockSpec(g.shape, lambda i: (0, 0))],
        out_specs=pl.BlockSpec((h1t.shape[0], g.shape[0]), lambda i: (0, 0)),
        out_shape=jax.ShapeDtypeStruct((h1t.shape[0], g.shape[0]), f32), compiler_params=cp(), name="wqkv")(h1t, g)

def back_body(tok, step, vec, w, gq, gk, gv, gx1, tg, sums):
    i = pl.program_id(0)
    D = tok.shape[1]
    v = vec[...]
    x = tok[...].astype(f32) + step[...].astype(f32)
    n, r = norm(x)
    gt = dot(w[:, :D], gq[...]) + dot(w[:, D : 2 * D], gk[...]) + dot(w[:, 2 * D :], gv[...])
    gh = gt.T
    gn = gh * row(v, 0)
    tg[...] = gx1[...] + r * (gn - jnp.mean(gn, axis=-1, keepdims=True) - n * jnp.mean(gn * n, axis=-1, keepdims=True))
    @pl.when(i == 0)
    def _():
        sums[...] = jnp.zeros_like(sums)
    s = lambda a: jnp.sum(a, axis=0, keepdims=True)
    sums[...] += jnp.concatenate([s(gh * n), s(gh), jnp.zeros((6, D), f32)], axis=0)

def back(tok, step, vec, w, gq, gk, gv, gx1, bm=256):
    T, D = tok.shape
    full = lambda a: pl.BlockSpec(a.shape, lambda i: (0,) * a.ndim)
    rows = lambda w: pl.BlockSpec((bm, w), lambda i: (i, 0))
    cols = lambda w: pl.BlockSpec((w, bm), lambda i: (0, i))
    S = jax.ShapeDtypeStruct
    return pl.pallas_call(back_body, grid=(T // bm,),
        in_specs=[rows(D), full(step), full(vec), full(w), cols(D), cols(D), cols(D), rows(D)],
        out_specs=[rows(D), pl.BlockSpec((8, D), lambda i: (0, 0))],
        out_shape=[S((T, D), f32), S((8, D), f32)], compiler_params=cp(), name="back")(tok, step, vec, w, gq, gk, gv, gx1)


def layer(tok, step, lens, cot, vec, upb, w_qkv, wo, wu, wd):
    tok = tok[0]
    cot = cot[0]
    D = tok.shape[1]
    h1t, kv, qkvt = front(tok, step, vec, w_qkv)
    et, mixed, mixedt, mixedf, linv = attn_fwd(lens, kv, qkvt)
    out, act, gup, h2t, gx1, gattn, gdt, gmt, sums2, upsum = ffn(lens, tok, step, vec, upb, cot, mixed, wo, wu, wd)
    gwd = mm(gdt, act, name="wdown").T
    gwu = mm(h2t, gup, name="wup")
    gwo = mm(mixedt, gattn, name="wout")
    gq, gk, gv = attn_bwd(kv, qkvt, gmt, mixedf, linv, et)
    h1a = jnp.concatenate([h1t, jnp.ones((16, h1t.shape[1]), bf16)], axis=0)
    ws = [wqkv(h1a, g) for g in (gq, gk, gv)]
    gwq = jnp.concatenate([w[:D] for w in ws], axis=1).astype(bf16)
    tg, sums1 = back(tok, step, vec, w_qkv, gq, gk, gv, gx1)
    small = jnp.stack([sums1[0], sums1[1], ws[0][D], ws[2][D], sums2[0], sums2[1], sums2[2], sums2[3]])
    return out[None], tg[None], gwq, gwo, gwu, gwd, small, upsum[0]


def shards(tokens, step_embed, lengths, cotangent, ln1_gain, ln1_bias, qkv_weight, q_bias, v_bias, out_weight, out_bias, ln2_gain, ln2_bias, up_weight, up_bias, down_weight, down_bias):
    gather = lambda a, ax=0: lax.all_gather(a, "shard", axis=ax, tiled=True)
    vec = gather(jnp.stack([ln1_gain, ln1_bias, q_bias, v_bias, out_bias, ln2_gain, ln2_bias, down_bias]), 1)
    upb = gather(up_bias[None], 1)
    w_qkv, wo, wu, wd = gather(qkv_weight), gather(out_weight), gather(up_weight), gather(down_weight)
    out, tg, gwq, gwo, gwu, gwd, small, upsum = layer(tokens, step_embed, lengths, cotangent, vec, upb, w_qkv, wo, wu, wd)
    scatter = lambda a, ax=0: lax.psum_scatter(a, "shard", scatter_dimension=ax, tiled=True)
    parts = [scatter(a) for a in (gwq, gwo, gwu, gwd)]
    sq, so, su, sd = [a.astype(f32) for a in lax.psum(tuple(parts), "rep")]
    n = lax.axis_size("shard")
    me = lax.axis_index("shard")
    small = lax.psum(small, ("rep", "shard"))
    upsum = lax.psum(upsum, ("rep", "shard"))
    w = small.shape[1] // n
    small = lax.dynamic_slice(small, (0, me * w), (8, w))
    w = upsum.shape[0] // n
    upsum = lax.dynamic_slice(upsum, (me * w,), (w,))
    return out, tg, small[0], small[1], sq, small[2], small[3], so, small[4], small[5], small[6], su, upsum, sd, small[7]


def solution(mesh):
    from jax.sharding import PartitionSpec as P

    in_specs = (
        P(("rep", "shard"), None, None),
        P(("rep", "shard"), None),
        P(("rep", "shard")),
        P(("rep", "shard"), None, None),
        P("shard"),
        P("shard"),
        P("shard", None),
        P("shard"),
        P("shard"),
        P("shard", None),
        P("shard"),
        P("shard"),
        P("shard"),
        P("shard", None),
        P("shard"),
        P("shard", None),
        P("shard"),
    )
    out_specs = (
        P(("rep", "shard"), None, None),
        P(("rep", "shard"), None, None),
        P("shard"),
        P("shard"),
        P("shard", None),
        P("shard"),
        P("shard"),
        P("shard", None),
        P("shard"),
        P("shard"),
        P("shard"),
        P("shard", None),
        P("shard"),
        P("shard", None),
        P("shard"),
    )
    return jax.shard_map(shards, mesh=mesh, in_specs=in_specs, out_specs=out_specs, check_vma=False)
```

time: 469 us -> 353 us (0.75); the launches traced: 461 us -> 352 us
  matrix products: 137 us -> 0 us
  Pallas kernels: 0 us -> 103 us
  local copies, waits for them, and re-layouts: 54.8 us -> 11 us
  other arithmetic: 30.6 us -> 5.43 us
    dot_general x60 -> x0, matrix products: 137 us -> none  [the longest x4 21.9 us: contract_rows(): jnp.einsum('jvc,jva->ca', left_operand, right_operand, preferred_element_...]
    pallas_call x0 -> x11, Pallas kernels: none -> 103 us  [the longest x1 21.6 us: attn_bwd(): pl.pallas_call(functools.partial(attn_bwd_body, HD, 1.0 / math.sqrt(HD)),...]
    unnamed x2 -> x0, blocking collectives: 40.7 us -> none
    unnamed x169 -> x11, local copies, waits for them, and re-layouts: 41.4 us -> 3.25 us
    psum x1, blocking collectives: 12.9 us -> 40.3 us  [shards(): small = lax.psum(small, ('rep', 'shard'))]
    all_gather x3, waiting for transfers between devices: 0.04 us -> 27.1 us  [shards(): gather = lambda a, ax=0: lax.all_gather(a, 'shard', axis=ax, tiled=True)]
    reduce_sum x18 -> x0, other arithmetic: 18.3 us -> none  [the longest x8 11.2 us: attend_forward(): total = jnp.sum(expo, axis=-1, keepdims=True)]
    psum x1, waiting for transfers between devices: 17.4 us -> 0.01 us  [shards(): sq, so, su, sd = [a.astype(f32) for a in lax.psum(tuple(parts), 'rep')]]
  transfers between devices with their start and end apart: 8 -> 8, of which waited for: 4 -> 4; matrix products, arithmetic and copies ran while one was open for 31% -> 3% of each run, Pallas kernels for 0% -> 22%
where the time goes in v1:
time: 353 us; the launch traced here: 352 us
  waiting for transfers between devices  145 us (41%)
  Pallas kernels  103 us (29%)
  blocking collectives  71.2 us (20%)
  between operations  14.9 us (4%)
  local copies, waits for them, and re-layouts  11 us (3%)
  other arithmetic  5.43 us (2%)
    reduce_scatter x4, waiting for transfers between devices, shards(): lax.psum_scatter(a, 'shard', scatter_dimension=ax, tiled=True)  116 us
    psum x1, blocking collectives, shards(): small = lax.psum(small, ('rep', 'shard'))  40.3 us
    all_gather x3, blocking collectives, shards(): gather = lambda a, ax=0: lax.all_gather(a, 'shard', axis=ax, tiled=True)  30.9 us
    all_gather x3, waiting for transfers between devices, shards(): gather = lambda a, ax=0: lax.all_gather(a, 'shard', axis=ax, tiled=True)  27.1 us
    pallas_call x1, Pallas kernels, attn_bwd(): pl.pallas_call(functools.partial(attn_bwd_body, HD, 1.0 / math.sqrt(HD)),...  21.6 us
    pallas_call x1, Pallas kernels, ffn(): pl.pallas_call(ffn_body, grid_spec=pltpu.PrefetchScalarGridSpec(num_scala...  21.5 us
    pallas_call x1, Pallas kernels, attn_fwd(): pl.pallas_call(functools.partial(attn_fwd_body, HD), grid_spec=pltpu.Pref...  21.2 us
    pallas_call x3, Pallas kernels, mm(): pl.pallas_call(mm_body, grid=(N // bn,), in_specs=[pl.BlockSpec((M, K), l...  15.4 us
  transfers between devices with their start and end apart: 8, of which 4 were waited for; matrix products, arithmetic and copies ran while one was open for 3% of the time, Pallas kernels for 22%

profile of v1, /device:TPU:0, one launch (start us, length us, event | category | flops | bytes accessed | tf_op | source)
XLA Modules:
  0.0 351.7 jit_solution(8676250499698555121)
XLA Ops:
  10.2 10.3 %all-gather.1 = bf16[8,64,8]{1,2,0:T(8,128)(2,1)S(1)} all-gather(bf16[1,64,8]{1,2,0:T(8,128)(2,1)S(1)} %bitcast.47), channel_id=1, replica_groups=mesh['rep'=4,'shard'=8] {'shard'}, dimensions={0}, use_global_device_ids=true | all-gather | bytes 9216 | tf_op jit(solution)/shard_map/all_gather | solution.py:268
  22.6 9.8 %all-gather.2 = bf16[8,1,256]{2,1,0:T(2,128)(2,1)} all-gather(bf16[1,1,256]{2,1,0:T(2,128)(2,1)S(1)} %reshape.33), channel_id=2, replica_groups=mesh['rep'=4,'shard'=8] {'shard'}, dimensions={0}, use_global_device_ids=true | all-gather | bytes 4608 | tf_op jit(solution)/shard_map/all_gather | solution.py:268
  32.4 10.8 %all_gather.21.wo = bf16[512,512]{1,0:T(8,128)(2,1)} all-gather(bf16[64,512]{1,0:T(8,128)(2,1)} %param.26), channel_id=1, replica_groups=mesh['rep'=4,'shard'=8] {'shard'}, dimensions={0}, use_global_device_ids=true | all-gather | bytes 589824 | tf_op jit(solution)/shard_map/all_gather | solution.py:268
  43.1 6.6 %front.1 = (bf16[512,1024]{1,0:T(8,128)(2,1)}, bf16[1024,1024]{1,0:T(8,128)(2,1)}, bf16[1536,1024]{1,0:T(8,128)(2,1)}) custom-call(bf16[1024,512]{1,0:T(8,128)(2,1)} %bitcast.37, bf16[1,512]{1,0:T(2,128)(2,1)} %step.5, bf16[8,512]{1,0:T(8,128)(2,1)} %bitcast.42, bf16[512,1536]{1,0:T(8,128)(2,1)} %all-gather.7.cloned.1.call-done.w), custom_call_target="tpu_custom_call" | custom-call | tf_op jit(solution)/shard_map/front/pallas_call | solution.py:53
  49.8 21.2 %attn_fwd.1 = (bf16[8,1024,1024]{2,1,0:T(8,128)(2,1)}, bf16[1024,512]{1,0:T(8,128)(2,1)}, bf16[512,1024]{1,0:T(8,128)(2,1)}, f32[512,1024]{1,0:T(8,128)}, f32[4,8,1024]{2,1,0:T(8,128)}) custom-call(s32[1]{0:T(128)S(6)} %copy.40.ln, bf16[1024,1024]{1,0:T(8,128)(2,1)} %get-tuple-element.38.k.v, bf16[1536,1024]{1,0:T(8,128)(2,1)} %get-tuple-element.39.qt.vt.kt, ...), custom_call_target="tpu_custom_call" | custom-call | tf_op jit(solution)/shard_map/attn_fwd/pallas_call | solution.py:93
  71.0 27.0 %all-gather.9.cloned.1.call-done.wu = bf16[512,2048]{1,0:T(8,128)(2,1)} async-done(((bf16[64,2048]{1,0:T(8,128)(2,1)}), bf16[512,2048]{1,0:T(8,128)(2,1)}) %all-gather.9.cloned.1.call-update) | async-done | bytes 2097168 | tf_op jit(solution)/shard_map/all_gather | solution.py:268
  98.0 21.5 %ffn.1 = (bf16[1024,512]{1,0:T(8,128)(2,1)}, bf16[1024,2048]{1,0:T(8,128)(2,1)}, bf16[1024,2048]{1,0:T(8,128)(2,1)}, bf16[512,1024]{1,0:T(8,128)(2,1)}, f32[1024...) custom-call(s32[1]{0:T(128)S(6)} %copy.40.ln, ...), custom_call_target="tpu_custom_call" | custom-call | tf_op jit(solution)/shard_map/ffn/pallas_call | solution.py:155
  119.5 3.1 wout.1
  124.0 21.6 %attn_bwd.1 = (bf16[512,1024]{1,0:T(8,128)(2,1)}, bf16[512,1024]{1,0:T(8,128)(2,1)}, bf16[512,1024]{1,0:T(8,128)(2,1)}) custom-call(bf16[1024,1024]{1,0:T(8,128)(2,1)} %get-tuple-element.38.k.v, bf16[1536,1024]{1,0:T(8,128)(2,1)} %get-tuple-element.39.qt.vt.kt, bf16[1536,1024]{1,0:T(8,128)(2,1)} %get-tuple-element.39.qt.vt.kt, ...), custom_call_target="tpu_custom_call" | custom-call | tf_op jit(solution)/shard_map/attn_bwd/pallas_call | solution.py:202
  145.6 3.3 wqkv.3
  148.9 1.3 slice.87
  150.2 3.3 wqkv.4
  153.5 1.3 slice.85
  154.8 3.3 wqkv.5
  160.7 6.1 %wup.1 = bf16[512,2048]{1,0:T(8,128)(2,1)} custom-call(bf16[512,1024]{1,0:T(8,128)(2,1)} %get-tuple-element.56.a, bf16[1024,2048]{1,0:T(8,128)(2,1)} %get-tuple-element.57.b), custom_call_target="tpu_custom_call" | custom-call | tf_op jit(solution)/shard_map/wup/pallas_call | solution.py:172
  166.9 6.2 %wdown.1 = bf16[512,2048]{1,0:T(8,128)(2,1)} custom-call(bf16[512,1024]{1,0:T(8,128)(2,1)} %get-tuple-element.59.a, bf16[1024,2048]{1,0:T(8,128)(2,1)} %get-tuple-element.60.b), custom_call_target="tpu_custom_call" | custom-call | tf_op jit(solution)/shard_map/wdown/pallas_call | solution.py:172
  173.1 26.1 %reduce-scatter.5.cloned.1.call-done = bf16[64,1536]{1,0:T(8,128)(2,1)} async-done(((bf16[512,1536]{1,0:T(8,128)(2,1)}), bf16[64,1536]{1,0:T(8,128)(2,1)}) %reduce-scatter.5.cloned.1.call-update) | async-done | bytes 196624 | tf_op jit(solution)/shard_map/reduce_scatter | solution.py:273
  199.3 44.8 %reduce-scatter.9.cloned.1.call-done = bf16[64,2048]{1,0:T(8,128)(2,1)} async-done(((bf16[512,2048]{1,0:T(8,128)(2,1)}), bf16[64,2048]{1,0:T(8,128)(2,1)}) %reduce-scatter.9.cloned.1.call-update) | async-done | bytes 262160 | tf_op jit(solution)/shard_map/reduce_scatter | solution.py:273
  244.0 45.1 %reduce-scatter.11.cloned.1.call-done = bf16[256,512]{0,1:T(8,128)(2,1)} async-done(((bf16[2048,512]{0,1:T(8,128)(2,1)}), bf16[256,512]{0,1:T(8,128)(2,1)}) %reduce-scatter.11.cloned.1.call-update) | async-done | bytes 262160 | tf_op jit(solution)/shard_map/reduce_scatter | solution.py:273
  289.2 7.2 %back.1 = (f32[1024,512]{1,0:T(8,128)}, f32[8,512]{1,0:T(8,128)}) custom-call(bf16[1024,512]{1,0:T(8,128)(2,1)} %bitcast.39, bf16[1,512]{1,0:T(2,128)(2,1)} %step.5, bf16[8,512]{1,0:T(8,128)(2,1)} %bitcast.44, bf16[512,1536]{1,0:T(8,128)(2,1)} %all-gather.7.cloned.1.call-done.w, bf16[512,1024]{1,0:T(8,128)(2,1)} %get-tuple-element.46.gq.g, ...), custom_call_target="tpu_custom_call" | custom-call | tf_op jit(solution)/shard_map/back/pallas_call | solution.py:242
  297.2 40.3 %all-reduce.1 = (f32[8,512]{1,0:T(8,128)S(1)}, f32[2048]{0:T(1024)S(1)}) all-reduce(f32[8,512]{1,0:T(8,128)S(1)} %pad_maximum_fusion.1, f32[2048]{0:T(1024)S(1)} %bitcast.46), channel_id=1, replica_groups=mesh['rep'=4,'shard'=8] {'rep','shard'}, use_global_device_ids=true, to_apply=%region_0.0 | all-reduce | flops 6144 | bytes 49152 | tf_op jit(solution)/shard_map/psum | solution.py:278
  338.8 1.8 convert_element_type.15
  340.6 1.9 copy.35
  342.5 1.7 convert_element_type.13
  (46 shorter events, 11.1 us)
Async XLA Ops:
  7.2 36.0 %all-gather.7.cloned.1.call-start = ((), (), s32[]{:S(2)}) async-start(), calls=%async_computation.4 | async-start | bytes 1769472 | tf_op jit(solution)/shard_map/all_gather | solution.py:268
  7.9 63.0 %all-gather.11.cloned.1.call-start = ((), (), s32[]{:S(2)}) async-start(), calls=%async_computation.6 | async-start | bytes 2359296 | tf_op jit(solution)/shard_map/all_gather | solution.py:268
  8.7 89.3 %all-gather.9.cloned.1.call-start = ((), (), s32[]{:S(2)}) async-start(), calls=%async_computation.5 | async-start | bytes 2359296 | tf_op jit(solution)/shard_map/all_gather | solution.py:268
  9.4 163.7 %reduce-scatter.7.cloned.1.call-start = ((), (), s32[]{:S(2)}) async-start(), calls=%async_computation.8 | async-start | bytes 589824 | tf_op jit(solution)/shard_map/reduce_scatter | solution.py:273
  119.5 3.4 copy-start
  122.7 76.6 %reduce-scatter.5.cloned.1.call-start = ((), (), s32[]{:S(2)}) async-start(), calls=%async_computation.7 | async-start | bytes 1769472 | tf_op jit(solution)/shard_map/reduce_scatter | solution.py:273
  160.7 83.3 %reduce-scatter.9.cloned.1.call-start = ((), (), s32[]{:S(2)}) async-start(), calls=%async_computation.9 | async-start | bytes 2359296 | tf_op jit(solution)/shard_map/reduce_scatter | solution.py:273
  166.8 122.3 %reduce-scatter.11.cloned.1.call-start = ((), (), s32[]{:S(2)}) async-start(), calls=%async_computation.10 | async-start | bytes 2359296 | tf_op jit(solution)/shard_map/reduce_scatter | solution.py:273
  173.1 165.7 %all-reduce.5.cloned.1.call-start = ((), (), s32[]{:S(2)}) async-start(), calls=%async_computation.11 | async-start | bytes 1572864 | tf_op jit(solution)/shard_map/psum | solution.py:275
  289.2 8.0 %copy-start.3 = (f32[8,512]{1,0:T(8,128)S(1)}, f32[8,512]{1,0:T(8,128)}, u32[]{:S(2)}) copy-start(f32[8,512]{1,0:T(8,128)} %get-tuple-element.53) | copy-start | bytes 49156
  289.2 7.9 %slice-start = ((f32[528,512]{1,0:T(8,128)}), f32[1,512]{1,0:T(1,128)S(1)}, s32[]{:S(2)}) async-start(f32[528,512]{1,0:T(8,128)} %wqkv.3), calls=%async_computation.12 | async-start | bytes 4096 | tf_op jit(solution)/shard_map/slice | solution.py:263
  289.2 7.9 %slice-start.1 = ((f32[528,512]{1,0:T(8,128)}), f32[1,512]{1,0:T(1,128)S(1)}, s32[]{:S(2)}) async-start(f32[528,512]{1,0:T(8,128)} %wqkv.4), calls=%async_computation.13 | async-start | bytes 4096 | tf_op jit(solution)/shard_map/slice | solution.py:263
  289.2 8.0 %copy-start.2 = (f32[1,2048]{1,0:T(1,128)S(1)}, f32[1,2048]{1,0:T(1,128)}, u32[]{:S(2)}) copy-start(f32[1,2048]{1,0:T(1,128)} %get-tuple-element.58) | copy-start | bytes 24580
  338.8 5.4 %copy-start.1 = (bf16[64,512]{1,0:T(8,128)(2,1)S(1)}, bf16[64,512]{1,0:T(8,128)(2,1)}, u32[]{:S(2)}) copy-start(bf16[64,512]{1,0:T(8,128)(2,1)} %get-tuple-element.95) | copy-start | bytes 196612
Sparse Core Ops, SparseCore 0:
  9.9 28.3 all-gather.6
  40.2 27.9 all-gather.10
  70.1 27.8 all-gather.8
  122.8 34.0 reduce-scatter.6
  160.8 38.4 reduce-scatter.4
  202.8 41.2 reduce-scatter.8
  247.9 41.2 reduce-scatter.10
  292.0 44.9 all-reduce.4

commit v2 on v1

v2 whole, which is shorter than its diff:
```python
import functools, math
import jax, jax.numpy as jnp
from jax import lax
from jax.experimental import pallas as pl
from jax.experimental.pallas import tpu as pltpu

f32 = jnp.float32
bf16 = jnp.bfloat16
EPS = 1e-05
HEADS = 8

def dot(a, b):
    return jnp.dot(a, b, preferred_element_type=f32)

def dot_t(a, b):
    return lax.dot_general(a, b, (((1,), (1,)), ((), ())), preferred_element_type=f32)

def cp(n=1, vmem=100):
    return pltpu.CompilerParams(dimension_semantics=("arbitrary",) * n, vmem_limit_bytes=60 * 1024 * 1024)

def norm(x):
    c = x - jnp.mean(x, axis=-1, keepdims=True)
    r = lax.rsqrt(jnp.mean(c * c, axis=-1, keepdims=True) + EPS)
    return c * r, r

def row(v, i):
    return v[i : i + 1, :].astype(f32)


VROWS = 16
LANES = 128


def xor_perm(n, k):
    return [(i, i ^ k) for i in range(n)]


def rep_perm(x, b):
    return lax.ppermute(x, "rep", xor_perm(lax.axis_size("rep"), b))


def swap(x, k):
    return lax.ppermute(x, "shard", xor_perm(lax.axis_size("shard"), k))


def after(x, *deps):
    return lax.optimization_barrier((x,) + deps)[0]


def gather_pieces(x, n, gate=()):
    R = x.shape[0]
    cut = R // 2 // 16 * 16
    bits = [b for b in (2 << i for i in range(16)) if b < n]
    whole = {0: [(0, x)]}
    halves = {}
    ks = sorted((k for k in range(2, n, 2)), key=lambda k: (bin(k).count("1"), k))
    for k in ks:
        if bin(k).count("1") == 1:
            y = swap(x, k)
            y = after(y, *gate) if gate else y
            whole[k] = [(0, y)]
            halves[k] = (y[:cut], y[cut:])
        else:
            low = k & -k
            high = 1 << (k.bit_length() - 1)
            a = swap(halves[k ^ low][0], low)
            b = swap(halves[k ^ high][1], high)
            whole[k] = [(0, a), (cut, b)]
            halves[k] = (a, b)
    out = []
    for k in [0] + ks:
        for r0, a in whole[k]:
            out.append((k, r0, a))
            out.append((k ^ 1, r0, swap(a, 1)))
    return out


def add16(a, b):
    return (a.astype(f32) + b.astype(f32)).astype(bf16)


def pair_sum(keep, send):
    return add16(keep, swap(send, 1))


def fold(s, n, t, reverse):
    m = (n // 2).bit_length() - 1
    h = s.shape[0] // 2
    return add16(s[:h], swap(s[h:], (2 << t) if reverse else (2 << (m - 1 - t))))


def folds(n):
    return range((n // 2).bit_length() - 1)


def rep_sum(x):
    nr = lax.axis_size("rep")
    if nr == 1:
        return x.astype(f32)
    h = x.shape[0] // 2
    odd = lax.axis_index("rep") % 2
    mine = lax.dynamic_slice_in_dim(x, odd * h, h, 0)
    other = lax.dynamic_slice_in_dim(x, (1 - odd) * h, h, 0)
    s = add16(mine, rep_perm(other, 1))
    b = 2
    while b < nr:
        s = add16(s, rep_perm(s, b))
        b *= 2
    o = rep_perm(s, 1)
    lo = jnp.where(odd == 0, s, o)
    hi = jnp.where(odd == 0, o, s)
    return jnp.concatenate([lo, hi], axis=0).astype(f32)


def vector_block(vecs, upb, n):
    me = lax.axis_index("shard")
    lane = lax.broadcasted_iota(jnp.int32, (1, LANES), 1)
    rows = []
    for v in list(vecs) + [upb]:
        w = v.shape[0]
        if w >= LANES:
            rows.append(v.reshape(w // LANES, LANES))
        else:
            t = LANES // w
            rows.append(jnp.where(lane // w == me % t, jnp.tile(v, t)[None], jnp.zeros((1, LANES), bf16)))
    b = jnp.concatenate(rows, axis=0)
    return jnp.pad(b, ((0, VROWS - b.shape[0]), (0, 0)))


def pull(me, refs, meta, segs, sems):
    copies = []
    for ref, (k, r0) in zip(refs, meta):
        s = jnp.bitwise_xor(me, k)
        r1 = r0 + ref.shape[0]
        for a, c, dst, lanes in segs:
            lo, hi = max(a, r0), min(a + c, r1)
            if lo < hi:
                src = ref.at[pl.ds(lo - r0, hi - lo), pl.ds(0, lanes)]
                copies.append(pltpu.make_async_copy(src, dst(s, lo - a, hi - lo), sems.at[len(copies)]))
    return copies


def mult(x, m):
    return pl.multiple_of(x, m)


def front_body(scale, n, meta, me, tok, step, *refs):
    np_ = len(meta)
    pieces = refs[:np_]
    xht, kv, qkvt, w, vec, upb, vbuf, sems = refs[np_:]
    D = tok.shape[-1]
    r = D // n
    FF = upb.shape[1]

    @pl.when(pl.program_id(0) == 0)
    def _():
        seg = lambda j: (j * r, r, lambda s, o, c: w.at[pl.ds(mult(s * r + o, 16), c), pl.ds(j * D, D)], D)
        segs = [seg(j) for j in range(3)] + [(3 * r, VROWS, lambda s, o, c: vbuf.at[s, pl.ds(o, c)], LANES)]
        cs = pull(me[0], pieces, meta, segs, sems)
        for c in cs:
            c.start()
        for c in cs:
            c.wait()
        per = LANES // r
        tiles = [sum(vbuf[s, 0:8, :].astype(f32) for s in range(t * per, (t + 1) * per)) for t in range(D // LANES)]
        vec[...] = jnp.concatenate(tiles, axis=1)
        wu = FF // n
        if wu >= LANES:
            rows = [vbuf[s, 8 + q : 9 + q, :].astype(f32) for s in range(n) for q in range(wu // LANES)]
        else:
            per = LANES // wu
            rows = [sum(vbuf[s, 8:9, :].astype(f32) for s in range(t * per, (t + 1) * per)) for t in range(FF // LANES)]
        upb[...] = jnp.concatenate(rows, axis=1)

    v = vec[...]
    x = tok[...].astype(f32) + step[...].astype(f32)
    nx, _ = norm(x)
    xht[...] = nx.astype(bf16).T
    h = (nx * row(v, 0) + row(v, 1)).astype(bf16)
    for j in range(3):
        y = dot(h, w[:, j * D : (j + 1) * D])
        if j == 0:
            y = y + row(v, 2)
        if j == 2:
            y = y + row(v, 3)
        y = y.astype(bf16)
        if j == 0:
            y = y * bf16(scale)
        else:
            kv[:, (j - 1) * D : j * D] = y
        qkvt[j * D : (j + 1) * D, :] = y.T


S = jax.ShapeDtypeStruct
ANY = pl.BlockSpec(memory_space=pl.ANY)


def cost(flops, nbytes, tr=0):
    return pl.CostEstimate(flops=int(flops), bytes_accessed=int(nbytes), transcendentals=int(tr))


def front(me, tok, step, pieces, n, FF, bm=256):
    T, D = tok.shape
    scale = 1.0 / math.sqrt(D // HEADS)
    meta = tuple((k, r0) for k, r0, _ in pieces)
    keep = lambda *sh: pl.BlockSpec(sh, lambda i, m: (0,) * len(sh))
    return pl.pallas_call(
        functools.partial(front_body, scale, n, meta),
        grid_spec=pltpu.PrefetchScalarGridSpec(
            num_scalar_prefetch=1, grid=(T // bm,),
            in_specs=[pl.BlockSpec((bm, D), lambda i, m: (i, 0)), keep(1, D)] + [ANY] * len(pieces),
            out_specs=[pl.BlockSpec((D, bm), lambda i, m: (0, i)), pl.BlockSpec((bm, 2 * D), lambda i, m: (i, 0)), pl.BlockSpec((3 * D, bm), lambda i, m: (0, i)), keep(D, 3 * D), keep(8, D), keep(1, FF)],
            scratch_shapes=[pltpu.VMEM((n, VROWS, LANES), bf16), pltpu.SemaphoreType.DMA((8 * len(pieces),))]),
        out_shape=[S((D, T), bf16), S((T, 2 * D), bf16), S((3 * D, T), bf16), S((D, 3 * D), bf16), S((8, D), f32), S((1, FF), f32)],
        compiler_params=cp(), name="front", cost_estimate=cost(6 * T * D * D, 10 * T * D * 2),
    )(me, tok, step, *[a for _, _, a in pieces])


def attn_fwd_body(HD, ln, k, qt, vt, *refs):
    et, mixed, mixedt, mixedf, linv = refs[-5:]
    T = k.shape[0]
    bi = qt.shape[1]
    n = ln[0]
    q = qt[...]
    rid = lax.broadcasted_iota(jnp.int32, q.shape, 0) // HD
    keep = lax.broadcasted_iota(jnp.int32, (T, bi), 0) < n
    outs = []
    for h in range(2):
        s = dot(k[...], jnp.where(rid == h, q, jnp.zeros_like(q)))
        s = jnp.where(keep, s, f32(-1e30))
        m = jnp.max(s, axis=0, keepdims=True)
        e = jnp.exp(s - m).astype(bf16)
        et[h] = e
        va = jnp.concatenate([vt[h * HD : (h + 1) * HD, :], jnp.ones((16, T), bf16)], axis=0)
        o = dot(va, e)
        inv = 1.0 / o[HD : HD + 1, :]
        linv[h : h + 1, :] = inv
        outs.append(o[:HD, :] * inv)
    mt = jnp.concatenate(outs, axis=0)
    mixedf[...] = mt
    mt = mt.astype(bf16)
    mixedt[...] = mt
    mixed[...] = mt.T


def attn_fwd(ln, kv, qkvt, p0, cnt, prev, bi=512):
    T = kv.shape[0]
    D = kv.shape[1] // 2
    HD = D // HEADS
    PW = 2 * HD
    NP = D // PW
    prev = list(prev)
    return pl.pallas_call(
        functools.partial(attn_fwd_body, HD),
        grid_spec=pltpu.PrefetchScalarGridSpec(
            num_scalar_prefetch=1, grid=(cnt, T // bi),
            in_specs=[pl.BlockSpec((T, PW), lambda p, i, r: (0, p0 + p)), pl.BlockSpec((PW, bi), lambda p, i, r: (p0 + p, i)), pl.BlockSpec((PW, T), lambda p, i, r: (2 * NP + p0 + p, 0))] + [ANY] * len(prev),
            out_specs=[pl.BlockSpec((2, T, bi), lambda p, i, r: (p0 + p, 0, i)), pl.BlockSpec((bi, PW), lambda p, i, r: (i, p0 + p)), pl.BlockSpec((PW, bi), lambda p, i, r: (p0 + p, i)), pl.BlockSpec((PW, bi), lambda p, i, r: (p0 + p, i)), pl.BlockSpec((None, 8, bi), lambda p, i, r: (p0 + p, 0, i))]),
        out_shape=[S((HEADS, T, T), bf16), S((T, D), bf16), S((D, T), bf16), S((D, T), f32), S((NP, 8, T), f32)],
        input_output_aliases={4 + i: i for i in range(len(prev))},
        compiler_params=cp(2), name="attn_fwd", cost_estimate=cost(cnt * 2 * 8 * T * T * 128, cnt * 2 * T * T * 2, cnt * 2 * T * T),
    )(ln, kv, qkvt, qkvt, *prev)


G0 = math.sqrt(2 / math.pi)


def ffn_body(n, meta, ln, me, tok, step, vec, upb, cot, mixed, *refs):
    np_ = len(meta)
    pieces = refs[:np_]
    out, act, gup, h2t, gx1, gattn, gdt, gmt, sums, upsum, wo, wu, wd, sems = refs[np_:]
    i = pl.program_id(0)
    bm, D = tok.shape
    FF = wu.shape[1]
    r = D // n
    rf = FF // n

    @pl.when(i == 0)
    def _():
        seg = lambda j: (r + j * r, r, lambda s, o, c: wu.at[pl.ds(mult(s * r + o, 16), c), pl.ds(j * D, D)], D)
        segs = [(0, r, lambda s, o, c: wo.at[pl.ds(mult(s * r + o, 16), c)], D)] + [seg(j) for j in range(FF // D)]
        segs += [(r + r * (FF // D), rf, lambda s, o, c: wd.at[pl.ds(mult(s * rf + o, 16), c)], D)]
        cs = pull(me[0], pieces, meta, segs, sems)
        for c in cs:
            c.start()
        for c in cs:
            c.wait()
        sums[...] = jnp.zeros_like(sums)
        upsum[...] = jnp.zeros_like(upsum)

    v = vec[...]
    x1 = tok[...].astype(f32) + step[...].astype(f32) + dot(mixed[...], wo[...]) + row(v, 4)
    nx, rr = norm(x1)
    h2 = (nx * row(v, 5) + row(v, 6)).astype(bf16)
    h2t[...] = h2.T
    live = (lax.broadcasted_iota(jnp.int32, (bm, 1), 0) + i * bm) < ln[0]
    gd = jnp.where(live, cot[...], jnp.zeros_like(cot))
    gdt[...] = gd.T
    acc = x1 + row(v, 7)
    gh = jnp.zeros((bm, D), f32)
    ch = 512
    for c in range(FF // ch):
        sl = slice(c * ch, (c + 1) * ch)
        u = dot(h2, wu[:, sl]) + upb[:, sl]
        u2 = u * u
        t = jnp.tanh(f32(G0) * u * (1.0 + f32(0.044715) * u2))
        half = 0.5 * (1.0 + t)
        a = (u * half).astype(bf16)
        act[:, sl] = a
        dg = half + 0.5 * u * (1.0 - t * t) * (f32(G0) * (1.0 + f32(3 * 0.044715) * u2))
        ga = dot_t(gd, wd[sl, :])
        gu = (ga * dg).astype(bf16)
        gup[:, sl] = gu
        upsum[:, sl] += jnp.sum(gu.astype(f32), axis=0, keepdims=True)
        acc = acc + dot(a, wd[sl, :])
        gh = gh + dot_t(gu, wu[:, sl])
    out[...] = jnp.where(live, acc, 0.0).astype(bf16)
    gn = gh * row(v, 5)
    gx = gd.astype(f32) + rr * (gn - jnp.mean(gn, axis=-1, keepdims=True) - nx * jnp.mean(gn * nx, axis=-1, keepdims=True))
    gx1[...] = gx
    gab = gx.astype(bf16)
    gattn[...] = gab
    gmt[...] = dot_t(gab, wo[...]).astype(bf16).T
    s = lambda a: jnp.sum(a.astype(f32), axis=0, keepdims=True)
    sums[...] += jnp.concatenate([s(gab), s(gh * nx), s(gh), s(gd), jnp.zeros((4, D), f32)], axis=0)


def ffn(ln, me, tok, step, vec, upb, cot, mixed, pieces, n, bm=256):
    T, D = tok.shape
    FF = upb.shape[1]
    meta = tuple((k, r0) for k, r0, _ in pieces)
    full = lambda a: pl.BlockSpec(a.shape, lambda i, l, m: (0,) * a.ndim)
    rows = lambda w: pl.BlockSpec((bm, w), lambda i, l, m: (i, 0))
    cols = lambda w: pl.BlockSpec((w, bm), lambda i, l, m: (0, i))
    return pl.pallas_call(
        functools.partial(ffn_body, n, meta),
        grid_spec=pltpu.PrefetchScalarGridSpec(
            num_scalar_prefetch=2, grid=(T // bm,),
            in_specs=[rows(D), full(step), full(vec), full(upb), rows(D), rows(D)] + [ANY] * len(pieces),
            out_specs=[rows(D), rows(FF), rows(FF), cols(D), rows(D), rows(D), cols(D), cols(D), pl.BlockSpec((8, D), lambda i, l, m: (0, 0)), pl.BlockSpec((1, FF), lambda i, l, m: (0, 0))],
            scratch_shapes=[pltpu.VMEM((D, D), bf16), pltpu.VMEM((D, FF), bf16), pltpu.VMEM((FF, D), bf16), pltpu.SemaphoreType.DMA((8 * len(pieces),))]),
        out_shape=[S((T, D), bf16), S((T, FF), bf16), S((T, FF), bf16), S((D, T), bf16), S((T, D), f32), S((T, D), bf16), S((D, T), bf16), S((D, T), bf16), S((8, D), f32), S((1, FF), f32)],
        compiler_params=cp(), name="ffn", cost_estimate=cost(2 * T * D * (4 * FF + 2 * D), 8 * T * FF, T * FF),
    )(ln, me, tok, step, vec, upb, cot, mixed, *[a for _, _, a in pieces])


def bit_reverse(x, m):
    y = jnp.zeros_like(x)
    for t in range(m):
        y = y | (((x >> t) & 1) << (m - 1 - t))
    return y


def push(me, n, s, reverse, src, keep, send, row0, sem):
    m = (n // 2).bit_length() - 1
    k = jnp.bitwise_xor(me, s)
    p = k >> 1
    if reverse:
        p = bit_reverse(p, m)
    odd = k & 1
    put = lambda dst: pltpu.make_async_copy(src, dst.at[p, pl.ds(row0, src.shape[0])], sem)

    @pl.when(odd == 0)
    def _():
        put(keep).start()

    @pl.when(odd == 1)
    def _():
        put(send).start()


def wdown_body(n, me, gdt, act, ka, sa, dn, sems):
    j = pl.program_id(0)
    rf = act.shape[1] * dn.shape[0] // n
    per = act.shape[1] // rf
    dn[j] = dot(gdt[...], act[...]).astype(bf16).T
    for t in range(per):
        s = j * per + t
        push(me[0], n, s, False, dn.at[j, pl.ds(t * rf, rf)], ka, sa, 0, sems.at[s])

    @pl.when(j == pl.num_programs(0) - 1)
    def _():
        for s in range(n):
            pltpu.make_async_copy(dn.at[0, pl.ds(0, rf)], ka.at[0], sems.at[s]).wait()


def wdown(me, gdt, act, n):
    D, T = gdt.shape
    FF = act.shape[1]
    nc = FF // D
    A = S((n // 2, FF // n, D), bf16)
    return pl.pallas_call(
        functools.partial(wdown_body, n),
        grid_spec=pltpu.PrefetchScalarGridSpec(
            num_scalar_prefetch=1, grid=(nc,),
            in_specs=[pl.BlockSpec((D, T), lambda j, m: (0, 0)), pl.BlockSpec((T, D), lambda j, m: (0, j))],
            out_specs=[ANY] * 2,
            scratch_shapes=[pltpu.VMEM((nc, D, D), bf16), pltpu.SemaphoreType.DMA((n,))]),
        out_shape=[A, A],
        compiler_params=cp(), name="wdown", cost_estimate=cost(2 * T * D * FF, 4 * T * FF),
    )(me, gdt, act)


def wup_body(n, me, h2t, gup, mixedt, gattn, sums, upsum, kb, sb, up, wo, vr, sems):
    j = pl.program_id(0)
    D = h2t.shape[0]
    nc = up.shape[0]
    r = D // n
    i0 = me[0]
    up[j] = dot(h2t[...], gup[...]).astype(bf16)
    for s in range(n):
        push(i0, n, s, True, up.at[j, pl.ds(s * r, r)], kb, sb, mult(j * r, 16), sems.at[j * n + s])

    @pl.when(j == nc - 1)
    def _():
        wo[...] = dot(mixedt[...], gattn[...]).astype(bf16)
        vr[...] = jnp.concatenate([sums[0:4, :]] + [upsum[:, c * D : (c + 1) * D] for c in range(nc)] + [jnp.zeros((VROWS - 4 - nc, D), f32)], axis=0).astype(bf16)
        b = n * nc
        for s in range(n):
            push(i0, n, s, True, wo.at[pl.ds(s * r, r)], kb, sb, nc * r, sems.at[b + s])
            push(i0, n, s, True, vr, kb, sb, (nc + 1) * r, sems.at[b + n + s])
        for s in range(n):
            for c in range(nc):
                pltpu.make_async_copy(up.at[0, pl.ds(0, r)], kb.at[0, pl.ds(0, r)], sems.at[c * n + s]).wait()
            pltpu.make_async_copy(wo.at[pl.ds(0, r)], kb.at[0, pl.ds(0, r)], sems.at[b + s]).wait()
            pltpu.make_async_copy(vr, kb.at[0, pl.ds(0, VROWS)], sems.at[b + n + s]).wait()


def wup(me, h2t, gup, mixedt, gattn, sums, upsum, n):
    D, T = h2t.shape
    FF = gup.shape[1]
    nc = FF // D
    r = D // n
    full = lambda a: pl.BlockSpec(a.shape, lambda j, m: (0,) * a.ndim)
    B = S((n // 2, (nc + 1) * r + VROWS, D), bf16)
    return pl.pallas_call(
        functools.partial(wup_body, n),
        grid_spec=pltpu.PrefetchScalarGridSpec(
            num_scalar_prefetch=1, grid=(nc,),
            in_specs=[full(h2t), pl.BlockSpec((T, D), lambda j, m: (0, j)), full(mixedt), full(gattn), full(sums), full(upsum)],
            out_specs=[ANY] * 2,
            scratch_shapes=[pltpu.VMEM((nc, D, D), bf16), pltpu.VMEM((D, D), bf16), pltpu.VMEM((VROWS, D), bf16), pltpu.SemaphoreType.DMA((n * (nc + 2),))]),
        out_shape=[B, B],
        compiler_params=cp(), name="wup", cost_estimate=cost(2 * T * D * (FF + D), 4 * T * FF),
    )(me, h2t, gup, mixedt, gattn, sums, upsum)


def attn_bwd_body(HD, scale, v, kt, qt, gt, mt, linv, et, *refs):
    gq = refs[-1]
    T = v.shape[0]
    rid = lax.broadcasted_iota(jnp.int32, gt.shape, 0) // HD
    g = gt[...].astype(f32)
    for h in range(2):
        hs = slice(h * HD, (h + 1) * HD)
        inv = linv[h : h + 1, :]
        gs = (g * inv).astype(bf16)
        dl = jnp.sum(gs[hs, :].astype(f32) * mt[hs, :], axis=0, keepdims=True)
        dp = dot(v[...], jnp.where(rid == h, gs, jnp.zeros_like(gs)))
        e = et[h]
        ds = (e.astype(f32) * (dp - dl)).astype(bf16)
        gq[2, hs, :] = dot_t(gs[hs, :], e).astype(bf16)
        gq[1, hs, :] = dot_t(qt[hs, :], ds).astype(bf16)
        gq[0, hs, :] = (dot(kt[hs, :], ds) * scale).astype(bf16)


def attn_bwd(kv, qkvt, gmt, mixedf, linv, et, p0, cnt, prev):
    T = kv.shape[0]
    D = kv.shape[1] // 2
    HD = D // HEADS
    PW = 2 * HD
    NP = D // PW
    prev = list(prev)
    pr = lambda o: pl.BlockSpec((PW, T), lambda p: (o + p0 + p, 0))
    return pl.pallas_call(
        functools.partial(attn_bwd_body, HD, 1.0 / math.sqrt(HD)),
        grid=(cnt,),
        in_specs=[pl.BlockSpec((T, PW), lambda p: (0, NP + p0 + p)), pr(NP), pr(0), pr(0), pr(0), pl.BlockSpec((None, 8, T), lambda p: (p0 + p, 0, 0)), pl.BlockSpec((2, T, T), lambda p: (p0 + p, 0, 0))] + [ANY] * len(prev),
        out_specs=pl.BlockSpec((3, PW, T), lambda p: (0, p0 + p, 0)),
        out_shape=S((3, D, T), bf16),
        input_output_aliases={7: 0} if prev else {},
        compiler_params=cp(), name="attn_bwd", cost_estimate=cost(cnt * 2 * 16 * T * T * 128, cnt * 2 * T * T * 2),
    )(kv, qkvt, qkvt, gmt, mixedf, linv, et, *prev)


def split_rows(n, D):
    R = 3 * (D // n) + VROWS
    return R // 2 // 16 * 16, R


def wqkv_body(n, cut, me, xht, g, ka, sa, kb, sb, res, vr, sems):
    j = pl.program_id(0)
    D = g.shape[0]
    r = D // n
    i0 = me[0]
    x = jnp.concatenate([xht[...], jnp.ones((16, xht.shape[1]), bf16)], axis=0)
    y = dot_t(x, g[...]).astype(bf16)
    res[j] = y[:D]
    vr[...] = jnp.where(lax.broadcasted_iota(jnp.int32, vr.shape, 0) == j, y[D:], jnp.where(j == 0, jnp.zeros_like(y[D:]), vr[...]))

    def parts(jj):
        a, b = jj * r, jj * r + r
        if b <= cut:
            return [(False, 0, r, a)]
        if a >= cut:
            return [(True, 0, r, a - cut)]
        return [(False, 0, cut - a, a), (True, cut - a, b - cut, 0)]

    def dst(rev):
        return (kb, sb) if rev else (ka, sa)

    for jj in range(3):

        @pl.when(j == jj)
        def _():
            for s in range(n):
                for q, (rev, o, c, d) in enumerate(parts(jj)):
                    push(i0, n, s, rev, res.at[jj, pl.ds(s * r + o, c)], *dst(rev), d, sems.at[(jj * n + s) * 2 + q])

    @pl.when(j == 2)
    def _():
        for s in range(n):
            push(i0, n, s, True, vr, kb, sb, 3 * r - cut, sems.at[6 * n + s])
        for s in range(n):
            for jj in range(3):
                for q, (rev, o, c, d) in enumerate(parts(jj)):
                    pltpu.make_async_copy(res.at[0, pl.ds(0, c)], dst(rev)[0].at[0, pl.ds(0, c)], sems.at[(jj * n + s) * 2 + q]).wait()
            pltpu.make_async_copy(vr, kb.at[0, pl.ds(0, VROWS)], sems.at[6 * n + s]).wait()


def wqkv(me, xht, g, n):
    D, T = xht.shape
    cut, R = split_rows(n, D)
    A = S((n // 2, cut, D), bf16)
    B = S((n // 2, R - cut, D), bf16)
    return pl.pallas_call(
        functools.partial(wqkv_body, n, cut),
        grid_spec=pltpu.PrefetchScalarGridSpec(
            num_scalar_prefetch=1, grid=(3,),
            in_specs=[pl.BlockSpec((D, T), lambda j, m: (0, 0)), pl.BlockSpec((None, D, T), lambda j, m: (j, 0, 0))],
            out_specs=[ANY] * 4,
            scratch_shapes=[pltpu.VMEM((3, D, D), bf16), pltpu.VMEM((VROWS, D), bf16), pltpu.SemaphoreType.DMA((7 * n,))]),
        out_shape=[A, A, B, B],
        compiler_params=cp(), name="wqkv", cost_estimate=cost(6 * T * D * D, 10 * T * D),
    )(me, xht, g)


def back_body(tok, step, vec, w, g, gx1, tg):
    D = tok.shape[1]
    x = tok[...].astype(f32) + step[...].astype(f32)
    nx, rr = norm(x)
    gt = dot(w[:, :D], g[0]) + dot(w[:, D : 2 * D], g[1]) + dot(w[:, 2 * D :], g[2])
    gn = gt.T * row(vec[...], 0)
    tg[...] = gx1[...] + rr * (gn - jnp.mean(gn, axis=-1, keepdims=True) - nx * jnp.mean(gn * nx, axis=-1, keepdims=True))


def back(tok, step, vec, w, g, gx1, bm=256):
    T, D = tok.shape
    full = lambda a: pl.BlockSpec(a.shape, lambda i: (0,) * a.ndim)
    rows = pl.BlockSpec((bm, D), lambda i: (i, 0))
    return pl.pallas_call(
        back_body, grid=(T // bm,),
        in_specs=[rows, full(step), full(vec), full(w), pl.BlockSpec((3, D, bm), lambda i: (0, 0, i)), rows],
        out_specs=rows, out_shape=S((T, D), f32), compiler_params=cp(), name="back", cost_estimate=cost(6 * T * D * D, 14 * T * D),
    )(tok, step, vec, w, g, gx1)


def shards(tokens, step_embed, lengths, cotangent, ln1_gain, ln1_bias, qkv_weight, q_bias, v_bias, out_weight, out_bias, ln2_gain, ln2_bias, up_weight, up_bias, down_weight, down_bias):
    n = lax.axis_size("shard")
    me = lax.axis_index("shard").astype(jnp.int32)
    mes = me[None]
    tok, cot, step = tokens[0], cotangent[0], step_embed
    T, D = tok.shape
    r = D // n
    FF = up_bias.shape[0] * n
    nc = FF // D
    vb = vector_block([ln1_gain, ln1_bias, q_bias, v_bias, out_bias, ln2_gain, ln2_bias, down_bias], up_bias, n)
    cols = lambda a: [a[:, j * D : (j + 1) * D] for j in range(a.shape[1] // D)]
    pack1 = jnp.concatenate(cols(qkv_weight) + [jnp.pad(vb, ((0, 0), (0, D - LANES)))], axis=0)
    pack2 = jnp.concatenate([out_weight] + cols(up_weight) + [down_weight], axis=0)
    pieces1 = gather_pieces(pack1, n)
    xht, kv, qkvt, w, vec, upb = front(mes, tok, step, pieces1, n, FF)
    NP = HEADS // 2
    fw = attn_fwd(lengths, kv, qkvt, 0, NP // 2, [])
    pieces2 = gather_pieces(after(pack2, *[a for _, _, a in pieces1[1:]]), n, (fw[4],))
    et, mixed, mixedt, mixedf, linv = attn_fwd(lengths, kv, qkvt, NP // 2, NP // 2, fw)
    out, act, gup, h2t, gx1, gattn, gdt, gmt, sums, upsum = ffn(lengths, mes, tok, step, vec, upb, cot, mixed, pieces2, n)
    ka, sa = wdown(mes, gdt, act, n)
    kb, sb = wup(mes, after(h2t, ka), gup, mixedt, gattn, sums, upsum, n)
    bwd = lambda p, g, *deps: attn_bwd(kv, qkvt, after(gmt, *deps), mixedf, linv, et, p, 1, g)
    fa = pair_sum(ka, sa)
    g = bwd(0, [], kb, fa)
    fb = pair_sum(kb, sb)
    g = bwd(1, [g], fb)
    g = bwd(2, [g])
    steps = list(folds(n))
    fa = fold(fa, n, steps[0], False)
    g = bwd(3, [g], fa)
    fb = fold(fb, n, steps[0], True)
    for t in steps[1:]:
        fa = fold(fa, n, t, False)
    ka, sa, kb, sb = wqkv(mes, after(xht, fb, fa), g, n)
    for t in steps[1:]:
        fb = fold(fb, n, t, True)
    za = rep_sum(fa[0])
    qa = pair_sum(ka, sa)
    qb = pair_sum(kb, sb)
    tg = back(tok, after(step, qa, qb), vec, w, g, gx1)
    for t in steps:
        qa = fold(qa, n, t, False)
        qb = fold(qb, n, t, True)
    zb = rep_sum(fb[0])
    z2 = rep_sum(jnp.concatenate([qa[0], qb[0]], axis=0))
    rf = FF // n
    g_down = za
    z1 = jnp.concatenate([za, zb], axis=0)
    wide = lambda a, c: jnp.concatenate([a[j * r : (j + 1) * r] for j in range(c)], axis=1)
    g_up = wide(z1[rf:], nc)
    g_out = z1[rf + nc * r : rf + (nc + 1) * r]
    small = z1[rf + (nc + 1) * r :]
    own = lambda a: lax.dynamic_slice(a, (me * r,), (r,))
    g_upb = lax.dynamic_slice(small[4 : 4 + nc].reshape(-1), (me * (FF // n),), (FF // n,))
    m = wide(z2, 3)
    sq = z2[3 * r : 3 * r + 3].reshape(1, 3 * D)
    wf = qkv_weight.astype(f32)
    g_qkv = ln1_gain.astype(f32)[:, None] * m + ln1_bias.astype(f32)[:, None] * sq
    g_g1 = jnp.sum(wf * m, axis=1)
    g_b1 = jnp.sum(wf * sq, axis=1)
    return (out[None], tg[None], g_g1, g_b1, g_qkv, own(z2[3 * r]), own(z2[3 * r + 2]), g_out, own(small[0]), own(small[1]), own(small[2]), g_up, g_upb, g_down, own(small[3]))


def solution(mesh):
    from jax.sharding import PartitionSpec as P

    in_specs = (
        P(("rep", "shard"), None, None),
        P(("rep", "shard"), None),
        P(("rep", "shard")),
        P(("rep", "shard"), None, None),
        P("shard"),
        P("shard"),
        P("shard", None),
        P("shard"),
        P("shard"),
        P("shard", None),
        P("shard"),
        P("shard"),
        P("shard"),
        P("shard", None),
        P("shard"),
        P("shard", None),
        P("shard"),
    )
    out_specs = (
        P(("rep", "shard"), None, None),
        P(("rep", "shard"), None, None),
        P("shard"),
        P("shard"),
        P("shard", None),
        P("shard"),
        P("shard"),
        P("shard", None),
        P("shard"),
        P("shard"),
        P("shard"),
        P("shard", None),
        P("shard"),
        P("shard", None),
        P("shard"),
    )
    return jax.shard_map(shards, mesh=mesh, in_specs=in_specs, out_specs=out_specs, check_vma=False)
```

time: 353 us -> 218 us (0.62)
  waiting for transfers between devices: 145 us -> 34.8 us
  blocking collectives: 71.2 us -> 0 us
  starting transfers between devices: 0.5 us -> 38.8 us
  between operations: 14.9 us -> 2.03 us
  Pallas kernels: 103 us -> 115 us
  local copies, waits for them, and re-layouts: 11 us -> 16.2 us
  other arithmetic: 5.43 us -> 10.1 us
    reduce_scatter x4 -> x0, waiting for transfers between devices: 116 us -> none  [shards(): lax.psum_scatter(a, 'shard', scatter_dimension=ax, tiled=True)]
    psum x1 -> x0, blocking collectives: 40.3 us -> none  [shards(): small = lax.psum(small, ('rep', 'shard'))]
    ppermute x0 -> x39, starting transfers between devices: none -> 38.8 us  [the longest x30 24.3 us: swap(): return lax.ppermute(x, 'shard', xor_perm(lax.axis_size('shard'), k))]
    ppermute x0 -> x39, waiting for transfers between devices: none -> 34.8 us  [the longest x30 17.9 us: swap(): return lax.ppermute(x, 'shard', xor_perm(lax.axis_size('shard'), k))]
    all_gather x3 -> x0, blocking collectives: 30.9 us -> none  [shards(): gather = lambda a, ax=0: lax.all_gather(a, 'shard', axis=ax, tiled=True)]
    all_gather x3 -> x0, waiting for transfers between devices: 27.1 us -> none  [shards(): gather = lambda a, ax=0: lax.all_gather(a, 'shard', axis=ax, tiled=True)]
    pallas_call x1 -> x4, Pallas kernels: 21.6 us -> 32.6 us  [attn_bwd(): pl.pallas_call(functools.partial(attn_bwd_body, HD, 1.0 / math.sqrt(HD)),...]
    another operation x1 -> x16, local copies, waits for them, and re-layouts: 0.8 us -> 5.98 us  [vector_block(): jnp.tile(v, t)[None]]
  transfers between devices with their start and end apart: 8 -> 39, of which waited for: 4 -> 13; matrix products, arithmetic and copies ran while one was open for 3% -> 7% of each run, Pallas kernels for 22% -> 40%
where the time goes in v2:
time: 218 us; the launch traced here: 217 us
  Pallas kernels  115 us (53%)
  starting transfers between devices  38.8 us (18%)
  waiting for transfers between devices  34.8 us (16%)
  local copies, waits for them, and re-layouts  16.2 us (7%)
  other arithmetic  10.1 us (5%)
    pallas_call x4, Pallas kernels, attn_bwd(): pl.pallas_call(functools.partial(attn_bwd_body, HD, 1.0 / math.sqrt(HD)),...  32.6 us
    ppermute x30, starting transfers between devices, swap(): return lax.ppermute(x, 'shard', xor_perm(lax.axis_size('shard'), k))  24.3 us
    pallas_call x2, Pallas kernels, attn_fwd(): pl.pallas_call(functools.partial(attn_fwd_body, HD), grid_spec=pltpu.Pref...  23.8 us
    pallas_call x1, Pallas kernels, ffn(): pl.pallas_call(functools.partial(ffn_body, n, meta), grid_spec=pltpu.Pref...  22.4 us
    ppermute x30, waiting for transfers between devices, swap(): return lax.ppermute(x, 'shard', xor_perm(lax.axis_size('shard'), k))  17.9 us
    ppermute x9, waiting for transfers between devices, rep_perm(): return lax.ppermute(x, 'rep', xor_perm(lax.axis_size('rep'), b))  16.9 us
    ppermute x9, starting transfers between devices, rep_perm(): return lax.ppermute(x, 'rep', xor_perm(lax.axis_size('rep'), b))  14.6 us
    pallas_call x1, Pallas kernels, front(): pl.pallas_call(functools.partial(front_body, scale, n, meta), grid_spec=p...  8.75 us
  transfers between devices with their start and end apart: 39, of which 13 were waited for; matrix products, arithmetic and copies ran while one was open for 7% of the time, Pallas kernels for 40%

profile of v2, /device:TPU:0, one launch (start us, length us, event | category | flops | bytes accessed | tf_op | source)
XLA Modules:
  0.0 216.9 jit_solution(6229970062218290054)
XLA Ops:
  8.4 3.0 %collective-permute-start.1 = (bf16[208,512]{1,0:T(8,128)(2,1)S(1)}, bf16[208,512]{1,0:T(8,128)(2,1)S(1)}, u32[]{:S(2)}, u32[]{:S(2)}) collective-permute-start(bf16[208,512]{1,0:T(8,128)(2,1)S(1)} %fusion.5.refs_0_), channel_id=1, source_target_pairs={{0,2},{1,3},{2,0},{3,1},{4,6},{5,7},{6,4},{7,5},{8,10},{9,11},{10,... | collective-permute-start | bytes 638984 | tf_op jit(solution)/shard_map/ppermute | solution.py:43
  27.5 8.8 %front.1 = (bf16[512,1024]{1,0:T(8,128)(2,1)}, bf16[1024,1024]{1,0:T(8,128)(2,1)}, bf16[1536,1024]{1,0:T(8,128)(2,1)}, bf16[512,1536]{1,0:T(8,128)(2,1)}, f32[8,512]{1,0:T(8,128)}, /*index=5*/f32[1,2048]{1,0:T(1,128)}) custom-call(s32[1]{0:T(128)} %bitcast.me, bf16[1024,512]{1,0:T(8,128)(2,1)} %bitcast.36, bf16[1,512]{1,0:T(2,128)(2,1)} %step.4, ...), custom_call_target="tpu_custom_call" | custom-call | flops 1610612736 | bytes 10485760 | tf_op jit(solution)/shard_map/front/pallas_call | solution.py:207
  36.2 11.8 %attn_fwd.2 = (bf16[8,1024,1024]{2,1,0:T(8,128)(2,1)}, bf16[1024,512]{1,0:T(8,128)(2,1)}, bf16[512,1024]{1,0:T(8,128)(2,1)}, f32[512,1024]{1,0:T(8,128)}, f32[4,8,1024]{2,1,0:T(8,128)}) custom-call(s32[1]{0:T(128)S(6)} %copy.54.ln, bf16[1024,1024]{1,0:T(8,128)(2,1)} %get-tuple-element.60.k.v, bf16[1536,1024]{1,0:T(8,128)(2,1)} %get-tuple-element.61.qt.vt.kt, ...), custom_call_target="tpu_custom_call" | custom-call | flops 4294967296 | bytes 8388608 | tf_op jit(solution)/shard_map/attn_fwd/pallas_call | solution.py:253
  50.8 6.0 %collective-permute-done.16.refs_8_ = bf16[288,512]{1,0:T(8,128)(2,1)S(1)} collective-permute-done((bf16[288,512]{1,0:T(8,128)(2,1)S(1)}, bf16[288,512]{1,0:T(8,128)(2,1)S(1)}, u32[]{:S(2)}, u32[]{:S(2)}) %collective-permute-start.16) | collective-permute-done | bytes 294944 | tf_op jit(solution)/shard_map/ppermute | solution.py:43
  58.2 12.0 %attn_fwd.3 = (bf16[8,1024,1024]{2,1,0:T(8,128)(2,1)}, bf16[1024,512]{1,0:T(8,128)(2,1)}, bf16[512,1024]{1,0:T(8,128)(2,1)}, f32[512,1024]{1,0:T(8,128)}, f32[4,8,1024]{2,1,0:T(8,128)}) custom-call(s32[1]{0:T(128)S(6)} %copy.54.ln, ...), custom_call_target="tpu_custom_call", output_to_operand_aliasing={{0}: (4, {}), {1}: (5, {}), {2}: (6, {}), {3}: (7, {}), {4}... | custom-call | flops 4294967296 | bytes 8388608 | tf_op jit(solution)/shard_map/attn_fwd/pallas_call | solution.py:253
  71.2 22.4 %ffn.1 = (bf16[1024,512]{1,0:T(8,128)(2,1)}, bf16[1024,2048]{1,0:T(8,128)(2,1)}, bf16[1024,2048]{1,0:T(8,128)(2,1)}, bf16[512,1024]{1,0:T(8,128)(2,1)}, f32[1024...) custom-call(s32[1]{0:T(128)S(6)} %copy.54.ln, ...), custom_call_target="tpu_custom_call" | custom-call | flops 9663676416 | bytes 16777216 | tf_op jit(solution)/shard_map/ffn/pallas_call | solution.py:335
  93.6 6.3 %wdown.1 = (bf16[4,256,512]{2,1,0:T(8,128)(2,1)}, bf16[4,256,512]{2,1,0:T(8,128)(2,1)}) custom-call(s32[1]{0:T(128)} %bitcast.me, bf16[512,1024]{1,0:T(8,128)(2,1)} %get-tuple-element.74.gdt, bf16[1024,2048]{1,0:T(8,128)(2,1)} %get-tuple-element.75.act), custom_call_target="tpu_custom_call" | custom-call | flops 2147483648 | bytes 8388608 | tf_op jit(solution)/shard_map/wdown/pallas_call | solution.py:392
  100.4 8.1 %wup.1 = (bf16[4,336,512]{2,1,0:T(8,128)(2,1)}, bf16[4,336,512]{2,1,0:T(8,128)(2,1)}) custom-call(s32[1]{0:T(128)} %bitcast.me, bf16[512,1024]{1,0:T(8,128)(2,1)} %get-tuple-element.77.h2t, bf16[1024,2048]{1,0:T(8,128)(2,1)} %get-tuple-element.78.gup, bf16[512,1024]{1,0:T(8,128)(2,1)} %get-tuple-element.79.mixedt, ...), custom_call_target="tpu_custom_call" | custom-call | flops 2684354560 | bytes 8388608 | tf_op jit(solution)/shard_map/wup/pallas_call | solution.py:436
  111.7 8.2 %attn_bwd.4.refs_0_ = bf16[3,512,1024]{2,1,0:T(8,128)(2,1)} custom-call(bf16[1024,1024]{1,0:T(8,128)(2,1)} %get-tuple-element.60.k.v, bf16[1536,1024]{1,0:T(8,128)(2,1)} %get-tuple-element.61.qt.vt.kt, bf16[1536,1024]{1,0:T(8,128)(2,1)} %get-tuple-element.61.qt.vt.kt, bf16[512,1024]{1,0:T(8,128)(2,1)} %get-tuple-element.93.gt, ...), custom_call_target="tpu_custom_call" | custom-call | flops 4294967296 | bytes 4194304 | tf_op jit(solution)/shard_map/attn_bwd/pallas_call | solution.py:474
  123.7 8.1 %attn_bwd.5.refs_0_ = bf16[3,512,1024]{2,1,0:T(8,128)(2,1)} custom-call(bf16[1024,1024]{1,0:T(8,128)(2,1)} %get-tuple-element.60.k.v, bf16[1536,1024]{1,0:T(8,128)(2,1)} %get-tuple-element.61.qt.vt.kt, bf16[1536,1024]{1,0:T(8,128)(2,1)} %get-tuple-element.61.qt.vt.kt, bf16[512,1024]{1,0:T(8,128)(2,1)} %get-tuple-element.93.gt, ...), custom_call_target="tpu_custom_call", output_to_operand_aliasing={{}: (7, {})} | custom-call | flops 4294967296 | bytes 4194304 | tf_op jit(solution)/shard_map/attn_bwd/pallas_call | solution.py:474
  134.0 8.1 %attn_bwd.6.refs_0_ = bf16[3,512,1024]{2,1,0:T(8,128)(2,1)} custom-call(bf16[1024,1024]{1,0:T(8,128)(2,1)} %get-tuple-element.60.k.v, bf16[1536,1024]{1,0:T(8,128)(2,1)} %get-tuple-element.61.qt.vt.kt, bf16[1536,1024]{1,0:T(8,128)(2,1)} %get-tuple-element.61.qt.vt.kt, bf16[512,1024]{1,0:T(8,128)(2,1)} %get-tuple-element.93.gt, ...), custom_call_target="tpu_custom_call", output_to_operand_aliasing={{}: (7, {})} | custom-call | flops 4294967296 | bytes 4194304 | tf_op jit(solution)/shard_map/attn_bwd/pallas_call | solution.py:474
  142.1 3.6 %collective-permute-done.22 = bf16[1,256,512]{2,1,0:T(8,128)(2,1)S(1)} collective-permute-done((bf16[1,256,512]{2,1,0:T(8,128)(2,1)S(1)}, bf16[1,256,512]{2,1,0:T(8,128)(2,1)S(1)}, u32[]{:S(2)}, u32[]{:S(2)}) %collective-permute-start.22) | collective-permute-done | bytes 262176 | tf_op jit(solution)/shard_map/ppermute | solution.py:43
  147.7 8.1 %attn_bwd.7.g = bf16[3,512,1024]{2,1,0:T(8,128)(2,1)} custom-call(bf16[1024,1024]{1,0:T(8,128)(2,1)} %get-tuple-element.60.k.v, bf16[1536,1024]{1,0:T(8,128)(2,1)} %get-tuple-element.61.qt.vt.kt, bf16[1536,1024]{1,0:T(8,128)(2,1)} %get-tuple-element.61.qt.vt.kt, bf16[512,1024]{1,0:T(8,128)(2,1)} %get-tuple-element.93.gt, ...), custom_call_target="tpu_custom_call", output_to_operand_aliasing={{}: (7, {})} | custom-call | flops 4294967296 | bytes 4194304 | tf_op jit(solution)/shard_map/attn_bwd/pallas_call | solution.py:474
  155.9 2.7 %collective-permute-start.37 = (bf16[128,512]{1,0:T(8,128)(2,1)S(1)}, bf16[128,512]{1,0:T(8,128)(2,1)S(1)}, u32[]{:S(2)}, u32[]{:S(2)}) collective-permute-start(bf16[128,512]{1,0:T(8,128)(2,1)S(1)} %fusion.4), channel_id=1, source_target_pairs={{0,16},{8,24},{16,0},{24,8},{1,17},{9,25},{17,1},{25,9},{2,18},{10... | collective-permute-start | bytes 393224 | tf_op jit(solution)/shard_map/ppermute | solution.py:39
  160.4 3.4 %collective-permute-done.37 = bf16[128,512]{1,0:T(8,128)(2,1)S(1)} collective-permute-done((bf16[128,512]{1,0:T(8,128)(2,1)S(1)}, bf16[128,512]{1,0:T(8,128)(2,1)S(1)}, u32[]{:S(2)}, u32[]{:S(2)}) %collective-permute-start.37) | collective-permute-done | bytes 131104 | tf_op jit(solution)/shard_map/ppermute | solution.py:39
  163.9 5.9 %wqkv.1 = (bf16[4,96,512]{2,1,0:T(8,128)(2,1)}, bf16[4,96,512]{2,1,0:T(8,128)(2,1)}, bf16[4,112,512]{2,1,0:T(8,128)(2,1)}, bf16[4,112,512]{2,1,0:T(8,128)(2,1)}) custom-call(s32[1]{0:T(128)} %bitcast.me, bf16[512,1024]{1,0:T(8,128)(2,1)} %get-tuple-element.86.xht, bf16[3,512,1024]{2,1,0:T(8,128)(2,1)} %attn_bwd.7.g), custom_call_target="tpu_custom_call" | custom-call | flops 1610612736 | bytes 5242880 | tf_op jit(solution)/shard_map/wqkv/pallas_call | solution.py:535
  171.4 2.1 collective-permute-start.33
  176.0 7.1 %back.1 = f32[1024,512]{1,0:T(8,128)} custom-call(bf16[1024,512]{1,0:T(8,128)(2,1)} %bitcast.38, bf16[1,512]{1,0:T(2,128)(2,1)} %step.4, f32[8,512]{1,0:T(8,128)} %get-tuple-element.58.vec, bf16[512,1536]{1,0:T(8,128)(2,1)} %get-tuple-element.99.w, bf16[3,512,1024]{2,1,0:T(8,128)(2,1)} %attn_bwd.7.g, f32[1024,512]{1,0:T(8,128)} %get-tuple-element.100.gx1), custom_call_target="tpu_custom_call" | custom-call | flops 1610612736 | bytes 7340032 | tf_op jit(solution)/shard_map/back/pallas_call | solution.py:560
  186.5 6.9 %collective-permute-done.34 = bf16[168,512]{1,0:T(8,128)(2,1)S(1)} collective-permute-done((bf16[168,512]{1,0:T(8,128)(2,1)S(1)}, bf16[168,512]{1,0:T(8,128)(2,1)S(1)}, u32[]{:S(2)}, u32[]{:S(2)}) %collective-permute-start.34) | collective-permute-done | bytes 172064 | tf_op jit(solution)/shard_map/ppermute | solution.py:39
  194.8 3.8 %collective-permute-done.28 = bf16[1,112,512]{2,1,0:T(8,128)(2,1)S(1)} collective-permute-done((bf16[1,112,512]{2,1,0:T(8,128)(2,1)S(1)}, bf16[1,112,512]{2,1,0:T(8,128)(2,1)S(1)}, u32[]{:S(2)}, u32[]{:S(2)}) %collective-permute-start.28) | collective-permute-done | bytes 114720 | tf_op jit(solution)/shard_map/ppermute | solution.py:43
  198.7 1.9 collective-permute-start.29
  203.6 3.0 %collective-permute-start.30 = (bf16[104,512]{1,0:T(8,128)(2,1)S(1)}, bf16[104,512]{1,0:T(8,128)(2,1)S(1)}, u32[]{:S(2)}, u32[]{:S(2)}) collective-permute-start(bf16[104,512]{1,0:T(8,128)(2,1)S(1)} %add_convert_fusion.14), channel_id=1, source_target_pairs={{0,16},{8,24},{16,0},{24,8},{1,17},{9,25},{17,1},{25,9},{2,18},{10... | collective-permute-start | bytes 319496 | tf_op jit(solution)/shard_map/ppermute | solution.py:39
  207.3 2.6 %collective-permute-done.30 = bf16[104,512]{1,0:T(8,128)(2,1)S(1)} collective-permute-done((bf16[104,512]{1,0:T(8,128)(2,1)S(1)}, bf16[104,512]{1,0:T(8,128)(2,1)S(1)}, u32[]{:S(2)}, u32[]{:S(2)}) %collective-permute-start.30) | collective-permute-done | bytes 106528 | tf_op jit(solution)/shard_map/ppermute | solution.py:39
  211.8 2.8 %collective-permute-done.31 = bf16[104,512]{1,0:T(8,128)(2,1)S(1)} collective-permute-done((bf16[104,512]{1,0:T(8,128)(2,1)S(1)}, bf16[104,512]{1,0:T(8,128)(2,1)S(1)}, u32[]{:S(2)}, u32[]{:S(2)}) %collective-permute-start.31) | collective-permute-done | bytes 106528 | tf_op jit(solution)/shard_map/ppermute | solution.py:39
  (197 shorter events, 58.1 us)
Async XLA Ops:
  8.4 8.3 %collective-permute-start.1 = (bf16[208,512]{1,0:T(8,128)(2,1)S(1)}, bf16[208,512]{1,0:T(8,128)(2,1)S(1)}, u32[]{:S(2)}, u32[]{:S(2)}) collective-permute-start(bf16[208,512]{1,0:T(8,128)(2,1)S(1)} %fusion.5.refs_0_), channel_id=1, source_target_pairs={{0,2},{1,3},{2,0},{3,1},{4,6},{5,7},{6,4},{7,5},{8,10},{9,11},{10,... | collective-permute-start | bytes 638984 | tf_op jit(solution)/shard_map/ppermute | solution.py:43
  12.9 10.8 %collective-permute-start = (bf16[208,512]{1,0:T(8,128)(2,1)S(1)}, bf16[208,512]{1,0:T(8,128)(2,1)S(1)}, u32[]{:S(2)}, u32[]{:S(2)}) collective-permute-start(bf16[208,512]{1,0:T(8,128)(2,1)S(1)} %fusion.5.refs_0_), channel_id=1, source_target_pairs={{0,1},{1,0},{2,3},{3,2},{4,5},{5,4},{6,7},{7,6},{8,9},{9,8},{10,11... | collective-permute-start | bytes 638984 | tf_op jit(solution)/shard_map/ppermute | solution.py:43
  24.7 23.3 %collective-permute-start.10 = (bf16[576,512]{1,0:T(8,128)(2,1)S(1)}, bf16[576,512]{1,0:T(8,128)(2,1)S(1)}, u32[]{:S(2)}, u32[]{:S(2)}) collective-permute-start(bf16[576,512]{1,0:T(8,128)(2,1)S(1)} %constant_dynamic-update-slice_fusion.refs_0_), channel_id=1, source_target_pairs={{0,2},{1,3},{2,0},{3,1},{4,6},{5,7},{6,4},{7,5},{8,10},{9,11},{10,... | collective-permute-start | bytes 1769480 | tf_op jit(solution)/shard_map/ppermute | solution.py:43
  26.2 21.8 %collective-permute-start.12 = (bf16[576,512]{1,0:T(8,128)(2,1)S(1)}, bf16[576,512]{1,0:T(8,128)(2,1)S(1)}, u32[]{:S(2)}, u32[]{:S(2)}) collective-permute-start(bf16[576,512]{1,0:T(8,128)(2,1)S(1)} %constant_dynamic-update-slice_fusion.refs_0_), channel_id=1, source_target_pairs={{0,4},{1,5},{2,6},{3,7},{4,0},{5,1},{6,2},{7,3},{8,12},{9,13},{10,... | collective-permute-start | bytes 1769480 | tf_op jit(solution)/shard_map/ppermute | solution.py:43
  48.1 8.7 %collective-permute-start.16 = (bf16[288,512]{1,0:T(8,128)(2,1)S(1)}, bf16[288,512]{1,0:T(8,128)(2,1)S(1)}, u32[]{:S(2)}, u32[]{:S(2)}) collective-permute-start(bf16[288,512]{1,0:T(8,128)(2,1)S(1)} %slice.145), channel_id=1, source_target_pairs={{0,4},{1,5},{2,6},{3,7},{4,0},{5,1},{6,2},{7,3},{8,12},{9,13},{10,... | collective-permute-start | bytes 884744 | tf_op jit(solution)/shard_map/ppermute | solution.py:43
  49.7 8.5 %collective-permute-start.14 = (bf16[288,512]{1,0:T(8,128)(2,1)S(1)}, bf16[288,512]{1,0:T(8,128)(2,1)S(1)}, u32[]{:S(2)}, u32[]{:S(2)}) collective-permute-start(bf16[288,512]{1,0:T(8,128)(2,1)S(1)} %slice.144), channel_id=1, source_target_pairs={{0,2},{1,3},{2,0},{3,1},{4,6},{5,7},{6,4},{7,5},{8,10},{9,11},{10,... | collective-permute-start | bytes 884744 | tf_op jit(solution)/shard_map/ppermute | solution.py:43
  50.3 19.9 %collective-permute-start.9 = (bf16[576,512]{1,0:T(8,128)(2,1)S(1)}, bf16[576,512]{1,0:T(8,128)(2,1)S(1)}, u32[]{:S(2)}, u32[]{:S(2)}) collective-permute-start(bf16[576,512]{1,0:T(8,128)(2,1)S(1)} %constant_dynamic-update-slice_fusion.refs_0_), channel_id=1, source_target_pairs={{0,1},{1,0},{2,3},{3,2},{4,5},{5,4},{6,7},{7,6},{8,9},{9,8},{10,11... | collective-permute-start | bytes 1769480 | tf_op jit(solution)/shard_map/ppermute | solution.py:43
  50.3 19.9 %collective-permute-start.11 = (bf16[576,512]{1,0:T(8,128)(2,1)S(1)}, bf16[576,512]{1,0:T(8,128)(2,1)S(1)}, u32[]{:S(2)}, u32[]{:S(2)}) collective-permute-start(bf16[576,512]{1,0:T(8,128)(2,1)S(1)} %collective-permute-done.10.refs_2_), channel_id=1, source_target_pairs={{0,1},{1,0},{2,3},{3,2},{4,5},{5,4},{6,7},{7,6},{8,9},{9,8},{10,11... | collective-permute-start | bytes 1769480 | tf_op jit(solution)/shard_map/ppermute | solution.py:43
  50.8 19.4 %collective-permute-start.13 = (bf16[576,512]{1,0:T(8,128)(2,1)S(1)}, bf16[576,512]{1,0:T(8,128)(2,1)}, u32[]{:S(2)}, u32[]{:S(2)}) collective-permute-start(bf16[576,512]{1,0:T(8,128)(2,1)S(1)} %collective-permute-done.12.refs_4_), channel_id=1, source_target_pairs={{0,1},{1,0},{2,3},{3,2},{4,5},{5,4},{6,7},{7,6},{8,9},{9,8},{10,11... | collective-permute-start | bytes 1769480 | tf_op jit(solution)/shard_map/ppermute | solution.py:43
  56.8 13.4 %collective-permute-start.17 = (bf16[288,512]{1,0:T(8,128)(2,1)S(1)}, bf16[288,512]{1,0:T(8,128)(2,1)}, u32[]{:S(2)}, u32[]{:S(2)}) collective-permute-start(bf16[288,512]{1,0:T(8,128)(2,1)S(1)} %collective-permute-done.16.refs_8_), channel_id=1, source_target_pairs={{0,1},{1,0},{2,3},{3,2},{4,5},{5,4},{6,7},{7,6},{8,9},{9,8},{10,11... | collective-permute-start | bytes 884744 | tf_op jit(solution)/shard_map/ppermute | solution.py:43
  58.2 12.1 %collective-permute-start.15 = (bf16[288,512]{1,0:T(8,128)(2,1)S(1)}, bf16[288,512]{1,0:T(8,128)(2,1)}, u32[]{:S(2)}, u32[]{:S(2)}) collective-permute-start(bf16[288,512]{1,0:T(8,128)(2,1)S(1)} %collective-permute-done.14.refs_6_), channel_id=1, source_target_pairs={{0,1},{1,0},{2,3},{3,2},{4,5},{5,4},{6,7},{7,6},{8,9},{9,8},{10,11... | collective-permute-start | bytes 884744 | tf_op jit(solution)/shard_map/ppermute | solution.py:43
  100.0 8.8 %collective-permute-start.20 = (bf16[4,256,512]{2,1,0:T(8,128)(2,1)}, bf16[4,256,512]{2,1,0:T(8,128)(2,1)}, u32[]{:S(2)}, u32[]{:S(2)}) collective-permute-start(bf16[4,256,512]{2,1,0:T(8,128)(2,1)} %get-tuple-element.85), channel_id=1, source_target_pairs={{0,1},{1,0},{2,3},{3,2},{4,5},{5,4},{6,7},{7,6},{8,9},{9,8},{10,11... | collective-permute-start | bytes 3145736 | tf_op jit(solution)/shard_map/ppermute | solution.py:43
  108.6 11.4 %collective-permute-start.18 = (bf16[4,336,512]{2,1,0:T(8,128)(2,1)}, bf16[4,336,512]{2,1,0:T(8,128)(2,1)}, u32[]{:S(2)}, u32[]{:S(2)}) collective-permute-start(bf16[4,336,512]{2,1,0:T(8,128)(2,1)} %get-tuple-element.84), channel_id=1, source_target_pairs={{0,1},{1,0},{2,3},{3,2},{4,5},{5,4},{6,7},{7,6},{8,9},{9,8},{10,11... | collective-permute-start | bytes 4128776 | tf_op jit(solution)/shard_map/ppermute | solution.py:43
  111.2 20.6 %collective-permute-start.21 = (bf16[2,256,512]{2,1,0:T(8,128)(2,1)}, bf16[2,256,512]{2,1,0:T(8,128)(2,1)}, u32[]{:S(2)}, u32[]{:S(2)}) collective-permute-start(bf16[2,256,512]{2,1,0:T(8,128)(2,1)} %slice.183), channel_id=1, source_target_pairs={{0,4},{1,5},{2,6},{3,7},{4,0},{5,1},{6,2},{7,3},{8,12},{9,13},{10,... | collective-permute-start | bytes 1572872 | tf_op jit(solution)/shard_map/ppermute | solution.py:43
  122.6 36.0 %collective-permute-start.19 = (bf16[2,336,512]{2,1,0:T(8,128)(2,1)}, bf16[2,336,512]{2,1,0:T(8,128)(2,1)S(1)}, u32[]{:S(2)}, u32[]{:S(2)}) collective-permute-start(bf16[2,336,512]{2,1,0:T(8,128)(2,1)} %slice.181), channel_id=1, source_target_pairs={{0,2},{1,3},{2,0},{3,1},{4,6},{5,7},{6,4},{7,5},{8,10},{9,11},{10,... | collective-permute-start | bytes 2064392 | tf_op jit(solution)/shard_map/ppermute | solution.py:43
  133.0 12.7 %collective-permute-start.22 = (bf16[1,256,512]{2,1,0:T(8,128)(2,1)S(1)}, bf16[1,256,512]{2,1,0:T(8,128)(2,1)S(1)}, u32[]{:S(2)}, u32[]{:S(2)}) collective-permute-start(bf16[1,256,512]{2,1,0:T(8,128)(2,1)S(1)} %slice.185), channel_id=1, source_target_pairs={{0,2},{1,3},{2,0},{3,1},{4,6},{5,7},{6,4},{7,5},{8,10},{9,11},{10,... | collective-permute-start | bytes 786440 | tf_op jit(solution)/shard_map/ppermute | solution.py:43
  145.8 10.0 %collective-permute-start.36 = (bf16[128,512]{1,0:T(8,128)(2,1)S(1)}, bf16[128,512]{1,0:T(8,128)(2,1)S(1)}, u32[]{:S(2)}, u32[]{:S(2)}) collective-permute-start(bf16[128,512]{1,0:T(8,128)(2,1)S(1)} %dynamic-slice_bitcast_fusion.1), channel_id=1, source_target_pairs={{0,8},{8,0},{16,24},{24,16},{1,9},{9,1},{17,25},{25,17},{2,10},{10... | collective-permute-start | bytes 393224 | tf_op jit(solution)/shard_map/ppermute | solution.py:39
  155.9 7.9 %collective-permute-start.37 = (bf16[128,512]{1,0:T(8,128)(2,1)S(1)}, bf16[128,512]{1,0:T(8,128)(2,1)S(1)}, u32[]{:S(2)}, u32[]{:S(2)}) collective-permute-start(bf16[128,512]{1,0:T(8,128)(2,1)S(1)} %fusion.4), channel_id=1, source_target_pairs={{0,16},{8,24},{16,0},{24,8},{1,17},{9,25},{17,1},{25,9},{2,18},{10... | collective-permute-start | bytes 393224 | tf_op jit(solution)/shard_map/ppermute | solution.py:39
  158.8 12.5 %collective-permute-start.32 = (bf16[1,336,512]{2,1,0:T(8,128)(2,1)S(1)}, bf16[1,336,512]{2,1,0:T(8,128)(2,1)S(1)}, u32[]{:S(2)}, u32[]{:S(2)}) collective-permute-start(bf16[1,336,512]{2,1,0:T(8,128)(2,1)S(1)} %slice.198), channel_id=1, source_target_pairs={{0,4},{1,5},{2,6},{3,7},{4,0},{5,1},{6,2},{7,3},{8,12},{9,13},{10,... | collective-permute-start | bytes 1032200 | tf_op jit(solution)/shard_map/ppermute | solution.py:43
  171.4 11.7 %collective-permute-start.33 = (bf16[168,512]{1,0:T(8,128)(2,1)S(1)}, bf16[168,512]{1,0:T(8,128)(2,1)S(1)}, u32[]{:S(2)}, u32[]{:S(2)}) collective-permute-start(bf16[168,512]{1,0:T(8,128)(2,1)S(1)} %dynamic-slice_bitcast_fusion), channel_id=1, source_target_pairs={{0,8},{8,0},{16,24},{24,16},{1,9},{9,1},{17,25},{25,17},{2,10},{10... | collective-permute-start | bytes 516104 | tf_op jit(solution)/shard_map/ppermute | solution.py:39
  173.6 11.1 %collective-permute-start.25 = (bf16[2,96,512]{2,1,0:T(8,128)(2,1)S(1)}, bf16[2,96,512]{2,1,0:T(8,128)(2,1)S(1)}, u32[]{:S(2)}, u32[]{:S(2)}) collective-permute-start(bf16[2,96,512]{2,1,0:T(8,128)(2,1)S(1)} %slice.187), channel_id=1, source_target_pairs={{0,4},{1,5},{2,6},{3,7},{4,0},{5,1},{6,2},{7,3},{8,12},{9,13},{10,... | collective-permute-start | bytes 589832 | tf_op jit(solution)/shard_map/ppermute | solution.py:43
  175.6 17.9 %collective-permute-start.27 = (bf16[2,112,512]{2,1,0:T(8,128)(2,1)S(1)}, bf16[2,112,512]{2,1,0:T(8,128)(2,1)S(1)}, u32[]{:S(2)}, u32[]{:S(2)}) collective-permute-start(bf16[2,112,512]{2,1,0:T(8,128)(2,1)S(1)} %slice.191), channel_id=1, source_target_pairs={{0,2},{1,3},{2,0},{3,1},{4,6},{5,7},{6,4},{7,5},{8,10},{9,11},{10,... | collective-permute-start | bytes 688136 | tf_op jit(solution)/shard_map/ppermute | solution.py:43
  183.2 10.2 %collective-permute-start.34 = (bf16[168,512]{1,0:T(8,128)(2,1)S(1)}, bf16[168,512]{1,0:T(8,128)(2,1)S(1)}, u32[]{:S(2)}, u32[]{:S(2)}) collective-permute-start(bf16[168,512]{1,0:T(8,128)(2,1)S(1)} %fusion.3), channel_id=1, source_target_pairs={{0,16},{8,24},{16,0},{24,8},{1,17},{9,25},{17,1},{25,9},{2,18},{10... | collective-permute-start | bytes 516104 | tf_op jit(solution)/shard_map/ppermute | solution.py:39
  184.8 10.0 %collective-permute-start.26 = (bf16[1,96,512]{2,1,0:T(8,128)(2,1)S(1)}, bf16[1,96,512]{2,1,0:T(8,128)(2,1)S(1)}, u32[]{:S(2)}, u32[]{:S(2)}) collective-permute-start(bf16[1,96,512]{2,1,0:T(8,128)(2,1)S(1)} %slice.189), channel_id=1, source_target_pairs={{0,2},{1,3},{2,0},{3,1},{4,6},{5,7},{6,4},{7,5},{8,10},{9,11},{10,... | collective-permute-start | bytes 294920 | tf_op jit(solution)/shard_map/ppermute | solution.py:43
  (40 other events, 312.3 us)

commit v3 on v2

v3 whole, which is shorter than its diff:
```python
import functools, math
import jax, jax.numpy as jnp
from jax import lax
from jax.experimental import pallas as pl
from jax.experimental.pallas import tpu as pltpu

f32 = jnp.float32
bf16 = jnp.bfloat16
EPS = 1e-05
HEADS = 8

def dot(a, b):
    return jnp.dot(a, b, preferred_element_type=f32)

def dot_t(a, b):
    return lax.dot_general(a, b, (((1,), (1,)), ((), ())), preferred_element_type=f32)

def cp(n=1, vmem=100):
    return pltpu.CompilerParams(dimension_semantics=("arbitrary",) * n, vmem_limit_bytes=60 * 1024 * 1024)

def norm(x):
    c = x - jnp.mean(x, axis=-1, keepdims=True)
    r = lax.rsqrt(jnp.mean(c * c, axis=-1, keepdims=True) + EPS)
    return c * r, r

def row(v, i):
    return v[i : i + 1, :].astype(f32)


VROWS = 16
LANES = 128


def xor_perm(n, k):
    return [(i, i ^ k) for i in range(n)]


def rep_perm(x, b):
    return lax.ppermute(x, "rep", xor_perm(lax.axis_size("rep"), b))


def swap(x, k):
    return lax.ppermute(x, "shard", xor_perm(lax.axis_size("shard"), k))


def after(x, *deps):
    return lax.optimization_barrier((x,) + deps)[0]


def gather_direct(x, n):
    out = [(0, 0, x)]
    far = [(k, swap(x, k)) for k in range(2, n, 2)]
    out += [(k, 0, y) for k, y in far]
    return out + [(k ^ 1, 0, swap(y, 1)) for k, _, y in out]


def gather_forward(x, n, gate1, gate2):
    R = x.shape[0]
    cut = R // 2 // 16 * 16
    near = []
    far = []
    halves = {}
    for k in sorted(range(2, n, 2), key=lambda k: (bin(k).count("1"), k)):
        if bin(k).count("1") == 1:
            y = after(swap(x, k), gate1)
            near.append((k, 0, y))
            halves[k] = (y[:cut], y[cut:])
        else:
            low = k & -k
            high = 1 << (k.bit_length() - 1)
            a = swap(halves[k ^ low][0], low)
            b = swap(halves[k ^ high][1], high)
            far += [(k, 0, a), (k, cut, b)]
            halves[k] = (a, b)
    near = [(0, 0, x)] + near
    late = [(k, r0, after(a, gate2)) for k, r0, a in far]
    out = near + [(k ^ 1, r0, swap(a, 1)) for k, r0, a in near]
    return out + late + [(k ^ 1, r0, swap(a, 1)) for k, r0, a in late]


def add16(a, b):
    return (a.astype(f32) + b.astype(f32)).astype(bf16)


def spread_sum(parts, *gate):
    got = [swap(parts[k], 2 * k) for k in range(len(parts) - 1, 0, -1)]
    if gate:
        got = [after(a, *gate) for a in got]
    t = parts[0].astype(f32)
    for a in got:
        t = t + a.astype(f32)
    return t.astype(bf16)


def halve(s, top, bit):
    m = s.shape[0] // 2
    keep, out = (s[:m], s[m:]) if top else (s[0::2], s[1::2])
    return keep, swap(out, bit)


def rep_half(x):
    h = x.shape[0] // 2
    odd = lax.axis_index("rep") % 2
    mine = lax.dynamic_slice_in_dim(x, odd * h, h, 0)
    other = lax.dynamic_slice_in_dim(x, (1 - odd) * h, h, 0)
    return mine, rep_perm(other, 1)


def rep_steps():
    nr = lax.axis_size("rep")
    return [b for b in (2 << i for i in range(16)) if b < nr]


def rep_join(s, o):
    odd = lax.axis_index("rep") % 2
    lo = jnp.where(odd == 0, s, o)
    hi = jnp.where(odd == 0, o, s)
    return jnp.concatenate([lo, hi], axis=0).astype(f32)


def vector_block(vecs, upb, n):
    me = lax.axis_index("shard")

    def spot(v):
        w = v.shape[1]
        if w >= LANES:
            return v.reshape(-1, LANES)
        t = LANES // w
        lane = lax.broadcasted_iota(jnp.int32, (v.shape[0], LANES), 1)
        return jnp.where(lane // w == me % t, jnp.concatenate([v] * t, axis=1), jnp.zeros((), bf16))

    b = jnp.concatenate([spot(jnp.stack(vecs)), spot(upb[None])], axis=0)
    return jnp.pad(b, ((0, VROWS - b.shape[0]), (0, 0)))


def pull(me, refs, meta, segs, sems):
    copies = []
    for ref, (k, r0) in zip(refs, meta):
        s = jnp.bitwise_xor(me, k)
        r1 = r0 + ref.shape[0]
        for a, c, dst, lanes in segs:
            lo, hi = max(a, r0), min(a + c, r1)
            if lo < hi:
                src = ref.at[pl.ds(lo - r0, hi - lo), pl.ds(0, lanes)]
                copies.append(pltpu.make_async_copy(src, dst(s, lo - a, hi - lo), sems.at[len(copies)]))
    return copies


def mult(x, m):
    return pl.multiple_of(x, m)


def front_body(scale, n, meta, me, tok, step, *refs):
    np_ = len(meta)
    pieces = refs[:np_]
    xht, kv, qkvt, w, vec, upb, vbuf, sems = refs[np_:]
    D = tok.shape[-1]
    r = D // n
    FF = upb.shape[1]
    first = pl.program_id(0) == 0
    seg = lambda j: (j * r, r, lambda s, o, c: w.at[pl.ds(mult(s * r + o, 16), c), pl.ds(j * D, D)], D)
    segs = [(3 * r, VROWS, lambda s, o, c: vbuf.at[s, pl.ds(o, c)], LANES)] + [seg(j) for j in range(3)]

    @pl.when(first)
    def _():
        for c in pull(me[0], pieces, meta, segs, sems):
            c.start()

    x = tok[...].astype(f32) + step[...].astype(f32)
    nx, _ = norm(x)
    xht[...] = nx.astype(bf16).T

    @pl.when(first)
    def _():
        for c in pull(me[0], pieces, meta, segs, sems):
            c.wait()
        per = LANES // r
        tiles = [sum(vbuf[s, 0:8, :].astype(f32) for s in range(t * per, (t + 1) * per)) for t in range(D // LANES)]
        vec[...] = jnp.concatenate(tiles, axis=1)
        wu = FF // n
        if wu >= LANES:
            rows = [vbuf[s, 8 + q : 9 + q, :].astype(f32) for s in range(n) for q in range(wu // LANES)]
        else:
            per = LANES // wu
            rows = [sum(vbuf[s, 8:9, :].astype(f32) for s in range(t * per, (t + 1) * per)) for t in range(FF // LANES)]
        upb[...] = jnp.concatenate(rows, axis=1)

    v = vec[...]
    h = (nx * row(v, 0) + row(v, 1)).astype(bf16)
    for j in range(3):
        y = dot(h, w[:, j * D : (j + 1) * D])
        if j == 0:
            y = y + row(v, 2)
        if j == 2:
            y = y + row(v, 3)
        y = y.astype(bf16)
        if j == 0:
            y = y * bf16(scale)
        else:
            kv[:, (j - 1) * D : j * D] = y
        qkvt[j * D : (j + 1) * D, :] = y.T


S = jax.ShapeDtypeStruct
ANY = pl.BlockSpec(memory_space=pl.ANY)


def cost(flops, nbytes, tr=0):
    return pl.CostEstimate(flops=int(flops), bytes_accessed=int(nbytes), transcendentals=int(tr))


def front(me, tok, step, pieces, n, FF, bm=512):
    T, D = tok.shape
    scale = 1.0 / math.sqrt(D // HEADS)
    meta = tuple((k, r0) for k, r0, _ in pieces)
    keep = lambda *sh: pl.BlockSpec(sh, lambda i, m: (0,) * len(sh))
    return pl.pallas_call(
        functools.partial(front_body, scale, n, meta),
        grid_spec=pltpu.PrefetchScalarGridSpec(
            num_scalar_prefetch=1, grid=(T // bm,),
            in_specs=[pl.BlockSpec((bm, D), lambda i, m: (i, 0)), keep(1, D)] + [ANY] * len(pieces),
            out_specs=[pl.BlockSpec((D, bm), lambda i, m: (0, i)), pl.BlockSpec((bm, 2 * D), lambda i, m: (i, 0)), pl.BlockSpec((3 * D, bm), lambda i, m: (0, i)), keep(D, 3 * D), keep(8, D), keep(1, FF)],
            scratch_shapes=[pltpu.VMEM((n, VROWS, LANES), bf16), pltpu.SemaphoreType.DMA((8 * len(pieces),))]),
        out_shape=[S((D, T), bf16), S((T, 2 * D), bf16), S((3 * D, T), bf16), S((D, 3 * D), bf16), S((8, D), f32), S((1, FF), f32)],
        compiler_params=cp(), name="front", cost_estimate=cost(6 * T * D * D, 10 * T * D * 2),
    )(me, tok, step, *[a for _, _, a in pieces])


def attn_fwd_body(HD, bi, CR, ln, k, qt, vt, *refs):
    et, mixed, mixedt, mixedf, linv, scr, ka = refs[-7:]
    T, PW = k.shape
    n = ln[0]
    rid = lax.broadcasted_iota(jnp.int32, (PW, bi), 0)
    lane = lax.broadcasted_iota(jnp.int32, (T, PW), 1)
    rows = lax.broadcasted_iota(jnp.int32, (T, PW), 0)
    ka[:, :PW] = k[...]
    ka[:, PW:] = jnp.where((lane == 0) & (rows >= n), f32(-1e30), f32(0)).astype(bf16)
    ones = jnp.where(rid == 0, f32(1), f32(0)).astype(bf16)
    va = [jnp.concatenate([vt[h * HD : (h + 1) * HD, :], jnp.ones((16, T), bf16)], axis=0) for h in range(2)]
    tasks = [(b, h) for b in range(T // bi) for h in range(2)]
    nch = T // CR

    def query(t):
        b, h = tasks[t]
        q = qt[:, b * bi : (b + 1) * bi]
        return jnp.concatenate([jnp.where(rid // HD == h, q, jnp.zeros_like(q)), ones], axis=0)

    def score(t, c, q):
        s = dot(ka[c * CR : (c + 1) * CR, :], q)
        scr[t % 2, c * CR : (c + 1) * CR, :] = s
        return jnp.max(s, axis=0, keepdims=True)

    q = query(0)
    m = functools.reduce(jnp.maximum, [score(0, c, q) for c in range(nch)])
    half = None
    for t, (b, h) in enumerate(tasks):
        sl = slice(b * bi, (b + 1) * bi)
        more = t + 1 < len(tasks)
        if more:
            q = query(t + 1)
        nxt = []
        for c in range(nch):
            cs = slice(c * CR, (c + 1) * CR)
            if more:
                nxt.append(score(t + 1, c, q))
            et[h, cs, sl] = jnp.exp(scr[t % 2, cs, :] - m).astype(bf16)
        o = dot(va[h], et[h, :, sl])
        if more:
            m = functools.reduce(jnp.maximum, nxt)
        inv = 1.0 / o[HD : HD + 1, :]
        linv[h : h + 1, sl] = inv
        o = o[:HD, :] * inv
        if h == 0:
            half = o
        else:
            mt = jnp.concatenate([half, o], axis=0)
            mixedf[:, sl] = mt
            mt = mt.astype(bf16)
            mixedt[:, sl] = mt
            mixed[sl, :] = mt.T


def attn_fwd(ln, kv, qkvt, p0, cnt, prev):
    T = kv.shape[0]
    D = kv.shape[1] // 2
    HD = D // HEADS
    PW = 2 * HD
    NP = D // PW
    bi = min(512, T)
    prev = list(prev)
    return pl.pallas_call(
        functools.partial(attn_fwd_body, HD, bi, min(256, T)),
        grid_spec=pltpu.PrefetchScalarGridSpec(
            num_scalar_prefetch=1, grid=(cnt,),
            in_specs=[pl.BlockSpec((T, PW), lambda p, r: (0, p0 + p)), pl.BlockSpec((PW, T), lambda p, r: (p0 + p, 0)), pl.BlockSpec((PW, T), lambda p, r: (2 * NP + p0 + p, 0))] + [ANY] * len(prev),
            out_specs=[pl.BlockSpec((2, T, T), lambda p, r: (p0 + p, 0, 0)), pl.BlockSpec((T, PW), lambda p, r: (0, p0 + p)), pl.BlockSpec((PW, T), lambda p, r: (p0 + p, 0)), pl.BlockSpec((PW, T), lambda p, r: (p0 + p, 0)), pl.BlockSpec((None, 8, T), lambda p, r: (p0 + p, 0, 0))],
            scratch_shapes=[pltpu.VMEM((2, T, bi), f32), pltpu.VMEM((T, 2 * PW), bf16)]),
        out_shape=[S((HEADS, T, T), bf16), S((T, D), bf16), S((D, T), bf16), S((D, T), f32), S((NP, 8, T), f32)],
        input_output_aliases={4 + i: i for i in range(len(prev))},
        compiler_params=cp(), name="attn_fwd", cost_estimate=cost(cnt * 2 * 8 * T * T * 128, cnt * 2 * T * T * 2, cnt * 2 * T * T),
    )(ln, kv, qkvt, qkvt, *prev)


G0 = math.sqrt(2 / math.pi)


def push(me, n, s, src, keep, send, row0, sem):
    k = jnp.bitwise_xor(me, s)
    p = k >> 1
    put = lambda dst: pltpu.make_async_copy(src, dst.at[p, pl.ds(row0, src.shape[0])], sem)

    @pl.when(k & 1 == 0)
    def _():
        put(keep).start()

    @pl.when(k & 1 == 1)
    def _():
        put(send).start()


def ffn_body(n, meta, ch, ln, me, tok, step, vec, upb, cot, mixed, mixedt, *refs):
    np_ = len(meta)
    pieces = refs[:np_]
    out, gx1, gmt, keep, send, wo, wu, wd, act, gup, h2t, gdt, gattn, sums, upsum, dn, up, gwo, vr, sems, psems = refs[np_:]
    i = pl.program_id(0)
    bm, D = tok.shape
    FF = wu.shape[1]
    r = D // n
    rf = FF // n
    nf = FF // D
    i0 = me[0]
    ro = pl.ds(mult(i * bm, 128), bm)
    first = i == 0
    seg = lambda j: (r + j * r, r, lambda s, o, c: wu.at[pl.ds(mult(s * r + o, 16), c), pl.ds(j * D, D)], D)
    segs = [(0, r, lambda s, o, c: wo.at[pl.ds(mult(s * r + o, 16), c)], D)] + [seg(j) for j in range(nf)]
    segs += [(r + r * nf, rf, lambda s, o, c: wd.at[pl.ds(mult(s * rf + o, 16), c)], D)]

    @pl.when(first)
    def _():
        for c in pull(i0, pieces, meta, segs, sems):
            c.start()
        sums[...] = jnp.zeros_like(sums)
        upsum[...] = jnp.zeros_like(upsum)
        for c in pull(i0, pieces, meta, segs, sems):
            c.wait()

    v = vec[...]
    x1 = tok[...].astype(f32) + step[...].astype(f32) + dot(mixed[...], wo[...]) + row(v, 4)
    nx, rr = norm(x1)
    h2 = (nx * row(v, 5) + row(v, 6)).astype(bf16)
    live = (lax.broadcasted_iota(jnp.int32, (bm, 1), 0) + i * bm) < ln[0]
    gd = jnp.where(live, cot[...], jnp.zeros_like(cot))
    acc = x1 + row(v, 7)
    gh = None
    nc = FF // ch
    sl = [slice(c * ch, (c + 1) * ch) for c in range(nc)]
    lead = lambda c: (dot(h2, wu[:, sl[c]]), dot_t(gd, wd[sl[c], :]))
    nxt = lead(0)
    h2t[:, ro] = h2.T
    gdt[:, ro] = gd.T
    for c in range(nc):
        u, ga = nxt
        nxt = lead(c + 1) if c + 1 < nc else None
        u = u + upb[:, sl[c]]
        u2 = u * u
        t = jnp.tanh(u * (f32(G0) + f32(G0 * 0.044715) * u2))
        half = 0.5 + 0.5 * t
        a = (u * half).astype(bf16)
        act[ro, sl[c]] = a
        dg = half + u * (half * (1.0 - half)) * (f32(2 * G0) + f32(6 * 0.044715 * G0) * u2)
        gu = (ga * dg).astype(bf16)
        gup[ro, sl[c]] = gu
        upsum[:, sl[c]] += jnp.sum(gu.astype(f32), axis=0, keepdims=True)
        acc = acc + dot(a, wd[sl[c], :])
        p = dot_t(gu, wu[:, sl[c]])
        gh = p if gh is None else gh + p
    out[...] = jnp.where(live, acc, 0.0).astype(bf16)
    gn = gh * row(v, 5)
    gx = gd.astype(f32) + rr * (gn - jnp.mean(gn, axis=-1, keepdims=True) - nx * jnp.mean(gn * nx, axis=-1, keepdims=True))
    gx1[...] = gx
    gab = gx.astype(bf16)
    gattn[ro, :] = gab
    gmt[...] = dot_t(gab, wo[...]).astype(bf16).T
    s_ = lambda a: jnp.sum(a.astype(f32), axis=0, keepdims=True)
    sums[...] += jnp.concatenate([s_(gab), s_(gh * nx), s_(gh), s_(gd), jnp.zeros((4, D), f32)], axis=0)

    @pl.when(i == pl.num_programs(0) - 1)
    def _():
        per = D // rf
        o_up, o_out, o_vec = rf, rf + nf * r, rf + (nf + 1) * r
        for j in range(nf):
            dn[j] = dot(gdt[...], act[:, j * D : (j + 1) * D]).astype(bf16).T
            for t in range(per):
                push(i0, n, j * per + t, dn.at[j, pl.ds(t * rf, rf)], keep, send, 0, psems.at[j * per + t])
            up[j] = dot(h2t[...], gup[:, j * D : (j + 1) * D]).astype(bf16)
            for s in range(n):
                push(i0, n, s, up.at[j, pl.ds(s * r, r)], keep, send, o_up + j * r, psems.at[n * (1 + j) + s])
        gwo[...] = dot(mixedt[...], gattn[...]).astype(bf16)
        vr[...] = jnp.concatenate([sums[0:4, :]] + [upsum[:, c * D : (c + 1) * D] for c in range(nf)] + [jnp.zeros((VROWS - 4 - nf, D), f32)], axis=0).astype(bf16)
        b = n * (1 + nf)
        for s in range(n):
            push(i0, n, s, gwo.at[pl.ds(s * r, r)], keep, send, o_out, psems.at[b + s])
            push(i0, n, s, vr, keep, send, o_vec, psems.at[b + n + s])
        done = lambda src, q: pltpu.make_async_copy(src, keep.at[0, pl.ds(0, src.shape[0])], psems.at[q]).wait()
        for s in range(n):
            done(dn.at[0, pl.ds(0, rf)], s)
            for c in range(nf):
                done(up.at[0, pl.ds(0, r)], n * (1 + c) + s)
            done(gwo.at[pl.ds(0, r)], b + s)
            done(vr, b + n + s)


def ffn(ln, me, tok, step, vec, upb, cot, mixed, mixedt, pieces, n):
    T, D = tok.shape
    FF = upb.shape[1]
    bm = min(512, T)
    nf = FF // D
    r = D // n
    meta = tuple((k, r0) for k, r0, _ in pieces)
    full = lambda a: pl.BlockSpec(a.shape, lambda i, l, m: (0,) * a.ndim)
    rows = pl.BlockSpec((bm, D), lambda i, l, m: (i, 0))
    B = S((n // 2, FF // n + (nf + 1) * r + VROWS, D), bf16)
    V = pltpu.VMEM
    return pl.pallas_call(
        functools.partial(ffn_body, n, meta, min(1024, FF)),
        grid_spec=pltpu.PrefetchScalarGridSpec(
            num_scalar_prefetch=2, grid=(T // bm,),
            in_specs=[rows, full(step), full(vec), full(upb), rows, rows, full(mixedt)] + [ANY] * len(pieces),
            out_specs=[rows, rows, pl.BlockSpec((D, bm), lambda i, l, m: (0, i)), ANY, ANY],
            scratch_shapes=[V((D, D), bf16), V((D, FF), bf16), V((FF, D), bf16), V((T, FF), bf16), V((T, FF), bf16), V((D, T), bf16), V((D, T), bf16), V((T, D), bf16), V((8, D), f32), V((1, FF), f32), V((nf, D, D), bf16), V((nf, D, D), bf16), V((D, D), bf16), V((VROWS, D), bf16), pltpu.SemaphoreType.DMA((8 * len(pieces),)), pltpu.SemaphoreType.DMA((n * (nf + 3),))]),
        out_shape=[S((T, D), bf16), S((T, D), f32), S((D, T), bf16), B, B],
        compiler_params=cp(), name="ffn", cost_estimate=cost(2 * T * D * (6 * FF + 3 * D), 16 * T * D, T * FF),
    )(ln, me, tok, step, vec, upb, cot, mixed, mixedt, *[a for _, _, a in pieces])


def attn_bwd_body(HD, scale, CR, v, kt, qt, gt, mt, linv, et, *refs):
    gq, ds = refs[-2:]
    T = v.shape[0]
    rid = lax.broadcasted_iota(jnp.int32, gt.shape, 0) // HD
    g = gt[...].astype(f32)
    q = qt[...]
    gv = gk = None
    for h in range(2):
        hs = slice(h * HD, (h + 1) * HD)
        gs = (g * linv[h : h + 1, :]).astype(bf16)
        gm = jnp.where(rid == h, gs, jnp.zeros_like(gs))
        dl = jnp.sum(gs[hs, :].astype(f32) * mt[hs, :], axis=0, keepdims=True)
        for c in range(T // CR):
            cs = slice(c * CR, (c + 1) * CR)
            ds[h, cs, :] = (et[h, cs, :].astype(f32) * (dot(v[cs, :], gm) - dl)).astype(bf16)
        a = dot(et[h], gm.T)
        b = dot(ds[h], jnp.where(rid == h, q, jnp.zeros_like(q)).T)
        gv = a if gv is None else gv + a
        gk = b if gk is None else gk + b
        gq[0, hs, :] = (dot(kt[hs, :], ds[h]) * scale).astype(bf16)
    gq[2] = gv.astype(bf16).T
    gq[1] = gk.astype(bf16).T


def attn_bwd(kv, qkvt, gmt, mixedf, linv, et, p0, cnt, prev):
    T = kv.shape[0]
    D = kv.shape[1] // 2
    HD = D // HEADS
    PW = 2 * HD
    NP = D // PW
    prev = list(prev)
    pr = lambda o: pl.BlockSpec((PW, T), lambda p: (o + p0 + p, 0))
    return pl.pallas_call(
        functools.partial(attn_bwd_body, HD, 1.0 / math.sqrt(HD), min(256, T)),
        grid=(cnt,),
        scratch_shapes=[pltpu.VMEM((2, T, T), bf16)],
        in_specs=[pl.BlockSpec((T, PW), lambda p: (0, NP + p0 + p)), pr(NP), pr(0), pr(0), pr(0), pl.BlockSpec((None, 8, T), lambda p: (p0 + p, 0, 0)), pl.BlockSpec((2, T, T), lambda p: (p0 + p, 0, 0))] + [ANY] * len(prev),
        out_specs=pl.BlockSpec((3, PW, T), lambda p: (0, p0 + p, 0)),
        out_shape=S((3, D, T), bf16),
        input_output_aliases={7: 0} if prev else {},
        compiler_params=cp(), name="attn_bwd", cost_estimate=cost(cnt * 2 * 16 * T * T * 128, cnt * 2 * T * T * 2),
    )(kv, qkvt, qkvt, gmt, mixedf, linv, et, *prev)


def wqkv_body(n, me, xht, g, keep, send, res, vr, sems):
    j = pl.program_id(0)
    D = g.shape[0]
    r = D // n
    i0 = me[0]
    x = jnp.concatenate([xht[...], jnp.ones((16, xht.shape[1]), bf16)], axis=0)
    y = dot_t(x, g[...]).astype(bf16)
    res[j] = y[:D]
    vr[...] = jnp.where(lax.broadcasted_iota(jnp.int32, vr.shape, 0) == j, y[D:], jnp.where(j == 0, jnp.zeros_like(y[D:]), vr[...]))
    for s in range(n):
        push(i0, n, s, res.at[j, pl.ds(s * r, r)], keep, send, mult(j * r, 16), sems.at[j * n + s])

    @pl.when(j == 2)
    def _():
        for s in range(n):
            push(i0, n, s, vr, keep, send, 3 * r, sems.at[3 * n + s])
        for s in range(n):
            for q in range(3):
                pltpu.make_async_copy(res.at[0, pl.ds(0, r)], keep.at[0, pl.ds(0, r)], sems.at[q * n + s]).wait()
            pltpu.make_async_copy(vr, keep.at[0, pl.ds(0, VROWS)], sems.at[3 * n + s]).wait()


def wqkv(me, xht, g, n):
    D, T = xht.shape
    A = S((n // 2, 3 * (D // n) + VROWS, D), bf16)
    return pl.pallas_call(
        functools.partial(wqkv_body, n),
        grid_spec=pltpu.PrefetchScalarGridSpec(
            num_scalar_prefetch=1, grid=(3,),
            in_specs=[pl.BlockSpec((D, T), lambda j, m: (0, 0)), pl.BlockSpec((None, D, T), lambda j, m: (j, 0, 0))],
            out_specs=[ANY] * 2,
            scratch_shapes=[pltpu.VMEM((3, D, D), bf16), pltpu.VMEM((VROWS, D), bf16), pltpu.SemaphoreType.DMA((4 * n,))]),
        out_shape=[A, A],
        compiler_params=cp(), name="wqkv", cost_estimate=cost(6 * T * D * D, 10 * T * D),
    )(me, xht, g)


def back_body(tok, step, vec, w, g, gx1, tg):
    D = tok.shape[1]
    x = tok[...].astype(f32) + step[...].astype(f32)
    nx, rr = norm(x)
    gt = dot(w[:, :D], g[0]) + dot(w[:, D : 2 * D], g[1]) + dot(w[:, 2 * D :], g[2])
    gn = gt.T * row(vec[...], 0)
    tg[...] = gx1[...] + rr * (gn - jnp.mean(gn, axis=-1, keepdims=True) - nx * jnp.mean(gn * nx, axis=-1, keepdims=True))


def back(tok, step, vec, w, g, gx1, bm=512):
    T, D = tok.shape
    full = lambda a: pl.BlockSpec(a.shape, lambda i: (0,) * a.ndim)
    rows = pl.BlockSpec((bm, D), lambda i: (i, 0))
    return pl.pallas_call(
        back_body, grid=(T // bm,),
        in_specs=[rows, full(step), full(vec), full(w), pl.BlockSpec((3, D, bm), lambda i: (0, 0, i)), rows],
        out_specs=rows, out_shape=S((T, D), f32), compiler_params=cp(), name="back", cost_estimate=cost(6 * T * D * D, 14 * T * D),
    )(tok, step, vec, w, g, gx1)


def shards(tokens, step_embed, lengths, cotangent, ln1_gain, ln1_bias, qkv_weight, q_bias, v_bias, out_weight, out_bias, ln2_gain, ln2_bias, up_weight, up_bias, down_weight, down_bias):
    n = lax.axis_size("shard")
    me = lax.axis_index("shard").astype(jnp.int32)
    mes = me[None]
    tok, cot, step = tokens[0], cotangent[0], step_embed
    T, D = tok.shape
    r = D // n
    FF = up_bias.shape[0] * n
    nc = FF // D
    vb = vector_block([ln1_gain, ln1_bias, q_bias, v_bias, out_bias, ln2_gain, ln2_bias, down_bias], up_bias, n)
    cols = lambda a: [a[:, j * D : (j + 1) * D] for j in range(a.shape[1] // D)]
    pack1 = jnp.concatenate(cols(qkv_weight) + [jnp.pad(vb, ((0, 0), (0, D - LANES)))], axis=0)
    pack2 = jnp.concatenate([out_weight] + cols(up_weight) + [down_weight], axis=0)
    pieces1 = gather_direct(pack1, n)
    xht, kv, qkvt, w, vec, upb = front(mes, tok, step, pieces1, n, FF)
    NP = HEADS // 2
    fw = attn_fwd(lengths, kv, qkvt, 0, NP // 2, [])
    fw2 = attn_fwd(lengths, kv, qkvt, NP // 2, NP // 2, fw)
    et, mixed, mixedt, mixedf, linv = fw2
    pieces2 = gather_forward(after(pack2, *[a for _, _, a in pieces1[1:]]), n, fw[4], linv)
    out, gx1, gmt, keep, send = ffn(lengths, mes, tok, step, vec, upb, cot, mixed, mixedt, pieces2, n)
    bwd = lambda p, c, g, *deps: attn_bwd(kv, qkvt, after(gmt, *deps) if deps else gmt, mixedf, linv, et, p, c, g)
    R = keep.shape[1]
    ra = R // 2 // 8 * 8
    got = swap(send, 1)
    g = bwd(0, 1, [])
    got = after(got, g)
    sa = add16(keep[:, :ra], got[:, :ra])
    sb = add16(keep[:, ra:], got[:, ra:])
    g = bwd(1, NP - 1, [g], sa, sb)
    m = (n // 2).bit_length() - 1
    for t in range(m):
        ka, ga = halve(sa, True, 1 << (m - t))
        kb, gb = halve(sb, False, 2 << t)
        dep = g if t == 0 else keep
        sa = add16(ka, after(ga, dep))
        sb = add16(kb, after(gb, dep))
        if t == 0:
            keep, send = wqkv(mes, after(xht, sa, sb), g, n)
    ua, ub = sa[0], sb[0]
    got = after(swap(send, 1), ua, ub)
    parts = [add16(keep[k], got[k]) for k in range(n // 2)]
    ma, ga = rep_half(ua)
    mb, gb = rep_half(ub)
    tg = back(tok, after(step, ua, ub, *parts), vec, w, g, gx1)
    za = add16(ma, after(ga, tg))
    zb = add16(mb, after(gb, tg))
    own2 = spread_sum(parts, za, zb)
    m2, g2 = rep_half(own2)
    z2 = add16(m2, g2)
    for b in rep_steps():
        za = add16(za, after(rep_perm(za, b), z2))
        zb = add16(zb, rep_perm(zb, b))
        z2 = add16(z2, after(rep_perm(z2, b), za, zb))
    z1 = jnp.concatenate([rep_join(za, rep_perm(za, 1)), rep_join(zb, rep_perm(zb, 1))], axis=0)
    z2 = rep_join(z2, rep_perm(z2, 1))
    rf = FF // n
    g_down = z1[:rf]
    wide = lambda a, c: jnp.concatenate([a[j * r : (j + 1) * r] for j in range(c)], axis=1)
    g_up = wide(z1[rf:], nc)
    g_out = z1[rf + nc * r : rf + (nc + 1) * r]
    small = z1[rf + (nc + 1) * r :]
    own = lambda a: lax.dynamic_slice(a, (me * r,), (r,))
    g_upb = lax.dynamic_slice(small[4 : 4 + nc].reshape(-1), (me * (FF // n),), (FF // n,))
    m = wide(z2, 3)
    sq = z2[3 * r : 3 * r + 3].reshape(1, 3 * D)
    wf = qkv_weight.astype(f32)
    g_qkv = ln1_gain.astype(f32)[:, None] * m + ln1_bias.astype(f32)[:, None] * sq
    g_g1 = jnp.sum(wf * m, axis=1)
    g_b1 = jnp.sum(wf * sq, axis=1)
    return (out[None], tg[None], g_g1, g_b1, g_qkv, own(z2[3 * r]), own(z2[3 * r + 2]), g_out, own(small[0]), own(small[1]), own(small[2]), g_up, g_upb, g_down, own(small[3]))


def solution(mesh):
    from jax.sharding import PartitionSpec as P

    in_specs = (
        P(("rep", "shard"), None, None),
        P(("rep", "shard"), None),
        P(("rep", "shard")),
        P(("rep", "shard"), None, None),
        P("shard"),
        P("shard"),
        P("shard", None),
        P("shard"),
        P("shard"),
        P("shard", None),
        P("shard"),
        P("shard"),
        P("shard"),
        P("shard", None),
        P("shard"),
        P("shard", None),
        P("shard"),
    )
    out_specs = (
        P(("rep", "shard"), None, None),
        P(("rep", "shard"), None, None),
        P("shard"),
        P("shard"),
        P("shard", None),
        P("shard"),
        P("shard"),
        P("shard", None),
        P("shard"),
        P("shard"),
        P("shard"),
        P("shard", None),
        P("shard"),
        P("shard", None),
        P("shard"),
    )
    return jax.shard_map(shards, mesh=mesh, in_specs=in_specs, out_specs=out_specs, check_vma=False)
```

time: 218 us -> 178 us (0.82)
  Pallas kernels: 115 us -> 90.4 us
  starting transfers between devices: 38.8 us -> 29.8 us
  waiting for transfers between devices: 34.8 us -> 29.3 us
    pallas_call x10 -> x6, Pallas kernels: 99.1 us -> 75.7 us  [the longest x1 26.3 us: ffn(): pl.pallas_call(functools.partial(ffn_body, n, meta, min(1024, FF)), grid_...]
    ppermute x30 -> x25, waiting for transfers between devices: 17.9 us -> 9.64 us  [swap(): return lax.ppermute(x, 'shard', xor_perm(lax.axis_size('shard'), k))]
    ppermute x30 -> x25, starting transfers between devices: 24.3 us -> 18.5 us  [swap(): return lax.ppermute(x, 'shard', xor_perm(lax.axis_size('shard'), k))]
    another operation x16 -> x1, local copies, waits for them, and re-layouts: 5.98 us -> 0.8 us  [vector_block(): b = jnp.concatenate([spot(jnp.stack(vecs)), spot(upb[None])], axis=0)]
    ppermute x9, starting transfers between devices: 14.6 us -> 11.3 us  [rep_perm(): return lax.ppermute(x, 'rep', xor_perm(lax.axis_size('rep'), b))]
    ppermute x9, waiting for transfers between devices: 16.9 us -> 19.7 us  [rep_perm(): return lax.ppermute(x, 'rep', xor_perm(lax.axis_size('rep'), b))]
    dynamic_slice x2 -> x7, local copies, waits for them, and re-layouts: 0.04 us -> 2.44 us  [the longest x4 2.33 us: shards(): own = lambda a: lax.dynamic_slice(a, (me * r,), (r,))]
    unnamed x56 -> x49, local copies, waits for them, and re-layouts: 5.27 us -> 6.77 us
  transfers between devices with their start and end apart: 39 -> 34, of which waited for: 13 -> 11; matrix products, arithmetic and copies ran while one was open for 7% -> 8% of each run, Pallas kernels for 40% -> 36%
where the time goes in v3:
time: 178 us; the launch traced here: 177 us
  Pallas kernels  90.4 us (51%)
  starting transfers between devices  29.8 us (17%)
  waiting for transfers between devices  29.3 us (16%)
  local copies, waits for them, and re-layouts  15.1 us (8%)
  other arithmetic  10.4 us (6%)
  between operations  1.97 us (1%)
    pallas_call x1, Pallas kernels, ffn(): pl.pallas_call(functools.partial(ffn_body, n, meta, min(1024, FF)), grid_...  26.3 us
    pallas_call x2, Pallas kernels, attn_bwd(): pl.pallas_call(functools.partial(attn_bwd_body, HD, 1.0 / math.sqrt(HD),...  23.8 us
    pallas_call x2, Pallas kernels, attn_fwd(): pl.pallas_call(functools.partial(attn_fwd_body, HD, bi, min(256, T)), gri...  20 us
    ppermute x9, waiting for transfers between devices, rep_perm(): return lax.ppermute(x, 'rep', xor_perm(lax.axis_size('rep'), b))  19.7 us
    ppermute x25, starting transfers between devices, swap(): return lax.ppermute(x, 'shard', xor_perm(lax.axis_size('shard'), k))  18.5 us
    ppermute x9, starting transfers between devices, rep_perm(): return lax.ppermute(x, 'rep', xor_perm(lax.axis_size('rep'), b))  11.3 us
    ppermute x25, waiting for transfers between devices, swap(): return lax.ppermute(x, 'shard', xor_perm(lax.axis_size('shard'), k))  9.64 us
    pallas_call x1, Pallas kernels, front(): pl.pallas_call(functools.partial(front_body, scale, n, meta), grid_spec=p...  7.74 us
  transfers between devices with their start and end apart: 34, of which 11 were waited for; matrix products, arithmetic and copies ran while one was open for 8% of the time, Pallas kernels for 36%

profile of v3, /device:TPU:0, one launch (start us, length us, event | category | flops | bytes accessed | tf_op | source)
XLA Modules:
  0.0 177.0 jit_solution(17020932147621932873)
XLA Ops:
  3.2 3.0 %collective-permute-start = (bf16[208,512]{1,0:T(8,128)(2,1)S(1)}, bf16[208,512]{1,0:T(8,128)(2,1)S(1)}, u32[]{:S(2)}, u32[]{:S(2)}) collective-permute-start(bf16[208,512]{1,0:T(8,128)(2,1)S(1)} %fusion.8.refs_0_), channel_id=1, source_target_pairs={{0,2},{1,3},{2,0},{3,1},{4,6},{5,7},{6,4},{7,5},{8,10},{9,11},{10,... | collective-permute-start | bytes 638984 | tf_op jit(solution)/shard_map/ppermute | solution.py:43
  6.2 1.5 collective-permute-start.1
  12.3 5.2 %collective-permute-done.1.refs_2_ = bf16[208,512]{1,0:T(8,128)(2,1)S(1)} collective-permute-done((bf16[208,512]{1,0:T(8,128)(2,1)S(1)}, bf16[208,512]{1,0:T(8,128)(2,1)S(1)}, u32[]{:S(2)}, u32[]{:S(2)}) %collective-permute-start.1) | collective-permute-done | bytes 213024 | tf_op jit(solution)/shard_map/ppermute | solution.py:43
  22.8 7.7 %front.1 = (bf16[512,1024]{1,0:T(8,128)(2,1)}, bf16[1024,1024]{1,0:T(8,128)(2,1)}, bf16[1536,1024]{1,0:T(8,128)(2,1)}, bf16[512,1536]{1,0:T(8,128)(2,1)}, f32[8,512]{1,0:T(8,128)}, /*index=5*/f32[1,2048]{1,0:T(1,128)}) custom-call(s32[1]{0:T(128)} %bitcast.me, bf16[1024,512]{1,0:T(8,128)(2,1)} %bitcast.50, bf16[1,512]{1,0:T(2,128)(2,1)} %step.4, ...), custom_call_target="tpu_custom_call" | custom-call | flops 1610612736 | bytes 10485760 | tf_op jit(solution)/shard_map/front/pallas_call | solution.py:217
  30.6 10.0 %attn_fwd.2 = (bf16[8,1024,1024]{2,1,0:T(8,128)(2,1)}, bf16[1024,512]{1,0:T(8,128)(2,1)}, bf16[512,1024]{1,0:T(8,128)(2,1)}, f32[512,1024]{1,0:T(8,128)}, f32[4,8,1024]{2,1,0:T(8,128)}) custom-call(s32[1]{0:T(128)S(6)} %copy.50.ln, bf16[1024,1024]{1,0:T(8,128)(2,1)} %get-tuple-element.61.k.v, bf16[1536,1024]{1,0:T(8,128)(2,1)} %get-tuple-element.62.qt.vt.kt, ...), custom_call_target="tpu_custom_call" | custom-call | flops 4294967296 | bytes 8388608 | tf_op jit(solution)/shard_map/attn_fwd/pallas_call | solution.py:291
  43.3 10.0 %attn_fwd.3 = (bf16[8,1024,1024]{2,1,0:T(8,128)(2,1)}, bf16[1024,512]{1,0:T(8,128)(2,1)}, bf16[512,1024]{1,0:T(8,128)(2,1)}, f32[512,1024]{1,0:T(8,128)}, f32[4,8,1024]{2,1,0:T(8,128)}) custom-call(s32[1]{0:T(128)S(6)} %copy.50.ln, ...), custom_call_target="tpu_custom_call", output_to_operand_aliasing={{0}: (4, {}), {1}: (5, {}), {2}: (6, {}), {3}: (7, {}), {4}... | custom-call | flops 4294967296 | bytes 8388608 | tf_op jit(solution)/shard_map/attn_fwd/pallas_call | solution.py:291
  56.7 26.3 %ffn.1 = (bf16[1024,512]{1,0:T(8,128)(2,1)}, f32[1024,512]{1,0:T(8,128)}, bf16[512,1024]{1,0:T(8,128)(2,1)}, bf16[4,592,512]{2,1,0:T(8,128)(2,1)}, bf16[4,592,512]{2,1,0:T(8,128)(2,1)}) custom-call(s32[1]{0:T(128)S(6)} %copy.50.ln, s32[1]{0:T(128)} %bitcast.me, bf16[1024,512]{1,0:T(8,128)(2,1)} %bitcast.51, bf16[1,512]{1,0:T(2,128)(2,1)} %step.4, ...), custom_call_target="tpu_custom_call" | custom-call | flops 14495514624 | bytes 8388608 | tf_op jit(solution)/shard_map/ffn/pallas_call | solution.py:424
  83.3 7.7 %attn_bwd.2.refs_0_ = bf16[3,512,1024]{2,1,0:T(8,128)(2,1)} custom-call(bf16[1024,1024]{1,0:T(8,128)(2,1)} %get-tuple-element.61.k.v, bf16[1536,1024]{1,0:T(8,128)(2,1)} %get-tuple-element.62.qt.vt.kt, bf16[1536,1024]{1,0:T(8,128)(2,1)} %get-tuple-element.62.qt.vt.kt, bf16[512,1024]{1,0:T(8,128)(2,1)} %get-tuple-element.83.gt, ...), custom_call_target="tpu_custom_call" | custom-call | flops 4294967296 | bytes 4194304 | tf_op jit(solution)/shard_map/attn_bwd/pallas_call | solution.py:468
  91.0 1.4 copy-done
  92.4 3.1 %add_convert_fusion = (bf16[4,296,512]{2,1,0:T(8,128)(2,1)S(1)}, bf16[4,296,512]{2,1,0:T(8,128)(2,1)S(1)}) fusion(bf16[4,592,512]{2,1,0:T(8,128)(2,1)} %copy-done, bf16[4,592,512]{2,1,0:T(8,128)(2,1)} %get-tuple-element.77), kind=kLoop, calls=%fused_computation | loop fusion | flops 4849664 | bytes 7274496 | tf_op jit(solution)/shard_map/convert_element_type | solution.py:82
  98.4 16.1 %attn_bwd.3.g = bf16[3,512,1024]{2,1,0:T(8,128)(2,1)} custom-call(bf16[1024,1024]{1,0:T(8,128)(2,1)} %get-tuple-element.61.k.v, bf16[1536,1024]{1,0:T(8,128)(2,1)} %get-tuple-element.62.qt.vt.kt, bf16[1536,1024]{1,0:T(8,128)(2,1)} %get-tuple-element.62.qt.vt.kt, bf16[512,1024]{1,0:T(8,128)(2,1)} %get-tuple-element.83.gt, ...), custom_call_target="tpu_custom_call", output_to_operand_aliasing={{}: (7, {})} | custom-call | flops 12884901888 | bytes 12582912 | tf_op jit(solution)/shard_map/attn_bwd/pallas_call | solution.py:468
  118.1 5.6 %wqkv.1 = (bf16[4,208,512]{2,1,0:T(8,128)(2,1)}, bf16[4,208,512]{2,1,0:T(8,128)(2,1)}) custom-call(s32[1]{0:T(128)} %bitcast.me, bf16[512,1024]{1,0:T(8,128)(2,1)} %get-tuple-element.87.xht, bf16[3,512,1024]{2,1,0:T(8,128)(2,1)} %attn_bwd.3.g), custom_call_target="tpu_custom_call" | custom-call | flops 1610612736 | bytes 5242880 | tf_op jit(solution)/shard_map/wqkv/pallas_call | solution.py:505
  125.6 1.6 collective-permute-start.24
  127.9 1.5 fusion.12
  129.4 2.3 %collective-permute-start.22 = (bf16[208,512]{1,0:T(8,128)(2,1)S(1)}, bf16[208,512]{1,0:T(8,128)(2,1)S(1)}, u32[]{:S(2)}, u32[]{:S(2)}) collective-permute-start(bf16[208,512]{1,0:T(8,128)(2,1)S(1)} %get-tuple-element.107), channel_id=1, source_target_pairs={{0,6},{1,7},{2,4},{3,5},{4,2},{5,3},{6,0},{7,1},{8,14},{9,15},{10,... | collective-permute-start | bytes 638984 | tf_op jit(solution)/shard_map/ppermute | solution.py:43
  133.0 7.0 %back.1 = f32[1024,512]{1,0:T(8,128)} custom-call(bf16[1024,512]{1,0:T(8,128)(2,1)} %bitcast.52, bf16[1,512]{1,0:T(2,128)(2,1)} %step.4, f32[8,512]{1,0:T(8,128)} %get-tuple-element.59.vec, bf16[512,1536]{1,0:T(8,128)(2,1)} %get-tuple-element.94.w, bf16[3,512,1024]{2,1,0:T(8,128)(2,1)} %attn_bwd.3.g, f32[1024,512]{1,0:T(8,128)} %get-tuple-element.95.gx1), custom_call_target="tpu_custom_call" | custom-call | flops 1610612736 | bytes 7340032 | tf_op jit(solution)/shard_map/back/pallas_call | solution.py:530
  140.0 2.6 %collective-permute-start.30 = (bf16[148,512]{1,0:T(8,128)(2,1)S(1)}, bf16[148,512]{1,0:T(8,128)(2,1)S(1)}, u32[]{:S(2)}, u32[]{:S(2)}) collective-permute-start(bf16[148,512]{1,0:T(8,128)(2,1)S(1)} %fusion.6), channel_id=1, source_target_pairs={{0,16},{8,24},{16,0},{24,8},{1,17},{9,25},{17,1},{25,9},{2,18},{10... | collective-permute-start | bytes 454664 | tf_op jit(solution)/shard_map/ppermute | solution.py:39
  143.1 9.8 %collective-permute-done.30 = bf16[148,512]{1,0:T(8,128)(2,1)S(1)} collective-permute-done((bf16[148,512]{1,0:T(8,128)(2,1)S(1)}, bf16[148,512]{1,0:T(8,128)(2,1)S(1)}, u32[]{:S(2)}, u32[]{:S(2)}) %collective-permute-start.30) | collective-permute-done | bytes 151584 | tf_op jit(solution)/shard_map/ppermute | solution.py:39
  153.2 2.1 %collective-permute-start.27 = (bf16[104,512]{1,0:T(8,128)(2,1)S(1)}, bf16[104,512]{1,0:T(8,128)(2,1)S(1)}, u32[]{:S(2)}, u32[]{:S(2)}) collective-permute-start(bf16[104,512]{1,0:T(8,128)(2,1)S(1)} %constant_dynamic-slice_fusion.8), channel_id=1, source_target_pairs={{0,8},{8,0},{16,24},{24,16},{1,9},{9,1},{17,25},{25,17},{2,10},{10... | collective-permute-start | bytes 319496 | tf_op jit(solution)/shard_map/ppermute | solution.py:39
  155.3 4.0 %collective-permute-done.32 = bf16[148,512]{1,0:T(8,128)(2,1)S(1)} collective-permute-done((bf16[148,512]{1,0:T(8,128)(2,1)S(1)}, bf16[148,512]{1,0:T(8,128)(2,1)S(1)}, u32[]{:S(2)}, u32[]{:S(2)}) %collective-permute-start.32) | collective-permute-done | bytes 151584 | tf_op jit(solution)/shard_map/ppermute | solution.py:39
  164.5 2.1 %collective-permute-start.33 = (bf16[148,512]{1,0:T(8,128)(2,1)S(1)}, bf16[148,512]{1,0:T(8,128)(2,1)S(1)}, u32[]{:S(2)}, u32[]{:S(2)}) collective-permute-start(bf16[148,512]{1,0:T(8,128)(2,1)S(1)} %add_convert_fusion.12), channel_id=1, source_target_pairs={{0,8},{8,0},{16,24},{24,16},{1,9},{9,1},{17,25},{25,17},{2,10},{10... | collective-permute-start | bytes 454664 | tf_op jit(solution)/shard_map/ppermute | solution.py:39
  166.6 3.3 %collective-permute-done.28 = bf16[104,512]{1,0:T(8,128)(2,1)S(1)} collective-permute-done((bf16[104,512]{1,0:T(8,128)(2,1)S(1)}, bf16[104,512]{1,0:T(8,128)(2,1)S(1)}, u32[]{:S(2)}, u32[]{:S(2)}) %collective-permute-start.28) | collective-permute-done | bytes 106528 | tf_op jit(solution)/shard_map/ppermute | solution.py:39
  170.5 1.6 collective-permute-done.33
  175.5 1.5 fusion.5
  (153 shorter events, 38.1 us)
Async XLA Ops:
  3.2 9.1 %collective-permute-start = (bf16[208,512]{1,0:T(8,128)(2,1)S(1)}, bf16[208,512]{1,0:T(8,128)(2,1)S(1)}, u32[]{:S(2)}, u32[]{:S(2)}) collective-permute-start(bf16[208,512]{1,0:T(8,128)(2,1)S(1)} %fusion.8.refs_0_), channel_id=1, source_target_pairs={{0,2},{1,3},{2,0},{3,1},{4,6},{5,7},{6,4},{7,5},{8,10},{9,11},{10,... | collective-permute-start | bytes 638984 | tf_op jit(solution)/shard_map/ppermute | solution.py:43
  6.2 11.3 %collective-permute-start.1 = (bf16[208,512]{1,0:T(8,128)(2,1)S(1)}, bf16[208,512]{1,0:T(8,128)(2,1)S(1)}, u32[]{:S(2)}, u32[]{:S(2)}) collective-permute-start(bf16[208,512]{1,0:T(8,128)(2,1)S(1)} %fusion.8.refs_0_), channel_id=1, source_target_pairs={{0,4},{1,5},{2,6},{3,7},{4,0},{5,1},{6,2},{7,3},{8,12},{9,13},{10,... | collective-permute-start | bytes 638984 | tf_op jit(solution)/shard_map/ppermute | solution.py:43
  7.7 9.8 %collective-permute-start.2 = (bf16[208,512]{1,0:T(8,128)(2,1)S(1)}, bf16[208,512]{1,0:T(8,128)(2,1)S(1)}, u32[]{:S(2)}, u32[]{:S(2)}) collective-permute-start(bf16[208,512]{1,0:T(8,128)(2,1)S(1)} %fusion.8.refs_0_), channel_id=1, source_target_pairs={{0,6},{1,7},{2,4},{3,5},{4,2},{5,3},{6,0},{7,1},{8,14},{9,15},{10,... | collective-permute-start | bytes 638984 | tf_op jit(solution)/shard_map/ppermute | solution.py:43
  7.7 12.1 %collective-permute-start.3 = (bf16[208,512]{1,0:T(8,128)(2,1)S(1)}, bf16[208,512]{1,0:T(8,128)(2,1)S(1)}, u32[]{:S(2)}, u32[]{:S(2)}) collective-permute-start(bf16[208,512]{1,0:T(8,128)(2,1)S(1)} %fusion.8.refs_0_), channel_id=1, source_target_pairs={{0,1},{1,0},{2,3},{3,2},{4,5},{5,4},{6,7},{7,6},{8,9},{9,8},{10,11... | collective-permute-start | bytes 638984 | tf_op jit(solution)/shard_map/ppermute | solution.py:43
  19.9 20.7 %collective-permute-start.7 = (bf16[576,512]{1,0:T(8,128)(2,1)S(1)}, bf16[576,512]{1,0:T(8,128)(2,1)S(1)}, u32[]{:S(2)}, u32[]{:S(2)}) collective-permute-start(bf16[576,512]{1,0:T(8,128)(2,1)S(1)} %constant_dynamic-update-slice_fusion.refs_0_), channel_id=1, source_target_pairs={{0,2},{1,3},{2,0},{3,1},{4,6},{5,7},{6,4},{7,5},{8,10},{9,11},{10,... | collective-permute-start | bytes 1769480 | tf_op jit(solution)/shard_map/ppermute | solution.py:43
  20.7 20.5 %collective-permute-start.8 = (bf16[576,512]{1,0:T(8,128)(2,1)S(1)}, bf16[576,512]{1,0:T(8,128)(2,1)S(1)}, u32[]{:S(2)}, u32[]{:S(2)}) collective-permute-start(bf16[576,512]{1,0:T(8,128)(2,1)S(1)} %constant_dynamic-update-slice_fusion.refs_0_), channel_id=1, source_target_pairs={{0,4},{1,5},{2,6},{3,7},{4,0},{5,1},{6,2},{7,3},{8,12},{9,13},{10,... | collective-permute-start | bytes 1769480 | tf_op jit(solution)/shard_map/ppermute | solution.py:43
  22.7 31.3 %collective-permute-start.9 = (bf16[576,512]{1,0:T(8,128)(2,1)S(1)}, bf16[576,512]{1,0:T(8,128)(2,1)S(1)}, u32[]{:S(2)}, u32[]{:S(2)}) collective-permute-start(bf16[576,512]{1,0:T(8,128)(2,1)S(1)} %constant_dynamic-update-slice_fusion.refs_0_), channel_id=1, source_target_pairs={{0,1},{1,0},{2,3},{3,2},{4,5},{5,4},{6,7},{7,6},{8,9},{9,8},{10,11... | collective-permute-start | bytes 1769480 | tf_op jit(solution)/shard_map/ppermute | solution.py:43
  40.6 15.0 %collective-permute-start.10 = (bf16[576,512]{1,0:T(8,128)(2,1)S(1)}, bf16[576,512]{1,0:T(8,128)(2,1)S(1)}, u32[]{:S(2)}, u32[]{:S(2)}) collective-permute-start(bf16[576,512]{1,0:T(8,128)(2,1)S(1)} %collective-permute-done.7.refs_1_), channel_id=1, source_target_pairs={{0,1},{1,0},{2,3},{3,2},{4,5},{5,4},{6,7},{7,6},{8,9},{9,8},{10,11... | collective-permute-start | bytes 1769480 | tf_op jit(solution)/shard_map/ppermute | solution.py:43
  41.2 14.4 %collective-permute-start.11 = (bf16[576,512]{1,0:T(8,128)(2,1)S(1)}, bf16[576,512]{1,0:T(8,128)(2,1)S(1)}, u32[]{:S(2)}, u32[]{:S(2)}) collective-permute-start(bf16[576,512]{1,0:T(8,128)(2,1)S(1)} %collective-permute-done.8.refs_2_), channel_id=1, source_target_pairs={{0,1},{1,0},{2,3},{3,2},{4,5},{5,4},{6,7},{7,6},{8,9},{9,8},{10,11... | collective-permute-start | bytes 1769480 | tf_op jit(solution)/shard_map/ppermute | solution.py:43
  41.3 12.0 %collective-permute-start.13 = (bf16[288,512]{1,0:T(8,128)(2,1)S(1)}, bf16[288,512]{1,0:T(8,128)(2,1)}, u32[]{:S(2)}, u32[]{:S(2)}) collective-permute-start(bf16[288,512]{1,0:T(8,128)(2,1)S(1)} %slice.162), channel_id=1, source_target_pairs={{0,4},{1,5},{2,6},{3,7},{4,0},{5,1},{6,2},{7,3},{8,12},{9,13},{10,... | collective-permute-start | bytes 884744 | tf_op jit(solution)/shard_map/ppermute | solution.py:43
  42.1 11.3 %collective-permute-start.12 = (bf16[288,512]{1,0:T(8,128)(2,1)S(1)}, bf16[288,512]{1,0:T(8,128)(2,1)}, u32[]{:S(2)}, u32[]{:S(2)}) collective-permute-start(bf16[288,512]{1,0:T(8,128)(2,1)S(1)} %slice.161), channel_id=1, source_target_pairs={{0,2},{1,3},{2,0},{3,1},{4,6},{5,7},{6,4},{7,5},{8,10},{9,11},{10,... | collective-permute-start | bytes 884744 | tf_op jit(solution)/shard_map/ppermute | solution.py:43
  83.0 7.9 %collective-permute-start.16 = (bf16[4,592,512]{2,1,0:T(8,128)(2,1)}, bf16[4,592,512]{2,1,0:T(8,128)(2,1)S(1)}, u32[]{:S(2)}, u32[]{:S(2)}) collective-permute-start(bf16[4,592,512]{2,1,0:T(8,128)(2,1)} %get-tuple-element.78), channel_id=1, source_target_pairs={{0,1},{1,0},{2,3},{3,2},{4,5},{5,4},{6,7},{7,6},{8,9},{9,8},{10,11... | collective-permute-start | bytes 7274504 | tf_op jit(solution)/shard_map/ppermute | solution.py:43
  96.4 18.1 %collective-permute-start.19 = (bf16[2,296,512]{2,1,0:T(8,128)(2,1)S(1)}, bf16[2,296,512]{2,1,0:T(8,128)(2,1)}, u32[]{:S(2)}, u32[]{:S(2)}) collective-permute-start(bf16[2,296,512]{2,1,0:T(8,128)(2,1)S(1)} %slice.172), channel_id=1, source_target_pairs={{0,2},{1,3},{2,0},{3,1},{4,6},{5,7},{6,4},{7,5},{8,10},{9,11},{10,... | collective-permute-start | bytes 1818632 | tf_op jit(solution)/shard_map/ppermute | solution.py:43
  97.1 18.6 %collective-permute-start.17 = (bf16[2,296,512]{2,1,0:T(8,128)(2,1)}, bf16[2,296,512]{2,1,0:T(8,128)(2,1)S(1)}, u32[]{:S(2)}, u32[]{:S(2)}) collective-permute-start(bf16[2,296,512]{2,1,0:T(8,128)(2,1)} %slice.201), channel_id=1, source_target_pairs={{0,4},{1,5},{2,6},{3,7},{4,0},{5,1},{6,2},{7,3},{8,12},{9,13},{10,... | collective-permute-start | bytes 1818632 | tf_op jit(solution)/shard_map/ppermute | solution.py:43
  115.7 9.0 %collective-permute-start.20 = (bf16[1,296,512]{2,1,0:T(8,128)(2,1)S(1)}, bf16[1,296,512]{2,1,0:T(8,128)(2,1)S(1)}, u32[]{:S(2)}, u32[]{:S(2)}) collective-permute-start(bf16[1,296,512]{2,1,0:T(8,128)(2,1)S(1)} %slice.205), channel_id=1, source_target_pairs={{0,4},{1,5},{2,6},{3,7},{4,0},{5,1},{6,2},{7,3},{8,12},{9,13},{10,... | collective-permute-start | bytes 909320 | tf_op jit(solution)/shard_map/ppermute | solution.py:43
  116.8 8.7 %collective-permute-start.18 = (bf16[1,296,512]{2,1,0:T(8,128)(2,1)S(1)}, bf16[1,296,512]{2,1,0:T(8,128)(2,1)S(1)}, u32[]{:S(2)}, u32[]{:S(2)}) collective-permute-start(bf16[1,296,512]{2,1,0:T(8,128)(2,1)S(1)} %slice.203), channel_id=1, source_target_pairs={{0,2},{1,3},{2,0},{3,1},{4,6},{5,7},{6,4},{7,5},{8,10},{9,11},{10,... | collective-permute-start | bytes 909320 | tf_op jit(solution)/shard_map/ppermute | solution.py:43
  125.6 14.3 %collective-permute-start.24 = (bf16[148,512]{1,0:T(8,128)(2,1)S(1)}, bf16[148,512]{1,0:T(8,128)(2,1)S(1)}, u32[]{:S(2)}, u32[]{:S(2)}) collective-permute-start(bf16[148,512]{1,0:T(8,128)(2,1)S(1)} %dynamic-slice_bitcast_fusion), channel_id=1, source_target_pairs={{0,8},{8,0},{16,24},{24,16},{1,9},{9,1},{17,25},{25,17},{2,10},{10... | collective-permute-start | bytes 454664 | tf_op jit(solution)/shard_map/ppermute | solution.py:39
  127.4 12.5 %collective-permute-start.23 = (bf16[148,512]{1,0:T(8,128)(2,1)S(1)}, bf16[148,512]{1,0:T(8,128)(2,1)S(1)}, u32[]{:S(2)}, u32[]{:S(2)}) collective-permute-start(bf16[148,512]{1,0:T(8,128)(2,1)S(1)} %dynamic-slice_bitcast_fusion.1), channel_id=1, source_target_pairs={{0,8},{8,0},{16,24},{24,16},{1,9},{9,1},{17,25},{25,17},{2,10},{10... | collective-permute-start | bytes 454664 | tf_op jit(solution)/shard_map/ppermute | solution.py:39
  129.4 23.7 %collective-permute-start.22 = (bf16[208,512]{1,0:T(8,128)(2,1)S(1)}, bf16[208,512]{1,0:T(8,128)(2,1)S(1)}, u32[]{:S(2)}, u32[]{:S(2)}) collective-permute-start(bf16[208,512]{1,0:T(8,128)(2,1)S(1)} %get-tuple-element.107), channel_id=1, source_target_pairs={{0,6},{1,7},{2,4},{3,5},{4,2},{5,3},{6,0},{7,1},{8,14},{9,15},{10,... | collective-permute-start | bytes 638984 | tf_op jit(solution)/shard_map/ppermute | solution.py:43
  131.7 21.4 %collective-permute-start.25 = (bf16[208,512]{1,0:T(8,128)(2,1)S(1)}, bf16[208,512]{1,0:T(8,128)(2,1)S(1)}, u32[]{:S(2)}, u32[]{:S(2)}) collective-permute-start(bf16[208,512]{1,0:T(8,128)(2,1)S(1)} %get-tuple-element.108), channel_id=1, source_target_pairs={{0,4},{1,5},{2,6},{3,7},{4,0},{5,1},{6,2},{7,3},{8,12},{9,13},{10,... | collective-permute-start | bytes 638984 | tf_op jit(solution)/shard_map/ppermute | solution.py:43
  132.2 20.9 %collective-permute-start.26 = (bf16[208,512]{1,0:T(8,128)(2,1)S(1)}, bf16[208,512]{1,0:T(8,128)(2,1)S(1)}, u32[]{:S(2)}, u32[]{:S(2)}) collective-permute-start(bf16[208,512]{1,0:T(8,128)(2,1)S(1)} %get-tuple-element.109), channel_id=1, source_target_pairs={{0,2},{1,3},{2,0},{3,1},{4,6},{5,7},{6,4},{7,5},{8,10},{9,11},{10,... | collective-permute-start | bytes 638984 | tf_op jit(solution)/shard_map/ppermute | solution.py:43
  140.0 12.9 %collective-permute-start.30 = (bf16[148,512]{1,0:T(8,128)(2,1)S(1)}, bf16[148,512]{1,0:T(8,128)(2,1)S(1)}, u32[]{:S(2)}, u32[]{:S(2)}) collective-permute-start(bf16[148,512]{1,0:T(8,128)(2,1)S(1)} %fusion.6), channel_id=1, source_target_pairs={{0,16},{8,24},{16,0},{24,8},{1,17},{9,25},{17,1},{25,9},{2,18},{10... | collective-permute-start | bytes 454664 | tf_op jit(solution)/shard_map/ppermute | solution.py:39
  142.7 21.8 %collective-permute-start.29 = (bf16[148,512]{1,0:T(8,128)(2,1)S(1)}, bf16[148,512]{1,0:T(8,128)(2,1)S(1)}, u32[]{:S(2)}, u32[]{:S(2)}) collective-permute-start(bf16[148,512]{1,0:T(8,128)(2,1)S(1)} %fusion.7), channel_id=1, source_target_pairs={{0,16},{8,24},{16,0},{24,8},{1,17},{9,25},{17,1},{25,9},{2,18},{10... | collective-permute-start | bytes 454664 | tf_op jit(solution)/shard_map/ppermute | solution.py:39
  153.2 9.9 %collective-permute-start.27 = (bf16[104,512]{1,0:T(8,128)(2,1)S(1)}, bf16[104,512]{1,0:T(8,128)(2,1)S(1)}, u32[]{:S(2)}, u32[]{:S(2)}) collective-permute-start(bf16[104,512]{1,0:T(8,128)(2,1)S(1)} %constant_dynamic-slice_fusion.8), channel_id=1, source_target_pairs={{0,8},{8,0},{16,24},{24,16},{1,9},{9,1},{17,25},{25,17},{2,10},{10... | collective-permute-start | bytes 319496 | tf_op jit(solution)/shard_map/ppermute | solution.py:39
  (31 other events, 158.2 us)

commit v4 on v3

--- a/solution.py
+++ b/solution.py
@@ -82,20 +82,15 @@
     return (a.astype(f32) + b.astype(f32)).astype(bf16)
 
 
-def spread_sum(parts, *gate):
-    got = [swap(parts[k], 2 * k) for k in range(len(parts) - 1, 0, -1)]
-    if gate:
-        got = [after(a, *gate) for a in got]
-    t = parts[0].astype(f32)
+def spread(parts):
+    return [swap(parts[k], 2 * k) for k in range(len(parts) - 1, 0, -1)]
+
+
+def total(own, got):
+    t = own.astype(f32)
     for a in got:
         t = t + a.astype(f32)
     return t.astype(bf16)
-
-
-def halve(s, top, bit):
-    m = s.shape[0] // 2
-    keep, out = (s[:m], s[m:]) if top else (s[0::2], s[1::2])
-    return keep, swap(out, bit)
 
 
 def rep_half(x):
@@ -103,7 +98,7 @@
     odd = lax.axis_index("rep") % 2
     mine = lax.dynamic_slice_in_dim(x, odd * h, h, 0)
     other = lax.dynamic_slice_in_dim(x, (1 - odd) * h, h, 0)
-    return mine, rep_perm(other, 1)
+    return mine, rep_perm(other, 1), other
 
 
 def rep_steps():
@@ -111,26 +106,156 @@
     return [b for b in (2 << i for i in range(16)) if b < nr]
 
 
-def rep_join(s, o):
-    odd = lax.axis_index("rep") % 2
-    lo = jnp.where(odd == 0, s, o)
-    hi = jnp.where(odd == 0, o, s)
-    return jnp.concatenate([lo, hi], axis=0).astype(f32)
-
-
-def vector_block(vecs, upb, n):
-    me = lax.axis_index("shard")
+def pack_first_body(me, w, upb, *refs):
+    vecs = refs[:-1]
+    out = refs[-1]
+    r, W = w.shape
+    D = out.shape[1]
+    for j in range(W // D):
+        out[j * r : (j + 1) * r, :] = w[:, j * D : (j + 1) * D]
 
     def spot(v):
-        w = v.shape[1]
-        if w >= LANES:
-            return v.reshape(-1, LANES)
-        t = LANES // w
-        lane = lax.broadcasted_iota(jnp.int32, (v.shape[0], LANES), 1)
-        return jnp.where(lane // w == me % t, jnp.concatenate([v] * t, axis=1), jnp.zeros((), bf16))
-
-    b = jnp.concatenate([spot(jnp.stack(vecs)), spot(upb[None])], axis=0)
-    return jnp.pad(b, ((0, VROWS - b.shape[0]), (0, 0)))
+        w_ = v.shape[1]
+        if w_ >= LANES:
+            return [v[:, q * LANES : (q + 1) * LANES] for q in range(w_ // LANES)]
+        t = LANES // w_
+        lane = lax.broadcasted_iota(jnp.int32, (1, LANES), 1)
+        return [jnp.where(lane // w_ == me[0] % t, jnp.concatenate([v] * t, axis=1), jnp.zeros((1, LANES), f32))]
+
+    rows = [a for v in vecs for a in spot(v[...].astype(f32))] + spot(upb[...].astype(f32))
+    b = jnp.concatenate(rows + [jnp.zeros((VROWS - len(rows), LANES), f32)], axis=0).astype(bf16)
+    out[W // D * r :, :] = jnp.concatenate([b, jnp.zeros((VROWS, D - LANES), bf16)], axis=1)
+
+
+def whole(n):
+    return [pl.BlockSpec(memory_space=pltpu.VMEM)] * n
+
+
+def pack_first(me, w, vecs, upb, D):
+    return pl.pallas_call(
+        pack_first_body,
+        in_specs=[pl.BlockSpec(memory_space=pltpu.SMEM)] + whole(2 + len(vecs)), out_specs=whole(1)[0],
+        out_shape=S((w.size // D + VROWS, D), bf16), compiler_params=pltpu.CompilerParams(vmem_limit_bytes=8 << 20), name="pack_first", cost_estimate=cost(0, 4 * w.size),
+    )(me, w, upb[None], *[v[None] for v in vecs])
+
+
+def pack_rest_body(wo, wu, wd, out):
+    r, D = wo.shape
+    out[:r, :] = wo[...]
+    for j in range(wu.shape[1] // D):
+        out[(1 + j) * r : (2 + j) * r, :] = wu[:, j * D : (j + 1) * D]
+    out[(1 + wu.shape[1] // D) * r :, :] = wd[...]
+
+
+def pack_rest(wo, wu, wd):
+    D = wo.shape[1]
+    return pl.pallas_call(
+        pack_rest_body, in_specs=whole(3), out_specs=whole(1)[0],
+        out_shape=S(((wo.size + wu.size + wd.size) // D, D), bf16), compiler_params=pltpu.CompilerParams(vmem_limit_bytes=8 << 20), name="pack_rest", cost_estimate=cost(0, 4 * wu.size),
+    )(wo, wu, wd)
+
+
+def own_lanes(tiles, me, w):
+    pick = lambda i: sum(jnp.where(i == t, a, jnp.zeros_like(a)) for t, a in enumerate(tiles))
+    if w >= LANES:
+        q = w // LANES
+        return jnp.concatenate([pick(me * q + c) for c in range(q)], axis=1)
+    per = LANES // w
+    x = pick(me // per)
+    off = me % per
+    return sum(jnp.where(off == o, x[:, o * w : (o + 1) * w], 0.0) for o in range(per))
+
+
+def rows_of(lo, hi, a, b):
+    h = lo.shape[0]
+    if b <= h:
+        return lo[a:b, :]
+    if a >= h:
+        return hi[a - h : b - h, :]
+    return jnp.concatenate([lo[a:h, :], hi[: b - h, :]], axis=0)
+
+
+def finish_rest_body(r, rf, n, ids, sa, oa, sb, ob, down, up, out, upb, *vecs):
+    D = out.shape[1]
+    nf = up.shape[1] // D
+
+    def run(la, ha, lb, hb):
+        f = lambda x, y, a, b: rows_of(x, y, a, b).astype(f32)
+        down[...] = f(la, ha, 0, rf)
+        out[...] = f(la, ha, rf, rf + r)
+        for j in range(nf):
+            up[:, j * D : (j + 1) * D] = f(lb, hb, j * r, (j + 1) * r)
+        v = f(lb, hb, nf * r, nf * r + VROWS)
+        me = ids[0]
+        tiles = [v[0:8, t * LANES : (t + 1) * LANES] for t in range(D // LANES)]
+        x = own_lanes(tiles, me, r)
+        for q, ref in enumerate(vecs):
+            ref[...] = x[q : q + 1, :]
+        tiles = [v[4 + q : 5 + q, t * LANES : (t + 1) * LANES] for q in range(nf) for t in range(D // LANES)]
+        upb[...] = own_lanes(tiles, me, nf * D // n)
+
+    @pl.when(ids[1] == 0)
+    def _():
+        run(sa, oa, sb, ob)
+
+    @pl.when(ids[1] == 1)
+    def _():
+        run(oa, sa, ob, sb)
+
+
+def finish_rest(ids, sa, oa, sb, ob, r, rf, nf, n):
+    D = sa.shape[1]
+    row1 = lambda w: S((1, w), f32)
+    return pl.pallas_call(
+        functools.partial(finish_rest_body, r, rf, n),
+        in_specs=[pl.BlockSpec(memory_space=pltpu.SMEM)] + whole(4), out_specs=whole(8),
+        out_shape=[S((rf, D), f32), S((r, nf * D), f32), S((r, D), f32), row1(nf * D // n)] + [row1(r)] * 4,
+        compiler_params=pltpu.CompilerParams(vmem_limit_bytes=16 << 20), name="finish_rest", cost_estimate=cost(0, 8 * sa.size),
+    )(ids, sa, oa, sb, ob)
+
+
+def finish_first_body(ids, s, o, w, gain, bias, qkv, gg, gb, qb, vb):
+    r, W = w.shape
+    D = s.shape[1]
+
+    def run(lo, hi):
+        f = lambda a, b: rows_of(lo, hi, a, b).astype(f32)
+        v = f(3 * r, 3 * r + VROWS)
+        nt = D // LANES
+        accg = accb = jnp.zeros((r, LANES), f32)
+        col = lambda g: jnp.concatenate([g[...].astype(f32), jnp.zeros((7, r), f32)], axis=0).T[:, 0:1]
+        cg, cb = col(gain), col(bias)
+        for j in range(3):
+            m = f(j * r, (j + 1) * r)
+            sq = v[j : j + 1, :]
+            ww = w[:, j * D : (j + 1) * D].astype(f32)
+            qkv[:, j * D : (j + 1) * D] = cg * m + cb * sq
+            pg, pb = ww * m, ww * sq
+            accg = accg + sum(pg[:, t * LANES : (t + 1) * LANES] for t in range(nt))
+            accb = accb + sum(pb[:, t * LANES : (t + 1) * LANES] for t in range(nt))
+        gg[...] = jnp.sum(accg.T, axis=0, keepdims=True)
+        gb[...] = jnp.sum(accb.T, axis=0, keepdims=True)
+        x = own_lanes([v[0:8, t * LANES : (t + 1) * LANES] for t in range(nt)], ids[0], r)
+        qb[...] = x[0:1, :]
+        vb[...] = x[2:3, :]
+
+    @pl.when(ids[1] == 0)
+    def _():
+        run(s, o)
+
+    @pl.when(ids[1] == 1)
+    def _():
+        run(o, s)
+
+
+def finish_first(ids, s, o, w, gain, bias):
+    r, W = w.shape
+    return pl.pallas_call(
+        finish_first_body,
+        in_specs=[pl.BlockSpec(memory_space=pltpu.SMEM)] + whole(5), out_specs=whole(5),
+        out_shape=[S((r, W), f32)] + [S((1, r), f32)] * 4,
+        compiler_params=pltpu.CompilerParams(vmem_limit_bytes=16 << 20), name="finish_first", cost_estimate=cost(0, 8 * w.size),
+    )(ids, s, o, w, gain[None], bias[None])
 
 
 def pull(me, refs, meta, segs, sems):
@@ -304,9 +429,18 @@
 G0 = math.sqrt(2 / math.pi)
 
 
-def push(me, n, s, src, keep, send, row0, sem):
+def bit_reverse(x, m):
+    y = jnp.zeros_like(x)
+    for t in range(m):
+        y = y | (((x >> t) & 1) << (m - 1 - t))
+    return y
+
+
+def push(me, n, s, src, keep, send, row0, sem, reverse=False):
     k = jnp.bitwise_xor(me, s)
     p = k >> 1
+    if reverse:
+        p = bit_reverse(p, (n // 2).bit_length() - 1)
     put = lambda dst: pltpu.make_async_copy(src, dst.at[p, pl.ds(row0, src.shape[0])], sem)
 
     @pl.when(k & 1 == 0)
@@ -387,20 +521,20 @@
     @pl.when(i == pl.num_programs(0) - 1)
     def _():
         per = D // rf
-        o_up, o_out, o_vec = rf, rf + nf * r, rf + (nf + 1) * r
+        o_out, o_up, o_vec = rf, rf + r, rf + (nf + 1) * r
         for j in range(nf):
             dn[j] = dot(gdt[...], act[:, j * D : (j + 1) * D]).astype(bf16).T
             for t in range(per):
                 push(i0, n, j * per + t, dn.at[j, pl.ds(t * rf, rf)], keep, send, 0, psems.at[j * per + t])
             up[j] = dot(h2t[...], gup[:, j * D : (j + 1) * D]).astype(bf16)
             for s in range(n):
-                push(i0, n, s, up.at[j, pl.ds(s * r, r)], keep, send, o_up + j * r, psems.at[n * (1 + j) + s])
+                push(i0, n, s, up.at[j, pl.ds(s * r, r)], keep, send, o_up + j * r, psems.at[n * (1 + j) + s], True)
         gwo[...] = dot(mixedt[...], gattn[...]).astype(bf16)
         vr[...] = jnp.concatenate([sums[0:4, :]] + [upsum[:, c * D : (c + 1) * D] for c in range(nf)] + [jnp.zeros((VROWS - 4 - nf, D), f32)], axis=0).astype(bf16)
         b = n * (1 + nf)
         for s in range(n):
             push(i0, n, s, gwo.at[pl.ds(s * r, r)], keep, send, o_out, psems.at[b + s])
-            push(i0, n, s, vr, keep, send, o_vec, psems.at[b + n + s])
+            push(i0, n, s, vr, keep, send, o_vec, psems.at[b + n + s], True)
         done = lambda src, q: pltpu.make_async_copy(src, keep.at[0, pl.ds(0, src.shape[0])], psems.at[q]).wait()
         for s in range(n):
             done(dn.at[0, pl.ds(0, rf)], s)
@@ -543,10 +677,9 @@
     r = D // n
     FF = up_bias.shape[0] * n
     nc = FF // D
-    vb = vector_block([ln1_gain, ln1_bias, q_bias, v_bias, out_bias, ln2_gain, ln2_bias, down_bias], up_bias, n)
-    cols = lambda a: [a[:, j * D : (j + 1) * D] for j in range(a.shape[1] // D)]
-    pack1 = jnp.concatenate(cols(qkv_weight) + [jnp.pad(vb, ((0, 0), (0, D - LANES)))], axis=0)
-    pack2 = jnp.concatenate([out_weight] + cols(up_weight) + [down_weight], axis=0)
+    rf = FF // n
+    pack1 = pack_first(mes, qkv_weight, [ln1_gain, ln1_bias, q_bias, v_bias, out_bias, ln2_gain, ln2_bias, down_bias], up_bias, D)
+    pack2 = pack_rest(out_weight, up_weight, down_weight)
     pieces1 = gather_direct(pack1, n)
     xht, kv, qkvt, w, vec, upb = front(mes, tok, step, pieces1, n, FF)
     NP = HEADS // 2
@@ -556,55 +689,52 @@
     pieces2 = gather_forward(after(pack2, *[a for _, _, a in pieces1[1:]]), n, fw[4], linv)
     out, gx1, gmt, keep, send = ffn(lengths, mes, tok, step, vec, upb, cot, mixed, mixedt, pieces2, n)
     bwd = lambda p, c, g, *deps: attn_bwd(kv, qkvt, after(gmt, *deps) if deps else gmt, mixedf, linv, et, p, c, g)
-    R = keep.shape[1]
-    ra = R // 2 // 8 * 8
+    ra = rf + r
     got = swap(send, 1)
     g = bwd(0, 1, [])
     got = after(got, g)
-    sa = add16(keep[:, :ra], got[:, :ra])
-    sb = add16(keep[:, ra:], got[:, ra:])
-    g = bwd(1, NP - 1, [g], sa, sb)
+    h = n // 4
+    add = lambda a, b, k: add16(a[k], b[k])
+    rows_a, rows_b = slice(0, ra), slice(ra, None)
+    lo, hi = slice(0, h), slice(h, None)
+    ka, xa, kb, xb = [add(keep, got, k) for k in ((lo, rows_a), (hi, rows_a), (lo, rows_b), (hi, rows_b))]
+    g = bwd(1, NP - 1, [g], ka, xa, kb, xb)
     m = (n // 2).bit_length() - 1
-    for t in range(m):
-        ka, ga = halve(sa, True, 1 << (m - t))
-        kb, gb = halve(sb, False, 2 << t)
-        dep = g if t == 0 else keep
-        sa = add16(ka, after(ga, dep))
-        sb = add16(kb, after(gb, dep))
-        if t == 0:
-            keep, send = wqkv(mes, after(xht, sa, sb), g, n)
-    ua, ub = sa[0], sb[0]
-    got = after(swap(send, 1), ua, ub)
-    parts = [add16(keep[k], got[k]) for k in range(n // 2)]
-    ma, ga = rep_half(ua)
-    mb, gb = rep_half(ub)
-    tg = back(tok, after(step, ua, ub, *parts), vec, w, g, gx1)
-    za = add16(ma, after(ga, tg))
-    zb = add16(mb, after(gb, tg))
-    own2 = spread_sum(parts, za, zb)
-    m2, g2 = rep_half(own2)
-    z2 = add16(m2, g2)
+    ga, gb = swap(xa, 2 << (m - 1)), swap(xb, 2)
+    for t in range(1, m):
+        dep = g if t == 1 else keep
+        ga, gb = after(ga, dep), after(gb, dep)
+        h //= 2
+        lo, hi = slice(0, h), slice(h, None)
+        ka, xa = add(ka, ga, lo), add(ka, ga, hi)
+        kb, xb = add(kb, gb, lo), add(kb, gb, hi)
+        ga, gb = swap(xa, 2 << (m - 1 - t)), swap(xb, 2 << t)
+        if t == 1:
+            keep, send = wqkv(mes, after(xht, ka, xa, kb, xb), g, n)
+    got = swap(send, 1)
+    p2 = [add16(keep[k], got[k]) for k in range(n // 2)]
+    far2 = spread(p2)
+    ua = add16(ka, after(ga, keep))[0]
+    ub = add16(kb, after(gb, keep))[0]
+    ma, oa, xa = rep_half(ua)
+    mb, ob, xb = rep_half(ub)
+    tg = back(tok, after(step, xa, xb), vec, w, g, gx1)
+    za = add16(ma, after(oa, tg))
+    zb = add16(mb, after(ob, tg))
+    own2 = total(p2[0], [after(a, za, zb) for a in far2])
+    m2, o2, _ = rep_half(own2)
+    z2 = add16(m2, o2)
     for b in rep_steps():
-        za = add16(za, after(rep_perm(za, b), z2))
-        zb = add16(zb, rep_perm(zb, b))
-        z2 = add16(z2, after(rep_perm(z2, b), za, zb))
-    z1 = jnp.concatenate([rep_join(za, rep_perm(za, 1)), rep_join(zb, rep_perm(zb, 1))], axis=0)
-    z2 = rep_join(z2, rep_perm(z2, 1))
-    rf = FF // n
-    g_down = z1[:rf]
-    wide = lambda a, c: jnp.concatenate([a[j * r : (j + 1) * r] for j in range(c)], axis=1)
-    g_up = wide(z1[rf:], nc)
-    g_out = z1[rf + nc * r : rf + (nc + 1) * r]
-    small = z1[rf + (nc + 1) * r :]
-    own = lambda a: lax.dynamic_slice(a, (me * r,), (r,))
-    g_upb = lax.dynamic_slice(small[4 : 4 + nc].reshape(-1), (me * (FF // n),), (FF // n,))
-    m = wide(z2, 3)
-    sq = z2[3 * r : 3 * r + 3].reshape(1, 3 * D)
-    wf = qkv_weight.astype(f32)
-    g_qkv = ln1_gain.astype(f32)[:, None] * m + ln1_bias.astype(f32)[:, None] * sq
-    g_g1 = jnp.sum(wf * m, axis=1)
-    g_b1 = jnp.sum(wf * sq, axis=1)
-    return (out[None], tg[None], g_g1, g_b1, g_qkv, own(z2[3 * r]), own(z2[3 * r + 2]), g_out, own(small[0]), own(small[1]), own(small[2]), g_up, g_upb, g_down, own(small[3]))
+        pa, pb = rep_perm(za, b), rep_perm(zb, b)
+        za = add16(za, after(pa, z2))
+        z2 = add16(z2, after(rep_perm(z2, b), za))
+        zb = add16(zb, after(pb, z2))
+    oa, ob, o2 = rep_perm(za, 1), rep_perm(zb, 1), rep_perm(z2, 1)
+    ids = jnp.stack([me, (lax.axis_index("rep") % 2).astype(jnp.int32)])
+    g_qkv, g_g1, g_b1, g_q, g_v = finish_first(ids, z2, o2, qkv_weight, ln1_gain, ln1_bias)
+    g_down, g_up, g_out, g_upb, g_ob, g_g2, g_b2, g_db = finish_rest(ids, za, oa, zb, ob, r, rf, nc, n)
+    flat = lambda a: a.reshape(-1)
+    return (out[None], tg[None], flat(g_g1), flat(g_b1), g_qkv, flat(g_q), flat(g_v), g_out, flat(g_ob), flat(g_g2), flat(g_b2), g_up, flat(g_upb), g_down, flat(g_db))
 
 
 def solution(mesh):

time: 178 us -> 185 us (1.039)
  waiting for transfers between devices: 29.3 us -> 39.8 us
  other arithmetic: 10.4 us -> 5.96 us
  local copies, waits for them, and re-layouts: 15.1 us -> 10.8 us
  Pallas kernels: 90.4 us -> 93.9 us
  starting transfers between devices: 29.8 us -> 32.4 us
    ppermute x25, waiting for transfers between devices: 9.64 us -> 19.5 us  [swap(): return lax.ppermute(x, 'shard', xor_perm(lax.axis_size('shard'), k))]
    slice x9 -> x0, local copies, waits for them, and re-layouts: 3.42 us -> none  [the longest x4 0.93 us: halve(): keep, out = (s[:m], s[m:]) if top else (s[0::2], s[1::2])]
    pallas_call x0 -> x4, Pallas kernels: none -> 3.39 us  [the longest x1 1.71 us: finish_rest(): pl.pallas_call(functools.partial(finish_rest_body, r, rf, n), in_specs=[p...]
    unnamed x49 -> x64, local copies, waits for them, and re-layouts: 6.77 us -> 10 us
    dynamic_slice x5 -> x0, local copies, waits for them, and re-layouts: 2.96 us -> none  [the longest x4 2.33 us: shards(): own = lambda a: lax.dynamic_slice(a, (me * r,), (r,))]
    ppermute x9, starting transfers between devices: 11.3 us -> 13.8 us  [rep_perm(): return lax.ppermute(x, 'rep', xor_perm(lax.axis_size('rep'), b))]
    convert_element_type x12 -> x13, other arithmetic: 6.36 us -> 5.75 us  [add16(): return (a.astype(f32) + b.astype(f32)).astype(bf16)]
  transfers between devices with their start and end apart: 34 -> 34, of which waited for: 11 -> 12; matrix products, arithmetic and copies ran while one was open for 8% -> 0% of each run, Pallas kernels for 36% -> 36%
where the time goes in v4:
time: 185 us
  Pallas kernels  93.9 us (51%)
  waiting for transfers between devices  39.8 us (22%)
  starting transfers between devices  32.4 us (18%)
  local copies, waits for them, and re-layouts  10.8 us (6%)
  other arithmetic  5.96 us (3%)
    pallas_call x1, Pallas kernels, ffn(): pl.pallas_call(functools.partial(ffn_body, n, meta, min(1024, FF)), grid_...  26.3 us
    pallas_call x2, Pallas kernels, attn_bwd(): pl.pallas_call(functools.partial(attn_bwd_body, HD, 1.0 / math.sqrt(HD),...  23.9 us
    ppermute x9, waiting for transfers between devices, rep_perm(): return lax.ppermute(x, 'rep', xor_perm(lax.axis_size('rep'), b))  20.3 us
    pallas_call x2, Pallas kernels, attn_fwd(): pl.pallas_call(functools.partial(attn_fwd_body, HD, bi, min(256, T)), gri...  19.9 us
    ppermute x25, waiting for transfers between devices, swap(): return lax.ppermute(x, 'shard', xor_perm(lax.axis_size('shard'), k))  19.5 us
    ppermute x25, starting transfers between devices, swap(): return lax.ppermute(x, 'shard', xor_perm(lax.axis_size('shard'), k))  18.5 us
    ppermute x9, starting transfers between devices, rep_perm(): return lax.ppermute(x, 'rep', xor_perm(lax.axis_size('rep'), b))  13.8 us
    unnamed x64, local copies, waits for them, and re-layouts  10 us
  transfers between devices with their start and end apart: 34, of which 12 were waited for; matrix products, arithmetic and copies ran while one was open for 0% of the time, Pallas kernels for 36%

profile of v4, /device:TPU:0, one launch (start us, length us, event | category | flops | bytes accessed | tf_op | source)
XLA Modules:
  0.0 184.6 jit_solution(13408562845344779629)
XLA Ops:
  7.6 3.0 %collective-permute-start = (bf16[208,512]{1,0:T(8,128)(2,1)S(1)}, bf16[208,512]{1,0:T(8,128)(2,1)S(1)}, u32[]{:S(2)}, u32[]{:S(2)}) collective-permute-start(bf16[208,512]{1,0:T(8,128)(2,1)S(1)} %pack_first.1.refs_0_), channel_id=1, source_target_pairs={{0,2},{1,3},{2,0},{3,1},{4,6},{5,7},{6,4},{7,5},{8,10},{9,11},{10,... | collective-permute-start | bytes 638984 | tf_op jit(solution)/shard_map/ppermute | solution.py:43
  12.1 4.5 %collective-permute-done.refs_1_ = bf16[208,512]{1,0:T(8,128)(2,1)S(1)} collective-permute-done((bf16[208,512]{1,0:T(8,128)(2,1)S(1)}, bf16[208,512]{1,0:T(8,128)(2,1)S(1)}, u32[]{:S(2)}, u32[]{:S(2)}) %collective-permute-start) | collective-permute-done | bytes 213024 | tf_op jit(solution)/shard_map/ppermute | solution.py:43
  16.7 5.2 %collective-permute-done.1.refs_2_ = bf16[208,512]{1,0:T(8,128)(2,1)S(1)} collective-permute-done((bf16[208,512]{1,0:T(8,128)(2,1)S(1)}, bf16[208,512]{1,0:T(8,128)(2,1)S(1)}, u32[]{:S(2)}, u32[]{:S(2)}) %collective-permute-start.1) | collective-permute-done | bytes 213024 | tf_op jit(solution)/shard_map/ppermute | solution.py:43
  28.2 7.8 %front.1 = (bf16[512,1024]{1,0:T(8,128)(2,1)}, bf16[1024,1024]{1,0:T(8,128)(2,1)}, bf16[1536,1024]{1,0:T(8,128)(2,1)}, bf16[512,1536]{1,0:T(8,128)(2,1)}, f32[8,512]{1,0:T(8,128)}, /*index=5*/f32[1,2048]{1,0:T(1,128)}) custom-call(s32[1]{0:T(128)} %bitcast.me, bf16[1024,512]{1,0:T(8,128)(2,1)} %bitcast.55, bf16[1,512]{1,0:T(2,128)(2,1)} %step.4, ...), custom_call_target="tpu_custom_call" | custom-call | flops 1610612736 | bytes 10485760 | tf_op jit(solution)/shard_map/front/pallas_call | solution.py:342
  35.9 10.0 %attn_fwd.2 = (bf16[8,1024,1024]{2,1,0:T(8,128)(2,1)}, bf16[1024,512]{1,0:T(8,128)(2,1)}, bf16[512,1024]{1,0:T(8,128)(2,1)}, f32[512,1024]{1,0:T(8,128)}, f32[4,8,1024]{2,1,0:T(8,128)}) custom-call(s32[1]{0:T(128)S(6)} %copy.44.ln, bf16[1024,1024]{1,0:T(8,128)(2,1)} %get-tuple-element.74.k.v, bf16[1536,1024]{1,0:T(8,128)(2,1)} %get-tuple-element.75.qt.vt.kt, ...), custom_call_target="tpu_custom_call" | custom-call | flops 4294967296 | bytes 8388608 | tf_op jit(solution)/shard_map/attn_fwd/pallas_call | solution.py:416
  48.7 9.9 %attn_fwd.3 = (bf16[8,1024,1024]{2,1,0:T(8,128)(2,1)}, bf16[1024,512]{1,0:T(8,128)(2,1)}, bf16[512,1024]{1,0:T(8,128)(2,1)}, f32[512,1024]{1,0:T(8,128)}, f32[4,8,1024]{2,1,0:T(8,128)}) custom-call(s32[1]{0:T(128)S(6)} %copy.44.ln, ...), custom_call_target="tpu_custom_call", output_to_operand_aliasing={{0}: (4, {}), {1}: (5, {}), {2}: (6, {}), {3}: (7, {}), {4}... | custom-call | flops 4294967296 | bytes 8388608 | tf_op jit(solution)/shard_map/attn_fwd/pallas_call | solution.py:416
  62.0 26.3 %ffn.1 = (bf16[1024,512]{1,0:T(8,128)(2,1)}, f32[1024,512]{1,0:T(8,128)}, bf16[512,1024]{1,0:T(8,128)(2,1)}, bf16[4,592,512]{2,1,0:T(8,128)(2,1)}, bf16[4,592,512]{2,1,0:T(8,128)(2,1)}) custom-call(s32[1]{0:T(128)S(6)} %copy.44.ln, s32[1]{0:T(128)} %bitcast.me, bf16[1024,512]{1,0:T(8,128)(2,1)} %bitcast.56, bf16[1,512]{1,0:T(2,128)(2,1)} %step.4, ...), custom_call_target="tpu_custom_call" | custom-call | flops 14495514624 | bytes 8388608 | tf_op jit(solution)/shard_map/ffn/pallas_call | solution.py:558
  88.6 7.8 %attn_bwd.2.refs_0_ = bf16[3,512,1024]{2,1,0:T(8,128)(2,1)} custom-call(bf16[1024,1024]{1,0:T(8,128)(2,1)} %get-tuple-element.74.k.v, bf16[1536,1024]{1,0:T(8,128)(2,1)} %get-tuple-element.75.qt.vt.kt, bf16[1536,1024]{1,0:T(8,128)(2,1)} %get-tuple-element.75.qt.vt.kt, bf16[512,1024]{1,0:T(8,128)(2,1)} %get-tuple-element.96.gt, ...), custom_call_target="tpu_custom_call" | custom-call | flops 4294967296 | bytes 4194304 | tf_op jit(solution)/shard_map/attn_bwd/pallas_call | solution.py:602
  96.4 2.4 %add_convert_fusion.2 = (bf16[2,272,512]{2,1,0:T(8,128)(2,1)}, bf16[2,272,512]{2,1,0:T(8,128)(2,1)S(1)}) fusion(bf16[4,592,512]{2,1,0:T(8,128)(2,1)} %collective-permute-done.16, bf16[4,592,512]{2,1,0:T(8,128)(2,1)S(1)} %copy-done.17), kind=kLoop, calls=%fused_computation.2 | loop fusion | flops 2228224 | bytes 3342336 | tf_op jit(solution)/shard_map/convert_element_type | solution.py:82
  98.8 2.5 %add_convert_fusion = (bf16[2,320,512]{2,1,0:T(8,128)(2,1)}, bf16[2,320,512]{2,1,0:T(8,128)(2,1)S(1)}) fusion(bf16[4,592,512]{2,1,0:T(8,128)(2,1)} %collective-permute-done.16, bf16[4,592,512]{2,1,0:T(8,128)(2,1)S(1)} %copy-done.17), kind=kLoop, calls=%fused_computation | loop fusion | flops 2621440 | bytes 3932160 | tf_op jit(solution)/shard_map/convert_element_type | solution.py:82
  103.3 16.0 %attn_bwd.3.g = bf16[3,512,1024]{2,1,0:T(8,128)(2,1)} custom-call(bf16[1024,1024]{1,0:T(8,128)(2,1)} %get-tuple-element.74.k.v, bf16[1536,1024]{1,0:T(8,128)(2,1)} %get-tuple-element.75.qt.vt.kt, bf16[1536,1024]{1,0:T(8,128)(2,1)} %get-tuple-element.75.qt.vt.kt, bf16[512,1024]{1,0:T(8,128)(2,1)} %get-tuple-element.96.gt, ...), custom_call_target="tpu_custom_call", output_to_operand_aliasing={{}: (7, {})} | custom-call | flops 12884901888 | bytes 12582912 | tf_op jit(solution)/shard_map/attn_bwd/pallas_call | solution.py:602
  121.8 5.7 %wqkv.1 = (bf16[4,208,512]{2,1,0:T(8,128)(2,1)}, bf16[4,208,512]{2,1,0:T(8,128)(2,1)}) custom-call(s32[1]{0:T(128)} %bitcast.me, bf16[512,1024]{1,0:T(8,128)(2,1)} %get-tuple-element.100.xht, bf16[3,512,1024]{2,1,0:T(8,128)(2,1)} %attn_bwd.3.g), custom_call_target="tpu_custom_call" | custom-call | flops 1610612736 | bytes 5242880 | tf_op jit(solution)/shard_map/wqkv/pallas_call | solution.py:639
  128.0 1.6 collective-permute-start.24
  129.9 1.7 collective-permute-start.23
  131.5 7.0 %back.1 = f32[1024,512]{1,0:T(8,128)} custom-call(bf16[1024,512]{1,0:T(8,128)(2,1)} %bitcast.57, bf16[1,512]{1,0:T(2,128)(2,1)} %step.4, f32[8,512]{1,0:T(8,128)} %get-tuple-element.72.vec, bf16[512,1536]{1,0:T(8,128)(2,1)} %get-tuple-element.105.w, bf16[3,512,1024]{2,1,0:T(8,128)(2,1)} %attn_bwd.3.g, f32[1024,512]{1,0:T(8,128)} %get-tuple-element.106.gx1), custom_call_target="tpu_custom_call" | custom-call | flops 1610612736 | bytes 7340032 | tf_op jit(solution)/shard_map/back/pallas_call | solution.py:664
  138.8 2.2 %collective-permute-start.22 = (bf16[208,512]{1,0:T(8,128)(2,1)S(1)}, bf16[208,512]{1,0:T(8,128)(2,1)S(1)}, u32[]{:S(2)}, u32[]{:S(2)}) collective-permute-start(bf16[208,512]{1,0:T(8,128)(2,1)S(1)} %get-tuple-element.133), channel_id=1, source_target_pairs={{0,6},{1,7},{2,4},{3,5},{4,2},{5,3},{6,0},{7,1},{8,14},{9,15},{10,... | collective-permute-start | bytes 638984 | tf_op jit(solution)/shard_map/ppermute | solution.py:43
  142.4 5.2 %collective-permute-done.22 = bf16[208,512]{1,0:T(8,128)(2,1)S(1)} collective-permute-done((bf16[208,512]{1,0:T(8,128)(2,1)S(1)}, bf16[208,512]{1,0:T(8,128)(2,1)S(1)}, u32[]{:S(2)}, u32[]{:S(2)}) %collective-permute-start.22) | collective-permute-done | bytes 213024 | tf_op jit(solution)/shard_map/ppermute | solution.py:43
  147.7 2.2 %collective-permute-done.25 = bf16[208,512]{1,0:T(8,128)(2,1)S(1)} collective-permute-done((bf16[208,512]{1,0:T(8,128)(2,1)S(1)}, bf16[208,512]{1,0:T(8,128)(2,1)S(1)}, u32[]{:S(2)}, u32[]{:S(2)}) %collective-permute-start.25) | collective-permute-done | bytes 213024 | tf_op jit(solution)/shard_map/ppermute | solution.py:43
  150.2 1.6 collective-permute-start.27
  151.9 2.6 %collective-permute-start.32 = (bf16[136,512]{1,0:T(8,128)(2,1)S(1)}, bf16[136,512]{1,0:T(8,128)(2,1)S(1)}, u32[]{:S(2)}, u32[]{:S(2)}) collective-permute-start(bf16[136,512]{1,0:T(8,128)(2,1)S(1)} %fusion.4), channel_id=1, source_target_pairs={{0,16},{8,24},{16,0},{24,8},{1,17},{9,25},{17,1},{25,9},{2,18},{10... | collective-permute-start | bytes 417800 | tf_op jit(solution)/shard_map/ppermute | solution.py:39
  155.0 3.8 %collective-permute-start.28 = (bf16[104,512]{1,0:T(8,128)(2,1)S(1)}, bf16[104,512]{1,0:T(8,128)(2,1)S(1)}, u32[]{:S(2)}, u32[]{:S(2)}) collective-permute-start(bf16[104,512]{1,0:T(8,128)(2,1)S(1)} %add_convert_fusion.17), channel_id=1, source_target_pairs={{0,16},{8,24},{16,0},{24,8},{1,17},{9,25},{17,1},{25,9},{2,18},{10... | collective-permute-start | bytes 319496 | tf_op jit(solution)/shard_map/ppermute | solution.py:39
  158.9 12.5 %collective-permute-done.29 = bf16[160,512]{1,0:T(8,128)(2,1)S(1)} collective-permute-done((bf16[160,512]{1,0:T(8,128)(2,1)S(1)}, bf16[160,512]{1,0:T(8,128)(2,1)S(1)}, u32[]{:S(2)}, u32[]{:S(2)}) %collective-permute-start.29) | collective-permute-done | bytes 163872 | tf_op jit(solution)/shard_map/ppermute | solution.py:39
  174.8 6.5 %collective-permute-done.30.o = bf16[104,512]{1,0:T(8,128)(2,1)S(1)} collective-permute-done((bf16[104,512]{1,0:T(8,128)(2,1)S(1)}, bf16[104,512]{1,0:T(8,128)(2,1)S(1)}, u32[]{:S(2)}, u32[]{:S(2)}) %collective-permute-start.30) | collective-permute-done | bytes 106528 | tf_op jit(solution)/shard_map/ppermute | solution.py:39
  182.9 1.7 finish_rest.1
  (141 shorter events, 32.9 us)
Async XLA Ops:
  7.6 9.1 %collective-permute-start = (bf16[208,512]{1,0:T(8,128)(2,1)S(1)}, bf16[208,512]{1,0:T(8,128)(2,1)S(1)}, u32[]{:S(2)}, u32[]{:S(2)}) collective-permute-start(bf16[208,512]{1,0:T(8,128)(2,1)S(1)} %pack_first.1.refs_0_), channel_id=1, source_target_pairs={{0,2},{1,3},{2,0},{3,1},{4,6},{5,7},{6,4},{7,5},{8,10},{9,11},{10,... | collective-permute-start | bytes 638984 | tf_op jit(solution)/shard_map/ppermute | solution.py:43
  10.6 11.3 %collective-permute-start.1 = (bf16[208,512]{1,0:T(8,128)(2,1)S(1)}, bf16[208,512]{1,0:T(8,128)(2,1)S(1)}, u32[]{:S(2)}, u32[]{:S(2)}) collective-permute-start(bf16[208,512]{1,0:T(8,128)(2,1)S(1)} %pack_first.1.refs_0_), channel_id=1, source_target_pairs={{0,4},{1,5},{2,6},{3,7},{4,0},{5,1},{6,2},{7,3},{8,12},{9,13},{10,... | collective-permute-start | bytes 638984 | tf_op jit(solution)/shard_map/ppermute | solution.py:43
  12.1 9.8 %collective-permute-start.2 = (bf16[208,512]{1,0:T(8,128)(2,1)S(1)}, bf16[208,512]{1,0:T(8,128)(2,1)S(1)}, u32[]{:S(2)}, u32[]{:S(2)}) collective-permute-start(bf16[208,512]{1,0:T(8,128)(2,1)S(1)} %pack_first.1.refs_0_), channel_id=1, source_target_pairs={{0,6},{1,7},{2,4},{3,5},{4,2},{5,3},{6,0},{7,1},{8,14},{9,15},{10,... | collective-permute-start | bytes 638984 | tf_op jit(solution)/shard_map/ppermute | solution.py:43
  12.1 13.1 %collective-permute-start.3 = (bf16[208,512]{1,0:T(8,128)(2,1)S(1)}, bf16[208,512]{1,0:T(8,128)(2,1)S(1)}, u32[]{:S(2)}, u32[]{:S(2)}) collective-permute-start(bf16[208,512]{1,0:T(8,128)(2,1)S(1)} %pack_first.1.refs_0_), channel_id=1, source_target_pairs={{0,1},{1,0},{2,3},{3,2},{4,5},{5,4},{6,7},{7,6},{8,9},{9,8},{10,11... | collective-permute-start | bytes 638984 | tf_op jit(solution)/shard_map/ppermute | solution.py:43
  25.2 20.7 %collective-permute-start.7 = (bf16[576,512]{1,0:T(8,128)(2,1)S(1)}, bf16[576,512]{1,0:T(8,128)(2,1)S(1)}, u32[]{:S(2)}, u32[]{:S(2)}) collective-permute-start(bf16[576,512]{1,0:T(8,128)(2,1)S(1)} %pack_rest.1.refs_0_), channel_id=1, source_target_pairs={{0,2},{1,3},{2,0},{3,1},{4,6},{5,7},{6,4},{7,5},{8,10},{9,11},{10,... | collective-permute-start | bytes 1769480 | tf_op jit(solution)/shard_map/ppermute | solution.py:43
  26.1 20.4 %collective-permute-start.8 = (bf16[576,512]{1,0:T(8,128)(2,1)S(1)}, bf16[576,512]{1,0:T(8,128)(2,1)S(1)}, u32[]{:S(2)}, u32[]{:S(2)}) collective-permute-start(bf16[576,512]{1,0:T(8,128)(2,1)S(1)} %pack_rest.1.refs_0_), channel_id=1, source_target_pairs={{0,4},{1,5},{2,6},{3,7},{4,0},{5,1},{6,2},{7,3},{8,12},{9,13},{10,... | collective-permute-start | bytes 1769480 | tf_op jit(solution)/shard_map/ppermute | solution.py:43
  28.0 31.2 %collective-permute-start.9 = (bf16[576,512]{1,0:T(8,128)(2,1)S(1)}, bf16[576,512]{1,0:T(8,128)(2,1)S(1)}, u32[]{:S(2)}, u32[]{:S(2)}) collective-permute-start(bf16[576,512]{1,0:T(8,128)(2,1)S(1)} %pack_rest.1.refs_0_), channel_id=1, source_target_pairs={{0,1},{1,0},{2,3},{3,2},{4,5},{5,4},{6,7},{7,6},{8,9},{9,8},{10,11... | collective-permute-start | bytes 1769480 | tf_op jit(solution)/shard_map/ppermute | solution.py:43
  46.0 15.0 %collective-permute-start.10 = (bf16[576,512]{1,0:T(8,128)(2,1)S(1)}, bf16[576,512]{1,0:T(8,128)(2,1)S(1)}, u32[]{:S(2)}, u32[]{:S(2)}) collective-permute-start(bf16[576,512]{1,0:T(8,128)(2,1)S(1)} %collective-permute-done.7.refs_1_), channel_id=1, source_target_pairs={{0,1},{1,0},{2,3},{3,2},{4,5},{5,4},{6,7},{7,6},{8,9},{9,8},{10,11... | collective-permute-start | bytes 1769480 | tf_op jit(solution)/shard_map/ppermute | solution.py:43
  46.5 14.4 %collective-permute-start.11 = (bf16[576,512]{1,0:T(8,128)(2,1)S(1)}, bf16[576,512]{1,0:T(8,128)(2,1)S(1)}, u32[]{:S(2)}, u32[]{:S(2)}) collective-permute-start(bf16[576,512]{1,0:T(8,128)(2,1)S(1)} %collective-permute-done.8.refs_2_), channel_id=1, source_target_pairs={{0,1},{1,0},{2,3},{3,2},{4,5},{5,4},{6,7},{7,6},{8,9},{9,8},{10,11... | collective-permute-start | bytes 1769480 | tf_op jit(solution)/shard_map/ppermute | solution.py:43
  46.6 12.0 %collective-permute-start.13 = (bf16[288,512]{1,0:T(8,128)(2,1)S(1)}, bf16[288,512]{1,0:T(8,128)(2,1)}, u32[]{:S(2)}, u32[]{:S(2)}) collective-permute-start(bf16[288,512]{1,0:T(8,128)(2,1)S(1)} %slice.79), channel_id=1, source_target_pairs={{0,4},{1,5},{2,6},{3,7},{4,0},{5,1},{6,2},{7,3},{8,12},{9,13},{10,... | collective-permute-start | bytes 884744 | tf_op jit(solution)/shard_map/ppermute | solution.py:43
  47.4 11.3 %collective-permute-start.12 = (bf16[288,512]{1,0:T(8,128)(2,1)S(1)}, bf16[288,512]{1,0:T(8,128)(2,1)}, u32[]{:S(2)}, u32[]{:S(2)}) collective-permute-start(bf16[288,512]{1,0:T(8,128)(2,1)S(1)} %slice.78), channel_id=1, source_target_pairs={{0,2},{1,3},{2,0},{3,1},{4,6},{5,7},{6,4},{7,5},{8,10},{9,11},{10,... | collective-permute-start | bytes 884744 | tf_op jit(solution)/shard_map/ppermute | solution.py:43
  101.3 18.1 %collective-permute-start.19 = (bf16[2,272,512]{2,1,0:T(8,128)(2,1)}, bf16[2,272,512]{2,1,0:T(8,128)(2,1)S(1)}, u32[]{:S(2)}, u32[]{:S(2)}) collective-permute-start(bf16[2,272,512]{2,1,0:T(8,128)(2,1)} %get-tuple-element.129), channel_id=1, source_target_pairs={{0,2},{1,3},{2,0},{3,1},{4,6},{5,7},{6,4},{7,5},{8,10},{9,11},{10,... | collective-permute-start | bytes 1671176 | tf_op jit(solution)/shard_map/ppermute | solution.py:43
  102.1 18.3 %collective-permute-start.17 = (bf16[2,320,512]{2,1,0:T(8,128)(2,1)}, bf16[2,320,512]{2,1,0:T(8,128)(2,1)S(1)}, u32[]{:S(2)}, u32[]{:S(2)}) collective-permute-start(bf16[2,320,512]{2,1,0:T(8,128)(2,1)} %get-tuple-element.131), channel_id=1, source_target_pairs={{0,4},{1,5},{2,6},{3,7},{4,0},{5,1},{6,2},{7,3},{8,12},{9,13},{10,... | collective-permute-start | bytes 1966088 | tf_op jit(solution)/shard_map/ppermute | solution.py:43
  120.5 9.2 %collective-permute-start.18 = (bf16[1,320,512]{2,1,0:T(8,128)(2,1)S(1)}, bf16[1,320,512]{2,1,0:T(8,128)(2,1)S(1)}, u32[]{:S(2)}, u32[]{:S(2)}) collective-permute-start(bf16[1,320,512]{2,1,0:T(8,128)(2,1)S(1)} %get-tuple-element.137), channel_id=1, source_target_pairs={{0,2},{1,3},{2,0},{3,1},{4,6},{5,7},{6,4},{7,5},{8,10},{9,11},{10,... | collective-permute-start | bytes 983048 | tf_op jit(solution)/shard_map/ppermute | solution.py:43
  127.5 11.1 %collective-permute-start.21 = (bf16[4,208,512]{2,1,0:T(8,128)(2,1)}, bf16[4,208,512]{2,1,0:T(8,128)(2,1)S(1)}, u32[]{:S(2)}, u32[]{:S(2)}) collective-permute-start(bf16[4,208,512]{2,1,0:T(8,128)(2,1)} %get-tuple-element.107), channel_id=1, source_target_pairs={{0,1},{1,0},{2,3},{3,2},{4,5},{5,4},{6,7},{7,6},{8,9},{9,8},{10,11... | collective-permute-start | bytes 2555912 | tf_op jit(solution)/shard_map/ppermute | solution.py:43
  128.0 10.5 %collective-permute-start.24 = (bf16[136,512]{1,0:T(8,128)(2,1)S(1)}, bf16[136,512]{1,0:T(8,128)(2,1)S(1)}, u32[]{:S(2)}, u32[]{:S(2)}) collective-permute-start(bf16[136,512]{1,0:T(8,128)(2,1)S(1)} %dynamic-slice_bitcast_fusion.1), channel_id=1, source_target_pairs={{0,8},{8,0},{16,24},{24,16},{1,9},{9,1},{17,25},{25,17},{2,10},{10... | collective-permute-start | bytes 417800 | tf_op jit(solution)/shard_map/ppermute | solution.py:39
  129.9 8.7 %collective-permute-start.23 = (bf16[160,512]{1,0:T(8,128)(2,1)S(1)}, bf16[160,512]{1,0:T(8,128)(2,1)S(1)}, u32[]{:S(2)}, u32[]{:S(2)}) collective-permute-start(bf16[160,512]{1,0:T(8,128)(2,1)S(1)} %dynamic-slice_bitcast_fusion), channel_id=1, source_target_pairs={{0,8},{8,0},{16,24},{24,16},{1,9},{9,1},{17,25},{25,17},{2,10},{10... | collective-permute-start | bytes 491528 | tf_op jit(solution)/shard_map/ppermute | solution.py:39
  138.8 8.8 %collective-permute-start.22 = (bf16[208,512]{1,0:T(8,128)(2,1)S(1)}, bf16[208,512]{1,0:T(8,128)(2,1)S(1)}, u32[]{:S(2)}, u32[]{:S(2)}) collective-permute-start(bf16[208,512]{1,0:T(8,128)(2,1)S(1)} %get-tuple-element.133), channel_id=1, source_target_pairs={{0,6},{1,7},{2,4},{3,5},{4,2},{5,3},{6,0},{7,1},{8,14},{9,15},{10,... | collective-permute-start | bytes 638984 | tf_op jit(solution)/shard_map/ppermute | solution.py:43
  141.1 8.8 %collective-permute-start.25 = (bf16[208,512]{1,0:T(8,128)(2,1)S(1)}, bf16[208,512]{1,0:T(8,128)(2,1)S(1)}, u32[]{:S(2)}, u32[]{:S(2)}) collective-permute-start(bf16[208,512]{1,0:T(8,128)(2,1)S(1)} %get-tuple-element.135), channel_id=1, source_target_pairs={{0,4},{1,5},{2,6},{3,7},{4,0},{5,1},{6,2},{7,3},{8,12},{9,13},{10,... | collective-permute-start | bytes 638984 | tf_op jit(solution)/shard_map/ppermute | solution.py:43
  151.9 20.7 %collective-permute-start.32 = (bf16[136,512]{1,0:T(8,128)(2,1)S(1)}, bf16[136,512]{1,0:T(8,128)(2,1)S(1)}, u32[]{:S(2)}, u32[]{:S(2)}) collective-permute-start(bf16[136,512]{1,0:T(8,128)(2,1)S(1)} %fusion.4), channel_id=1, source_target_pairs={{0,16},{8,24},{16,0},{24,8},{1,17},{9,25},{17,1},{25,9},{2,18},{10... | collective-permute-start | bytes 417800 | tf_op jit(solution)/shard_map/ppermute | solution.py:39
  154.5 16.9 %collective-permute-start.29 = (bf16[160,512]{1,0:T(8,128)(2,1)S(1)}, bf16[160,512]{1,0:T(8,128)(2,1)S(1)}, u32[]{:S(2)}, u32[]{:S(2)}) collective-permute-start(bf16[160,512]{1,0:T(8,128)(2,1)S(1)} %fusion.3), channel_id=1, source_target_pairs={{0,16},{8,24},{16,0},{24,8},{1,17},{9,25},{17,1},{25,9},{2,18},{10... | collective-permute-start | bytes 491528 | tf_op jit(solution)/shard_map/ppermute | solution.py:39
  155.0 17.5 %collective-permute-start.28 = (bf16[104,512]{1,0:T(8,128)(2,1)S(1)}, bf16[104,512]{1,0:T(8,128)(2,1)S(1)}, u32[]{:S(2)}, u32[]{:S(2)}) collective-permute-start(bf16[104,512]{1,0:T(8,128)(2,1)S(1)} %add_convert_fusion.17), channel_id=1, source_target_pairs={{0,16},{8,24},{16,0},{24,8},{1,17},{9,25},{17,1},{25,9},{2,18},{10... | collective-permute-start | bytes 319496 | tf_op jit(solution)/shard_map/ppermute | solution.py:39
  171.4 11.5 %collective-permute-start.31 = (bf16[160,512]{1,0:T(8,128)(2,1)S(1)}, bf16[160,512]{1,0:T(8,128)(2,1)S(1)}, u32[]{:S(2)}, u32[]{:S(2)}) collective-permute-start(bf16[160,512]{1,0:T(8,128)(2,1)S(1)} %add_convert_fusion.14.sa), channel_id=1, source_target_pairs={{0,8},{8,0},{16,24},{24,16},{1,9},{9,1},{17,25},{25,17},{2,10},{10... | collective-permute-start | bytes 491528 | tf_op jit(solution)/shard_map/ppermute | solution.py:39
  172.7 10.2 %collective-permute-start.33 = (bf16[136,512]{1,0:T(8,128)(2,1)S(1)}, bf16[136,512]{1,0:T(8,128)(2,1)S(1)}, u32[]{:S(2)}, u32[]{:S(2)}) collective-permute-start(bf16[136,512]{1,0:T(8,128)(2,1)S(1)} %add_convert_fusion.15.sb), channel_id=1, source_target_pairs={{0,8},{8,0},{16,24},{24,16},{1,9},{9,1},{17,25},{25,17},{2,10},{10... | collective-permute-start | bytes 417800 | tf_op jit(solution)/shard_map/ppermute | solution.py:39
  (42 other events, 302.1 us)

commit v5 on v4

--- a/solution.py
+++ b/solution.py
@@ -47,10 +47,10 @@
     return lax.optimization_barrier((x,) + deps)[0]
 
 
-def gather_direct(x, n):
+def gather_direct(x, n, *gate):
     out = [(0, 0, x)]
     far = [(k, swap(x, k)) for k in range(2, n, 2)]
-    out += [(k, 0, y) for k, y in far]
+    out += [(k, 0, after(y, *gate) if gate else y) for k, y in far]
     return out + [(k ^ 1, 0, swap(y, 1)) for k, _, y in out]
 
 
@@ -106,13 +106,18 @@
     return [b for b in (2 << i for i in range(16)) if b < nr]
 
 
+GROUPS = 2
+
+
 def pack_first_body(me, w, upb, *refs):
-    vecs = refs[:-1]
-    out = refs[-1]
+    vecs = refs[:-GROUPS]
+    outs = refs[-GROUPS:]
     r, W = w.shape
-    D = out.shape[1]
-    for j in range(W // D):
-        out[j * r : (j + 1) * r, :] = w[:, j * D : (j + 1) * D]
+    D = W // 3
+    gw = D // GROUPS
+    for g, out in enumerate(outs):
+        for j in range(3):
+            out[j * r : (j + 1) * r, :] = w[:, j * D + g * gw : j * D + (g + 1) * gw]
 
     def spot(v):
         w_ = v.shape[1]
@@ -124,19 +129,27 @@
 
     rows = [a for v in vecs for a in spot(v[...].astype(f32))] + spot(upb[...].astype(f32))
     b = jnp.concatenate(rows + [jnp.zeros((VROWS - len(rows), LANES), f32)], axis=0).astype(bf16)
-    out[W // D * r :, :] = jnp.concatenate([b, jnp.zeros((VROWS, D - LANES), bf16)], axis=1)
+    outs[0][3 * r :, :] = jnp.concatenate([b, jnp.zeros((VROWS, gw - LANES), bf16)], axis=1)
 
 
 def whole(n):
     return [pl.BlockSpec(memory_space=pltpu.VMEM)] * n
 
 
-def pack_first(me, w, vecs, upb, D):
+def once(*arrays):
+    return [pl.BlockSpec(a.shape, lambda i, *m, nd=len(a.shape): (0,) * nd) for a in arrays]
+
+
+def pack_first(me, w, vecs, upb):
+    r, W = w.shape
+    gw = W // 3 // GROUPS
+    args = [w, upb[None]] + [v[None] for v in vecs]
+    outs = [S((3 * r + (VROWS if g == 0 else 0), gw), bf16) for g in range(GROUPS)]
     return pl.pallas_call(
         pack_first_body,
-        in_specs=[pl.BlockSpec(memory_space=pltpu.SMEM)] + whole(2 + len(vecs)), out_specs=whole(1)[0],
-        out_shape=S((w.size // D + VROWS, D), bf16), compiler_params=pltpu.CompilerParams(vmem_limit_bytes=8 << 20), name="pack_first", cost_estimate=cost(0, 4 * w.size),
-    )(me, w, upb[None], *[v[None] for v in vecs])
+        grid_spec=pltpu.PrefetchScalarGridSpec(num_scalar_prefetch=1, grid=(1,), in_specs=once(*args), out_specs=once(*outs)),
+        out_shape=outs, compiler_params=pltpu.CompilerParams(vmem_limit_bytes=8 << 20), name="pack_first", cost_estimate=cost(0, 4 * w.size),
+    )(me, *args)
 
 
 def pack_rest_body(wo, wu, wd, out):
@@ -149,9 +162,10 @@
 
 def pack_rest(wo, wu, wd):
     D = wo.shape[1]
-    return pl.pallas_call(
-        pack_rest_body, in_specs=whole(3), out_specs=whole(1)[0],
-        out_shape=S(((wo.size + wu.size + wd.size) // D, D), bf16), compiler_params=pltpu.CompilerParams(vmem_limit_bytes=8 << 20), name="pack_rest", cost_estimate=cost(0, 4 * wu.size),
+    out = S(((wo.size + wu.size + wd.size) // D, D), bf16)
+    return pl.pallas_call(
+        pack_rest_body, grid=(1,), in_specs=once(wo, wu, wd), out_specs=once(out)[0],
+        out_shape=out, compiler_params=pltpu.CompilerParams(vmem_limit_bytes=8 << 20), name="pack_rest", cost_estimate=cost(0, 4 * wu.size),
     )(wo, wu, wd)
 
 
@@ -275,16 +289,38 @@
     return pl.multiple_of(x, m)
 
 
+def project(v, h, w, kv, qkvt, grp, scale):
+    gw = w.shape[1] // 3
+    bias = lambda i: v[i : i + 1, grp * gw : (grp + 1) * gw]
+    for j in range(3):
+        y = dot(h, w[:, j * gw : (j + 1) * gw])
+        if j == 0:
+            y = y + bias(2)
+        if j == 2:
+            y = y + bias(3)
+        y = y.astype(bf16)
+        if j == 0:
+            y = y * bf16(scale)
+        else:
+            kv[j - 1] = y
+        qkvt[j] = y.T
+
+
+def weight_segs(w, r):
+    gw = w.shape[1] // 3
+    seg = lambda j: (j * r, r, lambda s, o, c: w.at[pl.ds(mult(s * r + o, 16), c), pl.ds(j * gw, gw)], gw)
+    return [seg(j) for j in range(3)]
+
+
 def front_body(scale, n, meta, me, tok, step, *refs):
     np_ = len(meta)
     pieces = refs[:np_]
-    xht, kv, qkvt, w, vec, upb, vbuf, sems = refs[np_:]
+    xht, hs, kv, qkvt, w, vec, upb, vbuf, sems = refs[np_:]
     D = tok.shape[-1]
     r = D // n
     FF = upb.shape[1]
     first = pl.program_id(0) == 0
-    seg = lambda j: (j * r, r, lambda s, o, c: w.at[pl.ds(mult(s * r + o, 16), c), pl.ds(j * D, D)], D)
-    segs = [(3 * r, VROWS, lambda s, o, c: vbuf.at[s, pl.ds(o, c)], LANES)] + [seg(j) for j in range(3)]
+    segs = [(3 * r, VROWS, lambda s, o, c: vbuf.at[s, pl.ds(o, c)], LANES)] + weight_segs(w, r)
 
     @pl.when(first)
     def _():
@@ -312,18 +348,24 @@
 
     v = vec[...]
     h = (nx * row(v, 0) + row(v, 1)).astype(bf16)
-    for j in range(3):
-        y = dot(h, w[:, j * D : (j + 1) * D])
-        if j == 0:
-            y = y + row(v, 2)
-        if j == 2:
-            y = y + row(v, 3)
-        y = y.astype(bf16)
-        if j == 0:
-            y = y * bf16(scale)
-        else:
-            kv[:, (j - 1) * D : j * D] = y
-        qkvt[j * D : (j + 1) * D, :] = y.T
+    hs[...] = h
+    project(v, h, w, kv, qkvt, 0, scale)
+
+
+def front_next_body(scale, n, meta, grp, me, hs, vec, *refs):
+    np_ = len(meta)
+    pieces = refs[:np_]
+    kv, qkvt, w, sems = refs[np_ + 2 :]
+
+    @pl.when(pl.program_id(0) == 0)
+    def _():
+        cs = pull(me[0], pieces, meta, weight_segs(w, w.shape[0] // n), sems)
+        for c in cs:
+            c.start()
+        for c in cs:
+            c.wait()
+
+    project(vec[...], hs[...], w, kv, qkvt, grp, scale)
 
 
 S = jax.ShapeDtypeStruct
@@ -337,6 +379,7 @@
 def front(me, tok, step, pieces, n, FF, bm=512):
     T, D = tok.shape
     scale = 1.0 / math.sqrt(D // HEADS)
+    gw = D // GROUPS
     meta = tuple((k, r0) for k, r0, _ in pieces)
     keep = lambda *sh: pl.BlockSpec(sh, lambda i, m: (0,) * len(sh))
     return pl.pallas_call(
@@ -344,11 +387,30 @@
         grid_spec=pltpu.PrefetchScalarGridSpec(
             num_scalar_prefetch=1, grid=(T // bm,),
             in_specs=[pl.BlockSpec((bm, D), lambda i, m: (i, 0)), keep(1, D)] + [ANY] * len(pieces),
-            out_specs=[pl.BlockSpec((D, bm), lambda i, m: (0, i)), pl.BlockSpec((bm, 2 * D), lambda i, m: (i, 0)), pl.BlockSpec((3 * D, bm), lambda i, m: (0, i)), keep(D, 3 * D), keep(8, D), keep(1, FF)],
+            out_specs=[pl.BlockSpec((D, bm), lambda i, m: (0, i)), pl.BlockSpec((bm, D), lambda i, m: (i, 0)), pl.BlockSpec((2, bm, gw), lambda i, m: (0, i, 0)), pl.BlockSpec((3, gw, bm), lambda i, m: (0, 0, i)), keep(D, 3 * gw), keep(8, D), keep(1, FF)],
             scratch_shapes=[pltpu.VMEM((n, VROWS, LANES), bf16), pltpu.SemaphoreType.DMA((8 * len(pieces),))]),
-        out_shape=[S((D, T), bf16), S((T, 2 * D), bf16), S((3 * D, T), bf16), S((D, 3 * D), bf16), S((8, D), f32), S((1, FF), f32)],
-        compiler_params=cp(), name="front", cost_estimate=cost(6 * T * D * D, 10 * T * D * 2),
+        out_shape=[S((D, T), bf16), S((T, D), bf16), S((2, T, D), bf16), S((3, D, T), bf16), S((D, 3 * gw), bf16), S((8, D), f32), S((1, FF), f32)],
+        compiler_params=cp(), name="front", cost_estimate=cost(6 * T * D * gw, 8 * T * D),
     )(me, tok, step, *[a for _, _, a in pieces])
+
+
+def front_next(me, hs, vec, pieces, kv, qkvt, grp, n, bm=512):
+    T, D = hs.shape
+    scale = 1.0 / math.sqrt(D // HEADS)
+    gw = D // GROUPS
+    meta = tuple((k, r0) for k, r0, _ in pieces)
+    q = len(pieces)
+    return pl.pallas_call(
+        functools.partial(front_next_body, scale, n, meta, grp),
+        grid_spec=pltpu.PrefetchScalarGridSpec(
+            num_scalar_prefetch=1, grid=(T // bm,),
+            in_specs=[pl.BlockSpec((bm, D), lambda i, m: (i, 0)), pl.BlockSpec(vec.shape, lambda i, m: (0, 0))] + [ANY] * (q + 2),
+            out_specs=[pl.BlockSpec((2, bm, gw), lambda i, m: (0, i, grp)), pl.BlockSpec((3, gw, bm), lambda i, m: (0, grp, i)), pl.BlockSpec((D, 3 * gw), lambda i, m: (0, 0))],
+            scratch_shapes=[pltpu.SemaphoreType.DMA((8 * q,))]),
+        out_shape=[S((2, T, D), bf16), S((3, D, T), bf16), S((D, 3 * gw), bf16)],
+        input_output_aliases={3 + q: 0, 4 + q: 1},
+        compiler_params=cp(), name="front_next", cost_estimate=cost(6 * T * D * gw, 6 * T * D),
+    )(me, hs, vec, *[a for _, _, a in pieces], kv, qkvt)
 
 
 def attn_fwd_body(HD, bi, CR, ln, k, qt, vt, *refs):
@@ -406,8 +468,7 @@
 
 
 def attn_fwd(ln, kv, qkvt, p0, cnt, prev):
-    T = kv.shape[0]
-    D = kv.shape[1] // 2
+    _, T, D = kv.shape
     HD = D // HEADS
     PW = 2 * HD
     NP = D // PW
@@ -417,7 +478,7 @@
         functools.partial(attn_fwd_body, HD, bi, min(256, T)),
         grid_spec=pltpu.PrefetchScalarGridSpec(
             num_scalar_prefetch=1, grid=(cnt,),
-            in_specs=[pl.BlockSpec((T, PW), lambda p, r: (0, p0 + p)), pl.BlockSpec((PW, T), lambda p, r: (p0 + p, 0)), pl.BlockSpec((PW, T), lambda p, r: (2 * NP + p0 + p, 0))] + [ANY] * len(prev),
+            in_specs=[pl.BlockSpec((None, T, PW), lambda p, r: (0, 0, p0 + p)), pl.BlockSpec((None, PW, T), lambda p, r: (0, p0 + p, 0)), pl.BlockSpec((None, PW, T), lambda p, r: (2, p0 + p, 0))] + [ANY] * len(prev),
             out_specs=[pl.BlockSpec((2, T, T), lambda p, r: (p0 + p, 0, 0)), pl.BlockSpec((T, PW), lambda p, r: (0, p0 + p)), pl.BlockSpec((PW, T), lambda p, r: (p0 + p, 0)), pl.BlockSpec((PW, T), lambda p, r: (p0 + p, 0)), pl.BlockSpec((None, 8, T), lambda p, r: (p0 + p, 0, 0))],
             scratch_shapes=[pltpu.VMEM((2, T, bi), f32), pltpu.VMEM((T, 2 * PW), bf16)]),
         out_shape=[S((HEADS, T, T), bf16), S((T, D), bf16), S((D, T), bf16), S((D, T), f32), S((NP, 8, T), f32)],
@@ -592,18 +653,18 @@
 
 
 def attn_bwd(kv, qkvt, gmt, mixedf, linv, et, p0, cnt, prev):
-    T = kv.shape[0]
-    D = kv.shape[1] // 2
+    _, T, D = kv.shape
     HD = D // HEADS
     PW = 2 * HD
     NP = D // PW
     prev = list(prev)
-    pr = lambda o: pl.BlockSpec((PW, T), lambda p: (o + p0 + p, 0))
+    pr = pl.BlockSpec((PW, T), lambda p: (p0 + p, 0))
+    of = lambda j: pl.BlockSpec((None, PW, T), lambda p: (j, p0 + p, 0))
     return pl.pallas_call(
         functools.partial(attn_bwd_body, HD, 1.0 / math.sqrt(HD), min(256, T)),
         grid=(cnt,),
         scratch_shapes=[pltpu.VMEM((2, T, T), bf16)],
-        in_specs=[pl.BlockSpec((T, PW), lambda p: (0, NP + p0 + p)), pr(NP), pr(0), pr(0), pr(0), pl.BlockSpec((None, 8, T), lambda p: (p0 + p, 0, 0)), pl.BlockSpec((2, T, T), lambda p: (p0 + p, 0, 0))] + [ANY] * len(prev),
+        in_specs=[pl.BlockSpec((None, T, PW), lambda p: (1, 0, p0 + p)), of(1), of(0), pr, pr, pl.BlockSpec((None, 8, T), lambda p: (p0 + p, 0, 0)), pl.BlockSpec((2, T, T), lambda p: (p0 + p, 0, 0))] + [ANY] * len(prev),
         out_specs=pl.BlockSpec((3, PW, T), lambda p: (0, p0 + p, 0)),
         out_shape=S((3, D, T), bf16),
         input_output_aliases={7: 0} if prev else {},
@@ -648,24 +709,26 @@
     )(me, xht, g)
 
 
-def back_body(tok, step, vec, w, g, gx1, tg):
+def back_body(tok, step, vec, g, gx1, *refs):
+    ws, tg = refs[:-1], refs[-1]
     D = tok.shape[1]
+    gw = D // GROUPS
     x = tok[...].astype(f32) + step[...].astype(f32)
     nx, rr = norm(x)
-    gt = dot(w[:, :D], g[0]) + dot(w[:, D : 2 * D], g[1]) + dot(w[:, 2 * D :], g[2])
+    gt = sum(dot(w[:, j * gw : (j + 1) * gw], g[j, q * gw : (q + 1) * gw, :]) for q, w in enumerate(ws) for j in range(3))
     gn = gt.T * row(vec[...], 0)
     tg[...] = gx1[...] + rr * (gn - jnp.mean(gn, axis=-1, keepdims=True) - nx * jnp.mean(gn * nx, axis=-1, keepdims=True))
 
 
-def back(tok, step, vec, w, g, gx1, bm=512):
+def back(tok, step, vec, ws, g, gx1, bm=512):
     T, D = tok.shape
     full = lambda a: pl.BlockSpec(a.shape, lambda i: (0,) * a.ndim)
     rows = pl.BlockSpec((bm, D), lambda i: (i, 0))
     return pl.pallas_call(
         back_body, grid=(T // bm,),
-        in_specs=[rows, full(step), full(vec), full(w), pl.BlockSpec((3, D, bm), lambda i: (0, 0, i)), rows],
+        in_specs=[rows, full(step), full(vec), pl.BlockSpec((3, D, bm), lambda i: (0, 0, i)), rows] + [full(w) for w in ws],
         out_specs=rows, out_shape=S((T, D), f32), compiler_params=cp(), name="back", cost_estimate=cost(6 * T * D * D, 14 * T * D),
-    )(tok, step, vec, w, g, gx1)
+    )(tok, step, vec, g, gx1, *ws)
 
 
 def shards(tokens, step_embed, lengths, cotangent, ln1_gain, ln1_bias, qkv_weight, q_bias, v_bias, out_weight, out_bias, ln2_gain, ln2_bias, up_weight, up_bias, down_weight, down_bias):
@@ -678,15 +741,20 @@
     FF = up_bias.shape[0] * n
     nc = FF // D
     rf = FF // n
-    pack1 = pack_first(mes, qkv_weight, [ln1_gain, ln1_bias, q_bias, v_bias, out_bias, ln2_gain, ln2_bias, down_bias], up_bias, D)
+    packs = pack_first(mes, qkv_weight, [ln1_gain, ln1_bias, q_bias, v_bias, out_bias, ln2_gain, ln2_bias, down_bias], up_bias)
     pack2 = pack_rest(out_weight, up_weight, down_weight)
-    pieces1 = gather_direct(pack1, n)
-    xht, kv, qkvt, w, vec, upb = front(mes, tok, step, pieces1, n, FF)
     NP = HEADS // 2
-    fw = attn_fwd(lengths, kv, qkvt, 0, NP // 2, [])
-    fw2 = attn_fwd(lengths, kv, qkvt, NP // 2, NP // 2, fw)
+    GP = NP // GROUPS
+    arrays = lambda ps: [a for _, _, a in ps[1:]]
+    pieces = gather_direct(packs[0], n)
+    xht, hs, kv, qkvt, wa, vec, upb = front(mes, tok, after(step, pack2), pieces, n, FF)
+    nextp = gather_direct(packs[1], n, vec)
+    fw = attn_fwd(lengths, kv, qkvt, 0, GP, [])
+    kv, qkvt, wb = front_next(mes, hs, after(vec, fw[4]), nextp, kv, qkvt, 1, n)
+    fw2 = attn_fwd(lengths, kv, qkvt, GP, NP - GP, fw)
+    ws = [wa, wb]
     et, mixed, mixedt, mixedf, linv = fw2
-    pieces2 = gather_forward(after(pack2, *[a for _, _, a in pieces1[1:]]), n, fw[4], linv)
+    pieces2 = gather_forward(after(pack2, vec, *arrays(nextp)), n, wb, linv)
     out, gx1, gmt, keep, send = ffn(lengths, mes, tok, step, vec, upb, cot, mixed, mixedt, pieces2, n)
     bwd = lambda p, c, g, *deps: attn_bwd(kv, qkvt, after(gmt, *deps) if deps else gmt, mixedf, linv, et, p, c, g)
     ra = rf + r
@@ -703,7 +771,7 @@
     ga, gb = swap(xa, 2 << (m - 1)), swap(xb, 2)
     for t in range(1, m):
         dep = g if t == 1 else keep
-        ga, gb = after(ga, dep), after(gb, dep)
+        ga, gb, _ = lax.optimization_barrier((ga, gb, dep))
         h //= 2
         lo, hi = slice(0, h), slice(h, None)
         ka, xa = add(ka, ga, lo), add(ka, ga, hi)
@@ -714,25 +782,27 @@
     got = swap(send, 1)
     p2 = [add16(keep[k], got[k]) for k in range(n // 2)]
     far2 = spread(p2)
-    ua = add16(ka, after(ga, keep))[0]
-    ub = add16(kb, after(gb, keep))[0]
+    ga, gb, _ = lax.optimization_barrier((ga, gb, keep))
+    ua = add16(ka, ga)[0]
+    ub = add16(kb, gb)[0]
+    ua, ub = lax.optimization_barrier((ua, ub))
     ma, oa, xa = rep_half(ua)
     mb, ob, xb = rep_half(ub)
-    tg = back(tok, after(step, xa, xb), vec, w, g, gx1)
-    za = add16(ma, after(oa, tg))
-    zb = add16(mb, after(ob, tg))
-    own2 = total(p2[0], [after(a, za, zb) for a in far2])
-    m2, o2, _ = rep_half(own2)
+    za = add16(ma, after(oa, p2[1]))
+    zb = add16(mb, after(ob, p2[1]))
+    tg = back(tok, after(step, za, zb, *p2[1:]), vec, ws, g, gx1)
+    own2 = total(p2[0], [after(a, tg) for a in far2])
+    m2, o2, x2 = rep_half(own2)
     z2 = add16(m2, o2)
     for b in rep_steps():
-        pa, pb = rep_perm(za, b), rep_perm(zb, b)
-        za = add16(za, after(pa, z2))
-        z2 = add16(z2, after(rep_perm(z2, b), za))
-        zb = add16(zb, after(pb, z2))
+        pa, pb, pz = rep_perm(za, b), rep_perm(zb, b), rep_perm(z2, b)
+        za = add16(za, after(pa, x2))
+        zb = add16(zb, after(pb, x2))
+        z2 = add16(z2, after(pz, za, zb))
     oa, ob, o2 = rep_perm(za, 1), rep_perm(zb, 1), rep_perm(z2, 1)
     ids = jnp.stack([me, (lax.axis_index("rep") % 2).astype(jnp.int32)])
-    g_qkv, g_g1, g_b1, g_q, g_v = finish_first(ids, z2, o2, qkv_weight, ln1_gain, ln1_bias)
     g_down, g_up, g_out, g_upb, g_ob, g_g2, g_b2, g_db = finish_rest(ids, za, oa, zb, ob, r, rf, nc, n)
+    g_qkv, g_g1, g_b1, g_q, g_v = finish_first(ids, z2, after(o2, g_out), qkv_weight, ln1_gain, ln1_bias)
     flat = lambda a: a.reshape(-1)
     return (out[None], tg[None], flat(g_g1), flat(g_b1), g_qkv, flat(g_q), flat(g_v), g_out, flat(g_ob), flat(g_g2), flat(g_b2), g_up, flat(g_upb), g_down, flat(g_db))
 

time: 185 us -> 180 us (0.973)
  waiting for transfers between devices: 39.8 us -> 28.3 us
  Pallas kernels: 93.9 us -> 97.2 us
    ppermute x25 -> x32, waiting for transfers between devices: 19.5 us -> 10.4 us  [swap(): return lax.ppermute(x, 'shard', xor_perm(lax.axis_size('shard'), k))]
    pallas_call x2 -> x3, Pallas kernels: 0.12 us -> 5.49 us  [the longest x1 5.37 us: front_next(): pl.pallas_call(functools.partial(front_next_body, scale, n, meta, grp), g...]
    ppermute x25 -> x32, starting transfers between devices: 18.5 us -> 21.6 us  [swap(): return lax.ppermute(x, 'shard', xor_perm(lax.axis_size('shard'), k))]
    ppermute x9, starting transfers between devices: 13.8 us -> 11.2 us  [rep_perm(): return lax.ppermute(x, 'rep', xor_perm(lax.axis_size('rep'), b))]
    ppermute x9, waiting for transfers between devices: 20.3 us -> 17.9 us  [rep_perm(): return lax.ppermute(x, 'rep', xor_perm(lax.axis_size('rep'), b))]
    pallas_call x1, Pallas kernels: 7.75 us -> 5.9 us  [front(): pl.pallas_call(functools.partial(front_body, scale, n, meta), grid_spec=p...]
    convert_element_type x13 -> x11, other arithmetic: 5.75 us -> 7.04 us  [add16(): return (a.astype(f32) + b.astype(f32)).astype(bf16)]
    unnamed x64 -> x82, local copies, waits for them, and re-layouts: 10 us -> 10.5 us
  transfers between devices with their start and end apart: 34 -> 41, of which waited for: 12 -> 16; matrix products, arithmetic and copies ran while one was open for 0% -> 1% of each run, Pallas kernels for 36% -> 39%
where the time goes in v5:
time: 180 us; the launch traced here: 179 us
  Pallas kernels  97.2 us (54%)
  starting transfers between devices  32.9 us (18%)
  waiting for transfers between devices  28.3 us (16%)
  local copies, waits for them, and re-layouts  11.2 us (6%)
  other arithmetic  7.42 us (4%)
  between operations  1.94 us (1%)
    pallas_call x1, Pallas kernels, ffn(): pl.pallas_call(functools.partial(ffn_body, n, meta, min(1024, FF)), grid_...  26.3 us
    pallas_call x2, Pallas kernels, attn_bwd(): pl.pallas_call(functools.partial(attn_bwd_body, HD, 1.0 / math.sqrt(HD),...  23.8 us
    ppermute x32, starting transfers between devices, swap(): return lax.ppermute(x, 'shard', xor_perm(lax.axis_size('shard'), k))  21.6 us
    pallas_call x2, Pallas kernels, attn_fwd(): pl.pallas_call(functools.partial(attn_fwd_body, HD, bi, min(256, T)), gri...  19.9 us
    ppermute x9, waiting for transfers between devices, rep_perm(): return lax.ppermute(x, 'rep', xor_perm(lax.axis_size('rep'), b))  17.9 us
    ppermute x9, starting transfers between devices, rep_perm(): return lax.ppermute(x, 'rep', xor_perm(lax.axis_size('rep'), b))  11.2 us
    unnamed x82, local copies, waits for them, and re-layouts  10.5 us
    ppermute x32, waiting for transfers between devices, swap(): return lax.ppermute(x, 'shard', xor_perm(lax.axis_size('shard'), k))  10.4 us
  transfers between devices with their start and end apart: 41, of which 16 were waited for; matrix products, arithmetic and copies ran while one was open for 1% of the time, Pallas kernels for 39%

profile of v5, /device:TPU:0, one launch (start us, length us, event | category | flops | bytes accessed | tf_op | source)
XLA Modules:
  0.0 179.0 jit_solution(6242916894221683071)
XLA Ops:
  7.6 3.0 %collective-permute-start = (bf16[208,256]{1,0:T(8,128)(2,1)S(1)}, bf16[208,256]{1,0:T(8,128)(2,1)S(1)}, u32[]{:S(2)}, u32[]{:S(2)}) collective-permute-start(bf16[208,256]{1,0:T(8,128)(2,1)S(1)} %get-tuple-element.87.refs_0_), channel_id=1, source_target_pairs={{0,2},{1,3},{2,0},{3,1},{4,6},{5,7},{6,4},{7,5},{8,10},{9,11},{10,... | collective-permute-start | bytes 319496 | tf_op jit(solution)/shard_map/ppermute | solution.py:43
  12.1 1.7 collective-permute-done.refs_1_
  13.9 2.6 %collective-permute-done.1.refs_2_ = bf16[208,256]{1,0:T(8,128)(2,1)S(1)} collective-permute-done((bf16[208,256]{1,0:T(8,128)(2,1)S(1)}, bf16[208,256]{1,0:T(8,128)(2,1)S(1)}, u32[]{:S(2)}, u32[]{:S(2)}) %collective-permute-start.1) | collective-permute-done | bytes 106528 | tf_op jit(solution)/shard_map/ppermute | solution.py:43
  24.9 5.9 %front.1 = (bf16[512,1024]{1,0:T(8,128)(2,1)}, bf16[1024,512]{1,0:T(8,128)(2,1)}, bf16[2,1024,512]{2,1,0:T(8,128)(2,1)}, bf16[3,512,1024]{2,1,0:T(8,128)(2,1)}, ...) custom-call(s32[1]{0:T(128)} %bitcast.me, bf16[1024,512]{1,0:T(8,128)(2,1)} %bitcast.49, ...), custom_call_target="tpu_custom_call" | custom-call | flops 805306368 | bytes 4194304 | tf_op jit(solution)/shard_map/front/pallas_call | solution.py:385
  35.6 10.0 %attn_fwd.2 = (bf16[8,1024,1024]{2,1,0:T(8,128)(2,1)}, bf16[1024,512]{1,0:T(8,128)(2,1)}, bf16[512,1024]{1,0:T(8,128)(2,1)}, f32[512,1024]{1,0:T(8,128)}, f32[4,8,1024]{2,1,0:T(8,128)}) custom-call(s32[1]{0:T(128)S(6)} %copy.48.ln, bf16[2,1024,512]{2,1,0:T(8,128)(2,1)} %get-tuple-element.91.k.refs_8_, bf16[3,512,1024]{2,1,0:T(8,128)(2,1)} %get-tuple-element.92.qt.vt.refs_9_, ...), custom_call_target="tpu_custom_call" | custom-call | flops 4294967296 | bytes 8388608 | tf_op jit(solution)/shard_map/attn_fwd/pallas_call | solution.py:477
  45.8 5.4 %front_next.1 = (bf16[2,1024,512]{2,1,0:T(8,128)(2,1)}, bf16[3,512,1024]{2,1,0:T(8,128)(2,1)}, bf16[512,768]{1,0:T(8,128)(2,1)}) custom-call(s32[1]{0:T(128)} %bitcast.me, bf16[1024,512]{1,0:T(8,128)(2,1)} %get-tuple-element.90.hs, f32[8,512]{1,0:T(8,128)} %get-tuple-element.94.vec, ...), custom_call_target="tpu_custom_call", output_to_operand_aliasing={{0}: (11, {}), {1}: (12, {})} | custom-call | flops 805306368 | bytes 3145728 | tf_op jit(solution)/shard_map/front_next/pallas_call | solution.py:403
  53.8 10.0 %attn_fwd.3 = (bf16[8,1024,1024]{2,1,0:T(8,128)(2,1)}, bf16[1024,512]{1,0:T(8,128)(2,1)}, bf16[512,1024]{1,0:T(8,128)(2,1)}, f32[512,1024]{1,0:T(8,128)}, f32[4,8,1024]{2,1,0:T(8,128)}) custom-call(s32[1]{0:T(128)S(6)} %copy.48.ln, ...), custom_call_target="tpu_custom_call", output_to_operand_aliasing={{0}: (4, {}), {1}: (5, {}), {2}: (6, {}), {3}: (7, {}), {4}... | custom-call | flops 4294967296 | bytes 8388608 | tf_op jit(solution)/shard_map/attn_fwd/pallas_call | solution.py:477
  66.8 26.3 %ffn.1 = (bf16[1024,512]{1,0:T(8,128)(2,1)}, f32[1024,512]{1,0:T(8,128)}, bf16[512,1024]{1,0:T(8,128)(2,1)}, bf16[4,592,512]{2,1,0:T(8,128)(2,1)}, bf16[4,592,512]{2,1,0:T(8,128)(2,1)}) custom-call(s32[1]{0:T(128)S(6)} %copy.48.ln, s32[1]{0:T(128)} %bitcast.me, bf16[1024,512]{1,0:T(8,128)(2,1)} %bitcast.50, bf16[1,512]{1,0:T(2,128)(2,1)} %step.3, ...), custom_call_target="tpu_custom_call" | custom-call | flops 14495514624 | bytes 8388608 | tf_op jit(solution)/shard_map/ffn/pallas_call | solution.py:619
  93.3 7.8 %attn_bwd.2.refs_0_ = bf16[3,512,1024]{2,1,0:T(8,128)(2,1)} custom-call(bf16[2,1024,512]{2,1,0:T(8,128)(2,1)} %get-tuple-element.99.k.v, bf16[3,512,1024]{2,1,0:T(8,128)(2,1)} %get-tuple-element.100.qt.vt.kt, bf16[3,512,1024]{2,1,0:T(8,128)(2,1)} %get-tuple-element.100.qt.vt.kt, bf16[512,1024]{1,0:T(8,128)(2,1)} %get-tuple-element.121.gt, ...), custom_call_target="tpu_custom_call" | custom-call | flops 4294967296 | bytes 4194304 | tf_op jit(solution)/shard_map/attn_bwd/pallas_call | solution.py:663
  101.1 2.5 %add_convert_fusion = (bf16[2,320,512]{2,1,0:T(8,128)(2,1)}, bf16[2,320,512]{2,1,0:T(8,128)(2,1)S(1)}) fusion(bf16[4,592,512]{2,1,0:T(8,128)(2,1)} %collective-permute-done.23, bf16[4,592,512]{2,1,0:T(8,128)(2,1)S(1)} %copy-done.18), kind=kLoop, calls=%fused_computation | loop fusion | flops 2621440 | bytes 3932160 | tf_op jit(solution)/shard_map/convert_element_type | solution.py:82
  103.7 2.4 %add_convert_fusion.2 = (bf16[2,272,512]{2,1,0:T(8,128)(2,1)S(1)}, bf16[2,272,512]{2,1,0:T(8,128)(2,1)}) fusion(bf16[4,592,512]{2,1,0:T(8,128)(2,1)} %collective-permute-done.23, bf16[4,592,512]{2,1,0:T(8,128)(2,1)S(1)} %copy-done.18), kind=kLoop, calls=%fused_computation.2 | loop fusion | flops 2228224 | bytes 3342336 | tf_op jit(solution)/shard_map/convert_element_type | solution.py:82
  108.2 16.0 %attn_bwd.3.g = bf16[3,512,1024]{2,1,0:T(8,128)(2,1)} custom-call(bf16[2,1024,512]{2,1,0:T(8,128)(2,1)} %get-tuple-element.99.k.v, bf16[3,512,1024]{2,1,0:T(8,128)(2,1)} %get-tuple-element.100.qt.vt.kt, bf16[3,512,1024]{2,1,0:T(8,128)(2,1)} %get-tuple-element.100.qt.vt.kt, bf16[512,1024]{1,0:T(8,128)(2,1)} %get-tuple-element.121.gt, ...), custom_call_target="tpu_custom_call", output_to_operand_aliasing={{}: (7, {})} | custom-call | flops 12884901888 | bytes 12582912 | tf_op jit(solution)/shard_map/attn_bwd/pallas_call | solution.py:663
  127.9 5.6 %wqkv.1 = (bf16[4,208,512]{2,1,0:T(8,128)(2,1)}, bf16[4,208,512]{2,1,0:T(8,128)(2,1)}) custom-call(s32[1]{0:T(128)} %bitcast.me, bf16[512,1024]{1,0:T(8,128)(2,1)} %get-tuple-element.125.xht, bf16[3,512,1024]{2,1,0:T(8,128)(2,1)} %attn_bwd.3.g), custom_call_target="tpu_custom_call" | custom-call | flops 1610612736 | bytes 5242880 | tf_op jit(solution)/shard_map/wqkv/pallas_call | solution.py:700
  133.6 2.2 %collective-permute-done.27 = bf16[1,272,512]{2,1,0:T(8,128)(2,1)S(1)} collective-permute-done((bf16[1,272,512]{2,1,0:T(8,128)(2,1)}, bf16[1,272,512]{2,1,0:T(8,128)(2,1)S(1)}, u32[]{:S(2)}, u32[]{:S(2)}) %collective-permute-start.27) | collective-permute-done | bytes 278560 | tf_op jit(solution)/shard_map/ppermute | solution.py:43
  136.0 1.6 collective-permute-start.28
  139.0 3.3 %collective-permute-done.28 = bf16[160,512]{1,0:T(8,128)(2,1)S(1)} collective-permute-done((bf16[160,512]{1,0:T(8,128)(2,1)S(1)}, bf16[160,512]{1,0:T(8,128)(2,1)S(1)}, u32[]{:S(2)}, u32[]{:S(2)}) %collective-permute-start.28) | collective-permute-done | bytes 163872 | tf_op jit(solution)/shard_map/ppermute | solution.py:39
  146.0 2.6 %collective-permute-start.36 = (bf16[160,512]{1,0:T(8,128)(2,1)S(1)}, bf16[160,512]{1,0:T(8,128)(2,1)S(1)}, u32[]{:S(2)}, u32[]{:S(2)}) collective-permute-start(bf16[160,512]{1,0:T(8,128)(2,1)S(1)} %add_convert_fusion.15), channel_id=1, source_target_pairs={{0,16},{8,24},{16,0},{24,8},{1,17},{9,25},{17,1},{25,9},{2,18},{10... | collective-permute-start | bytes 491528 | tf_op jit(solution)/shard_map/ppermute | solution.py:39
  149.1 6.9 %back.1 = f32[1024,512]{1,0:T(8,128)} custom-call(bf16[1024,512]{1,0:T(8,128)(2,1)} %bitcast.51, bf16[1,512]{1,0:T(2,128)(2,1)} %step.3, f32[8,512]{1,0:T(8,128)} %get-tuple-element.94.vec, bf16[3,512,1024]{2,1,0:T(8,128)(2,1)} %attn_bwd.3.g, f32[1024,512]{1,0:T(8,128)} %get-tuple-element.135.gx1, bf16[512,768]{1,0:T(8,128)(2,1)} %get-tuple-element.136.refs_0_, ...), custom_call_target="tpu_custom_call" | custom-call | flops 1610612736 | bytes 7340032 | tf_op jit(solution)/shard_map/back/pallas_call | solution.py:727
  160.1 2.1 %collective-permute-done.34 = bf16[104,512]{1,0:T(8,128)(2,1)S(1)} collective-permute-done((bf16[104,512]{1,0:T(8,128)(2,1)S(1)}, bf16[104,512]{1,0:T(8,128)(2,1)S(1)}, u32[]{:S(2)}, u32[]{:S(2)}) %collective-permute-start.34) | collective-permute-done | bytes 106528 | tf_op jit(solution)/shard_map/ppermute | solution.py:39
  162.2 1.7 collective-permute-start.35
  163.9 2.5 %collective-permute-start.39 = (bf16[160,512]{1,0:T(8,128)(2,1)S(1)}, bf16[160,512]{1,0:T(8,128)(2,1)S(1)}, u32[]{:S(2)}, u32[]{:S(2)}) collective-permute-start(bf16[160,512]{1,0:T(8,128)(2,1)S(1)} %add_convert_fusion.14.sa), channel_id=1, source_target_pairs={{0,8},{8,0},{16,24},{24,16},{1,9},{9,1},{17,25},{25,17},{2,10},{10... | collective-permute-start | bytes 491528 | tf_op jit(solution)/shard_map/ppermute | solution.py:39
  166.5 3.8 %collective-permute-done.35 = bf16[104,512]{1,0:T(8,128)(2,1)S(1)} collective-permute-done((bf16[104,512]{1,0:T(8,128)(2,1)S(1)}, bf16[104,512]{1,0:T(8,128)(2,1)S(1)}, u32[]{:S(2)}, u32[]{:S(2)}) %collective-permute-start.35) | collective-permute-done | bytes 106528 | tf_op jit(solution)/shard_map/ppermute | solution.py:39
  170.5 5.2 %collective-permute-done.40.ob = bf16[136,512]{1,0:T(8,128)(2,1)S(1)} collective-permute-done((bf16[136,512]{1,0:T(8,128)(2,1)S(1)}, bf16[136,512]{1,0:T(8,128)(2,1)S(1)}, u32[]{:S(2)}, u32[]{:S(2)}) %collective-permute-start.40) | collective-permute-done | bytes 139296 | tf_op jit(solution)/shard_map/ppermute | solution.py:39
  175.7 1.7 finish_rest.1
  (174 shorter events, 44.3 us)
Async XLA Ops:
  17.7 13.1 %collective-permute-start.7 = (bf16[192,256]{1,0:T(8,128)(2,1)S(1)}, bf16[192,256]{1,0:T(8,128)(2,1)S(1)}, u32[]{:S(2)}, u32[]{:S(2)}) collective-permute-start(bf16[192,256]{1,0:T(8,128)(2,1)S(1)} %get-tuple-element.95.refs_0_), channel_id=1, source_target_pairs={{0,2},{1,3},{2,0},{3,1},{4,6},{5,7},{6,4},{7,5},{8,10},{9,11},{10,... | collective-permute-start | bytes 294920 | tf_op jit(solution)/shard_map/ppermute | solution.py:43
  18.6 12.3 %collective-permute-start.8 = (bf16[192,256]{1,0:T(8,128)(2,1)S(1)}, bf16[192,256]{1,0:T(8,128)(2,1)S(1)}, u32[]{:S(2)}, u32[]{:S(2)}) collective-permute-start(bf16[192,256]{1,0:T(8,128)(2,1)S(1)} %get-tuple-element.95.refs_0_), channel_id=1, source_target_pairs={{0,4},{1,5},{2,6},{3,7},{4,0},{5,1},{6,2},{7,3},{8,12},{9,13},{10,... | collective-permute-start | bytes 294920 | tf_op jit(solution)/shard_map/ppermute | solution.py:43
  19.9 11.0 %collective-permute-start.9 = (bf16[192,256]{1,0:T(8,128)(2,1)S(1)}, bf16[192,256]{1,0:T(8,128)(2,1)S(1)}, u32[]{:S(2)}, u32[]{:S(2)}) collective-permute-start(bf16[192,256]{1,0:T(8,128)(2,1)S(1)} %get-tuple-element.95.refs_0_), channel_id=1, source_target_pairs={{0,6},{1,7},{2,4},{3,5},{4,2},{5,3},{6,0},{7,1},{8,14},{9,15},{10,... | collective-permute-start | bytes 294920 | tf_op jit(solution)/shard_map/ppermute | solution.py:43
  24.0 7.8 %collective-permute-start.10 = (bf16[192,256]{1,0:T(8,128)(2,1)S(1)}, bf16[192,256]{1,0:T(8,128)(2,1)S(1)}, u32[]{:S(2)}, u32[]{:S(2)}) collective-permute-start(bf16[192,256]{1,0:T(8,128)(2,1)S(1)} %get-tuple-element.95.refs_0_), channel_id=1, source_target_pairs={{0,1},{1,0},{2,3},{3,2},{4,5},{5,4},{6,7},{7,6},{8,9},{9,8},{10,11... | collective-permute-start | bytes 294920 | tf_op jit(solution)/shard_map/ppermute | solution.py:43
  32.8 18.4 %collective-permute-start.15 = (bf16[576,512]{1,0:T(8,128)(2,1)S(1)}, bf16[576,512]{1,0:T(8,128)(2,1)S(1)}, u32[]{:S(2)}, u32[]{:S(2)}) collective-permute-start(bf16[576,512]{1,0:T(8,128)(2,1)S(1)} %pack_rest.1.refs_0_), channel_id=1, source_target_pairs={{0,4},{1,5},{2,6},{3,7},{4,0},{5,1},{6,2},{7,3},{8,12},{9,13},{10,... | collective-permute-start | bytes 1769480 | tf_op jit(solution)/shard_map/ppermute | solution.py:43
  34.4 17.3 %collective-permute-start.14 = (bf16[576,512]{1,0:T(8,128)(2,1)S(1)}, bf16[576,512]{1,0:T(8,128)(2,1)S(1)}, u32[]{:S(2)}, u32[]{:S(2)}) collective-permute-start(bf16[576,512]{1,0:T(8,128)(2,1)S(1)} %pack_rest.1.refs_0_), channel_id=1, source_target_pairs={{0,2},{1,3},{2,0},{3,1},{4,6},{5,7},{6,4},{7,5},{8,10},{9,11},{10,... | collective-permute-start | bytes 1769480 | tf_op jit(solution)/shard_map/ppermute | solution.py:43
  45.7 18.7 %collective-permute-start.16 = (bf16[576,512]{1,0:T(8,128)(2,1)S(1)}, bf16[576,512]{1,0:T(8,128)(2,1)S(1)}, u32[]{:S(2)}, u32[]{:S(2)}) collective-permute-start(bf16[576,512]{1,0:T(8,128)(2,1)S(1)} %pack_rest.1.refs_0_), channel_id=1, source_target_pairs={{0,1},{1,0},{2,3},{3,2},{4,5},{5,4},{6,7},{7,6},{8,9},{9,8},{10,11... | collective-permute-start | bytes 1769480 | tf_op jit(solution)/shard_map/ppermute | solution.py:43
  51.2 13.2 %collective-permute-start.18 = (bf16[576,512]{1,0:T(8,128)(2,1)S(1)}, bf16[576,512]{1,0:T(8,128)(2,1)S(1)}, u32[]{:S(2)}, u32[]{:S(2)}) collective-permute-start(bf16[576,512]{1,0:T(8,128)(2,1)S(1)} %collective-permute-done.15.refs_2_), channel_id=1, source_target_pairs={{0,1},{1,0},{2,3},{3,2},{4,5},{5,4},{6,7},{7,6},{8,9},{9,8},{10,11... | collective-permute-start | bytes 1769480 | tf_op jit(solution)/shard_map/ppermute | solution.py:43
  51.8 12.6 %collective-permute-start.17 = (bf16[576,512]{1,0:T(8,128)(2,1)S(1)}, bf16[576,512]{1,0:T(8,128)(2,1)}, u32[]{:S(2)}, u32[]{:S(2)}) collective-permute-start(bf16[576,512]{1,0:T(8,128)(2,1)S(1)} %collective-permute-done.14.refs_1_), channel_id=1, source_target_pairs={{0,1},{1,0},{2,3},{3,2},{4,5},{5,4},{6,7},{7,6},{8,9},{9,8},{10,11... | collective-permute-start | bytes 1769480 | tf_op jit(solution)/shard_map/ppermute | solution.py:43
  51.9 11.9 %collective-permute-start.19 = (bf16[288,512]{1,0:T(8,128)(2,1)S(1)}, bf16[288,512]{1,0:T(8,128)(2,1)S(1)}, u32[]{:S(2)}, u32[]{:S(2)}) collective-permute-start(bf16[288,512]{1,0:T(8,128)(2,1)S(1)} %slice.78), channel_id=1, source_target_pairs={{0,2},{1,3},{2,0},{3,1},{4,6},{5,7},{6,4},{7,5},{8,10},{9,11},{10,... | collective-permute-start | bytes 884744 | tf_op jit(solution)/shard_map/ppermute | solution.py:43
  53.4 10.4 %collective-permute-start.20 = (bf16[288,512]{1,0:T(8,128)(2,1)S(1)}, bf16[288,512]{1,0:T(8,128)(2,1)}, u32[]{:S(2)}, u32[]{:S(2)}) collective-permute-start(bf16[288,512]{1,0:T(8,128)(2,1)S(1)} %slice.79), channel_id=1, source_target_pairs={{0,4},{1,5},{2,6},{3,7},{4,0},{5,1},{6,2},{7,3},{8,12},{9,13},{10,... | collective-permute-start | bytes 884744 | tf_op jit(solution)/shard_map/ppermute | solution.py:43
  93.1 8.0 %collective-permute-start.23 = (bf16[4,592,512]{2,1,0:T(8,128)(2,1)}, bf16[4,592,512]{2,1,0:T(8,128)(2,1)}, u32[]{:S(2)}, u32[]{:S(2)}) collective-permute-start(bf16[4,592,512]{2,1,0:T(8,128)(2,1)} %get-tuple-element.116), channel_id=1, source_target_pairs={{0,1},{1,0},{2,3},{3,2},{4,5},{5,4},{6,7},{7,6},{8,9},{9,8},{10,11... | collective-permute-start | bytes 7274504 | tf_op jit(solution)/shard_map/ppermute | solution.py:43
  106.1 18.2 %collective-permute-start.24 = (bf16[2,320,512]{2,1,0:T(8,128)(2,1)}, bf16[2,320,512]{2,1,0:T(8,128)(2,1)S(1)}, u32[]{:S(2)}, u32[]{:S(2)}) collective-permute-start(bf16[2,320,512]{2,1,0:T(8,128)(2,1)} %get-tuple-element.159), channel_id=1, source_target_pairs={{0,4},{1,5},{2,6},{3,7},{4,0},{5,1},{6,2},{7,3},{8,12},{9,13},{10,... | collective-permute-start | bytes 1966088 | tf_op jit(solution)/shard_map/ppermute | solution.py:43
  107.7 16.6 %collective-permute-start.25 = (bf16[2,272,512]{2,1,0:T(8,128)(2,1)}, bf16[2,272,512]{2,1,0:T(8,128)(2,1)S(1)}, u32[]{:S(2)}, u32[]{:S(2)}) collective-permute-start(bf16[2,272,512]{2,1,0:T(8,128)(2,1)} %get-tuple-element.158), channel_id=1, source_target_pairs={{0,2},{1,3},{2,0},{3,1},{4,6},{5,7},{6,4},{7,5},{8,10},{9,11},{10,... | collective-permute-start | bytes 1671176 | tf_op jit(solution)/shard_map/ppermute | solution.py:43
  125.2 10.6 %collective-permute-start.26 = (bf16[1,320,512]{2,1,0:T(8,128)(2,1)}, bf16[1,320,512]{2,1,0:T(8,128)(2,1)S(1)}, u32[]{:S(2)}, u32[]{:S(2)}) collective-permute-start(bf16[1,320,512]{2,1,0:T(8,128)(2,1)} %get-tuple-element.165), channel_id=1, source_target_pairs={{0,2},{1,3},{2,0},{3,1},{4,6},{5,7},{6,4},{7,5},{8,10},{9,11},{10,... | collective-permute-start | bytes 983048 | tf_op jit(solution)/shard_map/ppermute | solution.py:43
  127.5 8.3 %collective-permute-start.27 = (bf16[1,272,512]{2,1,0:T(8,128)(2,1)}, bf16[1,272,512]{2,1,0:T(8,128)(2,1)S(1)}, u32[]{:S(2)}, u32[]{:S(2)}) collective-permute-start(bf16[1,272,512]{2,1,0:T(8,128)(2,1)} %get-tuple-element.167), channel_id=1, source_target_pairs={{0,4},{1,5},{2,6},{3,7},{4,0},{5,1},{6,2},{7,3},{8,12},{9,13},{10,... | collective-permute-start | bytes 835592 | tf_op jit(solution)/shard_map/ppermute | solution.py:43
  138.3 17.8 %collective-permute-start.33 = (bf16[208,512]{1,0:T(8,128)(2,1)S(1)}, bf16[208,512]{1,0:T(8,128)(2,1)S(1)}, u32[]{:S(2)}, u32[]{:S(2)}) collective-permute-start(bf16[208,512]{1,0:T(8,128)(2,1)S(1)} %get-tuple-element.163), channel_id=1, source_target_pairs={{0,2},{1,3},{2,0},{3,1},{4,6},{5,7},{6,4},{7,5},{8,10},{9,11},{10,... | collective-permute-start | bytes 638984 | tf_op jit(solution)/shard_map/ppermute | solution.py:43
  143.7 12.4 %collective-permute-start.32 = (bf16[208,512]{1,0:T(8,128)(2,1)S(1)}, bf16[208,512]{1,0:T(8,128)(2,1)S(1)}, u32[]{:S(2)}, u32[]{:S(2)}) collective-permute-start(bf16[208,512]{1,0:T(8,128)(2,1)S(1)} %get-tuple-element.162), channel_id=1, source_target_pairs={{0,4},{1,5},{2,6},{3,7},{4,0},{5,1},{6,2},{7,3},{8,12},{9,13},{10,... | collective-permute-start | bytes 638984 | tf_op jit(solution)/shard_map/ppermute | solution.py:43
  145.0 11.1 %collective-permute-start.31 = (bf16[208,512]{1,0:T(8,128)(2,1)S(1)}, bf16[208,512]{1,0:T(8,128)(2,1)S(1)}, u32[]{:S(2)}, u32[]{:S(2)}) collective-permute-start(bf16[208,512]{1,0:T(8,128)(2,1)S(1)} %get-tuple-element.161), channel_id=1, source_target_pairs={{0,6},{1,7},{2,4},{3,5},{4,2},{5,3},{6,0},{7,1},{8,14},{9,15},{10,... | collective-permute-start | bytes 638984 | tf_op jit(solution)/shard_map/ppermute | solution.py:43
  146.0 12.5 %collective-permute-start.36 = (bf16[160,512]{1,0:T(8,128)(2,1)S(1)}, bf16[160,512]{1,0:T(8,128)(2,1)S(1)}, u32[]{:S(2)}, u32[]{:S(2)}) collective-permute-start(bf16[160,512]{1,0:T(8,128)(2,1)S(1)} %add_convert_fusion.15), channel_id=1, source_target_pairs={{0,16},{8,24},{16,0},{24,8},{1,17},{9,25},{17,1},{25,9},{2,18},{10... | collective-permute-start | bytes 491528 | tf_op jit(solution)/shard_map/ppermute | solution.py:39
  148.7 11.4 %collective-permute-start.37 = (bf16[136,512]{1,0:T(8,128)(2,1)S(1)}, bf16[136,512]{1,0:T(8,128)(2,1)S(1)}, u32[]{:S(2)}, u32[]{:S(2)}) collective-permute-start(bf16[136,512]{1,0:T(8,128)(2,1)S(1)} %add_convert_fusion.17), channel_id=1, source_target_pairs={{0,16},{8,24},{16,0},{24,8},{1,17},{9,25},{17,1},{25,9},{2,18},{10... | collective-permute-start | bytes 417800 | tf_op jit(solution)/shard_map/ppermute | solution.py:39
  162.2 8.1 %collective-permute-start.35 = (bf16[104,512]{1,0:T(8,128)(2,1)S(1)}, bf16[104,512]{1,0:T(8,128)(2,1)S(1)}, u32[]{:S(2)}, u32[]{:S(2)}) collective-permute-start(bf16[104,512]{1,0:T(8,128)(2,1)S(1)} %add_convert_fusion.19), channel_id=1, source_target_pairs={{0,16},{8,24},{16,0},{24,8},{1,17},{9,25},{17,1},{25,9},{2,18},{10... | collective-permute-start | bytes 319496 | tf_op jit(solution)/shard_map/ppermute | solution.py:39
  163.9 11.8 %collective-permute-start.39 = (bf16[160,512]{1,0:T(8,128)(2,1)S(1)}, bf16[160,512]{1,0:T(8,128)(2,1)S(1)}, u32[]{:S(2)}, u32[]{:S(2)}) collective-permute-start(bf16[160,512]{1,0:T(8,128)(2,1)S(1)} %add_convert_fusion.14.sa), channel_id=1, source_target_pairs={{0,8},{8,0},{16,24},{24,16},{1,9},{9,1},{17,25},{25,17},{2,10},{10... | collective-permute-start | bytes 491528 | tf_op jit(solution)/shard_map/ppermute | solution.py:39
  166.5 9.2 %collective-permute-start.40 = (bf16[136,512]{1,0:T(8,128)(2,1)S(1)}, bf16[136,512]{1,0:T(8,128)(2,1)S(1)}, u32[]{:S(2)}, u32[]{:S(2)}) collective-permute-start(bf16[136,512]{1,0:T(8,128)(2,1)S(1)} %add_convert_fusion.16.sb), channel_id=1, source_target_pairs={{0,8},{8,0},{16,24},{24,16},{1,9},{9,1},{17,25},{25,17},{2,10},{10... | collective-permute-start | bytes 417800 | tf_op jit(solution)/shard_map/ppermute | solution.py:39
  (58 other events, 408.8 us)

commit v6 on v5

--- a/solution.py
+++ b/solution.py
@@ -106,7 +106,7 @@
     return [b for b in (2 << i for i in range(16)) if b < nr]
 
 
-GROUPS = 2
+GROUPS = 1
 
 
 def pack_first_body(me, w, upb, *refs):
@@ -129,7 +129,7 @@
 
     rows = [a for v in vecs for a in spot(v[...].astype(f32))] + spot(upb[...].astype(f32))
     b = jnp.concatenate(rows + [jnp.zeros((VROWS - len(rows), LANES), f32)], axis=0).astype(bf16)
-    outs[0][3 * r :, :] = jnp.concatenate([b, jnp.zeros((VROWS, gw - LANES), bf16)], axis=1)
+    outs[0][3 * r :, :] = jnp.concatenate([b, jnp.zeros((VROWS, gw - LANES), bf16)], axis=1) if gw > LANES else b
 
 
 def whole(n):
@@ -148,7 +148,7 @@
     return pl.pallas_call(
         pack_first_body,
         grid_spec=pltpu.PrefetchScalarGridSpec(num_scalar_prefetch=1, grid=(1,), in_specs=once(*args), out_specs=once(*outs)),
-        out_shape=outs, compiler_params=pltpu.CompilerParams(vmem_limit_bytes=8 << 20), name="pack_first", cost_estimate=cost(0, 4 * w.size),
+        out_shape=outs, compiler_params=cp(), name="pack_first", cost_estimate=cost(0, 4 * w.size),
     )(me, *args)
 
 
@@ -165,7 +165,7 @@
     out = S(((wo.size + wu.size + wd.size) // D, D), bf16)
     return pl.pallas_call(
         pack_rest_body, grid=(1,), in_specs=once(wo, wu, wd), out_specs=once(out)[0],
-        out_shape=out, compiler_params=pltpu.CompilerParams(vmem_limit_bytes=8 << 20), name="pack_rest", cost_estimate=cost(0, 4 * wu.size),
+        out_shape=out, compiler_params=cp(), name="pack_rest", cost_estimate=cost(0, 4 * wu.size),
     )(wo, wu, wd)
 
 
@@ -189,17 +189,18 @@
     return jnp.concatenate([lo[a:h, :], hi[: b - h, :]], axis=0)
 
 
-def finish_rest_body(r, rf, n, ids, sa, oa, sb, ob, down, up, out, upb, *vecs):
+def finish_rest_body(r, rf, n, ids, s, o, down, up, out, upb, *vecs):
     D = out.shape[1]
     nf = up.shape[1] // D
 
-    def run(la, ha, lb, hb):
-        f = lambda x, y, a, b: rows_of(x, y, a, b).astype(f32)
-        down[...] = f(la, ha, 0, rf)
-        out[...] = f(la, ha, rf, rf + r)
+    def run(lo, hi):
+        f = lambda a, b: rows_of(lo, hi, a, b).astype(f32)
+        down[...] = f(0, rf)
+        out[...] = f(rf, rf + r)
         for j in range(nf):
-            up[:, j * D : (j + 1) * D] = f(lb, hb, j * r, (j + 1) * r)
-        v = f(lb, hb, nf * r, nf * r + VROWS)
+            up[:, j * D : (j + 1) * D] = f(rf + (j + 1) * r, rf + (j + 2) * r)
+        b = rf + (nf + 1) * r
+        v = f(b, b + VROWS)
         me = ids[0]
         tiles = [v[0:8, t * LANES : (t + 1) * LANES] for t in range(D // LANES)]
         x = own_lanes(tiles, me, r)
@@ -210,22 +211,22 @@
 
     @pl.when(ids[1] == 0)
     def _():
-        run(sa, oa, sb, ob)
+        run(s, o)
 
     @pl.when(ids[1] == 1)
     def _():
-        run(oa, sa, ob, sb)
-
-
-def finish_rest(ids, sa, oa, sb, ob, r, rf, nf, n):
-    D = sa.shape[1]
+        run(o, s)
+
+
+def finish_rest(ids, s, o, r, rf, nf, n):
+    D = s.shape[1]
     row1 = lambda w: S((1, w), f32)
     return pl.pallas_call(
         functools.partial(finish_rest_body, r, rf, n),
-        in_specs=[pl.BlockSpec(memory_space=pltpu.SMEM)] + whole(4), out_specs=whole(8),
+        in_specs=[pl.BlockSpec(memory_space=pltpu.SMEM)] + whole(2), out_specs=whole(8),
         out_shape=[S((rf, D), f32), S((r, nf * D), f32), S((r, D), f32), row1(nf * D // n)] + [row1(r)] * 4,
-        compiler_params=pltpu.CompilerParams(vmem_limit_bytes=16 << 20), name="finish_rest", cost_estimate=cost(0, 8 * sa.size),
-    )(ids, sa, oa, sb, ob)
+        compiler_params=pltpu.CompilerParams(vmem_limit_bytes=16 << 20), name="finish_rest", cost_estimate=cost(0, 8 * s.size),
+    )(ids, s, o)
 
 
 def finish_first_body(ids, s, o, w, gain, bias, qkv, gg, gb, qb, vb):
@@ -312,28 +313,37 @@
     return [seg(j) for j in range(3)]
 
 
-def front_body(scale, n, meta, me, tok, step, *refs):
+def start_body(tok, step, nx, xht):
+    n, _ = norm(tok[...].astype(f32) + step[...].astype(f32))
+    nx[...] = n
+    xht[...] = n.astype(bf16).T
+
+
+def start(tok, step, bm=256):
+    T, D = tok.shape
+    rows = pl.BlockSpec((bm, D), lambda i: (i, 0))
+    return pl.pallas_call(
+        start_body, grid=(T // bm,),
+        in_specs=[rows, pl.BlockSpec((1, D), lambda i: (0, 0))], out_specs=[rows, pl.BlockSpec((D, bm), lambda i: (0, i))],
+        out_shape=[S((T, D), f32), S((D, T), bf16)], compiler_params=cp(), name="start", cost_estimate=cost(20 * T * D, 8 * T * D),
+    )(tok, step)
+
+
+def front_body(scale, n, meta, me, nx, *refs):
     np_ = len(meta)
     pieces = refs[:np_]
-    xht, hs, kv, qkvt, w, vec, upb, vbuf, sems = refs[np_:]
-    D = tok.shape[-1]
+    kv, qkvt, w, vec, upb, vbuf, sems = refs[np_:]
+    D = nx.shape[-1]
     r = D // n
     FF = upb.shape[1]
-    first = pl.program_id(0) == 0
     segs = [(3 * r, VROWS, lambda s, o, c: vbuf.at[s, pl.ds(o, c)], LANES)] + weight_segs(w, r)
 
-    @pl.when(first)
-    def _():
-        for c in pull(me[0], pieces, meta, segs, sems):
+    @pl.when(pl.program_id(0) == 0)
+    def _():
+        cs = pull(me[0], pieces, meta, segs, sems)
+        for c in cs:
             c.start()
-
-    x = tok[...].astype(f32) + step[...].astype(f32)
-    nx, _ = norm(x)
-    xht[...] = nx.astype(bf16).T
-
-    @pl.when(first)
-    def _():
-        for c in pull(me[0], pieces, meta, segs, sems):
+        for c in cs:
             c.wait()
         per = LANES // r
         tiles = [sum(vbuf[s, 0:8, :].astype(f32) for s in range(t * per, (t + 1) * per)) for t in range(D // LANES)]
@@ -347,25 +357,8 @@
         upb[...] = jnp.concatenate(rows, axis=1)
 
     v = vec[...]
-    h = (nx * row(v, 0) + row(v, 1)).astype(bf16)
-    hs[...] = h
+    h = (nx[...] * row(v, 0) + row(v, 1)).astype(bf16)
     project(v, h, w, kv, qkvt, 0, scale)
-
-
-def front_next_body(scale, n, meta, grp, me, hs, vec, *refs):
-    np_ = len(meta)
-    pieces = refs[:np_]
-    kv, qkvt, w, sems = refs[np_ + 2 :]
-
-    @pl.when(pl.program_id(0) == 0)
-    def _():
-        cs = pull(me[0], pieces, meta, weight_segs(w, w.shape[0] // n), sems)
-        for c in cs:
-            c.start()
-        for c in cs:
-            c.wait()
-
-    project(vec[...], hs[...], w, kv, qkvt, grp, scale)
 
 
 S = jax.ShapeDtypeStruct
@@ -376,41 +369,21 @@
     return pl.CostEstimate(flops=int(flops), bytes_accessed=int(nbytes), transcendentals=int(tr))
 
 
-def front(me, tok, step, pieces, n, FF, bm=512):
-    T, D = tok.shape
+def front(me, nx, pieces, n, FF, bm=512):
+    T, D = nx.shape
     scale = 1.0 / math.sqrt(D // HEADS)
-    gw = D // GROUPS
     meta = tuple((k, r0) for k, r0, _ in pieces)
     keep = lambda *sh: pl.BlockSpec(sh, lambda i, m: (0,) * len(sh))
     return pl.pallas_call(
         functools.partial(front_body, scale, n, meta),
         grid_spec=pltpu.PrefetchScalarGridSpec(
             num_scalar_prefetch=1, grid=(T // bm,),
-            in_specs=[pl.BlockSpec((bm, D), lambda i, m: (i, 0)), keep(1, D)] + [ANY] * len(pieces),
-            out_specs=[pl.BlockSpec((D, bm), lambda i, m: (0, i)), pl.BlockSpec((bm, D), lambda i, m: (i, 0)), pl.BlockSpec((2, bm, gw), lambda i, m: (0, i, 0)), pl.BlockSpec((3, gw, bm), lambda i, m: (0, 0, i)), keep(D, 3 * gw), keep(8, D), keep(1, FF)],
+            in_specs=[pl.BlockSpec((bm, D), lambda i, m: (i, 0))] + [ANY] * len(pieces),
+            out_specs=[pl.BlockSpec((2, bm, D), lambda i, m: (0, i, 0)), pl.BlockSpec((3, D, bm), lambda i, m: (0, 0, i)), keep(D, 3 * D), keep(8, D), keep(1, FF)],
             scratch_shapes=[pltpu.VMEM((n, VROWS, LANES), bf16), pltpu.SemaphoreType.DMA((8 * len(pieces),))]),
-        out_shape=[S((D, T), bf16), S((T, D), bf16), S((2, T, D), bf16), S((3, D, T), bf16), S((D, 3 * gw), bf16), S((8, D), f32), S((1, FF), f32)],
-        compiler_params=cp(), name="front", cost_estimate=cost(6 * T * D * gw, 8 * T * D),
-    )(me, tok, step, *[a for _, _, a in pieces])
-
-
-def front_next(me, hs, vec, pieces, kv, qkvt, grp, n, bm=512):
-    T, D = hs.shape
-    scale = 1.0 / math.sqrt(D // HEADS)
-    gw = D // GROUPS
-    meta = tuple((k, r0) for k, r0, _ in pieces)
-    q = len(pieces)
-    return pl.pallas_call(
-        functools.partial(front_next_body, scale, n, meta, grp),
-        grid_spec=pltpu.PrefetchScalarGridSpec(
-            num_scalar_prefetch=1, grid=(T // bm,),
-            in_specs=[pl.BlockSpec((bm, D), lambda i, m: (i, 0)), pl.BlockSpec(vec.shape, lambda i, m: (0, 0))] + [ANY] * (q + 2),
-            out_specs=[pl.BlockSpec((2, bm, gw), lambda i, m: (0, i, grp)), pl.BlockSpec((3, gw, bm), lambda i, m: (0, grp, i)), pl.BlockSpec((D, 3 * gw), lambda i, m: (0, 0))],
-            scratch_shapes=[pltpu.SemaphoreType.DMA((8 * q,))]),
-        out_shape=[S((2, T, D), bf16), S((3, D, T), bf16), S((D, 3 * gw), bf16)],
-        input_output_aliases={3 + q: 0, 4 + q: 1},
-        compiler_params=cp(), name="front_next", cost_estimate=cost(6 * T * D * gw, 6 * T * D),
-    )(me, hs, vec, *[a for _, _, a in pieces], kv, qkvt)
+        out_shape=[S((2, T, D), bf16), S((3, D, T), bf16), S((D, 3 * D), bf16), S((8, D), f32), S((1, FF), f32)],
+        compiler_params=cp(), name="front", cost_estimate=cost(6 * T * D * D, 12 * T * D),
+    )(me, nx, *[a for _, _, a in pieces])
 
 
 def attn_fwd_body(HD, bi, CR, ln, k, qt, vt, *refs):
@@ -744,17 +717,13 @@
     packs = pack_first(mes, qkv_weight, [ln1_gain, ln1_bias, q_bias, v_bias, out_bias, ln2_gain, ln2_bias, down_bias], up_bias)
     pack2 = pack_rest(out_weight, up_weight, down_weight)
     NP = HEADS // 2
-    GP = NP // GROUPS
-    arrays = lambda ps: [a for _, _, a in ps[1:]]
-    pieces = gather_direct(packs[0], n)
-    xht, hs, kv, qkvt, wa, vec, upb = front(mes, tok, after(step, pack2), pieces, n, FF)
-    nextp = gather_direct(packs[1], n, vec)
-    fw = attn_fwd(lengths, kv, qkvt, 0, GP, [])
-    kv, qkvt, wb = front_next(mes, hs, after(vec, fw[4]), nextp, kv, qkvt, 1, n)
-    fw2 = attn_fwd(lengths, kv, qkvt, GP, NP - GP, fw)
-    ws = [wa, wb]
+    nx, xht = start(tok, step)
+    pieces = gather_direct(packs[0], n, xht, pack2)
+    kv, qkvt, w, vec, upb = front(mes, nx, pieces, n, FF)
+    fw = attn_fwd(lengths, kv, qkvt, 0, NP // 2, [])
+    fw2 = attn_fwd(lengths, kv, qkvt, NP // 2, NP // 2, fw)
     et, mixed, mixedt, mixedf, linv = fw2
-    pieces2 = gather_forward(after(pack2, vec, *arrays(nextp)), n, wb, linv)
+    pieces2 = gather_forward(after(pack2, *[a for _, _, a in pieces[1:]]), n, fw[4], linv)
     out, gx1, gmt, keep, send = ffn(lengths, mes, tok, step, vec, upb, cot, mixed, mixedt, pieces2, n)
     bwd = lambda p, c, g, *deps: attn_bwd(kv, qkvt, after(gmt, *deps) if deps else gmt, mixedf, linv, et, p, c, g)
     ra = rf + r
@@ -783,25 +752,23 @@
     p2 = [add16(keep[k], got[k]) for k in range(n // 2)]
     far2 = spread(p2)
     ga, gb, _ = lax.optimization_barrier((ga, gb, keep))
-    ua = add16(ka, ga)[0]
-    ub = add16(kb, gb)[0]
-    ua, ub = lax.optimization_barrier((ua, ub))
-    ma, oa, xa = rep_half(ua)
-    mb, ob, xb = rep_half(ub)
-    za = add16(ma, after(oa, p2[1]))
-    zb = add16(mb, after(ob, p2[1]))
-    tg = back(tok, after(step, za, zb, *p2[1:]), vec, ws, g, gx1)
+    got = swap(send, 1)
+    p2 = [add16(keep[k], got[k]) for k in range(n // 2)]
+    far2 = spread(p2)
+    own1 = jnp.concatenate([add16(ka, ga)[0], add16(kb, gb)[0]], axis=0)
+    m1, o1, x1 = rep_half(own1)
+    z1 = add16(m1, after(o1, *p2[1:]))
+    tg = back(tok, after(step, z1, *p2[1:]), vec, [w], g, gx1)
     own2 = total(p2[0], [after(a, tg) for a in far2])
     m2, o2, x2 = rep_half(own2)
     z2 = add16(m2, o2)
     for b in rep_steps():
-        pa, pb, pz = rep_perm(za, b), rep_perm(zb, b), rep_perm(z2, b)
-        za = add16(za, after(pa, x2))
-        zb = add16(zb, after(pb, x2))
-        z2 = add16(z2, after(pz, za, zb))
-    oa, ob, o2 = rep_perm(za, 1), rep_perm(zb, 1), rep_perm(z2, 1)
+        pa, pz = rep_perm(z1, b), rep_perm(z2, b)
+        z1 = add16(z1, after(pa, x2))
+        z2 = add16(z2, after(pz, z1))
+    o1, o2 = rep_perm(z1, 1), rep_perm(z2, 1)
     ids = jnp.stack([me, (lax.axis_index("rep") % 2).astype(jnp.int32)])
-    g_down, g_up, g_out, g_upb, g_ob, g_g2, g_b2, g_db = finish_rest(ids, za, oa, zb, ob, r, rf, nc, n)
+    g_down, g_up, g_out, g_upb, g_ob, g_g2, g_b2, g_db = finish_rest(ids, z1, o1, r, rf, nc, n)
     g_qkv, g_g1, g_b1, g_q, g_v = finish_first(ids, z2, after(o2, g_out), qkv_weight, ln1_gain, ln1_bias)
     flat = lambda a: a.reshape(-1)
     return (out[None], tg[None], flat(g_g1), flat(g_b1), g_qkv, flat(g_q), flat(g_v), g_out, flat(g_ob), flat(g_g2), flat(g_b2), g_up, flat(g_upb), g_down, flat(g_db))

time: 180 us -> 168 us (0.933)
  local copies, waits for them, and re-layouts: 11.2 us -> 2.39 us
  waiting for transfers between devices: 28.3 us -> 24.1 us
  Pallas kernels: 97.2 us -> 101 us
  starting transfers between devices: 32.9 us -> 29.2 us
    unnamed x82 -> x42, local copies, waits for them, and re-layouts: 10.5 us -> 1.12 us
    ppermute x32 -> x25, starting transfers between devices: 21.6 us -> 19.1 us  [swap(): return lax.ppermute(x, 'shard', xor_perm(lax.axis_size('shard'), k))]
    ppermute x32 -> x25, waiting for transfers between devices: 10.4 us -> 7.94 us  [swap(): return lax.ppermute(x, 'shard', xor_perm(lax.axis_size('shard'), k))]
    pallas_call x1, Pallas kernels: 0.04 us -> 1.92 us  [pack_rest(): pl.pallas_call(pack_rest_body, grid=(1,), in_specs=once(wo, wu, wd), out_...]
    ppermute x9 -> x6, waiting for transfers between devices: 17.9 us -> 16.1 us  [rep_perm(): return lax.ppermute(x, 'rep', xor_perm(lax.axis_size('rep'), b))]
    ppermute x9 -> x6, starting transfers between devices: 11.2 us -> 10.1 us  [rep_perm(): return lax.ppermute(x, 'rep', xor_perm(lax.axis_size('rep'), b))]
    convert_element_type x11 -> x9, other arithmetic: 7.04 us -> 6.6 us  [add16(): return (a.astype(f32) + b.astype(f32)).astype(bf16)]
  transfers between devices with their start and end apart: 41 -> 31, of which waited for: 16 -> 12; matrix products, arithmetic and copies ran while one was open for 1% -> 2% of each run, Pallas kernels for 39% -> 43%
where the time goes in v6:
time: 168 us; the launch traced here: 167 us
  Pallas kernels  101 us (60%)
  starting transfers between devices  29.2 us (17%)
  waiting for transfers between devices  24.1 us (14%)
  other arithmetic  8.34 us (5%)
  local copies, waits for them, and re-layouts  2.39 us (1%)
  between operations  1.73 us (1%)
    pallas_call x1, Pallas kernels, ffn(): pl.pallas_call(functools.partial(ffn_body, n, meta, min(1024, FF)), grid_...  26.3 us
    pallas_call x2, Pallas kernels, attn_bwd(): pl.pallas_call(functools.partial(attn_bwd_body, HD, 1.0 / math.sqrt(HD),...  23.9 us
    pallas_call x2, Pallas kernels, attn_fwd(): pl.pallas_call(functools.partial(attn_fwd_body, HD, bi, min(256, T)), gri...  20 us
    ppermute x25, starting transfers between devices, swap(): return lax.ppermute(x, 'shard', xor_perm(lax.axis_size('shard'), k))  19.1 us
    ppermute x6, waiting for transfers between devices, rep_perm(): return lax.ppermute(x, 'rep', xor_perm(lax.axis_size('rep'), b))  16.1 us
    ppermute x6, starting transfers between devices, rep_perm(): return lax.ppermute(x, 'rep', xor_perm(lax.axis_size('rep'), b))  10.1 us
    ppermute x25, waiting for transfers between devices, swap(): return lax.ppermute(x, 'shard', xor_perm(lax.axis_size('shard'), k))  7.94 us
    pallas_call x1, Pallas kernels, front(): pl.pallas_call(functools.partial(front_body, scale, n, meta), grid_spec=p...  7.48 us
  transfers between devices with their start and end apart: 31, of which 12 were waited for; matrix products, arithmetic and copies ran while one was open for 2% of the time, Pallas kernels for 43%

profile of v6, /device:TPU:0, one launch (start us, length us, event | category | flops | bytes accessed | tf_op | source)
XLA Modules:
  0.0 167.1 jit_solution(1975064095248854057)
XLA Ops:
  1.9 1.8 %pack_first.1.refs_0_ = bf16[208,512]{1,0:T(8,128)(2,1)} custom-call(s32[1]{0:T(128)} %bitcast.me, bf16[64,1536]{1,0:T(8,128)(2,1)} %w.3, bf16[1,256]{1,0:T(2,128)(2,1)} %broadcast_in_dim.39.upb, bf16[1,64]{1,0:T(2,128)(2,1)} %bitcast.38, bf16[1,64]{1,0:T(2,128)(2,1)} %bitcast.40, bf16[1,64]{1,0:T(2,128)(2,1)} %bitcast.46, bf16[1,64]{1,0:T(2,128)(2,1)} %bitcast.47, ...), custom_call_target="tpu_custom_call" | custom-call | bytes 393216 | tf_op jit(solution)/shard_map/pack_first/pallas_call | solution.py:148
  3.6 2.9 %collective-permute-start = (bf16[208,512]{1,0:T(8,128)(2,1)}, bf16[208,512]{1,0:T(8,128)(2,1)S(1)}, u32[]{:S(2)}, u32[]{:S(2)}) collective-permute-start(bf16[208,512]{1,0:T(8,128)(2,1)} %pack_first.1.refs_0_), channel_id=1, source_target_pairs={{0,2},{1,3},{2,0},{3,1},{4,6},{5,7},{6,4},{7,5},{8,10},{9,11},{10,... | collective-permute-start | bytes 638984 | tf_op jit(solution)/shard_map/ppermute | solution.py:43
  8.1 1.9 %pack_rest.1.refs_0_ = bf16[576,512]{1,0:T(8,128)(2,1)} custom-call(bf16[64,512]{1,0:T(8,128)(2,1)} %wo.1, bf16[64,2048]{1,0:T(8,128)(2,1)} %wu.1, bf16[256,512]{1,0:T(8,128)(2,1)} %wd.1), custom_call_target="tpu_custom_call" | custom-call | bytes 524288 | tf_op jit(solution)/shard_map/pack_rest/pallas_call | solution.py:166
  10.0 4.2 %start.1 = (f32[1024,512]{1,0:T(8,128)}, bf16[512,1024]{1,0:T(8,128)(2,1)}) custom-call(bf16[1024,512]{1,0:T(8,128)(2,1)} %bitcast.42, bf16[1,512]{1,0:T(2,128)(2,1)} %step.4), custom_call_target="tpu_custom_call" | custom-call | flops 10485760 | bytes 4194304 | tf_op jit(solution)/shard_map/start/pallas_call | solution.py:325
  14.8 3.2 %collective-permute-done.1.refs_2_ = bf16[208,512]{1,0:T(8,128)(2,1)S(1)} collective-permute-done((bf16[208,512]{1,0:T(8,128)(2,1)}, bf16[208,512]{1,0:T(8,128)(2,1)S(1)}, u32[]{:S(2)}, u32[]{:S(2)}) %collective-permute-start.1) | collective-permute-done | bytes 213024 | tf_op jit(solution)/shard_map/ppermute | solution.py:43
  22.7 7.5 %front.1 = (bf16[2,1024,512]{2,1,0:T(8,128)(2,1)}, bf16[3,512,1024]{2,1,0:T(8,128)(2,1)}, bf16[512,1536]{1,0:T(8,128)(2,1)}, f32[8,512]{1,0:T(8,128)}, f32[1,2048]{1,0:T(1,128)}) custom-call(s32[1]{0:T(128)} %bitcast.me, f32[1024,512]{1,0:T(8,128)} %get-tuple-element.75.nx, bf16[208,512]{1,0:T(8,128)(2,1)} %pack_first.1.refs_0_, ...), custom_call_target="tpu_custom_call" | custom-call | flops 1610612736 | bytes 6291456 | tf_op jit(solution)/shard_map/front/pallas_call | solution.py:377
  30.2 10.0 %attn_fwd.2 = (bf16[8,1024,1024]{2,1,0:T(8,128)(2,1)}, bf16[1024,512]{1,0:T(8,128)(2,1)}, bf16[512,1024]{1,0:T(8,128)(2,1)}, f32[512,1024]{1,0:T(8,128)}, f32[4,8,1024]{2,1,0:T(8,128)}) custom-call(s32[1]{0:T(128)S(6)} %copy.44.ln, bf16[2,1024,512]{2,1,0:T(8,128)(2,1)} %get-tuple-element.82.k.v, bf16[3,512,1024]{2,1,0:T(8,128)(2,1)} %get-tuple-element.83.qt.vt.kt, ...), custom_call_target="tpu_custom_call" | custom-call | flops 4294967296 | bytes 8388608 | tf_op jit(solution)/shard_map/attn_fwd/pallas_call | solution.py:450
  42.9 10.0 %attn_fwd.3 = (bf16[8,1024,1024]{2,1,0:T(8,128)(2,1)}, bf16[1024,512]{1,0:T(8,128)(2,1)}, bf16[512,1024]{1,0:T(8,128)(2,1)}, f32[512,1024]{1,0:T(8,128)}, f32[4,8,1024]{2,1,0:T(8,128)}) custom-call(s32[1]{0:T(128)S(6)} %copy.44.ln, ...), custom_call_target="tpu_custom_call", output_to_operand_aliasing={{0}: (4, {}), {1}: (5, {}), {2}: (6, {}), {3}: (7, {}), {4}... | custom-call | flops 4294967296 | bytes 8388608 | tf_op jit(solution)/shard_map/attn_fwd/pallas_call | solution.py:450
  56.1 26.3 %ffn.1 = (bf16[1024,512]{1,0:T(8,128)(2,1)}, f32[1024,512]{1,0:T(8,128)}, bf16[512,1024]{1,0:T(8,128)(2,1)}, bf16[4,592,512]{2,1,0:T(8,128)(2,1)}, bf16[4,592,512]{2,1,0:T(8,128)(2,1)}) custom-call(s32[1]{0:T(128)S(6)} %copy.44.ln, s32[1]{0:T(128)} %bitcast.me, bf16[1024,512]{1,0:T(8,128)(2,1)} %bitcast.43, bf16[1,512]{1,0:T(2,128)(2,1)} %step.4, ...), custom_call_target="tpu_custom_call" | custom-call | flops 14495514624 | bytes 8388608 | tf_op jit(solution)/shard_map/ffn/pallas_call | solution.py:592
  82.6 7.8 %attn_bwd.2.refs_0_ = bf16[3,512,1024]{2,1,0:T(8,128)(2,1)} custom-call(bf16[2,1024,512]{2,1,0:T(8,128)(2,1)} %get-tuple-element.82.k.v, bf16[3,512,1024]{2,1,0:T(8,128)(2,1)} %get-tuple-element.83.qt.vt.kt, bf16[3,512,1024]{2,1,0:T(8,128)(2,1)} %get-tuple-element.83.qt.vt.kt, bf16[512,1024]{1,0:T(8,128)(2,1)} %get-tuple-element.104.gt, ...), custom_call_target="tpu_custom_call" | custom-call | flops 4294967296 | bytes 4194304 | tf_op jit(solution)/shard_map/attn_bwd/pallas_call | solution.py:636
  90.4 2.4 %add_convert_fusion.2 = (bf16[2,272,512]{2,1,0:T(8,128)(2,1)S(1)}, bf16[2,272,512]{2,1,0:T(8,128)(2,1)}) fusion(bf16[4,592,512]{2,1,0:T(8,128)(2,1)} %collective-permute-done.16, bf16[4,592,512]{2,1,0:T(8,128)(2,1)S(1)} %copy-done.3), kind=kLoop, calls=%fused_computation.2 | loop fusion | flops 2228224 | bytes 3342336 | tf_op jit(solution)/shard_map/convert_element_type | solution.py:82
  92.8 2.5 %add_convert_fusion = (bf16[2,320,512]{2,1,0:T(8,128)(2,1)}, bf16[2,320,512]{2,1,0:T(8,128)(2,1)S(1)}) fusion(bf16[4,592,512]{2,1,0:T(8,128)(2,1)} %collective-permute-done.16, bf16[4,592,512]{2,1,0:T(8,128)(2,1)S(1)} %copy-done.3), kind=kLoop, calls=%fused_computation | loop fusion | flops 2621440 | bytes 3932160 | tf_op jit(solution)/shard_map/convert_element_type | solution.py:82
  97.4 16.0 %attn_bwd.3.g = bf16[3,512,1024]{2,1,0:T(8,128)(2,1)} custom-call(bf16[2,1024,512]{2,1,0:T(8,128)(2,1)} %get-tuple-element.82.k.v, bf16[3,512,1024]{2,1,0:T(8,128)(2,1)} %get-tuple-element.83.qt.vt.kt, bf16[3,512,1024]{2,1,0:T(8,128)(2,1)} %get-tuple-element.83.qt.vt.kt, bf16[512,1024]{1,0:T(8,128)(2,1)} %get-tuple-element.104.gt, ...), custom_call_target="tpu_custom_call", output_to_operand_aliasing={{}: (7, {})} | custom-call | flops 12884901888 | bytes 12582912 | tf_op jit(solution)/shard_map/attn_bwd/pallas_call | solution.py:636
  116.2 5.6 %wqkv.1 = (bf16[4,208,512]{2,1,0:T(8,128)(2,1)}, bf16[4,208,512]{2,1,0:T(8,128)(2,1)}) custom-call(s32[1]{0:T(128)} %bitcast.me, bf16[512,1024]{1,0:T(8,128)(2,1)} %get-tuple-element.107.xht, bf16[3,512,1024]{2,1,0:T(8,128)(2,1)} %attn_bwd.3.g), custom_call_target="tpu_custom_call" | custom-call | flops 1610612736 | bytes 5242880 | tf_op jit(solution)/shard_map/wqkv/pallas_call | solution.py:673
  127.9 2.1 %collective-permute-start.23 = (bf16[208,512]{1,0:T(8,128)(2,1)}, bf16[208,512]{1,0:T(8,128)(2,1)S(1)}, u32[]{:S(2)}, u32[]{:S(2)}) collective-permute-start(bf16[208,512]{1,0:T(8,128)(2,1)} %get-tuple-element.139), channel_id=1, source_target_pairs={{0,6},{1,7},{2,4},{3,5},{4,2},{5,3},{6,0},{7,1},{8,14},{9,15},{10,... | collective-permute-start | bytes 638984 | tf_op jit(solution)/shard_map/ppermute | solution.py:43
  131.4 1.8 %collective-permute-done.21 = bf16[296,512]{1,0:T(8,128)(2,1)S(1)} collective-permute-done((bf16[296,512]{1,0:T(8,128)(2,1)S(1)}, bf16[296,512]{1,0:T(8,128)(2,1)S(1)}, u32[]{:S(2)}, u32[]{:S(2)}) %collective-permute-start.21) | collective-permute-done | bytes 303136 | tf_op jit(solution)/shard_map/ppermute | solution.py:39
  133.6 2.6 %collective-permute-start.28 = (bf16[296,512]{1,0:T(8,128)(2,1)S(1)}, bf16[296,512]{1,0:T(8,128)(2,1)S(1)}, u32[]{:S(2)}, u32[]{:S(2)}) collective-permute-start(bf16[296,512]{1,0:T(8,128)(2,1)S(1)} %add_convert_fusion.8), channel_id=1, source_target_pairs={{0,16},{8,24},{16,0},{24,8},{1,17},{9,25},{17,1},{25,9},{2,18},{10... | collective-permute-start | bytes 909320 | tf_op jit(solution)/shard_map/ppermute | solution.py:39
  136.2 7.0 %back.1 = f32[1024,512]{1,0:T(8,128)} custom-call(bf16[1024,512]{1,0:T(8,128)(2,1)} %bitcast.44, bf16[1,512]{1,0:T(2,128)(2,1)} %step.4, f32[8,512]{1,0:T(8,128)} %get-tuple-element.80.vec, bf16[3,512,1024]{2,1,0:T(8,128)(2,1)} %attn_bwd.3.g, f32[1024,512]{1,0:T(8,128)} %get-tuple-element.114.gx1, bf16[512,1536]{1,0:T(8,128)(2,1)} %get-tuple-element.115.refs_0_), custom_call_target="tpu_custom_call" | custom-call | flops 1610612736 | bytes 7340032 | tf_op jit(solution)/shard_map/back/pallas_call | solution.py:700
  145.0 2.9 %collective-permute-done.28 = bf16[296,512]{1,0:T(8,128)(2,1)S(1)} collective-permute-done((bf16[296,512]{1,0:T(8,128)(2,1)S(1)}, bf16[296,512]{1,0:T(8,128)(2,1)S(1)}, u32[]{:S(2)}, u32[]{:S(2)}) %collective-permute-start.28) | collective-permute-done | bytes 303136 | tf_op jit(solution)/shard_map/ppermute | solution.py:39
  147.9 2.2 %collective-permute-done.26 = bf16[104,512]{1,0:T(8,128)(2,1)S(1)} collective-permute-done((bf16[104,512]{1,0:T(8,128)(2,1)S(1)}, bf16[104,512]{1,0:T(8,128)(2,1)S(1)}, u32[]{:S(2)}, u32[]{:S(2)}) %collective-permute-start.26) | collective-permute-done | bytes 106528 | tf_op jit(solution)/shard_map/ppermute | solution.py:39
  151.8 2.5 %collective-permute-start.30 = (bf16[296,512]{1,0:T(8,128)(2,1)S(1)}, bf16[296,512]{1,0:T(8,128)(2,1)S(1)}, u32[]{:S(2)}, u32[]{:S(2)}) collective-permute-start(bf16[296,512]{1,0:T(8,128)(2,1)S(1)} %add_convert_fusion.7.s), channel_id=1, source_target_pairs={{0,8},{8,0},{16,24},{24,16},{1,9},{9,1},{17,25},{25,17},{2,10},{10... | collective-permute-start | bytes 909320 | tf_op jit(solution)/shard_map/ppermute | solution.py:39
  154.3 4.1 %collective-permute-done.27 = bf16[104,512]{1,0:T(8,128)(2,1)S(1)} collective-permute-done((bf16[104,512]{1,0:T(8,128)(2,1)S(1)}, bf16[104,512]{1,0:T(8,128)(2,1)S(1)}, u32[]{:S(2)}, u32[]{:S(2)}) %collective-permute-start.27) | collective-permute-done | bytes 106528 | tf_op jit(solution)/shard_map/ppermute | solution.py:39
  158.6 5.3 %collective-permute-done.30.o = bf16[296,512]{1,0:T(8,128)(2,1)S(1)} collective-permute-done((bf16[296,512]{1,0:T(8,128)(2,1)S(1)}, bf16[296,512]{1,0:T(8,128)(2,1)S(1)}, u32[]{:S(2)}, u32[]{:S(2)}) %collective-permute-start.30) | collective-permute-done | bytes 303136 | tf_op jit(solution)/shard_map/ppermute | solution.py:39
  163.8 1.7 %finish_rest.1 = (f32[256,512]{1,0:T(8,128)}, f32[64,2048]{1,0:T(8,128)}, f32[64,512]{1,0:T(8,128)}, f32[1,256]{1,0:T(1,128)}, f32[1,64]{1,0:T(1,128)}, /*index=...) custom-call(s32[2]{0:T(128)S(1)} %pad_add_fusion.ids, bf16[296,512]{1,0:T(8,128)(2,1)S(1)} %add_convert_fusion.7.s, ...), custom_call_target="tpu_custom_call" | custom-call | bytes 1212416 | tf_op jit(solution)/shard_map/finish_rest/pallas_call | solution.py:224
  (111 shorter events, 31.2 us)
Async XLA Ops:
  3.6 10.6 %collective-permute-start = (bf16[208,512]{1,0:T(8,128)(2,1)}, bf16[208,512]{1,0:T(8,128)(2,1)S(1)}, u32[]{:S(2)}, u32[]{:S(2)}) collective-permute-start(bf16[208,512]{1,0:T(8,128)(2,1)} %pack_first.1.refs_0_), channel_id=1, source_target_pairs={{0,2},{1,3},{2,0},{3,1},{4,6},{5,7},{6,4},{7,5},{8,10},{9,11},{10,... | collective-permute-start | bytes 638984 | tf_op jit(solution)/shard_map/ppermute | solution.py:43
  6.6 11.5 %collective-permute-start.1 = (bf16[208,512]{1,0:T(8,128)(2,1)}, bf16[208,512]{1,0:T(8,128)(2,1)S(1)}, u32[]{:S(2)}, u32[]{:S(2)}) collective-permute-start(bf16[208,512]{1,0:T(8,128)(2,1)} %pack_first.1.refs_0_), channel_id=1, source_target_pairs={{0,4},{1,5},{2,6},{3,7},{4,0},{5,1},{6,2},{7,3},{8,12},{9,13},{10,... | collective-permute-start | bytes 638984 | tf_op jit(solution)/shard_map/ppermute | solution.py:43
  8.1 10.0 %collective-permute-start.2 = (bf16[208,512]{1,0:T(8,128)(2,1)}, bf16[208,512]{1,0:T(8,128)(2,1)S(1)}, u32[]{:S(2)}, u32[]{:S(2)}) collective-permute-start(bf16[208,512]{1,0:T(8,128)(2,1)} %pack_first.1.refs_0_), channel_id=1, source_target_pairs={{0,6},{1,7},{2,4},{3,5},{4,2},{5,3},{6,0},{7,1},{8,14},{9,15},{10,... | collective-permute-start | bytes 638984 | tf_op jit(solution)/shard_map/ppermute | solution.py:43
  8.1 10.5 %collective-permute-start.3 = (bf16[208,512]{1,0:T(8,128)(2,1)}, bf16[208,512]{1,0:T(8,128)(2,1)S(1)}, u32[]{:S(2)}, u32[]{:S(2)}) collective-permute-start(bf16[208,512]{1,0:T(8,128)(2,1)} %pack_first.1.refs_0_), channel_id=1, source_target_pairs={{0,1},{1,0},{2,3},{3,2},{4,5},{5,4},{6,7},{7,6},{8,9},{9,8},{10,11... | collective-permute-start | bytes 638984 | tf_op jit(solution)/shard_map/ppermute | solution.py:43
  19.8 20.4 %collective-permute-start.7 = (bf16[576,512]{1,0:T(8,128)(2,1)}, bf16[576,512]{1,0:T(8,128)(2,1)S(1)}, u32[]{:S(2)}, u32[]{:S(2)}) collective-permute-start(bf16[576,512]{1,0:T(8,128)(2,1)} %pack_rest.1.refs_0_), channel_id=1, source_target_pairs={{0,2},{1,3},{2,0},{3,1},{4,6},{5,7},{6,4},{7,5},{8,10},{9,11},{10,... | collective-permute-start | bytes 1769480 | tf_op jit(solution)/shard_map/ppermute | solution.py:43
  20.8 20.0 %collective-permute-start.8 = (bf16[576,512]{1,0:T(8,128)(2,1)}, bf16[576,512]{1,0:T(8,128)(2,1)S(1)}, u32[]{:S(2)}, u32[]{:S(2)}) collective-permute-start(bf16[576,512]{1,0:T(8,128)(2,1)} %pack_rest.1.refs_0_), channel_id=1, source_target_pairs={{0,4},{1,5},{2,6},{3,7},{4,0},{5,1},{6,2},{7,3},{8,12},{9,13},{10,... | collective-permute-start | bytes 1769480 | tf_op jit(solution)/shard_map/ppermute | solution.py:43
  22.5 31.0 %collective-permute-start.9 = (bf16[576,512]{1,0:T(8,128)(2,1)}, bf16[576,512]{1,0:T(8,128)(2,1)S(1)}, u32[]{:S(2)}, u32[]{:S(2)}) collective-permute-start(bf16[576,512]{1,0:T(8,128)(2,1)} %pack_rest.1.refs_0_), channel_id=1, source_target_pairs={{0,1},{1,0},{2,3},{3,2},{4,5},{5,4},{6,7},{7,6},{8,9},{9,8},{10,11... | collective-permute-start | bytes 1769480 | tf_op jit(solution)/shard_map/ppermute | solution.py:43
  40.2 14.8 %collective-permute-start.10 = (bf16[576,512]{1,0:T(8,128)(2,1)S(1)}, bf16[576,512]{1,0:T(8,128)(2,1)S(1)}, u32[]{:S(2)}, u32[]{:S(2)}) collective-permute-start(bf16[576,512]{1,0:T(8,128)(2,1)S(1)} %collective-permute-done.7.refs_1_), channel_id=1, source_target_pairs={{0,1},{1,0},{2,3},{3,2},{4,5},{5,4},{6,7},{7,6},{8,9},{9,8},{10,11... | collective-permute-start | bytes 1769480 | tf_op jit(solution)/shard_map/ppermute | solution.py:43
  40.8 14.3 %collective-permute-start.11 = (bf16[576,512]{1,0:T(8,128)(2,1)S(1)}, bf16[576,512]{1,0:T(8,128)(2,1)S(1)}, u32[]{:S(2)}, u32[]{:S(2)}) collective-permute-start(bf16[576,512]{1,0:T(8,128)(2,1)S(1)} %collective-permute-done.8.refs_2_), channel_id=1, source_target_pairs={{0,1},{1,0},{2,3},{3,2},{4,5},{5,4},{6,7},{7,6},{8,9},{9,8},{10,11... | collective-permute-start | bytes 1769480 | tf_op jit(solution)/shard_map/ppermute | solution.py:43
  40.9 12.1 %collective-permute-start.13 = (bf16[288,512]{1,0:T(8,128)(2,1)S(1)}, bf16[288,512]{1,0:T(8,128)(2,1)S(1)}, u32[]{:S(2)}, u32[]{:S(2)}) collective-permute-start(bf16[288,512]{1,0:T(8,128)(2,1)S(1)} %slice.79), channel_id=1, source_target_pairs={{0,4},{1,5},{2,6},{3,7},{4,0},{5,1},{6,2},{7,3},{8,12},{9,13},{10,... | collective-permute-start | bytes 884744 | tf_op jit(solution)/shard_map/ppermute | solution.py:43
  41.9 11.2 %collective-permute-start.12 = (bf16[288,512]{1,0:T(8,128)(2,1)S(1)}, bf16[288,512]{1,0:T(8,128)(2,1)S(1)}, u32[]{:S(2)}, u32[]{:S(2)}) collective-permute-start(bf16[288,512]{1,0:T(8,128)(2,1)S(1)} %slice.78), channel_id=1, source_target_pairs={{0,2},{1,3},{2,0},{3,1},{4,6},{5,7},{6,4},{7,5},{8,10},{9,11},{10,... | collective-permute-start | bytes 884744 | tf_op jit(solution)/shard_map/ppermute | solution.py:43
  82.4 8.0 %collective-permute-start.16 = (bf16[4,592,512]{2,1,0:T(8,128)(2,1)}, bf16[4,592,512]{2,1,0:T(8,128)(2,1)}, u32[]{:S(2)}, u32[]{:S(2)}) collective-permute-start(bf16[4,592,512]{2,1,0:T(8,128)(2,1)} %get-tuple-element.99), channel_id=1, source_target_pairs={{0,1},{1,0},{2,3},{3,2},{4,5},{5,4},{6,7},{7,6},{8,9},{9,8},{10,11... | collective-permute-start | bytes 7274504 | tf_op jit(solution)/shard_map/ppermute | solution.py:43
  95.3 18.1 %collective-permute-start.18 = (bf16[2,272,512]{2,1,0:T(8,128)(2,1)}, bf16[2,272,512]{2,1,0:T(8,128)(2,1)S(1)}, u32[]{:S(2)}, u32[]{:S(2)}) collective-permute-start(bf16[2,272,512]{2,1,0:T(8,128)(2,1)} %get-tuple-element.136), channel_id=1, source_target_pairs={{0,2},{1,3},{2,0},{3,1},{4,6},{5,7},{6,4},{7,5},{8,10},{9,11},{10,... | collective-permute-start | bytes 1671176 | tf_op jit(solution)/shard_map/ppermute | solution.py:43
  96.3 17.2 %collective-permute-start.17 = (bf16[2,320,512]{2,1,0:T(8,128)(2,1)}, bf16[2,320,512]{2,1,0:T(8,128)(2,1)S(1)}, u32[]{:S(2)}, u32[]{:S(2)}) collective-permute-start(bf16[2,320,512]{2,1,0:T(8,128)(2,1)} %get-tuple-element.137), channel_id=1, source_target_pairs={{0,4},{1,5},{2,6},{3,7},{4,0},{5,1},{6,2},{7,3},{8,12},{9,13},{10,... | collective-permute-start | bytes 1966088 | tf_op jit(solution)/shard_map/ppermute | solution.py:43
  113.8 8.5 %collective-permute-start.20 = (bf16[1,272,512]{2,1,0:T(8,128)(2,1)S(1)}, bf16[1,272,512]{2,1,0:T(8,128)(2,1)}, u32[]{:S(2)}, u32[]{:S(2)}) collective-permute-start(bf16[1,272,512]{2,1,0:T(8,128)(2,1)S(1)} %get-tuple-element.145), channel_id=1, source_target_pairs={{0,4},{1,5},{2,6},{3,7},{4,0},{5,1},{6,2},{7,3},{8,12},{9,13},{10,... | collective-permute-start | bytes 835592 | tf_op jit(solution)/shard_map/ppermute | solution.py:43
  114.7 9.1 %collective-permute-start.19 = (bf16[1,320,512]{2,1,0:T(8,128)(2,1)S(1)}, bf16[1,320,512]{2,1,0:T(8,128)(2,1)S(1)}, u32[]{:S(2)}, u32[]{:S(2)}) collective-permute-start(bf16[1,320,512]{2,1,0:T(8,128)(2,1)S(1)} %get-tuple-element.143), channel_id=1, source_target_pairs={{0,2},{1,3},{2,0},{3,1},{4,6},{5,7},{6,4},{7,5},{8,10},{9,11},{10,... | collective-permute-start | bytes 983048 | tf_op jit(solution)/shard_map/ppermute | solution.py:43
  125.4 7.8 %collective-permute-start.21 = (bf16[296,512]{1,0:T(8,128)(2,1)S(1)}, bf16[296,512]{1,0:T(8,128)(2,1)S(1)}, u32[]{:S(2)}, u32[]{:S(2)}) collective-permute-start(bf16[296,512]{1,0:T(8,128)(2,1)S(1)} %fusion.4), channel_id=1, source_target_pairs={{0,8},{8,0},{16,24},{24,16},{1,9},{9,1},{17,25},{25,17},{2,10},{10... | collective-permute-start | bytes 909320 | tf_op jit(solution)/shard_map/ppermute | solution.py:39
  127.9 15.3 %collective-permute-start.23 = (bf16[208,512]{1,0:T(8,128)(2,1)}, bf16[208,512]{1,0:T(8,128)(2,1)S(1)}, u32[]{:S(2)}, u32[]{:S(2)}) collective-permute-start(bf16[208,512]{1,0:T(8,128)(2,1)} %get-tuple-element.139), channel_id=1, source_target_pairs={{0,6},{1,7},{2,4},{3,5},{4,2},{5,3},{6,0},{7,1},{8,14},{9,15},{10,... | collective-permute-start | bytes 638984 | tf_op jit(solution)/shard_map/ppermute | solution.py:43
  129.9 13.3 %collective-permute-start.24 = (bf16[208,512]{1,0:T(8,128)(2,1)S(1)}, bf16[208,512]{1,0:T(8,128)(2,1)S(1)}, u32[]{:S(2)}, u32[]{:S(2)}) collective-permute-start(bf16[208,512]{1,0:T(8,128)(2,1)S(1)} %get-tuple-element.140), channel_id=1, source_target_pairs={{0,4},{1,5},{2,6},{3,7},{4,0},{5,1},{6,2},{7,3},{8,12},{9,13},{10,... | collective-permute-start | bytes 638984 | tf_op jit(solution)/shard_map/ppermute | solution.py:43
  130.5 12.7 %collective-permute-start.25 = (bf16[208,512]{1,0:T(8,128)(2,1)S(1)}, bf16[208,512]{1,0:T(8,128)(2,1)S(1)}, u32[]{:S(2)}, u32[]{:S(2)}) collective-permute-start(bf16[208,512]{1,0:T(8,128)(2,1)S(1)} %get-tuple-element.141), channel_id=1, source_target_pairs={{0,2},{1,3},{2,0},{3,1},{4,6},{5,7},{6,4},{7,5},{8,10},{9,11},{10,... | collective-permute-start | bytes 638984 | tf_op jit(solution)/shard_map/ppermute | solution.py:43
  133.6 14.3 %collective-permute-start.28 = (bf16[296,512]{1,0:T(8,128)(2,1)S(1)}, bf16[296,512]{1,0:T(8,128)(2,1)S(1)}, u32[]{:S(2)}, u32[]{:S(2)}) collective-permute-start(bf16[296,512]{1,0:T(8,128)(2,1)S(1)} %add_convert_fusion.8), channel_id=1, source_target_pairs={{0,16},{8,24},{16,0},{24,8},{1,17},{9,25},{17,1},{25,9},{2,18},{10... | collective-permute-start | bytes 909320 | tf_op jit(solution)/shard_map/ppermute | solution.py:39
  150.1 8.2 %collective-permute-start.27 = (bf16[104,512]{1,0:T(8,128)(2,1)S(1)}, bf16[104,512]{1,0:T(8,128)(2,1)S(1)}, u32[]{:S(2)}, u32[]{:S(2)}) collective-permute-start(bf16[104,512]{1,0:T(8,128)(2,1)S(1)} %add_convert_fusion.17), channel_id=1, source_target_pairs={{0,16},{8,24},{16,0},{24,8},{1,17},{9,25},{17,1},{25,9},{2,18},{10... | collective-permute-start | bytes 319496 | tf_op jit(solution)/shard_map/ppermute | solution.py:39
  151.8 12.1 %collective-permute-start.30 = (bf16[296,512]{1,0:T(8,128)(2,1)S(1)}, bf16[296,512]{1,0:T(8,128)(2,1)S(1)}, u32[]{:S(2)}, u32[]{:S(2)}) collective-permute-start(bf16[296,512]{1,0:T(8,128)(2,1)S(1)} %add_convert_fusion.7.s), channel_id=1, source_target_pairs={{0,8},{8,0},{16,24},{24,16},{1,9},{9,1},{17,25},{25,17},{2,10},{10... | collective-permute-start | bytes 909320 | tf_op jit(solution)/shard_map/ppermute | solution.py:39
  158.4 7.1 %collective-permute-start.29 = (bf16[104,512]{1,0:T(8,128)(2,1)S(1)}, bf16[104,512]{1,0:T(8,128)(2,1)S(1)}, u32[]{:S(2)}, u32[]{:S(2)}) collective-permute-start(bf16[104,512]{1,0:T(8,128)(2,1)S(1)} %add_convert_fusion.16.s), channel_id=1, source_target_pairs={{0,8},{8,0},{16,24},{24,16},{1,9},{9,1},{17,25},{25,17},{2,10},{10... | collective-permute-start | bytes 319496 | tf_op jit(solution)/shard_map/ppermute | solution.py:39
  (28 other events, 168.9 us)

commit v7 on v6

--- a/solution.py
+++ b/solution.py
@@ -79,7 +79,7 @@
 
 
 def add16(a, b):
-    return (a.astype(f32) + b.astype(f32)).astype(bf16)
+    return a + b
 
 
 def spread(parts):
@@ -290,23 +290,6 @@
     return pl.multiple_of(x, m)
 
 
-def project(v, h, w, kv, qkvt, grp, scale):
-    gw = w.shape[1] // 3
-    bias = lambda i: v[i : i + 1, grp * gw : (grp + 1) * gw]
-    for j in range(3):
-        y = dot(h, w[:, j * gw : (j + 1) * gw])
-        if j == 0:
-            y = y + bias(2)
-        if j == 2:
-            y = y + bias(3)
-        y = y.astype(bf16)
-        if j == 0:
-            y = y * bf16(scale)
-        else:
-            kv[j - 1] = y
-        qkvt[j] = y.T
-
-
 def weight_segs(w, r):
     gw = w.shape[1] // 3
     seg = lambda j: (j * r, r, lambda s, o, c: w.at[pl.ds(mult(s * r + o, 16), c), pl.ds(j * gw, gw)], gw)
@@ -332,19 +315,26 @@
 def front_body(scale, n, meta, me, nx, *refs):
     np_ = len(meta)
     pieces = refs[:np_]
-    kv, qkvt, w, vec, upb, vbuf, sems = refs[np_:]
-    D = nx.shape[-1]
+    kv, qkvt, wout, vec, upb, nv, h, w, vbuf, sems, own = refs[np_:]
+    T, D = nv.shape
     r = D // n
     FF = upb.shape[1]
+    i = pl.program_id(0)
+    cw = kv.shape[2]
+    per_j = D // cw
     segs = [(3 * r, VROWS, lambda s, o, c: vbuf.at[s, pl.ds(o, c)], LANES)] + weight_segs(w, r)
-
-    @pl.when(pl.program_id(0) == 0)
+    load = pltpu.make_async_copy(nx, nv, own.at[0])
+    save = pltpu.make_async_copy(w, wout, own.at[1])
+
+    @pl.when(i == 0)
     def _():
         cs = pull(me[0], pieces, meta, segs, sems)
         for c in cs:
             c.start()
+        load.start()
         for c in cs:
             c.wait()
+        save.start()
         per = LANES // r
         tiles = [sum(vbuf[s, 0:8, :].astype(f32) for s in range(t * per, (t + 1) * per)) for t in range(D // LANES)]
         vec[...] = jnp.concatenate(tiles, axis=1)
@@ -355,10 +345,21 @@
             per = LANES // wu
             rows = [sum(vbuf[s, 8:9, :].astype(f32) for s in range(t * per, (t + 1) * per)) for t in range(FF // LANES)]
         upb[...] = jnp.concatenate(rows, axis=1)
-
-    v = vec[...]
-    h = (nx[...] * row(v, 0) + row(v, 1)).astype(bf16)
-    project(v, h, w, kv, qkvt, 0, scale)
+        load.wait()
+        v = vec[...]
+        h[...] = (nv[...] * row(v, 0) + row(v, 1)).astype(bf16)
+
+    cols = pl.ds(mult(i * cw, 128), cw)
+    y = dot(h[...], w[:, cols])
+    here = pl.ds(mult((i % per_j) * cw, 128), cw)
+    kind = i // per_j
+    y = (y + jnp.where(kind == 0, vec[2:3, here], jnp.where(kind == 2, vec[3:4, here], 0.0))).astype(bf16)
+    kv[0] = y
+    qkvt[0] = jnp.where(kind == 0, y * bf16(scale), y).T
+
+    @pl.when(i == pl.num_programs(0) - 1)
+    def _():
+        save.wait()
 
 
 S = jax.ShapeDtypeStruct
@@ -369,18 +370,21 @@
     return pl.CostEstimate(flops=int(flops), bytes_accessed=int(nbytes), transcendentals=int(tr))
 
 
-def front(me, nx, pieces, n, FF, bm=512):
+def front(me, nx, pieces, n, FF, cw=256):
     T, D = nx.shape
     scale = 1.0 / math.sqrt(D // HEADS)
     meta = tuple((k, r0) for k, r0, _ in pieces)
+    q = D // cw
     keep = lambda *sh: pl.BlockSpec(sh, lambda i, m: (0,) * len(sh))
+    rest = lambda i: jnp.maximum(i - q, 0)
+    V = pltpu.VMEM
     return pl.pallas_call(
         functools.partial(front_body, scale, n, meta),
         grid_spec=pltpu.PrefetchScalarGridSpec(
-            num_scalar_prefetch=1, grid=(T // bm,),
-            in_specs=[pl.BlockSpec((bm, D), lambda i, m: (i, 0))] + [ANY] * len(pieces),
-            out_specs=[pl.BlockSpec((2, bm, D), lambda i, m: (0, i, 0)), pl.BlockSpec((3, D, bm), lambda i, m: (0, 0, i)), keep(D, 3 * D), keep(8, D), keep(1, FF)],
-            scratch_shapes=[pltpu.VMEM((n, VROWS, LANES), bf16), pltpu.SemaphoreType.DMA((8 * len(pieces),))]),
+            num_scalar_prefetch=1, grid=(3 * q,),
+            in_specs=[ANY] * (1 + len(pieces)),
+            out_specs=[pl.BlockSpec((1, T, cw), lambda i, m: (rest(i) // q, 0, rest(i) % q)), pl.BlockSpec((1, cw, T), lambda i, m: (i // q, i % q, 0)), ANY, keep(8, D), keep(1, FF)],
+            scratch_shapes=[V((T, D), f32), V((T, D), bf16), V((D, 3 * D), bf16), V((n, VROWS, LANES), bf16), pltpu.SemaphoreType.DMA((8 * len(pieces),)), pltpu.SemaphoreType.DMA((2,))]),
         out_shape=[S((2, T, D), bf16), S((3, D, T), bf16), S((D, 3 * D), bf16), S((8, D), f32), S((1, FF), f32)],
         compiler_params=cp(), name="front", cost_estimate=cost(6 * T * D * D, 12 * T * D),
     )(me, nx, *[a for _, _, a in pieces])
@@ -489,7 +493,7 @@
 def ffn_body(n, meta, ch, ln, me, tok, step, vec, upb, cot, mixed, mixedt, *refs):
     np_ = len(meta)
     pieces = refs[:np_]
-    out, gx1, gmt, keep, send, wo, wu, wd, act, gup, h2t, gdt, gattn, sums, upsum, dn, up, gwo, vr, sems, psems = refs[np_:]
+    out, gx1, gmt, keep, send, wo, wu, wd, act, gup, h2t, gdt, gattn, sums, upsum, dn, up, gwo, vr, mtv, sems, psems = refs[np_:]
     i = pl.program_id(0)
     bm, D = tok.shape
     FF = wu.shape[1]
@@ -500,16 +504,22 @@
     ro = pl.ds(mult(i * bm, 128), bm)
     first = i == 0
     seg = lambda j: (r + j * r, r, lambda s, o, c: wu.at[pl.ds(mult(s * r + o, 16), c), pl.ds(j * D, D)], D)
-    segs = [(0, r, lambda s, o, c: wo.at[pl.ds(mult(s * r + o, 16), c)], D)] + [seg(j) for j in range(nf)]
-    segs += [(r + r * nf, rf, lambda s, o, c: wd.at[pl.ds(mult(s * rf + o, 16), c)], D)]
+    seg_o = [(0, r, lambda s, o, c: wo.at[pl.ds(mult(s * r + o, 16), c)], D)]
+    seg_u = [seg(j) for j in range(nf)]
+    seg_d = [(r + r * nf, rf, lambda s, o, c: wd.at[pl.ds(mult(s * rf + o, 16), c)], D)]
+    q = sems.shape[0] // 4
+    parts = [(seg_o, sems.at[pl.ds(0, q)]), (seg_d, sems.at[pl.ds(q, q)]), (seg_u, sems.at[pl.ds(2 * q, 2 * q)])]
+    load = pltpu.make_async_copy(mixedt, mtv, psems.at[psems.shape[0] - 1])
 
     @pl.when(first)
     def _():
-        for c in pull(i0, pieces, meta, segs, sems):
-            c.start()
+        for sg, sm in parts:
+            for c in pull(i0, pieces, meta, sg, sm):
+                c.start()
+        load.start()
         sums[...] = jnp.zeros_like(sums)
         upsum[...] = jnp.zeros_like(upsum)
-        for c in pull(i0, pieces, meta, segs, sems):
+        for c in pull(i0, pieces, meta, *parts[0]):
             c.wait()
 
     v = vec[...]
@@ -523,9 +533,16 @@
     nc = FF // ch
     sl = [slice(c * ch, (c + 1) * ch) for c in range(nc)]
     lead = lambda c: (dot(h2, wu[:, sl[c]]), dot_t(gd, wd[sl[c], :]))
-    nxt = lead(0)
     h2t[:, ro] = h2.T
     gdt[:, ro] = gd.T
+
+    @pl.when(first)
+    def _():
+        for sg, sm in parts[1:]:
+            for c in pull(i0, pieces, meta, sg, sm):
+                c.wait()
+
+    nxt = lead(0)
     for c in range(nc):
         u, ga = nxt
         nxt = lead(c + 1) if c + 1 < nc else None
@@ -563,7 +580,8 @@
             up[j] = dot(h2t[...], gup[:, j * D : (j + 1) * D]).astype(bf16)
             for s in range(n):
                 push(i0, n, s, up.at[j, pl.ds(s * r, r)], keep, send, o_up + j * r, psems.at[n * (1 + j) + s], True)
-        gwo[...] = dot(mixedt[...], gattn[...]).astype(bf16)
+        load.wait()
+        gwo[...] = dot(mtv[...], gattn[...]).astype(bf16)
         vr[...] = jnp.concatenate([sums[0:4, :]] + [upsum[:, c * D : (c + 1) * D] for c in range(nf)] + [jnp.zeros((VROWS - 4 - nf, D), f32)], axis=0).astype(bf16)
         b = n * (1 + nf)
         for s in range(n):
@@ -593,9 +611,9 @@
         functools.partial(ffn_body, n, meta, min(1024, FF)),
         grid_spec=pltpu.PrefetchScalarGridSpec(
             num_scalar_prefetch=2, grid=(T // bm,),
-            in_specs=[rows, full(step), full(vec), full(upb), rows, rows, full(mixedt)] + [ANY] * len(pieces),
+            in_specs=[rows, full(step), full(vec), full(upb), rows, rows, ANY] + [ANY] * len(pieces),
             out_specs=[rows, rows, pl.BlockSpec((D, bm), lambda i, l, m: (0, i)), ANY, ANY],
-            scratch_shapes=[V((D, D), bf16), V((D, FF), bf16), V((FF, D), bf16), V((T, FF), bf16), V((T, FF), bf16), V((D, T), bf16), V((D, T), bf16), V((T, D), bf16), V((8, D), f32), V((1, FF), f32), V((nf, D, D), bf16), V((nf, D, D), bf16), V((D, D), bf16), V((VROWS, D), bf16), pltpu.SemaphoreType.DMA((8 * len(pieces),)), pltpu.SemaphoreType.DMA((n * (nf + 3),))]),
+            scratch_shapes=[V((D, D), bf16), V((D, FF), bf16), V((FF, D), bf16), V((T, FF), bf16), V((T, FF), bf16), V((D, T), bf16), V((D, T), bf16), V((T, D), bf16), V((8, D), f32), V((1, FF), f32), V((nf, D, D), bf16), V((nf, D, D), bf16), V((D, D), bf16), V((VROWS, D), bf16), V((D, T), bf16), pltpu.SemaphoreType.DMA((16 * len(pieces),)), pltpu.SemaphoreType.DMA((n * (nf + 3) + 1,))]),
         out_shape=[S((T, D), bf16), S((T, D), f32), S((D, T), bf16), B, B],
         compiler_params=cp(), name="ffn", cost_estimate=cost(2 * T * D * (6 * FF + 3 * D), 16 * T * D, T * FF),
     )(ln, me, tok, step, vec, upb, cot, mixed, mixedt, *[a for _, _, a in pieces])
@@ -761,10 +779,13 @@
     tg = back(tok, after(step, z1, *p2[1:]), vec, [w], g, gx1)
     own2 = total(p2[0], [after(a, tg) for a in far2])
     m2, o2, x2 = rep_half(own2)
-    z2 = add16(m2, o2)
-    for b in rep_steps():
-        pa, pz = rep_perm(z1, b), rep_perm(z2, b)
-        z1 = add16(z1, after(pa, x2))
+    steps = rep_steps()
+    z2 = None if steps else add16(m2, o2)
+    for b in steps:
+        z1 = add16(z1, after(rep_perm(z1, b), x2))
+        if z2 is None:
+            z2 = add16(m2, after(o2, z1))
+        pz = rep_perm(z2, b)
         z2 = add16(z2, after(pz, z1))
     o1, o2 = rep_perm(z1, 1), rep_perm(z2, 1)
     ids = jnp.stack([me, (lax.axis_index("rep") % 2).astype(jnp.int32)])

time: 168 us -> 167 us (level)
  waiting for transfers between devices: 24.1 us -> 20.5 us
  starting transfers between devices: 29.2 us -> 31.9 us
    convert_element_type x9 -> x0, other arithmetic: 6.6 us -> none  [add16(): return (a.astype(f32) + b.astype(f32)).astype(bf16)]
    add x0 -> x9, other arithmetic: none -> 5.89 us  [add16(): return a + b]
    ppermute x6, waiting for transfers between devices: 16.1 us -> 12.5 us  [rep_perm(): return lax.ppermute(x, 'rep', xor_perm(lax.axis_size('rep'), b))]
    ppermute x6, starting transfers between devices: 10.1 us -> 12.8 us  [rep_perm(): return lax.ppermute(x, 'rep', xor_perm(lax.axis_size('rep'), b))]
  transfers between devices with their start and end apart: 31 -> 31, of which waited for: 12 -> 12; matrix products, arithmetic and copies ran while one was open for 2% -> 2% of each run, Pallas kernels for 43% -> 44%
where the time goes in v7:
time: 167 us; the launch traced here: 166 us
  Pallas kernels  102 us (61%)
  starting transfers between devices  31.9 us (19%)
  waiting for transfers between devices  20.5 us (12%)
  other arithmetic  7.54 us (5%)
  local copies, waits for them, and re-layouts  2.39 us (1%)
  between operations  1.7 us (1%)
    pallas_call x1, Pallas kernels, ffn(): pl.pallas_call(functools.partial(ffn_body, n, meta, min(1024, FF)), grid_...  26.5 us
    pallas_call x2, Pallas kernels, attn_bwd(): pl.pallas_call(functools.partial(attn_bwd_body, HD, 1.0 / math.sqrt(HD),...  23.9 us
    pallas_call x2, Pallas kernels, attn_fwd(): pl.pallas_call(functools.partial(attn_fwd_body, HD, bi, min(256, T)), gri...  20 us
    ppermute x25, starting transfers between devices, swap(): return lax.ppermute(x, 'shard', xor_perm(lax.axis_size('shard'), k))  19.1 us
    ppermute x6, starting transfers between devices, rep_perm(): return lax.ppermute(x, 'rep', xor_perm(lax.axis_size('rep'), b))  12.8 us
    ppermute x6, waiting for transfers between devices, rep_perm(): return lax.ppermute(x, 'rep', xor_perm(lax.axis_size('rep'), b))  12.5 us
    pallas_call x1, Pallas kernels, front(): pl.pallas_call(functools.partial(front_body, scale, n, meta), grid_spec=p...  8.06 us
    ppermute x25, waiting for transfers between devices, swap(): return lax.ppermute(x, 'shard', xor_perm(lax.axis_size('shard'), k))  7.97 us
  transfers between devices with their start and end apart: 31, of which 12 were waited for; matrix products, arithmetic and copies ran while one was open for 2% of the time, Pallas kernels for 44%

profile of v7, /device:TPU:0, one launch (start us, length us, event | category | flops | bytes accessed | tf_op | source)
XLA Modules:
  0.0 166.2 jit_solution(16338472382364224443)
XLA Ops:
  1.9 1.8 %pack_first.1.refs_0_ = bf16[208,512]{1,0:T(8,128)(2,1)} custom-call(s32[1]{0:T(128)} %bitcast.me, bf16[64,1536]{1,0:T(8,128)(2,1)} %w.3, bf16[1,256]{1,0:T(2,128)(2,1)} %broadcast_in_dim.39.upb, bf16[1,64]{1,0:T(2,128)(2,1)} %bitcast.38, bf16[1,64]{1,0:T(2,128)(2,1)} %bitcast.40, bf16[1,64]{1,0:T(2,128)(2,1)} %bitcast.46, bf16[1,64]{1,0:T(2,128)(2,1)} %bitcast.47, ...), custom_call_target="tpu_custom_call" | custom-call | bytes 393216 | tf_op jit(solution)/shard_map/pack_first/pallas_call | solution.py:148
  3.6 2.9 %collective-permute-start = (bf16[208,512]{1,0:T(8,128)(2,1)}, bf16[208,512]{1,0:T(8,128)(2,1)S(1)}, u32[]{:S(2)}, u32[]{:S(2)}) collective-permute-start(bf16[208,512]{1,0:T(8,128)(2,1)} %pack_first.1.refs_0_), channel_id=1, source_target_pairs={{0,2},{1,3},{2,0},{3,1},{4,6},{5,7},{6,4},{7,5},{8,10},{9,11},{10,... | collective-permute-start | bytes 638984 | tf_op jit(solution)/shard_map/ppermute | solution.py:43
  8.1 1.9 %pack_rest.1.refs_0_ = bf16[576,512]{1,0:T(8,128)(2,1)} custom-call(bf16[64,512]{1,0:T(8,128)(2,1)} %wo.1, bf16[64,2048]{1,0:T(8,128)(2,1)} %wu.1, bf16[256,512]{1,0:T(8,128)(2,1)} %wd.1), custom_call_target="tpu_custom_call" | custom-call | bytes 524288 | tf_op jit(solution)/shard_map/pack_rest/pallas_call | solution.py:166
  10.0 4.2 %start.1 = (f32[1024,512]{1,0:T(8,128)}, bf16[512,1024]{1,0:T(8,128)(2,1)}) custom-call(bf16[1024,512]{1,0:T(8,128)(2,1)} %bitcast.42, bf16[1,512]{1,0:T(2,128)(2,1)} %step.4), custom_call_target="tpu_custom_call" | custom-call | flops 10485760 | bytes 4194304 | tf_op jit(solution)/shard_map/start/pallas_call | solution.py:308
  14.8 3.2 %collective-permute-done.1.refs_2_ = bf16[208,512]{1,0:T(8,128)(2,1)S(1)} collective-permute-done((bf16[208,512]{1,0:T(8,128)(2,1)}, bf16[208,512]{1,0:T(8,128)(2,1)S(1)}, u32[]{:S(2)}, u32[]{:S(2)}) %collective-permute-start.1) | collective-permute-done | bytes 213024 | tf_op jit(solution)/shard_map/ppermute | solution.py:43
  22.7 8.1 %front.1 = (bf16[2,1024,512]{2,1,0:T(8,128)(2,1)}, bf16[3,512,1024]{2,1,0:T(8,128)(2,1)}, bf16[512,1536]{1,0:T(8,128)(2,1)}, f32[8,512]{1,0:T(8,128)}, f32[1,2048]{1,0:T(1,128)}) custom-call(s32[1]{0:T(128)} %bitcast.me, f32[1024,512]{1,0:T(8,128)} %get-tuple-element.76.nx, bf16[208,512]{1,0:T(8,128)(2,1)} %pack_first.1.refs_0_, ...), custom_call_target="tpu_custom_call" | custom-call | flops 1610612736 | bytes 6291456 | tf_op jit(solution)/shard_map/front/pallas_call | solution.py:381
  30.8 10.0 %attn_fwd.2 = (bf16[8,1024,1024]{2,1,0:T(8,128)(2,1)}, bf16[1024,512]{1,0:T(8,128)(2,1)}, bf16[512,1024]{1,0:T(8,128)(2,1)}, f32[512,1024]{1,0:T(8,128)}, f32[4,8,1024]{2,1,0:T(8,128)}) custom-call(s32[1]{0:T(128)S(6)} %copy.44.ln, bf16[2,1024,512]{2,1,0:T(8,128)(2,1)} %get-tuple-element.83.k.v, bf16[3,512,1024]{2,1,0:T(8,128)(2,1)} %get-tuple-element.84.qt.vt.kt, ...), custom_call_target="tpu_custom_call" | custom-call | flops 4294967296 | bytes 8388608 | tf_op jit(solution)/shard_map/attn_fwd/pallas_call | solution.py:454
  43.5 10.0 %attn_fwd.3 = (bf16[8,1024,1024]{2,1,0:T(8,128)(2,1)}, bf16[1024,512]{1,0:T(8,128)(2,1)}, bf16[512,1024]{1,0:T(8,128)(2,1)}, f32[512,1024]{1,0:T(8,128)}, f32[4,8,1024]{2,1,0:T(8,128)}) custom-call(s32[1]{0:T(128)S(6)} %copy.44.ln, ...), custom_call_target="tpu_custom_call", output_to_operand_aliasing={{0}: (4, {}), {1}: (5, {}), {2}: (6, {}), {3}: (7, {}), {4}... | custom-call | flops 4294967296 | bytes 8388608 | tf_op jit(solution)/shard_map/attn_fwd/pallas_call | solution.py:454
  56.7 26.5 %ffn.1 = (bf16[1024,512]{1,0:T(8,128)(2,1)}, f32[1024,512]{1,0:T(8,128)}, bf16[512,1024]{1,0:T(8,128)(2,1)}, bf16[4,592,512]{2,1,0:T(8,128)(2,1)}, bf16[4,592,512]{2,1,0:T(8,128)(2,1)}) custom-call(s32[1]{0:T(128)S(6)} %copy.44.ln, s32[1]{0:T(128)} %bitcast.me, bf16[1024,512]{1,0:T(8,128)(2,1)} %bitcast.43, bf16[1,512]{1,0:T(2,128)(2,1)} %step.4, ...), custom_call_target="tpu_custom_call" | custom-call | flops 14495514624 | bytes 8388608 | tf_op jit(solution)/shard_map/ffn/pallas_call | solution.py:610
  83.4 7.8 %attn_bwd.2.refs_0_ = bf16[3,512,1024]{2,1,0:T(8,128)(2,1)} custom-call(bf16[2,1024,512]{2,1,0:T(8,128)(2,1)} %get-tuple-element.83.k.v, bf16[3,512,1024]{2,1,0:T(8,128)(2,1)} %get-tuple-element.84.qt.vt.kt, bf16[3,512,1024]{2,1,0:T(8,128)(2,1)} %get-tuple-element.84.qt.vt.kt, bf16[512,1024]{1,0:T(8,128)(2,1)} %get-tuple-element.105.gt, ...), custom_call_target="tpu_custom_call" | custom-call | flops 4294967296 | bytes 4194304 | tf_op jit(solution)/shard_map/attn_bwd/pallas_call | solution.py:654
  91.3 2.2 %slice_add_fusion.2 = (bf16[2,272,512]{2,1,0:T(8,128)(2,1)S(1)}, bf16[2,272,512]{2,1,0:T(8,128)(2,1)}) fusion(bf16[4,592,512]{2,1,0:T(8,128)(2,1)} %collective-permute-done.16, bf16[4,592,512]{2,1,0:T(8,128)(2,1)S(1)} %copy-done.3), kind=kLoop, calls=%fused_computation.6 | loop fusion | flops 557056 | bytes 3342336 | tf_op jit(solution)/shard_map/add | solution.py:82
  93.5 2.2 %slice_add_fusion = (bf16[2,320,512]{2,1,0:T(8,128)(2,1)}, bf16[2,320,512]{2,1,0:T(8,128)(2,1)S(1)}) fusion(bf16[4,592,512]{2,1,0:T(8,128)(2,1)} %collective-permute-done.16, bf16[4,592,512]{2,1,0:T(8,128)(2,1)S(1)} %copy-done.3), kind=kLoop, calls=%fused_computation.4 | loop fusion | flops 655360 | bytes 3932160 | tf_op jit(solution)/shard_map/add | solution.py:82
  97.8 16.0 %attn_bwd.3.g = bf16[3,512,1024]{2,1,0:T(8,128)(2,1)} custom-call(bf16[2,1024,512]{2,1,0:T(8,128)(2,1)} %get-tuple-element.83.k.v, bf16[3,512,1024]{2,1,0:T(8,128)(2,1)} %get-tuple-element.84.qt.vt.kt, bf16[3,512,1024]{2,1,0:T(8,128)(2,1)} %get-tuple-element.84.qt.vt.kt, bf16[512,1024]{1,0:T(8,128)(2,1)} %get-tuple-element.105.gt, ...), custom_call_target="tpu_custom_call", output_to_operand_aliasing={{}: (7, {})} | custom-call | flops 12884901888 | bytes 12582912 | tf_op jit(solution)/shard_map/attn_bwd/pallas_call | solution.py:654
  116.4 5.6 %wqkv.1 = (bf16[4,208,512]{2,1,0:T(8,128)(2,1)}, bf16[4,208,512]{2,1,0:T(8,128)(2,1)}) custom-call(s32[1]{0:T(128)} %bitcast.me, bf16[512,1024]{1,0:T(8,128)(2,1)} %get-tuple-element.108.xht, bf16[3,512,1024]{2,1,0:T(8,128)(2,1)} %attn_bwd.3.g), custom_call_target="tpu_custom_call" | custom-call | flops 1610612736 | bytes 5242880 | tf_op jit(solution)/shard_map/wqkv/pallas_call | solution.py:691
  127.9 2.0 %collective-permute-start.23 = (bf16[208,512]{1,0:T(8,128)(2,1)}, bf16[208,512]{1,0:T(8,128)(2,1)S(1)}, u32[]{:S(2)}, u32[]{:S(2)}) collective-permute-start(bf16[208,512]{1,0:T(8,128)(2,1)} %get-tuple-element.141), channel_id=1, source_target_pairs={{0,6},{1,7},{2,4},{3,5},{4,2},{5,3},{6,0},{7,1},{8,14},{9,15},{10,... | collective-permute-start | bytes 638984 | tf_op jit(solution)/shard_map/ppermute | solution.py:43
  131.4 1.9 %collective-permute-done.21 = bf16[296,512]{1,0:T(8,128)(2,1)S(1)} collective-permute-done((bf16[296,512]{1,0:T(8,128)(2,1)S(1)}, bf16[296,512]{1,0:T(8,128)(2,1)S(1)}, u32[]{:S(2)}, u32[]{:S(2)}) %collective-permute-start.21) | collective-permute-done | bytes 303136 | tf_op jit(solution)/shard_map/ppermute | solution.py:39
  133.7 2.6 %collective-permute-start.27 = (bf16[296,512]{1,0:T(8,128)(2,1)S(1)}, bf16[296,512]{1,0:T(8,128)(2,1)S(1)}, u32[]{:S(2)}, u32[]{:S(2)}) collective-permute-start(bf16[296,512]{1,0:T(8,128)(2,1)S(1)} %fusion.5), channel_id=1, source_target_pairs={{0,16},{8,24},{16,0},{24,8},{1,17},{9,25},{17,1},{25,9},{2,18},{10... | collective-permute-start | bytes 909320 | tf_op jit(solution)/shard_map/ppermute | solution.py:39
  136.4 7.0 %back.1 = f32[1024,512]{1,0:T(8,128)} custom-call(bf16[1024,512]{1,0:T(8,128)(2,1)} %bitcast.44, bf16[1,512]{1,0:T(2,128)(2,1)} %step.4, f32[8,512]{1,0:T(8,128)} %get-tuple-element.81.vec, bf16[3,512,1024]{2,1,0:T(8,128)(2,1)} %attn_bwd.3.g, f32[1024,512]{1,0:T(8,128)} %get-tuple-element.115.gx1, bf16[512,1536]{1,0:T(8,128)(2,1)} %get-tuple-element.116.refs_0_), custom_call_target="tpu_custom_call" | custom-call | flops 1610612736 | bytes 7340032 | tf_op jit(solution)/shard_map/back/pallas_call | solution.py:718
  143.5 1.6 collective-permute-start.26
  145.2 2.9 %collective-permute-done.27 = bf16[296,512]{1,0:T(8,128)(2,1)S(1)} collective-permute-done((bf16[296,512]{1,0:T(8,128)(2,1)S(1)}, bf16[296,512]{1,0:T(8,128)(2,1)S(1)}, u32[]{:S(2)}, u32[]{:S(2)}) %collective-permute-start.27) | collective-permute-done | bytes 303136 | tf_op jit(solution)/shard_map/ppermute | solution.py:39
  150.3 2.0 %collective-permute-start.28 = (bf16[104,512]{1,0:T(8,128)(2,1)S(1)}, bf16[104,512]{1,0:T(8,128)(2,1)S(1)}, u32[]{:S(2)}, u32[]{:S(2)}) collective-permute-start(bf16[104,512]{1,0:T(8,128)(2,1)S(1)} %dynamic-slice_add_fusion), channel_id=1, source_target_pairs={{0,16},{8,24},{16,0},{24,8},{1,17},{9,25},{17,1},{25,9},{2,18},{10... | collective-permute-start | bytes 319496 | tf_op jit(solution)/shard_map/ppermute | solution.py:39
  152.3 5.4 %collective-permute-done.28 = bf16[104,512]{1,0:T(8,128)(2,1)S(1)} collective-permute-done((bf16[104,512]{1,0:T(8,128)(2,1)S(1)}, bf16[104,512]{1,0:T(8,128)(2,1)S(1)}, u32[]{:S(2)}, u32[]{:S(2)}) %collective-permute-start.28) | collective-permute-done | bytes 106528 | tf_op jit(solution)/shard_map/ppermute | solution.py:39
  157.7 4.2 %collective-permute-start.29 = (bf16[104,512]{1,0:T(8,128)(2,1)S(1)}, bf16[104,512]{1,0:T(8,128)(2,1)S(1)}, u32[]{:S(2)}, u32[]{:S(2)}) collective-permute-start(bf16[104,512]{1,0:T(8,128)(2,1)S(1)} %add.119.s), channel_id=1, source_target_pairs={{0,8},{8,0},{16,24},{24,16},{1,9},{9,1},{17,25},{25,17},{2,10},{10... | collective-permute-start | bytes 319496 | tf_op jit(solution)/shard_map/ppermute | solution.py:39
  162.0 1.7 %finish_rest.1 = (f32[256,512]{1,0:T(8,128)}, f32[64,2048]{1,0:T(8,128)}, f32[64,512]{1,0:T(8,128)}, f32[1,256]{1,0:T(1,128)}, f32[1,64]{1,0:T(1,128)}, /*index=...) custom-call(s32[2]{0:T(128)S(1)} %pad_add_fusion.ids, bf16[296,512]{1,0:T(8,128)(2,1)S(1)} %add.117.s, ...), custom_call_target="tpu_custom_call" | custom-call | bytes 1212416 | tf_op jit(solution)/shard_map/finish_rest/pallas_call | solution.py:224
  (111 shorter events, 30.7 us)
Async XLA Ops:
  3.6 10.6 %collective-permute-start = (bf16[208,512]{1,0:T(8,128)(2,1)}, bf16[208,512]{1,0:T(8,128)(2,1)S(1)}, u32[]{:S(2)}, u32[]{:S(2)}) collective-permute-start(bf16[208,512]{1,0:T(8,128)(2,1)} %pack_first.1.refs_0_), channel_id=1, source_target_pairs={{0,2},{1,3},{2,0},{3,1},{4,6},{5,7},{6,4},{7,5},{8,10},{9,11},{10,... | collective-permute-start | bytes 638984 | tf_op jit(solution)/shard_map/ppermute | solution.py:43
  6.6 11.5 %collective-permute-start.1 = (bf16[208,512]{1,0:T(8,128)(2,1)}, bf16[208,512]{1,0:T(8,128)(2,1)S(1)}, u32[]{:S(2)}, u32[]{:S(2)}) collective-permute-start(bf16[208,512]{1,0:T(8,128)(2,1)} %pack_first.1.refs_0_), channel_id=1, source_target_pairs={{0,4},{1,5},{2,6},{3,7},{4,0},{5,1},{6,2},{7,3},{8,12},{9,13},{10,... | collective-permute-start | bytes 638984 | tf_op jit(solution)/shard_map/ppermute | solution.py:43
  8.1 10.0 %collective-permute-start.2 = (bf16[208,512]{1,0:T(8,128)(2,1)}, bf16[208,512]{1,0:T(8,128)(2,1)S(1)}, u32[]{:S(2)}, u32[]{:S(2)}) collective-permute-start(bf16[208,512]{1,0:T(8,128)(2,1)} %pack_first.1.refs_0_), channel_id=1, source_target_pairs={{0,6},{1,7},{2,4},{3,5},{4,2},{5,3},{6,0},{7,1},{8,14},{9,15},{10,... | collective-permute-start | bytes 638984 | tf_op jit(solution)/shard_map/ppermute | solution.py:43
  8.1 10.5 %collective-permute-start.3 = (bf16[208,512]{1,0:T(8,128)(2,1)}, bf16[208,512]{1,0:T(8,128)(2,1)S(1)}, u32[]{:S(2)}, u32[]{:S(2)}) collective-permute-start(bf16[208,512]{1,0:T(8,128)(2,1)} %pack_first.1.refs_0_), channel_id=1, source_target_pairs={{0,1},{1,0},{2,3},{3,2},{4,5},{5,4},{6,7},{7,6},{8,9},{9,8},{10,11... | collective-permute-start | bytes 638984 | tf_op jit(solution)/shard_map/ppermute | solution.py:43
  19.8 20.9 %collective-permute-start.7 = (bf16[576,512]{1,0:T(8,128)(2,1)}, bf16[576,512]{1,0:T(8,128)(2,1)S(1)}, u32[]{:S(2)}, u32[]{:S(2)}) collective-permute-start(bf16[576,512]{1,0:T(8,128)(2,1)} %pack_rest.1.refs_0_), channel_id=1, source_target_pairs={{0,2},{1,3},{2,0},{3,1},{4,6},{5,7},{6,4},{7,5},{8,10},{9,11},{10,... | collective-permute-start | bytes 1769480 | tf_op jit(solution)/shard_map/ppermute | solution.py:43
  20.8 20.6 %collective-permute-start.8 = (bf16[576,512]{1,0:T(8,128)(2,1)}, bf16[576,512]{1,0:T(8,128)(2,1)S(1)}, u32[]{:S(2)}, u32[]{:S(2)}) collective-permute-start(bf16[576,512]{1,0:T(8,128)(2,1)} %pack_rest.1.refs_0_), channel_id=1, source_target_pairs={{0,4},{1,5},{2,6},{3,7},{4,0},{5,1},{6,2},{7,3},{8,12},{9,13},{10,... | collective-permute-start | bytes 1769480 | tf_op jit(solution)/shard_map/ppermute | solution.py:43
  22.5 31.6 %collective-permute-start.9 = (bf16[576,512]{1,0:T(8,128)(2,1)}, bf16[576,512]{1,0:T(8,128)(2,1)S(1)}, u32[]{:S(2)}, u32[]{:S(2)}) collective-permute-start(bf16[576,512]{1,0:T(8,128)(2,1)} %pack_rest.1.refs_0_), channel_id=1, source_target_pairs={{0,1},{1,0},{2,3},{3,2},{4,5},{5,4},{6,7},{7,6},{8,9},{9,8},{10,11... | collective-permute-start | bytes 1769480 | tf_op jit(solution)/shard_map/ppermute | solution.py:43
  40.8 14.8 %collective-permute-start.10 = (bf16[576,512]{1,0:T(8,128)(2,1)S(1)}, bf16[576,512]{1,0:T(8,128)(2,1)S(1)}, u32[]{:S(2)}, u32[]{:S(2)}) collective-permute-start(bf16[576,512]{1,0:T(8,128)(2,1)S(1)} %collective-permute-done.7.refs_1_), channel_id=1, source_target_pairs={{0,1},{1,0},{2,3},{3,2},{4,5},{5,4},{6,7},{7,6},{8,9},{9,8},{10,11... | collective-permute-start | bytes 1769480 | tf_op jit(solution)/shard_map/ppermute | solution.py:43
  41.4 14.3 %collective-permute-start.11 = (bf16[576,512]{1,0:T(8,128)(2,1)S(1)}, bf16[576,512]{1,0:T(8,128)(2,1)S(1)}, u32[]{:S(2)}, u32[]{:S(2)}) collective-permute-start(bf16[576,512]{1,0:T(8,128)(2,1)S(1)} %collective-permute-done.8.refs_2_), channel_id=1, source_target_pairs={{0,1},{1,0},{2,3},{3,2},{4,5},{5,4},{6,7},{7,6},{8,9},{9,8},{10,11... | collective-permute-start | bytes 1769480 | tf_op jit(solution)/shard_map/ppermute | solution.py:43
  41.5 12.1 %collective-permute-start.13 = (bf16[288,512]{1,0:T(8,128)(2,1)S(1)}, bf16[288,512]{1,0:T(8,128)(2,1)S(1)}, u32[]{:S(2)}, u32[]{:S(2)}) collective-permute-start(bf16[288,512]{1,0:T(8,128)(2,1)S(1)} %slice.79), channel_id=1, source_target_pairs={{0,4},{1,5},{2,6},{3,7},{4,0},{5,1},{6,2},{7,3},{8,12},{9,13},{10,... | collective-permute-start | bytes 884744 | tf_op jit(solution)/shard_map/ppermute | solution.py:43
  42.4 11.2 %collective-permute-start.12 = (bf16[288,512]{1,0:T(8,128)(2,1)S(1)}, bf16[288,512]{1,0:T(8,128)(2,1)S(1)}, u32[]{:S(2)}, u32[]{:S(2)}) collective-permute-start(bf16[288,512]{1,0:T(8,128)(2,1)S(1)} %slice.78), channel_id=1, source_target_pairs={{0,2},{1,3},{2,0},{3,1},{4,6},{5,7},{6,4},{7,5},{8,10},{9,11},{10,... | collective-permute-start | bytes 884744 | tf_op jit(solution)/shard_map/ppermute | solution.py:43
  83.2 8.0 %collective-permute-start.16 = (bf16[4,592,512]{2,1,0:T(8,128)(2,1)}, bf16[4,592,512]{2,1,0:T(8,128)(2,1)}, u32[]{:S(2)}, u32[]{:S(2)}) collective-permute-start(bf16[4,592,512]{2,1,0:T(8,128)(2,1)} %get-tuple-element.100), channel_id=1, source_target_pairs={{0,1},{1,0},{2,3},{3,2},{4,5},{5,4},{6,7},{7,6},{8,9},{9,8},{10,11... | collective-permute-start | bytes 7274504 | tf_op jit(solution)/shard_map/ppermute | solution.py:43
  95.7 18.1 %collective-permute-start.18 = (bf16[2,272,512]{2,1,0:T(8,128)(2,1)}, bf16[2,272,512]{2,1,0:T(8,128)(2,1)S(1)}, u32[]{:S(2)}, u32[]{:S(2)}) collective-permute-start(bf16[2,272,512]{2,1,0:T(8,128)(2,1)} %get-tuple-element.138), channel_id=1, source_target_pairs={{0,2},{1,3},{2,0},{3,1},{4,6},{5,7},{6,4},{7,5},{8,10},{9,11},{10,... | collective-permute-start | bytes 1671176 | tf_op jit(solution)/shard_map/ppermute | solution.py:43
  96.7 17.1 %collective-permute-start.17 = (bf16[2,320,512]{2,1,0:T(8,128)(2,1)}, bf16[2,320,512]{2,1,0:T(8,128)(2,1)S(1)}, u32[]{:S(2)}, u32[]{:S(2)}) collective-permute-start(bf16[2,320,512]{2,1,0:T(8,128)(2,1)} %get-tuple-element.139), channel_id=1, source_target_pairs={{0,4},{1,5},{2,6},{3,7},{4,0},{5,1},{6,2},{7,3},{8,12},{9,13},{10,... | collective-permute-start | bytes 1966088 | tf_op jit(solution)/shard_map/ppermute | solution.py:43
  113.9 8.5 %collective-permute-start.20 = (bf16[1,272,512]{2,1,0:T(8,128)(2,1)S(1)}, bf16[1,272,512]{2,1,0:T(8,128)(2,1)}, u32[]{:S(2)}, u32[]{:S(2)}) collective-permute-start(bf16[1,272,512]{2,1,0:T(8,128)(2,1)S(1)} %get-tuple-element.147), channel_id=1, source_target_pairs={{0,4},{1,5},{2,6},{3,7},{4,0},{5,1},{6,2},{7,3},{8,12},{9,13},{10,... | collective-permute-start | bytes 835592 | tf_op jit(solution)/shard_map/ppermute | solution.py:43
  115.0 9.1 %collective-permute-start.19 = (bf16[1,320,512]{2,1,0:T(8,128)(2,1)S(1)}, bf16[1,320,512]{2,1,0:T(8,128)(2,1)S(1)}, u32[]{:S(2)}, u32[]{:S(2)}) collective-permute-start(bf16[1,320,512]{2,1,0:T(8,128)(2,1)S(1)} %get-tuple-element.144), channel_id=1, source_target_pairs={{0,2},{1,3},{2,0},{3,1},{4,6},{5,7},{6,4},{7,5},{8,10},{9,11},{10,... | collective-permute-start | bytes 983048 | tf_op jit(solution)/shard_map/ppermute | solution.py:43
  125.5 7.7 %collective-permute-start.21 = (bf16[296,512]{1,0:T(8,128)(2,1)S(1)}, bf16[296,512]{1,0:T(8,128)(2,1)S(1)}, u32[]{:S(2)}, u32[]{:S(2)}) collective-permute-start(bf16[296,512]{1,0:T(8,128)(2,1)S(1)} %fusion.3), channel_id=1, source_target_pairs={{0,8},{8,0},{16,24},{24,16},{1,9},{9,1},{17,25},{25,17},{2,10},{10... | collective-permute-start | bytes 909320 | tf_op jit(solution)/shard_map/ppermute | solution.py:39
  127.9 15.4 %collective-permute-start.23 = (bf16[208,512]{1,0:T(8,128)(2,1)}, bf16[208,512]{1,0:T(8,128)(2,1)S(1)}, u32[]{:S(2)}, u32[]{:S(2)}) collective-permute-start(bf16[208,512]{1,0:T(8,128)(2,1)} %get-tuple-element.141), channel_id=1, source_target_pairs={{0,6},{1,7},{2,4},{3,5},{4,2},{5,3},{6,0},{7,1},{8,14},{9,15},{10,... | collective-permute-start | bytes 638984 | tf_op jit(solution)/shard_map/ppermute | solution.py:43
  129.9 13.4 %collective-permute-start.24 = (bf16[208,512]{1,0:T(8,128)(2,1)S(1)}, bf16[208,512]{1,0:T(8,128)(2,1)S(1)}, u32[]{:S(2)}, u32[]{:S(2)}) collective-permute-start(bf16[208,512]{1,0:T(8,128)(2,1)S(1)} %get-tuple-element.142), channel_id=1, source_target_pairs={{0,4},{1,5},{2,6},{3,7},{4,0},{5,1},{6,2},{7,3},{8,12},{9,13},{10,... | collective-permute-start | bytes 638984 | tf_op jit(solution)/shard_map/ppermute | solution.py:43
  130.5 12.9 %collective-permute-start.25 = (bf16[208,512]{1,0:T(8,128)(2,1)S(1)}, bf16[208,512]{1,0:T(8,128)(2,1)S(1)}, u32[]{:S(2)}, u32[]{:S(2)}) collective-permute-start(bf16[208,512]{1,0:T(8,128)(2,1)S(1)} %get-tuple-element.143), channel_id=1, source_target_pairs={{0,2},{1,3},{2,0},{3,1},{4,6},{5,7},{6,4},{7,5},{8,10},{9,11},{10,... | collective-permute-start | bytes 638984 | tf_op jit(solution)/shard_map/ppermute | solution.py:43
  133.7 14.3 %collective-permute-start.27 = (bf16[296,512]{1,0:T(8,128)(2,1)S(1)}, bf16[296,512]{1,0:T(8,128)(2,1)S(1)}, u32[]{:S(2)}, u32[]{:S(2)}) collective-permute-start(bf16[296,512]{1,0:T(8,128)(2,1)S(1)} %fusion.5), channel_id=1, source_target_pairs={{0,16},{8,24},{16,0},{24,8},{1,17},{9,25},{17,1},{25,9},{2,18},{10... | collective-permute-start | bytes 909320 | tf_op jit(solution)/shard_map/ppermute | solution.py:39
  148.1 13.9 %collective-permute-start.30 = (bf16[296,512]{1,0:T(8,128)(2,1)S(1)}, bf16[296,512]{1,0:T(8,128)(2,1)S(1)}, u32[]{:S(2)}, u32[]{:S(2)}) collective-permute-start(bf16[296,512]{1,0:T(8,128)(2,1)S(1)} %add.117.s), channel_id=1, source_target_pairs={{0,8},{8,0},{16,24},{24,16},{1,9},{9,1},{17,25},{25,17},{2,10},{10... | collective-permute-start | bytes 909320 | tf_op jit(solution)/shard_map/ppermute | solution.py:39
  150.3 7.4 %collective-permute-start.28 = (bf16[104,512]{1,0:T(8,128)(2,1)S(1)}, bf16[104,512]{1,0:T(8,128)(2,1)S(1)}, u32[]{:S(2)}, u32[]{:S(2)}) collective-permute-start(bf16[104,512]{1,0:T(8,128)(2,1)S(1)} %dynamic-slice_add_fusion), channel_id=1, source_target_pairs={{0,16},{8,24},{16,0},{24,8},{1,17},{9,25},{17,1},{25,9},{2,18},{10... | collective-permute-start | bytes 319496 | tf_op jit(solution)/shard_map/ppermute | solution.py:39
  157.7 6.9 %collective-permute-start.29 = (bf16[104,512]{1,0:T(8,128)(2,1)S(1)}, bf16[104,512]{1,0:T(8,128)(2,1)S(1)}, u32[]{:S(2)}, u32[]{:S(2)}) collective-permute-start(bf16[104,512]{1,0:T(8,128)(2,1)S(1)} %add.119.s), channel_id=1, source_target_pairs={{0,8},{8,0},{16,24},{24,16},{1,9},{9,1},{17,25},{25,17},{2,10},{10... | collective-permute-start | bytes 319496 | tf_op jit(solution)/shard_map/ppermute | solution.py:39
  (28 other events, 165.6 us)

commit v8 on v7

--- a/solution.py
+++ b/solution.py
@@ -106,18 +106,8 @@
     return [b for b in (2 << i for i in range(16)) if b < nr]
 
 
-GROUPS = 1
-
-
-def pack_first_body(me, w, upb, *refs):
-    vecs = refs[:-GROUPS]
-    outs = refs[-GROUPS:]
-    r, W = w.shape
-    D = W // 3
-    gw = D // GROUPS
-    for g, out in enumerate(outs):
-        for j in range(3):
-            out[j * r : (j + 1) * r, :] = w[:, j * D + g * gw : j * D + (g + 1) * gw]
+def pack_body(nv, me, wo, wu, wd, upb, *refs):
+    vecs, (block, out) = refs[:nv], refs[nv:]
 
     def spot(v):
         w_ = v.shape[1]
@@ -128,31 +118,7 @@
         return [jnp.where(lane // w_ == me[0] % t, jnp.concatenate([v] * t, axis=1), jnp.zeros((1, LANES), f32))]
 
     rows = [a for v in vecs for a in spot(v[...].astype(f32))] + spot(upb[...].astype(f32))
-    b = jnp.concatenate(rows + [jnp.zeros((VROWS - len(rows), LANES), f32)], axis=0).astype(bf16)
-    outs[0][3 * r :, :] = jnp.concatenate([b, jnp.zeros((VROWS, gw - LANES), bf16)], axis=1) if gw > LANES else b
-
-
-def whole(n):
-    return [pl.BlockSpec(memory_space=pltpu.VMEM)] * n
-
-
-def once(*arrays):
-    return [pl.BlockSpec(a.shape, lambda i, *m, nd=len(a.shape): (0,) * nd) for a in arrays]
-
-
-def pack_first(me, w, vecs, upb):
-    r, W = w.shape
-    gw = W // 3 // GROUPS
-    args = [w, upb[None]] + [v[None] for v in vecs]
-    outs = [S((3 * r + (VROWS if g == 0 else 0), gw), bf16) for g in range(GROUPS)]
-    return pl.pallas_call(
-        pack_first_body,
-        grid_spec=pltpu.PrefetchScalarGridSpec(num_scalar_prefetch=1, grid=(1,), in_specs=once(*args), out_specs=once(*outs)),
-        out_shape=outs, compiler_params=cp(), name="pack_first", cost_estimate=cost(0, 4 * w.size),
-    )(me, *args)
-
-
-def pack_rest_body(wo, wu, wd, out):
+    block[...] = jnp.concatenate(rows + [jnp.zeros((VROWS - len(rows), LANES), f32)], axis=0).astype(bf16)
     r, D = wo.shape
     out[:r, :] = wo[...]
     for j in range(wu.shape[1] // D):
@@ -160,13 +126,23 @@
     out[(1 + wu.shape[1] // D) * r :, :] = wd[...]
 
 
-def pack_rest(wo, wu, wd):
+def whole(n):
+    return [pl.BlockSpec(memory_space=pltpu.VMEM)] * n
+
+
+def once(*arrays):
+    return [pl.BlockSpec(a.shape, lambda i, *m, nd=len(a.shape): (0,) * nd) for a in arrays]
+
+
+def pack(me, vecs, upb, wo, wu, wd):
+    args = [wo, wu, wd, upb[None]] + [v[None] for v in vecs]
     D = wo.shape[1]
-    out = S(((wo.size + wu.size + wd.size) // D, D), bf16)
-    return pl.pallas_call(
-        pack_rest_body, grid=(1,), in_specs=once(wo, wu, wd), out_specs=once(out)[0],
-        out_shape=out, compiler_params=cp(), name="pack_rest", cost_estimate=cost(0, 4 * wu.size),
-    )(wo, wu, wd)
+    outs = [S((VROWS, LANES), bf16), S(((wo.size + wu.size + wd.size) // D, D), bf16)]
+    return pl.pallas_call(
+        functools.partial(pack_body, len(vecs)),
+        grid_spec=pltpu.PrefetchScalarGridSpec(num_scalar_prefetch=1, grid=(1,), in_specs=once(*args), out_specs=once(*outs)),
+        out_shape=outs, compiler_params=cp(), name="pack", cost_estimate=cost(0, 4 * wu.size),
+    )(me, *args)
 
 
 def own_lanes(tiles, me, w):
@@ -290,12 +266,6 @@
     return pl.multiple_of(x, m)
 
 
-def weight_segs(w, r):
-    gw = w.shape[1] // 3
-    seg = lambda j: (j * r, r, lambda s, o, c: w.at[pl.ds(mult(s * r + o, 16), c), pl.ds(j * gw, gw)], gw)
-    return [seg(j) for j in range(3)]
-
-
 def start_body(tok, step, nx, xht):
     n, _ = norm(tok[...].astype(f32) + step[...].astype(f32))
     nx[...] = n
@@ -312,26 +282,30 @@
     )(tok, step)
 
 
-def front_body(scale, n, meta, me, nx, *refs):
+def front_body(scale, n, meta, vmeta, me, nx, *refs):
     np_ = len(meta)
     pieces = refs[:np_]
-    kv, qkvt, wout, vec, upb, nv, h, w, vbuf, sems, own = refs[np_:]
+    vpieces = refs[np_ : np_ + len(vmeta)]
+    kv, qkvt, wout, vec, upb, nv, h, w, vbuf, sems, own = refs[np_ + len(vmeta) :]
     T, D = nv.shape
     r = D // n
     FF = upb.shape[1]
     i = pl.program_id(0)
     cw = kv.shape[2]
     per_j = D // cw
-    segs = [(3 * r, VROWS, lambda s, o, c: vbuf.at[s, pl.ds(o, c)], LANES)] + weight_segs(w, r)
+    vsegs = [(0, VROWS, lambda s, o, c: vbuf.at[s, pl.ds(o, c)], LANES)]
+    wsegs = [(0, r, lambda s, o, c: w.at[pl.ds(mult(s * r + o, 16), c)], 3 * D)]
+    half = sems.shape[0] // 2
     load = pltpu.make_async_copy(nx, nv, own.at[0])
     save = pltpu.make_async_copy(w, wout, own.at[1])
 
     @pl.when(i == 0)
     def _():
-        cs = pull(me[0], pieces, meta, segs, sems)
+        cs = pull(me[0], vpieces, vmeta, vsegs, sems.at[pl.ds(0, half)])
+        cs += pull(me[0], pieces, meta, wsegs, sems.at[pl.ds(half, half)])
+        load.start()
         for c in cs:
             c.start()
-        load.start()
         for c in cs:
             c.wait()
         save.start()
@@ -370,30 +344,33 @@
     return pl.CostEstimate(flops=int(flops), bytes_accessed=int(nbytes), transcendentals=int(tr))
 
 
-def front(me, nx, pieces, n, FF, cw=256):
+def front(me, nx, pieces, vpieces, n, FF, cw=512):
     T, D = nx.shape
     scale = 1.0 / math.sqrt(D // HEADS)
     meta = tuple((k, r0) for k, r0, _ in pieces)
+    vmeta = tuple((k, r0) for k, r0, _ in vpieces)
     q = D // cw
     keep = lambda *sh: pl.BlockSpec(sh, lambda i, m: (0,) * len(sh))
     rest = lambda i: jnp.maximum(i - q, 0)
     V = pltpu.VMEM
     return pl.pallas_call(
-        functools.partial(front_body, scale, n, meta),
+        functools.partial(front_body, scale, n, meta, vmeta),
         grid_spec=pltpu.PrefetchScalarGridSpec(
             num_scalar_prefetch=1, grid=(3 * q,),
-            in_specs=[ANY] * (1 + len(pieces)),
+            in_specs=[ANY] * (1 + len(pieces) + len(vpieces)),
             out_specs=[pl.BlockSpec((1, T, cw), lambda i, m: (rest(i) // q, 0, rest(i) % q)), pl.BlockSpec((1, cw, T), lambda i, m: (i // q, i % q, 0)), ANY, keep(8, D), keep(1, FF)],
             scratch_shapes=[V((T, D), f32), V((T, D), bf16), V((D, 3 * D), bf16), V((n, VROWS, LANES), bf16), pltpu.SemaphoreType.DMA((8 * len(pieces),)), pltpu.SemaphoreType.DMA((2,))]),
         out_shape=[S((2, T, D), bf16), S((3, D, T), bf16), S((D, 3 * D), bf16), S((8, D), f32), S((1, FF), f32)],
         compiler_params=cp(), name="front", cost_estimate=cost(6 * T * D * D, 12 * T * D),
-    )(me, nx, *[a for _, _, a in pieces])
-
-
-def attn_fwd_body(HD, bi, CR, ln, k, qt, vt, *refs):
-    et, mixed, mixedt, mixedf, linv, scr, ka = refs[-7:]
+    )(me, nx, *[a for _, _, a in pieces + vpieces])
+
+
+def attn_fwd_body(HD, bi, CR, p0, ln, k, qt, vt, *refs):
+    et, mixed, mixedt, mixedf, linv, scr, ka, eb, esem = refs[-9:]
     T, PW = k.shape
     n = ln[0]
+    p = pl.program_id(0)
+    last = p == pl.num_programs(0) - 1
     rid = lax.broadcasted_iota(jnp.int32, (PW, bi), 0)
     lane = lax.broadcasted_iota(jnp.int32, (T, PW), 1)
     rows = lax.broadcasted_iota(jnp.int32, (T, PW), 0)
@@ -420,6 +397,15 @@
     for t, (b, h) in enumerate(tasks):
         sl = slice(b * bi, (b + 1) * bi)
         more = t + 1 < len(tasks)
+        put = pltpu.make_async_copy(eb.at[t % 2], et.at[2 * (p0 + p) + h, :, pl.ds(b * bi, bi)], esem.at[t % 2])
+        if t < 2:
+
+            @pl.when(p > 0)
+            def _():
+                put.wait()
+
+        else:
+            put.wait()
         if more:
             q = query(t + 1)
         nxt = []
@@ -427,8 +413,9 @@
             cs = slice(c * CR, (c + 1) * CR)
             if more:
                 nxt.append(score(t + 1, c, q))
-            et[h, cs, sl] = jnp.exp(scr[t % 2, cs, :] - m).astype(bf16)
-        o = dot(va[h], et[h, :, sl])
+            eb[t % 2, cs, :] = jnp.exp(scr[t % 2, cs, :] - m).astype(bf16)
+        put.start()
+        o = dot(va[h], eb[t % 2])
         if more:
             m = functools.reduce(jnp.maximum, nxt)
         inv = 1.0 / o[HD : HD + 1, :]
@@ -443,6 +430,11 @@
             mixedt[:, sl] = mt
             mixed[sl, :] = mt.T
 
+    @pl.when(last)
+    def _():
+        for q in range(2):
+            pltpu.make_async_copy(eb.at[q], et.at[0, :, pl.ds(0, bi)], esem.at[q]).wait()
+
 
 def attn_fwd(ln, kv, qkvt, p0, cnt, prev):
     _, T, D = kv.shape
@@ -452,12 +444,12 @@
     bi = min(512, T)
     prev = list(prev)
     return pl.pallas_call(
-        functools.partial(attn_fwd_body, HD, bi, min(256, T)),
+        functools.partial(attn_fwd_body, HD, bi, min(256, T), p0),
         grid_spec=pltpu.PrefetchScalarGridSpec(
             num_scalar_prefetch=1, grid=(cnt,),
             in_specs=[pl.BlockSpec((None, T, PW), lambda p, r: (0, 0, p0 + p)), pl.BlockSpec((None, PW, T), lambda p, r: (0, p0 + p, 0)), pl.BlockSpec((None, PW, T), lambda p, r: (2, p0 + p, 0))] + [ANY] * len(prev),
-            out_specs=[pl.BlockSpec((2, T, T), lambda p, r: (p0 + p, 0, 0)), pl.BlockSpec((T, PW), lambda p, r: (0, p0 + p)), pl.BlockSpec((PW, T), lambda p, r: (p0 + p, 0)), pl.BlockSpec((PW, T), lambda p, r: (p0 + p, 0)), pl.BlockSpec((None, 8, T), lambda p, r: (p0 + p, 0, 0))],
-            scratch_shapes=[pltpu.VMEM((2, T, bi), f32), pltpu.VMEM((T, 2 * PW), bf16)]),
+            out_specs=[ANY, pl.BlockSpec((T, PW), lambda p, r: (0, p0 + p)), pl.BlockSpec((PW, T), lambda p, r: (p0 + p, 0)), pl.BlockSpec((PW, T), lambda p, r: (p0 + p, 0)), pl.BlockSpec((None, 8, T), lambda p, r: (p0 + p, 0, 0))],
+            scratch_shapes=[pltpu.VMEM((2, T, bi), f32), pltpu.VMEM((T, 2 * PW), bf16), pltpu.VMEM((2, T, bi), bf16), pltpu.SemaphoreType.DMA((2,))]),
         out_shape=[S((HEADS, T, T), bf16), S((T, D), bf16), S((D, T), bf16), S((D, T), f32), S((NP, 8, T), f32)],
         input_output_aliases={4 + i: i for i in range(len(prev))},
         compiler_params=cp(), name="attn_fwd", cost_estimate=cost(cnt * 2 * 8 * T * T * 128, cnt * 2 * T * T * 2, cnt * 2 * T * T),
@@ -529,7 +521,6 @@
     live = (lax.broadcasted_iota(jnp.int32, (bm, 1), 0) + i * bm) < ln[0]
     gd = jnp.where(live, cot[...], jnp.zeros_like(cot))
     acc = x1 + row(v, 7)
-    gh = None
     nc = FF // ch
     sl = [slice(c * ch, (c + 1) * ch) for c in range(nc)]
     lead = lambda c: (dot(h2, wu[:, sl[c]]), dot_t(gd, wd[sl[c], :]))
@@ -556,16 +547,15 @@
         gu = (ga * dg).astype(bf16)
         gup[ro, sl[c]] = gu
         upsum[:, sl[c]] += jnp.sum(gu.astype(f32), axis=0, keepdims=True)
-        acc = acc + dot(a, wd[sl[c], :])
-        p = dot_t(gu, wu[:, sl[c]])
-        gh = p if gh is None else gh + p
-    out[...] = jnp.where(live, acc, 0.0).astype(bf16)
+    gh = dot_t(gup[ro, :], wu[...])
     gn = gh * row(v, 5)
     gx = gd.astype(f32) + rr * (gn - jnp.mean(gn, axis=-1, keepdims=True) - nx * jnp.mean(gn * nx, axis=-1, keepdims=True))
     gx1[...] = gx
     gab = gx.astype(bf16)
     gattn[ro, :] = gab
     gmt[...] = dot_t(gab, wo[...]).astype(bf16).T
+    acc = acc + dot(act[ro, :], wd[...])
+    out[...] = jnp.where(live, acc, 0.0).astype(bf16)
     s_ = lambda a: jnp.sum(a.astype(f32), axis=0, keepdims=True)
     sums[...] += jnp.concatenate([s_(gab), s_(gh * nx), s_(gh), s_(gd), jnp.zeros((4, D), f32)], axis=0)
 
@@ -703,7 +693,7 @@
 def back_body(tok, step, vec, g, gx1, *refs):
     ws, tg = refs[:-1], refs[-1]
     D = tok.shape[1]
-    gw = D // GROUPS
+    gw = D
     x = tok[...].astype(f32) + step[...].astype(f32)
     nx, rr = norm(x)
     gt = sum(dot(w[:, j * gw : (j + 1) * gw], g[j, q * gw : (q + 1) * gw, :]) for q, w in enumerate(ws) for j in range(3))
@@ -732,12 +722,12 @@
     FF = up_bias.shape[0] * n
     nc = FF // D
     rf = FF // n
-    packs = pack_first(mes, qkv_weight, [ln1_gain, ln1_bias, q_bias, v_bias, out_bias, ln2_gain, ln2_bias, down_bias], up_bias)
-    pack2 = pack_rest(out_weight, up_weight, down_weight)
+    vblock, pack2 = pack(mes, [ln1_gain, ln1_bias, q_bias, v_bias, out_bias, ln2_gain, ln2_bias, down_bias], up_bias, out_weight, up_weight, down_weight)
     NP = HEADS // 2
     nx, xht = start(tok, step)
-    pieces = gather_direct(packs[0], n, xht, pack2)
-    kv, qkvt, w, vec, upb = front(mes, nx, pieces, n, FF)
+    vpieces = gather_direct(vblock, n, xht)
+    pieces = gather_direct(qkv_weight, n, xht, *[a for _, _, a in vpieces[1:]])
+    kv, qkvt, w, vec, upb = front(mes, nx, pieces, vpieces, n, FF)
     fw = attn_fwd(lengths, kv, qkvt, 0, NP // 2, [])
     fw2 = attn_fwd(lengths, kv, qkvt, NP // 2, NP // 2, fw)
     et, mixed, mixedt, mixedf, linv = fw2

time: 167 us -> 173 us (1.036)
  starting transfers between devices: 31.9 us -> 37.9 us
    ppermute x25 -> x32, starting transfers between devices: 19.1 us -> 25.2 us  [swap(): return lax.ppermute(x, 'shard', xor_perm(lax.axis_size('shard'), k))]
    pallas_call x5 -> x4, Pallas kernels: 31.7 us -> 28.2 us  [the longest x2 19.4 us: attn_fwd(): pl.pallas_call(functools.partial(attn_fwd_body, HD, bi, min(256, T), p0),...]
    pallas_call x1, Pallas kernels: 26.5 us -> 29.6 us  [ffn(): pl.pallas_call(functools.partial(ffn_body, n, meta, min(1024, FF)), grid_...]
    ppermute x25 -> x32, waiting for transfers between devices: 7.97 us -> 8.11 us  [swap(): return lax.ppermute(x, 'shard', xor_perm(lax.axis_size('shard'), k))]
  transfers between devices with their start and end apart: 31 -> 38, of which waited for: 12 -> 16; matrix products, arithmetic and copies ran while one was open for 2% -> 2% of each run, Pallas kernels for 44% -> 41%
where the time goes in v8:
time: 173 us
  Pallas kernels  102 us (59%)
  starting transfers between devices  37.9 us (22%)
  waiting for transfers between devices  21.6 us (12%)
  other arithmetic  7.54 us (4%)
  local copies, waits for them, and re-layouts  2.43 us (1%)
  between operations  1.79 us (1%)
    pallas_call x1, Pallas kernels, ffn(): pl.pallas_call(functools.partial(ffn_body, n, meta, min(1024, FF)), grid_...  29.6 us
    ppermute x32, starting transfers between devices, swap(): return lax.ppermute(x, 'shard', xor_perm(lax.axis_size('shard'), k))  25.2 us
    pallas_call x2, Pallas kernels, attn_bwd(): pl.pallas_call(functools.partial(attn_bwd_body, HD, 1.0 / math.sqrt(HD),...  23.9 us
    pallas_call x2, Pallas kernels, attn_fwd(): pl.pallas_call(functools.partial(attn_fwd_body, HD, bi, min(256, T), p0),...  19.4 us
    ppermute x6, waiting for transfers between devices, rep_perm(): return lax.ppermute(x, 'rep', xor_perm(lax.axis_size('rep'), b))  13.4 us
    ppermute x6, starting transfers between devices, rep_perm(): return lax.ppermute(x, 'rep', xor_perm(lax.axis_size('rep'), b))  12.7 us
    ppermute x32, waiting for transfers between devices, swap(): return lax.ppermute(x, 'shard', xor_perm(lax.axis_size('shard'), k))  8.11 us
    pallas_call x1, Pallas kernels, back(): pl.pallas_call(back_body, grid=(T // bm,), in_specs=[rows, full(step), fu...  6.96 us
  transfers between devices with their start and end apart: 38, of which 16 were waited for; matrix products, arithmetic and copies ran while one was open for 2% of the time, Pallas kernels for 41%

profile of v8, /device:TPU:0, one launch (start us, length us, event | category | flops | bytes accessed | tf_op | source)
XLA Modules:
  0.0 172.9 jit_solution(9983256936557335185)
XLA Ops:
  0.6 4.0 %collective-permute-start.9 = (bf16[64,1536]{1,0:T(8,128)(2,1)}, bf16[64,1536]{1,0:T(8,128)(2,1)S(1)}, u32[]{:S(2)}, u32[]{:S(2)}) collective-permute-start(bf16[64,1536]{1,0:T(8,128)(2,1)} %w.1), channel_id=1, source_target_pairs={{0,6},{1,7},{2,4},{3,5},{4,2},{5,3},{6,0},{7,1},{8,14},{9,15},{10,... | collective-permute-start | bytes 589832 | tf_op jit(solution)/shard_map/ppermute | solution.py:43
  6.5 2.0 %pack.1 = (bf16[16,128]{1,0:T(8,128)(2,1)}, bf16[576,512]{1,0:T(8,128)(2,1)}) custom-call(s32[1]{0:T(128)} %bitcast.me, bf16[64,512]{1,0:T(8,128)(2,1)} %wo.1, bf16[64,2048]{1,0:T(8,128)(2,1)} %wu.1, bf16[256,512]{1,0:T(8,128)(2,1)} %wd.1, bf16[1,256]{1,0:T(2,128)(2,1)} %broadcast_in_dim.39.upb, bf16[1,64]{1,0:T(2,128)(2,1)} %bitcast.38, ...), custom_call_target="tpu_custom_call" | custom-call | bytes 524288 | tf_op jit(solution)/shard_map/pack/pallas_call | solution.py:141
  8.5 1.9 %collective-permute-start.1 = (bf16[16,128]{1,0:T(8,128)(2,1)}, bf16[16,128]{1,0:T(8,128)(2,1)S(1)}, u32[]{:S(2)}, u32[]{:S(2)}) collective-permute-start(bf16[16,128]{1,0:T(8,128)(2,1)} %get-tuple-element.83.refs_8_), channel_id=1, source_target_pairs={{0,2},{1,3},{2,0},{3,1},{4,6},{5,7},{6,4},{7,5},{8,10},{9,11},{10,... | collective-permute-start | bytes 12296 | tf_op jit(solution)/shard_map/ppermute | solution.py:43
  11.9 2.4 %collective-permute-done.1.refs_9_ = bf16[16,128]{1,0:T(8,128)(2,1)S(1)} collective-permute-done((bf16[16,128]{1,0:T(8,128)(2,1)}, bf16[16,128]{1,0:T(8,128)(2,1)S(1)}, u32[]{:S(2)}, u32[]{:S(2)}) %collective-permute-start.1) | collective-permute-done | bytes 4128 | tf_op jit(solution)/shard_map/ppermute | solution.py:43
  15.7 4.2 %start.1 = (f32[1024,512]{1,0:T(8,128)}, bf16[512,1024]{1,0:T(8,128)(2,1)}) custom-call(bf16[1024,512]{1,0:T(8,128)(2,1)} %bitcast.42, bf16[1,512]{1,0:T(2,128)(2,1)} %step.4), custom_call_target="tpu_custom_call" | custom-call | flops 10485760 | bytes 4194304 | tf_op jit(solution)/shard_map/start/pallas_call | solution.py:278
  27.9 6.8 %front.1 = (bf16[2,1024,512]{2,1,0:T(8,128)(2,1)}, bf16[3,512,1024]{2,1,0:T(8,128)(2,1)}, bf16[512,1536]{1,0:T(8,128)(2,1)}, f32[8,512]{1,0:T(8,128)}, f32[1,2048]{1,0:T(1,128)}) custom-call(s32[1]{0:T(128)} %bitcast.me, f32[1024,512]{1,0:T(8,128)} %get-tuple-element.81.nx, bf16[64,1536]{1,0:T(8,128)(2,1)} %w.1, bf16[64,1536]{1,0:T(8,128)(2,1)} %copy-done.16, ...), custom_call_target="tpu_custom_call" | custom-call | flops 1610612736 | bytes 6291456 | tf_op jit(solution)/shard_map/front/pallas_call | solution.py:356
  34.7 9.7 %attn_fwd.2 = (bf16[8,1024,1024]{2,1,0:T(8,128)(2,1)}, bf16[1024,512]{1,0:T(8,128)(2,1)}, bf16[512,1024]{1,0:T(8,128)(2,1)}, f32[512,1024]{1,0:T(8,128)}, f32[4,8,1024]{2,1,0:T(8,128)}) custom-call(s32[1]{0:T(128)S(6)} %copy.44.ln, bf16[2,1024,512]{2,1,0:T(8,128)(2,1)} %get-tuple-element.92.k.v, bf16[3,512,1024]{2,1,0:T(8,128)(2,1)} %get-tuple-element.93.qt.vt.kt, ...), custom_call_target="tpu_custom_call" | custom-call | flops 4294967296 | bytes 8388608 | tf_op jit(solution)/shard_map/attn_fwd/pallas_call | solution.py:446
  47.2 9.6 %attn_fwd.3 = (bf16[8,1024,1024]{2,1,0:T(8,128)(2,1)}, bf16[1024,512]{1,0:T(8,128)(2,1)}, bf16[512,1024]{1,0:T(8,128)(2,1)}, f32[512,1024]{1,0:T(8,128)}, f32[4,8,1024]{2,1,0:T(8,128)}) custom-call(s32[1]{0:T(128)S(6)} %copy.44.ln, ...), custom_call_target="tpu_custom_call", output_to_operand_aliasing={{0}: (4, {}), {1}: (5, {}), {2}: (6, {}), {3}: (7, {}), {4}... | custom-call | flops 4294967296 | bytes 8388608 | tf_op jit(solution)/shard_map/attn_fwd/pallas_call | solution.py:446
  60.1 29.6 %ffn.1 = (bf16[1024,512]{1,0:T(8,128)(2,1)}, f32[1024,512]{1,0:T(8,128)}, bf16[512,1024]{1,0:T(8,128)(2,1)}, bf16[4,592,512]{2,1,0:T(8,128)(2,1)}, bf16[4,592,512]{2,1,0:T(8,128)(2,1)}) custom-call(s32[1]{0:T(128)S(6)} %copy.44.ln, s32[1]{0:T(128)} %bitcast.me, bf16[1024,512]{1,0:T(8,128)(2,1)} %bitcast.43, bf16[1,512]{1,0:T(2,128)(2,1)} %step.4, ...), custom_call_target="tpu_custom_call" | custom-call | flops 14495514624 | bytes 8388608 | tf_op jit(solution)/shard_map/ffn/pallas_call | solution.py:600
  89.9 7.8 %attn_bwd.2.refs_0_ = bf16[3,512,1024]{2,1,0:T(8,128)(2,1)} custom-call(bf16[2,1024,512]{2,1,0:T(8,128)(2,1)} %get-tuple-element.92.k.v, bf16[3,512,1024]{2,1,0:T(8,128)(2,1)} %get-tuple-element.93.qt.vt.kt, bf16[3,512,1024]{2,1,0:T(8,128)(2,1)} %get-tuple-element.93.qt.vt.kt, bf16[512,1024]{1,0:T(8,128)(2,1)} %get-tuple-element.115.gt, ...), custom_call_target="tpu_custom_call" | custom-call | flops 4294967296 | bytes 4194304 | tf_op jit(solution)/shard_map/attn_bwd/pallas_call | solution.py:644
  97.7 2.2 %slice_add_fusion.2 = (bf16[2,272,512]{2,1,0:T(8,128)(2,1)S(1)}, bf16[2,272,512]{2,1,0:T(8,128)(2,1)}) fusion(bf16[4,592,512]{2,1,0:T(8,128)(2,1)} %collective-permute-done.23, bf16[4,592,512]{2,1,0:T(8,128)(2,1)S(1)} %copy-done.3), kind=kLoop, calls=%fused_computation.6 | loop fusion | flops 557056 | bytes 3342336 | tf_op jit(solution)/shard_map/add | solution.py:82
  99.9 2.3 %slice_add_fusion = (bf16[2,320,512]{2,1,0:T(8,128)(2,1)}, bf16[2,320,512]{2,1,0:T(8,128)(2,1)S(1)}) fusion(bf16[4,592,512]{2,1,0:T(8,128)(2,1)} %collective-permute-done.23, bf16[4,592,512]{2,1,0:T(8,128)(2,1)S(1)} %copy-done.3), kind=kLoop, calls=%fused_computation.4 | loop fusion | flops 655360 | bytes 3932160 | tf_op jit(solution)/shard_map/add | solution.py:82
  102.5 1.7 collective-permute-start.24
  104.2 16.0 %attn_bwd.3.g = bf16[3,512,1024]{2,1,0:T(8,128)(2,1)} custom-call(bf16[2,1024,512]{2,1,0:T(8,128)(2,1)} %get-tuple-element.92.k.v, bf16[3,512,1024]{2,1,0:T(8,128)(2,1)} %get-tuple-element.93.qt.vt.kt, bf16[3,512,1024]{2,1,0:T(8,128)(2,1)} %get-tuple-element.93.qt.vt.kt, bf16[512,1024]{1,0:T(8,128)(2,1)} %get-tuple-element.115.gt, ...), custom_call_target="tpu_custom_call", output_to_operand_aliasing={{}: (7, {})} | custom-call | flops 12884901888 | bytes 12582912 | tf_op jit(solution)/shard_map/attn_bwd/pallas_call | solution.py:644
  122.9 5.6 %wqkv.1 = (bf16[4,208,512]{2,1,0:T(8,128)(2,1)}, bf16[4,208,512]{2,1,0:T(8,128)(2,1)}) custom-call(s32[1]{0:T(128)} %bitcast.me, bf16[512,1024]{1,0:T(8,128)(2,1)} %get-tuple-element.118.xht, bf16[3,512,1024]{2,1,0:T(8,128)(2,1)} %attn_bwd.3.g), custom_call_target="tpu_custom_call" | custom-call | flops 1610612736 | bytes 5242880 | tf_op jit(solution)/shard_map/wqkv/pallas_call | solution.py:681
  131.4 1.8 %collective-permute-start.28 = (bf16[296,512]{1,0:T(8,128)(2,1)S(1)}, bf16[296,512]{1,0:T(8,128)(2,1)S(1)}, u32[]{:S(2)}, u32[]{:S(2)}) collective-permute-start(bf16[296,512]{1,0:T(8,128)(2,1)S(1)} %fusion.3), channel_id=1, source_target_pairs={{0,8},{8,0},{16,24},{24,16},{1,9},{9,1},{17,25},{25,17},{2,10},{10... | collective-permute-start | bytes 909320 | tf_op jit(solution)/shard_map/ppermute | solution.py:39
  134.0 2.5 %collective-permute-start.30 = (bf16[208,512]{1,0:T(8,128)(2,1)}, bf16[208,512]{1,0:T(8,128)(2,1)S(1)}, u32[]{:S(2)}, u32[]{:S(2)}) collective-permute-start(bf16[208,512]{1,0:T(8,128)(2,1)} %get-tuple-element.151), channel_id=1, source_target_pairs={{0,6},{1,7},{2,4},{3,5},{4,2},{5,3},{6,0},{7,1},{8,14},{9,15},{10,... | collective-permute-start | bytes 638984 | tf_op jit(solution)/shard_map/ppermute | solution.py:43
  137.4 2.2 %collective-permute-done.28 = bf16[296,512]{1,0:T(8,128)(2,1)S(1)} collective-permute-done((bf16[296,512]{1,0:T(8,128)(2,1)S(1)}, bf16[296,512]{1,0:T(8,128)(2,1)S(1)}, u32[]{:S(2)}, u32[]{:S(2)}) %collective-permute-start.28) | collective-permute-done | bytes 303136 | tf_op jit(solution)/shard_map/ppermute | solution.py:39
  140.1 2.7 %collective-permute-start.34 = (bf16[296,512]{1,0:T(8,128)(2,1)S(1)}, bf16[296,512]{1,0:T(8,128)(2,1)S(1)}, u32[]{:S(2)}, u32[]{:S(2)}) collective-permute-start(bf16[296,512]{1,0:T(8,128)(2,1)S(1)} %fusion.5), channel_id=1, source_target_pairs={{0,16},{8,24},{16,0},{24,8},{1,17},{9,25},{17,1},{25,9},{2,18},{10... | collective-permute-start | bytes 909320 | tf_op jit(solution)/shard_map/ppermute | solution.py:39
  142.7 7.0 %back.1 = f32[1024,512]{1,0:T(8,128)} custom-call(bf16[1024,512]{1,0:T(8,128)(2,1)} %bitcast.44, bf16[1,512]{1,0:T(2,128)(2,1)} %step.4, f32[8,512]{1,0:T(8,128)} %get-tuple-element.90.vec, bf16[3,512,1024]{2,1,0:T(8,128)(2,1)} %attn_bwd.3.g, f32[1024,512]{1,0:T(8,128)} %get-tuple-element.125.gx1, bf16[512,1536]{1,0:T(8,128)(2,1)} %get-tuple-element.126.refs_0_), custom_call_target="tpu_custom_call" | custom-call | flops 1610612736 | bytes 7340032 | tf_op jit(solution)/shard_map/back/pallas_call | solution.py:708
  151.5 3.3 %collective-permute-done.34 = bf16[296,512]{1,0:T(8,128)(2,1)S(1)} collective-permute-done((bf16[296,512]{1,0:T(8,128)(2,1)S(1)}, bf16[296,512]{1,0:T(8,128)(2,1)S(1)}, u32[]{:S(2)}, u32[]{:S(2)}) %collective-permute-start.34) | collective-permute-done | bytes 303136 | tf_op jit(solution)/shard_map/ppermute | solution.py:39
  157.2 1.9 %collective-permute-start.35 = (bf16[104,512]{1,0:T(8,128)(2,1)S(1)}, bf16[104,512]{1,0:T(8,128)(2,1)S(1)}, u32[]{:S(2)}, u32[]{:S(2)}) collective-permute-start(bf16[104,512]{1,0:T(8,128)(2,1)S(1)} %dynamic-slice_add_fusion), channel_id=1, source_target_pairs={{0,16},{8,24},{16,0},{24,8},{1,17},{9,25},{17,1},{25,9},{2,18},{10... | collective-permute-start | bytes 319496 | tf_op jit(solution)/shard_map/ppermute | solution.py:39
  159.1 5.4 %collective-permute-done.35 = bf16[104,512]{1,0:T(8,128)(2,1)S(1)} collective-permute-done((bf16[104,512]{1,0:T(8,128)(2,1)S(1)}, bf16[104,512]{1,0:T(8,128)(2,1)S(1)}, u32[]{:S(2)}, u32[]{:S(2)}) %collective-permute-start.35) | collective-permute-done | bytes 106528 | tf_op jit(solution)/shard_map/ppermute | solution.py:39
  164.5 4.2 %collective-permute-start.36 = (bf16[104,512]{1,0:T(8,128)(2,1)S(1)}, bf16[104,512]{1,0:T(8,128)(2,1)S(1)}, u32[]{:S(2)}, u32[]{:S(2)}) collective-permute-start(bf16[104,512]{1,0:T(8,128)(2,1)S(1)} %add.119.s), channel_id=1, source_target_pairs={{0,8},{8,0},{16,24},{24,16},{1,9},{9,1},{17,25},{25,17},{2,10},{10... | collective-permute-start | bytes 319496 | tf_op jit(solution)/shard_map/ppermute | solution.py:39
  (138 shorter events, 34.4 us)
Async XLA Ops:
  0.6 22.1 %collective-permute-start.9 = (bf16[64,1536]{1,0:T(8,128)(2,1)}, bf16[64,1536]{1,0:T(8,128)(2,1)S(1)}, u32[]{:S(2)}, u32[]{:S(2)}) collective-permute-start(bf16[64,1536]{1,0:T(8,128)(2,1)} %w.1), channel_id=1, source_target_pairs={{0,6},{1,7},{2,4},{3,5},{4,2},{5,3},{6,0},{7,1},{8,14},{9,15},{10,... | collective-permute-start | bytes 589832 | tf_op jit(solution)/shard_map/ppermute | solution.py:43
  4.6 18.6 %collective-permute-start.8 = (bf16[64,1536]{1,0:T(8,128)(2,1)}, bf16[64,1536]{1,0:T(8,128)(2,1)S(1)}, u32[]{:S(2)}, u32[]{:S(2)}) collective-permute-start(bf16[64,1536]{1,0:T(8,128)(2,1)} %w.1), channel_id=1, source_target_pairs={{0,4},{1,5},{2,6},{3,7},{4,0},{5,1},{6,2},{7,3},{8,12},{9,13},{10,... | collective-permute-start | bytes 589832 | tf_op jit(solution)/shard_map/ppermute | solution.py:43
  5.1 18.3 %collective-permute-start = (bf16[64,1536]{1,0:T(8,128)(2,1)}, bf16[64,1536]{1,0:T(8,128)(2,1)S(1)}, u32[]{:S(2)}, u32[]{:S(2)}) collective-permute-start(bf16[64,1536]{1,0:T(8,128)(2,1)} %w.1), channel_id=1, source_target_pairs={{0,2},{1,3},{2,0},{3,1},{4,6},{5,7},{6,4},{7,5},{8,10},{9,11},{10,... | collective-permute-start | bytes 589832 | tf_op jit(solution)/shard_map/ppermute | solution.py:43
  10.3 9.6 %collective-permute-start.2 = (bf16[16,128]{1,0:T(8,128)(2,1)}, bf16[16,128]{1,0:T(8,128)(2,1)S(1)}, u32[]{:S(2)}, u32[]{:S(2)}) collective-permute-start(bf16[16,128]{1,0:T(8,128)(2,1)} %get-tuple-element.83.refs_8_), channel_id=1, source_target_pairs={{0,4},{1,5},{2,6},{3,7},{4,0},{5,1},{6,2},{7,3},{8,12},{9,13},{10,... | collective-permute-start | bytes 12296 | tf_op jit(solution)/shard_map/ppermute | solution.py:43
  24.9 19.5 %collective-permute-start.14 = (bf16[576,512]{1,0:T(8,128)(2,1)}, bf16[576,512]{1,0:T(8,128)(2,1)S(1)}, u32[]{:S(2)}, u32[]{:S(2)}) collective-permute-start(bf16[576,512]{1,0:T(8,128)(2,1)} %get-tuple-element.102.refs_0_), channel_id=1, source_target_pairs={{0,2},{1,3},{2,0},{3,1},{4,6},{5,7},{6,4},{7,5},{8,10},{9,11},{10,... | collective-permute-start | bytes 1769480 | tf_op jit(solution)/shard_map/ppermute | solution.py:43
  25.3 19.8 %collective-permute-start.15 = (bf16[576,512]{1,0:T(8,128)(2,1)}, bf16[576,512]{1,0:T(8,128)(2,1)S(1)}, u32[]{:S(2)}, u32[]{:S(2)}) collective-permute-start(bf16[576,512]{1,0:T(8,128)(2,1)} %get-tuple-element.102.refs_0_), channel_id=1, source_target_pairs={{0,4},{1,5},{2,6},{3,7},{4,0},{5,1},{6,2},{7,3},{8,12},{9,13},{10,... | collective-permute-start | bytes 1769480 | tf_op jit(solution)/shard_map/ppermute | solution.py:43
  27.6 29.8 %collective-permute-start.16 = (bf16[576,512]{1,0:T(8,128)(2,1)}, bf16[576,512]{1,0:T(8,128)(2,1)S(1)}, u32[]{:S(2)}, u32[]{:S(2)}) collective-permute-start(bf16[576,512]{1,0:T(8,128)(2,1)} %get-tuple-element.102.refs_0_), channel_id=1, source_target_pairs={{0,1},{1,0},{2,3},{3,2},{4,5},{5,4},{6,7},{7,6},{8,9},{9,8},{10,11... | collective-permute-start | bytes 1769480 | tf_op jit(solution)/shard_map/ppermute | solution.py:43
  44.5 14.5 %collective-permute-start.17 = (bf16[576,512]{1,0:T(8,128)(2,1)S(1)}, bf16[576,512]{1,0:T(8,128)(2,1)S(1)}, u32[]{:S(2)}, u32[]{:S(2)}) collective-permute-start(bf16[576,512]{1,0:T(8,128)(2,1)S(1)} %collective-permute-done.14.refs_1_), channel_id=1, source_target_pairs={{0,1},{1,0},{2,3},{3,2},{4,5},{5,4},{6,7},{7,6},{8,9},{9,8},{10,11... | collective-permute-start | bytes 1769480 | tf_op jit(solution)/shard_map/ppermute | solution.py:43
  45.1 13.9 %collective-permute-start.18 = (bf16[576,512]{1,0:T(8,128)(2,1)S(1)}, bf16[576,512]{1,0:T(8,128)(2,1)S(1)}, u32[]{:S(2)}, u32[]{:S(2)}) collective-permute-start(bf16[576,512]{1,0:T(8,128)(2,1)S(1)} %collective-permute-done.15.refs_2_), channel_id=1, source_target_pairs={{0,1},{1,0},{2,3},{3,2},{4,5},{5,4},{6,7},{7,6},{8,9},{9,8},{10,11... | collective-permute-start | bytes 1769480 | tf_op jit(solution)/shard_map/ppermute | solution.py:43
  45.2 11.7 %collective-permute-start.20 = (bf16[288,512]{1,0:T(8,128)(2,1)S(1)}, bf16[288,512]{1,0:T(8,128)(2,1)S(1)}, u32[]{:S(2)}, u32[]{:S(2)}) collective-permute-start(bf16[288,512]{1,0:T(8,128)(2,1)S(1)} %slice.79), channel_id=1, source_target_pairs={{0,4},{1,5},{2,6},{3,7},{4,0},{5,1},{6,2},{7,3},{8,12},{9,13},{10,... | collective-permute-start | bytes 884744 | tf_op jit(solution)/shard_map/ppermute | solution.py:43
  45.5 11.4 %collective-permute-start.19 = (bf16[288,512]{1,0:T(8,128)(2,1)S(1)}, bf16[288,512]{1,0:T(8,128)(2,1)S(1)}, u32[]{:S(2)}, u32[]{:S(2)}) collective-permute-start(bf16[288,512]{1,0:T(8,128)(2,1)S(1)} %slice.78), channel_id=1, source_target_pairs={{0,2},{1,3},{2,0},{3,1},{4,6},{5,7},{6,4},{7,5},{8,10},{9,11},{10,... | collective-permute-start | bytes 884744 | tf_op jit(solution)/shard_map/ppermute | solution.py:43
  89.6 8.1 %collective-permute-start.23 = (bf16[4,592,512]{2,1,0:T(8,128)(2,1)}, bf16[4,592,512]{2,1,0:T(8,128)(2,1)}, u32[]{:S(2)}, u32[]{:S(2)}) collective-permute-start(bf16[4,592,512]{2,1,0:T(8,128)(2,1)} %get-tuple-element.110), channel_id=1, source_target_pairs={{0,1},{1,0},{2,3},{3,2},{4,5},{5,4},{6,7},{7,6},{8,9},{9,8},{10,11... | collective-permute-start | bytes 7274504 | tf_op jit(solution)/shard_map/ppermute | solution.py:43
  102.2 18.1 %collective-permute-start.25 = (bf16[2,272,512]{2,1,0:T(8,128)(2,1)}, bf16[2,272,512]{2,1,0:T(8,128)(2,1)S(1)}, u32[]{:S(2)}, u32[]{:S(2)}) collective-permute-start(bf16[2,272,512]{2,1,0:T(8,128)(2,1)} %get-tuple-element.148), channel_id=1, source_target_pairs={{0,2},{1,3},{2,0},{3,1},{4,6},{5,7},{6,4},{7,5},{8,10},{9,11},{10,... | collective-permute-start | bytes 1671176 | tf_op jit(solution)/shard_map/ppermute | solution.py:43
  102.5 17.8 %collective-permute-start.24 = (bf16[2,320,512]{2,1,0:T(8,128)(2,1)}, bf16[2,320,512]{2,1,0:T(8,128)(2,1)S(1)}, u32[]{:S(2)}, u32[]{:S(2)}) collective-permute-start(bf16[2,320,512]{2,1,0:T(8,128)(2,1)} %get-tuple-element.149), channel_id=1, source_target_pairs={{0,4},{1,5},{2,6},{3,7},{4,0},{5,1},{6,2},{7,3},{8,12},{9,13},{10,... | collective-permute-start | bytes 1966088 | tf_op jit(solution)/shard_map/ppermute | solution.py:43
  120.4 8.5 %collective-permute-start.27 = (bf16[1,272,512]{2,1,0:T(8,128)(2,1)S(1)}, bf16[1,272,512]{2,1,0:T(8,128)(2,1)}, u32[]{:S(2)}, u32[]{:S(2)}) collective-permute-start(bf16[1,272,512]{2,1,0:T(8,128)(2,1)S(1)} %get-tuple-element.157), channel_id=1, source_target_pairs={{0,4},{1,5},{2,6},{3,7},{4,0},{5,1},{6,2},{7,3},{8,12},{9,13},{10,... | collective-permute-start | bytes 835592 | tf_op jit(solution)/shard_map/ppermute | solution.py:43
  121.4 8.6 %collective-permute-start.26 = (bf16[1,320,512]{2,1,0:T(8,128)(2,1)S(1)}, bf16[1,320,512]{2,1,0:T(8,128)(2,1)S(1)}, u32[]{:S(2)}, u32[]{:S(2)}) collective-permute-start(bf16[1,320,512]{2,1,0:T(8,128)(2,1)S(1)} %get-tuple-element.154), channel_id=1, source_target_pairs={{0,2},{1,3},{2,0},{3,1},{4,6},{5,7},{6,4},{7,5},{8,10},{9,11},{10,... | collective-permute-start | bytes 983048 | tf_op jit(solution)/shard_map/ppermute | solution.py:43
  131.4 8.2 %collective-permute-start.28 = (bf16[296,512]{1,0:T(8,128)(2,1)S(1)}, bf16[296,512]{1,0:T(8,128)(2,1)S(1)}, u32[]{:S(2)}, u32[]{:S(2)}) collective-permute-start(bf16[296,512]{1,0:T(8,128)(2,1)S(1)} %fusion.3), channel_id=1, source_target_pairs={{0,8},{8,0},{16,24},{24,16},{1,9},{9,1},{17,25},{25,17},{2,10},{10... | collective-permute-start | bytes 909320 | tf_op jit(solution)/shard_map/ppermute | solution.py:39
  134.0 15.8 %collective-permute-start.30 = (bf16[208,512]{1,0:T(8,128)(2,1)}, bf16[208,512]{1,0:T(8,128)(2,1)S(1)}, u32[]{:S(2)}, u32[]{:S(2)}) collective-permute-start(bf16[208,512]{1,0:T(8,128)(2,1)} %get-tuple-element.151), channel_id=1, source_target_pairs={{0,6},{1,7},{2,4},{3,5},{4,2},{5,3},{6,0},{7,1},{8,14},{9,15},{10,... | collective-permute-start | bytes 638984 | tf_op jit(solution)/shard_map/ppermute | solution.py:43
  136.4 13.3 %collective-permute-start.31 = (bf16[208,512]{1,0:T(8,128)(2,1)S(1)}, bf16[208,512]{1,0:T(8,128)(2,1)S(1)}, u32[]{:S(2)}, u32[]{:S(2)}) collective-permute-start(bf16[208,512]{1,0:T(8,128)(2,1)S(1)} %get-tuple-element.152), channel_id=1, source_target_pairs={{0,4},{1,5},{2,6},{3,7},{4,0},{5,1},{6,2},{7,3},{8,12},{9,13},{10,... | collective-permute-start | bytes 638984 | tf_op jit(solution)/shard_map/ppermute | solution.py:43
  136.9 12.8 %collective-permute-start.32 = (bf16[208,512]{1,0:T(8,128)(2,1)S(1)}, bf16[208,512]{1,0:T(8,128)(2,1)S(1)}, u32[]{:S(2)}, u32[]{:S(2)}) collective-permute-start(bf16[208,512]{1,0:T(8,128)(2,1)S(1)} %get-tuple-element.153), channel_id=1, source_target_pairs={{0,2},{1,3},{2,0},{3,1},{4,6},{5,7},{6,4},{7,5},{8,10},{9,11},{10,... | collective-permute-start | bytes 638984 | tf_op jit(solution)/shard_map/ppermute | solution.py:43
  140.1 14.8 %collective-permute-start.34 = (bf16[296,512]{1,0:T(8,128)(2,1)S(1)}, bf16[296,512]{1,0:T(8,128)(2,1)S(1)}, u32[]{:S(2)}, u32[]{:S(2)}) collective-permute-start(bf16[296,512]{1,0:T(8,128)(2,1)S(1)} %fusion.5), channel_id=1, source_target_pairs={{0,16},{8,24},{16,0},{24,8},{1,17},{9,25},{17,1},{25,9},{2,18},{10... | collective-permute-start | bytes 909320 | tf_op jit(solution)/shard_map/ppermute | solution.py:39
  149.9 7.2 %collective-permute-start.33 = (bf16[104,512]{1,0:T(8,128)(2,1)S(1)}, bf16[104,512]{1,0:T(8,128)(2,1)S(1)}, u32[]{:S(2)}, u32[]{:S(2)}) collective-permute-start(bf16[104,512]{1,0:T(8,128)(2,1)S(1)} %constant_dynamic-slice_fusion), channel_id=1, source_target_pairs={{0,8},{8,0},{16,24},{24,16},{1,9},{9,1},{17,25},{25,17},{2,10},{10... | collective-permute-start | bytes 319496 | tf_op jit(solution)/shard_map/ppermute | solution.py:39
  155.0 13.8 %collective-permute-start.37 = (bf16[296,512]{1,0:T(8,128)(2,1)S(1)}, bf16[296,512]{1,0:T(8,128)(2,1)S(1)}, u32[]{:S(2)}, u32[]{:S(2)}) collective-permute-start(bf16[296,512]{1,0:T(8,128)(2,1)S(1)} %add.117.s), channel_id=1, source_target_pairs={{0,8},{8,0},{16,24},{24,16},{1,9},{9,1},{17,25},{25,17},{2,10},{10... | collective-permute-start | bytes 909320 | tf_op jit(solution)/shard_map/ppermute | solution.py:39
  157.2 7.2 %collective-permute-start.35 = (bf16[104,512]{1,0:T(8,128)(2,1)S(1)}, bf16[104,512]{1,0:T(8,128)(2,1)S(1)}, u32[]{:S(2)}, u32[]{:S(2)}) collective-permute-start(bf16[104,512]{1,0:T(8,128)(2,1)S(1)} %dynamic-slice_add_fusion), channel_id=1, source_target_pairs={{0,16},{8,24},{16,0},{24,8},{1,17},{9,25},{17,1},{25,9},{2,18},{10... | collective-permute-start | bytes 319496 | tf_op jit(solution)/shard_map/ppermute | solution.py:39
  (42 other events, 227.8 us)

commit v9 on v7

--- a/solution.py
+++ b/solution.py
@@ -122,7 +122,7 @@
     def spot(v):
         w_ = v.shape[1]
         if w_ >= LANES:
-            return [v[:, q * LANES : (q + 1) * LANES] for q in range(w_ // LANES)]
+            return [v[q : q + 1, :] for q in range(v.shape[0])]
         t = LANES // w_
         lane = lax.broadcasted_iota(jnp.int32, (1, LANES), 1)
         return [jnp.where(lane // w_ == me[0] % t, jnp.concatenate([v] * t, axis=1), jnp.zeros((1, LANES), f32))]
@@ -143,7 +143,8 @@
 def pack_first(me, w, vecs, upb):
     r, W = w.shape
     gw = W // 3 // GROUPS
-    args = [w, upb[None]] + [v[None] for v in vecs]
+    lanes = lambda v: v.reshape(-1, min(LANES, v.shape[0]))
+    args = [w] + [lanes(v) for v in [upb] + vecs]
     outs = [S((3 * r + (VROWS if g == 0 else 0), gw), bf16) for g in range(GROUPS)]
     return pl.pallas_call(
         pack_first_body,
@@ -370,7 +371,7 @@
     return pl.CostEstimate(flops=int(flops), bytes_accessed=int(nbytes), transcendentals=int(tr))
 
 
-def front(me, nx, pieces, n, FF, cw=256):
+def front(me, nx, pieces, n, FF, cw=512):
     T, D = nx.shape
     scale = 1.0 / math.sqrt(D // HEADS)
     meta = tuple((k, r0) for k, r0, _ in pieces)
@@ -390,10 +391,12 @@
     )(me, nx, *[a for _, _, a in pieces])
 
 
-def attn_fwd_body(HD, bi, CR, ln, k, qt, vt, *refs):
-    et, mixed, mixedt, mixedf, linv, scr, ka = refs[-7:]
+def attn_fwd_body(HD, bi, CR, p0, ln, k, qt, vt, *refs):
+    et, mixed, mixedt, mixedf, linv, scr, ka, eb, esem = refs[-9:]
     T, PW = k.shape
     n = ln[0]
+    p = pl.program_id(0)
+    last = p == pl.num_programs(0) - 1
     rid = lax.broadcasted_iota(jnp.int32, (PW, bi), 0)
     lane = lax.broadcasted_iota(jnp.int32, (T, PW), 1)
     rows = lax.broadcasted_iota(jnp.int32, (T, PW), 0)
@@ -420,6 +423,15 @@
     for t, (b, h) in enumerate(tasks):
         sl = slice(b * bi, (b + 1) * bi)
         more = t + 1 < len(tasks)
+        put = pltpu.make_async_copy(eb.at[t % 2], et.at[2 * (p0 + p) + h, :, pl.ds(b * bi, bi)], esem.at[t % 2])
+        if t < 2:
+
+            @pl.when(p > 0)
+            def _():
+                put.wait()
+
+        else:
+            put.wait()
         if more:
             q = query(t + 1)
         nxt = []
@@ -427,8 +439,9 @@
             cs = slice(c * CR, (c + 1) * CR)
             if more:
                 nxt.append(score(t + 1, c, q))
-            et[h, cs, sl] = jnp.exp(scr[t % 2, cs, :] - m).astype(bf16)
-        o = dot(va[h], et[h, :, sl])
+            eb[t % 2, cs, :] = jnp.exp(scr[t % 2, cs, :] - m).astype(bf16)
+        put.start()
+        o = dot(va[h], eb[t % 2])
         if more:
             m = functools.reduce(jnp.maximum, nxt)
         inv = 1.0 / o[HD : HD + 1, :]
@@ -443,6 +456,11 @@
             mixedt[:, sl] = mt
             mixed[sl, :] = mt.T
 
+    @pl.when(last)
+    def _():
+        for q in range(2):
+            pltpu.make_async_copy(eb.at[q], et.at[0, :, pl.ds(0, bi)], esem.at[q]).wait()
+
 
 def attn_fwd(ln, kv, qkvt, p0, cnt, prev):
     _, T, D = kv.shape
@@ -452,12 +470,12 @@
     bi = min(512, T)
     prev = list(prev)
     return pl.pallas_call(
-        functools.partial(attn_fwd_body, HD, bi, min(256, T)),
+        functools.partial(attn_fwd_body, HD, bi, min(256, T), p0),
         grid_spec=pltpu.PrefetchScalarGridSpec(
             num_scalar_prefetch=1, grid=(cnt,),
             in_specs=[pl.BlockSpec((None, T, PW), lambda p, r: (0, 0, p0 + p)), pl.BlockSpec((None, PW, T), lambda p, r: (0, p0 + p, 0)), pl.BlockSpec((None, PW, T), lambda p, r: (2, p0 + p, 0))] + [ANY] * len(prev),
-            out_specs=[pl.BlockSpec((2, T, T), lambda p, r: (p0 + p, 0, 0)), pl.BlockSpec((T, PW), lambda p, r: (0, p0 + p)), pl.BlockSpec((PW, T), lambda p, r: (p0 + p, 0)), pl.BlockSpec((PW, T), lambda p, r: (p0 + p, 0)), pl.BlockSpec((None, 8, T), lambda p, r: (p0 + p, 0, 0))],
-            scratch_shapes=[pltpu.VMEM((2, T, bi), f32), pltpu.VMEM((T, 2 * PW), bf16)]),
+            out_specs=[ANY, pl.BlockSpec((T, PW), lambda p, r: (0, p0 + p)), pl.BlockSpec((PW, T), lambda p, r: (p0 + p, 0)), pl.BlockSpec((PW, T), lambda p, r: (p0 + p, 0)), pl.BlockSpec((None, 8, T), lambda p, r: (p0 + p, 0, 0))],
+            scratch_shapes=[pltpu.VMEM((2, T, bi), f32), pltpu.VMEM((T, 2 * PW), bf16), pltpu.VMEM((2, T, bi), bf16), pltpu.SemaphoreType.DMA((2,))]),
         out_shape=[S((HEADS, T, T), bf16), S((T, D), bf16), S((D, T), bf16), S((D, T), f32), S((NP, 8, T), f32)],
         input_output_aliases={4 + i: i for i in range(len(prev))},
         compiler_params=cp(), name="attn_fwd", cost_estimate=cost(cnt * 2 * 8 * T * T * 128, cnt * 2 * T * T * 2, cnt * 2 * T * T),

time: 167 us -> 164 us (0.982)
  transfers between devices with their start and end apart: 31 -> 31, of which waited for: 12 -> 12; matrix products, arithmetic and copies ran while one was open for 2% -> 2% of each run, Pallas kernels for 44% -> 43%
where the time goes in v9:
time: 164 us; the launch traced here: 163 us
  Pallas kernels  101 us (62%)
  starting transfers between devices  31.9 us (19%)
  waiting for transfers between devices  20.5 us (12%)
  other arithmetic  7.54 us (5%)
  between operations  1.72 us (1%)
    pallas_call x1, Pallas kernels, ffn(): pl.pallas_call(functools.partial(ffn_body, n, meta, min(1024, FF)), grid_...  26.5 us
    pallas_call x2, Pallas kernels, attn_bwd(): pl.pallas_call(functools.partial(attn_bwd_body, HD, 1.0 / math.sqrt(HD),...  23.9 us
    pallas_call x2, Pallas kernels, attn_fwd(): pl.pallas_call(functools.partial(attn_fwd_body, HD, bi, min(256, T), p0),...  19.3 us
    ppermute x25, starting transfers between devices, swap(): return lax.ppermute(x, 'shard', xor_perm(lax.axis_size('shard'), k))  19.1 us
    ppermute x6, starting transfers between devices, rep_perm(): return lax.ppermute(x, 'rep', xor_perm(lax.axis_size('rep'), b))  12.8 us
    ppermute x6, waiting for transfers between devices, rep_perm(): return lax.ppermute(x, 'rep', xor_perm(lax.axis_size('rep'), b))  12.5 us
    ppermute x25, waiting for transfers between devices, swap(): return lax.ppermute(x, 'shard', xor_perm(lax.axis_size('shard'), k))  7.96 us
    pallas_call x1, Pallas kernels, front(): pl.pallas_call(functools.partial(front_body, scale, n, meta), grid_spec=p...  7.13 us
  transfers between devices with their start and end apart: 31, of which 12 were waited for; matrix products, arithmetic and copies ran while one was open for 2% of the time, Pallas kernels for 43%

profile of v9, /device:TPU:0, one launch (start us, length us, event | category | flops | bytes accessed | tf_op | source)
XLA Modules:
  0.0 163.4 jit_solution(3087045033546766215)
XLA Ops:
  0.7 1.8 %pack_first.1.refs_0_ = bf16[208,512]{1,0:T(8,128)(2,1)} custom-call(s32[1]{0:T(128)} %bitcast.me, bf16[64,1536]{1,0:T(8,128)(2,1)} %w.3, bf16[2,128]{1,0:T(2,128)(2,1)} %bitcast.47, bf16[1,64]{1,0:T(2,128)(2,1)} %bitcast.39, bf16[1,64]{1,0:T(2,128)(2,1)} %bitcast.41, bf16[1,64]{1,0:T(2,128)(2,1)} %bitcast.48, bf16[1,64]{1,0:T(2,128)(2,1)} %bitcast.49, ...), custom_call_target="tpu_custom_call" | custom-call | bytes 393216 | tf_op jit(solution)/shard_map/pack_first/pallas_call | solution.py:149
  2.4 2.9 %collective-permute-start = (bf16[208,512]{1,0:T(8,128)(2,1)}, bf16[208,512]{1,0:T(8,128)(2,1)S(1)}, u32[]{:S(2)}, u32[]{:S(2)}) collective-permute-start(bf16[208,512]{1,0:T(8,128)(2,1)} %pack_first.1.refs_0_), channel_id=1, source_target_pairs={{0,2},{1,3},{2,0},{3,1},{4,6},{5,7},{6,4},{7,5},{8,10},{9,11},{10,... | collective-permute-start | bytes 638984 | tf_op jit(solution)/shard_map/ppermute | solution.py:43
  6.9 1.9 %pack_rest.1.refs_0_ = bf16[576,512]{1,0:T(8,128)(2,1)} custom-call(bf16[64,512]{1,0:T(8,128)(2,1)} %wo.1, bf16[64,2048]{1,0:T(8,128)(2,1)} %wu.1, bf16[256,512]{1,0:T(8,128)(2,1)} %wd.1), custom_call_target="tpu_custom_call" | custom-call | bytes 524288 | tf_op jit(solution)/shard_map/pack_rest/pallas_call | solution.py:167
  8.8 4.2 %start.1 = (f32[1024,512]{1,0:T(8,128)}, bf16[512,1024]{1,0:T(8,128)(2,1)}) custom-call(bf16[1024,512]{1,0:T(8,128)(2,1)} %bitcast.43, bf16[1,512]{1,0:T(2,128)(2,1)} %step.4), custom_call_target="tpu_custom_call" | custom-call | flops 10485760 | bytes 4194304 | tf_op jit(solution)/shard_map/start/pallas_call | solution.py:309
  13.6 3.2 %collective-permute-done.1.refs_2_ = bf16[208,512]{1,0:T(8,128)(2,1)S(1)} collective-permute-done((bf16[208,512]{1,0:T(8,128)(2,1)}, bf16[208,512]{1,0:T(8,128)(2,1)S(1)}, u32[]{:S(2)}, u32[]{:S(2)}) %collective-permute-start.1) | collective-permute-done | bytes 213024 | tf_op jit(solution)/shard_map/ppermute | solution.py:43
  21.5 7.1 %front.1 = (bf16[2,1024,512]{2,1,0:T(8,128)(2,1)}, bf16[3,512,1024]{2,1,0:T(8,128)(2,1)}, bf16[512,1536]{1,0:T(8,128)(2,1)}, f32[8,512]{1,0:T(8,128)}, f32[1,2048]{1,0:T(1,128)}) custom-call(s32[1]{0:T(128)} %bitcast.me, f32[1024,512]{1,0:T(8,128)} %get-tuple-element.76.nx, bf16[208,512]{1,0:T(8,128)(2,1)} %pack_first.1.refs_0_, ...), custom_call_target="tpu_custom_call" | custom-call | flops 1610612736 | bytes 6291456 | tf_op jit(solution)/shard_map/front/pallas_call | solution.py:382
  28.6 9.7 %attn_fwd.2 = (bf16[8,1024,1024]{2,1,0:T(8,128)(2,1)}, bf16[1024,512]{1,0:T(8,128)(2,1)}, bf16[512,1024]{1,0:T(8,128)(2,1)}, f32[512,1024]{1,0:T(8,128)}, f32[4,8,1024]{2,1,0:T(8,128)}) custom-call(s32[1]{0:T(128)S(6)} %copy.44.ln, bf16[2,1024,512]{2,1,0:T(8,128)(2,1)} %get-tuple-element.83.k.v, bf16[3,512,1024]{2,1,0:T(8,128)(2,1)} %get-tuple-element.84.qt.vt.kt, ...), custom_call_target="tpu_custom_call" | custom-call | flops 4294967296 | bytes 8388608 | tf_op jit(solution)/shard_map/attn_fwd/pallas_call | solution.py:472
  41.1 9.6 %attn_fwd.3 = (bf16[8,1024,1024]{2,1,0:T(8,128)(2,1)}, bf16[1024,512]{1,0:T(8,128)(2,1)}, bf16[512,1024]{1,0:T(8,128)(2,1)}, f32[512,1024]{1,0:T(8,128)}, f32[4,8,1024]{2,1,0:T(8,128)}) custom-call(s32[1]{0:T(128)S(6)} %copy.44.ln, ...), custom_call_target="tpu_custom_call", output_to_operand_aliasing={{0}: (4, {}), {1}: (5, {}), {2}: (6, {}), {3}: (7, {}), {4}... | custom-call | flops 4294967296 | bytes 8388608 | tf_op jit(solution)/shard_map/attn_fwd/pallas_call | solution.py:472
  53.9 26.5 %ffn.1 = (bf16[1024,512]{1,0:T(8,128)(2,1)}, f32[1024,512]{1,0:T(8,128)}, bf16[512,1024]{1,0:T(8,128)(2,1)}, bf16[4,592,512]{2,1,0:T(8,128)(2,1)}, bf16[4,592,512]{2,1,0:T(8,128)(2,1)}) custom-call(s32[1]{0:T(128)S(6)} %copy.44.ln, s32[1]{0:T(128)} %bitcast.me, bf16[1024,512]{1,0:T(8,128)(2,1)} %bitcast.44, bf16[1,512]{1,0:T(2,128)(2,1)} %step.4, ...), custom_call_target="tpu_custom_call" | custom-call | flops 14495514624 | bytes 8388608 | tf_op jit(solution)/shard_map/ffn/pallas_call | solution.py:628
  80.6 7.8 %attn_bwd.2.refs_0_ = bf16[3,512,1024]{2,1,0:T(8,128)(2,1)} custom-call(bf16[2,1024,512]{2,1,0:T(8,128)(2,1)} %get-tuple-element.83.k.v, bf16[3,512,1024]{2,1,0:T(8,128)(2,1)} %get-tuple-element.84.qt.vt.kt, bf16[3,512,1024]{2,1,0:T(8,128)(2,1)} %get-tuple-element.84.qt.vt.kt, bf16[512,1024]{1,0:T(8,128)(2,1)} %get-tuple-element.105.gt, ...), custom_call_target="tpu_custom_call" | custom-call | flops 4294967296 | bytes 4194304 | tf_op jit(solution)/shard_map/attn_bwd/pallas_call | solution.py:672
  88.5 2.2 %slice_add_fusion.2 = (bf16[2,272,512]{2,1,0:T(8,128)(2,1)S(1)}, bf16[2,272,512]{2,1,0:T(8,128)(2,1)}) fusion(bf16[4,592,512]{2,1,0:T(8,128)(2,1)} %collective-permute-done.16, bf16[4,592,512]{2,1,0:T(8,128)(2,1)S(1)} %copy-done.3), kind=kLoop, calls=%fused_computation.6 | loop fusion | flops 557056 | bytes 3342336 | tf_op jit(solution)/shard_map/add | solution.py:82
  90.7 2.2 %slice_add_fusion = (bf16[2,320,512]{2,1,0:T(8,128)(2,1)}, bf16[2,320,512]{2,1,0:T(8,128)(2,1)S(1)}) fusion(bf16[4,592,512]{2,1,0:T(8,128)(2,1)} %collective-permute-done.16, bf16[4,592,512]{2,1,0:T(8,128)(2,1)S(1)} %copy-done.3), kind=kLoop, calls=%fused_computation.4 | loop fusion | flops 655360 | bytes 3932160 | tf_op jit(solution)/shard_map/add | solution.py:82
  95.0 16.0 %attn_bwd.3.g = bf16[3,512,1024]{2,1,0:T(8,128)(2,1)} custom-call(bf16[2,1024,512]{2,1,0:T(8,128)(2,1)} %get-tuple-element.83.k.v, bf16[3,512,1024]{2,1,0:T(8,128)(2,1)} %get-tuple-element.84.qt.vt.kt, bf16[3,512,1024]{2,1,0:T(8,128)(2,1)} %get-tuple-element.84.qt.vt.kt, bf16[512,1024]{1,0:T(8,128)(2,1)} %get-tuple-element.105.gt, ...), custom_call_target="tpu_custom_call", output_to_operand_aliasing={{}: (7, {})} | custom-call | flops 12884901888 | bytes 12582912 | tf_op jit(solution)/shard_map/attn_bwd/pallas_call | solution.py:672
  113.6 5.6 %wqkv.1 = (bf16[4,208,512]{2,1,0:T(8,128)(2,1)}, bf16[4,208,512]{2,1,0:T(8,128)(2,1)}) custom-call(s32[1]{0:T(128)} %bitcast.me, bf16[512,1024]{1,0:T(8,128)(2,1)} %get-tuple-element.108.xht, bf16[3,512,1024]{2,1,0:T(8,128)(2,1)} %attn_bwd.3.g), custom_call_target="tpu_custom_call" | custom-call | flops 1610612736 | bytes 5242880 | tf_op jit(solution)/shard_map/wqkv/pallas_call | solution.py:709
  122.7 1.6 %collective-permute-start.21 = (bf16[296,512]{1,0:T(8,128)(2,1)S(1)}, bf16[296,512]{1,0:T(8,128)(2,1)S(1)}, u32[]{:S(2)}, u32[]{:S(2)}) collective-permute-start(bf16[296,512]{1,0:T(8,128)(2,1)S(1)} %fusion.3), channel_id=1, source_target_pairs={{0,8},{8,0},{16,24},{24,16},{1,9},{9,1},{17,25},{25,17},{2,10},{10... | collective-permute-start | bytes 909320 | tf_op jit(solution)/shard_map/ppermute | solution.py:39
  125.1 2.0 %collective-permute-start.23 = (bf16[208,512]{1,0:T(8,128)(2,1)}, bf16[208,512]{1,0:T(8,128)(2,1)S(1)}, u32[]{:S(2)}, u32[]{:S(2)}) collective-permute-start(bf16[208,512]{1,0:T(8,128)(2,1)} %get-tuple-element.141), channel_id=1, source_target_pairs={{0,6},{1,7},{2,4},{3,5},{4,2},{5,3},{6,0},{7,1},{8,14},{9,15},{10,... | collective-permute-start | bytes 638984 | tf_op jit(solution)/shard_map/ppermute | solution.py:43
  128.6 1.9 %collective-permute-done.21 = bf16[296,512]{1,0:T(8,128)(2,1)S(1)} collective-permute-done((bf16[296,512]{1,0:T(8,128)(2,1)S(1)}, bf16[296,512]{1,0:T(8,128)(2,1)S(1)}, u32[]{:S(2)}, u32[]{:S(2)}) %collective-permute-start.21) | collective-permute-done | bytes 303136 | tf_op jit(solution)/shard_map/ppermute | solution.py:39
  130.9 2.7 %collective-permute-start.27 = (bf16[296,512]{1,0:T(8,128)(2,1)S(1)}, bf16[296,512]{1,0:T(8,128)(2,1)S(1)}, u32[]{:S(2)}, u32[]{:S(2)}) collective-permute-start(bf16[296,512]{1,0:T(8,128)(2,1)S(1)} %fusion.5), channel_id=1, source_target_pairs={{0,16},{8,24},{16,0},{24,8},{1,17},{9,25},{17,1},{25,9},{2,18},{10... | collective-permute-start | bytes 909320 | tf_op jit(solution)/shard_map/ppermute | solution.py:39
  133.6 7.0 %back.1 = f32[1024,512]{1,0:T(8,128)} custom-call(bf16[1024,512]{1,0:T(8,128)(2,1)} %bitcast.45, bf16[1,512]{1,0:T(2,128)(2,1)} %step.4, f32[8,512]{1,0:T(8,128)} %get-tuple-element.81.vec, bf16[3,512,1024]{2,1,0:T(8,128)(2,1)} %attn_bwd.3.g, f32[1024,512]{1,0:T(8,128)} %get-tuple-element.115.gx1, bf16[512,1536]{1,0:T(8,128)(2,1)} %get-tuple-element.116.refs_0_), custom_call_target="tpu_custom_call" | custom-call | flops 1610612736 | bytes 7340032 | tf_op jit(solution)/shard_map/back/pallas_call | solution.py:736
  142.4 2.9 %collective-permute-done.27 = bf16[296,512]{1,0:T(8,128)(2,1)S(1)} collective-permute-done((bf16[296,512]{1,0:T(8,128)(2,1)S(1)}, bf16[296,512]{1,0:T(8,128)(2,1)S(1)}, u32[]{:S(2)}, u32[]{:S(2)}) %collective-permute-start.27) | collective-permute-done | bytes 303136 | tf_op jit(solution)/shard_map/ppermute | solution.py:39
  147.6 2.0 %collective-permute-start.28 = (bf16[104,512]{1,0:T(8,128)(2,1)S(1)}, bf16[104,512]{1,0:T(8,128)(2,1)S(1)}, u32[]{:S(2)}, u32[]{:S(2)}) collective-permute-start(bf16[104,512]{1,0:T(8,128)(2,1)S(1)} %dynamic-slice_add_fusion), channel_id=1, source_target_pairs={{0,16},{8,24},{16,0},{24,8},{1,17},{9,25},{17,1},{25,9},{2,18},{10... | collective-permute-start | bytes 319496 | tf_op jit(solution)/shard_map/ppermute | solution.py:39
  149.6 5.4 %collective-permute-done.28 = bf16[104,512]{1,0:T(8,128)(2,1)S(1)} collective-permute-done((bf16[104,512]{1,0:T(8,128)(2,1)S(1)}, bf16[104,512]{1,0:T(8,128)(2,1)S(1)}, u32[]{:S(2)}, u32[]{:S(2)}) %collective-permute-start.28) | collective-permute-done | bytes 106528 | tf_op jit(solution)/shard_map/ppermute | solution.py:39
  155.0 4.2 %collective-permute-start.29 = (bf16[104,512]{1,0:T(8,128)(2,1)S(1)}, bf16[104,512]{1,0:T(8,128)(2,1)S(1)}, u32[]{:S(2)}, u32[]{:S(2)}) collective-permute-start(bf16[104,512]{1,0:T(8,128)(2,1)S(1)} %add.119.s), channel_id=1, source_target_pairs={{0,8},{8,0},{16,24},{24,16},{1,9},{9,1},{17,25},{25,17},{2,10},{10... | collective-permute-start | bytes 319496 | tf_op jit(solution)/shard_map/ppermute | solution.py:39
  159.2 1.7 %finish_rest.1 = (f32[256,512]{1,0:T(8,128)}, f32[64,2048]{1,0:T(8,128)}, f32[64,512]{1,0:T(8,128)}, f32[1,256]{1,0:T(1,128)}, f32[1,64]{1,0:T(1,128)}, /*index=...) custom-call(s32[2]{0:T(128)S(1)} %pad_add_fusion.ids, bf16[296,512]{1,0:T(8,128)(2,1)S(1)} %add.117.s, ...), custom_call_target="tpu_custom_call" | custom-call | bytes 1212416 | tf_op jit(solution)/shard_map/finish_rest/pallas_call | solution.py:225
  (110 shorter events, 29.5 us)
Async XLA Ops:
  2.4 10.6 %collective-permute-start = (bf16[208,512]{1,0:T(8,128)(2,1)}, bf16[208,512]{1,0:T(8,128)(2,1)S(1)}, u32[]{:S(2)}, u32[]{:S(2)}) collective-permute-start(bf16[208,512]{1,0:T(8,128)(2,1)} %pack_first.1.refs_0_), channel_id=1, source_target_pairs={{0,2},{1,3},{2,0},{3,1},{4,6},{5,7},{6,4},{7,5},{8,10},{9,11},{10,... | collective-permute-start | bytes 638984 | tf_op jit(solution)/shard_map/ppermute | solution.py:43
  5.4 11.5 %collective-permute-start.1 = (bf16[208,512]{1,0:T(8,128)(2,1)}, bf16[208,512]{1,0:T(8,128)(2,1)S(1)}, u32[]{:S(2)}, u32[]{:S(2)}) collective-permute-start(bf16[208,512]{1,0:T(8,128)(2,1)} %pack_first.1.refs_0_), channel_id=1, source_target_pairs={{0,4},{1,5},{2,6},{3,7},{4,0},{5,1},{6,2},{7,3},{8,12},{9,13},{10,... | collective-permute-start | bytes 638984 | tf_op jit(solution)/shard_map/ppermute | solution.py:43
  6.9 10.0 %collective-permute-start.2 = (bf16[208,512]{1,0:T(8,128)(2,1)}, bf16[208,512]{1,0:T(8,128)(2,1)S(1)}, u32[]{:S(2)}, u32[]{:S(2)}) collective-permute-start(bf16[208,512]{1,0:T(8,128)(2,1)} %pack_first.1.refs_0_), channel_id=1, source_target_pairs={{0,6},{1,7},{2,4},{3,5},{4,2},{5,3},{6,0},{7,1},{8,14},{9,15},{10,... | collective-permute-start | bytes 638984 | tf_op jit(solution)/shard_map/ppermute | solution.py:43
  6.9 10.5 %collective-permute-start.3 = (bf16[208,512]{1,0:T(8,128)(2,1)}, bf16[208,512]{1,0:T(8,128)(2,1)S(1)}, u32[]{:S(2)}, u32[]{:S(2)}) collective-permute-start(bf16[208,512]{1,0:T(8,128)(2,1)} %pack_first.1.refs_0_), channel_id=1, source_target_pairs={{0,1},{1,0},{2,3},{3,2},{4,5},{5,4},{6,7},{7,6},{8,9},{9,8},{10,11... | collective-permute-start | bytes 638984 | tf_op jit(solution)/shard_map/ppermute | solution.py:43
  18.6 19.7 %collective-permute-start.7 = (bf16[576,512]{1,0:T(8,128)(2,1)}, bf16[576,512]{1,0:T(8,128)(2,1)S(1)}, u32[]{:S(2)}, u32[]{:S(2)}) collective-permute-start(bf16[576,512]{1,0:T(8,128)(2,1)} %pack_rest.1.refs_0_), channel_id=1, source_target_pairs={{0,2},{1,3},{2,0},{3,1},{4,6},{5,7},{6,4},{7,5},{8,10},{9,11},{10,... | collective-permute-start | bytes 1769480 | tf_op jit(solution)/shard_map/ppermute | solution.py:43
  19.6 19.4 %collective-permute-start.8 = (bf16[576,512]{1,0:T(8,128)(2,1)}, bf16[576,512]{1,0:T(8,128)(2,1)S(1)}, u32[]{:S(2)}, u32[]{:S(2)}) collective-permute-start(bf16[576,512]{1,0:T(8,128)(2,1)} %pack_rest.1.refs_0_), channel_id=1, source_target_pairs={{0,4},{1,5},{2,6},{3,7},{4,0},{5,1},{6,2},{7,3},{8,12},{9,13},{10,... | collective-permute-start | bytes 1769480 | tf_op jit(solution)/shard_map/ppermute | solution.py:43
  21.3 30.0 %collective-permute-start.9 = (bf16[576,512]{1,0:T(8,128)(2,1)}, bf16[576,512]{1,0:T(8,128)(2,1)S(1)}, u32[]{:S(2)}, u32[]{:S(2)}) collective-permute-start(bf16[576,512]{1,0:T(8,128)(2,1)} %pack_rest.1.refs_0_), channel_id=1, source_target_pairs={{0,1},{1,0},{2,3},{3,2},{4,5},{5,4},{6,7},{7,6},{8,9},{9,8},{10,11... | collective-permute-start | bytes 1769480 | tf_op jit(solution)/shard_map/ppermute | solution.py:43
  38.4 14.4 %collective-permute-start.10 = (bf16[576,512]{1,0:T(8,128)(2,1)S(1)}, bf16[576,512]{1,0:T(8,128)(2,1)S(1)}, u32[]{:S(2)}, u32[]{:S(2)}) collective-permute-start(bf16[576,512]{1,0:T(8,128)(2,1)S(1)} %collective-permute-done.7.refs_1_), channel_id=1, source_target_pairs={{0,1},{1,0},{2,3},{3,2},{4,5},{5,4},{6,7},{7,6},{8,9},{9,8},{10,11... | collective-permute-start | bytes 1769480 | tf_op jit(solution)/shard_map/ppermute | solution.py:43
  39.0 13.8 %collective-permute-start.11 = (bf16[576,512]{1,0:T(8,128)(2,1)S(1)}, bf16[576,512]{1,0:T(8,128)(2,1)S(1)}, u32[]{:S(2)}, u32[]{:S(2)}) collective-permute-start(bf16[576,512]{1,0:T(8,128)(2,1)S(1)} %collective-permute-done.8.refs_2_), channel_id=1, source_target_pairs={{0,1},{1,0},{2,3},{3,2},{4,5},{5,4},{6,7},{7,6},{8,9},{9,8},{10,11... | collective-permute-start | bytes 1769480 | tf_op jit(solution)/shard_map/ppermute | solution.py:43
  39.1 11.6 %collective-permute-start.13 = (bf16[288,512]{1,0:T(8,128)(2,1)S(1)}, bf16[288,512]{1,0:T(8,128)(2,1)S(1)}, u32[]{:S(2)}, u32[]{:S(2)}) collective-permute-start(bf16[288,512]{1,0:T(8,128)(2,1)S(1)} %slice.79), channel_id=1, source_target_pairs={{0,4},{1,5},{2,6},{3,7},{4,0},{5,1},{6,2},{7,3},{8,12},{9,13},{10,... | collective-permute-start | bytes 884744 | tf_op jit(solution)/shard_map/ppermute | solution.py:43
  40.0 10.8 %collective-permute-start.12 = (bf16[288,512]{1,0:T(8,128)(2,1)S(1)}, bf16[288,512]{1,0:T(8,128)(2,1)S(1)}, u32[]{:S(2)}, u32[]{:S(2)}) collective-permute-start(bf16[288,512]{1,0:T(8,128)(2,1)S(1)} %slice.78), channel_id=1, source_target_pairs={{0,2},{1,3},{2,0},{3,1},{4,6},{5,7},{6,4},{7,5},{8,10},{9,11},{10,... | collective-permute-start | bytes 884744 | tf_op jit(solution)/shard_map/ppermute | solution.py:43
  80.4 8.0 %collective-permute-start.16 = (bf16[4,592,512]{2,1,0:T(8,128)(2,1)}, bf16[4,592,512]{2,1,0:T(8,128)(2,1)}, u32[]{:S(2)}, u32[]{:S(2)}) collective-permute-start(bf16[4,592,512]{2,1,0:T(8,128)(2,1)} %get-tuple-element.100), channel_id=1, source_target_pairs={{0,1},{1,0},{2,3},{3,2},{4,5},{5,4},{6,7},{7,6},{8,9},{9,8},{10,11... | collective-permute-start | bytes 7274504 | tf_op jit(solution)/shard_map/ppermute | solution.py:43
  92.9 18.1 %collective-permute-start.18 = (bf16[2,272,512]{2,1,0:T(8,128)(2,1)}, bf16[2,272,512]{2,1,0:T(8,128)(2,1)S(1)}, u32[]{:S(2)}, u32[]{:S(2)}) collective-permute-start(bf16[2,272,512]{2,1,0:T(8,128)(2,1)} %get-tuple-element.138), channel_id=1, source_target_pairs={{0,2},{1,3},{2,0},{3,1},{4,6},{5,7},{6,4},{7,5},{8,10},{9,11},{10,... | collective-permute-start | bytes 1671176 | tf_op jit(solution)/shard_map/ppermute | solution.py:43
  93.9 17.1 %collective-permute-start.17 = (bf16[2,320,512]{2,1,0:T(8,128)(2,1)}, bf16[2,320,512]{2,1,0:T(8,128)(2,1)S(1)}, u32[]{:S(2)}, u32[]{:S(2)}) collective-permute-start(bf16[2,320,512]{2,1,0:T(8,128)(2,1)} %get-tuple-element.139), channel_id=1, source_target_pairs={{0,4},{1,5},{2,6},{3,7},{4,0},{5,1},{6,2},{7,3},{8,12},{9,13},{10,... | collective-permute-start | bytes 1966088 | tf_op jit(solution)/shard_map/ppermute | solution.py:43
  111.2 8.5 %collective-permute-start.20 = (bf16[1,272,512]{2,1,0:T(8,128)(2,1)S(1)}, bf16[1,272,512]{2,1,0:T(8,128)(2,1)}, u32[]{:S(2)}, u32[]{:S(2)}) collective-permute-start(bf16[1,272,512]{2,1,0:T(8,128)(2,1)S(1)} %get-tuple-element.147), channel_id=1, source_target_pairs={{0,4},{1,5},{2,6},{3,7},{4,0},{5,1},{6,2},{7,3},{8,12},{9,13},{10,... | collective-permute-start | bytes 835592 | tf_op jit(solution)/shard_map/ppermute | solution.py:43
  112.2 9.1 %collective-permute-start.19 = (bf16[1,320,512]{2,1,0:T(8,128)(2,1)S(1)}, bf16[1,320,512]{2,1,0:T(8,128)(2,1)S(1)}, u32[]{:S(2)}, u32[]{:S(2)}) collective-permute-start(bf16[1,320,512]{2,1,0:T(8,128)(2,1)S(1)} %get-tuple-element.144), channel_id=1, source_target_pairs={{0,2},{1,3},{2,0},{3,1},{4,6},{5,7},{6,4},{7,5},{8,10},{9,11},{10,... | collective-permute-start | bytes 983048 | tf_op jit(solution)/shard_map/ppermute | solution.py:43
  122.7 7.8 %collective-permute-start.21 = (bf16[296,512]{1,0:T(8,128)(2,1)S(1)}, bf16[296,512]{1,0:T(8,128)(2,1)S(1)}, u32[]{:S(2)}, u32[]{:S(2)}) collective-permute-start(bf16[296,512]{1,0:T(8,128)(2,1)S(1)} %fusion.3), channel_id=1, source_target_pairs={{0,8},{8,0},{16,24},{24,16},{1,9},{9,1},{17,25},{25,17},{2,10},{10... | collective-permute-start | bytes 909320 | tf_op jit(solution)/shard_map/ppermute | solution.py:39
  125.1 15.4 %collective-permute-start.23 = (bf16[208,512]{1,0:T(8,128)(2,1)}, bf16[208,512]{1,0:T(8,128)(2,1)S(1)}, u32[]{:S(2)}, u32[]{:S(2)}) collective-permute-start(bf16[208,512]{1,0:T(8,128)(2,1)} %get-tuple-element.141), channel_id=1, source_target_pairs={{0,6},{1,7},{2,4},{3,5},{4,2},{5,3},{6,0},{7,1},{8,14},{9,15},{10,... | collective-permute-start | bytes 638984 | tf_op jit(solution)/shard_map/ppermute | solution.py:43
  127.2 13.4 %collective-permute-start.24 = (bf16[208,512]{1,0:T(8,128)(2,1)S(1)}, bf16[208,512]{1,0:T(8,128)(2,1)S(1)}, u32[]{:S(2)}, u32[]{:S(2)}) collective-permute-start(bf16[208,512]{1,0:T(8,128)(2,1)S(1)} %get-tuple-element.142), channel_id=1, source_target_pairs={{0,4},{1,5},{2,6},{3,7},{4,0},{5,1},{6,2},{7,3},{8,12},{9,13},{10,... | collective-permute-start | bytes 638984 | tf_op jit(solution)/shard_map/ppermute | solution.py:43
  127.7 12.9 %collective-permute-start.25 = (bf16[208,512]{1,0:T(8,128)(2,1)S(1)}, bf16[208,512]{1,0:T(8,128)(2,1)S(1)}, u32[]{:S(2)}, u32[]{:S(2)}) collective-permute-start(bf16[208,512]{1,0:T(8,128)(2,1)S(1)} %get-tuple-element.143), channel_id=1, source_target_pairs={{0,2},{1,3},{2,0},{3,1},{4,6},{5,7},{6,4},{7,5},{8,10},{9,11},{10,... | collective-permute-start | bytes 638984 | tf_op jit(solution)/shard_map/ppermute | solution.py:43
  130.9 14.3 %collective-permute-start.27 = (bf16[296,512]{1,0:T(8,128)(2,1)S(1)}, bf16[296,512]{1,0:T(8,128)(2,1)S(1)}, u32[]{:S(2)}, u32[]{:S(2)}) collective-permute-start(bf16[296,512]{1,0:T(8,128)(2,1)S(1)} %fusion.5), channel_id=1, source_target_pairs={{0,16},{8,24},{16,0},{24,8},{1,17},{9,25},{17,1},{25,9},{2,18},{10... | collective-permute-start | bytes 909320 | tf_op jit(solution)/shard_map/ppermute | solution.py:39
  145.4 13.9 %collective-permute-start.30 = (bf16[296,512]{1,0:T(8,128)(2,1)S(1)}, bf16[296,512]{1,0:T(8,128)(2,1)S(1)}, u32[]{:S(2)}, u32[]{:S(2)}) collective-permute-start(bf16[296,512]{1,0:T(8,128)(2,1)S(1)} %add.117.s), channel_id=1, source_target_pairs={{0,8},{8,0},{16,24},{24,16},{1,9},{9,1},{17,25},{25,17},{2,10},{10... | collective-permute-start | bytes 909320 | tf_op jit(solution)/shard_map/ppermute | solution.py:39
  147.6 7.4 %collective-permute-start.28 = (bf16[104,512]{1,0:T(8,128)(2,1)S(1)}, bf16[104,512]{1,0:T(8,128)(2,1)S(1)}, u32[]{:S(2)}, u32[]{:S(2)}) collective-permute-start(bf16[104,512]{1,0:T(8,128)(2,1)S(1)} %dynamic-slice_add_fusion), channel_id=1, source_target_pairs={{0,16},{8,24},{16,0},{24,8},{1,17},{9,25},{17,1},{25,9},{2,18},{10... | collective-permute-start | bytes 319496 | tf_op jit(solution)/shard_map/ppermute | solution.py:39
  155.0 6.9 %collective-permute-start.29 = (bf16[104,512]{1,0:T(8,128)(2,1)S(1)}, bf16[104,512]{1,0:T(8,128)(2,1)S(1)}, u32[]{:S(2)}, u32[]{:S(2)}) collective-permute-start(bf16[104,512]{1,0:T(8,128)(2,1)S(1)} %add.119.s), channel_id=1, source_target_pairs={{0,8},{8,0},{16,24},{24,16},{1,9},{9,1},{17,25},{25,17},{2,10},{10... | collective-permute-start | bytes 319496 | tf_op jit(solution)/shard_map/ppermute | solution.py:39
  (28 other events, 164.8 us)

commit v10 on v9

--- a/solution.py
+++ b/solution.py
@@ -759,7 +759,7 @@
     fw = attn_fwd(lengths, kv, qkvt, 0, NP // 2, [])
     fw2 = attn_fwd(lengths, kv, qkvt, NP // 2, NP // 2, fw)
     et, mixed, mixedt, mixedf, linv = fw2
-    pieces2 = gather_forward(after(pack2, *[a for _, _, a in pieces[1:]]), n, fw[4], linv)
+    pieces2 = gather_forward(after(pack2, xht), n, fw[4], linv)
     out, gx1, gmt, keep, send = ffn(lengths, mes, tok, step, vec, upb, cot, mixed, mixedt, pieces2, n)
     bwd = lambda p, c, g, *deps: attn_bwd(kv, qkvt, after(gmt, *deps) if deps else gmt, mixedf, linv, et, p, c, g)
     ra = rf + r
@@ -770,8 +770,10 @@
     add = lambda a, b, k: add16(a[k], b[k])
     rows_a, rows_b = slice(0, ra), slice(ra, None)
     lo, hi = slice(0, h), slice(h, None)
-    ka, xa, kb, xb = [add(keep, got, k) for k in ((lo, rows_a), (hi, rows_a), (lo, rows_b), (hi, rows_b))]
-    g = bwd(1, NP - 1, [g], ka, xa, kb, xb)
+    xa, xb = add(keep, got, (hi, rows_a)), add(keep, got, (hi, rows_b))
+    g = bwd(1, NP - 1, [g], xa, xb)
+    mine, got, _ = lax.optimization_barrier((keep, got, g))
+    ka, kb = add(mine, got, (lo, rows_a)), add(mine, got, (lo, rows_b))
     m = (n // 2).bit_length() - 1
     ga, gb = swap(xa, 2 << (m - 1)), swap(xb, 2)
     for t in range(1, m):

time: 164 us -> 164 us (level)
    add x9 -> x11, other arithmetic: 5.89 us -> 7.9 us  [add16(): return a + b]
  transfers between devices with their start and end apart: 31 -> 31, of which waited for: 12 -> 10; matrix products, arithmetic and copies ran while one was open for 2% -> 3% of each run, Pallas kernels for 43% -> 43%
where the time goes in v10:
time: 164 us
  Pallas kernels  100 us (61%)
  starting transfers between devices  31.7 us (19%)
  waiting for transfers between devices  19.3 us (12%)
  other arithmetic  8.59 us (5%)
  local copies, waits for them, and re-layouts  1.86 us (1%)
  between operations  1.75 us (1%)
    pallas_call x1, Pallas kernels, ffn(): pl.pallas_call(functools.partial(ffn_body, n, meta, min(1024, FF)), grid_...  26.5 us
    pallas_call x2, Pallas kernels, attn_bwd(): pl.pallas_call(functools.partial(attn_bwd_body, HD, 1.0 / math.sqrt(HD),...  23.9 us
    pallas_call x2, Pallas kernels, attn_fwd(): pl.pallas_call(functools.partial(attn_fwd_body, HD, bi, min(256, T), p0),...  19.3 us
    ppermute x25, starting transfers between devices, swap(): return lax.ppermute(x, 'shard', xor_perm(lax.axis_size('shard'), k))  18.9 us
    ppermute x6, starting transfers between devices, rep_perm(): return lax.ppermute(x, 'rep', xor_perm(lax.axis_size('rep'), b))  12.8 us
    ppermute x6, waiting for transfers between devices, rep_perm(): return lax.ppermute(x, 'rep', xor_perm(lax.axis_size('rep'), b))  12.4 us
    add x11, other arithmetic, add16(): return a + b  7.9 us
    pallas_call x1, Pallas kernels, front(): pl.pallas_call(functools.partial(front_body, scale, n, meta), grid_spec=p...  7.06 us
  transfers between devices with their start and end apart: 31, of which 10 were waited for; matrix products, arithmetic and copies ran while one was open for 3% of the time, Pallas kernels for 43%

profile of v10, /device:TPU:0, one launch (start us, length us, event | category | flops | bytes accessed | tf_op | source)
XLA Modules:
  0.0 163.7 jit_solution(1766472942110752744)
XLA Ops:
  0.7 1.8 %pack_first.1.refs_0_ = bf16[208,512]{1,0:T(8,128)(2,1)} custom-call(s32[1]{0:T(128)} %bitcast.me, bf16[64,1536]{1,0:T(8,128)(2,1)} %w.3, bf16[2,128]{1,0:T(2,128)(2,1)} %bitcast.47, bf16[1,64]{1,0:T(2,128)(2,1)} %bitcast.39, bf16[1,64]{1,0:T(2,128)(2,1)} %bitcast.41, bf16[1,64]{1,0:T(2,128)(2,1)} %bitcast.48, bf16[1,64]{1,0:T(2,128)(2,1)} %bitcast.49, ...), custom_call_target="tpu_custom_call" | custom-call | bytes 393216 | tf_op jit(solution)/shard_map/pack_first/pallas_call | solution.py:149
  2.4 2.9 %collective-permute-start = (bf16[208,512]{1,0:T(8,128)(2,1)}, bf16[208,512]{1,0:T(8,128)(2,1)S(1)}, u32[]{:S(2)}, u32[]{:S(2)}) collective-permute-start(bf16[208,512]{1,0:T(8,128)(2,1)} %pack_first.1.refs_0_), channel_id=1, source_target_pairs={{0,2},{1,3},{2,0},{3,1},{4,6},{5,7},{6,4},{7,5},{8,10},{9,11},{10,... | collective-permute-start | bytes 638984 | tf_op jit(solution)/shard_map/ppermute | solution.py:43
  6.9 1.9 %pack_rest.1.refs_0_ = bf16[576,512]{1,0:T(8,128)(2,1)} custom-call(bf16[64,512]{1,0:T(8,128)(2,1)} %wo.1, bf16[64,2048]{1,0:T(8,128)(2,1)} %wu.1, bf16[256,512]{1,0:T(8,128)(2,1)} %wd.1), custom_call_target="tpu_custom_call" | custom-call | bytes 524288 | tf_op jit(solution)/shard_map/pack_rest/pallas_call | solution.py:167
  8.8 4.2 %start.1 = (f32[1024,512]{1,0:T(8,128)}, bf16[512,1024]{1,0:T(8,128)(2,1)}) custom-call(bf16[1024,512]{1,0:T(8,128)(2,1)} %bitcast.43, bf16[1,512]{1,0:T(2,128)(2,1)} %step.4), custom_call_target="tpu_custom_call" | custom-call | flops 10485760 | bytes 4194304 | tf_op jit(solution)/shard_map/start/pallas_call | solution.py:309
  13.6 3.2 %collective-permute-done.1.refs_2_ = bf16[208,512]{1,0:T(8,128)(2,1)S(1)} collective-permute-done((bf16[208,512]{1,0:T(8,128)(2,1)}, bf16[208,512]{1,0:T(8,128)(2,1)S(1)}, u32[]{:S(2)}, u32[]{:S(2)}) %collective-permute-start.1) | collective-permute-done | bytes 213024 | tf_op jit(solution)/shard_map/ppermute | solution.py:43
  20.9 7.1 %front.1 = (bf16[2,1024,512]{2,1,0:T(8,128)(2,1)}, bf16[3,512,1024]{2,1,0:T(8,128)(2,1)}, bf16[512,1536]{1,0:T(8,128)(2,1)}, f32[8,512]{1,0:T(8,128)}, f32[1,2048]{1,0:T(1,128)}) custom-call(s32[1]{0:T(128)} %bitcast.me, f32[1024,512]{1,0:T(8,128)} %get-tuple-element.78.nx, bf16[208,512]{1,0:T(8,128)(2,1)} %pack_first.1.refs_0_, ...), custom_call_target="tpu_custom_call" | custom-call | flops 1610612736 | bytes 6291456 | tf_op jit(solution)/shard_map/front/pallas_call | solution.py:382
  28.0 9.7 %attn_fwd.2 = (bf16[8,1024,1024]{2,1,0:T(8,128)(2,1)}, bf16[1024,512]{1,0:T(8,128)(2,1)}, bf16[512,1024]{1,0:T(8,128)(2,1)}, f32[512,1024]{1,0:T(8,128)}, f32[4,8,1024]{2,1,0:T(8,128)}) custom-call(s32[1]{0:T(128)S(6)} %copy.44.ln, bf16[2,1024,512]{2,1,0:T(8,128)(2,1)} %get-tuple-element.85.k.v, bf16[3,512,1024]{2,1,0:T(8,128)(2,1)} %get-tuple-element.86.qt.vt.kt, ...), custom_call_target="tpu_custom_call" | custom-call | flops 4294967296 | bytes 8388608 | tf_op jit(solution)/shard_map/attn_fwd/pallas_call | solution.py:472
  40.5 9.6 %attn_fwd.3 = (bf16[8,1024,1024]{2,1,0:T(8,128)(2,1)}, bf16[1024,512]{1,0:T(8,128)(2,1)}, bf16[512,1024]{1,0:T(8,128)(2,1)}, f32[512,1024]{1,0:T(8,128)}, f32[4,8,1024]{2,1,0:T(8,128)}) custom-call(s32[1]{0:T(128)S(6)} %copy.44.ln, ...), custom_call_target="tpu_custom_call", output_to_operand_aliasing={{0}: (4, {}), {1}: (5, {}), {2}: (6, {}), {3}: (7, {}), {4}... | custom-call | flops 4294967296 | bytes 8388608 | tf_op jit(solution)/shard_map/attn_fwd/pallas_call | solution.py:472
  53.3 26.5 %ffn.1 = (bf16[1024,512]{1,0:T(8,128)(2,1)}, f32[1024,512]{1,0:T(8,128)}, bf16[512,1024]{1,0:T(8,128)(2,1)}, bf16[4,592,512]{2,1,0:T(8,128)(2,1)}, bf16[4,592,512]{2,1,0:T(8,128)(2,1)}) custom-call(s32[1]{0:T(128)S(6)} %copy.44.ln, s32[1]{0:T(128)} %bitcast.me, bf16[1024,512]{1,0:T(8,128)(2,1)} %bitcast.44, bf16[1,512]{1,0:T(2,128)(2,1)} %step.4, ...), custom_call_target="tpu_custom_call" | custom-call | flops 14495514624 | bytes 8388608 | tf_op jit(solution)/shard_map/ffn/pallas_call | solution.py:628
  80.0 7.8 %attn_bwd.2.refs_0_ = bf16[3,512,1024]{2,1,0:T(8,128)(2,1)} custom-call(bf16[2,1024,512]{2,1,0:T(8,128)(2,1)} %get-tuple-element.85.k.v, bf16[3,512,1024]{2,1,0:T(8,128)(2,1)} %get-tuple-element.86.qt.vt.kt, bf16[3,512,1024]{2,1,0:T(8,128)(2,1)} %get-tuple-element.86.qt.vt.kt, bf16[512,1024]{1,0:T(8,128)(2,1)} %get-tuple-element.107.gt, ...), custom_call_target="tpu_custom_call" | custom-call | flops 4294967296 | bytes 4194304 | tf_op jit(solution)/shard_map/attn_bwd/pallas_call | solution.py:672
  87.9 1.9 %slice_add_fusion.3 = bf16[2,272,512]{2,1,0:T(8,128)(2,1)} fusion(bf16[4,592,512]{2,1,0:T(8,128)(2,1)} %collective-permute-done.16, bf16[4,592,512]{2,1,0:T(8,128)(2,1)S(1)} %copy-done.3), kind=kLoop, calls=%fused_computation.7 | loop fusion | flops 278528 | bytes 1671168 | tf_op jit(solution)/shard_map/add | solution.py:82
  93.1 16.0 %attn_bwd.3.g = bf16[3,512,1024]{2,1,0:T(8,128)(2,1)} custom-call(bf16[2,1024,512]{2,1,0:T(8,128)(2,1)} %get-tuple-element.85.k.v, bf16[3,512,1024]{2,1,0:T(8,128)(2,1)} %get-tuple-element.86.qt.vt.kt, bf16[3,512,1024]{2,1,0:T(8,128)(2,1)} %get-tuple-element.86.qt.vt.kt, bf16[512,1024]{1,0:T(8,128)(2,1)} %get-tuple-element.107.gt, ...), custom_call_target="tpu_custom_call", output_to_operand_aliasing={{}: (7, {})} | custom-call | flops 12884901888 | bytes 12582912 | tf_op jit(solution)/shard_map/attn_bwd/pallas_call | solution.py:672
  114.7 5.6 %wqkv.1 = (bf16[4,208,512]{2,1,0:T(8,128)(2,1)}, bf16[4,208,512]{2,1,0:T(8,128)(2,1)}) custom-call(s32[1]{0:T(128)} %bitcast.me, bf16[512,1024]{1,0:T(8,128)(2,1)} %get-tuple-element.112.xht, bf16[3,512,1024]{2,1,0:T(8,128)(2,1)} %attn_bwd.3.g), custom_call_target="tpu_custom_call" | custom-call | flops 1610612736 | bytes 5242880 | tf_op jit(solution)/shard_map/wqkv/pallas_call | solution.py:709
  123.0 1.6 %collective-permute-start.21 = (bf16[296,512]{1,0:T(8,128)(2,1)S(1)}, bf16[296,512]{1,0:T(8,128)(2,1)S(1)}, u32[]{:S(2)}, u32[]{:S(2)}) collective-permute-start(bf16[296,512]{1,0:T(8,128)(2,1)S(1)} %fusion.3), channel_id=1, source_target_pairs={{0,8},{8,0},{16,24},{24,16},{1,9},{9,1},{17,25},{25,17},{2,10},{10... | collective-permute-start | bytes 909320 | tf_op jit(solution)/shard_map/ppermute | solution.py:39
  125.5 2.2 %collective-permute-start.23 = (bf16[208,512]{1,0:T(8,128)(2,1)}, bf16[208,512]{1,0:T(8,128)(2,1)S(1)}, u32[]{:S(2)}, u32[]{:S(2)}) collective-permute-start(bf16[208,512]{1,0:T(8,128)(2,1)} %get-tuple-element.141), channel_id=1, source_target_pairs={{0,6},{1,7},{2,4},{3,5},{4,2},{5,3},{6,0},{7,1},{8,14},{9,15},{10,... | collective-permute-start | bytes 638984 | tf_op jit(solution)/shard_map/ppermute | solution.py:43
  129.0 1.8 %collective-permute-done.21 = bf16[296,512]{1,0:T(8,128)(2,1)S(1)} collective-permute-done((bf16[296,512]{1,0:T(8,128)(2,1)S(1)}, bf16[296,512]{1,0:T(8,128)(2,1)S(1)}, u32[]{:S(2)}, u32[]{:S(2)}) %collective-permute-start.21) | collective-permute-done | bytes 303136 | tf_op jit(solution)/shard_map/ppermute | solution.py:39
  131.2 2.7 %collective-permute-start.27 = (bf16[296,512]{1,0:T(8,128)(2,1)S(1)}, bf16[296,512]{1,0:T(8,128)(2,1)S(1)}, u32[]{:S(2)}, u32[]{:S(2)}) collective-permute-start(bf16[296,512]{1,0:T(8,128)(2,1)S(1)} %fusion.5), channel_id=1, source_target_pairs={{0,16},{8,24},{16,0},{24,8},{1,17},{9,25},{17,1},{25,9},{2,18},{10... | collective-permute-start | bytes 909320 | tf_op jit(solution)/shard_map/ppermute | solution.py:39
  133.9 7.0 %back.1 = f32[1024,512]{1,0:T(8,128)} custom-call(bf16[1024,512]{1,0:T(8,128)(2,1)} %bitcast.45, bf16[1,512]{1,0:T(2,128)(2,1)} %step.4, f32[8,512]{1,0:T(8,128)} %get-tuple-element.83.vec, bf16[3,512,1024]{2,1,0:T(8,128)(2,1)} %attn_bwd.3.g, f32[1024,512]{1,0:T(8,128)} %get-tuple-element.119.gx1, bf16[512,1536]{1,0:T(8,128)(2,1)} %get-tuple-element.120.refs_0_), custom_call_target="tpu_custom_call" | custom-call | flops 1610612736 | bytes 7340032 | tf_op jit(solution)/shard_map/back/pallas_call | solution.py:736
  141.1 1.6 collective-permute-start.26
  142.7 2.9 %collective-permute-done.27 = bf16[296,512]{1,0:T(8,128)(2,1)S(1)} collective-permute-done((bf16[296,512]{1,0:T(8,128)(2,1)S(1)}, bf16[296,512]{1,0:T(8,128)(2,1)S(1)}, u32[]{:S(2)}, u32[]{:S(2)}) %collective-permute-start.27) | collective-permute-done | bytes 303136 | tf_op jit(solution)/shard_map/ppermute | solution.py:39
  147.9 2.0 %collective-permute-start.28 = (bf16[104,512]{1,0:T(8,128)(2,1)S(1)}, bf16[104,512]{1,0:T(8,128)(2,1)S(1)}, u32[]{:S(2)}, u32[]{:S(2)}) collective-permute-start(bf16[104,512]{1,0:T(8,128)(2,1)S(1)} %dynamic-slice_add_fusion), channel_id=1, source_target_pairs={{0,16},{8,24},{16,0},{24,8},{1,17},{9,25},{17,1},{25,9},{2,18},{10... | collective-permute-start | bytes 319496 | tf_op jit(solution)/shard_map/ppermute | solution.py:39
  149.9 5.4 %collective-permute-done.28 = bf16[104,512]{1,0:T(8,128)(2,1)S(1)} collective-permute-done((bf16[104,512]{1,0:T(8,128)(2,1)S(1)}, bf16[104,512]{1,0:T(8,128)(2,1)S(1)}, u32[]{:S(2)}, u32[]{:S(2)}) %collective-permute-start.28) | collective-permute-done | bytes 106528 | tf_op jit(solution)/shard_map/ppermute | solution.py:39
  155.3 4.2 %collective-permute-start.29 = (bf16[104,512]{1,0:T(8,128)(2,1)S(1)}, bf16[104,512]{1,0:T(8,128)(2,1)S(1)}, u32[]{:S(2)}, u32[]{:S(2)}) collective-permute-start(bf16[104,512]{1,0:T(8,128)(2,1)S(1)} %add.119.s), channel_id=1, source_target_pairs={{0,8},{8,0},{16,24},{24,16},{1,9},{9,1},{17,25},{25,17},{2,10},{10... | collective-permute-start | bytes 319496 | tf_op jit(solution)/shard_map/ppermute | solution.py:39
  159.5 1.7 %finish_rest.1 = (f32[256,512]{1,0:T(8,128)}, f32[64,2048]{1,0:T(8,128)}, f32[64,512]{1,0:T(8,128)}, f32[1,256]{1,0:T(1,128)}, f32[1,64]{1,0:T(1,128)}, /*index=...) custom-call(s32[2]{0:T(128)S(1)} %pad_add_fusion.ids, bf16[296,512]{1,0:T(8,128)(2,1)S(1)} %add.117.s, ...), custom_call_target="tpu_custom_call" | custom-call | bytes 1212416 | tf_op jit(solution)/shard_map/finish_rest/pallas_call | solution.py:225
  (112 shorter events, 30.6 us)
Async XLA Ops:
  2.4 10.6 %collective-permute-start = (bf16[208,512]{1,0:T(8,128)(2,1)}, bf16[208,512]{1,0:T(8,128)(2,1)S(1)}, u32[]{:S(2)}, u32[]{:S(2)}) collective-permute-start(bf16[208,512]{1,0:T(8,128)(2,1)} %pack_first.1.refs_0_), channel_id=1, source_target_pairs={{0,2},{1,3},{2,0},{3,1},{4,6},{5,7},{6,4},{7,5},{8,10},{9,11},{10,... | collective-permute-start | bytes 638984 | tf_op jit(solution)/shard_map/ppermute | solution.py:43
  5.4 11.5 %collective-permute-start.1 = (bf16[208,512]{1,0:T(8,128)(2,1)}, bf16[208,512]{1,0:T(8,128)(2,1)S(1)}, u32[]{:S(2)}, u32[]{:S(2)}) collective-permute-start(bf16[208,512]{1,0:T(8,128)(2,1)} %pack_first.1.refs_0_), channel_id=1, source_target_pairs={{0,4},{1,5},{2,6},{3,7},{4,0},{5,1},{6,2},{7,3},{8,12},{9,13},{10,... | collective-permute-start | bytes 638984 | tf_op jit(solution)/shard_map/ppermute | solution.py:43
  6.9 10.0 %collective-permute-start.2 = (bf16[208,512]{1,0:T(8,128)(2,1)}, bf16[208,512]{1,0:T(8,128)(2,1)S(1)}, u32[]{:S(2)}, u32[]{:S(2)}) collective-permute-start(bf16[208,512]{1,0:T(8,128)(2,1)} %pack_first.1.refs_0_), channel_id=1, source_target_pairs={{0,6},{1,7},{2,4},{3,5},{4,2},{5,3},{6,0},{7,1},{8,14},{9,15},{10,... | collective-permute-start | bytes 638984 | tf_op jit(solution)/shard_map/ppermute | solution.py:43
  6.9 11.2 %collective-permute-start.3 = (bf16[208,512]{1,0:T(8,128)(2,1)}, bf16[208,512]{1,0:T(8,128)(2,1)S(1)}, u32[]{:S(2)}, u32[]{:S(2)}) collective-permute-start(bf16[208,512]{1,0:T(8,128)(2,1)} %pack_first.1.refs_0_), channel_id=1, source_target_pairs={{0,1},{1,0},{2,3},{3,2},{4,5},{5,4},{6,7},{7,6},{8,9},{9,8},{10,11... | collective-permute-start | bytes 638984 | tf_op jit(solution)/shard_map/ppermute | solution.py:43
  13.0 7.1 %collective-permute-start.4 = (bf16[208,512]{1,0:T(8,128)(2,1)S(1)}, bf16[208,512]{1,0:T(8,128)(2,1)S(1)}, u32[]{:S(2)}, u32[]{:S(2)}) collective-permute-start(bf16[208,512]{1,0:T(8,128)(2,1)S(1)} %collective-permute-done.refs_1_), channel_id=1, source_target_pairs={{0,1},{1,0},{2,3},{3,2},{4,5},{5,4},{6,7},{7,6},{8,9},{9,8},{10,11... | collective-permute-start | bytes 638984 | tf_op jit(solution)/shard_map/ppermute | solution.py:43
  17.4 20.4 %collective-permute-start.7 = (bf16[576,512]{1,0:T(8,128)(2,1)}, bf16[576,512]{1,0:T(8,128)(2,1)S(1)}, u32[]{:S(2)}, u32[]{:S(2)}) collective-permute-start(bf16[576,512]{1,0:T(8,128)(2,1)} %pack_rest.1.refs_0_), channel_id=1, source_target_pairs={{0,2},{1,3},{2,0},{3,1},{4,6},{5,7},{6,4},{7,5},{8,10},{9,11},{10,... | collective-permute-start | bytes 1769480 | tf_op jit(solution)/shard_map/ppermute | solution.py:43
  18.1 20.2 %collective-permute-start.8 = (bf16[576,512]{1,0:T(8,128)(2,1)}, bf16[576,512]{1,0:T(8,128)(2,1)S(1)}, u32[]{:S(2)}, u32[]{:S(2)}) collective-permute-start(bf16[576,512]{1,0:T(8,128)(2,1)} %pack_rest.1.refs_0_), channel_id=1, source_target_pairs={{0,4},{1,5},{2,6},{3,7},{4,0},{5,1},{6,2},{7,3},{8,12},{9,13},{10,... | collective-permute-start | bytes 1769480 | tf_op jit(solution)/shard_map/ppermute | solution.py:43
  20.1 30.6 %collective-permute-start.9 = (bf16[576,512]{1,0:T(8,128)(2,1)}, bf16[576,512]{1,0:T(8,128)(2,1)S(1)}, u32[]{:S(2)}, u32[]{:S(2)}) collective-permute-start(bf16[576,512]{1,0:T(8,128)(2,1)} %pack_rest.1.refs_0_), channel_id=1, source_target_pairs={{0,1},{1,0},{2,3},{3,2},{4,5},{5,4},{6,7},{7,6},{8,9},{9,8},{10,11... | collective-permute-start | bytes 1769480 | tf_op jit(solution)/shard_map/ppermute | solution.py:43
  37.8 14.5 %collective-permute-start.10 = (bf16[576,512]{1,0:T(8,128)(2,1)S(1)}, bf16[576,512]{1,0:T(8,128)(2,1)S(1)}, u32[]{:S(2)}, u32[]{:S(2)}) collective-permute-start(bf16[576,512]{1,0:T(8,128)(2,1)S(1)} %collective-permute-done.7.refs_1_), channel_id=1, source_target_pairs={{0,1},{1,0},{2,3},{3,2},{4,5},{5,4},{6,7},{7,6},{8,9},{9,8},{10,11... | collective-permute-start | bytes 1769480 | tf_op jit(solution)/shard_map/ppermute | solution.py:43
  38.4 13.9 %collective-permute-start.11 = (bf16[576,512]{1,0:T(8,128)(2,1)S(1)}, bf16[576,512]{1,0:T(8,128)(2,1)S(1)}, u32[]{:S(2)}, u32[]{:S(2)}) collective-permute-start(bf16[576,512]{1,0:T(8,128)(2,1)S(1)} %collective-permute-done.8.refs_2_), channel_id=1, source_target_pairs={{0,1},{1,0},{2,3},{3,2},{4,5},{5,4},{6,7},{7,6},{8,9},{9,8},{10,11... | collective-permute-start | bytes 1769480 | tf_op jit(solution)/shard_map/ppermute | solution.py:43
  38.5 11.7 %collective-permute-start.13 = (bf16[288,512]{1,0:T(8,128)(2,1)S(1)}, bf16[288,512]{1,0:T(8,128)(2,1)S(1)}, u32[]{:S(2)}, u32[]{:S(2)}) collective-permute-start(bf16[288,512]{1,0:T(8,128)(2,1)S(1)} %slice.79), channel_id=1, source_target_pairs={{0,4},{1,5},{2,6},{3,7},{4,0},{5,1},{6,2},{7,3},{8,12},{9,13},{10,... | collective-permute-start | bytes 884744 | tf_op jit(solution)/shard_map/ppermute | solution.py:43
  39.2 11.0 %collective-permute-start.12 = (bf16[288,512]{1,0:T(8,128)(2,1)S(1)}, bf16[288,512]{1,0:T(8,128)(2,1)S(1)}, u32[]{:S(2)}, u32[]{:S(2)}) collective-permute-start(bf16[288,512]{1,0:T(8,128)(2,1)S(1)} %slice.78), channel_id=1, source_target_pairs={{0,2},{1,3},{2,0},{3,1},{4,6},{5,7},{6,4},{7,5},{8,10},{9,11},{10,... | collective-permute-start | bytes 884744 | tf_op jit(solution)/shard_map/ppermute | solution.py:43
  79.8 8.0 %collective-permute-start.16 = (bf16[4,592,512]{2,1,0:T(8,128)(2,1)}, bf16[4,592,512]{2,1,0:T(8,128)(2,1)}, u32[]{:S(2)}, u32[]{:S(2)}) collective-permute-start(bf16[4,592,512]{2,1,0:T(8,128)(2,1)} %get-tuple-element.102), channel_id=1, source_target_pairs={{0,1},{1,0},{2,3},{3,2},{4,5},{5,4},{6,7},{7,6},{8,9},{9,8},{10,11... | collective-permute-start | bytes 7274504 | tf_op jit(solution)/shard_map/ppermute | solution.py:43
  91.0 20.4 %collective-permute-start.18 = (bf16[2,272,512]{2,1,0:T(8,128)(2,1)}, bf16[2,272,512]{2,1,0:T(8,128)(2,1)}, u32[]{:S(2)}, u32[]{:S(2)}) collective-permute-start(bf16[2,272,512]{2,1,0:T(8,128)(2,1)} %slice_add_fusion.3), channel_id=1, source_target_pairs={{0,2},{1,3},{2,0},{3,1},{4,6},{5,7},{6,4},{7,5},{8,10},{9,11},{10,... | collective-permute-start | bytes 1671176 | tf_op jit(solution)/shard_map/ppermute | solution.py:43
  91.7 19.7 %collective-permute-start.17 = (bf16[2,320,512]{2,1,0:T(8,128)(2,1)S(1)}, bf16[2,320,512]{2,1,0:T(8,128)(2,1)S(1)}, u32[]{:S(2)}, u32[]{:S(2)}) collective-permute-start(bf16[2,320,512]{2,1,0:T(8,128)(2,1)S(1)} %slice_add_fusion.1), channel_id=1, source_target_pairs={{0,4},{1,5},{2,6},{3,7},{4,0},{5,1},{6,2},{7,3},{8,12},{9,13},{10,... | collective-permute-start | bytes 1966088 | tf_op jit(solution)/shard_map/ppermute | solution.py:43
  112.5 8.4 %collective-permute-start.20 = (bf16[1,272,512]{2,1,0:T(8,128)(2,1)S(1)}, bf16[1,272,512]{2,1,0:T(8,128)(2,1)S(1)}, u32[]{:S(2)}, u32[]{:S(2)}) collective-permute-start(bf16[1,272,512]{2,1,0:T(8,128)(2,1)S(1)} %get-tuple-element.147), channel_id=1, source_target_pairs={{0,4},{1,5},{2,6},{3,7},{4,0},{5,1},{6,2},{7,3},{8,12},{9,13},{10,... | collective-permute-start | bytes 835592 | tf_op jit(solution)/shard_map/ppermute | solution.py:43
  113.3 9.2 %collective-permute-start.19 = (bf16[1,320,512]{2,1,0:T(8,128)(2,1)S(1)}, bf16[1,320,512]{2,1,0:T(8,128)(2,1)S(1)}, u32[]{:S(2)}, u32[]{:S(2)}) collective-permute-start(bf16[1,320,512]{2,1,0:T(8,128)(2,1)S(1)} %get-tuple-element.144), channel_id=1, source_target_pairs={{0,2},{1,3},{2,0},{3,1},{4,6},{5,7},{6,4},{7,5},{8,10},{9,11},{10,... | collective-permute-start | bytes 983048 | tf_op jit(solution)/shard_map/ppermute | solution.py:43
  123.0 7.8 %collective-permute-start.21 = (bf16[296,512]{1,0:T(8,128)(2,1)S(1)}, bf16[296,512]{1,0:T(8,128)(2,1)S(1)}, u32[]{:S(2)}, u32[]{:S(2)}) collective-permute-start(bf16[296,512]{1,0:T(8,128)(2,1)S(1)} %fusion.3), channel_id=1, source_target_pairs={{0,8},{8,0},{16,24},{24,16},{1,9},{9,1},{17,25},{25,17},{2,10},{10... | collective-permute-start | bytes 909320 | tf_op jit(solution)/shard_map/ppermute | solution.py:39
  125.5 15.4 %collective-permute-start.23 = (bf16[208,512]{1,0:T(8,128)(2,1)}, bf16[208,512]{1,0:T(8,128)(2,1)S(1)}, u32[]{:S(2)}, u32[]{:S(2)}) collective-permute-start(bf16[208,512]{1,0:T(8,128)(2,1)} %get-tuple-element.141), channel_id=1, source_target_pairs={{0,6},{1,7},{2,4},{3,5},{4,2},{5,3},{6,0},{7,1},{8,14},{9,15},{10,... | collective-permute-start | bytes 638984 | tf_op jit(solution)/shard_map/ppermute | solution.py:43
  127.8 13.1 %collective-permute-start.24 = (bf16[208,512]{1,0:T(8,128)(2,1)}, bf16[208,512]{1,0:T(8,128)(2,1)S(1)}, u32[]{:S(2)}, u32[]{:S(2)}) collective-permute-start(bf16[208,512]{1,0:T(8,128)(2,1)} %get-tuple-element.142), channel_id=1, source_target_pairs={{0,4},{1,5},{2,6},{3,7},{4,0},{5,1},{6,2},{7,3},{8,12},{9,13},{10,... | collective-permute-start | bytes 638984 | tf_op jit(solution)/shard_map/ppermute | solution.py:43
  128.3 12.6 %collective-permute-start.25 = (bf16[208,512]{1,0:T(8,128)(2,1)S(1)}, bf16[208,512]{1,0:T(8,128)(2,1)S(1)}, u32[]{:S(2)}, u32[]{:S(2)}) collective-permute-start(bf16[208,512]{1,0:T(8,128)(2,1)S(1)} %get-tuple-element.143), channel_id=1, source_target_pairs={{0,2},{1,3},{2,0},{3,1},{4,6},{5,7},{6,4},{7,5},{8,10},{9,11},{10,... | collective-permute-start | bytes 638984 | tf_op jit(solution)/shard_map/ppermute | solution.py:43
  131.2 14.3 %collective-permute-start.27 = (bf16[296,512]{1,0:T(8,128)(2,1)S(1)}, bf16[296,512]{1,0:T(8,128)(2,1)S(1)}, u32[]{:S(2)}, u32[]{:S(2)}) collective-permute-start(bf16[296,512]{1,0:T(8,128)(2,1)S(1)} %fusion.5), channel_id=1, source_target_pairs={{0,16},{8,24},{16,0},{24,8},{1,17},{9,25},{17,1},{25,9},{2,18},{10... | collective-permute-start | bytes 909320 | tf_op jit(solution)/shard_map/ppermute | solution.py:39
  145.6 13.9 %collective-permute-start.30 = (bf16[296,512]{1,0:T(8,128)(2,1)S(1)}, bf16[296,512]{1,0:T(8,128)(2,1)S(1)}, u32[]{:S(2)}, u32[]{:S(2)}) collective-permute-start(bf16[296,512]{1,0:T(8,128)(2,1)S(1)} %add.117.s), channel_id=1, source_target_pairs={{0,8},{8,0},{16,24},{24,16},{1,9},{9,1},{17,25},{25,17},{2,10},{10... | collective-permute-start | bytes 909320 | tf_op jit(solution)/shard_map/ppermute | solution.py:39
  147.9 7.4 %collective-permute-start.28 = (bf16[104,512]{1,0:T(8,128)(2,1)S(1)}, bf16[104,512]{1,0:T(8,128)(2,1)S(1)}, u32[]{:S(2)}, u32[]{:S(2)}) collective-permute-start(bf16[104,512]{1,0:T(8,128)(2,1)S(1)} %dynamic-slice_add_fusion), channel_id=1, source_target_pairs={{0,16},{8,24},{16,0},{24,8},{1,17},{9,25},{17,1},{25,9},{2,18},{10... | collective-permute-start | bytes 319496 | tf_op jit(solution)/shard_map/ppermute | solution.py:39
  (28 other events, 155.8 us)

commit v11 on v10

--- a/solution.py
+++ b/solution.py
@@ -766,26 +766,29 @@
     got = swap(send, 1)
     g = bwd(0, 1, [])
     got = after(got, g)
+    pick = lambda terms, s: [t[s] for t in terms]
+    sum_of = lambda terms: total(terms[0], terms[1:])
     h = n // 4
-    add = lambda a, b, k: add16(a[k], b[k])
+    lo, hi = slice(0, h), slice(h, None)
+    of = lambda s, rows: [keep[s, rows], got[s, rows]]
     rows_a, rows_b = slice(0, ra), slice(ra, None)
-    lo, hi = slice(0, h), slice(h, None)
-    xa, xb = add(keep, got, (hi, rows_a)), add(keep, got, (hi, rows_b))
+    xa, xb = sum_of(of(hi, rows_a)), sum_of(of(hi, rows_b))
     g = bwd(1, NP - 1, [g], xa, xb)
-    mine, got, _ = lax.optimization_barrier((keep, got, g))
-    ka, kb = add(mine, got, (lo, rows_a)), add(mine, got, (lo, rows_b))
     m = (n // 2).bit_length() - 1
     ga, gb = swap(xa, 2 << (m - 1)), swap(xb, 2)
+    keep, got, ga, gb, _ = lax.optimization_barrier((keep, got, ga, gb, g))
+    ta, tb = of(lo, rows_a) + [ga], of(lo, rows_b) + [gb]
     for t in range(1, m):
-        dep = g if t == 1 else keep
-        ga, gb, _ = lax.optimization_barrier((ga, gb, dep))
         h //= 2
         lo, hi = slice(0, h), slice(h, None)
-        ka, xa = add(ka, ga, lo), add(ka, ga, hi)
-        kb, xb = add(kb, gb, lo), add(kb, gb, hi)
+        xa, xb = sum_of(pick(ta, hi)), sum_of(pick(tb, hi))
+        ta, tb = pick(ta, lo), pick(tb, lo)
         ga, gb = swap(xa, 2 << (m - 1 - t)), swap(xb, 2 << t)
         if t == 1:
-            keep, send = wqkv(mes, after(xht, ka, xa, kb, xb), g, n)
+            keep, send = wqkv(mes, after(xht, xa, xb), g, n)
+        ga, gb, *rest, _ = lax.optimization_barrier((ga, gb, *ta, *tb, keep))
+        ta, tb = rest[: len(ta)] + [ga], rest[len(ta) :] + [gb]
+    ga, gb = sum_of(ta), sum_of(tb)
     got = swap(send, 1)
     p2 = [add16(keep[k], got[k]) for k in range(n // 2)]
     far2 = spread(p2)
@@ -793,7 +796,7 @@
     got = swap(send, 1)
     p2 = [add16(keep[k], got[k]) for k in range(n // 2)]
     far2 = spread(p2)
-    own1 = jnp.concatenate([add16(ka, ga)[0], add16(kb, gb)[0]], axis=0)
+    own1 = jnp.concatenate([ga[0], gb[0]], axis=0)
     m1, o1, x1 = rep_half(own1)
     z1 = add16(m1, after(o1, *p2[1:]))
     tg = back(tok, after(step, z1, *p2[1:]), vec, [w], g, gx1)

time: 164 us -> 172 us (1.049)
  other arithmetic: 8.59 us -> 13.7 us
  local copies, waits for them, and re-layouts: 1.86 us -> 4.02 us
    convert_element_type x1 -> x7, other arithmetic: 0.14 us -> 11.4 us  [total(): return t.astype(bf16)]
    add x11 -> x5, other arithmetic: 7.9 us -> 1.79 us  [add16(): return a + b]
    ppermute x6, waiting for transfers between devices: 12.4 us -> 14.8 us  [rep_perm(): return lax.ppermute(x, 'rep', xor_perm(lax.axis_size('rep'), b))]
    ppermute x25, waiting for transfers between devices: 6.89 us -> 4.72 us  [swap(): return lax.ppermute(x, 'shard', xor_perm(lax.axis_size('shard'), k))]
    slice x0 -> x8, local copies, waits for them, and re-layouts: none -> 2.11 us  [shards(): pick = lambda terms, s: [t[s] for t in terms]]
  transfers between devices with their start and end apart: 31 -> 31, of which waited for: 10 -> 8; matrix products, arithmetic and copies ran while one was open for 3% -> 6% of each run, Pallas kernels for 43% -> 41%
where the time goes in v11:
time: 172 us
  Pallas kernels  101 us (59%)
  starting transfers between devices  31.9 us (19%)
  waiting for transfers between devices  19.6 us (11%)
  other arithmetic  13.7 us (8%)
  local copies, waits for them, and re-layouts  4.02 us (2%)
  between operations  1.81 us (1%)
    pallas_call x1, Pallas kernels, ffn(): pl.pallas_call(functools.partial(ffn_body, n, meta, min(1024, FF)), grid_...  26.5 us
    pallas_call x2, Pallas kernels, attn_bwd(): pl.pallas_call(functools.partial(attn_bwd_body, HD, 1.0 / math.sqrt(HD),...  23.9 us
    pallas_call x2, Pallas kernels, attn_fwd(): pl.pallas_call(functools.partial(attn_fwd_body, HD, bi, min(256, T), p0),...  19.3 us
    ppermute x25, starting transfers between devices, swap(): return lax.ppermute(x, 'shard', xor_perm(lax.axis_size('shard'), k))  19.1 us
    ppermute x6, waiting for transfers between devices, rep_perm(): return lax.ppermute(x, 'rep', xor_perm(lax.axis_size('rep'), b))  14.8 us
    ppermute x6, starting transfers between devices, rep_perm(): return lax.ppermute(x, 'rep', xor_perm(lax.axis_size('rep'), b))  12.8 us
    convert_element_type x7, other arithmetic, total(): return t.astype(bf16)  11.4 us
    pallas_call x1, Pallas kernels, front(): pl.pallas_call(functools.partial(front_body, scale, n, meta), grid_spec=p...  7.02 us
  transfers between devices with their start and end apart: 31, of which 8 were waited for; matrix products, arithmetic and copies ran while one was open for 6% of the time, Pallas kernels for 41%

profile of v11, /device:TPU:0, one launch (start us, length us, event | category | flops | bytes accessed | tf_op | source)
XLA Modules:
  0.0 171.5 jit_solution(6618993721718263804)
XLA Ops:
  0.7 1.8 %pack_first.1.refs_0_ = bf16[208,512]{1,0:T(8,128)(2,1)} custom-call(s32[1]{0:T(128)} %bitcast.me, bf16[64,1536]{1,0:T(8,128)(2,1)} %w.3, bf16[2,128]{1,0:T(2,128)(2,1)} %bitcast.49, bf16[1,64]{1,0:T(2,128)(2,1)} %bitcast.37, bf16[1,64]{1,0:T(2,128)(2,1)} %bitcast.39, bf16[1,64]{1,0:T(2,128)(2,1)} %bitcast.50, bf16[1,64]{1,0:T(2,128)(2,1)} %bitcast.51, ...), custom_call_target="tpu_custom_call" | custom-call | bytes 393216 | tf_op jit(solution)/shard_map/pack_first/pallas_call | solution.py:149
  2.4 2.9 %collective-permute-start = (bf16[208,512]{1,0:T(8,128)(2,1)}, bf16[208,512]{1,0:T(8,128)(2,1)S(1)}, u32[]{:S(2)}, u32[]{:S(2)}) collective-permute-start(bf16[208,512]{1,0:T(8,128)(2,1)} %pack_first.1.refs_0_), channel_id=1, source_target_pairs={{0,2},{1,3},{2,0},{3,1},{4,6},{5,7},{6,4},{7,5},{8,10},{9,11},{10,... | collective-permute-start | bytes 638984 | tf_op jit(solution)/shard_map/ppermute | solution.py:43
  6.9 1.9 %pack_rest.1.refs_0_ = bf16[576,512]{1,0:T(8,128)(2,1)} custom-call(bf16[64,512]{1,0:T(8,128)(2,1)} %wo.1, bf16[64,2048]{1,0:T(8,128)(2,1)} %wu.1, bf16[256,512]{1,0:T(8,128)(2,1)} %wd.1), custom_call_target="tpu_custom_call" | custom-call | bytes 524288 | tf_op jit(solution)/shard_map/pack_rest/pallas_call | solution.py:167
  8.8 4.3 %start.1 = (f32[1024,512]{1,0:T(8,128)}, bf16[512,1024]{1,0:T(8,128)(2,1)}) custom-call(bf16[1024,512]{1,0:T(8,128)(2,1)} %bitcast.41, bf16[1,512]{1,0:T(2,128)(2,1)} %step.4), custom_call_target="tpu_custom_call" | custom-call | flops 10485760 | bytes 4194304 | tf_op jit(solution)/shard_map/start/pallas_call | solution.py:309
  13.7 3.2 %collective-permute-done.1.refs_2_ = bf16[208,512]{1,0:T(8,128)(2,1)S(1)} collective-permute-done((bf16[208,512]{1,0:T(8,128)(2,1)}, bf16[208,512]{1,0:T(8,128)(2,1)S(1)}, u32[]{:S(2)}, u32[]{:S(2)}) %collective-permute-start.1) | collective-permute-done | bytes 213024 | tf_op jit(solution)/shard_map/ppermute | solution.py:43
  21.0 7.0 %front.1 = (bf16[2,1024,512]{2,1,0:T(8,128)(2,1)}, bf16[3,512,1024]{2,1,0:T(8,128)(2,1)}, bf16[512,1536]{1,0:T(8,128)(2,1)}, f32[8,512]{1,0:T(8,128)}, f32[1,2048]{1,0:T(1,128)}) custom-call(s32[1]{0:T(128)} %bitcast.me, f32[1024,512]{1,0:T(8,128)} %get-tuple-element.86.nx, bf16[208,512]{1,0:T(8,128)(2,1)} %pack_first.1.refs_0_, ...), custom_call_target="tpu_custom_call" | custom-call | flops 1610612736 | bytes 6291456 | tf_op jit(solution)/shard_map/front/pallas_call | solution.py:382
  28.0 9.7 %attn_fwd.2 = (bf16[8,1024,1024]{2,1,0:T(8,128)(2,1)}, bf16[1024,512]{1,0:T(8,128)(2,1)}, bf16[512,1024]{1,0:T(8,128)(2,1)}, f32[512,1024]{1,0:T(8,128)}, f32[4,8,1024]{2,1,0:T(8,128)}) custom-call(s32[1]{0:T(128)S(6)} %copy.44.ln, bf16[2,1024,512]{2,1,0:T(8,128)(2,1)} %get-tuple-element.93.k.v, bf16[3,512,1024]{2,1,0:T(8,128)(2,1)} %get-tuple-element.94.qt.vt.kt, ...), custom_call_target="tpu_custom_call" | custom-call | flops 4294967296 | bytes 8388608 | tf_op jit(solution)/shard_map/attn_fwd/pallas_call | solution.py:472
  40.5 9.6 %attn_fwd.3 = (bf16[8,1024,1024]{2,1,0:T(8,128)(2,1)}, bf16[1024,512]{1,0:T(8,128)(2,1)}, bf16[512,1024]{1,0:T(8,128)(2,1)}, f32[512,1024]{1,0:T(8,128)}, f32[4,8,1024]{2,1,0:T(8,128)}) custom-call(s32[1]{0:T(128)S(6)} %copy.44.ln, ...), custom_call_target="tpu_custom_call", output_to_operand_aliasing={{0}: (4, {}), {1}: (5, {}), {2}: (6, {}), {3}: (7, {}), {4}... | custom-call | flops 4294967296 | bytes 8388608 | tf_op jit(solution)/shard_map/attn_fwd/pallas_call | solution.py:472
  53.4 26.5 %ffn.1 = (bf16[1024,512]{1,0:T(8,128)(2,1)}, f32[1024,512]{1,0:T(8,128)}, bf16[512,1024]{1,0:T(8,128)(2,1)}, bf16[4,592,512]{2,1,0:T(8,128)(2,1)}, bf16[4,592,512]{2,1,0:T(8,128)(2,1)}) custom-call(s32[1]{0:T(128)S(6)} %copy.44.ln, s32[1]{0:T(128)} %bitcast.me, bf16[1024,512]{1,0:T(8,128)(2,1)} %bitcast.42, bf16[1,512]{1,0:T(2,128)(2,1)} %step.4, ...), custom_call_target="tpu_custom_call" | custom-call | flops 14495514624 | bytes 8388608 | tf_op jit(solution)/shard_map/ffn/pallas_call | solution.py:628
  80.1 7.8 %attn_bwd.2.refs_0_ = bf16[3,512,1024]{2,1,0:T(8,128)(2,1)} custom-call(bf16[2,1024,512]{2,1,0:T(8,128)(2,1)} %get-tuple-element.93.k.v, bf16[3,512,1024]{2,1,0:T(8,128)(2,1)} %get-tuple-element.94.qt.vt.kt, bf16[3,512,1024]{2,1,0:T(8,128)(2,1)} %get-tuple-element.94.qt.vt.kt, bf16[512,1024]{1,0:T(8,128)(2,1)} %get-tuple-element.115.gt, ...), custom_call_target="tpu_custom_call" | custom-call | flops 4294967296 | bytes 4194304 | tf_op jit(solution)/shard_map/attn_bwd/pallas_call | solution.py:672
  88.0 2.0 %add_convert_fusion.1 = bf16[2,272,512]{2,1,0:T(8,128)(2,1)} fusion(bf16[4,592,512]{2,1,0:T(8,128)(2,1)} %collective-permute-done.16, bf16[4,592,512]{2,1,0:T(8,128)(2,1)S(1)} %copy-done.3), kind=kLoop, calls=%fused_computation.1 | loop fusion | flops 1114112 | bytes 1671168 | tf_op jit(solution)/shard_map/convert_element_type | solution.py:93
  90.0 2.1 %add_convert_fusion = bf16[2,320,512]{2,1,0:T(8,128)(2,1)} fusion(bf16[4,592,512]{2,1,0:T(8,128)(2,1)} %collective-permute-done.16, bf16[4,592,512]{2,1,0:T(8,128)(2,1)S(1)} %copy-done.3), kind=kLoop, calls=%fused_computation | loop fusion | flops 1310720 | bytes 1966080 | tf_op jit(solution)/shard_map/convert_element_type | solution.py:93
  94.2 16.1 %attn_bwd.3.g = bf16[3,512,1024]{2,1,0:T(8,128)(2,1)} custom-call(bf16[2,1024,512]{2,1,0:T(8,128)(2,1)} %get-tuple-element.93.k.v, bf16[3,512,1024]{2,1,0:T(8,128)(2,1)} %get-tuple-element.94.qt.vt.kt, bf16[3,512,1024]{2,1,0:T(8,128)(2,1)} %get-tuple-element.94.qt.vt.kt, bf16[512,1024]{1,0:T(8,128)(2,1)} %get-tuple-element.115.gt, ...), custom_call_target="tpu_custom_call", output_to_operand_aliasing={{}: (7, {})} | custom-call | flops 12884901888 | bytes 12582912 | tf_op jit(solution)/shard_map/attn_bwd/pallas_call | solution.py:672
  110.3 2.1 %add_convert_fusion.3 = bf16[1,320,512]{2,1,0:T(8,128)(2,1)} fusion(bf16[2,320,512]{2,1,0:T(8,128)(2,1)S(1)} %collective-permute-done.17, bf16[4,592,512]{2,1,0:T(8,128)(2,1)} %collective-permute-done.16, bf16[4,592,512]{2,1,0:T(8,128)(2,1)S(1)} %copy-done.3), kind=kLoop, calls=%fused_computation.7 | loop fusion | flops 983040 | bytes 1310720 | tf_op jit(solution)/shard_map/convert_element_type | solution.py:93
  113.8 1.8 %add_convert_fusion.5 = bf16[1,272,512]{2,1,0:T(8,128)(2,1)} fusion(bf16[2,272,512]{2,1,0:T(8,128)(2,1)S(1)} %collective-permute-done.18, bf16[4,592,512]{2,1,0:T(8,128)(2,1)} %collective-permute-done.16, bf16[4,592,512]{2,1,0:T(8,128)(2,1)S(1)} %copy-done.3), kind=kLoop, calls=%fused_computation.9 | loop fusion | flops 835584 | bytes 1114112 | tf_op jit(solution)/shard_map/convert_element_type | solution.py:93
  116.4 5.6 %wqkv.1 = (bf16[4,208,512]{2,1,0:T(8,128)(2,1)}, bf16[4,208,512]{2,1,0:T(8,128)(2,1)}) custom-call(s32[1]{0:T(128)} %bitcast.me, bf16[512,1024]{1,0:T(8,128)(2,1)} %get-tuple-element.120.xht, bf16[3,512,1024]{2,1,0:T(8,128)(2,1)} %attn_bwd.3.g), custom_call_target="tpu_custom_call" | custom-call | flops 1610612736 | bytes 5242880 | tf_op jit(solution)/shard_map/wqkv/pallas_call | solution.py:709
  133.4 3.2 %collective-permute-done.21 = bf16[296,512]{1,0:T(8,128)(2,1)S(1)} collective-permute-done((bf16[296,512]{1,0:T(8,128)(2,1)S(1)}, bf16[296,512]{1,0:T(8,128)(2,1)S(1)}, u32[]{:S(2)}, u32[]{:S(2)}) %collective-permute-start.21) | collective-permute-done | bytes 303136 | tf_op jit(solution)/shard_map/ppermute | solution.py:39
  137.0 2.7 %collective-permute-start.27 = (bf16[296,512]{1,0:T(8,128)(2,1)S(1)}, bf16[296,512]{1,0:T(8,128)(2,1)S(1)}, u32[]{:S(2)}, u32[]{:S(2)}) collective-permute-start(bf16[296,512]{1,0:T(8,128)(2,1)S(1)} %fusion.5), channel_id=1, source_target_pairs={{0,16},{8,24},{16,0},{24,8},{1,17},{9,25},{17,1},{25,9},{2,18},{10... | collective-permute-start | bytes 909320 | tf_op jit(solution)/shard_map/ppermute | solution.py:39
  139.7 7.0 %back.1 = f32[1024,512]{1,0:T(8,128)} custom-call(bf16[1024,512]{1,0:T(8,128)(2,1)} %bitcast.43, bf16[1,512]{1,0:T(2,128)(2,1)} %step.4, f32[8,512]{1,0:T(8,128)} %get-tuple-element.91.vec, bf16[3,512,1024]{2,1,0:T(8,128)(2,1)} %attn_bwd.3.g, f32[1024,512]{1,0:T(8,128)} %get-tuple-element.135.gx1, bf16[512,1536]{1,0:T(8,128)(2,1)} %get-tuple-element.136.refs_0_), custom_call_target="tpu_custom_call" | custom-call | flops 1610612736 | bytes 7340032 | tf_op jit(solution)/shard_map/back/pallas_call | solution.py:736
  149.5 3.9 %collective-permute-done.27 = bf16[296,512]{1,0:T(8,128)(2,1)S(1)} collective-permute-done((bf16[296,512]{1,0:T(8,128)(2,1)S(1)}, bf16[296,512]{1,0:T(8,128)(2,1)S(1)}, u32[]{:S(2)}, u32[]{:S(2)}) %collective-permute-start.27) | collective-permute-done | bytes 303136 | tf_op jit(solution)/shard_map/ppermute | solution.py:39
  155.7 2.0 %collective-permute-start.28 = (bf16[104,512]{1,0:T(8,128)(2,1)S(1)}, bf16[104,512]{1,0:T(8,128)(2,1)S(1)}, u32[]{:S(2)}, u32[]{:S(2)}) collective-permute-start(bf16[104,512]{1,0:T(8,128)(2,1)S(1)} %dynamic-slice_add_fusion), channel_id=1, source_target_pairs={{0,16},{8,24},{16,0},{24,8},{1,17},{9,25},{17,1},{25,9},{2,18},{10... | collective-permute-start | bytes 319496 | tf_op jit(solution)/shard_map/ppermute | solution.py:39
  157.7 5.4 %collective-permute-done.28 = bf16[104,512]{1,0:T(8,128)(2,1)S(1)} collective-permute-done((bf16[104,512]{1,0:T(8,128)(2,1)S(1)}, bf16[104,512]{1,0:T(8,128)(2,1)S(1)}, u32[]{:S(2)}, u32[]{:S(2)}) %collective-permute-start.28) | collective-permute-done | bytes 106528 | tf_op jit(solution)/shard_map/ppermute | solution.py:39
  163.1 4.2 %collective-permute-start.29 = (bf16[104,512]{1,0:T(8,128)(2,1)S(1)}, bf16[104,512]{1,0:T(8,128)(2,1)S(1)}, u32[]{:S(2)}, u32[]{:S(2)}) collective-permute-start(bf16[104,512]{1,0:T(8,128)(2,1)S(1)} %add.127.s), channel_id=1, source_target_pairs={{0,8},{8,0},{16,24},{24,16},{1,9},{9,1},{17,25},{25,17},{2,10},{10... | collective-permute-start | bytes 319496 | tf_op jit(solution)/shard_map/ppermute | solution.py:39
  167.3 1.7 finish_rest.1
  (122 shorter events, 35.3 us)
Async XLA Ops:
  2.4 10.7 %collective-permute-start = (bf16[208,512]{1,0:T(8,128)(2,1)}, bf16[208,512]{1,0:T(8,128)(2,1)S(1)}, u32[]{:S(2)}, u32[]{:S(2)}) collective-permute-start(bf16[208,512]{1,0:T(8,128)(2,1)} %pack_first.1.refs_0_), channel_id=1, source_target_pairs={{0,2},{1,3},{2,0},{3,1},{4,6},{5,7},{6,4},{7,5},{8,10},{9,11},{10,... | collective-permute-start | bytes 638984 | tf_op jit(solution)/shard_map/ppermute | solution.py:43
  5.4 11.5 %collective-permute-start.1 = (bf16[208,512]{1,0:T(8,128)(2,1)}, bf16[208,512]{1,0:T(8,128)(2,1)S(1)}, u32[]{:S(2)}, u32[]{:S(2)}) collective-permute-start(bf16[208,512]{1,0:T(8,128)(2,1)} %pack_first.1.refs_0_), channel_id=1, source_target_pairs={{0,4},{1,5},{2,6},{3,7},{4,0},{5,1},{6,2},{7,3},{8,12},{9,13},{10,... | collective-permute-start | bytes 638984 | tf_op jit(solution)/shard_map/ppermute | solution.py:43
  6.9 10.0 %collective-permute-start.2 = (bf16[208,512]{1,0:T(8,128)(2,1)}, bf16[208,512]{1,0:T(8,128)(2,1)S(1)}, u32[]{:S(2)}, u32[]{:S(2)}) collective-permute-start(bf16[208,512]{1,0:T(8,128)(2,1)} %pack_first.1.refs_0_), channel_id=1, source_target_pairs={{0,6},{1,7},{2,4},{3,5},{4,2},{5,3},{6,0},{7,1},{8,14},{9,15},{10,... | collective-permute-start | bytes 638984 | tf_op jit(solution)/shard_map/ppermute | solution.py:43
  6.9 11.2 %collective-permute-start.3 = (bf16[208,512]{1,0:T(8,128)(2,1)}, bf16[208,512]{1,0:T(8,128)(2,1)S(1)}, u32[]{:S(2)}, u32[]{:S(2)}) collective-permute-start(bf16[208,512]{1,0:T(8,128)(2,1)} %pack_first.1.refs_0_), channel_id=1, source_target_pairs={{0,1},{1,0},{2,3},{3,2},{4,5},{5,4},{6,7},{7,6},{8,9},{9,8},{10,11... | collective-permute-start | bytes 638984 | tf_op jit(solution)/shard_map/ppermute | solution.py:43
  17.4 20.4 %collective-permute-start.7 = (bf16[576,512]{1,0:T(8,128)(2,1)}, bf16[576,512]{1,0:T(8,128)(2,1)S(1)}, u32[]{:S(2)}, u32[]{:S(2)}) collective-permute-start(bf16[576,512]{1,0:T(8,128)(2,1)} %pack_rest.1.refs_0_), channel_id=1, source_target_pairs={{0,2},{1,3},{2,0},{3,1},{4,6},{5,7},{6,4},{7,5},{8,10},{9,11},{10,... | collective-permute-start | bytes 1769480 | tf_op jit(solution)/shard_map/ppermute | solution.py:43
  18.1 20.3 %collective-permute-start.8 = (bf16[576,512]{1,0:T(8,128)(2,1)}, bf16[576,512]{1,0:T(8,128)(2,1)S(1)}, u32[]{:S(2)}, u32[]{:S(2)}) collective-permute-start(bf16[576,512]{1,0:T(8,128)(2,1)} %pack_rest.1.refs_0_), channel_id=1, source_target_pairs={{0,4},{1,5},{2,6},{3,7},{4,0},{5,1},{6,2},{7,3},{8,12},{9,13},{10,... | collective-permute-start | bytes 1769480 | tf_op jit(solution)/shard_map/ppermute | solution.py:43
  20.1 30.7 %collective-permute-start.9 = (bf16[576,512]{1,0:T(8,128)(2,1)}, bf16[576,512]{1,0:T(8,128)(2,1)S(1)}, u32[]{:S(2)}, u32[]{:S(2)}) collective-permute-start(bf16[576,512]{1,0:T(8,128)(2,1)} %pack_rest.1.refs_0_), channel_id=1, source_target_pairs={{0,1},{1,0},{2,3},{3,2},{4,5},{5,4},{6,7},{7,6},{8,9},{9,8},{10,11... | collective-permute-start | bytes 1769480 | tf_op jit(solution)/shard_map/ppermute | solution.py:43
  37.8 14.5 %collective-permute-start.10 = (bf16[576,512]{1,0:T(8,128)(2,1)S(1)}, bf16[576,512]{1,0:T(8,128)(2,1)S(1)}, u32[]{:S(2)}, u32[]{:S(2)}) collective-permute-start(bf16[576,512]{1,0:T(8,128)(2,1)S(1)} %collective-permute-done.7.refs_1_), channel_id=1, source_target_pairs={{0,1},{1,0},{2,3},{3,2},{4,5},{5,4},{6,7},{7,6},{8,9},{9,8},{10,11... | collective-permute-start | bytes 1769480 | tf_op jit(solution)/shard_map/ppermute | solution.py:43
  38.4 13.9 %collective-permute-start.11 = (bf16[576,512]{1,0:T(8,128)(2,1)S(1)}, bf16[576,512]{1,0:T(8,128)(2,1)S(1)}, u32[]{:S(2)}, u32[]{:S(2)}) collective-permute-start(bf16[576,512]{1,0:T(8,128)(2,1)S(1)} %collective-permute-done.8.refs_2_), channel_id=1, source_target_pairs={{0,1},{1,0},{2,3},{3,2},{4,5},{5,4},{6,7},{7,6},{8,9},{9,8},{10,11... | collective-permute-start | bytes 1769480 | tf_op jit(solution)/shard_map/ppermute | solution.py:43
  38.5 11.7 %collective-permute-start.13 = (bf16[288,512]{1,0:T(8,128)(2,1)S(1)}, bf16[288,512]{1,0:T(8,128)(2,1)S(1)}, u32[]{:S(2)}, u32[]{:S(2)}) collective-permute-start(bf16[288,512]{1,0:T(8,128)(2,1)S(1)} %slice.91), channel_id=1, source_target_pairs={{0,4},{1,5},{2,6},{3,7},{4,0},{5,1},{6,2},{7,3},{8,12},{9,13},{10,... | collective-permute-start | bytes 884744 | tf_op jit(solution)/shard_map/ppermute | solution.py:43
  39.2 11.0 %collective-permute-start.12 = (bf16[288,512]{1,0:T(8,128)(2,1)S(1)}, bf16[288,512]{1,0:T(8,128)(2,1)S(1)}, u32[]{:S(2)}, u32[]{:S(2)}) collective-permute-start(bf16[288,512]{1,0:T(8,128)(2,1)S(1)} %slice.90), channel_id=1, source_target_pairs={{0,2},{1,3},{2,0},{3,1},{4,6},{5,7},{6,4},{7,5},{8,10},{9,11},{10,... | collective-permute-start | bytes 884744 | tf_op jit(solution)/shard_map/ppermute | solution.py:43
  79.9 8.0 %collective-permute-start.16 = (bf16[4,592,512]{2,1,0:T(8,128)(2,1)}, bf16[4,592,512]{2,1,0:T(8,128)(2,1)}, u32[]{:S(2)}, u32[]{:S(2)}) collective-permute-start(bf16[4,592,512]{2,1,0:T(8,128)(2,1)} %get-tuple-element.110), channel_id=1, source_target_pairs={{0,1},{1,0},{2,3},{3,2},{4,5},{5,4},{6,7},{7,6},{8,9},{9,8},{10,11... | collective-permute-start | bytes 7274504 | tf_op jit(solution)/shard_map/ppermute | solution.py:43
  92.1 18.2 %collective-permute-start.18 = (bf16[2,272,512]{2,1,0:T(8,128)(2,1)}, bf16[2,272,512]{2,1,0:T(8,128)(2,1)S(1)}, u32[]{:S(2)}, u32[]{:S(2)}) collective-permute-start(bf16[2,272,512]{2,1,0:T(8,128)(2,1)} %add_convert_fusion.1), channel_id=1, source_target_pairs={{0,2},{1,3},{2,0},{3,1},{4,6},{5,7},{6,4},{7,5},{8,10},{9,11},{10,... | collective-permute-start | bytes 1671176 | tf_op jit(solution)/shard_map/ppermute | solution.py:43
  92.8 17.4 %collective-permute-start.17 = (bf16[2,320,512]{2,1,0:T(8,128)(2,1)}, bf16[2,320,512]{2,1,0:T(8,128)(2,1)S(1)}, u32[]{:S(2)}, u32[]{:S(2)}) collective-permute-start(bf16[2,320,512]{2,1,0:T(8,128)(2,1)} %add_convert_fusion), channel_id=1, source_target_pairs={{0,4},{1,5},{2,6},{3,7},{4,0},{5,1},{6,2},{7,3},{8,12},{9,13},{10,... | collective-permute-start | bytes 1966088 | tf_op jit(solution)/shard_map/ppermute | solution.py:43
  112.4 11.9 %collective-permute-start.19 = (bf16[1,320,512]{2,1,0:T(8,128)(2,1)}, bf16[1,320,512]{2,1,0:T(8,128)(2,1)}, u32[]{:S(2)}, u32[]{:S(2)}) collective-permute-start(bf16[1,320,512]{2,1,0:T(8,128)(2,1)} %add_convert_fusion.3), channel_id=1, source_target_pairs={{0,2},{1,3},{2,0},{3,1},{4,6},{5,7},{6,4},{7,5},{8,10},{9,11},{10,... | collective-permute-start | bytes 983048 | tf_op jit(solution)/shard_map/ppermute | solution.py:43
  115.6 8.7 %collective-permute-start.20 = (bf16[1,272,512]{2,1,0:T(8,128)(2,1)}, bf16[1,272,512]{2,1,0:T(8,128)(2,1)}, u32[]{:S(2)}, u32[]{:S(2)}) collective-permute-start(bf16[1,272,512]{2,1,0:T(8,128)(2,1)} %add_convert_fusion.5), channel_id=1, source_target_pairs={{0,4},{1,5},{2,6},{3,7},{4,0},{5,1},{6,2},{7,3},{8,12},{9,13},{10,... | collective-permute-start | bytes 835592 | tf_op jit(solution)/shard_map/ppermute | solution.py:43
  127.0 9.6 %collective-permute-start.21 = (bf16[296,512]{1,0:T(8,128)(2,1)S(1)}, bf16[296,512]{1,0:T(8,128)(2,1)S(1)}, u32[]{:S(2)}, u32[]{:S(2)}) collective-permute-start(bf16[296,512]{1,0:T(8,128)(2,1)S(1)} %fusion.3), channel_id=1, source_target_pairs={{0,8},{8,0},{16,24},{24,16},{1,9},{9,1},{17,25},{25,17},{2,10},{10... | collective-permute-start | bytes 909320 | tf_op jit(solution)/shard_map/ppermute | solution.py:39
  129.8 16.8 %collective-permute-start.23 = (bf16[208,512]{1,0:T(8,128)(2,1)S(1)}, bf16[208,512]{1,0:T(8,128)(2,1)S(1)}, u32[]{:S(2)}, u32[]{:S(2)}) collective-permute-start(bf16[208,512]{1,0:T(8,128)(2,1)S(1)} %get-tuple-element.157), channel_id=1, source_target_pairs={{0,6},{1,7},{2,4},{3,5},{4,2},{5,3},{6,0},{7,1},{8,14},{9,15},{10,... | collective-permute-start | bytes 638984 | tf_op jit(solution)/shard_map/ppermute | solution.py:43
  131.1 15.6 %collective-permute-start.24 = (bf16[208,512]{1,0:T(8,128)(2,1)S(1)}, bf16[208,512]{1,0:T(8,128)(2,1)S(1)}, u32[]{:S(2)}, u32[]{:S(2)}) collective-permute-start(bf16[208,512]{1,0:T(8,128)(2,1)S(1)} %get-tuple-element.158), channel_id=1, source_target_pairs={{0,4},{1,5},{2,6},{3,7},{4,0},{5,1},{6,2},{7,3},{8,12},{9,13},{10,... | collective-permute-start | bytes 638984 | tf_op jit(solution)/shard_map/ppermute | solution.py:43
  131.9 14.7 %collective-permute-start.25 = (bf16[208,512]{1,0:T(8,128)(2,1)S(1)}, bf16[208,512]{1,0:T(8,128)(2,1)S(1)}, u32[]{:S(2)}, u32[]{:S(2)}) collective-permute-start(bf16[208,512]{1,0:T(8,128)(2,1)S(1)} %get-tuple-element.159), channel_id=1, source_target_pairs={{0,2},{1,3},{2,0},{3,1},{4,6},{5,7},{6,4},{7,5},{8,10},{9,11},{10,... | collective-permute-start | bytes 638984 | tf_op jit(solution)/shard_map/ppermute | solution.py:43
  137.0 16.3 %collective-permute-start.27 = (bf16[296,512]{1,0:T(8,128)(2,1)S(1)}, bf16[296,512]{1,0:T(8,128)(2,1)S(1)}, u32[]{:S(2)}, u32[]{:S(2)}) collective-permute-start(bf16[296,512]{1,0:T(8,128)(2,1)S(1)} %fusion.5), channel_id=1, source_target_pairs={{0,16},{8,24},{16,0},{24,8},{1,17},{9,25},{17,1},{25,9},{2,18},{10... | collective-permute-start | bytes 909320 | tf_op jit(solution)/shard_map/ppermute | solution.py:39
  147.9 7.8 %collective-permute-start.26 = (bf16[104,512]{1,0:T(8,128)(2,1)S(1)}, bf16[104,512]{1,0:T(8,128)(2,1)S(1)}, u32[]{:S(2)}, u32[]{:S(2)}) collective-permute-start(bf16[104,512]{1,0:T(8,128)(2,1)S(1)} %constant_dynamic-slice_fusion), channel_id=1, source_target_pairs={{0,8},{8,0},{16,24},{24,16},{1,9},{9,1},{17,25},{25,17},{2,10},{10... | collective-permute-start | bytes 319496 | tf_op jit(solution)/shard_map/ppermute | solution.py:39
  153.5 13.9 %collective-permute-start.30 = (bf16[296,512]{1,0:T(8,128)(2,1)S(1)}, bf16[296,512]{1,0:T(8,128)(2,1)S(1)}, u32[]{:S(2)}, u32[]{:S(2)}) collective-permute-start(bf16[296,512]{1,0:T(8,128)(2,1)S(1)} %add.125.s), channel_id=1, source_target_pairs={{0,8},{8,0},{16,24},{24,16},{1,9},{9,1},{17,25},{25,17},{2,10},{10... | collective-permute-start | bytes 909320 | tf_op jit(solution)/shard_map/ppermute | solution.py:39
  155.7 7.4 %collective-permute-start.28 = (bf16[104,512]{1,0:T(8,128)(2,1)S(1)}, bf16[104,512]{1,0:T(8,128)(2,1)S(1)}, u32[]{:S(2)}, u32[]{:S(2)}) collective-permute-start(bf16[104,512]{1,0:T(8,128)(2,1)S(1)} %dynamic-slice_add_fusion), channel_id=1, source_target_pairs={{0,16},{8,24},{16,0},{24,8},{1,17},{9,25},{17,1},{25,9},{2,18},{10... | collective-permute-start | bytes 319496 | tf_op jit(solution)/shard_map/ppermute | solution.py:39
  (32 other events, 194.6 us)

commit v12 on v9

--- a/solution.py
+++ b/solution.py
@@ -52,30 +52,6 @@
     far = [(k, swap(x, k)) for k in range(2, n, 2)]
     out += [(k, 0, after(y, *gate) if gate else y) for k, y in far]
     return out + [(k ^ 1, 0, swap(y, 1)) for k, _, y in out]
-
-
-def gather_forward(x, n, gate1, gate2):
-    R = x.shape[0]
-    cut = R // 2 // 16 * 16
-    near = []
-    far = []
-    halves = {}
-    for k in sorted(range(2, n, 2), key=lambda k: (bin(k).count("1"), k)):
-        if bin(k).count("1") == 1:
-            y = after(swap(x, k), gate1)
-            near.append((k, 0, y))
-            halves[k] = (y[:cut], y[cut:])
-        else:
-            low = k & -k
-            high = 1 << (k.bit_length() - 1)
-            a = swap(halves[k ^ low][0], low)
-            b = swap(halves[k ^ high][1], high)
-            far += [(k, 0, a), (k, cut, b)]
-            halves[k] = (a, b)
-    near = [(0, 0, x)] + near
-    late = [(k, r0, after(a, gate2)) for k, r0, a in far]
-    out = near + [(k ^ 1, r0, swap(a, 1)) for k, r0, a in near]
-    return out + late + [(k ^ 1, r0, swap(a, 1)) for k, r0, a in late]
 
 
 def add16(a, b):
@@ -756,10 +732,8 @@
     nx, xht = start(tok, step)
     pieces = gather_direct(packs[0], n, xht, pack2)
     kv, qkvt, w, vec, upb = front(mes, nx, pieces, n, FF)
-    fw = attn_fwd(lengths, kv, qkvt, 0, NP // 2, [])
-    fw2 = attn_fwd(lengths, kv, qkvt, NP // 2, NP // 2, fw)
-    et, mixed, mixedt, mixedf, linv = fw2
-    pieces2 = gather_forward(after(pack2, *[a for _, _, a in pieces[1:]]), n, fw[4], linv)
+    et, mixed, mixedt, mixedf, linv = attn_fwd(lengths, kv, qkvt, 0, NP, [])
+    pieces2 = gather_direct(after(pack2, xht), n, linv)
     out, gx1, gmt, keep, send = ffn(lengths, mes, tok, step, vec, upb, cot, mixed, mixedt, pieces2, n)
     bwd = lambda p, c, g, *deps: attn_bwd(kv, qkvt, after(gmt, *deps) if deps else gmt, mixedf, linv, et, p, c, g)
     ra = rf + r

time: 164 us -> 160 us (0.976)
  Pallas kernels: 101 us -> 97.3 us
    pallas_call x2 -> x1, Pallas kernels: 19.3 us -> 16.5 us  [attn_fwd(): pl.pallas_call(functools.partial(attn_fwd_body, HD, bi, min(256, T), p0),...]
    ppermute x25 -> x23, starting transfers between devices: 19.1 us -> 18.4 us  [swap(): return lax.ppermute(x, 'shard', xor_perm(lax.axis_size('shard'), k))]
    ppermute x25 -> x23, waiting for transfers between devices: 7.96 us -> 7.86 us  [swap(): return lax.ppermute(x, 'shard', xor_perm(lax.axis_size('shard'), k))]
  transfers between devices with their start and end apart: 31 -> 29, of which waited for: 12 -> 11; matrix products, arithmetic and copies ran while one was open for 2% -> 2% of each run, Pallas kernels for 43% -> 42%
where the time goes in v12:
time: 160 us
  Pallas kernels  97.3 us (61%)
  starting transfers between devices  31.2 us (20%)
  waiting for transfers between devices  20.6 us (13%)
  other arithmetic  7.5 us (5%)
  between operations  1.64 us (1%)
    pallas_call x1, Pallas kernels, ffn(): pl.pallas_call(functools.partial(ffn_body, n, meta, min(1024, FF)), grid_...  26.3 us
    pallas_call x2, Pallas kernels, attn_bwd(): pl.pallas_call(functools.partial(attn_bwd_body, HD, 1.0 / math.sqrt(HD),...  23.8 us
    ppermute x23, starting transfers between devices, swap(): return lax.ppermute(x, 'shard', xor_perm(lax.axis_size('shard'), k))  18.4 us
    pallas_call x1, Pallas kernels, attn_fwd(): pl.pallas_call(functools.partial(attn_fwd_body, HD, bi, min(256, T), p0),...  16.5 us
    ppermute x6, starting transfers between devices, rep_perm(): return lax.ppermute(x, 'rep', xor_perm(lax.axis_size('rep'), b))  12.8 us
    ppermute x6, waiting for transfers between devices, rep_perm(): return lax.ppermute(x, 'rep', xor_perm(lax.axis_size('rep'), b))  12.8 us
    ppermute x23, waiting for transfers between devices, swap(): return lax.ppermute(x, 'shard', xor_perm(lax.axis_size('shard'), k))  7.86 us
    pallas_call x1, Pallas kernels, front(): pl.pallas_call(functools.partial(front_body, scale, n, meta), grid_spec=p...  7 us
  transfers between devices with their start and end apart: 29, of which 11 were waited for; matrix products, arithmetic and copies ran while one was open for 2% of the time, Pallas kernels for 42%

profile of v12, /device:TPU:0, one launch (start us, length us, event | category | flops | bytes accessed | tf_op | source)
XLA Modules:
  0.0 159.8 jit_solution(8104348967436806747)
XLA Ops:
  0.7 1.8 %pack_first.1.refs_0_ = bf16[208,512]{1,0:T(8,128)(2,1)} custom-call(s32[1]{0:T(128)} %bitcast.me, bf16[64,1536]{1,0:T(8,128)(2,1)} %w.3, bf16[2,128]{1,0:T(2,128)(2,1)} %bitcast.47, bf16[1,64]{1,0:T(2,128)(2,1)} %bitcast.39, bf16[1,64]{1,0:T(2,128)(2,1)} %bitcast.41, bf16[1,64]{1,0:T(2,128)(2,1)} %bitcast.48, bf16[1,64]{1,0:T(2,128)(2,1)} %bitcast.49, ...), custom_call_target="tpu_custom_call" | custom-call | bytes 393216 | tf_op jit(solution)/shard_map/pack_first/pallas_call | solution.py:125
  2.4 2.9 %collective-permute-start = (bf16[208,512]{1,0:T(8,128)(2,1)}, bf16[208,512]{1,0:T(8,128)(2,1)S(1)}, u32[]{:S(2)}, u32[]{:S(2)}) collective-permute-start(bf16[208,512]{1,0:T(8,128)(2,1)} %pack_first.1.refs_0_), channel_id=1, source_target_pairs={{0,2},{1,3},{2,0},{3,1},{4,6},{5,7},{6,4},{7,5},{8,10},{9,11},{10,... | collective-permute-start | bytes 638984 | tf_op jit(solution)/shard_map/ppermute | solution.py:43
  6.9 1.9 %pack_rest.1.refs_0_ = bf16[576,512]{1,0:T(8,128)(2,1)} custom-call(bf16[64,512]{1,0:T(8,128)(2,1)} %wo.1, bf16[64,2048]{1,0:T(8,128)(2,1)} %wu.1, bf16[256,512]{1,0:T(8,128)(2,1)} %wd.1), custom_call_target="tpu_custom_call" | custom-call | bytes 524288 | tf_op jit(solution)/shard_map/pack_rest/pallas_call | solution.py:143
  8.8 4.2 %start.1 = (f32[1024,512]{1,0:T(8,128)}, bf16[512,1024]{1,0:T(8,128)(2,1)}) custom-call(bf16[1024,512]{1,0:T(8,128)(2,1)} %bitcast.43, bf16[1,512]{1,0:T(2,128)(2,1)} %step.4), custom_call_target="tpu_custom_call" | custom-call | flops 10485760 | bytes 4194304 | tf_op jit(solution)/shard_map/start/pallas_call | solution.py:285
  13.6 3.3 %collective-permute-done.1.refs_2_ = bf16[208,512]{1,0:T(8,128)(2,1)S(1)} collective-permute-done((bf16[208,512]{1,0:T(8,128)(2,1)}, bf16[208,512]{1,0:T(8,128)(2,1)S(1)}, u32[]{:S(2)}, u32[]{:S(2)}) %collective-permute-start.1) | collective-permute-done | bytes 213024 | tf_op jit(solution)/shard_map/ppermute | solution.py:43
  22.4 7.0 %front.1 = (bf16[2,1024,512]{2,1,0:T(8,128)(2,1)}, bf16[3,512,1024]{2,1,0:T(8,128)(2,1)}, bf16[512,1536]{1,0:T(8,128)(2,1)}, f32[8,512]{1,0:T(8,128)}, f32[1,2048]{1,0:T(1,128)}) custom-call(s32[1]{0:T(128)} %bitcast.me, f32[1024,512]{1,0:T(8,128)} %get-tuple-element.70.nx, bf16[208,512]{1,0:T(8,128)(2,1)} %pack_first.1.refs_0_, ...), custom_call_target="tpu_custom_call" | custom-call | flops 1610612736 | bytes 6291456 | tf_op jit(solution)/shard_map/front/pallas_call | solution.py:358
  29.4 16.5 %attn_fwd.1 = (bf16[8,1024,1024]{2,1,0:T(8,128)(2,1)}, bf16[1024,512]{1,0:T(8,128)(2,1)}, bf16[512,1024]{1,0:T(8,128)(2,1)}, f32[512,1024]{1,0:T(8,128)}, f32[4,8,1024]{2,1,0:T(8,128)}) custom-call(s32[1]{0:T(128)S(6)} %copy.34.ln, bf16[2,1024,512]{2,1,0:T(8,128)(2,1)} %get-tuple-element.77.k.v, bf16[3,512,1024]{2,1,0:T(8,128)(2,1)} %get-tuple-element.78.qt.vt.kt, ...), custom_call_target="tpu_custom_call" | custom-call | flops 8589934592 | bytes 16777216 | tf_op jit(solution)/shard_map/attn_fwd/pallas_call | solution.py:448
  50.6 26.3 %ffn.1 = (bf16[1024,512]{1,0:T(8,128)(2,1)}, f32[1024,512]{1,0:T(8,128)}, bf16[512,1024]{1,0:T(8,128)(2,1)}, bf16[4,592,512]{2,1,0:T(8,128)(2,1)}, bf16[4,592,512]{2,1,0:T(8,128)(2,1)}) custom-call(s32[1]{0:T(128)S(6)} %copy.34.ln, s32[1]{0:T(128)} %bitcast.me, bf16[1024,512]{1,0:T(8,128)(2,1)} %bitcast.44, bf16[1,512]{1,0:T(2,128)(2,1)} %step.4, ...), custom_call_target="tpu_custom_call" | custom-call | flops 14495514624 | bytes 8388608 | tf_op jit(solution)/shard_map/ffn/pallas_call | solution.py:604
  77.3 7.8 %attn_bwd.2.refs_0_ = bf16[3,512,1024]{2,1,0:T(8,128)(2,1)} custom-call(bf16[2,1024,512]{2,1,0:T(8,128)(2,1)} %get-tuple-element.77.k.v, bf16[3,512,1024]{2,1,0:T(8,128)(2,1)} %get-tuple-element.78.qt.vt.kt, bf16[3,512,1024]{2,1,0:T(8,128)(2,1)} %get-tuple-element.78.qt.vt.kt, bf16[512,1024]{1,0:T(8,128)(2,1)} %get-tuple-element.93.gt, ...), custom_call_target="tpu_custom_call" | custom-call | flops 4294967296 | bytes 4194304 | tf_op jit(solution)/shard_map/attn_bwd/pallas_call | solution.py:648
  85.1 2.2 %slice_add_fusion.2 = (bf16[2,272,512]{2,1,0:T(8,128)(2,1)S(1)}, bf16[2,272,512]{2,1,0:T(8,128)(2,1)}) fusion(bf16[4,592,512]{2,1,0:T(8,128)(2,1)} %collective-permute-done.14, bf16[4,592,512]{2,1,0:T(8,128)(2,1)S(1)} %copy-done.3), kind=kLoop, calls=%fused_computation.6 | loop fusion | flops 557056 | bytes 3342336 | tf_op jit(solution)/shard_map/add | solution.py:58
  87.3 2.2 %slice_add_fusion = (bf16[2,320,512]{2,1,0:T(8,128)(2,1)}, bf16[2,320,512]{2,1,0:T(8,128)(2,1)S(1)}) fusion(bf16[4,592,512]{2,1,0:T(8,128)(2,1)} %collective-permute-done.14, bf16[4,592,512]{2,1,0:T(8,128)(2,1)S(1)} %copy-done.3), kind=kLoop, calls=%fused_computation.4 | loop fusion | flops 655360 | bytes 3932160 | tf_op jit(solution)/shard_map/add | solution.py:58
  91.6 16.0 %attn_bwd.3.g = bf16[3,512,1024]{2,1,0:T(8,128)(2,1)} custom-call(bf16[2,1024,512]{2,1,0:T(8,128)(2,1)} %get-tuple-element.77.k.v, bf16[3,512,1024]{2,1,0:T(8,128)(2,1)} %get-tuple-element.78.qt.vt.kt, bf16[3,512,1024]{2,1,0:T(8,128)(2,1)} %get-tuple-element.78.qt.vt.kt, bf16[512,1024]{1,0:T(8,128)(2,1)} %get-tuple-element.93.gt, ...), custom_call_target="tpu_custom_call", output_to_operand_aliasing={{}: (7, {})} | custom-call | flops 12884901888 | bytes 12582912 | tf_op jit(solution)/shard_map/attn_bwd/pallas_call | solution.py:648
  110.0 5.6 %wqkv.1 = (bf16[4,208,512]{2,1,0:T(8,128)(2,1)}, bf16[4,208,512]{2,1,0:T(8,128)(2,1)}) custom-call(s32[1]{0:T(128)} %bitcast.me, bf16[512,1024]{1,0:T(8,128)(2,1)} %get-tuple-element.96.xht, bf16[3,512,1024]{2,1,0:T(8,128)(2,1)} %attn_bwd.3.g), custom_call_target="tpu_custom_call" | custom-call | flops 1610612736 | bytes 5242880 | tf_op jit(solution)/shard_map/wqkv/pallas_call | solution.py:685
  118.9 1.6 %collective-permute-start.19 = (bf16[296,512]{1,0:T(8,128)(2,1)S(1)}, bf16[296,512]{1,0:T(8,128)(2,1)S(1)}, u32[]{:S(2)}, u32[]{:S(2)}) collective-permute-start(bf16[296,512]{1,0:T(8,128)(2,1)S(1)} %fusion.3), channel_id=1, source_target_pairs={{0,8},{8,0},{16,24},{24,16},{1,9},{9,1},{17,25},{25,17},{2,10},{10... | collective-permute-start | bytes 909320 | tf_op jit(solution)/shard_map/ppermute | solution.py:39
  121.3 2.2 %collective-permute-start.21 = (bf16[208,512]{1,0:T(8,128)(2,1)}, bf16[208,512]{1,0:T(8,128)(2,1)S(1)}, u32[]{:S(2)}, u32[]{:S(2)}) collective-permute-start(bf16[208,512]{1,0:T(8,128)(2,1)} %get-tuple-element.129), channel_id=1, source_target_pairs={{0,6},{1,7},{2,4},{3,5},{4,2},{5,3},{6,0},{7,1},{8,14},{9,15},{10,... | collective-permute-start | bytes 638984 | tf_op jit(solution)/shard_map/ppermute | solution.py:43
  124.8 2.0 %collective-permute-done.19 = bf16[296,512]{1,0:T(8,128)(2,1)S(1)} collective-permute-done((bf16[296,512]{1,0:T(8,128)(2,1)S(1)}, bf16[296,512]{1,0:T(8,128)(2,1)S(1)}, u32[]{:S(2)}, u32[]{:S(2)}) %collective-permute-start.19) | collective-permute-done | bytes 303136 | tf_op jit(solution)/shard_map/ppermute | solution.py:39
  127.2 2.7 %collective-permute-start.25 = (bf16[296,512]{1,0:T(8,128)(2,1)S(1)}, bf16[296,512]{1,0:T(8,128)(2,1)S(1)}, u32[]{:S(2)}, u32[]{:S(2)}) collective-permute-start(bf16[296,512]{1,0:T(8,128)(2,1)S(1)} %fusion.5), channel_id=1, source_target_pairs={{0,16},{8,24},{16,0},{24,8},{1,17},{9,25},{17,1},{25,9},{2,18},{10... | collective-permute-start | bytes 909320 | tf_op jit(solution)/shard_map/ppermute | solution.py:39
  129.9 7.0 %back.1 = f32[1024,512]{1,0:T(8,128)} custom-call(bf16[1024,512]{1,0:T(8,128)(2,1)} %bitcast.45, bf16[1,512]{1,0:T(2,128)(2,1)} %step.4, f32[8,512]{1,0:T(8,128)} %get-tuple-element.75.vec, bf16[3,512,1024]{2,1,0:T(8,128)(2,1)} %attn_bwd.3.g, f32[1024,512]{1,0:T(8,128)} %get-tuple-element.103.gx1, bf16[512,1536]{1,0:T(8,128)(2,1)} %get-tuple-element.104.refs_0_), custom_call_target="tpu_custom_call" | custom-call | flops 1610612736 | bytes 7340032 | tf_op jit(solution)/shard_map/back/pallas_call | solution.py:712
  137.0 1.6 %collective-permute-start.24 = (bf16[104,512]{1,0:T(8,128)(2,1)S(1)}, bf16[104,512]{1,0:T(8,128)(2,1)S(1)}, u32[]{:S(2)}, u32[]{:S(2)}) collective-permute-start(bf16[104,512]{1,0:T(8,128)(2,1)S(1)} %constant_dynamic-slice_fusion), channel_id=1, source_target_pairs={{0,8},{8,0},{16,24},{24,16},{1,9},{9,1},{17,25},{25,17},{2,10},{10... | collective-permute-start | bytes 319496 | tf_op jit(solution)/shard_map/ppermute | solution.py:39
  138.7 3.0 %collective-permute-done.25 = bf16[296,512]{1,0:T(8,128)(2,1)S(1)} collective-permute-done((bf16[296,512]{1,0:T(8,128)(2,1)S(1)}, bf16[296,512]{1,0:T(8,128)(2,1)S(1)}, u32[]{:S(2)}, u32[]{:S(2)}) %collective-permute-start.25) | collective-permute-done | bytes 303136 | tf_op jit(solution)/shard_map/ppermute | solution.py:39
  144.0 2.0 %collective-permute-start.26 = (bf16[104,512]{1,0:T(8,128)(2,1)S(1)}, bf16[104,512]{1,0:T(8,128)(2,1)S(1)}, u32[]{:S(2)}, u32[]{:S(2)}) collective-permute-start(bf16[104,512]{1,0:T(8,128)(2,1)S(1)} %dynamic-slice_add_fusion), channel_id=1, source_target_pairs={{0,16},{8,24},{16,0},{24,8},{1,17},{9,25},{17,1},{25,9},{2,18},{10... | collective-permute-start | bytes 319496 | tf_op jit(solution)/shard_map/ppermute | solution.py:39
  146.0 5.4 %collective-permute-done.26 = bf16[104,512]{1,0:T(8,128)(2,1)S(1)} collective-permute-done((bf16[104,512]{1,0:T(8,128)(2,1)S(1)}, bf16[104,512]{1,0:T(8,128)(2,1)S(1)}, u32[]{:S(2)}, u32[]{:S(2)}) %collective-permute-start.26) | collective-permute-done | bytes 106528 | tf_op jit(solution)/shard_map/ppermute | solution.py:39
  151.4 4.2 %collective-permute-start.27 = (bf16[104,512]{1,0:T(8,128)(2,1)S(1)}, bf16[104,512]{1,0:T(8,128)(2,1)S(1)}, u32[]{:S(2)}, u32[]{:S(2)}) collective-permute-start(bf16[104,512]{1,0:T(8,128)(2,1)S(1)} %add.119.s), channel_id=1, source_target_pairs={{0,8},{8,0},{16,24},{24,16},{1,9},{9,1},{17,25},{25,17},{2,10},{10... | collective-permute-start | bytes 319496 | tf_op jit(solution)/shard_map/ppermute | solution.py:39
  155.7 1.7 %finish_rest.1 = (f32[256,512]{1,0:T(8,128)}, f32[64,2048]{1,0:T(8,128)}, f32[64,512]{1,0:T(8,128)}, f32[1,256]{1,0:T(1,128)}, f32[1,64]{1,0:T(1,128)}, /*index=...) custom-call(s32[2]{0:T(128)S(1)} %pad_add_fusion.ids, bf16[296,512]{1,0:T(8,128)(2,1)S(1)} %add.117.s, ...), custom_call_target="tpu_custom_call" | custom-call | bytes 1212416 | tf_op jit(solution)/shard_map/finish_rest/pallas_call | solution.py:201
  (99 shorter events, 27.1 us)
Async XLA Ops:
  2.4 10.6 %collective-permute-start = (bf16[208,512]{1,0:T(8,128)(2,1)}, bf16[208,512]{1,0:T(8,128)(2,1)S(1)}, u32[]{:S(2)}, u32[]{:S(2)}) collective-permute-start(bf16[208,512]{1,0:T(8,128)(2,1)} %pack_first.1.refs_0_), channel_id=1, source_target_pairs={{0,2},{1,3},{2,0},{3,1},{4,6},{5,7},{6,4},{7,5},{8,10},{9,11},{10,... | collective-permute-start | bytes 638984 | tf_op jit(solution)/shard_map/ppermute | solution.py:43
  5.4 11.5 %collective-permute-start.1 = (bf16[208,512]{1,0:T(8,128)(2,1)}, bf16[208,512]{1,0:T(8,128)(2,1)S(1)}, u32[]{:S(2)}, u32[]{:S(2)}) collective-permute-start(bf16[208,512]{1,0:T(8,128)(2,1)} %pack_first.1.refs_0_), channel_id=1, source_target_pairs={{0,4},{1,5},{2,6},{3,7},{4,0},{5,1},{6,2},{7,3},{8,12},{9,13},{10,... | collective-permute-start | bytes 638984 | tf_op jit(solution)/shard_map/ppermute | solution.py:43
  6.9 10.0 %collective-permute-start.2 = (bf16[208,512]{1,0:T(8,128)(2,1)}, bf16[208,512]{1,0:T(8,128)(2,1)S(1)}, u32[]{:S(2)}, u32[]{:S(2)}) collective-permute-start(bf16[208,512]{1,0:T(8,128)(2,1)} %pack_first.1.refs_0_), channel_id=1, source_target_pairs={{0,6},{1,7},{2,4},{3,5},{4,2},{5,3},{6,0},{7,1},{8,14},{9,15},{10,... | collective-permute-start | bytes 638984 | tf_op jit(solution)/shard_map/ppermute | solution.py:43
  6.9 12.6 %collective-permute-start.3 = (bf16[208,512]{1,0:T(8,128)(2,1)}, bf16[208,512]{1,0:T(8,128)(2,1)S(1)}, u32[]{:S(2)}, u32[]{:S(2)}) collective-permute-start(bf16[208,512]{1,0:T(8,128)(2,1)} %pack_first.1.refs_0_), channel_id=1, source_target_pairs={{0,1},{1,0},{2,3},{3,2},{4,5},{5,4},{6,7},{7,6},{8,9},{9,8},{10,11... | collective-permute-start | bytes 638984 | tf_op jit(solution)/shard_map/ppermute | solution.py:43
  13.0 7.3 %collective-permute-start.4 = (bf16[208,512]{1,0:T(8,128)(2,1)S(1)}, bf16[208,512]{1,0:T(8,128)(2,1)S(1)}, u32[]{:S(2)}, u32[]{:S(2)}) collective-permute-start(bf16[208,512]{1,0:T(8,128)(2,1)S(1)} %collective-permute-done.refs_1_), channel_id=1, source_target_pairs={{0,1},{1,0},{2,3},{3,2},{4,5},{5,4},{6,7},{7,6},{8,9},{9,8},{10,11... | collective-permute-start | bytes 638984 | tf_op jit(solution)/shard_map/ppermute | solution.py:43
  17.4 28.5 %collective-permute-start.9 = (bf16[576,512]{1,0:T(8,128)(2,1)}, bf16[576,512]{1,0:T(8,128)(2,1)S(1)}, u32[]{:S(2)}, u32[]{:S(2)}) collective-permute-start(bf16[576,512]{1,0:T(8,128)(2,1)} %pack_rest.1.refs_0_), channel_id=1, source_target_pairs={{0,6},{1,7},{2,4},{3,5},{4,2},{5,3},{6,0},{7,1},{8,14},{9,15},{10,... | collective-permute-start | bytes 1769480 | tf_op jit(solution)/shard_map/ppermute | solution.py:43
  19.5 26.9 %collective-permute-start.8 = (bf16[576,512]{1,0:T(8,128)(2,1)}, bf16[576,512]{1,0:T(8,128)(2,1)S(1)}, u32[]{:S(2)}, u32[]{:S(2)}) collective-permute-start(bf16[576,512]{1,0:T(8,128)(2,1)} %pack_rest.1.refs_0_), channel_id=1, source_target_pairs={{0,4},{1,5},{2,6},{3,7},{4,0},{5,1},{6,2},{7,3},{8,12},{9,13},{10,... | collective-permute-start | bytes 1769480 | tf_op jit(solution)/shard_map/ppermute | solution.py:43
  20.3 26.2 %collective-permute-start.7 = (bf16[576,512]{1,0:T(8,128)(2,1)}, bf16[576,512]{1,0:T(8,128)(2,1)S(1)}, u32[]{:S(2)}, u32[]{:S(2)}) collective-permute-start(bf16[576,512]{1,0:T(8,128)(2,1)} %pack_rest.1.refs_0_), channel_id=1, source_target_pairs={{0,2},{1,3},{2,0},{3,1},{4,6},{5,7},{6,4},{7,5},{8,10},{9,11},{10,... | collective-permute-start | bytes 1769480 | tf_op jit(solution)/shard_map/ppermute | solution.py:43
  21.6 25.4 %collective-permute-start.10 = (bf16[576,512]{1,0:T(8,128)(2,1)}, bf16[576,512]{1,0:T(8,128)(2,1)S(1)}, u32[]{:S(2)}, u32[]{:S(2)}) collective-permute-start(bf16[576,512]{1,0:T(8,128)(2,1)} %pack_rest.1.refs_0_), channel_id=1, source_target_pairs={{0,1},{1,0},{2,3},{3,2},{4,5},{5,4},{6,7},{7,6},{8,9},{9,8},{10,11... | collective-permute-start | bytes 1769480 | tf_op jit(solution)/shard_map/ppermute | solution.py:43
  76.9 8.3 %collective-permute-start.14 = (bf16[4,592,512]{2,1,0:T(8,128)(2,1)}, bf16[4,592,512]{2,1,0:T(8,128)(2,1)}, u32[]{:S(2)}, u32[]{:S(2)}) collective-permute-start(bf16[4,592,512]{2,1,0:T(8,128)(2,1)} %get-tuple-element.88), channel_id=1, source_target_pairs={{0,1},{1,0},{2,3},{3,2},{4,5},{5,4},{6,7},{7,6},{8,9},{9,8},{10,11... | collective-permute-start | bytes 7274504 | tf_op jit(solution)/shard_map/ppermute | solution.py:43
  89.6 18.0 %collective-permute-start.16 = (bf16[2,272,512]{2,1,0:T(8,128)(2,1)}, bf16[2,272,512]{2,1,0:T(8,128)(2,1)S(1)}, u32[]{:S(2)}, u32[]{:S(2)}) collective-permute-start(bf16[2,272,512]{2,1,0:T(8,128)(2,1)} %get-tuple-element.126), channel_id=1, source_target_pairs={{0,2},{1,3},{2,0},{3,1},{4,6},{5,7},{6,4},{7,5},{8,10},{9,11},{10,... | collective-permute-start | bytes 1671176 | tf_op jit(solution)/shard_map/ppermute | solution.py:43
  90.3 17.3 %collective-permute-start.15 = (bf16[2,320,512]{2,1,0:T(8,128)(2,1)}, bf16[2,320,512]{2,1,0:T(8,128)(2,1)S(1)}, u32[]{:S(2)}, u32[]{:S(2)}) collective-permute-start(bf16[2,320,512]{2,1,0:T(8,128)(2,1)} %get-tuple-element.127), channel_id=1, source_target_pairs={{0,4},{1,5},{2,6},{3,7},{4,0},{5,1},{6,2},{7,3},{8,12},{9,13},{10,... | collective-permute-start | bytes 1966088 | tf_op jit(solution)/shard_map/ppermute | solution.py:43
  107.8 8.3 %collective-permute-start.18 = (bf16[1,272,512]{2,1,0:T(8,128)(2,1)S(1)}, bf16[1,272,512]{2,1,0:T(8,128)(2,1)}, u32[]{:S(2)}, u32[]{:S(2)}) collective-permute-start(bf16[1,272,512]{2,1,0:T(8,128)(2,1)S(1)} %get-tuple-element.135), channel_id=1, source_target_pairs={{0,4},{1,5},{2,6},{3,7},{4,0},{5,1},{6,2},{7,3},{8,12},{9,13},{10,... | collective-permute-start | bytes 835592 | tf_op jit(solution)/shard_map/ppermute | solution.py:43
  108.5 8.9 %collective-permute-start.17 = (bf16[1,320,512]{2,1,0:T(8,128)(2,1)S(1)}, bf16[1,320,512]{2,1,0:T(8,128)(2,1)S(1)}, u32[]{:S(2)}, u32[]{:S(2)}) collective-permute-start(bf16[1,320,512]{2,1,0:T(8,128)(2,1)S(1)} %get-tuple-element.132), channel_id=1, source_target_pairs={{0,2},{1,3},{2,0},{3,1},{4,6},{5,7},{6,4},{7,5},{8,10},{9,11},{10,... | collective-permute-start | bytes 983048 | tf_op jit(solution)/shard_map/ppermute | solution.py:43
  115.6 4.9 %collective-permute-start.20 = (bf16[4,208,512]{2,1,0:T(8,128)(2,1)}, bf16[4,208,512]{2,1,0:T(8,128)(2,1)S(1)}, u32[]{:S(2)}, u32[]{:S(2)}) collective-permute-start(bf16[4,208,512]{2,1,0:T(8,128)(2,1)} %get-tuple-element.100), channel_id=1, source_target_pairs={{0,1},{1,0},{2,3},{3,2},{4,5},{5,4},{6,7},{7,6},{8,9},{9,8},{10,11... | collective-permute-start | bytes 2555912 | tf_op jit(solution)/shard_map/ppermute | solution.py:43
  118.9 7.9 %collective-permute-start.19 = (bf16[296,512]{1,0:T(8,128)(2,1)S(1)}, bf16[296,512]{1,0:T(8,128)(2,1)S(1)}, u32[]{:S(2)}, u32[]{:S(2)}) collective-permute-start(bf16[296,512]{1,0:T(8,128)(2,1)S(1)} %fusion.3), channel_id=1, source_target_pairs={{0,8},{8,0},{16,24},{24,16},{1,9},{9,1},{17,25},{25,17},{2,10},{10... | collective-permute-start | bytes 909320 | tf_op jit(solution)/shard_map/ppermute | solution.py:39
  121.3 15.6 %collective-permute-start.21 = (bf16[208,512]{1,0:T(8,128)(2,1)}, bf16[208,512]{1,0:T(8,128)(2,1)S(1)}, u32[]{:S(2)}, u32[]{:S(2)}) collective-permute-start(bf16[208,512]{1,0:T(8,128)(2,1)} %get-tuple-element.129), channel_id=1, source_target_pairs={{0,6},{1,7},{2,4},{3,5},{4,2},{5,3},{6,0},{7,1},{8,14},{9,15},{10,... | collective-permute-start | bytes 638984 | tf_op jit(solution)/shard_map/ppermute | solution.py:43
  123.5 13.3 %collective-permute-start.22 = (bf16[208,512]{1,0:T(8,128)(2,1)S(1)}, bf16[208,512]{1,0:T(8,128)(2,1)S(1)}, u32[]{:S(2)}, u32[]{:S(2)}) collective-permute-start(bf16[208,512]{1,0:T(8,128)(2,1)S(1)} %get-tuple-element.130), channel_id=1, source_target_pairs={{0,4},{1,5},{2,6},{3,7},{4,0},{5,1},{6,2},{7,3},{8,12},{9,13},{10,... | collective-permute-start | bytes 638984 | tf_op jit(solution)/shard_map/ppermute | solution.py:43
  124.0 12.8 %collective-permute-start.23 = (bf16[208,512]{1,0:T(8,128)(2,1)S(1)}, bf16[208,512]{1,0:T(8,128)(2,1)S(1)}, u32[]{:S(2)}, u32[]{:S(2)}) collective-permute-start(bf16[208,512]{1,0:T(8,128)(2,1)S(1)} %get-tuple-element.131), channel_id=1, source_target_pairs={{0,2},{1,3},{2,0},{3,1},{4,6},{5,7},{6,4},{7,5},{8,10},{9,11},{10,... | collective-permute-start | bytes 638984 | tf_op jit(solution)/shard_map/ppermute | solution.py:43
  127.2 14.5 %collective-permute-start.25 = (bf16[296,512]{1,0:T(8,128)(2,1)S(1)}, bf16[296,512]{1,0:T(8,128)(2,1)S(1)}, u32[]{:S(2)}, u32[]{:S(2)}) collective-permute-start(bf16[296,512]{1,0:T(8,128)(2,1)S(1)} %fusion.5), channel_id=1, source_target_pairs={{0,16},{8,24},{16,0},{24,8},{1,17},{9,25},{17,1},{25,9},{2,18},{10... | collective-permute-start | bytes 909320 | tf_op jit(solution)/shard_map/ppermute | solution.py:39
  137.0 6.9 %collective-permute-start.24 = (bf16[104,512]{1,0:T(8,128)(2,1)S(1)}, bf16[104,512]{1,0:T(8,128)(2,1)S(1)}, u32[]{:S(2)}, u32[]{:S(2)}) collective-permute-start(bf16[104,512]{1,0:T(8,128)(2,1)S(1)} %constant_dynamic-slice_fusion), channel_id=1, source_target_pairs={{0,8},{8,0},{16,24},{24,16},{1,9},{9,1},{17,25},{25,17},{2,10},{10... | collective-permute-start | bytes 319496 | tf_op jit(solution)/shard_map/ppermute | solution.py:39
  141.8 13.9 %collective-permute-start.28 = (bf16[296,512]{1,0:T(8,128)(2,1)S(1)}, bf16[296,512]{1,0:T(8,128)(2,1)S(1)}, u32[]{:S(2)}, u32[]{:S(2)}) collective-permute-start(bf16[296,512]{1,0:T(8,128)(2,1)S(1)} %add.117.s), channel_id=1, source_target_pairs={{0,8},{8,0},{16,24},{24,16},{1,9},{9,1},{17,25},{25,17},{2,10},{10... | collective-permute-start | bytes 909320 | tf_op jit(solution)/shard_map/ppermute | solution.py:39
  144.0 7.4 %collective-permute-start.26 = (bf16[104,512]{1,0:T(8,128)(2,1)S(1)}, bf16[104,512]{1,0:T(8,128)(2,1)S(1)}, u32[]{:S(2)}, u32[]{:S(2)}) collective-permute-start(bf16[104,512]{1,0:T(8,128)(2,1)S(1)} %dynamic-slice_add_fusion), channel_id=1, source_target_pairs={{0,16},{8,24},{16,0},{24,8},{1,17},{9,25},{17,1},{25,9},{2,18},{10... | collective-permute-start | bytes 319496 | tf_op jit(solution)/shard_map/ppermute | solution.py:39
  151.4 6.9 %collective-permute-start.27 = (bf16[104,512]{1,0:T(8,128)(2,1)S(1)}, bf16[104,512]{1,0:T(8,128)(2,1)S(1)}, u32[]{:S(2)}, u32[]{:S(2)}) collective-permute-start(bf16[104,512]{1,0:T(8,128)(2,1)S(1)} %add.119.s), channel_id=1, source_target_pairs={{0,8},{8,0},{16,24},{24,16},{1,9},{9,1},{17,25},{25,17},{2,10},{10... | collective-permute-start | bytes 319496 | tf_op jit(solution)/shard_map/ppermute | solution.py:39
  (24 other events, 134.2 us)

commit v13 on v12

--- a/solution.py
+++ b/solution.py
@@ -15,8 +15,8 @@
 def dot_t(a, b):
     return lax.dot_general(a, b, (((1,), (1,)), ((), ())), preferred_element_type=f32)
 
-def cp(n=1, vmem=100):
-    return pltpu.CompilerParams(dimension_semantics=("arbitrary",) * n, vmem_limit_bytes=60 * 1024 * 1024)
+def cp(mib=60):
+    return pltpu.CompilerParams(dimension_semantics=("arbitrary",), vmem_limit_bytes=mib << 20)
 
 def norm(x):
     c = x - jnp.mean(x, axis=-1, keepdims=True)
@@ -443,10 +443,10 @@
     HD = D // HEADS
     PW = 2 * HD
     NP = D // PW
-    bi = min(512, T)
+    bi = T
     prev = list(prev)
     return pl.pallas_call(
-        functools.partial(attn_fwd_body, HD, bi, min(256, T), p0),
+        functools.partial(attn_fwd_body, HD, bi, min(512, T), p0),
         grid_spec=pltpu.PrefetchScalarGridSpec(
             num_scalar_prefetch=1, grid=(cnt,),
             in_specs=[pl.BlockSpec((None, T, PW), lambda p, r: (0, 0, p0 + p)), pl.BlockSpec((None, PW, T), lambda p, r: (0, p0 + p, 0)), pl.BlockSpec((None, PW, T), lambda p, r: (2, p0 + p, 0))] + [ANY] * len(prev),
@@ -609,7 +609,7 @@
             out_specs=[rows, rows, pl.BlockSpec((D, bm), lambda i, l, m: (0, i)), ANY, ANY],
             scratch_shapes=[V((D, D), bf16), V((D, FF), bf16), V((FF, D), bf16), V((T, FF), bf16), V((T, FF), bf16), V((D, T), bf16), V((D, T), bf16), V((T, D), bf16), V((8, D), f32), V((1, FF), f32), V((nf, D, D), bf16), V((nf, D, D), bf16), V((D, D), bf16), V((VROWS, D), bf16), V((D, T), bf16), pltpu.SemaphoreType.DMA((16 * len(pieces),)), pltpu.SemaphoreType.DMA((n * (nf + 3) + 1,))]),
         out_shape=[S((T, D), bf16), S((T, D), f32), S((D, T), bf16), B, B],
-        compiler_params=cp(), name="ffn", cost_estimate=cost(2 * T * D * (6 * FF + 3 * D), 16 * T * D, T * FF),
+        compiler_params=cp(48), name="ffn", cost_estimate=cost(2 * T * D * (6 * FF + 3 * D), 16 * T * D, T * FF),
     )(ln, me, tok, step, vec, upb, cot, mixed, mixedt, *[a for _, _, a in pieces])
 
 

time: 160 us -> 160 us (level)
  transfers between devices with their start and end apart: 29 -> 29, of which waited for: 11 -> 12; matrix products, arithmetic and copies ran while one was open for 2% -> 2% of each run, Pallas kernels for 42% -> 41%
where the time goes in v13:
time: 160 us
  Pallas kernels  95.7 us (60%)
  starting transfers between devices  31.2 us (20%)
  waiting for transfers between devices  21.8 us (14%)
  other arithmetic  7.53 us (5%)
  local copies, waits for them, and re-layouts  1.77 us (1%)
  between operations  1.65 us (1%)
    pallas_call x1, Pallas kernels, ffn(): pl.pallas_call(functools.partial(ffn_body, n, meta, min(1024, FF)), grid_...  26.1 us
    pallas_call x2, Pallas kernels, attn_bwd(): pl.pallas_call(functools.partial(attn_bwd_body, HD, 1.0 / math.sqrt(HD),...  23.8 us
    ppermute x23, starting transfers between devices, swap(): return lax.ppermute(x, 'shard', xor_perm(lax.axis_size('shard'), k))  18.3 us
    pallas_call x1, Pallas kernels, attn_fwd(): pl.pallas_call(functools.partial(attn_fwd_body, HD, bi, min(512, T), p0),...  15.1 us
    ppermute x6, starting transfers between devices, rep_perm(): return lax.ppermute(x, 'rep', xor_perm(lax.axis_size('rep'), b))  13 us
    ppermute x6, waiting for transfers between devices, rep_perm(): return lax.ppermute(x, 'rep', xor_perm(lax.axis_size('rep'), b))  12.5 us
    ppermute x23, waiting for transfers between devices, swap(): return lax.ppermute(x, 'shard', xor_perm(lax.axis_size('shard'), k))  9.3 us
    pallas_call x1, Pallas kernels, front(): pl.pallas_call(functools.partial(front_body, scale, n, meta), grid_spec=p...  6.99 us
  transfers between devices with their start and end apart: 29, of which 12 were waited for; matrix products, arithmetic and copies ran while one was open for 2% of the time, Pallas kernels for 41%

profile of v13, /device:TPU:0, one launch (start us, length us, event | category | flops | bytes accessed | tf_op | source)
XLA Modules:
  0.0 159.7 jit_solution(1242195526858290406)
XLA Ops:
  0.7 1.8 %pack_first.1.refs_0_ = bf16[208,512]{1,0:T(8,128)(2,1)} custom-call(s32[1]{0:T(128)} %bitcast.me, bf16[64,1536]{1,0:T(8,128)(2,1)} %w.3, bf16[2,128]{1,0:T(2,128)(2,1)} %bitcast.47, bf16[1,64]{1,0:T(2,128)(2,1)} %bitcast.39, bf16[1,64]{1,0:T(2,128)(2,1)} %bitcast.41, bf16[1,64]{1,0:T(2,128)(2,1)} %bitcast.48, bf16[1,64]{1,0:T(2,128)(2,1)} %bitcast.49, ...), custom_call_target="tpu_custom_call" | custom-call | bytes 393216 | tf_op jit(solution)/shard_map/pack_first/pallas_call | solution.py:125
  2.4 2.9 %collective-permute-start = (bf16[208,512]{1,0:T(8,128)(2,1)}, bf16[208,512]{1,0:T(8,128)(2,1)S(1)}, u32[]{:S(2)}, u32[]{:S(2)}) collective-permute-start(bf16[208,512]{1,0:T(8,128)(2,1)} %pack_first.1.refs_0_), channel_id=1, source_target_pairs={{0,2},{1,3},{2,0},{3,1},{4,6},{5,7},{6,4},{7,5},{8,10},{9,11},{10,... | collective-permute-start | bytes 638984 | tf_op jit(solution)/shard_map/ppermute | solution.py:43
  6.9 1.9 %pack_rest.1.refs_0_ = bf16[576,512]{1,0:T(8,128)(2,1)} custom-call(bf16[64,512]{1,0:T(8,128)(2,1)} %wo.1, bf16[64,2048]{1,0:T(8,128)(2,1)} %wu.1, bf16[256,512]{1,0:T(8,128)(2,1)} %wd.1), custom_call_target="tpu_custom_call" | custom-call | bytes 524288 | tf_op jit(solution)/shard_map/pack_rest/pallas_call | solution.py:143
  8.8 4.2 %start.1 = (f32[1024,512]{1,0:T(8,128)}, bf16[512,1024]{1,0:T(8,128)(2,1)}) custom-call(bf16[1024,512]{1,0:T(8,128)(2,1)} %bitcast.43, bf16[1,512]{1,0:T(2,128)(2,1)} %step.4), custom_call_target="tpu_custom_call" | custom-call | flops 10485760 | bytes 4194304 | tf_op jit(solution)/shard_map/start/pallas_call | solution.py:285
  13.6 3.3 %collective-permute-done.1.refs_2_ = bf16[208,512]{1,0:T(8,128)(2,1)S(1)} collective-permute-done((bf16[208,512]{1,0:T(8,128)(2,1)}, bf16[208,512]{1,0:T(8,128)(2,1)S(1)}, u32[]{:S(2)}, u32[]{:S(2)}) %collective-permute-start.1) | collective-permute-done | bytes 213024 | tf_op jit(solution)/shard_map/ppermute | solution.py:43
  22.4 7.0 %front.1 = (bf16[2,1024,512]{2,1,0:T(8,128)(2,1)}, bf16[3,512,1024]{2,1,0:T(8,128)(2,1)}, bf16[512,1536]{1,0:T(8,128)(2,1)}, f32[8,512]{1,0:T(8,128)}, f32[1,2048]{1,0:T(1,128)}) custom-call(s32[1]{0:T(128)} %bitcast.me, f32[1024,512]{1,0:T(8,128)} %get-tuple-element.70.nx, bf16[208,512]{1,0:T(8,128)(2,1)} %pack_first.1.refs_0_, ...), custom_call_target="tpu_custom_call" | custom-call | flops 1610612736 | bytes 6291456 | tf_op jit(solution)/shard_map/front/pallas_call | solution.py:358
  29.4 15.1 %attn_fwd.1 = (bf16[8,1024,1024]{2,1,0:T(8,128)(2,1)}, bf16[1024,512]{1,0:T(8,128)(2,1)}, bf16[512,1024]{1,0:T(8,128)(2,1)}, f32[512,1024]{1,0:T(8,128)}, f32[4,8,1024]{2,1,0:T(8,128)}) custom-call(s32[1]{0:T(128)S(6)} %copy.34.ln, bf16[2,1024,512]{2,1,0:T(8,128)(2,1)} %get-tuple-element.77.k.v, bf16[3,512,1024]{2,1,0:T(8,128)(2,1)} %get-tuple-element.78.qt.vt.kt, ...), custom_call_target="tpu_custom_call" | custom-call | flops 8589934592 | bytes 16777216 | tf_op jit(solution)/shard_map/attn_fwd/pallas_call | solution.py:448
  49.3 26.1 %ffn.1 = (bf16[1024,512]{1,0:T(8,128)(2,1)}, f32[1024,512]{1,0:T(8,128)}, bf16[512,1024]{1,0:T(8,128)(2,1)S(1)}, bf16[4,592,512]{2,1,0:T(8,128)(2,1)}, bf16[4,592,512]{2,1,0:T(8,128)(2,1)}) custom-call(s32[1]{0:T(128)S(6)} %copy.34.ln, s32[1]{0:T(128)} %bitcast.me, bf16[1024,512]{1,0:T(8,128)(2,1)} %bitcast.44, bf16[1,512]{1,0:T(2,128)(2,1)S(1)} %copy-done.4, ...), custom_call_target="tpu_custom_call" | custom-call | flops 14495514624 | bytes 8388608 | tf_op jit(solution)/shard_map/ffn/pallas_call | solution.py:604
  76.5 7.8 %attn_bwd.2.refs_0_ = bf16[3,512,1024]{2,1,0:T(8,128)(2,1)} custom-call(bf16[2,1024,512]{2,1,0:T(8,128)(2,1)} %get-tuple-element.77.k.v, bf16[3,512,1024]{2,1,0:T(8,128)(2,1)} %get-tuple-element.78.qt.vt.kt, bf16[3,512,1024]{2,1,0:T(8,128)(2,1)} %get-tuple-element.78.qt.vt.kt, bf16[512,1024]{1,0:T(8,128)(2,1)} %copy-done, f32[512,1024]{1,0:T(8,128)} %get-tuple-element.90.mt, ...), custom_call_target="tpu_custom_call" | custom-call | flops 4294967296 | bytes 4194304 | tf_op jit(solution)/shard_map/attn_bwd/pallas_call | solution.py:648
  84.3 2.2 %slice_add_fusion.2 = (bf16[2,272,512]{2,1,0:T(8,128)(2,1)S(1)}, bf16[2,272,512]{2,1,0:T(8,128)(2,1)}) fusion(bf16[4,592,512]{2,1,0:T(8,128)(2,1)} %collective-permute-done.14, bf16[4,592,512]{2,1,0:T(8,128)(2,1)S(1)} %copy-done.8), kind=kLoop, calls=%fused_computation.6 | loop fusion | flops 557056 | bytes 3342336 | tf_op jit(solution)/shard_map/add | solution.py:58
  86.5 2.3 %slice_add_fusion = (bf16[2,320,512]{2,1,0:T(8,128)(2,1)}, bf16[2,320,512]{2,1,0:T(8,128)(2,1)S(1)}) fusion(bf16[4,592,512]{2,1,0:T(8,128)(2,1)} %collective-permute-done.14, bf16[4,592,512]{2,1,0:T(8,128)(2,1)S(1)} %copy-done.8), kind=kLoop, calls=%fused_computation.4 | loop fusion | flops 655360 | bytes 3932160 | tf_op jit(solution)/shard_map/add | solution.py:58
  90.9 16.0 %attn_bwd.3.g = bf16[3,512,1024]{2,1,0:T(8,128)(2,1)} custom-call(bf16[2,1024,512]{2,1,0:T(8,128)(2,1)} %get-tuple-element.77.k.v, bf16[3,512,1024]{2,1,0:T(8,128)(2,1)} %get-tuple-element.78.qt.vt.kt, bf16[3,512,1024]{2,1,0:T(8,128)(2,1)} %get-tuple-element.78.qt.vt.kt, bf16[512,1024]{1,0:T(8,128)(2,1)} %copy-done, ...), custom_call_target="tpu_custom_call", output_to_operand_aliasing={{}: (7, {})} | custom-call | flops 12884901888 | bytes 12582912 | tf_op jit(solution)/shard_map/attn_bwd/pallas_call | solution.py:648
  109.5 5.6 %wqkv.1 = (bf16[4,208,512]{2,1,0:T(8,128)(2,1)}, bf16[4,208,512]{2,1,0:T(8,128)(2,1)}) custom-call(s32[1]{0:T(128)} %bitcast.me, bf16[512,1024]{1,0:T(8,128)(2,1)} %get-tuple-element.96.xht, bf16[3,512,1024]{2,1,0:T(8,128)(2,1)} %attn_bwd.3.g), custom_call_target="tpu_custom_call" | custom-call | flops 1610612736 | bytes 5242880 | tf_op jit(solution)/shard_map/wqkv/pallas_call | solution.py:685
  115.6 1.8 %collective-permute-done.17 = bf16[1,320,512]{2,1,0:T(8,128)(2,1)S(1)} collective-permute-done((bf16[1,320,512]{2,1,0:T(8,128)(2,1)S(1)}, bf16[1,320,512]{2,1,0:T(8,128)(2,1)S(1)}, u32[]{:S(2)}, u32[]{:S(2)}) %collective-permute-start.17) | collective-permute-done | bytes 327712 | tf_op jit(solution)/shard_map/ppermute | solution.py:43
  121.2 1.8 %collective-permute-start.21 = (bf16[208,512]{1,0:T(8,128)(2,1)}, bf16[208,512]{1,0:T(8,128)(2,1)S(1)}, u32[]{:S(2)}, u32[]{:S(2)}) collective-permute-start(bf16[208,512]{1,0:T(8,128)(2,1)} %get-tuple-element.129), channel_id=1, source_target_pairs={{0,6},{1,7},{2,4},{3,5},{4,2},{5,3},{6,0},{7,1},{8,14},{9,15},{10,... | collective-permute-start | bytes 638984 | tf_op jit(solution)/shard_map/ppermute | solution.py:43
  124.7 1.9 %collective-permute-done.19 = bf16[296,512]{1,0:T(8,128)(2,1)S(1)} collective-permute-done((bf16[296,512]{1,0:T(8,128)(2,1)S(1)}, bf16[296,512]{1,0:T(8,128)(2,1)S(1)}, u32[]{:S(2)}, u32[]{:S(2)}) %collective-permute-start.19) | collective-permute-done | bytes 303136 | tf_op jit(solution)/shard_map/ppermute | solution.py:39
  127.0 2.7 %collective-permute-start.25 = (bf16[296,512]{1,0:T(8,128)(2,1)S(1)}, bf16[296,512]{1,0:T(8,128)(2,1)S(1)}, u32[]{:S(2)}, u32[]{:S(2)}) collective-permute-start(bf16[296,512]{1,0:T(8,128)(2,1)S(1)} %fusion.5), channel_id=1, source_target_pairs={{0,16},{8,24},{16,0},{24,8},{1,17},{9,25},{17,1},{25,9},{2,18},{10... | collective-permute-start | bytes 909320 | tf_op jit(solution)/shard_map/ppermute | solution.py:39
  129.7 7.0 %back.1 = f32[1024,512]{1,0:T(8,128)} custom-call(bf16[1024,512]{1,0:T(8,128)(2,1)} %bitcast.45, bf16[1,512]{1,0:T(2,128)(2,1)} %step.4, f32[8,512]{1,0:T(8,128)} %get-tuple-element.75.vec, bf16[3,512,1024]{2,1,0:T(8,128)(2,1)} %attn_bwd.3.g, f32[1024,512]{1,0:T(8,128)} %get-tuple-element.103.gx1, bf16[512,1536]{1,0:T(8,128)(2,1)} %get-tuple-element.104.refs_0_), custom_call_target="tpu_custom_call" | custom-call | flops 1610612736 | bytes 7340032 | tf_op jit(solution)/shard_map/back/pallas_call | solution.py:712
  136.9 1.6 %collective-permute-start.24 = (bf16[104,512]{1,0:T(8,128)(2,1)S(1)}, bf16[104,512]{1,0:T(8,128)(2,1)S(1)}, u32[]{:S(2)}, u32[]{:S(2)}) collective-permute-start(bf16[104,512]{1,0:T(8,128)(2,1)S(1)} %constant_dynamic-slice_fusion), channel_id=1, source_target_pairs={{0,8},{8,0},{16,24},{24,16},{1,9},{9,1},{17,25},{25,17},{2,10},{10... | collective-permute-start | bytes 319496 | tf_op jit(solution)/shard_map/ppermute | solution.py:39
  138.6 2.9 %collective-permute-done.25 = bf16[296,512]{1,0:T(8,128)(2,1)S(1)} collective-permute-done((bf16[296,512]{1,0:T(8,128)(2,1)S(1)}, bf16[296,512]{1,0:T(8,128)(2,1)S(1)}, u32[]{:S(2)}, u32[]{:S(2)}) %collective-permute-start.25) | collective-permute-done | bytes 303136 | tf_op jit(solution)/shard_map/ppermute | solution.py:39
  143.8 2.1 %collective-permute-start.26 = (bf16[104,512]{1,0:T(8,128)(2,1)S(1)}, bf16[104,512]{1,0:T(8,128)(2,1)S(1)}, u32[]{:S(2)}, u32[]{:S(2)}) collective-permute-start(bf16[104,512]{1,0:T(8,128)(2,1)S(1)} %dynamic-slice_add_fusion), channel_id=1, source_target_pairs={{0,16},{8,24},{16,0},{24,8},{1,17},{9,25},{17,1},{25,9},{2,18},{10... | collective-permute-start | bytes 319496 | tf_op jit(solution)/shard_map/ppermute | solution.py:39
  145.8 5.4 %collective-permute-done.26 = bf16[104,512]{1,0:T(8,128)(2,1)S(1)} collective-permute-done((bf16[104,512]{1,0:T(8,128)(2,1)S(1)}, bf16[104,512]{1,0:T(8,128)(2,1)S(1)}, u32[]{:S(2)}, u32[]{:S(2)}) %collective-permute-start.26) | collective-permute-done | bytes 106528 | tf_op jit(solution)/shard_map/ppermute | solution.py:39
  151.2 4.2 %collective-permute-start.27 = (bf16[104,512]{1,0:T(8,128)(2,1)S(1)}, bf16[104,512]{1,0:T(8,128)(2,1)S(1)}, u32[]{:S(2)}, u32[]{:S(2)}) collective-permute-start(bf16[104,512]{1,0:T(8,128)(2,1)S(1)} %add.119.s), channel_id=1, source_target_pairs={{0,8},{8,0},{16,24},{24,16},{1,9},{9,1},{17,25},{25,17},{2,10},{10... | collective-permute-start | bytes 319496 | tf_op jit(solution)/shard_map/ppermute | solution.py:39
  155.5 1.7 %finish_rest.1 = (f32[256,512]{1,0:T(8,128)}, f32[64,2048]{1,0:T(8,128)}, f32[64,512]{1,0:T(8,128)}, f32[1,256]{1,0:T(1,128)}, f32[1,64]{1,0:T(1,128)}, /*index=...) custom-call(s32[2]{0:T(128)S(1)} %pad_add_fusion.ids, bf16[296,512]{1,0:T(8,128)(2,1)S(1)} %add.117.s, ...), custom_call_target="tpu_custom_call" | custom-call | bytes 1212416 | tf_op jit(solution)/shard_map/finish_rest/pallas_call | solution.py:201
  (95 shorter events, 28.9 us)
Async XLA Ops:
  2.4 10.6 %collective-permute-start = (bf16[208,512]{1,0:T(8,128)(2,1)}, bf16[208,512]{1,0:T(8,128)(2,1)S(1)}, u32[]{:S(2)}, u32[]{:S(2)}) collective-permute-start(bf16[208,512]{1,0:T(8,128)(2,1)} %pack_first.1.refs_0_), channel_id=1, source_target_pairs={{0,2},{1,3},{2,0},{3,1},{4,6},{5,7},{6,4},{7,5},{8,10},{9,11},{10,... | collective-permute-start | bytes 638984 | tf_op jit(solution)/shard_map/ppermute | solution.py:43
  5.4 11.5 %collective-permute-start.1 = (bf16[208,512]{1,0:T(8,128)(2,1)}, bf16[208,512]{1,0:T(8,128)(2,1)S(1)}, u32[]{:S(2)}, u32[]{:S(2)}) collective-permute-start(bf16[208,512]{1,0:T(8,128)(2,1)} %pack_first.1.refs_0_), channel_id=1, source_target_pairs={{0,4},{1,5},{2,6},{3,7},{4,0},{5,1},{6,2},{7,3},{8,12},{9,13},{10,... | collective-permute-start | bytes 638984 | tf_op jit(solution)/shard_map/ppermute | solution.py:43
  6.9 10.0 %collective-permute-start.2 = (bf16[208,512]{1,0:T(8,128)(2,1)}, bf16[208,512]{1,0:T(8,128)(2,1)S(1)}, u32[]{:S(2)}, u32[]{:S(2)}) collective-permute-start(bf16[208,512]{1,0:T(8,128)(2,1)} %pack_first.1.refs_0_), channel_id=1, source_target_pairs={{0,6},{1,7},{2,4},{3,5},{4,2},{5,3},{6,0},{7,1},{8,14},{9,15},{10,... | collective-permute-start | bytes 638984 | tf_op jit(solution)/shard_map/ppermute | solution.py:43
  6.9 12.6 %collective-permute-start.3 = (bf16[208,512]{1,0:T(8,128)(2,1)}, bf16[208,512]{1,0:T(8,128)(2,1)S(1)}, u32[]{:S(2)}, u32[]{:S(2)}) collective-permute-start(bf16[208,512]{1,0:T(8,128)(2,1)} %pack_first.1.refs_0_), channel_id=1, source_target_pairs={{0,1},{1,0},{2,3},{3,2},{4,5},{5,4},{6,7},{7,6},{8,9},{9,8},{10,11... | collective-permute-start | bytes 638984 | tf_op jit(solution)/shard_map/ppermute | solution.py:43
  13.0 7.3 %collective-permute-start.4 = (bf16[208,512]{1,0:T(8,128)(2,1)S(1)}, bf16[208,512]{1,0:T(8,128)(2,1)S(1)}, u32[]{:S(2)}, u32[]{:S(2)}) collective-permute-start(bf16[208,512]{1,0:T(8,128)(2,1)S(1)} %collective-permute-done.refs_1_), channel_id=1, source_target_pairs={{0,1},{1,0},{2,3},{3,2},{4,5},{5,4},{6,7},{7,6},{8,9},{9,8},{10,11... | collective-permute-start | bytes 638984 | tf_op jit(solution)/shard_map/ppermute | solution.py:43
  17.4 27.1 %collective-permute-start.9 = (bf16[576,512]{1,0:T(8,128)(2,1)}, bf16[576,512]{1,0:T(8,128)(2,1)S(1)}, u32[]{:S(2)}, u32[]{:S(2)}) collective-permute-start(bf16[576,512]{1,0:T(8,128)(2,1)} %pack_rest.1.refs_0_), channel_id=1, source_target_pairs={{0,6},{1,7},{2,4},{3,5},{4,2},{5,3},{6,0},{7,1},{8,14},{9,15},{10,... | collective-permute-start | bytes 1769480 | tf_op jit(solution)/shard_map/ppermute | solution.py:43
  19.5 26.9 %collective-permute-start.8 = (bf16[576,512]{1,0:T(8,128)(2,1)}, bf16[576,512]{1,0:T(8,128)(2,1)S(1)}, u32[]{:S(2)}, u32[]{:S(2)}) collective-permute-start(bf16[576,512]{1,0:T(8,128)(2,1)} %pack_rest.1.refs_0_), channel_id=1, source_target_pairs={{0,4},{1,5},{2,6},{3,7},{4,0},{5,1},{6,2},{7,3},{8,12},{9,13},{10,... | collective-permute-start | bytes 1769480 | tf_op jit(solution)/shard_map/ppermute | solution.py:43
  20.3 26.2 %collective-permute-start.7 = (bf16[576,512]{1,0:T(8,128)(2,1)}, bf16[576,512]{1,0:T(8,128)(2,1)S(1)}, u32[]{:S(2)}, u32[]{:S(2)}) collective-permute-start(bf16[576,512]{1,0:T(8,128)(2,1)} %pack_rest.1.refs_0_), channel_id=1, source_target_pairs={{0,2},{1,3},{2,0},{3,1},{4,6},{5,7},{6,4},{7,5},{8,10},{9,11},{10,... | collective-permute-start | bytes 1769480 | tf_op jit(solution)/shard_map/ppermute | solution.py:43
  21.6 25.3 %collective-permute-start.10 = (bf16[576,512]{1,0:T(8,128)(2,1)}, bf16[576,512]{1,0:T(8,128)(2,1)S(1)}, u32[]{:S(2)}, u32[]{:S(2)}) collective-permute-start(bf16[576,512]{1,0:T(8,128)(2,1)} %pack_rest.1.refs_0_), channel_id=1, source_target_pairs={{0,1},{1,0},{2,3},{3,2},{4,5},{5,4},{6,7},{7,6},{8,9},{9,8},{10,11... | collective-permute-start | bytes 1769480 | tf_op jit(solution)/shard_map/ppermute | solution.py:43
  76.4 7.9 %collective-permute-start.14 = (bf16[4,592,512]{2,1,0:T(8,128)(2,1)}, bf16[4,592,512]{2,1,0:T(8,128)(2,1)}, u32[]{:S(2)}, u32[]{:S(2)}) collective-permute-start(bf16[4,592,512]{2,1,0:T(8,128)(2,1)} %get-tuple-element.88), channel_id=1, source_target_pairs={{0,1},{1,0},{2,3},{3,2},{4,5},{5,4},{6,7},{7,6},{8,9},{9,8},{10,11... | collective-permute-start | bytes 7274504 | tf_op jit(solution)/shard_map/ppermute | solution.py:43
  88.8 18.1 %collective-permute-start.16 = (bf16[2,272,512]{2,1,0:T(8,128)(2,1)}, bf16[2,272,512]{2,1,0:T(8,128)(2,1)S(1)}, u32[]{:S(2)}, u32[]{:S(2)}) collective-permute-start(bf16[2,272,512]{2,1,0:T(8,128)(2,1)} %get-tuple-element.126), channel_id=1, source_target_pairs={{0,2},{1,3},{2,0},{3,1},{4,6},{5,7},{6,4},{7,5},{8,10},{9,11},{10,... | collective-permute-start | bytes 1671176 | tf_op jit(solution)/shard_map/ppermute | solution.py:43
  90.0 16.9 %collective-permute-start.15 = (bf16[2,320,512]{2,1,0:T(8,128)(2,1)}, bf16[2,320,512]{2,1,0:T(8,128)(2,1)S(1)}, u32[]{:S(2)}, u32[]{:S(2)}) collective-permute-start(bf16[2,320,512]{2,1,0:T(8,128)(2,1)} %get-tuple-element.127), channel_id=1, source_target_pairs={{0,4},{1,5},{2,6},{3,7},{4,0},{5,1},{6,2},{7,3},{8,12},{9,13},{10,... | collective-permute-start | bytes 1966088 | tf_op jit(solution)/shard_map/ppermute | solution.py:43
  107.0 8.5 %collective-permute-start.18 = (bf16[1,272,512]{2,1,0:T(8,128)(2,1)S(1)}, bf16[1,272,512]{2,1,0:T(8,128)(2,1)}, u32[]{:S(2)}, u32[]{:S(2)}) collective-permute-start(bf16[1,272,512]{2,1,0:T(8,128)(2,1)S(1)} %get-tuple-element.135), channel_id=1, source_target_pairs={{0,4},{1,5},{2,6},{3,7},{4,0},{5,1},{6,2},{7,3},{8,12},{9,13},{10,... | collective-permute-start | bytes 835592 | tf_op jit(solution)/shard_map/ppermute | solution.py:43
  108.2 9.1 %collective-permute-start.17 = (bf16[1,320,512]{2,1,0:T(8,128)(2,1)S(1)}, bf16[1,320,512]{2,1,0:T(8,128)(2,1)S(1)}, u32[]{:S(2)}, u32[]{:S(2)}) collective-permute-start(bf16[1,320,512]{2,1,0:T(8,128)(2,1)S(1)} %get-tuple-element.132), channel_id=1, source_target_pairs={{0,2},{1,3},{2,0},{3,1},{4,6},{5,7},{6,4},{7,5},{8,10},{9,11},{10,... | collective-permute-start | bytes 983048 | tf_op jit(solution)/shard_map/ppermute | solution.py:43
  115.1 5.4 %collective-permute-start.20 = (bf16[4,208,512]{2,1,0:T(8,128)(2,1)}, bf16[4,208,512]{2,1,0:T(8,128)(2,1)S(1)}, u32[]{:S(2)}, u32[]{:S(2)}) collective-permute-start(bf16[4,208,512]{2,1,0:T(8,128)(2,1)} %get-tuple-element.100), channel_id=1, source_target_pairs={{0,1},{1,0},{2,3},{3,2},{4,5},{5,4},{6,7},{7,6},{8,9},{9,8},{10,11... | collective-permute-start | bytes 2555912 | tf_op jit(solution)/shard_map/ppermute | solution.py:43
  118.8 7.8 %collective-permute-start.19 = (bf16[296,512]{1,0:T(8,128)(2,1)S(1)}, bf16[296,512]{1,0:T(8,128)(2,1)S(1)}, u32[]{:S(2)}, u32[]{:S(2)}) collective-permute-start(bf16[296,512]{1,0:T(8,128)(2,1)S(1)} %fusion.3), channel_id=1, source_target_pairs={{0,8},{8,0},{16,24},{24,16},{1,9},{9,1},{17,25},{25,17},{2,10},{10... | collective-permute-start | bytes 909320 | tf_op jit(solution)/shard_map/ppermute | solution.py:39
  121.2 15.5 %collective-permute-start.21 = (bf16[208,512]{1,0:T(8,128)(2,1)}, bf16[208,512]{1,0:T(8,128)(2,1)S(1)}, u32[]{:S(2)}, u32[]{:S(2)}) collective-permute-start(bf16[208,512]{1,0:T(8,128)(2,1)} %get-tuple-element.129), channel_id=1, source_target_pairs={{0,6},{1,7},{2,4},{3,5},{4,2},{5,3},{6,0},{7,1},{8,14},{9,15},{10,... | collective-permute-start | bytes 638984 | tf_op jit(solution)/shard_map/ppermute | solution.py:43
  123.0 13.7 %collective-permute-start.22 = (bf16[208,512]{1,0:T(8,128)(2,1)S(1)}, bf16[208,512]{1,0:T(8,128)(2,1)S(1)}, u32[]{:S(2)}, u32[]{:S(2)}) collective-permute-start(bf16[208,512]{1,0:T(8,128)(2,1)S(1)} %get-tuple-element.130), channel_id=1, source_target_pairs={{0,4},{1,5},{2,6},{3,7},{4,0},{5,1},{6,2},{7,3},{8,12},{9,13},{10,... | collective-permute-start | bytes 638984 | tf_op jit(solution)/shard_map/ppermute | solution.py:43
  123.5 13.2 %collective-permute-start.23 = (bf16[208,512]{1,0:T(8,128)(2,1)S(1)}, bf16[208,512]{1,0:T(8,128)(2,1)S(1)}, u32[]{:S(2)}, u32[]{:S(2)}) collective-permute-start(bf16[208,512]{1,0:T(8,128)(2,1)S(1)} %get-tuple-element.131), channel_id=1, source_target_pairs={{0,2},{1,3},{2,0},{3,1},{4,6},{5,7},{6,4},{7,5},{8,10},{9,11},{10,... | collective-permute-start | bytes 638984 | tf_op jit(solution)/shard_map/ppermute | solution.py:43
  127.0 14.5 %collective-permute-start.25 = (bf16[296,512]{1,0:T(8,128)(2,1)S(1)}, bf16[296,512]{1,0:T(8,128)(2,1)S(1)}, u32[]{:S(2)}, u32[]{:S(2)}) collective-permute-start(bf16[296,512]{1,0:T(8,128)(2,1)S(1)} %fusion.5), channel_id=1, source_target_pairs={{0,16},{8,24},{16,0},{24,8},{1,17},{9,25},{17,1},{25,9},{2,18},{10... | collective-permute-start | bytes 909320 | tf_op jit(solution)/shard_map/ppermute | solution.py:39
  136.9 6.8 %collective-permute-start.24 = (bf16[104,512]{1,0:T(8,128)(2,1)S(1)}, bf16[104,512]{1,0:T(8,128)(2,1)S(1)}, u32[]{:S(2)}, u32[]{:S(2)}) collective-permute-start(bf16[104,512]{1,0:T(8,128)(2,1)S(1)} %constant_dynamic-slice_fusion), channel_id=1, source_target_pairs={{0,8},{8,0},{16,24},{24,16},{1,9},{9,1},{17,25},{25,17},{2,10},{10... | collective-permute-start | bytes 319496 | tf_op jit(solution)/shard_map/ppermute | solution.py:39
  141.5 13.9 %collective-permute-start.28 = (bf16[296,512]{1,0:T(8,128)(2,1)S(1)}, bf16[296,512]{1,0:T(8,128)(2,1)S(1)}, u32[]{:S(2)}, u32[]{:S(2)}) collective-permute-start(bf16[296,512]{1,0:T(8,128)(2,1)S(1)} %add.117.s), channel_id=1, source_target_pairs={{0,8},{8,0},{16,24},{24,16},{1,9},{9,1},{17,25},{25,17},{2,10},{10... | collective-permute-start | bytes 909320 | tf_op jit(solution)/shard_map/ppermute | solution.py:39
  143.8 7.4 %collective-permute-start.26 = (bf16[104,512]{1,0:T(8,128)(2,1)S(1)}, bf16[104,512]{1,0:T(8,128)(2,1)S(1)}, u32[]{:S(2)}, u32[]{:S(2)}) collective-permute-start(bf16[104,512]{1,0:T(8,128)(2,1)S(1)} %dynamic-slice_add_fusion), channel_id=1, source_target_pairs={{0,16},{8,24},{16,0},{24,8},{1,17},{9,25},{17,1},{25,9},{2,18},{10... | collective-permute-start | bytes 319496 | tf_op jit(solution)/shard_map/ppermute | solution.py:39
  151.2 6.9 %collective-permute-start.27 = (bf16[104,512]{1,0:T(8,128)(2,1)S(1)}, bf16[104,512]{1,0:T(8,128)(2,1)S(1)}, u32[]{:S(2)}, u32[]{:S(2)}) collective-permute-start(bf16[104,512]{1,0:T(8,128)(2,1)S(1)} %add.119.s), channel_id=1, source_target_pairs={{0,8},{8,0},{16,24},{24,16},{1,9},{9,1},{17,25},{25,17},{2,10},{10... | collective-permute-start | bytes 319496 | tf_op jit(solution)/shard_map/ppermute | solution.py:39
  (22 other events, 197.8 us)

commit v14 on v13

--- a/solution.py
+++ b/solution.py
@@ -275,8 +275,10 @@
 
 def start_body(tok, step, nx, xht):
     n, _ = norm(tok[...].astype(f32) + step[...].astype(f32))
+    D = tok.shape[1]
     nx[...] = n
-    xht[...] = n.astype(bf16).T
+    xht[:D, :] = n.astype(bf16).T
+    xht[D:, :] = jnp.ones((16, tok.shape[0]), bf16)
 
 
 def start(tok, step, bm=256):
@@ -284,8 +286,8 @@
     rows = pl.BlockSpec((bm, D), lambda i: (i, 0))
     return pl.pallas_call(
         start_body, grid=(T // bm,),
-        in_specs=[rows, pl.BlockSpec((1, D), lambda i: (0, 0))], out_specs=[rows, pl.BlockSpec((D, bm), lambda i: (0, i))],
-        out_shape=[S((T, D), f32), S((D, T), bf16)], compiler_params=cp(), name="start", cost_estimate=cost(20 * T * D, 8 * T * D),
+        in_specs=[rows, pl.BlockSpec((1, D), lambda i: (0, 0))], out_specs=[rows, pl.BlockSpec((D + 16, bm), lambda i: (0, i))],
+        out_shape=[S((T, D), f32), S((D + 16, T), bf16)], compiler_params=cp(), name="start", cost_estimate=cost(20 * T * D, 8 * T * D),
     )(tok, step)
 
 
@@ -556,8 +558,8 @@
     out[...] = jnp.where(live, acc, 0.0).astype(bf16)
     gn = gh * row(v, 5)
     gx = gd.astype(f32) + rr * (gn - jnp.mean(gn, axis=-1, keepdims=True) - nx * jnp.mean(gn * nx, axis=-1, keepdims=True))
-    gx1[...] = gx
     gab = gx.astype(bf16)
+    gx1[...] = gab
     gattn[ro, :] = gab
     gmt[...] = dot_t(gab, wo[...]).astype(bf16).T
     s_ = lambda a: jnp.sum(a.astype(f32), axis=0, keepdims=True)
@@ -608,8 +610,8 @@
             in_specs=[rows, full(step), full(vec), full(upb), rows, rows, ANY] + [ANY] * len(pieces),
             out_specs=[rows, rows, pl.BlockSpec((D, bm), lambda i, l, m: (0, i)), ANY, ANY],
             scratch_shapes=[V((D, D), bf16), V((D, FF), bf16), V((FF, D), bf16), V((T, FF), bf16), V((T, FF), bf16), V((D, T), bf16), V((D, T), bf16), V((T, D), bf16), V((8, D), f32), V((1, FF), f32), V((nf, D, D), bf16), V((nf, D, D), bf16), V((D, D), bf16), V((VROWS, D), bf16), V((D, T), bf16), pltpu.SemaphoreType.DMA((16 * len(pieces),)), pltpu.SemaphoreType.DMA((n * (nf + 3) + 1,))]),
-        out_shape=[S((T, D), bf16), S((T, D), f32), S((D, T), bf16), B, B],
-        compiler_params=cp(48), name="ffn", cost_estimate=cost(2 * T * D * (6 * FF + 3 * D), 16 * T * D, T * FF),
+        out_shape=[S((T, D), bf16), S((T, D), bf16), S((D, T), bf16), B, B],
+        compiler_params=cp(49), name="ffn", cost_estimate=cost(2 * T * D * (6 * FF + 3 * D), 16 * T * D, T * FF),
     )(ln, me, tok, step, vec, upb, cot, mixed, mixedt, *[a for _, _, a in pieces])
 
 
@@ -662,8 +664,7 @@
     D = g.shape[0]
     r = D // n
     i0 = me[0]
-    x = jnp.concatenate([xht[...], jnp.ones((16, xht.shape[1]), bf16)], axis=0)
-    y = dot_t(x, g[...]).astype(bf16)
+    y = dot_t(xht[...], g[...]).astype(bf16)
     res[j] = y[:D]
     vr[...] = jnp.where(lax.broadcasted_iota(jnp.int32, vr.shape, 0) == j, y[D:], jnp.where(j == 0, jnp.zeros_like(y[D:]), vr[...]))
     for s in range(n):
@@ -680,13 +681,13 @@
 
 
 def wqkv(me, xht, g, n):
-    D, T = xht.shape
+    _, D, T = g.shape
     A = S((n // 2, 3 * (D // n) + VROWS, D), bf16)
     return pl.pallas_call(
         functools.partial(wqkv_body, n),
         grid_spec=pltpu.PrefetchScalarGridSpec(
             num_scalar_prefetch=1, grid=(3,),
-            in_specs=[pl.BlockSpec((D, T), lambda j, m: (0, 0)), pl.BlockSpec((None, D, T), lambda j, m: (j, 0, 0))],
+            in_specs=[pl.BlockSpec((D + 16, T), lambda j, m: (0, 0)), pl.BlockSpec((None, D, T), lambda j, m: (j, 0, 0))],
             out_specs=[ANY] * 2,
             scratch_shapes=[pltpu.VMEM((3, D, D), bf16), pltpu.VMEM((VROWS, D), bf16), pltpu.SemaphoreType.DMA((4 * n,))]),
         out_shape=[A, A],
@@ -702,7 +703,7 @@
     nx, rr = norm(x)
     gt = sum(dot(w[:, j * gw : (j + 1) * gw], g[j, q * gw : (q + 1) * gw, :]) for q, w in enumerate(ws) for j in range(3))
     gn = gt.T * row(vec[...], 0)
-    tg[...] = gx1[...] + rr * (gn - jnp.mean(gn, axis=-1, keepdims=True) - nx * jnp.mean(gn * nx, axis=-1, keepdims=True))
+    tg[...] = gx1[...].astype(f32) + rr * (gn - jnp.mean(gn, axis=-1, keepdims=True) - nx * jnp.mean(gn * nx, axis=-1, keepdims=True))
 
 
 def back(tok, step, vec, ws, g, gx1, bm=512):

time: 160 us -> 159 us (level)
  transfers between devices with their start and end apart: 29 -> 29, of which waited for: 12 -> 13; matrix products, arithmetic and copies ran while one was open for 2% -> 2% of each run, Pallas kernels for 41% -> 42%
where the time goes in v14:
time: 159 us; the launch traced here: 158 us
  Pallas kernels  95.5 us (60%)
  starting transfers between devices  30.8 us (19%)
  waiting for transfers between devices  22.3 us (14%)
  other arithmetic  7.52 us (5%)
  between operations  1.64 us (1%)
    pallas_call x1, Pallas kernels, ffn(): pl.pallas_call(functools.partial(ffn_body, n, meta, min(1024, FF)), grid_...  26 us
    pallas_call x2, Pallas kernels, attn_bwd(): pl.pallas_call(functools.partial(attn_bwd_body, HD, 1.0 / math.sqrt(HD),...  23.8 us
    ppermute x23, starting transfers between devices, swap(): return lax.ppermute(x, 'shard', xor_perm(lax.axis_size('shard'), k))  18.3 us
    pallas_call x1, Pallas kernels, attn_fwd(): pl.pallas_call(functools.partial(attn_fwd_body, HD, bi, min(512, T), p0),...  15.1 us
    ppermute x6, waiting for transfers between devices, rep_perm(): return lax.ppermute(x, 'rep', xor_perm(lax.axis_size('rep'), b))  12.9 us
    ppermute x6, starting transfers between devices, rep_perm(): return lax.ppermute(x, 'rep', xor_perm(lax.axis_size('rep'), b))  12.5 us
    ppermute x23, waiting for transfers between devices, swap(): return lax.ppermute(x, 'shard', xor_perm(lax.axis_size('shard'), k))  9.36 us
    pallas_call x1, Pallas kernels, front(): pl.pallas_call(functools.partial(front_body, scale, n, meta), grid_spec=p...  7.01 us
  transfers between devices with their start and end apart: 29, of which 13 were waited for; matrix products, arithmetic and copies ran while one was open for 2% of the time, Pallas kernels for 42%

profile of v14, /device:TPU:0, one launch (start us, length us, event | category | flops | bytes accessed | tf_op | source)
XLA Modules:
  0.0 158.4 jit_solution(5348793827918711951)
XLA Ops:
  0.7 1.8 %pack_first.1.refs_0_ = bf16[208,512]{1,0:T(8,128)(2,1)} custom-call(s32[1]{0:T(128)} %bitcast.me, bf16[64,1536]{1,0:T(8,128)(2,1)} %w.3, bf16[2,128]{1,0:T(2,128)(2,1)} %bitcast.47, bf16[1,64]{1,0:T(2,128)(2,1)} %bitcast.39, bf16[1,64]{1,0:T(2,128)(2,1)} %bitcast.41, bf16[1,64]{1,0:T(2,128)(2,1)} %bitcast.48, bf16[1,64]{1,0:T(2,128)(2,1)} %bitcast.49, ...), custom_call_target="tpu_custom_call" | custom-call | bytes 393216 | tf_op jit(solution)/shard_map/pack_first/pallas_call | solution.py:125
  2.4 2.9 %collective-permute-start = (bf16[208,512]{1,0:T(8,128)(2,1)}, bf16[208,512]{1,0:T(8,128)(2,1)S(1)}, u32[]{:S(2)}, u32[]{:S(2)}) collective-permute-start(bf16[208,512]{1,0:T(8,128)(2,1)} %pack_first.1.refs_0_), channel_id=1, source_target_pairs={{0,2},{1,3},{2,0},{3,1},{4,6},{5,7},{6,4},{7,5},{8,10},{9,11},{10,... | collective-permute-start | bytes 638984 | tf_op jit(solution)/shard_map/ppermute | solution.py:43
  6.9 1.9 %pack_rest.1.refs_0_ = bf16[576,512]{1,0:T(8,128)(2,1)} custom-call(bf16[64,512]{1,0:T(8,128)(2,1)} %wo.1, bf16[64,2048]{1,0:T(8,128)(2,1)} %wu.1, bf16[256,512]{1,0:T(8,128)(2,1)} %wd.1), custom_call_target="tpu_custom_call" | custom-call | bytes 524288 | tf_op jit(solution)/shard_map/pack_rest/pallas_call | solution.py:143
  8.8 4.2 %start.1 = (f32[1024,512]{1,0:T(8,128)}, bf16[528,1024]{1,0:T(8,128)(2,1)}) custom-call(bf16[1024,512]{1,0:T(8,128)(2,1)} %bitcast.43, bf16[1,512]{1,0:T(2,128)(2,1)} %step.4), custom_call_target="tpu_custom_call" | custom-call | flops 10485760 | bytes 4194304 | tf_op jit(solution)/shard_map/start/pallas_call | solution.py:287
  13.6 3.3 %collective-permute-done.1.refs_2_ = bf16[208,512]{1,0:T(8,128)(2,1)S(1)} collective-permute-done((bf16[208,512]{1,0:T(8,128)(2,1)}, bf16[208,512]{1,0:T(8,128)(2,1)S(1)}, u32[]{:S(2)}, u32[]{:S(2)}) %collective-permute-start.1) | collective-permute-done | bytes 213024 | tf_op jit(solution)/shard_map/ppermute | solution.py:43
  22.4 7.0 %front.1 = (bf16[2,1024,512]{2,1,0:T(8,128)(2,1)}, bf16[3,512,1024]{2,1,0:T(8,128)(2,1)}, bf16[512,1536]{1,0:T(8,128)(2,1)}, f32[8,512]{1,0:T(8,128)}, f32[1,2048]{1,0:T(1,128)}) custom-call(s32[1]{0:T(128)} %bitcast.me, f32[1024,512]{1,0:T(8,128)} %get-tuple-element.70.nx, bf16[208,512]{1,0:T(8,128)(2,1)} %pack_first.1.refs_0_, bf16[208,512]{1,0:T(8,128)(2,1)} %copy-done.9, ...), custom_call_target="tpu_custom_call" | custom-call | flops 1610612736 | bytes 6291456 | tf_op jit(solution)/shard_map/front/pallas_call | solution.py:360
  29.4 15.1 %attn_fwd.1 = (bf16[8,1024,1024]{2,1,0:T(8,128)(2,1)}, bf16[1024,512]{1,0:T(8,128)(2,1)}, bf16[512,1024]{1,0:T(8,128)(2,1)}, f32[512,1024]{1,0:T(8,128)}, f32[4,8,1024]{2,1,0:T(8,128)}) custom-call(s32[1]{0:T(128)S(6)} %copy.34.ln, bf16[2,1024,512]{2,1,0:T(8,128)(2,1)} %get-tuple-element.77.k.v, bf16[3,512,1024]{2,1,0:T(8,128)(2,1)} %get-tuple-element.78.qt.vt.kt, ...), custom_call_target="tpu_custom_call" | custom-call | flops 8589934592 | bytes 16777216 | tf_op jit(solution)/shard_map/attn_fwd/pallas_call | solution.py:450
  49.3 26.0 %ffn.1 = (bf16[1024,512]{1,0:T(8,128)(2,1)}, bf16[1024,512]{1,0:T(8,128)(2,1)}, bf16[512,1024]{1,0:T(8,128)(2,1)}, bf16[4,592,512]{2,1,0:T(8,128)(2,1)}, bf16[4,592,512]{2,1,0:T(8,128)(2,1)}) custom-call(s32[1]{0:T(128)S(6)} %copy.34.ln, s32[1]{0:T(128)} %bitcast.me, bf16[1024,512]{1,0:T(8,128)(2,1)} %bitcast.44, bf16[1,512]{1,0:T(2,128)(2,1)S(1)} %copy-done.3, ...), custom_call_target="tpu_custom_call" | custom-call | flops 14495514624 | bytes 8388608 | tf_op jit(solution)/shard_map/ffn/pallas_call | solution.py:606
  75.4 7.8 %attn_bwd.2.refs_0_ = bf16[3,512,1024]{2,1,0:T(8,128)(2,1)} custom-call(bf16[2,1024,512]{2,1,0:T(8,128)(2,1)} %get-tuple-element.77.k.v, bf16[3,512,1024]{2,1,0:T(8,128)(2,1)} %get-tuple-element.78.qt.vt.kt, bf16[3,512,1024]{2,1,0:T(8,128)(2,1)} %get-tuple-element.78.qt.vt.kt, bf16[512,1024]{1,0:T(8,128)(2,1)} %get-tuple-element.93.gt, ...), custom_call_target="tpu_custom_call" | custom-call | flops 4294967296 | bytes 4194304 | tf_op jit(solution)/shard_map/attn_bwd/pallas_call | solution.py:650
  83.3 2.2 %slice_add_fusion.2 = (bf16[2,272,512]{2,1,0:T(8,128)(2,1)S(1)}, bf16[2,272,512]{2,1,0:T(8,128)(2,1)}) fusion(bf16[4,592,512]{2,1,0:T(8,128)(2,1)} %collective-permute-done.14, bf16[4,592,512]{2,1,0:T(8,128)(2,1)S(1)} %copy-done.7), kind=kLoop, calls=%fused_computation.6 | loop fusion | flops 557056 | bytes 3342336 | tf_op jit(solution)/shard_map/add | solution.py:58
  85.4 2.3 %slice_add_fusion = (bf16[2,320,512]{2,1,0:T(8,128)(2,1)}, bf16[2,320,512]{2,1,0:T(8,128)(2,1)S(1)}) fusion(bf16[4,592,512]{2,1,0:T(8,128)(2,1)} %collective-permute-done.14, bf16[4,592,512]{2,1,0:T(8,128)(2,1)S(1)} %copy-done.7), kind=kLoop, calls=%fused_computation.4 | loop fusion | flops 655360 | bytes 3932160 | tf_op jit(solution)/shard_map/add | solution.py:58
  89.8 16.0 %attn_bwd.3.g = bf16[3,512,1024]{2,1,0:T(8,128)(2,1)} custom-call(bf16[2,1024,512]{2,1,0:T(8,128)(2,1)} %get-tuple-element.77.k.v, bf16[3,512,1024]{2,1,0:T(8,128)(2,1)} %get-tuple-element.78.qt.vt.kt, bf16[3,512,1024]{2,1,0:T(8,128)(2,1)} %get-tuple-element.78.qt.vt.kt, bf16[512,1024]{1,0:T(8,128)(2,1)} %get-tuple-element.93.gt, ...), custom_call_target="tpu_custom_call", output_to_operand_aliasing={{}: (7, {})} | custom-call | flops 12884901888 | bytes 12582912 | tf_op jit(solution)/shard_map/attn_bwd/pallas_call | solution.py:650
  108.4 5.6 %wqkv.1 = (bf16[4,208,512]{2,1,0:T(8,128)(2,1)}, bf16[4,208,512]{2,1,0:T(8,128)(2,1)}) custom-call(s32[1]{0:T(128)} %bitcast.me, bf16[528,1024]{1,0:T(8,128)(2,1)} %get-tuple-element.96.xht, bf16[3,512,1024]{2,1,0:T(8,128)(2,1)} %attn_bwd.3.g), custom_call_target="tpu_custom_call" | custom-call | flops 1610612736 | bytes 5242880 | tf_op jit(solution)/shard_map/wqkv/pallas_call | solution.py:686
  114.5 1.9 %collective-permute-done.17 = bf16[1,320,512]{2,1,0:T(8,128)(2,1)S(1)} collective-permute-done((bf16[1,320,512]{2,1,0:T(8,128)(2,1)S(1)}, bf16[1,320,512]{2,1,0:T(8,128)(2,1)S(1)}, u32[]{:S(2)}, u32[]{:S(2)}) %collective-permute-start.17) | collective-permute-done | bytes 327712 | tf_op jit(solution)/shard_map/ppermute | solution.py:43
  117.8 1.6 %collective-permute-start.19 = (bf16[296,512]{1,0:T(8,128)(2,1)S(1)}, bf16[296,512]{1,0:T(8,128)(2,1)S(1)}, u32[]{:S(2)}, u32[]{:S(2)}) collective-permute-start(bf16[296,512]{1,0:T(8,128)(2,1)S(1)} %fusion.3), channel_id=1, source_target_pairs={{0,8},{8,0},{16,24},{24,16},{1,9},{9,1},{17,25},{25,17},{2,10},{10... | collective-permute-start | bytes 909320 | tf_op jit(solution)/shard_map/ppermute | solution.py:39
  120.1 1.8 %collective-permute-start.21 = (bf16[208,512]{1,0:T(8,128)(2,1)}, bf16[208,512]{1,0:T(8,128)(2,1)S(1)}, u32[]{:S(2)}, u32[]{:S(2)}) collective-permute-start(bf16[208,512]{1,0:T(8,128)(2,1)} %get-tuple-element.129), channel_id=1, source_target_pairs={{0,6},{1,7},{2,4},{3,5},{4,2},{5,3},{6,0},{7,1},{8,14},{9,15},{10,... | collective-permute-start | bytes 638984 | tf_op jit(solution)/shard_map/ppermute | solution.py:43
  123.6 2.0 %collective-permute-done.19 = bf16[296,512]{1,0:T(8,128)(2,1)S(1)} collective-permute-done((bf16[296,512]{1,0:T(8,128)(2,1)S(1)}, bf16[296,512]{1,0:T(8,128)(2,1)S(1)}, u32[]{:S(2)}, u32[]{:S(2)}) %collective-permute-start.19) | collective-permute-done | bytes 303136 | tf_op jit(solution)/shard_map/ppermute | solution.py:39
  126.0 2.6 %collective-permute-start.25 = (bf16[296,512]{1,0:T(8,128)(2,1)S(1)}, bf16[296,512]{1,0:T(8,128)(2,1)S(1)}, u32[]{:S(2)}, u32[]{:S(2)}) collective-permute-start(bf16[296,512]{1,0:T(8,128)(2,1)S(1)} %fusion.5), channel_id=1, source_target_pairs={{0,16},{8,24},{16,0},{24,8},{1,17},{9,25},{17,1},{25,9},{2,18},{10... | collective-permute-start | bytes 909320 | tf_op jit(solution)/shard_map/ppermute | solution.py:39
  128.7 6.9 %back.1 = f32[1024,512]{1,0:T(8,128)} custom-call(bf16[1024,512]{1,0:T(8,128)(2,1)} %bitcast.45, bf16[1,512]{1,0:T(2,128)(2,1)} %step.4, f32[8,512]{1,0:T(8,128)} %get-tuple-element.75.vec, bf16[3,512,1024]{2,1,0:T(8,128)(2,1)} %attn_bwd.3.g, bf16[1024,512]{1,0:T(8,128)(2,1)} %get-tuple-element.103.gx1, bf16[512,1536]{1,0:T(8,128)(2,1)} %get-tuple-element.104.refs_0_), custom_call_target="tpu_custom_call" | custom-call | flops 1610612736 | bytes 7340032 | tf_op jit(solution)/shard_map/back/pallas_call | solution.py:713
  137.3 3.2 %collective-permute-done.25 = bf16[296,512]{1,0:T(8,128)(2,1)S(1)} collective-permute-done((bf16[296,512]{1,0:T(8,128)(2,1)S(1)}, bf16[296,512]{1,0:T(8,128)(2,1)S(1)}, u32[]{:S(2)}, u32[]{:S(2)}) %collective-permute-start.25) | collective-permute-done | bytes 303136 | tf_op jit(solution)/shard_map/ppermute | solution.py:39
  142.7 1.9 %collective-permute-start.26 = (bf16[104,512]{1,0:T(8,128)(2,1)S(1)}, bf16[104,512]{1,0:T(8,128)(2,1)S(1)}, u32[]{:S(2)}, u32[]{:S(2)}) collective-permute-start(bf16[104,512]{1,0:T(8,128)(2,1)S(1)} %dynamic-slice_add_fusion), channel_id=1, source_target_pairs={{0,16},{8,24},{16,0},{24,8},{1,17},{9,25},{17,1},{25,9},{2,18},{10... | collective-permute-start | bytes 319496 | tf_op jit(solution)/shard_map/ppermute | solution.py:39
  144.7 5.3 %collective-permute-done.26 = bf16[104,512]{1,0:T(8,128)(2,1)S(1)} collective-permute-done((bf16[104,512]{1,0:T(8,128)(2,1)S(1)}, bf16[104,512]{1,0:T(8,128)(2,1)S(1)}, u32[]{:S(2)}, u32[]{:S(2)}) %collective-permute-start.26) | collective-permute-done | bytes 106528 | tf_op jit(solution)/shard_map/ppermute | solution.py:39
  150.0 4.2 %collective-permute-start.27 = (bf16[104,512]{1,0:T(8,128)(2,1)S(1)}, bf16[104,512]{1,0:T(8,128)(2,1)S(1)}, u32[]{:S(2)}, u32[]{:S(2)}) collective-permute-start(bf16[104,512]{1,0:T(8,128)(2,1)S(1)} %add.119.s), channel_id=1, source_target_pairs={{0,8},{8,0},{16,24},{24,16},{1,9},{9,1},{17,25},{25,17},{2,10},{10... | collective-permute-start | bytes 319496 | tf_op jit(solution)/shard_map/ppermute | solution.py:39
  154.2 1.7 %finish_rest.1 = (f32[256,512]{1,0:T(8,128)}, f32[64,2048]{1,0:T(8,128)}, f32[64,512]{1,0:T(8,128)}, f32[1,256]{1,0:T(1,128)}, f32[1,64]{1,0:T(1,128)}, /*index=...) custom-call(s32[2]{0:T(128)S(1)} %pad_add_fusion.ids, bf16[296,512]{1,0:T(8,128)(2,1)S(1)} %add.117.s, ...), custom_call_target="tpu_custom_call" | custom-call | bytes 1212416 | tf_op jit(solution)/shard_map/finish_rest/pallas_call | solution.py:201
  (93 shorter events, 27.8 us)
Async XLA Ops:
  2.4 10.6 %collective-permute-start = (bf16[208,512]{1,0:T(8,128)(2,1)}, bf16[208,512]{1,0:T(8,128)(2,1)S(1)}, u32[]{:S(2)}, u32[]{:S(2)}) collective-permute-start(bf16[208,512]{1,0:T(8,128)(2,1)} %pack_first.1.refs_0_), channel_id=1, source_target_pairs={{0,2},{1,3},{2,0},{3,1},{4,6},{5,7},{6,4},{7,5},{8,10},{9,11},{10,... | collective-permute-start | bytes 638984 | tf_op jit(solution)/shard_map/ppermute | solution.py:43
  5.4 11.5 %collective-permute-start.1 = (bf16[208,512]{1,0:T(8,128)(2,1)}, bf16[208,512]{1,0:T(8,128)(2,1)S(1)}, u32[]{:S(2)}, u32[]{:S(2)}) collective-permute-start(bf16[208,512]{1,0:T(8,128)(2,1)} %pack_first.1.refs_0_), channel_id=1, source_target_pairs={{0,4},{1,5},{2,6},{3,7},{4,0},{5,1},{6,2},{7,3},{8,12},{9,13},{10,... | collective-permute-start | bytes 638984 | tf_op jit(solution)/shard_map/ppermute | solution.py:43
  6.9 10.0 %collective-permute-start.2 = (bf16[208,512]{1,0:T(8,128)(2,1)}, bf16[208,512]{1,0:T(8,128)(2,1)S(1)}, u32[]{:S(2)}, u32[]{:S(2)}) collective-permute-start(bf16[208,512]{1,0:T(8,128)(2,1)} %pack_first.1.refs_0_), channel_id=1, source_target_pairs={{0,6},{1,7},{2,4},{3,5},{4,2},{5,3},{6,0},{7,1},{8,14},{9,15},{10,... | collective-permute-start | bytes 638984 | tf_op jit(solution)/shard_map/ppermute | solution.py:43
  6.9 12.6 %collective-permute-start.3 = (bf16[208,512]{1,0:T(8,128)(2,1)}, bf16[208,512]{1,0:T(8,128)(2,1)S(1)}, u32[]{:S(2)}, u32[]{:S(2)}) collective-permute-start(bf16[208,512]{1,0:T(8,128)(2,1)} %pack_first.1.refs_0_), channel_id=1, source_target_pairs={{0,1},{1,0},{2,3},{3,2},{4,5},{5,4},{6,7},{7,6},{8,9},{9,8},{10,11... | collective-permute-start | bytes 638984 | tf_op jit(solution)/shard_map/ppermute | solution.py:43
  13.0 7.3 %collective-permute-start.4 = (bf16[208,512]{1,0:T(8,128)(2,1)S(1)}, bf16[208,512]{1,0:T(8,128)(2,1)S(1)}, u32[]{:S(2)}, u32[]{:S(2)}) collective-permute-start(bf16[208,512]{1,0:T(8,128)(2,1)S(1)} %collective-permute-done.refs_1_), channel_id=1, source_target_pairs={{0,1},{1,0},{2,3},{3,2},{4,5},{5,4},{6,7},{7,6},{8,9},{9,8},{10,11... | collective-permute-start | bytes 638984 | tf_op jit(solution)/shard_map/ppermute | solution.py:43
  17.4 27.2 %collective-permute-start.9 = (bf16[576,512]{1,0:T(8,128)(2,1)}, bf16[576,512]{1,0:T(8,128)(2,1)S(1)}, u32[]{:S(2)}, u32[]{:S(2)}) collective-permute-start(bf16[576,512]{1,0:T(8,128)(2,1)} %pack_rest.1.refs_0_), channel_id=1, source_target_pairs={{0,6},{1,7},{2,4},{3,5},{4,2},{5,3},{6,0},{7,1},{8,14},{9,15},{10,... | collective-permute-start | bytes 1769480 | tf_op jit(solution)/shard_map/ppermute | solution.py:43
  19.5 26.9 %collective-permute-start.8 = (bf16[576,512]{1,0:T(8,128)(2,1)}, bf16[576,512]{1,0:T(8,128)(2,1)S(1)}, u32[]{:S(2)}, u32[]{:S(2)}) collective-permute-start(bf16[576,512]{1,0:T(8,128)(2,1)} %pack_rest.1.refs_0_), channel_id=1, source_target_pairs={{0,4},{1,5},{2,6},{3,7},{4,0},{5,1},{6,2},{7,3},{8,12},{9,13},{10,... | collective-permute-start | bytes 1769480 | tf_op jit(solution)/shard_map/ppermute | solution.py:43
  20.3 26.2 %collective-permute-start.7 = (bf16[576,512]{1,0:T(8,128)(2,1)}, bf16[576,512]{1,0:T(8,128)(2,1)S(1)}, u32[]{:S(2)}, u32[]{:S(2)}) collective-permute-start(bf16[576,512]{1,0:T(8,128)(2,1)} %pack_rest.1.refs_0_), channel_id=1, source_target_pairs={{0,2},{1,3},{2,0},{3,1},{4,6},{5,7},{6,4},{7,5},{8,10},{9,11},{10,... | collective-permute-start | bytes 1769480 | tf_op jit(solution)/shard_map/ppermute | solution.py:43
  21.6 25.3 %collective-permute-start.10 = (bf16[576,512]{1,0:T(8,128)(2,1)}, bf16[576,512]{1,0:T(8,128)(2,1)S(1)}, u32[]{:S(2)}, u32[]{:S(2)}) collective-permute-start(bf16[576,512]{1,0:T(8,128)(2,1)} %pack_rest.1.refs_0_), channel_id=1, source_target_pairs={{0,1},{1,0},{2,3},{3,2},{4,5},{5,4},{6,7},{7,6},{8,9},{9,8},{10,11... | collective-permute-start | bytes 1769480 | tf_op jit(solution)/shard_map/ppermute | solution.py:43
  75.3 8.0 %collective-permute-start.14 = (bf16[4,592,512]{2,1,0:T(8,128)(2,1)}, bf16[4,592,512]{2,1,0:T(8,128)(2,1)}, u32[]{:S(2)}, u32[]{:S(2)}) collective-permute-start(bf16[4,592,512]{2,1,0:T(8,128)(2,1)} %get-tuple-element.88), channel_id=1, source_target_pairs={{0,1},{1,0},{2,3},{3,2},{4,5},{5,4},{6,7},{7,6},{8,9},{9,8},{10,11... | collective-permute-start | bytes 7274504 | tf_op jit(solution)/shard_map/ppermute | solution.py:43
  87.7 18.1 %collective-permute-start.16 = (bf16[2,272,512]{2,1,0:T(8,128)(2,1)}, bf16[2,272,512]{2,1,0:T(8,128)(2,1)S(1)}, u32[]{:S(2)}, u32[]{:S(2)}) collective-permute-start(bf16[2,272,512]{2,1,0:T(8,128)(2,1)} %get-tuple-element.126), channel_id=1, source_target_pairs={{0,2},{1,3},{2,0},{3,1},{4,6},{5,7},{6,4},{7,5},{8,10},{9,11},{10,... | collective-permute-start | bytes 1671176 | tf_op jit(solution)/shard_map/ppermute | solution.py:43
  88.9 17.0 %collective-permute-start.15 = (bf16[2,320,512]{2,1,0:T(8,128)(2,1)}, bf16[2,320,512]{2,1,0:T(8,128)(2,1)S(1)}, u32[]{:S(2)}, u32[]{:S(2)}) collective-permute-start(bf16[2,320,512]{2,1,0:T(8,128)(2,1)} %get-tuple-element.127), channel_id=1, source_target_pairs={{0,4},{1,5},{2,6},{3,7},{4,0},{5,1},{6,2},{7,3},{8,12},{9,13},{10,... | collective-permute-start | bytes 1966088 | tf_op jit(solution)/shard_map/ppermute | solution.py:43
  106.0 8.5 %collective-permute-start.18 = (bf16[1,272,512]{2,1,0:T(8,128)(2,1)S(1)}, bf16[1,272,512]{2,1,0:T(8,128)(2,1)}, u32[]{:S(2)}, u32[]{:S(2)}) collective-permute-start(bf16[1,272,512]{2,1,0:T(8,128)(2,1)S(1)} %get-tuple-element.135), channel_id=1, source_target_pairs={{0,4},{1,5},{2,6},{3,7},{4,0},{5,1},{6,2},{7,3},{8,12},{9,13},{10,... | collective-permute-start | bytes 835592 | tf_op jit(solution)/shard_map/ppermute | solution.py:43
  107.1 9.2 %collective-permute-start.17 = (bf16[1,320,512]{2,1,0:T(8,128)(2,1)S(1)}, bf16[1,320,512]{2,1,0:T(8,128)(2,1)S(1)}, u32[]{:S(2)}, u32[]{:S(2)}) collective-permute-start(bf16[1,320,512]{2,1,0:T(8,128)(2,1)S(1)} %get-tuple-element.132), channel_id=1, source_target_pairs={{0,2},{1,3},{2,0},{3,1},{4,6},{5,7},{6,4},{7,5},{8,10},{9,11},{10,... | collective-permute-start | bytes 983048 | tf_op jit(solution)/shard_map/ppermute | solution.py:43
  114.0 5.4 %collective-permute-start.20 = (bf16[4,208,512]{2,1,0:T(8,128)(2,1)}, bf16[4,208,512]{2,1,0:T(8,128)(2,1)S(1)}, u32[]{:S(2)}, u32[]{:S(2)}) collective-permute-start(bf16[4,208,512]{2,1,0:T(8,128)(2,1)} %get-tuple-element.100), channel_id=1, source_target_pairs={{0,1},{1,0},{2,3},{3,2},{4,5},{5,4},{6,7},{7,6},{8,9},{9,8},{10,11... | collective-permute-start | bytes 2555912 | tf_op jit(solution)/shard_map/ppermute | solution.py:43
  117.8 7.8 %collective-permute-start.19 = (bf16[296,512]{1,0:T(8,128)(2,1)S(1)}, bf16[296,512]{1,0:T(8,128)(2,1)S(1)}, u32[]{:S(2)}, u32[]{:S(2)}) collective-permute-start(bf16[296,512]{1,0:T(8,128)(2,1)S(1)} %fusion.3), channel_id=1, source_target_pairs={{0,8},{8,0},{16,24},{24,16},{1,9},{9,1},{17,25},{25,17},{2,10},{10... | collective-permute-start | bytes 909320 | tf_op jit(solution)/shard_map/ppermute | solution.py:39
  120.1 15.4 %collective-permute-start.21 = (bf16[208,512]{1,0:T(8,128)(2,1)}, bf16[208,512]{1,0:T(8,128)(2,1)S(1)}, u32[]{:S(2)}, u32[]{:S(2)}) collective-permute-start(bf16[208,512]{1,0:T(8,128)(2,1)} %get-tuple-element.129), channel_id=1, source_target_pairs={{0,6},{1,7},{2,4},{3,5},{4,2},{5,3},{6,0},{7,1},{8,14},{9,15},{10,... | collective-permute-start | bytes 638984 | tf_op jit(solution)/shard_map/ppermute | solution.py:43
  122.0 13.6 %collective-permute-start.22 = (bf16[208,512]{1,0:T(8,128)(2,1)S(1)}, bf16[208,512]{1,0:T(8,128)(2,1)S(1)}, u32[]{:S(2)}, u32[]{:S(2)}) collective-permute-start(bf16[208,512]{1,0:T(8,128)(2,1)S(1)} %get-tuple-element.130), channel_id=1, source_target_pairs={{0,4},{1,5},{2,6},{3,7},{4,0},{5,1},{6,2},{7,3},{8,12},{9,13},{10,... | collective-permute-start | bytes 638984 | tf_op jit(solution)/shard_map/ppermute | solution.py:43
  122.4 13.1 %collective-permute-start.23 = (bf16[208,512]{1,0:T(8,128)(2,1)S(1)}, bf16[208,512]{1,0:T(8,128)(2,1)S(1)}, u32[]{:S(2)}, u32[]{:S(2)}) collective-permute-start(bf16[208,512]{1,0:T(8,128)(2,1)S(1)} %get-tuple-element.131), channel_id=1, source_target_pairs={{0,2},{1,3},{2,0},{3,1},{4,6},{5,7},{6,4},{7,5},{8,10},{9,11},{10,... | collective-permute-start | bytes 638984 | tf_op jit(solution)/shard_map/ppermute | solution.py:43
  126.0 14.4 %collective-permute-start.25 = (bf16[296,512]{1,0:T(8,128)(2,1)S(1)}, bf16[296,512]{1,0:T(8,128)(2,1)S(1)}, u32[]{:S(2)}, u32[]{:S(2)}) collective-permute-start(bf16[296,512]{1,0:T(8,128)(2,1)S(1)} %fusion.5), channel_id=1, source_target_pairs={{0,16},{8,24},{16,0},{24,8},{1,17},{9,25},{17,1},{25,9},{2,18},{10... | collective-permute-start | bytes 909320 | tf_op jit(solution)/shard_map/ppermute | solution.py:39
  135.7 7.0 %collective-permute-start.24 = (bf16[104,512]{1,0:T(8,128)(2,1)S(1)}, bf16[104,512]{1,0:T(8,128)(2,1)S(1)}, u32[]{:S(2)}, u32[]{:S(2)}) collective-permute-start(bf16[104,512]{1,0:T(8,128)(2,1)S(1)} %constant_dynamic-slice_fusion), channel_id=1, source_target_pairs={{0,8},{8,0},{16,24},{24,16},{1,9},{9,1},{17,25},{25,17},{2,10},{10... | collective-permute-start | bytes 319496 | tf_op jit(solution)/shard_map/ppermute | solution.py:39
  140.5 13.7 %collective-permute-start.28 = (bf16[296,512]{1,0:T(8,128)(2,1)S(1)}, bf16[296,512]{1,0:T(8,128)(2,1)S(1)}, u32[]{:S(2)}, u32[]{:S(2)}) collective-permute-start(bf16[296,512]{1,0:T(8,128)(2,1)S(1)} %add.117.s), channel_id=1, source_target_pairs={{0,8},{8,0},{16,24},{24,16},{1,9},{9,1},{17,25},{25,17},{2,10},{10... | collective-permute-start | bytes 909320 | tf_op jit(solution)/shard_map/ppermute | solution.py:39
  142.7 7.2 %collective-permute-start.26 = (bf16[104,512]{1,0:T(8,128)(2,1)S(1)}, bf16[104,512]{1,0:T(8,128)(2,1)S(1)}, u32[]{:S(2)}, u32[]{:S(2)}) collective-permute-start(bf16[104,512]{1,0:T(8,128)(2,1)S(1)} %dynamic-slice_add_fusion), channel_id=1, source_target_pairs={{0,16},{8,24},{16,0},{24,8},{1,17},{9,25},{17,1},{25,9},{2,18},{10... | collective-permute-start | bytes 319496 | tf_op jit(solution)/shard_map/ppermute | solution.py:39
  150.0 6.9 %collective-permute-start.27 = (bf16[104,512]{1,0:T(8,128)(2,1)S(1)}, bf16[104,512]{1,0:T(8,128)(2,1)S(1)}, u32[]{:S(2)}, u32[]{:S(2)}) collective-permute-start(bf16[104,512]{1,0:T(8,128)(2,1)S(1)} %add.119.s), channel_id=1, source_target_pairs={{0,8},{8,0},{16,24},{24,16},{1,9},{9,1},{17,25},{25,17},{2,10},{10... | collective-permute-start | bytes 319496 | tf_op jit(solution)/shard_map/ppermute | solution.py:39
  (21 other events, 196.5 us)

commit v15 on v14

--- a/solution.py
+++ b/solution.py
@@ -489,7 +489,7 @@
 def ffn_body(n, meta, ch, ln, me, tok, step, vec, upb, cot, mixed, mixedt, *refs):
     np_ = len(meta)
     pieces = refs[:np_]
-    out, gx1, gmt, keep, send, wo, wu, wd, act, gup, h2t, gdt, gattn, sums, upsum, dn, up, gwo, vr, mtv, sems, psems = refs[np_:]
+    out, gx1, gmt, ka, sa, kb, sb, wo, wu, wd, act, gup, h2t, gdt, gattn, sums, upsum, dn, up, gwo, vr, mtv, sems, psems = refs[np_:]
     i = pl.program_id(0)
     bm, D = tok.shape
     FF = wu.shape[1]
@@ -568,22 +568,21 @@
     @pl.when(i == pl.num_programs(0) - 1)
     def _():
         per = D // rf
-        o_out, o_up, o_vec = rf, rf + r, rf + (nf + 1) * r
         for j in range(nf):
             dn[j] = dot(gdt[...], act[:, j * D : (j + 1) * D]).astype(bf16).T
             for t in range(per):
-                push(i0, n, j * per + t, dn.at[j, pl.ds(t * rf, rf)], keep, send, 0, psems.at[j * per + t])
+                push(i0, n, j * per + t, dn.at[j, pl.ds(t * rf, rf)], ka, sa, 0, psems.at[j * per + t])
             up[j] = dot(h2t[...], gup[:, j * D : (j + 1) * D]).astype(bf16)
             for s in range(n):
-                push(i0, n, s, up.at[j, pl.ds(s * r, r)], keep, send, o_up + j * r, psems.at[n * (1 + j) + s], True)
+                push(i0, n, s, up.at[j, pl.ds(s * r, r)], kb, sb, j * r, psems.at[n * (1 + j) + s], True)
         load.wait()
         gwo[...] = dot(mtv[...], gattn[...]).astype(bf16)
         vr[...] = jnp.concatenate([sums[0:4, :]] + [upsum[:, c * D : (c + 1) * D] for c in range(nf)] + [jnp.zeros((VROWS - 4 - nf, D), f32)], axis=0).astype(bf16)
         b = n * (1 + nf)
         for s in range(n):
-            push(i0, n, s, gwo.at[pl.ds(s * r, r)], keep, send, o_out, psems.at[b + s])
-            push(i0, n, s, vr, keep, send, o_vec, psems.at[b + n + s], True)
-        done = lambda src, q: pltpu.make_async_copy(src, keep.at[0, pl.ds(0, src.shape[0])], psems.at[q]).wait()
+            push(i0, n, s, gwo.at[pl.ds(s * r, r)], ka, sa, rf, psems.at[b + s])
+            push(i0, n, s, vr, kb, sb, nf * r, psems.at[b + n + s], True)
+        done = lambda src, q: pltpu.make_async_copy(src, (ka if src.shape[0] == rf else kb).at[0, pl.ds(0, src.shape[0])], psems.at[q]).wait()
         for s in range(n):
             done(dn.at[0, pl.ds(0, rf)], s)
             for c in range(nf):
@@ -601,16 +600,17 @@
     meta = tuple((k, r0) for k, r0, _ in pieces)
     full = lambda a: pl.BlockSpec(a.shape, lambda i, l, m: (0,) * a.ndim)
     rows = pl.BlockSpec((bm, D), lambda i, l, m: (i, 0))
-    B = S((n // 2, FF // n + (nf + 1) * r + VROWS, D), bf16)
+    A = S((n // 2, FF // n + r, D), bf16)
+    B = S((n // 2, nf * r + VROWS, D), bf16)
     V = pltpu.VMEM
     return pl.pallas_call(
         functools.partial(ffn_body, n, meta, min(1024, FF)),
         grid_spec=pltpu.PrefetchScalarGridSpec(
             num_scalar_prefetch=2, grid=(T // bm,),
             in_specs=[rows, full(step), full(vec), full(upb), rows, rows, ANY] + [ANY] * len(pieces),
-            out_specs=[rows, rows, pl.BlockSpec((D, bm), lambda i, l, m: (0, i)), ANY, ANY],
+            out_specs=[rows, rows, pl.BlockSpec((D, bm), lambda i, l, m: (0, i))] + [ANY] * 4,
             scratch_shapes=[V((D, D), bf16), V((D, FF), bf16), V((FF, D), bf16), V((T, FF), bf16), V((T, FF), bf16), V((D, T), bf16), V((D, T), bf16), V((T, D), bf16), V((8, D), f32), V((1, FF), f32), V((nf, D, D), bf16), V((nf, D, D), bf16), V((D, D), bf16), V((VROWS, D), bf16), V((D, T), bf16), pltpu.SemaphoreType.DMA((16 * len(pieces),)), pltpu.SemaphoreType.DMA((n * (nf + 3) + 1,))]),
-        out_shape=[S((T, D), bf16), S((T, D), bf16), S((D, T), bf16), B, B],
+        out_shape=[S((T, D), bf16), S((T, D), bf16), S((D, T), bf16), A, A, B, B],
         compiler_params=cp(49), name="ffn", cost_estimate=cost(2 * T * D * (6 * FF + 3 * D), 16 * T * D, T * FF),
     )(ln, me, tok, step, vec, upb, cot, mixed, mixedt, *[a for _, _, a in pieces])
 
@@ -735,17 +735,15 @@
     kv, qkvt, w, vec, upb = front(mes, nx, pieces, n, FF)
     et, mixed, mixedt, mixedf, linv = attn_fwd(lengths, kv, qkvt, 0, NP, [])
     pieces2 = gather_direct(after(pack2, xht), n, linv)
-    out, gx1, gmt, keep, send = ffn(lengths, mes, tok, step, vec, upb, cot, mixed, mixedt, pieces2, n)
+    out, gx1, gmt, ka, sa, kb, sb = ffn(lengths, mes, tok, step, vec, upb, cot, mixed, mixedt, pieces2, n)
     bwd = lambda p, c, g, *deps: attn_bwd(kv, qkvt, after(gmt, *deps) if deps else gmt, mixedf, linv, et, p, c, g)
-    ra = rf + r
-    got = swap(send, 1)
+    ga, gb = swap(sa, 1), swap(sb, 1)
     g = bwd(0, 1, [])
-    got = after(got, g)
+    ga, gb, _ = lax.optimization_barrier((ga, gb, g))
     h = n // 4
-    add = lambda a, b, k: add16(a[k], b[k])
-    rows_a, rows_b = slice(0, ra), slice(ra, None)
     lo, hi = slice(0, h), slice(h, None)
-    ka, xa, kb, xb = [add(keep, got, k) for k in ((lo, rows_a), (hi, rows_a), (lo, rows_b), (hi, rows_b))]
+    add = lambda a, b, s: add16(a[s], b[s])
+    ka, xa, kb, xb = add(ka, ga, lo), add(ka, ga, hi), add(kb, gb, lo), add(kb, gb, hi)
     g = bwd(1, NP - 1, [g], ka, xa, kb, xb)
     m = (n // 2).bit_length() - 1
     ga, gb = swap(xa, 2 << (m - 1)), swap(xb, 2)

time: 159 us -> 155 us (0.975)
  other arithmetic: 7.52 us -> 4.4 us
    add x9, other arithmetic: 5.87 us -> 3.71 us  [add16(): return a + b]
    ppermute x23 -> x24, starting transfers between devices: 18.3 us -> 18.3 us  [swap(): return lax.ppermute(x, 'shard', xor_perm(lax.axis_size('shard'), k))]
    ppermute x23 -> x24, waiting for transfers between devices: 9.36 us -> 9.37 us  [swap(): return lax.ppermute(x, 'shard', xor_perm(lax.axis_size('shard'), k))]
  transfers between devices with their start and end apart: 29 -> 30, of which waited for: 13 -> 12; matrix products, arithmetic and copies ran while one was open for 2% -> 2% of each run, Pallas kernels for 42% -> 43%
where the time goes in v15:
time: 155 us
  Pallas kernels  95.5 us (62%)
  starting transfers between devices  31.1 us (20%)
  waiting for transfers between devices  21.2 us (14%)
  other arithmetic  4.4 us (3%)
  between operations  1.66 us (1%)
    pallas_call x1, Pallas kernels, ffn(): pl.pallas_call(functools.partial(ffn_body, n, meta, min(1024, FF)), grid_...  26 us
    pallas_call x2, Pallas kernels, attn_bwd(): pl.pallas_call(functools.partial(attn_bwd_body, HD, 1.0 / math.sqrt(HD),...  23.8 us
    ppermute x24, starting transfers between devices, swap(): return lax.ppermute(x, 'shard', xor_perm(lax.axis_size('shard'), k))  18.3 us
    pallas_call x1, Pallas kernels, attn_fwd(): pl.pallas_call(functools.partial(attn_fwd_body, HD, bi, min(512, T), p0),...  15.1 us
    ppermute x6, starting transfers between devices, rep_perm(): return lax.ppermute(x, 'rep', xor_perm(lax.axis_size('rep'), b))  12.7 us
    ppermute x6, waiting for transfers between devices, rep_perm(): return lax.ppermute(x, 'rep', xor_perm(lax.axis_size('rep'), b))  11.8 us
    ppermute x24, waiting for transfers between devices, swap(): return lax.ppermute(x, 'shard', xor_perm(lax.axis_size('shard'), k))  9.37 us
    pallas_call x1, Pallas kernels, front(): pl.pallas_call(functools.partial(front_body, scale, n, meta), grid_spec=p...  7.08 us
  transfers between devices with their start and end apart: 30, of which 12 were waited for; matrix products, arithmetic and copies ran while one was open for 2% of the time, Pallas kernels for 43%

profile of v15, /device:TPU:0, one launch (start us, length us, event | category | flops | bytes accessed | tf_op | source)
XLA Modules:
  0.0 154.7 jit_solution(15720806179782279859)
XLA Ops:
  0.7 1.8 %pack_first.1.refs_0_ = bf16[208,512]{1,0:T(8,128)(2,1)} custom-call(s32[1]{0:T(128)} %bitcast.me, bf16[64,1536]{1,0:T(8,128)(2,1)} %w.3, bf16[2,128]{1,0:T(2,128)(2,1)} %bitcast.47, bf16[1,64]{1,0:T(2,128)(2,1)} %bitcast.39, bf16[1,64]{1,0:T(2,128)(2,1)} %bitcast.41, bf16[1,64]{1,0:T(2,128)(2,1)} %bitcast.48, bf16[1,64]{1,0:T(2,128)(2,1)} %bitcast.49, ...), custom_call_target="tpu_custom_call" | custom-call | bytes 393216 | tf_op jit(solution)/shard_map/pack_first/pallas_call | solution.py:125
  2.4 2.9 %collective-permute-start = (bf16[208,512]{1,0:T(8,128)(2,1)}, bf16[208,512]{1,0:T(8,128)(2,1)S(1)}, u32[]{:S(2)}, u32[]{:S(2)}) collective-permute-start(bf16[208,512]{1,0:T(8,128)(2,1)} %pack_first.1.refs_0_), channel_id=1, source_target_pairs={{0,2},{1,3},{2,0},{3,1},{4,6},{5,7},{6,4},{7,5},{8,10},{9,11},{10,... | collective-permute-start | bytes 638984 | tf_op jit(solution)/shard_map/ppermute | solution.py:43
  6.9 1.9 %pack_rest.1.refs_0_ = bf16[576,512]{1,0:T(8,128)(2,1)} custom-call(bf16[64,512]{1,0:T(8,128)(2,1)} %wo.1, bf16[64,2048]{1,0:T(8,128)(2,1)} %wu.1, bf16[256,512]{1,0:T(8,128)(2,1)} %wd.1), custom_call_target="tpu_custom_call" | custom-call | bytes 524288 | tf_op jit(solution)/shard_map/pack_rest/pallas_call | solution.py:143
  8.8 4.2 %start.1 = (f32[1024,512]{1,0:T(8,128)}, bf16[528,1024]{1,0:T(8,128)(2,1)}) custom-call(bf16[1024,512]{1,0:T(8,128)(2,1)} %bitcast.43, bf16[1,512]{1,0:T(2,128)(2,1)} %step.4), custom_call_target="tpu_custom_call" | custom-call | flops 10485760 | bytes 4194304 | tf_op jit(solution)/shard_map/start/pallas_call | solution.py:287
  13.6 3.3 %collective-permute-done.1.refs_2_ = bf16[208,512]{1,0:T(8,128)(2,1)S(1)} collective-permute-done((bf16[208,512]{1,0:T(8,128)(2,1)}, bf16[208,512]{1,0:T(8,128)(2,1)S(1)}, u32[]{:S(2)}, u32[]{:S(2)}) %collective-permute-start.1) | collective-permute-done | bytes 213024 | tf_op jit(solution)/shard_map/ppermute | solution.py:43
  22.4 7.1 %front.1 = (bf16[2,1024,512]{2,1,0:T(8,128)(2,1)}, bf16[3,512,1024]{2,1,0:T(8,128)(2,1)}, bf16[512,1536]{1,0:T(8,128)(2,1)}, f32[8,512]{1,0:T(8,128)}, f32[1,2048]{1,0:T(1,128)}) custom-call(s32[1]{0:T(128)} %bitcast.me, f32[1024,512]{1,0:T(8,128)} %get-tuple-element.73.nx, bf16[208,512]{1,0:T(8,128)(2,1)} %pack_first.1.refs_0_, ...), custom_call_target="tpu_custom_call" | custom-call | flops 1610612736 | bytes 6291456 | tf_op jit(solution)/shard_map/front/pallas_call | solution.py:360
  29.5 15.1 %attn_fwd.1 = (bf16[8,1024,1024]{2,1,0:T(8,128)(2,1)}, bf16[1024,512]{1,0:T(8,128)(2,1)}, bf16[512,1024]{1,0:T(8,128)(2,1)}, f32[512,1024]{1,0:T(8,128)}, f32[4,8,1024]{2,1,0:T(8,128)}) custom-call(s32[1]{0:T(128)S(6)} %copy.34.ln, bf16[2,1024,512]{2,1,0:T(8,128)(2,1)} %get-tuple-element.80.k.v, bf16[3,512,1024]{2,1,0:T(8,128)(2,1)} %get-tuple-element.81.qt.vt.kt, ...), custom_call_target="tpu_custom_call" | custom-call | flops 8589934592 | bytes 16777216 | tf_op jit(solution)/shard_map/attn_fwd/pallas_call | solution.py:450
  49.3 26.0 %ffn.1 = (bf16[1024,512]{1,0:T(8,128)(2,1)}, bf16[1024,512]{1,0:T(8,128)(2,1)}, bf16[512,1024]{1,0:T(8,128)(2,1)}, bf16[4,320,512]{2,1,0:T(8,128)(2,1)}, bf16[4,...) custom-call(s32[1]{0:T(128)S(6)} %copy.34.ln, s32[1]{0:T(128)} %bitcast.me, ...), custom_call_target="tpu_custom_call" | custom-call | flops 14495514624 | bytes 8388608 | tf_op jit(solution)/shard_map/ffn/pallas_call | solution.py:606
  75.9 7.8 %attn_bwd.2.refs_0_ = bf16[3,512,1024]{2,1,0:T(8,128)(2,1)} custom-call(bf16[2,1024,512]{2,1,0:T(8,128)(2,1)} %get-tuple-element.80.k.v, bf16[3,512,1024]{2,1,0:T(8,128)(2,1)} %get-tuple-element.81.qt.vt.kt, bf16[3,512,1024]{2,1,0:T(8,128)(2,1)} %get-tuple-element.81.qt.vt.kt, bf16[512,1024]{1,0:T(8,128)(2,1)} %get-tuple-element.99.gt, ...), custom_call_target="tpu_custom_call" | custom-call | flops 4294967296 | bytes 4194304 | tf_op jit(solution)/shard_map/attn_bwd/pallas_call | solution.py:650
  87.0 16.0 %attn_bwd.3.g = bf16[3,512,1024]{2,1,0:T(8,128)(2,1)} custom-call(bf16[2,1024,512]{2,1,0:T(8,128)(2,1)} %get-tuple-element.80.k.v, bf16[3,512,1024]{2,1,0:T(8,128)(2,1)} %get-tuple-element.81.qt.vt.kt, bf16[3,512,1024]{2,1,0:T(8,128)(2,1)} %get-tuple-element.81.qt.vt.kt, bf16[512,1024]{1,0:T(8,128)(2,1)} %get-tuple-element.99.gt, ...), custom_call_target="tpu_custom_call", output_to_operand_aliasing={{}: (7, {})} | custom-call | flops 12884901888 | bytes 12582912 | tf_op jit(solution)/shard_map/attn_bwd/pallas_call | solution.py:650
  106.2 5.6 %wqkv.1 = (bf16[4,208,512]{2,1,0:T(8,128)(2,1)}, bf16[4,208,512]{2,1,0:T(8,128)(2,1)}) custom-call(s32[1]{0:T(128)} %bitcast.me, bf16[528,1024]{1,0:T(8,128)(2,1)} %get-tuple-element.102.xht, bf16[3,512,1024]{2,1,0:T(8,128)(2,1)} %attn_bwd.3.g), custom_call_target="tpu_custom_call" | custom-call | flops 1610612736 | bytes 5242880 | tf_op jit(solution)/shard_map/wqkv/pallas_call | solution.py:686
  112.6 1.6 %collective-permute-done.18 = bf16[1,320,512]{2,1,0:T(8,128)(2,1)S(1)} collective-permute-done((bf16[1,320,512]{2,1,0:T(8,128)(2,1)S(1)}, bf16[1,320,512]{2,1,0:T(8,128)(2,1)S(1)}, u32[]{:S(2)}, u32[]{:S(2)}) %collective-permute-start.18) | collective-permute-done | bytes 327712 | tf_op jit(solution)/shard_map/ppermute | solution.py:43
  114.7 1.6 %collective-permute-start.20 = (bf16[296,512]{1,0:T(8,128)(2,1)S(1)}, bf16[296,512]{1,0:T(8,128)(2,1)S(1)}, u32[]{:S(2)}, u32[]{:S(2)}) collective-permute-start(bf16[296,512]{1,0:T(8,128)(2,1)S(1)} %fusion.3), channel_id=1, source_target_pairs={{0,8},{8,0},{16,24},{24,16},{1,9},{9,1},{17,25},{25,17},{2,10},{10... | collective-permute-start | bytes 909320 | tf_op jit(solution)/shard_map/ppermute | solution.py:39
  117.2 1.8 %collective-permute-start.22 = (bf16[208,512]{1,0:T(8,128)(2,1)}, bf16[208,512]{1,0:T(8,128)(2,1)S(1)}, u32[]{:S(2)}, u32[]{:S(2)}) collective-permute-start(bf16[208,512]{1,0:T(8,128)(2,1)} %get-tuple-element.135), channel_id=1, source_target_pairs={{0,6},{1,7},{2,4},{3,5},{4,2},{5,3},{6,0},{7,1},{8,14},{9,15},{10,... | collective-permute-start | bytes 638984 | tf_op jit(solution)/shard_map/ppermute | solution.py:43
  120.7 1.5 collective-permute-done.20
  122.6 2.7 %collective-permute-start.26 = (bf16[296,512]{1,0:T(8,128)(2,1)S(1)}, bf16[296,512]{1,0:T(8,128)(2,1)S(1)}, u32[]{:S(2)}, u32[]{:S(2)}) collective-permute-start(bf16[296,512]{1,0:T(8,128)(2,1)S(1)} %fusion.5), channel_id=1, source_target_pairs={{0,16},{8,24},{16,0},{24,8},{1,17},{9,25},{17,1},{25,9},{2,18},{10... | collective-permute-start | bytes 909320 | tf_op jit(solution)/shard_map/ppermute | solution.py:39
  125.3 6.9 %back.1 = f32[1024,512]{1,0:T(8,128)} custom-call(bf16[1024,512]{1,0:T(8,128)(2,1)} %bitcast.45, bf16[1,512]{1,0:T(2,128)(2,1)} %step.4, f32[8,512]{1,0:T(8,128)} %get-tuple-element.78.vec, bf16[3,512,1024]{2,1,0:T(8,128)(2,1)} %attn_bwd.3.g, bf16[1024,512]{1,0:T(8,128)(2,1)} %get-tuple-element.109.gx1, bf16[512,1536]{1,0:T(8,128)(2,1)} %get-tuple-element.110.refs_0_), custom_call_target="tpu_custom_call" | custom-call | flops 1610612736 | bytes 7340032 | tf_op jit(solution)/shard_map/back/pallas_call | solution.py:713
  132.4 1.6 %collective-permute-start.25 = (bf16[104,512]{1,0:T(8,128)(2,1)S(1)}, bf16[104,512]{1,0:T(8,128)(2,1)S(1)}, u32[]{:S(2)}, u32[]{:S(2)}) collective-permute-start(bf16[104,512]{1,0:T(8,128)(2,1)S(1)} %constant_dynamic-slice_fusion), channel_id=1, source_target_pairs={{0,8},{8,0},{16,24},{24,16},{1,9},{9,1},{17,25},{25,17},{2,10},{10... | collective-permute-start | bytes 319496 | tf_op jit(solution)/shard_map/ppermute | solution.py:39
  134.0 2.7 %collective-permute-done.26 = bf16[296,512]{1,0:T(8,128)(2,1)S(1)} collective-permute-done((bf16[296,512]{1,0:T(8,128)(2,1)S(1)}, bf16[296,512]{1,0:T(8,128)(2,1)S(1)}, u32[]{:S(2)}, u32[]{:S(2)}) %collective-permute-start.26) | collective-permute-done | bytes 303136 | tf_op jit(solution)/shard_map/ppermute | solution.py:39
  139.0 2.0 %collective-permute-start.27 = (bf16[104,512]{1,0:T(8,128)(2,1)S(1)}, bf16[104,512]{1,0:T(8,128)(2,1)S(1)}, u32[]{:S(2)}, u32[]{:S(2)}) collective-permute-start(bf16[104,512]{1,0:T(8,128)(2,1)S(1)} %dynamic-slice_add_fusion), channel_id=1, source_target_pairs={{0,16},{8,24},{16,0},{24,8},{1,17},{9,25},{17,1},{25,9},{2,18},{10... | collective-permute-start | bytes 319496 | tf_op jit(solution)/shard_map/ppermute | solution.py:39
  141.0 5.2 %collective-permute-done.27 = bf16[104,512]{1,0:T(8,128)(2,1)S(1)} collective-permute-done((bf16[104,512]{1,0:T(8,128)(2,1)S(1)}, bf16[104,512]{1,0:T(8,128)(2,1)S(1)}, u32[]{:S(2)}, u32[]{:S(2)}) %collective-permute-start.27) | collective-permute-done | bytes 106528 | tf_op jit(solution)/shard_map/ppermute | solution.py:39
  146.3 4.1 %collective-permute-start.28 = (bf16[104,512]{1,0:T(8,128)(2,1)S(1)}, bf16[104,512]{1,0:T(8,128)(2,1)S(1)}, u32[]{:S(2)}, u32[]{:S(2)}) collective-permute-start(bf16[104,512]{1,0:T(8,128)(2,1)S(1)} %add.119.s), channel_id=1, source_target_pairs={{0,8},{8,0},{16,24},{24,16},{1,9},{9,1},{17,25},{25,17},{2,10},{10... | collective-permute-start | bytes 319496 | tf_op jit(solution)/shard_map/ppermute | solution.py:39
  150.5 1.7 %finish_rest.1 = (f32[256,512]{1,0:T(8,128)}, f32[64,2048]{1,0:T(8,128)}, f32[64,512]{1,0:T(8,128)}, f32[1,256]{1,0:T(1,128)}, f32[1,64]{1,0:T(1,128)}, /*index=...) custom-call(s32[2]{0:T(128)S(1)} %pad_add_fusion.ids, bf16[296,512]{1,0:T(8,128)(2,1)S(1)} %add.117.s, ...), custom_call_target="tpu_custom_call" | custom-call | bytes 1212416 | tf_op jit(solution)/shard_map/finish_rest/pallas_call | solution.py:201
  153.1 1.6 %finish_first.1 = (f32[64,1536]{1,0:T(8,128)}, f32[1,64]{1,0:T(1,128)}, f32[1,64]{1,0:T(1,128)}, f32[1,64]{1,0:T(1,128)}, f32[1,64]{1,0:T(1,128)}) custom-call(s32[2]{0:T(128)S(1)} %pad_add_fusion.ids, bf16[104,512]{1,0:T(8,128)(2,1)S(1)} %add.119.s, bf16[104,512]{1,0:T(8,128)(2,1)S(1)} %collective-permute-done.28.o, bf16[64,1536]{1,0:T(8,128)(2,1)S(1)} %copy-done, ...), custom_call_target="tpu_custom_call" | custom-call | bytes 786432 | tf_op jit(solution)/shard_map/finish_first/pallas_call | solution.py:245
  (97 shorter events, 26.4 us)
Async XLA Ops:
  2.4 10.6 %collective-permute-start = (bf16[208,512]{1,0:T(8,128)(2,1)}, bf16[208,512]{1,0:T(8,128)(2,1)S(1)}, u32[]{:S(2)}, u32[]{:S(2)}) collective-permute-start(bf16[208,512]{1,0:T(8,128)(2,1)} %pack_first.1.refs_0_), channel_id=1, source_target_pairs={{0,2},{1,3},{2,0},{3,1},{4,6},{5,7},{6,4},{7,5},{8,10},{9,11},{10,... | collective-permute-start | bytes 638984 | tf_op jit(solution)/shard_map/ppermute | solution.py:43
  5.4 11.5 %collective-permute-start.1 = (bf16[208,512]{1,0:T(8,128)(2,1)}, bf16[208,512]{1,0:T(8,128)(2,1)S(1)}, u32[]{:S(2)}, u32[]{:S(2)}) collective-permute-start(bf16[208,512]{1,0:T(8,128)(2,1)} %pack_first.1.refs_0_), channel_id=1, source_target_pairs={{0,4},{1,5},{2,6},{3,7},{4,0},{5,1},{6,2},{7,3},{8,12},{9,13},{10,... | collective-permute-start | bytes 638984 | tf_op jit(solution)/shard_map/ppermute | solution.py:43
  6.9 10.0 %collective-permute-start.2 = (bf16[208,512]{1,0:T(8,128)(2,1)}, bf16[208,512]{1,0:T(8,128)(2,1)S(1)}, u32[]{:S(2)}, u32[]{:S(2)}) collective-permute-start(bf16[208,512]{1,0:T(8,128)(2,1)} %pack_first.1.refs_0_), channel_id=1, source_target_pairs={{0,6},{1,7},{2,4},{3,5},{4,2},{5,3},{6,0},{7,1},{8,14},{9,15},{10,... | collective-permute-start | bytes 638984 | tf_op jit(solution)/shard_map/ppermute | solution.py:43
  6.9 12.6 %collective-permute-start.3 = (bf16[208,512]{1,0:T(8,128)(2,1)}, bf16[208,512]{1,0:T(8,128)(2,1)S(1)}, u32[]{:S(2)}, u32[]{:S(2)}) collective-permute-start(bf16[208,512]{1,0:T(8,128)(2,1)} %pack_first.1.refs_0_), channel_id=1, source_target_pairs={{0,1},{1,0},{2,3},{3,2},{4,5},{5,4},{6,7},{7,6},{8,9},{9,8},{10,11... | collective-permute-start | bytes 638984 | tf_op jit(solution)/shard_map/ppermute | solution.py:43
  13.0 7.3 %collective-permute-start.4 = (bf16[208,512]{1,0:T(8,128)(2,1)S(1)}, bf16[208,512]{1,0:T(8,128)(2,1)S(1)}, u32[]{:S(2)}, u32[]{:S(2)}) collective-permute-start(bf16[208,512]{1,0:T(8,128)(2,1)S(1)} %collective-permute-done.refs_1_), channel_id=1, source_target_pairs={{0,1},{1,0},{2,3},{3,2},{4,5},{5,4},{6,7},{7,6},{8,9},{9,8},{10,11... | collective-permute-start | bytes 638984 | tf_op jit(solution)/shard_map/ppermute | solution.py:43
  17.4 27.2 %collective-permute-start.9 = (bf16[576,512]{1,0:T(8,128)(2,1)}, bf16[576,512]{1,0:T(8,128)(2,1)S(1)}, u32[]{:S(2)}, u32[]{:S(2)}) collective-permute-start(bf16[576,512]{1,0:T(8,128)(2,1)} %pack_rest.1.refs_0_), channel_id=1, source_target_pairs={{0,6},{1,7},{2,4},{3,5},{4,2},{5,3},{6,0},{7,1},{8,14},{9,15},{10,... | collective-permute-start | bytes 1769480 | tf_op jit(solution)/shard_map/ppermute | solution.py:43
  19.5 26.9 %collective-permute-start.8 = (bf16[576,512]{1,0:T(8,128)(2,1)}, bf16[576,512]{1,0:T(8,128)(2,1)S(1)}, u32[]{:S(2)}, u32[]{:S(2)}) collective-permute-start(bf16[576,512]{1,0:T(8,128)(2,1)} %pack_rest.1.refs_0_), channel_id=1, source_target_pairs={{0,4},{1,5},{2,6},{3,7},{4,0},{5,1},{6,2},{7,3},{8,12},{9,13},{10,... | collective-permute-start | bytes 1769480 | tf_op jit(solution)/shard_map/ppermute | solution.py:43
  20.3 26.2 %collective-permute-start.7 = (bf16[576,512]{1,0:T(8,128)(2,1)}, bf16[576,512]{1,0:T(8,128)(2,1)S(1)}, u32[]{:S(2)}, u32[]{:S(2)}) collective-permute-start(bf16[576,512]{1,0:T(8,128)(2,1)} %pack_rest.1.refs_0_), channel_id=1, source_target_pairs={{0,2},{1,3},{2,0},{3,1},{4,6},{5,7},{6,4},{7,5},{8,10},{9,11},{10,... | collective-permute-start | bytes 1769480 | tf_op jit(solution)/shard_map/ppermute | solution.py:43
  21.6 25.3 %collective-permute-start.10 = (bf16[576,512]{1,0:T(8,128)(2,1)}, bf16[576,512]{1,0:T(8,128)(2,1)S(1)}, u32[]{:S(2)}, u32[]{:S(2)}) collective-permute-start(bf16[576,512]{1,0:T(8,128)(2,1)} %pack_rest.1.refs_0_), channel_id=1, source_target_pairs={{0,1},{1,0},{2,3},{3,2},{4,5},{5,4},{6,7},{7,6},{8,9},{9,8},{10,11... | collective-permute-start | bytes 1769480 | tf_op jit(solution)/shard_map/ppermute | solution.py:43
  75.3 8.4 %collective-permute-start.14 = (bf16[4,320,512]{2,1,0:T(8,128)(2,1)}, bf16[4,320,512]{2,1,0:T(8,128)(2,1)S(1)}, u32[]{:S(2)}, u32[]{:S(2)}) collective-permute-start(bf16[4,320,512]{2,1,0:T(8,128)(2,1)} %get-tuple-element.91), channel_id=1, source_target_pairs={{0,1},{1,0},{2,3},{3,2},{4,5},{5,4},{6,7},{7,6},{8,9},{9,8},{10,11... | collective-permute-start | bytes 3932168 | tf_op jit(solution)/shard_map/ppermute | solution.py:43
  75.5 8.1 %collective-permute-start.15 = (bf16[4,272,512]{2,1,0:T(8,128)(2,1)}, bf16[4,272,512]{2,1,0:T(8,128)(2,1)S(1)}, u32[]{:S(2)}, u32[]{:S(2)}) collective-permute-start(bf16[4,272,512]{2,1,0:T(8,128)(2,1)} %get-tuple-element.92), channel_id=1, source_target_pairs={{0,1},{1,0},{2,3},{3,2},{4,5},{5,4},{6,7},{7,6},{8,9},{9,8},{10,11... | collective-permute-start | bytes 3342344 | tf_op jit(solution)/shard_map/ppermute | solution.py:43
  84.6 18.4 %collective-permute-start.17 = (bf16[2,272,512]{2,1,0:T(8,128)(2,1)}, bf16[2,272,512]{2,1,0:T(8,128)(2,1)}, u32[]{:S(2)}, u32[]{:S(2)}) collective-permute-start(bf16[2,272,512]{2,1,0:T(8,128)(2,1)} %get-tuple-element.134), channel_id=1, source_target_pairs={{0,2},{1,3},{2,0},{3,1},{4,6},{5,7},{6,4},{7,5},{8,10},{9,11},{10,... | collective-permute-start | bytes 1671176 | tf_op jit(solution)/shard_map/ppermute | solution.py:43
  86.0 17.0 %collective-permute-start.16 = (bf16[2,320,512]{2,1,0:T(8,128)(2,1)S(1)}, bf16[2,320,512]{2,1,0:T(8,128)(2,1)S(1)}, u32[]{:S(2)}, u32[]{:S(2)}) collective-permute-start(bf16[2,320,512]{2,1,0:T(8,128)(2,1)S(1)} %get-tuple-element.131), channel_id=1, source_target_pairs={{0,4},{1,5},{2,6},{3,7},{4,0},{5,1},{6,2},{7,3},{8,12},{9,13},{10,... | collective-permute-start | bytes 1966088 | tf_op jit(solution)/shard_map/ppermute | solution.py:43
  104.2 8.5 %collective-permute-start.19 = (bf16[1,272,512]{2,1,0:T(8,128)(2,1)S(1)}, bf16[1,272,512]{2,1,0:T(8,128)(2,1)S(1)}, u32[]{:S(2)}, u32[]{:S(2)}) collective-permute-start(bf16[1,272,512]{2,1,0:T(8,128)(2,1)S(1)} %get-tuple-element.141), channel_id=1, source_target_pairs={{0,4},{1,5},{2,6},{3,7},{4,0},{5,1},{6,2},{7,3},{8,12},{9,13},{10,... | collective-permute-start | bytes 835592 | tf_op jit(solution)/shard_map/ppermute | solution.py:43
  105.3 8.9 %collective-permute-start.18 = (bf16[1,320,512]{2,1,0:T(8,128)(2,1)S(1)}, bf16[1,320,512]{2,1,0:T(8,128)(2,1)S(1)}, u32[]{:S(2)}, u32[]{:S(2)}) collective-permute-start(bf16[1,320,512]{2,1,0:T(8,128)(2,1)S(1)} %get-tuple-element.138), channel_id=1, source_target_pairs={{0,2},{1,3},{2,0},{3,1},{4,6},{5,7},{6,4},{7,5},{8,10},{9,11},{10,... | collective-permute-start | bytes 983048 | tf_op jit(solution)/shard_map/ppermute | solution.py:43
  114.7 7.5 %collective-permute-start.20 = (bf16[296,512]{1,0:T(8,128)(2,1)S(1)}, bf16[296,512]{1,0:T(8,128)(2,1)S(1)}, u32[]{:S(2)}, u32[]{:S(2)}) collective-permute-start(bf16[296,512]{1,0:T(8,128)(2,1)S(1)} %fusion.3), channel_id=1, source_target_pairs={{0,8},{8,0},{16,24},{24,16},{1,9},{9,1},{17,25},{25,17},{2,10},{10... | collective-permute-start | bytes 909320 | tf_op jit(solution)/shard_map/ppermute | solution.py:39
  117.2 15.0 %collective-permute-start.22 = (bf16[208,512]{1,0:T(8,128)(2,1)}, bf16[208,512]{1,0:T(8,128)(2,1)S(1)}, u32[]{:S(2)}, u32[]{:S(2)}) collective-permute-start(bf16[208,512]{1,0:T(8,128)(2,1)} %get-tuple-element.135), channel_id=1, source_target_pairs={{0,6},{1,7},{2,4},{3,5},{4,2},{5,3},{6,0},{7,1},{8,14},{9,15},{10,... | collective-permute-start | bytes 638984 | tf_op jit(solution)/shard_map/ppermute | solution.py:43
  119.0 13.1 %collective-permute-start.23 = (bf16[208,512]{1,0:T(8,128)(2,1)}, bf16[208,512]{1,0:T(8,128)(2,1)S(1)}, u32[]{:S(2)}, u32[]{:S(2)}) collective-permute-start(bf16[208,512]{1,0:T(8,128)(2,1)} %get-tuple-element.136), channel_id=1, source_target_pairs={{0,4},{1,5},{2,6},{3,7},{4,0},{5,1},{6,2},{7,3},{8,12},{9,13},{10,... | collective-permute-start | bytes 638984 | tf_op jit(solution)/shard_map/ppermute | solution.py:43
  119.6 12.6 %collective-permute-start.24 = (bf16[208,512]{1,0:T(8,128)(2,1)}, bf16[208,512]{1,0:T(8,128)(2,1)S(1)}, u32[]{:S(2)}, u32[]{:S(2)}) collective-permute-start(bf16[208,512]{1,0:T(8,128)(2,1)} %get-tuple-element.137), channel_id=1, source_target_pairs={{0,2},{1,3},{2,0},{3,1},{4,6},{5,7},{6,4},{7,5},{8,10},{9,11},{10,... | collective-permute-start | bytes 638984 | tf_op jit(solution)/shard_map/ppermute | solution.py:43
  122.6 14.1 %collective-permute-start.26 = (bf16[296,512]{1,0:T(8,128)(2,1)S(1)}, bf16[296,512]{1,0:T(8,128)(2,1)S(1)}, u32[]{:S(2)}, u32[]{:S(2)}) collective-permute-start(bf16[296,512]{1,0:T(8,128)(2,1)S(1)} %fusion.5), channel_id=1, source_target_pairs={{0,16},{8,24},{16,0},{24,8},{1,17},{9,25},{17,1},{25,9},{2,18},{10... | collective-permute-start | bytes 909320 | tf_op jit(solution)/shard_map/ppermute | solution.py:39
  132.4 6.6 %collective-permute-start.25 = (bf16[104,512]{1,0:T(8,128)(2,1)S(1)}, bf16[104,512]{1,0:T(8,128)(2,1)S(1)}, u32[]{:S(2)}, u32[]{:S(2)}) collective-permute-start(bf16[104,512]{1,0:T(8,128)(2,1)S(1)} %constant_dynamic-slice_fusion), channel_id=1, source_target_pairs={{0,8},{8,0},{16,24},{24,16},{1,9},{9,1},{17,25},{25,17},{2,10},{10... | collective-permute-start | bytes 319496 | tf_op jit(solution)/shard_map/ppermute | solution.py:39
  136.8 13.7 %collective-permute-start.29 = (bf16[296,512]{1,0:T(8,128)(2,1)S(1)}, bf16[296,512]{1,0:T(8,128)(2,1)S(1)}, u32[]{:S(2)}, u32[]{:S(2)}) collective-permute-start(bf16[296,512]{1,0:T(8,128)(2,1)S(1)} %add.117.s), channel_id=1, source_target_pairs={{0,8},{8,0},{16,24},{24,16},{1,9},{9,1},{17,25},{25,17},{2,10},{10... | collective-permute-start | bytes 909320 | tf_op jit(solution)/shard_map/ppermute | solution.py:39
  139.0 7.2 %collective-permute-start.27 = (bf16[104,512]{1,0:T(8,128)(2,1)S(1)}, bf16[104,512]{1,0:T(8,128)(2,1)S(1)}, u32[]{:S(2)}, u32[]{:S(2)}) collective-permute-start(bf16[104,512]{1,0:T(8,128)(2,1)S(1)} %dynamic-slice_add_fusion), channel_id=1, source_target_pairs={{0,16},{8,24},{16,0},{24,8},{1,17},{9,25},{17,1},{25,9},{2,18},{10... | collective-permute-start | bytes 319496 | tf_op jit(solution)/shard_map/ppermute | solution.py:39
  146.3 6.8 %collective-permute-start.28 = (bf16[104,512]{1,0:T(8,128)(2,1)S(1)}, bf16[104,512]{1,0:T(8,128)(2,1)S(1)}, u32[]{:S(2)}, u32[]{:S(2)}) collective-permute-start(bf16[104,512]{1,0:T(8,128)(2,1)S(1)} %add.119.s), channel_id=1, source_target_pairs={{0,8},{8,0},{16,24},{24,16},{1,9},{9,1},{17,25},{25,17},{2,10},{10... | collective-permute-start | bytes 319496 | tf_op jit(solution)/shard_map/ppermute | solution.py:39
  (23 other events, 197.8 us)

commit v16 on v15

--- a/solution.py
+++ b/solution.py
@@ -743,7 +743,9 @@
     h = n // 4
     lo, hi = slice(0, h), slice(h, None)
     add = lambda a, b, s: add16(a[s], b[s])
-    ka, xa, kb, xb = add(ka, ga, lo), add(ka, ga, hi), add(kb, gb, lo), add(kb, gb, hi)
+    ka, xa = add(ka, ga, lo), add(ka, ga, hi)
+    kb, gb, _ = lax.optimization_barrier((kb, gb, xa))
+    kb, xb = add(kb, gb, lo), add(kb, gb, hi)
     g = bwd(1, NP - 1, [g], ka, xa, kb, xb)
     m = (n // 2).bit_length() - 1
     ga, gb = swap(xa, 2 << (m - 1)), swap(xb, 2)
@@ -753,6 +755,7 @@
         h //= 2
         lo, hi = slice(0, h), slice(h, None)
         ka, xa = add(ka, ga, lo), add(ka, ga, hi)
+        kb, gb, _ = lax.optimization_barrier((kb, gb, xa))
         kb, xb = add(kb, gb, lo), add(kb, gb, hi)
         ga, gb = swap(xa, 2 << (m - 1 - t)), swap(xb, 2 << t)
         if t == 1:

time: 155 us -> 157 us (1.013)
    ppermute x6, waiting for transfers between devices: 11.8 us -> 14 us  [rep_perm(): return lax.ppermute(x, 'rep', xor_perm(lax.axis_size('rep'), b))]
  transfers between devices with their start and end apart: 30 -> 30, of which waited for: 12 -> 11; matrix products, arithmetic and copies ran while one was open for 2% -> 3% of each run, Pallas kernels for 43% -> 42%
where the time goes in v16:
time: 157 us
  Pallas kernels  95.6 us (61%)
  starting transfers between devices  31.8 us (20%)
  waiting for transfers between devices  22.2 us (14%)
  other arithmetic  4.77 us (3%)
  between operations  1.66 us (1%)
    pallas_call x1, Pallas kernels, ffn(): pl.pallas_call(functools.partial(ffn_body, n, meta, min(1024, FF)), grid_...  26 us
    pallas_call x2, Pallas kernels, attn_bwd(): pl.pallas_call(functools.partial(attn_bwd_body, HD, 1.0 / math.sqrt(HD),...  23.8 us
    ppermute x24, starting transfers between devices, swap(): return lax.ppermute(x, 'shard', xor_perm(lax.axis_size('shard'), k))  19 us
    pallas_call x1, Pallas kernels, attn_fwd(): pl.pallas_call(functools.partial(attn_fwd_body, HD, bi, min(512, T), p0),...  15.1 us
    ppermute x6, waiting for transfers between devices, rep_perm(): return lax.ppermute(x, 'rep', xor_perm(lax.axis_size('rep'), b))  14 us
    ppermute x6, starting transfers between devices, rep_perm(): return lax.ppermute(x, 'rep', xor_perm(lax.axis_size('rep'), b))  12.8 us
    ppermute x24, waiting for transfers between devices, swap(): return lax.ppermute(x, 'shard', xor_perm(lax.axis_size('shard'), k))  8.14 us
    pallas_call x1, Pallas kernels, front(): pl.pallas_call(functools.partial(front_body, scale, n, meta), grid_spec=p...  7.08 us
  transfers between devices with their start and end apart: 30, of which 11 were waited for; matrix products, arithmetic and copies ran while one was open for 3% of the time, Pallas kernels for 42%

profile of v16, /device:TPU:0, one launch (start us, length us, event | category | flops | bytes accessed | tf_op | source)
XLA Modules:
  0.0 156.8 jit_solution(15106891617393860162)
XLA Ops:
  0.7 1.8 %pack_first.1.refs_0_ = bf16[208,512]{1,0:T(8,128)(2,1)} custom-call(s32[1]{0:T(128)} %bitcast.me, bf16[64,1536]{1,0:T(8,128)(2,1)} %w.3, bf16[2,128]{1,0:T(2,128)(2,1)} %bitcast.47, bf16[1,64]{1,0:T(2,128)(2,1)} %bitcast.39, bf16[1,64]{1,0:T(2,128)(2,1)} %bitcast.41, bf16[1,64]{1,0:T(2,128)(2,1)} %bitcast.48, bf16[1,64]{1,0:T(2,128)(2,1)} %bitcast.49, ...), custom_call_target="tpu_custom_call" | custom-call | bytes 393216 | tf_op jit(solution)/shard_map/pack_first/pallas_call | solution.py:125
  2.4 2.9 %collective-permute-start = (bf16[208,512]{1,0:T(8,128)(2,1)}, bf16[208,512]{1,0:T(8,128)(2,1)S(1)}, u32[]{:S(2)}, u32[]{:S(2)}) collective-permute-start(bf16[208,512]{1,0:T(8,128)(2,1)} %pack_first.1.refs_0_), channel_id=1, source_target_pairs={{0,2},{1,3},{2,0},{3,1},{4,6},{5,7},{6,4},{7,5},{8,10},{9,11},{10,... | collective-permute-start | bytes 638984 | tf_op jit(solution)/shard_map/ppermute | solution.py:43
  5.4 1.5 collective-permute-start.1
  6.9 1.9 %pack_rest.1.refs_0_ = bf16[576,512]{1,0:T(8,128)(2,1)} custom-call(bf16[64,512]{1,0:T(8,128)(2,1)} %wo.1, bf16[64,2048]{1,0:T(8,128)(2,1)} %wu.1, bf16[256,512]{1,0:T(8,128)(2,1)} %wd.1), custom_call_target="tpu_custom_call" | custom-call | bytes 524288 | tf_op jit(solution)/shard_map/pack_rest/pallas_call | solution.py:143
  8.8 4.2 %start.1 = (f32[1024,512]{1,0:T(8,128)}, bf16[528,1024]{1,0:T(8,128)(2,1)}) custom-call(bf16[1024,512]{1,0:T(8,128)(2,1)} %bitcast.43, bf16[1,512]{1,0:T(2,128)(2,1)} %step.4), custom_call_target="tpu_custom_call" | custom-call | flops 10485760 | bytes 4194304 | tf_op jit(solution)/shard_map/start/pallas_call | solution.py:287
  13.6 3.2 %collective-permute-done.1.refs_2_ = bf16[208,512]{1,0:T(8,128)(2,1)S(1)} collective-permute-done((bf16[208,512]{1,0:T(8,128)(2,1)}, bf16[208,512]{1,0:T(8,128)(2,1)S(1)}, u32[]{:S(2)}, u32[]{:S(2)}) %collective-permute-start.1) | collective-permute-done | bytes 213024 | tf_op jit(solution)/shard_map/ppermute | solution.py:43
  22.4 7.1 %front.1 = (bf16[2,1024,512]{2,1,0:T(8,128)(2,1)}, bf16[3,512,1024]{2,1,0:T(8,128)(2,1)}, bf16[512,1536]{1,0:T(8,128)(2,1)}, f32[8,512]{1,0:T(8,128)}, f32[1,2048]{1,0:T(1,128)}) custom-call(s32[1]{0:T(128)} %bitcast.me, f32[1024,512]{1,0:T(8,128)} %get-tuple-element.77.nx, bf16[208,512]{1,0:T(8,128)(2,1)} %pack_first.1.refs_0_, ...), custom_call_target="tpu_custom_call" | custom-call | flops 1610612736 | bytes 6291456 | tf_op jit(solution)/shard_map/front/pallas_call | solution.py:360
  29.5 15.1 %attn_fwd.1 = (bf16[8,1024,1024]{2,1,0:T(8,128)(2,1)}, bf16[1024,512]{1,0:T(8,128)(2,1)}, bf16[512,1024]{1,0:T(8,128)(2,1)}, f32[512,1024]{1,0:T(8,128)}, f32[4,8,1024]{2,1,0:T(8,128)}) custom-call(s32[1]{0:T(128)S(6)} %copy.34.ln, bf16[2,1024,512]{2,1,0:T(8,128)(2,1)} %get-tuple-element.84.k.v, bf16[3,512,1024]{2,1,0:T(8,128)(2,1)} %get-tuple-element.85.qt.vt.kt, ...), custom_call_target="tpu_custom_call" | custom-call | flops 8589934592 | bytes 16777216 | tf_op jit(solution)/shard_map/attn_fwd/pallas_call | solution.py:450
  49.3 26.0 %ffn.1 = (bf16[1024,512]{1,0:T(8,128)(2,1)}, bf16[1024,512]{1,0:T(8,128)(2,1)}, bf16[512,1024]{1,0:T(8,128)(2,1)}, bf16[4,320,512]{2,1,0:T(8,128)(2,1)}, bf16[4,...) custom-call(s32[1]{0:T(128)S(6)} %copy.34.ln, s32[1]{0:T(128)} %bitcast.me, ...), custom_call_target="tpu_custom_call" | custom-call | flops 14495514624 | bytes 8388608 | tf_op jit(solution)/shard_map/ffn/pallas_call | solution.py:606
  75.9 7.8 %attn_bwd.2.refs_0_ = bf16[3,512,1024]{2,1,0:T(8,128)(2,1)} custom-call(bf16[2,1024,512]{2,1,0:T(8,128)(2,1)} %get-tuple-element.84.k.v, bf16[3,512,1024]{2,1,0:T(8,128)(2,1)} %get-tuple-element.85.qt.vt.kt, bf16[3,512,1024]{2,1,0:T(8,128)(2,1)} %get-tuple-element.85.qt.vt.kt, bf16[512,1024]{1,0:T(8,128)(2,1)} %get-tuple-element.105.gt, ...), custom_call_target="tpu_custom_call" | custom-call | flops 4294967296 | bytes 4194304 | tf_op jit(solution)/shard_map/attn_bwd/pallas_call | solution.py:650
  83.8 1.6 %collective-permute-start.16 = (bf16[2,320,512]{2,1,0:T(8,128)(2,1)S(1)}, bf16[2,320,512]{2,1,0:T(8,128)(2,1)S(1)}, u32[]{:S(2)}, u32[]{:S(2)}) collective-permute-start(bf16[2,320,512]{2,1,0:T(8,128)(2,1)S(1)} %get-tuple-element.139), channel_id=1, source_target_pairs={{0,4},{1,5},{2,6},{3,7},{4,0},{5,1},{6,2},{7,3},{8,12},{9,13},{10,... | collective-permute-start | bytes 1966088 | tf_op jit(solution)/shard_map/ppermute | solution.py:43
  87.6 16.0 %attn_bwd.3.g = bf16[3,512,1024]{2,1,0:T(8,128)(2,1)} custom-call(bf16[2,1024,512]{2,1,0:T(8,128)(2,1)} %get-tuple-element.84.k.v, bf16[3,512,1024]{2,1,0:T(8,128)(2,1)} %get-tuple-element.85.qt.vt.kt, bf16[3,512,1024]{2,1,0:T(8,128)(2,1)} %get-tuple-element.85.qt.vt.kt, bf16[512,1024]{1,0:T(8,128)(2,1)} %get-tuple-element.105.gt, ...), custom_call_target="tpu_custom_call", output_to_operand_aliasing={{}: (7, {})} | custom-call | flops 12884901888 | bytes 12582912 | tf_op jit(solution)/shard_map/attn_bwd/pallas_call | solution.py:650
  107.3 5.6 %wqkv.1 = (bf16[4,208,512]{2,1,0:T(8,128)(2,1)}, bf16[4,208,512]{2,1,0:T(8,128)(2,1)}) custom-call(s32[1]{0:T(128)} %bitcast.me, bf16[528,1024]{1,0:T(8,128)(2,1)} %get-tuple-element.110.xht, bf16[3,512,1024]{2,1,0:T(8,128)(2,1)} %attn_bwd.3.g), custom_call_target="tpu_custom_call" | custom-call | flops 1610612736 | bytes 5242880 | tf_op jit(solution)/shard_map/wqkv/pallas_call | solution.py:686
  114.6 1.6 %collective-permute-start.20 = (bf16[296,512]{1,0:T(8,128)(2,1)S(1)}, bf16[296,512]{1,0:T(8,128)(2,1)S(1)}, u32[]{:S(2)}, u32[]{:S(2)}) collective-permute-start(bf16[296,512]{1,0:T(8,128)(2,1)S(1)} %fusion.3), channel_id=1, source_target_pairs={{0,8},{8,0},{16,24},{24,16},{1,9},{9,1},{17,25},{25,17},{2,10},{10... | collective-permute-start | bytes 909320 | tf_op jit(solution)/shard_map/ppermute | solution.py:39
  120.5 2.6 %collective-permute-done.20 = bf16[296,512]{1,0:T(8,128)(2,1)S(1)} collective-permute-done((bf16[296,512]{1,0:T(8,128)(2,1)S(1)}, bf16[296,512]{1,0:T(8,128)(2,1)S(1)}, u32[]{:S(2)}, u32[]{:S(2)}) %collective-permute-start.20) | collective-permute-done | bytes 303136 | tf_op jit(solution)/shard_map/ppermute | solution.py:39
  123.5 2.7 %collective-permute-start.26 = (bf16[296,512]{1,0:T(8,128)(2,1)S(1)}, bf16[296,512]{1,0:T(8,128)(2,1)S(1)}, u32[]{:S(2)}, u32[]{:S(2)}) collective-permute-start(bf16[296,512]{1,0:T(8,128)(2,1)S(1)} %fusion.5), channel_id=1, source_target_pairs={{0,16},{8,24},{16,0},{24,8},{1,17},{9,25},{17,1},{25,9},{2,18},{10... | collective-permute-start | bytes 909320 | tf_op jit(solution)/shard_map/ppermute | solution.py:39
  126.2 6.9 %back.1 = f32[1024,512]{1,0:T(8,128)} custom-call(bf16[1024,512]{1,0:T(8,128)(2,1)} %bitcast.45, bf16[1,512]{1,0:T(2,128)(2,1)} %step.4, f32[8,512]{1,0:T(8,128)} %get-tuple-element.82.vec, bf16[3,512,1024]{2,1,0:T(8,128)(2,1)} %attn_bwd.3.g, bf16[1024,512]{1,0:T(8,128)(2,1)} %get-tuple-element.117.gx1, bf16[512,1536]{1,0:T(8,128)(2,1)} %get-tuple-element.118.refs_0_), custom_call_target="tpu_custom_call" | custom-call | flops 1610612736 | bytes 7340032 | tf_op jit(solution)/shard_map/back/pallas_call | solution.py:713
  133.3 1.6 %collective-permute-start.25 = (bf16[104,512]{1,0:T(8,128)(2,1)S(1)}, bf16[104,512]{1,0:T(8,128)(2,1)S(1)}, u32[]{:S(2)}, u32[]{:S(2)}) collective-permute-start(bf16[104,512]{1,0:T(8,128)(2,1)S(1)} %constant_dynamic-slice_fusion), channel_id=1, source_target_pairs={{0,8},{8,0},{16,24},{24,16},{1,9},{9,1},{17,25},{25,17},{2,10},{10... | collective-permute-start | bytes 319496 | tf_op jit(solution)/shard_map/ppermute | solution.py:39
  134.9 3.7 %collective-permute-done.26 = bf16[296,512]{1,0:T(8,128)(2,1)S(1)} collective-permute-done((bf16[296,512]{1,0:T(8,128)(2,1)S(1)}, bf16[296,512]{1,0:T(8,128)(2,1)S(1)}, u32[]{:S(2)}, u32[]{:S(2)}) %collective-permute-start.26) | collective-permute-done | bytes 303136 | tf_op jit(solution)/shard_map/ppermute | solution.py:39
  140.9 2.0 %collective-permute-start.27 = (bf16[104,512]{1,0:T(8,128)(2,1)S(1)}, bf16[104,512]{1,0:T(8,128)(2,1)S(1)}, u32[]{:S(2)}, u32[]{:S(2)}) collective-permute-start(bf16[104,512]{1,0:T(8,128)(2,1)S(1)} %dynamic-slice_add_fusion), channel_id=1, source_target_pairs={{0,16},{8,24},{16,0},{24,8},{1,17},{9,25},{17,1},{25,9},{2,18},{10... | collective-permute-start | bytes 319496 | tf_op jit(solution)/shard_map/ppermute | solution.py:39
  142.9 5.4 %collective-permute-done.27 = bf16[104,512]{1,0:T(8,128)(2,1)S(1)} collective-permute-done((bf16[104,512]{1,0:T(8,128)(2,1)S(1)}, bf16[104,512]{1,0:T(8,128)(2,1)S(1)}, u32[]{:S(2)}, u32[]{:S(2)}) %collective-permute-start.27) | collective-permute-done | bytes 106528 | tf_op jit(solution)/shard_map/ppermute | solution.py:39
  148.3 4.2 %collective-permute-start.28 = (bf16[104,512]{1,0:T(8,128)(2,1)S(1)}, bf16[104,512]{1,0:T(8,128)(2,1)S(1)}, u32[]{:S(2)}, u32[]{:S(2)}) collective-permute-start(bf16[104,512]{1,0:T(8,128)(2,1)S(1)} %add.119.s), channel_id=1, source_target_pairs={{0,8},{8,0},{16,24},{24,16},{1,9},{9,1},{17,25},{25,17},{2,10},{10... | collective-permute-start | bytes 319496 | tf_op jit(solution)/shard_map/ppermute | solution.py:39
  152.6 1.7 %finish_rest.1 = (f32[256,512]{1,0:T(8,128)}, f32[64,2048]{1,0:T(8,128)}, f32[64,512]{1,0:T(8,128)}, f32[1,256]{1,0:T(1,128)}, f32[1,64]{1,0:T(1,128)}, /*index=...) custom-call(s32[2]{0:T(128)S(1)} %pad_add_fusion.ids, bf16[296,512]{1,0:T(8,128)(2,1)S(1)} %add.117.s, ...), custom_call_target="tpu_custom_call" | custom-call | bytes 1212416 | tf_op jit(solution)/shard_map/finish_rest/pallas_call | solution.py:201
  155.2 1.6 finish_first.1
  (97 shorter events, 26.5 us)
Async XLA Ops:
  2.4 10.6 %collective-permute-start = (bf16[208,512]{1,0:T(8,128)(2,1)}, bf16[208,512]{1,0:T(8,128)(2,1)S(1)}, u32[]{:S(2)}, u32[]{:S(2)}) collective-permute-start(bf16[208,512]{1,0:T(8,128)(2,1)} %pack_first.1.refs_0_), channel_id=1, source_target_pairs={{0,2},{1,3},{2,0},{3,1},{4,6},{5,7},{6,4},{7,5},{8,10},{9,11},{10,... | collective-permute-start | bytes 638984 | tf_op jit(solution)/shard_map/ppermute | solution.py:43
  5.4 11.5 %collective-permute-start.1 = (bf16[208,512]{1,0:T(8,128)(2,1)}, bf16[208,512]{1,0:T(8,128)(2,1)S(1)}, u32[]{:S(2)}, u32[]{:S(2)}) collective-permute-start(bf16[208,512]{1,0:T(8,128)(2,1)} %pack_first.1.refs_0_), channel_id=1, source_target_pairs={{0,4},{1,5},{2,6},{3,7},{4,0},{5,1},{6,2},{7,3},{8,12},{9,13},{10,... | collective-permute-start | bytes 638984 | tf_op jit(solution)/shard_map/ppermute | solution.py:43
  6.9 10.0 %collective-permute-start.2 = (bf16[208,512]{1,0:T(8,128)(2,1)}, bf16[208,512]{1,0:T(8,128)(2,1)S(1)}, u32[]{:S(2)}, u32[]{:S(2)}) collective-permute-start(bf16[208,512]{1,0:T(8,128)(2,1)} %pack_first.1.refs_0_), channel_id=1, source_target_pairs={{0,6},{1,7},{2,4},{3,5},{4,2},{5,3},{6,0},{7,1},{8,14},{9,15},{10,... | collective-permute-start | bytes 638984 | tf_op jit(solution)/shard_map/ppermute | solution.py:43
  6.9 12.6 %collective-permute-start.3 = (bf16[208,512]{1,0:T(8,128)(2,1)}, bf16[208,512]{1,0:T(8,128)(2,1)S(1)}, u32[]{:S(2)}, u32[]{:S(2)}) collective-permute-start(bf16[208,512]{1,0:T(8,128)(2,1)} %pack_first.1.refs_0_), channel_id=1, source_target_pairs={{0,1},{1,0},{2,3},{3,2},{4,5},{5,4},{6,7},{7,6},{8,9},{9,8},{10,11... | collective-permute-start | bytes 638984 | tf_op jit(solution)/shard_map/ppermute | solution.py:43
  13.0 7.3 %collective-permute-start.4 = (bf16[208,512]{1,0:T(8,128)(2,1)S(1)}, bf16[208,512]{1,0:T(8,128)(2,1)S(1)}, u32[]{:S(2)}, u32[]{:S(2)}) collective-permute-start(bf16[208,512]{1,0:T(8,128)(2,1)S(1)} %collective-permute-done.refs_1_), channel_id=1, source_target_pairs={{0,1},{1,0},{2,3},{3,2},{4,5},{5,4},{6,7},{7,6},{8,9},{9,8},{10,11... | collective-permute-start | bytes 638984 | tf_op jit(solution)/shard_map/ppermute | solution.py:43
  17.4 27.2 %collective-permute-start.9 = (bf16[576,512]{1,0:T(8,128)(2,1)}, bf16[576,512]{1,0:T(8,128)(2,1)S(1)}, u32[]{:S(2)}, u32[]{:S(2)}) collective-permute-start(bf16[576,512]{1,0:T(8,128)(2,1)} %pack_rest.1.refs_0_), channel_id=1, source_target_pairs={{0,6},{1,7},{2,4},{3,5},{4,2},{5,3},{6,0},{7,1},{8,14},{9,15},{10,... | collective-permute-start | bytes 1769480 | tf_op jit(solution)/shard_map/ppermute | solution.py:43
  19.5 26.9 %collective-permute-start.8 = (bf16[576,512]{1,0:T(8,128)(2,1)}, bf16[576,512]{1,0:T(8,128)(2,1)S(1)}, u32[]{:S(2)}, u32[]{:S(2)}) collective-permute-start(bf16[576,512]{1,0:T(8,128)(2,1)} %pack_rest.1.refs_0_), channel_id=1, source_target_pairs={{0,4},{1,5},{2,6},{3,7},{4,0},{5,1},{6,2},{7,3},{8,12},{9,13},{10,... | collective-permute-start | bytes 1769480 | tf_op jit(solution)/shard_map/ppermute | solution.py:43
  20.3 26.2 %collective-permute-start.7 = (bf16[576,512]{1,0:T(8,128)(2,1)}, bf16[576,512]{1,0:T(8,128)(2,1)S(1)}, u32[]{:S(2)}, u32[]{:S(2)}) collective-permute-start(bf16[576,512]{1,0:T(8,128)(2,1)} %pack_rest.1.refs_0_), channel_id=1, source_target_pairs={{0,2},{1,3},{2,0},{3,1},{4,6},{5,7},{6,4},{7,5},{8,10},{9,11},{10,... | collective-permute-start | bytes 1769480 | tf_op jit(solution)/shard_map/ppermute | solution.py:43
  21.6 25.3 %collective-permute-start.10 = (bf16[576,512]{1,0:T(8,128)(2,1)}, bf16[576,512]{1,0:T(8,128)(2,1)S(1)}, u32[]{:S(2)}, u32[]{:S(2)}) collective-permute-start(bf16[576,512]{1,0:T(8,128)(2,1)} %pack_rest.1.refs_0_), channel_id=1, source_target_pairs={{0,1},{1,0},{2,3},{3,2},{4,5},{5,4},{6,7},{7,6},{8,9},{9,8},{10,11... | collective-permute-start | bytes 1769480 | tf_op jit(solution)/shard_map/ppermute | solution.py:43
  75.3 8.4 %collective-permute-start.14 = (bf16[4,320,512]{2,1,0:T(8,128)(2,1)}, bf16[4,320,512]{2,1,0:T(8,128)(2,1)S(1)}, u32[]{:S(2)}, u32[]{:S(2)}) collective-permute-start(bf16[4,320,512]{2,1,0:T(8,128)(2,1)} %get-tuple-element.95), channel_id=1, source_target_pairs={{0,1},{1,0},{2,3},{3,2},{4,5},{5,4},{6,7},{7,6},{8,9},{9,8},{10,11... | collective-permute-start | bytes 3932168 | tf_op jit(solution)/shard_map/ppermute | solution.py:43
  75.5 8.1 %collective-permute-start.15 = (bf16[4,272,512]{2,1,0:T(8,128)(2,1)}, bf16[4,272,512]{2,1,0:T(8,128)(2,1)}, u32[]{:S(2)}, u32[]{:S(2)}) collective-permute-start(bf16[4,272,512]{2,1,0:T(8,128)(2,1)} %get-tuple-element.96), channel_id=1, source_target_pairs={{0,1},{1,0},{2,3},{3,2},{4,5},{5,4},{6,7},{7,6},{8,9},{9,8},{10,11... | collective-permute-start | bytes 3342344 | tf_op jit(solution)/shard_map/ppermute | solution.py:43
  83.8 19.7 %collective-permute-start.16 = (bf16[2,320,512]{2,1,0:T(8,128)(2,1)S(1)}, bf16[2,320,512]{2,1,0:T(8,128)(2,1)S(1)}, u32[]{:S(2)}, u32[]{:S(2)}) collective-permute-start(bf16[2,320,512]{2,1,0:T(8,128)(2,1)S(1)} %get-tuple-element.139), channel_id=1, source_target_pairs={{0,4},{1,5},{2,6},{3,7},{4,0},{5,1},{6,2},{7,3},{8,12},{9,13},{10,... | collective-permute-start | bytes 1966088 | tf_op jit(solution)/shard_map/ppermute | solution.py:43
  86.8 16.7 %collective-permute-start.17 = (bf16[2,272,512]{2,1,0:T(8,128)(2,1)S(1)}, bf16[2,272,512]{2,1,0:T(8,128)(2,1)}, u32[]{:S(2)}, u32[]{:S(2)}) collective-permute-start(bf16[2,272,512]{2,1,0:T(8,128)(2,1)S(1)} %get-tuple-element.142), channel_id=1, source_target_pairs={{0,2},{1,3},{2,0},{3,1},{4,6},{5,7},{6,4},{7,5},{8,10},{9,11},{10,... | collective-permute-start | bytes 1671176 | tf_op jit(solution)/shard_map/ppermute | solution.py:43
  103.6 10.4 %collective-permute-start.18 = (bf16[1,320,512]{2,1,0:T(8,128)(2,1)S(1)}, bf16[1,320,512]{2,1,0:T(8,128)(2,1)S(1)}, u32[]{:S(2)}, u32[]{:S(2)}) collective-permute-start(bf16[1,320,512]{2,1,0:T(8,128)(2,1)S(1)} %get-tuple-element.146), channel_id=1, source_target_pairs={{0,2},{1,3},{2,0},{3,1},{4,6},{5,7},{6,4},{7,5},{8,10},{9,11},{10,... | collective-permute-start | bytes 983048 | tf_op jit(solution)/shard_map/ppermute | solution.py:43
  106.2 7.9 %collective-permute-start.19 = (bf16[1,272,512]{2,1,0:T(8,128)(2,1)S(1)}, bf16[1,272,512]{2,1,0:T(8,128)(2,1)S(1)}, u32[]{:S(2)}, u32[]{:S(2)}) collective-permute-start(bf16[1,272,512]{2,1,0:T(8,128)(2,1)S(1)} %get-tuple-element.149), channel_id=1, source_target_pairs={{0,4},{1,5},{2,6},{3,7},{4,0},{5,1},{6,2},{7,3},{8,12},{9,13},{10,... | collective-permute-start | bytes 835592 | tf_op jit(solution)/shard_map/ppermute | solution.py:43
  114.6 8.5 %collective-permute-start.20 = (bf16[296,512]{1,0:T(8,128)(2,1)S(1)}, bf16[296,512]{1,0:T(8,128)(2,1)S(1)}, u32[]{:S(2)}, u32[]{:S(2)}) collective-permute-start(bf16[296,512]{1,0:T(8,128)(2,1)S(1)} %fusion.3), channel_id=1, source_target_pairs={{0,8},{8,0},{16,24},{24,16},{1,9},{9,1},{17,25},{25,17},{2,10},{10... | collective-permute-start | bytes 909320 | tf_op jit(solution)/shard_map/ppermute | solution.py:39
  117.0 16.0 %collective-permute-start.22 = (bf16[208,512]{1,0:T(8,128)(2,1)}, bf16[208,512]{1,0:T(8,128)(2,1)S(1)}, u32[]{:S(2)}, u32[]{:S(2)}) collective-permute-start(bf16[208,512]{1,0:T(8,128)(2,1)} %get-tuple-element.143), channel_id=1, source_target_pairs={{0,6},{1,7},{2,4},{3,5},{4,2},{5,3},{6,0},{7,1},{8,14},{9,15},{10,... | collective-permute-start | bytes 638984 | tf_op jit(solution)/shard_map/ppermute | solution.py:43
  118.3 14.7 %collective-permute-start.23 = (bf16[208,512]{1,0:T(8,128)(2,1)}, bf16[208,512]{1,0:T(8,128)(2,1)S(1)}, u32[]{:S(2)}, u32[]{:S(2)}) collective-permute-start(bf16[208,512]{1,0:T(8,128)(2,1)} %get-tuple-element.144), channel_id=1, source_target_pairs={{0,4},{1,5},{2,6},{3,7},{4,0},{5,1},{6,2},{7,3},{8,12},{9,13},{10,... | collective-permute-start | bytes 638984 | tf_op jit(solution)/shard_map/ppermute | solution.py:43
  119.4 13.6 %collective-permute-start.24 = (bf16[208,512]{1,0:T(8,128)(2,1)S(1)}, bf16[208,512]{1,0:T(8,128)(2,1)S(1)}, u32[]{:S(2)}, u32[]{:S(2)}) collective-permute-start(bf16[208,512]{1,0:T(8,128)(2,1)S(1)} %get-tuple-element.145), channel_id=1, source_target_pairs={{0,2},{1,3},{2,0},{3,1},{4,6},{5,7},{6,4},{7,5},{8,10},{9,11},{10,... | collective-permute-start | bytes 638984 | tf_op jit(solution)/shard_map/ppermute | solution.py:43
  123.5 15.1 %collective-permute-start.26 = (bf16[296,512]{1,0:T(8,128)(2,1)S(1)}, bf16[296,512]{1,0:T(8,128)(2,1)S(1)}, u32[]{:S(2)}, u32[]{:S(2)}) collective-permute-start(bf16[296,512]{1,0:T(8,128)(2,1)S(1)} %fusion.5), channel_id=1, source_target_pairs={{0,16},{8,24},{16,0},{24,8},{1,17},{9,25},{17,1},{25,9},{2,18},{10... | collective-permute-start | bytes 909320 | tf_op jit(solution)/shard_map/ppermute | solution.py:39
  133.3 7.6 %collective-permute-start.25 = (bf16[104,512]{1,0:T(8,128)(2,1)S(1)}, bf16[104,512]{1,0:T(8,128)(2,1)S(1)}, u32[]{:S(2)}, u32[]{:S(2)}) collective-permute-start(bf16[104,512]{1,0:T(8,128)(2,1)S(1)} %constant_dynamic-slice_fusion), channel_id=1, source_target_pairs={{0,8},{8,0},{16,24},{24,16},{1,9},{9,1},{17,25},{25,17},{2,10},{10... | collective-permute-start | bytes 319496 | tf_op jit(solution)/shard_map/ppermute | solution.py:39
  138.7 13.9 %collective-permute-start.29 = (bf16[296,512]{1,0:T(8,128)(2,1)S(1)}, bf16[296,512]{1,0:T(8,128)(2,1)S(1)}, u32[]{:S(2)}, u32[]{:S(2)}) collective-permute-start(bf16[296,512]{1,0:T(8,128)(2,1)S(1)} %add.117.s), channel_id=1, source_target_pairs={{0,8},{8,0},{16,24},{24,16},{1,9},{9,1},{17,25},{25,17},{2,10},{10... | collective-permute-start | bytes 909320 | tf_op jit(solution)/shard_map/ppermute | solution.py:39
  140.9 7.4 %collective-permute-start.27 = (bf16[104,512]{1,0:T(8,128)(2,1)S(1)}, bf16[104,512]{1,0:T(8,128)(2,1)S(1)}, u32[]{:S(2)}, u32[]{:S(2)}) collective-permute-start(bf16[104,512]{1,0:T(8,128)(2,1)S(1)} %dynamic-slice_add_fusion), channel_id=1, source_target_pairs={{0,16},{8,24},{16,0},{24,8},{1,17},{9,25},{17,1},{25,9},{2,18},{10... | collective-permute-start | bytes 319496 | tf_op jit(solution)/shard_map/ppermute | solution.py:39
  148.3 6.9 %collective-permute-start.28 = (bf16[104,512]{1,0:T(8,128)(2,1)S(1)}, bf16[104,512]{1,0:T(8,128)(2,1)S(1)}, u32[]{:S(2)}, u32[]{:S(2)}) collective-permute-start(bf16[104,512]{1,0:T(8,128)(2,1)S(1)} %add.119.s), channel_id=1, source_target_pairs={{0,8},{8,0},{16,24},{24,16},{1,9},{9,1},{17,25},{25,17},{2,10},{10... | collective-permute-start | bytes 319496 | tf_op jit(solution)/shard_map/ppermute | solution.py:39
  (23 other events, 199.9 us)

commit v17 on v15

--- a/solution.py
+++ b/solution.py
@@ -655,7 +655,7 @@
         out_specs=pl.BlockSpec((3, PW, T), lambda p: (0, p0 + p, 0)),
         out_shape=S((3, D, T), bf16),
         input_output_aliases={7: 0} if prev else {},
-        compiler_params=cp(), name="attn_bwd", cost_estimate=cost(cnt * 2 * 16 * T * T * 128, cnt * 2 * T * T * 2),
+        compiler_params=cp(56), name="attn_bwd", cost_estimate=cost(cnt * 2 * 16 * T * T * 128, cnt * 2 * T * T * 2),
     )(kv, qkvt, qkvt, gmt, mixedf, linv, et, *prev)
 
 

time: 155 us -> 154 us (level)
  other arithmetic: 4.4 us -> 2.52 us
    add x9, other arithmetic: 3.71 us -> 1.83 us  [add16(): return a + b]
  transfers between devices with their start and end apart: 30 -> 30, of which waited for: 12 -> 12; matrix products, arithmetic and copies ran while one was open for 2% -> 1% of each run, Pallas kernels for 43% -> 43%
where the time goes in v17:
time: 154 us; the launch traced here: 153 us
  Pallas kernels  95.5 us (62%)
  starting transfers between devices  31.5 us (20%)
  waiting for transfers between devices  21.4 us (14%)
  other arithmetic  2.52 us (2%)
  between operations  1.67 us (1%)
    pallas_call x1, Pallas kernels, ffn(): pl.pallas_call(functools.partial(ffn_body, n, meta, min(1024, FF)), grid_...  26 us
    pallas_call x2, Pallas kernels, attn_bwd(): pl.pallas_call(functools.partial(attn_bwd_body, HD, 1.0 / math.sqrt(HD),...  23.8 us
    ppermute x24, starting transfers between devices, swap(): return lax.ppermute(x, 'shard', xor_perm(lax.axis_size('shard'), k))  18.7 us
    pallas_call x1, Pallas kernels, attn_fwd(): pl.pallas_call(functools.partial(attn_fwd_body, HD, bi, min(512, T), p0),...  15.1 us
    ppermute x6, starting transfers between devices, rep_perm(): return lax.ppermute(x, 'rep', xor_perm(lax.axis_size('rep'), b))  12.8 us
    ppermute x6, waiting for transfers between devices, rep_perm(): return lax.ppermute(x, 'rep', xor_perm(lax.axis_size('rep'), b))  12 us
    ppermute x24, waiting for transfers between devices, swap(): return lax.ppermute(x, 'shard', xor_perm(lax.axis_size('shard'), k))  9.37 us
    pallas_call x1, Pallas kernels, front(): pl.pallas_call(functools.partial(front_body, scale, n, meta), grid_spec=p...  7.08 us
  transfers between devices with their start and end apart: 30, of which 12 were waited for; matrix products, arithmetic and copies ran while one was open for 1% of the time, Pallas kernels for 43%

profile of v17, /device:TPU:0, one launch (start us, length us, event | category | flops | bytes accessed | tf_op | source)
XLA Modules:
  0.0 153.4 jit_solution(3850707510898112209)
XLA Ops:
  0.7 1.8 %pack_first.1.refs_0_ = bf16[208,512]{1,0:T(8,128)(2,1)} custom-call(s32[1]{0:T(128)} %bitcast.me, bf16[64,1536]{1,0:T(8,128)(2,1)} %w.3, bf16[2,128]{1,0:T(2,128)(2,1)} %bitcast.47, bf16[1,64]{1,0:T(2,128)(2,1)} %bitcast.39, bf16[1,64]{1,0:T(2,128)(2,1)} %bitcast.41, bf16[1,64]{1,0:T(2,128)(2,1)} %bitcast.48, bf16[1,64]{1,0:T(2,128)(2,1)} %bitcast.49, ...), custom_call_target="tpu_custom_call" | custom-call | bytes 393216 | tf_op jit(solution)/shard_map/pack_first/pallas_call | solution.py:125
  2.4 2.9 %collective-permute-start = (bf16[208,512]{1,0:T(8,128)(2,1)}, bf16[208,512]{1,0:T(8,128)(2,1)S(1)}, u32[]{:S(2)}, u32[]{:S(2)}) collective-permute-start(bf16[208,512]{1,0:T(8,128)(2,1)} %pack_first.1.refs_0_), channel_id=1, source_target_pairs={{0,2},{1,3},{2,0},{3,1},{4,6},{5,7},{6,4},{7,5},{8,10},{9,11},{10,... | collective-permute-start | bytes 638984 | tf_op jit(solution)/shard_map/ppermute | solution.py:43
  6.9 1.9 %pack_rest.1.refs_0_ = bf16[576,512]{1,0:T(8,128)(2,1)} custom-call(bf16[64,512]{1,0:T(8,128)(2,1)} %wo.1, bf16[64,2048]{1,0:T(8,128)(2,1)} %wu.1, bf16[256,512]{1,0:T(8,128)(2,1)} %wd.1), custom_call_target="tpu_custom_call" | custom-call | bytes 524288 | tf_op jit(solution)/shard_map/pack_rest/pallas_call | solution.py:143
  8.8 4.2 %start.1 = (f32[1024,512]{1,0:T(8,128)}, bf16[528,1024]{1,0:T(8,128)(2,1)}) custom-call(bf16[1024,512]{1,0:T(8,128)(2,1)} %bitcast.43, bf16[1,512]{1,0:T(2,128)(2,1)} %step.4), custom_call_target="tpu_custom_call" | custom-call | flops 10485760 | bytes 4194304 | tf_op jit(solution)/shard_map/start/pallas_call | solution.py:287
  13.6 3.3 %collective-permute-done.1.refs_2_ = bf16[208,512]{1,0:T(8,128)(2,1)S(1)} collective-permute-done((bf16[208,512]{1,0:T(8,128)(2,1)}, bf16[208,512]{1,0:T(8,128)(2,1)S(1)}, u32[]{:S(2)}, u32[]{:S(2)}) %collective-permute-start.1) | collective-permute-done | bytes 213024 | tf_op jit(solution)/shard_map/ppermute | solution.py:43
  22.4 7.1 %front.1 = (bf16[2,1024,512]{2,1,0:T(8,128)(2,1)}, bf16[3,512,1024]{2,1,0:T(8,128)(2,1)}, bf16[512,1536]{1,0:T(8,128)(2,1)}, f32[8,512]{1,0:T(8,128)}, f32[1,2048]{1,0:T(1,128)}) custom-call(s32[1]{0:T(128)} %bitcast.me, f32[1024,512]{1,0:T(8,128)} %get-tuple-element.73.nx, bf16[208,512]{1,0:T(8,128)(2,1)} %pack_first.1.refs_0_, ...), custom_call_target="tpu_custom_call" | custom-call | flops 1610612736 | bytes 6291456 | tf_op jit(solution)/shard_map/front/pallas_call | solution.py:360
  29.5 15.1 %attn_fwd.1 = (bf16[8,1024,1024]{2,1,0:T(8,128)(2,1)}, bf16[1024,512]{1,0:T(8,128)(2,1)}, bf16[512,1024]{1,0:T(8,128)(2,1)}, f32[512,1024]{1,0:T(8,128)}, f32[4,8,1024]{2,1,0:T(8,128)}) custom-call(s32[1]{0:T(128)S(6)} %copy.34.ln, bf16[2,1024,512]{2,1,0:T(8,128)(2,1)} %get-tuple-element.80.k.v, bf16[3,512,1024]{2,1,0:T(8,128)(2,1)} %get-tuple-element.81.qt.vt.kt, ...), custom_call_target="tpu_custom_call" | custom-call | flops 8589934592 | bytes 16777216 | tf_op jit(solution)/shard_map/attn_fwd/pallas_call | solution.py:450
  49.3 26.0 %ffn.1 = (bf16[1024,512]{1,0:T(8,128)(2,1)}, bf16[1024,512]{1,0:T(8,128)(2,1)}, bf16[512,1024]{1,0:T(8,128)(2,1)}, bf16[4,320,512]{2,1,0:T(8,128)(2,1)}, bf16[4,...) custom-call(s32[1]{0:T(128)S(6)} %copy.34.ln, s32[1]{0:T(128)} %bitcast.me, ...), custom_call_target="tpu_custom_call" | custom-call | flops 14495514624 | bytes 8388608 | tf_op jit(solution)/shard_map/ffn/pallas_call | solution.py:606
  75.9 7.8 %attn_bwd.2.refs_0_ = bf16[3,512,1024]{2,1,0:T(8,128)(2,1)} custom-call(bf16[2,1024,512]{2,1,0:T(8,128)(2,1)} %get-tuple-element.80.k.v, bf16[3,512,1024]{2,1,0:T(8,128)(2,1)} %get-tuple-element.81.qt.vt.kt, bf16[3,512,1024]{2,1,0:T(8,128)(2,1)} %get-tuple-element.81.qt.vt.kt, bf16[512,1024]{1,0:T(8,128)(2,1)} %get-tuple-element.99.gt, ...), custom_call_target="tpu_custom_call" | custom-call | flops 4294967296 | bytes 4194304 | tf_op jit(solution)/shard_map/attn_bwd/pallas_call | solution.py:650
  85.2 1.5 collective-permute-start.16
  86.8 16.0 %attn_bwd.3.g = bf16[3,512,1024]{2,1,0:T(8,128)(2,1)} custom-call(bf16[2,1024,512]{2,1,0:T(8,128)(2,1)} %get-tuple-element.80.k.v, bf16[3,512,1024]{2,1,0:T(8,128)(2,1)} %get-tuple-element.81.qt.vt.kt, bf16[3,512,1024]{2,1,0:T(8,128)(2,1)} %get-tuple-element.81.qt.vt.kt, bf16[512,1024]{1,0:T(8,128)(2,1)} %get-tuple-element.99.gt, ...), custom_call_target="tpu_custom_call", output_to_operand_aliasing={{}: (7, {})} | custom-call | flops 12884901888 | bytes 12582912 | tf_op jit(solution)/shard_map/attn_bwd/pallas_call | solution.py:650
  104.7 5.6 %wqkv.1 = (bf16[4,208,512]{2,1,0:T(8,128)(2,1)}, bf16[4,208,512]{2,1,0:T(8,128)(2,1)}) custom-call(s32[1]{0:T(128)} %bitcast.me, bf16[528,1024]{1,0:T(8,128)(2,1)} %get-tuple-element.102.xht, bf16[3,512,1024]{2,1,0:T(8,128)(2,1)} %attn_bwd.3.g), custom_call_target="tpu_custom_call" | custom-call | flops 1610612736 | bytes 5242880 | tf_op jit(solution)/shard_map/wqkv/pallas_call | solution.py:686
  113.2 1.6 %collective-permute-start.20 = (bf16[296,512]{1,0:T(8,128)(2,1)S(1)}, bf16[296,512]{1,0:T(8,128)(2,1)S(1)}, u32[]{:S(2)}, u32[]{:S(2)}) collective-permute-start(bf16[296,512]{1,0:T(8,128)(2,1)S(1)} %fusion.3), channel_id=1, source_target_pairs={{0,8},{8,0},{16,24},{24,16},{1,9},{9,1},{17,25},{25,17},{2,10},{10... | collective-permute-start | bytes 909320 | tf_op jit(solution)/shard_map/ppermute | solution.py:39
  115.7 1.6 %collective-permute-start.22 = (bf16[208,512]{1,0:T(8,128)(2,1)}, bf16[208,512]{1,0:T(8,128)(2,1)S(1)}, u32[]{:S(2)}, u32[]{:S(2)}) collective-permute-start(bf16[208,512]{1,0:T(8,128)(2,1)} %get-tuple-element.135), channel_id=1, source_target_pairs={{0,6},{1,7},{2,4},{3,5},{4,2},{5,3},{6,0},{7,1},{8,14},{9,15},{10,... | collective-permute-start | bytes 638984 | tf_op jit(solution)/shard_map/ppermute | solution.py:43
  119.1 1.6 %collective-permute-done.20 = bf16[296,512]{1,0:T(8,128)(2,1)S(1)} collective-permute-done((bf16[296,512]{1,0:T(8,128)(2,1)S(1)}, bf16[296,512]{1,0:T(8,128)(2,1)S(1)}, u32[]{:S(2)}, u32[]{:S(2)}) %collective-permute-start.20) | collective-permute-done | bytes 303136 | tf_op jit(solution)/shard_map/ppermute | solution.py:39
  121.2 2.7 %collective-permute-start.26 = (bf16[296,512]{1,0:T(8,128)(2,1)S(1)}, bf16[296,512]{1,0:T(8,128)(2,1)S(1)}, u32[]{:S(2)}, u32[]{:S(2)}) collective-permute-start(bf16[296,512]{1,0:T(8,128)(2,1)S(1)} %fusion.5), channel_id=1, source_target_pairs={{0,16},{8,24},{16,0},{24,8},{1,17},{9,25},{17,1},{25,9},{2,18},{10... | collective-permute-start | bytes 909320 | tf_op jit(solution)/shard_map/ppermute | solution.py:39
  123.8 6.9 %back.1 = f32[1024,512]{1,0:T(8,128)} custom-call(bf16[1024,512]{1,0:T(8,128)(2,1)} %bitcast.45, bf16[1,512]{1,0:T(2,128)(2,1)} %step.4, f32[8,512]{1,0:T(8,128)} %get-tuple-element.78.vec, bf16[3,512,1024]{2,1,0:T(8,128)(2,1)} %attn_bwd.3.g, bf16[1024,512]{1,0:T(8,128)(2,1)} %get-tuple-element.109.gx1, bf16[512,1536]{1,0:T(8,128)(2,1)} %get-tuple-element.110.refs_0_), custom_call_target="tpu_custom_call" | custom-call | flops 1610612736 | bytes 7340032 | tf_op jit(solution)/shard_map/back/pallas_call | solution.py:713
  130.9 1.6 %collective-permute-start.25 = (bf16[104,512]{1,0:T(8,128)(2,1)S(1)}, bf16[104,512]{1,0:T(8,128)(2,1)S(1)}, u32[]{:S(2)}, u32[]{:S(2)}) collective-permute-start(bf16[104,512]{1,0:T(8,128)(2,1)S(1)} %constant_dynamic-slice_fusion), channel_id=1, source_target_pairs={{0,8},{8,0},{16,24},{24,16},{1,9},{9,1},{17,25},{25,17},{2,10},{10... | collective-permute-start | bytes 319496 | tf_op jit(solution)/shard_map/ppermute | solution.py:39
  132.6 2.8 %collective-permute-done.26 = bf16[296,512]{1,0:T(8,128)(2,1)S(1)} collective-permute-done((bf16[296,512]{1,0:T(8,128)(2,1)S(1)}, bf16[296,512]{1,0:T(8,128)(2,1)S(1)}, u32[]{:S(2)}, u32[]{:S(2)}) %collective-permute-start.26) | collective-permute-done | bytes 303136 | tf_op jit(solution)/shard_map/ppermute | solution.py:39
  137.6 2.0 %collective-permute-start.27 = (bf16[104,512]{1,0:T(8,128)(2,1)S(1)}, bf16[104,512]{1,0:T(8,128)(2,1)S(1)}, u32[]{:S(2)}, u32[]{:S(2)}) collective-permute-start(bf16[104,512]{1,0:T(8,128)(2,1)S(1)} %dynamic-slice_add_fusion), channel_id=1, source_target_pairs={{0,16},{8,24},{16,0},{24,8},{1,17},{9,25},{17,1},{25,9},{2,18},{10... | collective-permute-start | bytes 319496 | tf_op jit(solution)/shard_map/ppermute | solution.py:39
  139.6 5.2 %collective-permute-done.27 = bf16[104,512]{1,0:T(8,128)(2,1)S(1)} collective-permute-done((bf16[104,512]{1,0:T(8,128)(2,1)S(1)}, bf16[104,512]{1,0:T(8,128)(2,1)S(1)}, u32[]{:S(2)}, u32[]{:S(2)}) %collective-permute-start.27) | collective-permute-done | bytes 106528 | tf_op jit(solution)/shard_map/ppermute | solution.py:39
  144.9 4.2 %collective-permute-start.28 = (bf16[104,512]{1,0:T(8,128)(2,1)S(1)}, bf16[104,512]{1,0:T(8,128)(2,1)S(1)}, u32[]{:S(2)}, u32[]{:S(2)}) collective-permute-start(bf16[104,512]{1,0:T(8,128)(2,1)S(1)} %add.119.s), channel_id=1, source_target_pairs={{0,8},{8,0},{16,24},{24,16},{1,9},{9,1},{17,25},{25,17},{2,10},{10... | collective-permute-start | bytes 319496 | tf_op jit(solution)/shard_map/ppermute | solution.py:39
  149.2 1.7 %finish_rest.1 = (f32[256,512]{1,0:T(8,128)}, f32[64,2048]{1,0:T(8,128)}, f32[64,512]{1,0:T(8,128)}, f32[1,256]{1,0:T(1,128)}, f32[1,64]{1,0:T(1,128)}, /*index=...) custom-call(s32[2]{0:T(128)S(1)} %pad_add_fusion.ids, bf16[296,512]{1,0:T(8,128)(2,1)S(1)} %add.117.s, ...), custom_call_target="tpu_custom_call" | custom-call | bytes 1212416 | tf_op jit(solution)/shard_map/finish_rest/pallas_call | solution.py:201
  151.8 1.6 %finish_first.1 = (f32[64,1536]{1,0:T(8,128)}, f32[1,64]{1,0:T(1,128)}, f32[1,64]{1,0:T(1,128)}, f32[1,64]{1,0:T(1,128)}, f32[1,64]{1,0:T(1,128)}) custom-call(s32[2]{0:T(128)S(1)} %pad_add_fusion.ids, bf16[104,512]{1,0:T(8,128)(2,1)S(1)} %add.119.s, bf16[104,512]{1,0:T(8,128)(2,1)S(1)} %collective-permute-done.28.o, bf16[64,1536]{1,0:T(8,128)(2,1)S(1)} %copy-done, ...), custom_call_target="tpu_custom_call" | custom-call | bytes 786432 | tf_op jit(solution)/shard_map/finish_first/pallas_call | solution.py:245
  (97 shorter events, 25.1 us)
Async XLA Ops:
  2.4 10.6 %collective-permute-start = (bf16[208,512]{1,0:T(8,128)(2,1)}, bf16[208,512]{1,0:T(8,128)(2,1)S(1)}, u32[]{:S(2)}, u32[]{:S(2)}) collective-permute-start(bf16[208,512]{1,0:T(8,128)(2,1)} %pack_first.1.refs_0_), channel_id=1, source_target_pairs={{0,2},{1,3},{2,0},{3,1},{4,6},{5,7},{6,4},{7,5},{8,10},{9,11},{10,... | collective-permute-start | bytes 638984 | tf_op jit(solution)/shard_map/ppermute | solution.py:43
  5.4 11.5 %collective-permute-start.1 = (bf16[208,512]{1,0:T(8,128)(2,1)}, bf16[208,512]{1,0:T(8,128)(2,1)S(1)}, u32[]{:S(2)}, u32[]{:S(2)}) collective-permute-start(bf16[208,512]{1,0:T(8,128)(2,1)} %pack_first.1.refs_0_), channel_id=1, source_target_pairs={{0,4},{1,5},{2,6},{3,7},{4,0},{5,1},{6,2},{7,3},{8,12},{9,13},{10,... | collective-permute-start | bytes 638984 | tf_op jit(solution)/shard_map/ppermute | solution.py:43
  6.9 10.0 %collective-permute-start.2 = (bf16[208,512]{1,0:T(8,128)(2,1)}, bf16[208,512]{1,0:T(8,128)(2,1)S(1)}, u32[]{:S(2)}, u32[]{:S(2)}) collective-permute-start(bf16[208,512]{1,0:T(8,128)(2,1)} %pack_first.1.refs_0_), channel_id=1, source_target_pairs={{0,6},{1,7},{2,4},{3,5},{4,2},{5,3},{6,0},{7,1},{8,14},{9,15},{10,... | collective-permute-start | bytes 638984 | tf_op jit(solution)/shard_map/ppermute | solution.py:43
  6.9 12.6 %collective-permute-start.3 = (bf16[208,512]{1,0:T(8,128)(2,1)}, bf16[208,512]{1,0:T(8,128)(2,1)S(1)}, u32[]{:S(2)}, u32[]{:S(2)}) collective-permute-start(bf16[208,512]{1,0:T(8,128)(2,1)} %pack_first.1.refs_0_), channel_id=1, source_target_pairs={{0,1},{1,0},{2,3},{3,2},{4,5},{5,4},{6,7},{7,6},{8,9},{9,8},{10,11... | collective-permute-start | bytes 638984 | tf_op jit(solution)/shard_map/ppermute | solution.py:43
  13.0 7.3 %collective-permute-start.4 = (bf16[208,512]{1,0:T(8,128)(2,1)S(1)}, bf16[208,512]{1,0:T(8,128)(2,1)S(1)}, u32[]{:S(2)}, u32[]{:S(2)}) collective-permute-start(bf16[208,512]{1,0:T(8,128)(2,1)S(1)} %collective-permute-done.refs_1_), channel_id=1, source_target_pairs={{0,1},{1,0},{2,3},{3,2},{4,5},{5,4},{6,7},{7,6},{8,9},{9,8},{10,11... | collective-permute-start | bytes 638984 | tf_op jit(solution)/shard_map/ppermute | solution.py:43
  17.4 27.2 %collective-permute-start.9 = (bf16[576,512]{1,0:T(8,128)(2,1)}, bf16[576,512]{1,0:T(8,128)(2,1)S(1)}, u32[]{:S(2)}, u32[]{:S(2)}) collective-permute-start(bf16[576,512]{1,0:T(8,128)(2,1)} %pack_rest.1.refs_0_), channel_id=1, source_target_pairs={{0,6},{1,7},{2,4},{3,5},{4,2},{5,3},{6,0},{7,1},{8,14},{9,15},{10,... | collective-permute-start | bytes 1769480 | tf_op jit(solution)/shard_map/ppermute | solution.py:43
  19.5 26.9 %collective-permute-start.8 = (bf16[576,512]{1,0:T(8,128)(2,1)}, bf16[576,512]{1,0:T(8,128)(2,1)S(1)}, u32[]{:S(2)}, u32[]{:S(2)}) collective-permute-start(bf16[576,512]{1,0:T(8,128)(2,1)} %pack_rest.1.refs_0_), channel_id=1, source_target_pairs={{0,4},{1,5},{2,6},{3,7},{4,0},{5,1},{6,2},{7,3},{8,12},{9,13},{10,... | collective-permute-start | bytes 1769480 | tf_op jit(solution)/shard_map/ppermute | solution.py:43
  20.3 26.2 %collective-permute-start.7 = (bf16[576,512]{1,0:T(8,128)(2,1)}, bf16[576,512]{1,0:T(8,128)(2,1)S(1)}, u32[]{:S(2)}, u32[]{:S(2)}) collective-permute-start(bf16[576,512]{1,0:T(8,128)(2,1)} %pack_rest.1.refs_0_), channel_id=1, source_target_pairs={{0,2},{1,3},{2,0},{3,1},{4,6},{5,7},{6,4},{7,5},{8,10},{9,11},{10,... | collective-permute-start | bytes 1769480 | tf_op jit(solution)/shard_map/ppermute | solution.py:43
  21.6 25.3 %collective-permute-start.10 = (bf16[576,512]{1,0:T(8,128)(2,1)}, bf16[576,512]{1,0:T(8,128)(2,1)S(1)}, u32[]{:S(2)}, u32[]{:S(2)}) collective-permute-start(bf16[576,512]{1,0:T(8,128)(2,1)} %pack_rest.1.refs_0_), channel_id=1, source_target_pairs={{0,1},{1,0},{2,3},{3,2},{4,5},{5,4},{6,7},{7,6},{8,9},{9,8},{10,11... | collective-permute-start | bytes 1769480 | tf_op jit(solution)/shard_map/ppermute | solution.py:43
  75.3 8.4 %collective-permute-start.14 = (bf16[4,320,512]{2,1,0:T(8,128)(2,1)}, bf16[4,320,512]{2,1,0:T(8,128)(2,1)S(1)}, u32[]{:S(2)}, u32[]{:S(2)}) collective-permute-start(bf16[4,320,512]{2,1,0:T(8,128)(2,1)} %get-tuple-element.91), channel_id=1, source_target_pairs={{0,1},{1,0},{2,3},{3,2},{4,5},{5,4},{6,7},{7,6},{8,9},{9,8},{10,11... | collective-permute-start | bytes 3932168 | tf_op jit(solution)/shard_map/ppermute | solution.py:43
  75.5 8.1 %collective-permute-start.15 = (bf16[4,272,512]{2,1,0:T(8,128)(2,1)}, bf16[4,272,512]{2,1,0:T(8,128)(2,1)S(1)}, u32[]{:S(2)}, u32[]{:S(2)}) collective-permute-start(bf16[4,272,512]{2,1,0:T(8,128)(2,1)} %get-tuple-element.92), channel_id=1, source_target_pairs={{0,1},{1,0},{2,3},{3,2},{4,5},{5,4},{6,7},{7,6},{8,9},{9,8},{10,11... | collective-permute-start | bytes 3342344 | tf_op jit(solution)/shard_map/ppermute | solution.py:43
  83.8 19.0 %collective-permute-start.17 = (bf16[2,272,512]{2,1,0:T(8,128)(2,1)S(1)}, bf16[2,272,512]{2,1,0:T(8,128)(2,1)S(1)}, u32[]{:S(2)}, u32[]{:S(2)}) collective-permute-start(bf16[2,272,512]{2,1,0:T(8,128)(2,1)S(1)} %get-tuple-element.134), channel_id=1, source_target_pairs={{0,2},{1,3},{2,0},{3,1},{4,6},{5,7},{6,4},{7,5},{8,10},{9,11},{10,... | collective-permute-start | bytes 1671176 | tf_op jit(solution)/shard_map/ppermute | solution.py:43
  85.2 17.5 %collective-permute-start.16 = (bf16[2,320,512]{2,1,0:T(8,128)(2,1)S(1)}, bf16[2,320,512]{2,1,0:T(8,128)(2,1)S(1)}, u32[]{:S(2)}, u32[]{:S(2)}) collective-permute-start(bf16[2,320,512]{2,1,0:T(8,128)(2,1)S(1)} %get-tuple-element.131), channel_id=1, source_target_pairs={{0,4},{1,5},{2,6},{3,7},{4,0},{5,1},{6,2},{7,3},{8,12},{9,13},{10,... | collective-permute-start | bytes 1966088 | tf_op jit(solution)/shard_map/ppermute | solution.py:43
  102.9 8.5 %collective-permute-start.19 = (bf16[1,272,512]{2,1,0:T(8,128)(2,1)S(1)}, bf16[1,272,512]{2,1,0:T(8,128)(2,1)S(1)}, u32[]{:S(2)}, u32[]{:S(2)}) collective-permute-start(bf16[1,272,512]{2,1,0:T(8,128)(2,1)S(1)} %get-tuple-element.141), channel_id=1, source_target_pairs={{0,4},{1,5},{2,6},{3,7},{4,0},{5,1},{6,2},{7,3},{8,12},{9,13},{10,... | collective-permute-start | bytes 835592 | tf_op jit(solution)/shard_map/ppermute | solution.py:43
  103.7 9.0 %collective-permute-start.18 = (bf16[1,320,512]{2,1,0:T(8,128)(2,1)S(1)}, bf16[1,320,512]{2,1,0:T(8,128)(2,1)S(1)}, u32[]{:S(2)}, u32[]{:S(2)}) collective-permute-start(bf16[1,320,512]{2,1,0:T(8,128)(2,1)S(1)} %get-tuple-element.138), channel_id=1, source_target_pairs={{0,2},{1,3},{2,0},{3,1},{4,6},{5,7},{6,4},{7,5},{8,10},{9,11},{10,... | collective-permute-start | bytes 983048 | tf_op jit(solution)/shard_map/ppermute | solution.py:43
  113.2 7.6 %collective-permute-start.20 = (bf16[296,512]{1,0:T(8,128)(2,1)S(1)}, bf16[296,512]{1,0:T(8,128)(2,1)S(1)}, u32[]{:S(2)}, u32[]{:S(2)}) collective-permute-start(bf16[296,512]{1,0:T(8,128)(2,1)S(1)} %fusion.3), channel_id=1, source_target_pairs={{0,8},{8,0},{16,24},{24,16},{1,9},{9,1},{17,25},{25,17},{2,10},{10... | collective-permute-start | bytes 909320 | tf_op jit(solution)/shard_map/ppermute | solution.py:39
  115.7 15.0 %collective-permute-start.22 = (bf16[208,512]{1,0:T(8,128)(2,1)}, bf16[208,512]{1,0:T(8,128)(2,1)S(1)}, u32[]{:S(2)}, u32[]{:S(2)}) collective-permute-start(bf16[208,512]{1,0:T(8,128)(2,1)} %get-tuple-element.135), channel_id=1, source_target_pairs={{0,6},{1,7},{2,4},{3,5},{4,2},{5,3},{6,0},{7,1},{8,14},{9,15},{10,... | collective-permute-start | bytes 638984 | tf_op jit(solution)/shard_map/ppermute | solution.py:43
  117.2 13.5 %collective-permute-start.23 = (bf16[208,512]{1,0:T(8,128)(2,1)}, bf16[208,512]{1,0:T(8,128)(2,1)S(1)}, u32[]{:S(2)}, u32[]{:S(2)}) collective-permute-start(bf16[208,512]{1,0:T(8,128)(2,1)} %get-tuple-element.136), channel_id=1, source_target_pairs={{0,4},{1,5},{2,6},{3,7},{4,0},{5,1},{6,2},{7,3},{8,12},{9,13},{10,... | collective-permute-start | bytes 638984 | tf_op jit(solution)/shard_map/ppermute | solution.py:43
  118.2 12.5 %collective-permute-start.24 = (bf16[208,512]{1,0:T(8,128)(2,1)S(1)}, bf16[208,512]{1,0:T(8,128)(2,1)S(1)}, u32[]{:S(2)}, u32[]{:S(2)}) collective-permute-start(bf16[208,512]{1,0:T(8,128)(2,1)S(1)} %get-tuple-element.137), channel_id=1, source_target_pairs={{0,2},{1,3},{2,0},{3,1},{4,6},{5,7},{6,4},{7,5},{8,10},{9,11},{10,... | collective-permute-start | bytes 638984 | tf_op jit(solution)/shard_map/ppermute | solution.py:43
  121.2 14.1 %collective-permute-start.26 = (bf16[296,512]{1,0:T(8,128)(2,1)S(1)}, bf16[296,512]{1,0:T(8,128)(2,1)S(1)}, u32[]{:S(2)}, u32[]{:S(2)}) collective-permute-start(bf16[296,512]{1,0:T(8,128)(2,1)S(1)} %fusion.5), channel_id=1, source_target_pairs={{0,16},{8,24},{16,0},{24,8},{1,17},{9,25},{17,1},{25,9},{2,18},{10... | collective-permute-start | bytes 909320 | tf_op jit(solution)/shard_map/ppermute | solution.py:39
  130.9 6.7 %collective-permute-start.25 = (bf16[104,512]{1,0:T(8,128)(2,1)S(1)}, bf16[104,512]{1,0:T(8,128)(2,1)S(1)}, u32[]{:S(2)}, u32[]{:S(2)}) collective-permute-start(bf16[104,512]{1,0:T(8,128)(2,1)S(1)} %constant_dynamic-slice_fusion), channel_id=1, source_target_pairs={{0,8},{8,0},{16,24},{24,16},{1,9},{9,1},{17,25},{25,17},{2,10},{10... | collective-permute-start | bytes 319496 | tf_op jit(solution)/shard_map/ppermute | solution.py:39
  135.4 13.8 %collective-permute-start.29 = (bf16[296,512]{1,0:T(8,128)(2,1)S(1)}, bf16[296,512]{1,0:T(8,128)(2,1)S(1)}, u32[]{:S(2)}, u32[]{:S(2)}) collective-permute-start(bf16[296,512]{1,0:T(8,128)(2,1)S(1)} %add.117.s), channel_id=1, source_target_pairs={{0,8},{8,0},{16,24},{24,16},{1,9},{9,1},{17,25},{25,17},{2,10},{10... | collective-permute-start | bytes 909320 | tf_op jit(solution)/shard_map/ppermute | solution.py:39
  137.6 7.2 %collective-permute-start.27 = (bf16[104,512]{1,0:T(8,128)(2,1)S(1)}, bf16[104,512]{1,0:T(8,128)(2,1)S(1)}, u32[]{:S(2)}, u32[]{:S(2)}) collective-permute-start(bf16[104,512]{1,0:T(8,128)(2,1)S(1)} %dynamic-slice_add_fusion), channel_id=1, source_target_pairs={{0,16},{8,24},{16,0},{24,8},{1,17},{9,25},{17,1},{25,9},{2,18},{10... | collective-permute-start | bytes 319496 | tf_op jit(solution)/shard_map/ppermute | solution.py:39
  144.9 6.9 %collective-permute-start.28 = (bf16[104,512]{1,0:T(8,128)(2,1)S(1)}, bf16[104,512]{1,0:T(8,128)(2,1)S(1)}, u32[]{:S(2)}, u32[]{:S(2)}) collective-permute-start(bf16[104,512]{1,0:T(8,128)(2,1)S(1)} %add.119.s), channel_id=1, source_target_pairs={{0,8},{8,0},{16,24},{24,16},{1,9},{9,1},{17,25},{25,17},{2,10},{10... | collective-permute-start | bytes 319496 | tf_op jit(solution)/shard_map/ppermute | solution.py:39
  (23 other events, 197.5 us)

commit v18 on v17

--- a/solution.py
+++ b/solution.py
@@ -713,7 +713,7 @@
     return pl.pallas_call(
         back_body, grid=(T // bm,),
         in_specs=[rows, full(step), full(vec), pl.BlockSpec((3, D, bm), lambda i: (0, 0, i)), rows] + [full(w) for w in ws],
-        out_specs=rows, out_shape=S((T, D), f32), compiler_params=cp(), name="back", cost_estimate=cost(6 * T * D * D, 14 * T * D),
+        out_specs=rows, out_shape=S((T, D), f32), compiler_params=cp(56), name="back", cost_estimate=cost(6 * T * D * D, 14 * T * D),
     )(tok, step, vec, g, gx1, *ws)
 
 

time: 154 us -> 154 us (level)
  no operation moved by 1% of the time
where the time goes in v18:
time: 154 us; the launch traced here: 153 us
  Pallas kernels  95.5 us (62%)
  starting transfers between devices  31.5 us (20%)
  waiting for transfers between devices  22.1 us (14%)
  other arithmetic  1.77 us (1%)
  between operations  1.67 us (1%)
    pallas_call x1, Pallas kernels, ffn(): pl.pallas_call(functools.partial(ffn_body, n, meta, min(1024, FF)), grid_...  26 us
    pallas_call x2, Pallas kernels, attn_bwd(): pl.pallas_call(functools.partial(attn_bwd_body, HD, 1.0 / math.sqrt(HD),...  23.8 us
    ppermute x24, starting transfers between devices, swap(): return lax.ppermute(x, 'shard', xor_perm(lax.axis_size('shard'), k))  18.7 us
    pallas_call x1, Pallas kernels, attn_fwd(): pl.pallas_call(functools.partial(attn_fwd_body, HD, bi, min(512, T), p0),...  15.1 us
    ppermute x6, starting transfers between devices, rep_perm(): return lax.ppermute(x, 'rep', xor_perm(lax.axis_size('rep'), b))  12.8 us
    ppermute x6, waiting for transfers between devices, rep_perm(): return lax.ppermute(x, 'rep', xor_perm(lax.axis_size('rep'), b))  12.7 us
    ppermute x24, waiting for transfers between devices, swap(): return lax.ppermute(x, 'shard', xor_perm(lax.axis_size('shard'), k))  9.37 us
    pallas_call x1, Pallas kernels, front(): pl.pallas_call(functools.partial(front_body, scale, n, meta), grid_spec=p...  7.08 us
  transfers between devices with their start and end apart: 30, of which 12 were waited for; matrix products, arithmetic and copies ran while one was open for 1% of the time, Pallas kernels for 43%

profile of v18, /device:TPU:0, one launch (start us, length us, event | category | flops | bytes accessed | tf_op | source)
XLA Modules:
  0.0 153.4 jit_solution(10667354644905665035)
XLA Ops:
  0.7 1.8 %pack_first.1.refs_0_ = bf16[208,512]{1,0:T(8,128)(2,1)} custom-call(s32[1]{0:T(128)} %bitcast.me, bf16[64,1536]{1,0:T(8,128)(2,1)} %w.3, bf16[2,128]{1,0:T(2,128)(2,1)} %bitcast.47, bf16[1,64]{1,0:T(2,128)(2,1)} %bitcast.39, bf16[1,64]{1,0:T(2,128)(2,1)} %bitcast.41, bf16[1,64]{1,0:T(2,128)(2,1)} %bitcast.48, bf16[1,64]{1,0:T(2,128)(2,1)} %bitcast.49, ...), custom_call_target="tpu_custom_call" | custom-call | bytes 393216 | tf_op jit(solution)/shard_map/pack_first/pallas_call | solution.py:125
  2.4 2.9 %collective-permute-start = (bf16[208,512]{1,0:T(8,128)(2,1)}, bf16[208,512]{1,0:T(8,128)(2,1)S(1)}, u32[]{:S(2)}, u32[]{:S(2)}) collective-permute-start(bf16[208,512]{1,0:T(8,128)(2,1)} %pack_first.1.refs_0_), channel_id=1, source_target_pairs={{0,2},{1,3},{2,0},{3,1},{4,6},{5,7},{6,4},{7,5},{8,10},{9,11},{10,... | collective-permute-start | bytes 638984 | tf_op jit(solution)/shard_map/ppermute | solution.py:43
  6.9 1.9 %pack_rest.1.refs_0_ = bf16[576,512]{1,0:T(8,128)(2,1)} custom-call(bf16[64,512]{1,0:T(8,128)(2,1)} %wo.1, bf16[64,2048]{1,0:T(8,128)(2,1)} %wu.1, bf16[256,512]{1,0:T(8,128)(2,1)} %wd.1), custom_call_target="tpu_custom_call" | custom-call | bytes 524288 | tf_op jit(solution)/shard_map/pack_rest/pallas_call | solution.py:143
  8.8 4.2 %start.1 = (f32[1024,512]{1,0:T(8,128)}, bf16[528,1024]{1,0:T(8,128)(2,1)}) custom-call(bf16[1024,512]{1,0:T(8,128)(2,1)} %bitcast.43, bf16[1,512]{1,0:T(2,128)(2,1)} %step.4), custom_call_target="tpu_custom_call" | custom-call | flops 10485760 | bytes 4194304 | tf_op jit(solution)/shard_map/start/pallas_call | solution.py:287
  13.6 3.3 %collective-permute-done.1.refs_2_ = bf16[208,512]{1,0:T(8,128)(2,1)S(1)} collective-permute-done((bf16[208,512]{1,0:T(8,128)(2,1)}, bf16[208,512]{1,0:T(8,128)(2,1)S(1)}, u32[]{:S(2)}, u32[]{:S(2)}) %collective-permute-start.1) | collective-permute-done | bytes 213024 | tf_op jit(solution)/shard_map/ppermute | solution.py:43
  22.4 7.1 %front.1 = (bf16[2,1024,512]{2,1,0:T(8,128)(2,1)}, bf16[3,512,1024]{2,1,0:T(8,128)(2,1)}, bf16[512,1536]{1,0:T(8,128)(2,1)}, f32[8,512]{1,0:T(8,128)}, f32[1,2048]{1,0:T(1,128)}) custom-call(s32[1]{0:T(128)} %bitcast.me, f32[1024,512]{1,0:T(8,128)} %get-tuple-element.73.nx, bf16[208,512]{1,0:T(8,128)(2,1)} %pack_first.1.refs_0_, ...), custom_call_target="tpu_custom_call" | custom-call | flops 1610612736 | bytes 6291456 | tf_op jit(solution)/shard_map/front/pallas_call | solution.py:360
  29.5 15.1 %attn_fwd.1 = (bf16[8,1024,1024]{2,1,0:T(8,128)(2,1)}, bf16[1024,512]{1,0:T(8,128)(2,1)}, bf16[512,1024]{1,0:T(8,128)(2,1)}, f32[512,1024]{1,0:T(8,128)}, f32[4,8,1024]{2,1,0:T(8,128)}) custom-call(s32[1]{0:T(128)S(6)} %copy.34.ln, bf16[2,1024,512]{2,1,0:T(8,128)(2,1)} %get-tuple-element.80.k.v, bf16[3,512,1024]{2,1,0:T(8,128)(2,1)} %get-tuple-element.81.qt.vt.kt, ...), custom_call_target="tpu_custom_call" | custom-call | flops 8589934592 | bytes 16777216 | tf_op jit(solution)/shard_map/attn_fwd/pallas_call | solution.py:450
  49.3 26.0 %ffn.1 = (bf16[1024,512]{1,0:T(8,128)(2,1)}, bf16[1024,512]{1,0:T(8,128)(2,1)}, bf16[512,1024]{1,0:T(8,128)(2,1)}, bf16[4,320,512]{2,1,0:T(8,128)(2,1)}, bf16[4,...) custom-call(s32[1]{0:T(128)S(6)} %copy.34.ln, s32[1]{0:T(128)} %bitcast.me, ...), custom_call_target="tpu_custom_call" | custom-call | flops 14495514624 | bytes 8388608 | tf_op jit(solution)/shard_map/ffn/pallas_call | solution.py:606
  75.9 7.8 %attn_bwd.2.refs_0_ = bf16[3,512,1024]{2,1,0:T(8,128)(2,1)} custom-call(bf16[2,1024,512]{2,1,0:T(8,128)(2,1)} %get-tuple-element.80.k.v, bf16[3,512,1024]{2,1,0:T(8,128)(2,1)} %get-tuple-element.81.qt.vt.kt, bf16[3,512,1024]{2,1,0:T(8,128)(2,1)} %get-tuple-element.81.qt.vt.kt, bf16[512,1024]{1,0:T(8,128)(2,1)} %get-tuple-element.99.gt, ...), custom_call_target="tpu_custom_call" | custom-call | flops 4294967296 | bytes 4194304 | tf_op jit(solution)/shard_map/attn_bwd/pallas_call | solution.py:650
  85.2 1.5 collective-permute-start.16
  86.8 16.0 %attn_bwd.3.g = bf16[3,512,1024]{2,1,0:T(8,128)(2,1)} custom-call(bf16[2,1024,512]{2,1,0:T(8,128)(2,1)} %get-tuple-element.80.k.v, bf16[3,512,1024]{2,1,0:T(8,128)(2,1)} %get-tuple-element.81.qt.vt.kt, bf16[3,512,1024]{2,1,0:T(8,128)(2,1)} %get-tuple-element.81.qt.vt.kt, bf16[512,1024]{1,0:T(8,128)(2,1)} %get-tuple-element.99.gt, ...), custom_call_target="tpu_custom_call", output_to_operand_aliasing={{}: (7, {})} | custom-call | flops 12884901888 | bytes 12582912 | tf_op jit(solution)/shard_map/attn_bwd/pallas_call | solution.py:650
  104.7 5.6 %wqkv.1 = (bf16[4,208,512]{2,1,0:T(8,128)(2,1)}, bf16[4,208,512]{2,1,0:T(8,128)(2,1)}) custom-call(s32[1]{0:T(128)} %bitcast.me, bf16[528,1024]{1,0:T(8,128)(2,1)} %get-tuple-element.102.xht, bf16[3,512,1024]{2,1,0:T(8,128)(2,1)} %attn_bwd.3.g), custom_call_target="tpu_custom_call" | custom-call | flops 1610612736 | bytes 5242880 | tf_op jit(solution)/shard_map/wqkv/pallas_call | solution.py:686
  113.2 1.6 %collective-permute-start.20 = (bf16[296,512]{1,0:T(8,128)(2,1)S(1)}, bf16[296,512]{1,0:T(8,128)(2,1)S(1)}, u32[]{:S(2)}, u32[]{:S(2)}) collective-permute-start(bf16[296,512]{1,0:T(8,128)(2,1)S(1)} %fusion.3), channel_id=1, source_target_pairs={{0,8},{8,0},{16,24},{24,16},{1,9},{9,1},{17,25},{25,17},{2,10},{10... | collective-permute-start | bytes 909320 | tf_op jit(solution)/shard_map/ppermute | solution.py:39
  114.9 1.6 %collective-permute-start.22 = (bf16[208,512]{1,0:T(8,128)(2,1)S(1)}, bf16[208,512]{1,0:T(8,128)(2,1)S(1)}, u32[]{:S(2)}, u32[]{:S(2)}) collective-permute-start(bf16[208,512]{1,0:T(8,128)(2,1)S(1)} %get-tuple-element.135), channel_id=1, source_target_pairs={{0,6},{1,7},{2,4},{3,5},{4,2},{5,3},{6,0},{7,1},{8,14},{9,15},{10,... | collective-permute-start | bytes 638984 | tf_op jit(solution)/shard_map/ppermute | solution.py:43
  118.5 2.3 %collective-permute-done.20 = bf16[296,512]{1,0:T(8,128)(2,1)S(1)} collective-permute-done((bf16[296,512]{1,0:T(8,128)(2,1)S(1)}, bf16[296,512]{1,0:T(8,128)(2,1)S(1)}, u32[]{:S(2)}, u32[]{:S(2)}) %collective-permute-start.20) | collective-permute-done | bytes 303136 | tf_op jit(solution)/shard_map/ppermute | solution.py:39
  121.2 2.7 %collective-permute-start.26 = (bf16[296,512]{1,0:T(8,128)(2,1)S(1)}, bf16[296,512]{1,0:T(8,128)(2,1)S(1)}, u32[]{:S(2)}, u32[]{:S(2)}) collective-permute-start(bf16[296,512]{1,0:T(8,128)(2,1)S(1)} %fusion.5), channel_id=1, source_target_pairs={{0,16},{8,24},{16,0},{24,8},{1,17},{9,25},{17,1},{25,9},{2,18},{10... | collective-permute-start | bytes 909320 | tf_op jit(solution)/shard_map/ppermute | solution.py:39
  123.8 6.9 %back.1 = f32[1024,512]{1,0:T(8,128)} custom-call(bf16[1024,512]{1,0:T(8,128)(2,1)} %bitcast.45, bf16[1,512]{1,0:T(2,128)(2,1)} %step.4, f32[8,512]{1,0:T(8,128)} %get-tuple-element.78.vec, bf16[3,512,1024]{2,1,0:T(8,128)(2,1)} %attn_bwd.3.g, bf16[1024,512]{1,0:T(8,128)(2,1)} %get-tuple-element.109.gx1, bf16[512,1536]{1,0:T(8,128)(2,1)} %get-tuple-element.110.refs_0_), custom_call_target="tpu_custom_call" | custom-call | flops 1610612736 | bytes 7340032 | tf_op jit(solution)/shard_map/back/pallas_call | solution.py:713
  130.9 1.6 %collective-permute-start.25 = (bf16[104,512]{1,0:T(8,128)(2,1)S(1)}, bf16[104,512]{1,0:T(8,128)(2,1)S(1)}, u32[]{:S(2)}, u32[]{:S(2)}) collective-permute-start(bf16[104,512]{1,0:T(8,128)(2,1)S(1)} %constant_dynamic-slice_fusion), channel_id=1, source_target_pairs={{0,8},{8,0},{16,24},{24,16},{1,9},{9,1},{17,25},{25,17},{2,10},{10... | collective-permute-start | bytes 319496 | tf_op jit(solution)/shard_map/ppermute | solution.py:39
  132.6 2.8 %collective-permute-done.26 = bf16[296,512]{1,0:T(8,128)(2,1)S(1)} collective-permute-done((bf16[296,512]{1,0:T(8,128)(2,1)S(1)}, bf16[296,512]{1,0:T(8,128)(2,1)S(1)}, u32[]{:S(2)}, u32[]{:S(2)}) %collective-permute-start.26) | collective-permute-done | bytes 303136 | tf_op jit(solution)/shard_map/ppermute | solution.py:39
  137.6 2.0 %collective-permute-start.27 = (bf16[104,512]{1,0:T(8,128)(2,1)S(1)}, bf16[104,512]{1,0:T(8,128)(2,1)S(1)}, u32[]{:S(2)}, u32[]{:S(2)}) collective-permute-start(bf16[104,512]{1,0:T(8,128)(2,1)S(1)} %dynamic-slice_add_fusion), channel_id=1, source_target_pairs={{0,16},{8,24},{16,0},{24,8},{1,17},{9,25},{17,1},{25,9},{2,18},{10... | collective-permute-start | bytes 319496 | tf_op jit(solution)/shard_map/ppermute | solution.py:39
  139.6 5.2 %collective-permute-done.27 = bf16[104,512]{1,0:T(8,128)(2,1)S(1)} collective-permute-done((bf16[104,512]{1,0:T(8,128)(2,1)S(1)}, bf16[104,512]{1,0:T(8,128)(2,1)S(1)}, u32[]{:S(2)}, u32[]{:S(2)}) %collective-permute-start.27) | collective-permute-done | bytes 106528 | tf_op jit(solution)/shard_map/ppermute | solution.py:39
  144.9 4.2 %collective-permute-start.28 = (bf16[104,512]{1,0:T(8,128)(2,1)S(1)}, bf16[104,512]{1,0:T(8,128)(2,1)S(1)}, u32[]{:S(2)}, u32[]{:S(2)}) collective-permute-start(bf16[104,512]{1,0:T(8,128)(2,1)S(1)} %add.119.s), channel_id=1, source_target_pairs={{0,8},{8,0},{16,24},{24,16},{1,9},{9,1},{17,25},{25,17},{2,10},{10... | collective-permute-start | bytes 319496 | tf_op jit(solution)/shard_map/ppermute | solution.py:39
  149.2 1.7 %finish_rest.1 = (f32[256,512]{1,0:T(8,128)}, f32[64,2048]{1,0:T(8,128)}, f32[64,512]{1,0:T(8,128)}, f32[1,256]{1,0:T(1,128)}, f32[1,64]{1,0:T(1,128)}, /*index=...) custom-call(s32[2]{0:T(128)S(1)} %pad_add_fusion.ids, bf16[296,512]{1,0:T(8,128)(2,1)S(1)} %add.117.s, ...), custom_call_target="tpu_custom_call" | custom-call | bytes 1212416 | tf_op jit(solution)/shard_map/finish_rest/pallas_call | solution.py:201
  151.8 1.6 %finish_first.1 = (f32[64,1536]{1,0:T(8,128)}, f32[1,64]{1,0:T(1,128)}, f32[1,64]{1,0:T(1,128)}, f32[1,64]{1,0:T(1,128)}, f32[1,64]{1,0:T(1,128)}) custom-call(s32[2]{0:T(128)S(1)} %pad_add_fusion.ids, bf16[104,512]{1,0:T(8,128)(2,1)S(1)} %add.119.s, bf16[104,512]{1,0:T(8,128)(2,1)S(1)} %collective-permute-done.28.o, bf16[64,1536]{1,0:T(8,128)(2,1)S(1)} %copy-done, ...), custom_call_target="tpu_custom_call" | custom-call | bytes 786432 | tf_op jit(solution)/shard_map/finish_first/pallas_call | solution.py:245
  (97 shorter events, 24.4 us)
Async XLA Ops:
  2.4 10.6 %collective-permute-start = (bf16[208,512]{1,0:T(8,128)(2,1)}, bf16[208,512]{1,0:T(8,128)(2,1)S(1)}, u32[]{:S(2)}, u32[]{:S(2)}) collective-permute-start(bf16[208,512]{1,0:T(8,128)(2,1)} %pack_first.1.refs_0_), channel_id=1, source_target_pairs={{0,2},{1,3},{2,0},{3,1},{4,6},{5,7},{6,4},{7,5},{8,10},{9,11},{10,... | collective-permute-start | bytes 638984 | tf_op jit(solution)/shard_map/ppermute | solution.py:43
  5.4 11.5 %collective-permute-start.1 = (bf16[208,512]{1,0:T(8,128)(2,1)}, bf16[208,512]{1,0:T(8,128)(2,1)S(1)}, u32[]{:S(2)}, u32[]{:S(2)}) collective-permute-start(bf16[208,512]{1,0:T(8,128)(2,1)} %pack_first.1.refs_0_), channel_id=1, source_target_pairs={{0,4},{1,5},{2,6},{3,7},{4,0},{5,1},{6,2},{7,3},{8,12},{9,13},{10,... | collective-permute-start | bytes 638984 | tf_op jit(solution)/shard_map/ppermute | solution.py:43
  6.9 10.0 %collective-permute-start.2 = (bf16[208,512]{1,0:T(8,128)(2,1)}, bf16[208,512]{1,0:T(8,128)(2,1)S(1)}, u32[]{:S(2)}, u32[]{:S(2)}) collective-permute-start(bf16[208,512]{1,0:T(8,128)(2,1)} %pack_first.1.refs_0_), channel_id=1, source_target_pairs={{0,6},{1,7},{2,4},{3,5},{4,2},{5,3},{6,0},{7,1},{8,14},{9,15},{10,... | collective-permute-start | bytes 638984 | tf_op jit(solution)/shard_map/ppermute | solution.py:43
  6.9 12.6 %collective-permute-start.3 = (bf16[208,512]{1,0:T(8,128)(2,1)}, bf16[208,512]{1,0:T(8,128)(2,1)S(1)}, u32[]{:S(2)}, u32[]{:S(2)}) collective-permute-start(bf16[208,512]{1,0:T(8,128)(2,1)} %pack_first.1.refs_0_), channel_id=1, source_target_pairs={{0,1},{1,0},{2,3},{3,2},{4,5},{5,4},{6,7},{7,6},{8,9},{9,8},{10,11... | collective-permute-start | bytes 638984 | tf_op jit(solution)/shard_map/ppermute | solution.py:43
  13.0 7.3 %collective-permute-start.4 = (bf16[208,512]{1,0:T(8,128)(2,1)S(1)}, bf16[208,512]{1,0:T(8,128)(2,1)S(1)}, u32[]{:S(2)}, u32[]{:S(2)}) collective-permute-start(bf16[208,512]{1,0:T(8,128)(2,1)S(1)} %collective-permute-done.refs_1_), channel_id=1, source_target_pairs={{0,1},{1,0},{2,3},{3,2},{4,5},{5,4},{6,7},{7,6},{8,9},{9,8},{10,11... | collective-permute-start | bytes 638984 | tf_op jit(solution)/shard_map/ppermute | solution.py:43
  17.4 27.2 %collective-permute-start.9 = (bf16[576,512]{1,0:T(8,128)(2,1)}, bf16[576,512]{1,0:T(8,128)(2,1)S(1)}, u32[]{:S(2)}, u32[]{:S(2)}) collective-permute-start(bf16[576,512]{1,0:T(8,128)(2,1)} %pack_rest.1.refs_0_), channel_id=1, source_target_pairs={{0,6},{1,7},{2,4},{3,5},{4,2},{5,3},{6,0},{7,1},{8,14},{9,15},{10,... | collective-permute-start | bytes 1769480 | tf_op jit(solution)/shard_map/ppermute | solution.py:43
  19.5 26.9 %collective-permute-start.8 = (bf16[576,512]{1,0:T(8,128)(2,1)}, bf16[576,512]{1,0:T(8,128)(2,1)S(1)}, u32[]{:S(2)}, u32[]{:S(2)}) collective-permute-start(bf16[576,512]{1,0:T(8,128)(2,1)} %pack_rest.1.refs_0_), channel_id=1, source_target_pairs={{0,4},{1,5},{2,6},{3,7},{4,0},{5,1},{6,2},{7,3},{8,12},{9,13},{10,... | collective-permute-start | bytes 1769480 | tf_op jit(solution)/shard_map/ppermute | solution.py:43
  20.3 26.2 %collective-permute-start.7 = (bf16[576,512]{1,0:T(8,128)(2,1)}, bf16[576,512]{1,0:T(8,128)(2,1)S(1)}, u32[]{:S(2)}, u32[]{:S(2)}) collective-permute-start(bf16[576,512]{1,0:T(8,128)(2,1)} %pack_rest.1.refs_0_), channel_id=1, source_target_pairs={{0,2},{1,3},{2,0},{3,1},{4,6},{5,7},{6,4},{7,5},{8,10},{9,11},{10,... | collective-permute-start | bytes 1769480 | tf_op jit(solution)/shard_map/ppermute | solution.py:43
  21.6 25.3 %collective-permute-start.10 = (bf16[576,512]{1,0:T(8,128)(2,1)}, bf16[576,512]{1,0:T(8,128)(2,1)S(1)}, u32[]{:S(2)}, u32[]{:S(2)}) collective-permute-start(bf16[576,512]{1,0:T(8,128)(2,1)} %pack_rest.1.refs_0_), channel_id=1, source_target_pairs={{0,1},{1,0},{2,3},{3,2},{4,5},{5,4},{6,7},{7,6},{8,9},{9,8},{10,11... | collective-permute-start | bytes 1769480 | tf_op jit(solution)/shard_map/ppermute | solution.py:43
  75.3 8.4 %collective-permute-start.14 = (bf16[4,320,512]{2,1,0:T(8,128)(2,1)}, bf16[4,320,512]{2,1,0:T(8,128)(2,1)S(1)}, u32[]{:S(2)}, u32[]{:S(2)}) collective-permute-start(bf16[4,320,512]{2,1,0:T(8,128)(2,1)} %get-tuple-element.91), channel_id=1, source_target_pairs={{0,1},{1,0},{2,3},{3,2},{4,5},{5,4},{6,7},{7,6},{8,9},{9,8},{10,11... | collective-permute-start | bytes 3932168 | tf_op jit(solution)/shard_map/ppermute | solution.py:43
  75.5 8.1 %collective-permute-start.15 = (bf16[4,272,512]{2,1,0:T(8,128)(2,1)}, bf16[4,272,512]{2,1,0:T(8,128)(2,1)S(1)}, u32[]{:S(2)}, u32[]{:S(2)}) collective-permute-start(bf16[4,272,512]{2,1,0:T(8,128)(2,1)} %get-tuple-element.92), channel_id=1, source_target_pairs={{0,1},{1,0},{2,3},{3,2},{4,5},{5,4},{6,7},{7,6},{8,9},{9,8},{10,11... | collective-permute-start | bytes 3342344 | tf_op jit(solution)/shard_map/ppermute | solution.py:43
  83.8 19.0 %collective-permute-start.17 = (bf16[2,272,512]{2,1,0:T(8,128)(2,1)S(1)}, bf16[2,272,512]{2,1,0:T(8,128)(2,1)S(1)}, u32[]{:S(2)}, u32[]{:S(2)}) collective-permute-start(bf16[2,272,512]{2,1,0:T(8,128)(2,1)S(1)} %get-tuple-element.134), channel_id=1, source_target_pairs={{0,2},{1,3},{2,0},{3,1},{4,6},{5,7},{6,4},{7,5},{8,10},{9,11},{10,... | collective-permute-start | bytes 1671176 | tf_op jit(solution)/shard_map/ppermute | solution.py:43
  85.2 17.5 %collective-permute-start.16 = (bf16[2,320,512]{2,1,0:T(8,128)(2,1)S(1)}, bf16[2,320,512]{2,1,0:T(8,128)(2,1)S(1)}, u32[]{:S(2)}, u32[]{:S(2)}) collective-permute-start(bf16[2,320,512]{2,1,0:T(8,128)(2,1)S(1)} %get-tuple-element.131), channel_id=1, source_target_pairs={{0,4},{1,5},{2,6},{3,7},{4,0},{5,1},{6,2},{7,3},{8,12},{9,13},{10,... | collective-permute-start | bytes 1966088 | tf_op jit(solution)/shard_map/ppermute | solution.py:43
  102.9 8.5 %collective-permute-start.19 = (bf16[1,272,512]{2,1,0:T(8,128)(2,1)S(1)}, bf16[1,272,512]{2,1,0:T(8,128)(2,1)S(1)}, u32[]{:S(2)}, u32[]{:S(2)}) collective-permute-start(bf16[1,272,512]{2,1,0:T(8,128)(2,1)S(1)} %get-tuple-element.141), channel_id=1, source_target_pairs={{0,4},{1,5},{2,6},{3,7},{4,0},{5,1},{6,2},{7,3},{8,12},{9,13},{10,... | collective-permute-start | bytes 835592 | tf_op jit(solution)/shard_map/ppermute | solution.py:43
  103.7 9.0 %collective-permute-start.18 = (bf16[1,320,512]{2,1,0:T(8,128)(2,1)S(1)}, bf16[1,320,512]{2,1,0:T(8,128)(2,1)S(1)}, u32[]{:S(2)}, u32[]{:S(2)}) collective-permute-start(bf16[1,320,512]{2,1,0:T(8,128)(2,1)S(1)} %get-tuple-element.138), channel_id=1, source_target_pairs={{0,2},{1,3},{2,0},{3,1},{4,6},{5,7},{6,4},{7,5},{8,10},{9,11},{10,... | collective-permute-start | bytes 983048 | tf_op jit(solution)/shard_map/ppermute | solution.py:43
  113.2 7.6 %collective-permute-start.20 = (bf16[296,512]{1,0:T(8,128)(2,1)S(1)}, bf16[296,512]{1,0:T(8,128)(2,1)S(1)}, u32[]{:S(2)}, u32[]{:S(2)}) collective-permute-start(bf16[296,512]{1,0:T(8,128)(2,1)S(1)} %fusion.3), channel_id=1, source_target_pairs={{0,8},{8,0},{16,24},{24,16},{1,9},{9,1},{17,25},{25,17},{2,10},{10... | collective-permute-start | bytes 909320 | tf_op jit(solution)/shard_map/ppermute | solution.py:39
  114.9 15.8 %collective-permute-start.22 = (bf16[208,512]{1,0:T(8,128)(2,1)S(1)}, bf16[208,512]{1,0:T(8,128)(2,1)S(1)}, u32[]{:S(2)}, u32[]{:S(2)}) collective-permute-start(bf16[208,512]{1,0:T(8,128)(2,1)S(1)} %get-tuple-element.135), channel_id=1, source_target_pairs={{0,6},{1,7},{2,4},{3,5},{4,2},{5,3},{6,0},{7,1},{8,14},{9,15},{10,... | collective-permute-start | bytes 638984 | tf_op jit(solution)/shard_map/ppermute | solution.py:43
  116.5 14.2 %collective-permute-start.23 = (bf16[208,512]{1,0:T(8,128)(2,1)S(1)}, bf16[208,512]{1,0:T(8,128)(2,1)S(1)}, u32[]{:S(2)}, u32[]{:S(2)}) collective-permute-start(bf16[208,512]{1,0:T(8,128)(2,1)S(1)} %get-tuple-element.136), channel_id=1, source_target_pairs={{0,4},{1,5},{2,6},{3,7},{4,0},{5,1},{6,2},{7,3},{8,12},{9,13},{10,... | collective-permute-start | bytes 638984 | tf_op jit(solution)/shard_map/ppermute | solution.py:43
  117.6 13.2 %collective-permute-start.24 = (bf16[208,512]{1,0:T(8,128)(2,1)S(1)}, bf16[208,512]{1,0:T(8,128)(2,1)S(1)}, u32[]{:S(2)}, u32[]{:S(2)}) collective-permute-start(bf16[208,512]{1,0:T(8,128)(2,1)S(1)} %get-tuple-element.137), channel_id=1, source_target_pairs={{0,2},{1,3},{2,0},{3,1},{4,6},{5,7},{6,4},{7,5},{8,10},{9,11},{10,... | collective-permute-start | bytes 638984 | tf_op jit(solution)/shard_map/ppermute | solution.py:43
  121.2 14.1 %collective-permute-start.26 = (bf16[296,512]{1,0:T(8,128)(2,1)S(1)}, bf16[296,512]{1,0:T(8,128)(2,1)S(1)}, u32[]{:S(2)}, u32[]{:S(2)}) collective-permute-start(bf16[296,512]{1,0:T(8,128)(2,1)S(1)} %fusion.5), channel_id=1, source_target_pairs={{0,16},{8,24},{16,0},{24,8},{1,17},{9,25},{17,1},{25,9},{2,18},{10... | collective-permute-start | bytes 909320 | tf_op jit(solution)/shard_map/ppermute | solution.py:39
  130.9 6.7 %collective-permute-start.25 = (bf16[104,512]{1,0:T(8,128)(2,1)S(1)}, bf16[104,512]{1,0:T(8,128)(2,1)S(1)}, u32[]{:S(2)}, u32[]{:S(2)}) collective-permute-start(bf16[104,512]{1,0:T(8,128)(2,1)S(1)} %constant_dynamic-slice_fusion), channel_id=1, source_target_pairs={{0,8},{8,0},{16,24},{24,16},{1,9},{9,1},{17,25},{25,17},{2,10},{10... | collective-permute-start | bytes 319496 | tf_op jit(solution)/shard_map/ppermute | solution.py:39
  135.4 13.8 %collective-permute-start.29 = (bf16[296,512]{1,0:T(8,128)(2,1)S(1)}, bf16[296,512]{1,0:T(8,128)(2,1)S(1)}, u32[]{:S(2)}, u32[]{:S(2)}) collective-permute-start(bf16[296,512]{1,0:T(8,128)(2,1)S(1)} %add.117.s), channel_id=1, source_target_pairs={{0,8},{8,0},{16,24},{24,16},{1,9},{9,1},{17,25},{25,17},{2,10},{10... | collective-permute-start | bytes 909320 | tf_op jit(solution)/shard_map/ppermute | solution.py:39
  137.6 7.2 %collective-permute-start.27 = (bf16[104,512]{1,0:T(8,128)(2,1)S(1)}, bf16[104,512]{1,0:T(8,128)(2,1)S(1)}, u32[]{:S(2)}, u32[]{:S(2)}) collective-permute-start(bf16[104,512]{1,0:T(8,128)(2,1)S(1)} %dynamic-slice_add_fusion), channel_id=1, source_target_pairs={{0,16},{8,24},{16,0},{24,8},{1,17},{9,25},{17,1},{25,9},{2,18},{10... | collective-permute-start | bytes 319496 | tf_op jit(solution)/shard_map/ppermute | solution.py:39
  144.9 6.9 %collective-permute-start.28 = (bf16[104,512]{1,0:T(8,128)(2,1)S(1)}, bf16[104,512]{1,0:T(8,128)(2,1)S(1)}, u32[]{:S(2)}, u32[]{:S(2)}) collective-permute-start(bf16[104,512]{1,0:T(8,128)(2,1)S(1)} %add.119.s), channel_id=1, source_target_pairs={{0,8},{8,0},{16,24},{24,16},{1,9},{9,1},{17,25},{25,17},{2,10},{10... | collective-permute-start | bytes 319496 | tf_op jit(solution)/shard_map/ppermute | solution.py:39
  (23 other events, 197.5 us)
